TPU v7x, 32 devices: a whole 2x2x4 slice. The times are simulated.
32 devices in a mesh: pb: 4 (over y, x), pa: 8 (over z, core).
Axes of the slice: x: 2, y: 2, z: 4, core: 2. Of those that a mesh axis runs over, the one named last changes fastest.
Arguments:
- question_in: bfloat16 [256, 64, 768], P(('pb', 'pa')), may hold values from -6 to 6
- passage_in: bfloat16 [64, 256, 768], P(('pb', 'pa')), may hold values from -6 to 6
- question_len: int32 [256], P(('pb', 'pa')), may hold values from 8 to 64, as said below
- passage_len: int32 [64], P(('pb', 'pa')), may hold values from 40 to 256, as said below
- positive: int32 [256], P('pb'), may hold values from 0 to 63, as said below
- question_cot: bfloat16 [256, 64, 768], P(('pb', 'pa')), may hold values from -6 to 6
- passage_cot: bfloat16 [64, 256, 768], P(('pb', 'pa')), may hold values from -6 to 6
- w_joined: bfloat16 [2, 768, 2304], P(None, ('pb', 'pa')), may hold values from -0.21875 to 0.21875
- w_output: bfloat16 [2, 768, 768], P(None, ('pb', 'pa')), may hold values from -0.875 to 0.875
- w_expand: bfloat16 [2, 768, 3072], P(None, ('pb', 'pa')), may hold values from -0.21875 to 0.21875
- w_reduce: bfloat16 [2, 3072, 768], P(None, ('pb', 'pa')), may hold values from -0.109375 to 0.109375
- vectors: bfloat16 [2, 8, 768], P(None, None, ('pb', 'pa'))
- b_expand: bfloat16 [2, 3072], P(None, ('pb', 'pa')), may hold values from -4 to 4
Outputs:
- question_out: bfloat16 [256, 64, 768], P(('pb', 'pa'))
- passage_out: bfloat16 [64, 256, 768], P(('pb', 'pa'))
- question_loss: float32 [256], P(('pb', 'pa'))
- question_grad: float32 [256, 64, 768], P(('pb', 'pa'))
- passage_grad: float32 [64, 256, 768], P(('pb', 'pa'))
- grad_joined: float32 [2, 768, 2304], P(None, ('pb', 'pa'))
- grad_output: float32 [2, 768, 768], P(None, ('pb', 'pa'))
- grad_expand: float32 [2, 768, 3072], P(None, ('pb', 'pa'))
- grad_reduce: float32 [2, 3072, 768], P(None, ('pb', 'pa'))
- grad_vectors: float32 [2, 8, 768], P(None, None, ('pb', 'pa'))
- grad_b_expand: float32 [2, 3072], P(None, ('pb', 'pa'))
Inputs may be any that keep to these rules, and one draw needn't show every extreme that they name: `question_len`: valid tokens of a question; slot 0 is always valid. `passage_len`: valid tokens of a passage; slot 0 is always valid. `positive`: any passage of the batch.
All inputs are finite; a program needn't handle non-finite values.
Results may differ from a plain program's by a relative error of at most 0.014.
Values may be sent and summed in bfloat16 or wider, within the bound.
No kernel may reach another device: no remote copies, remote signals or barrier semaphores. Data moves between devices by JAX's collectives and lax.ppermute only.
A program may use at most 256 MiB of HBM per device.

v0:
```python
import jax
import jax.numpy as jnp
from jax import lax
from jax.sharding import PartitionSpec as P

D = 768
HEADS = 12
HDIM = 64
FF = 3072


norm_eps = 1e-06
masked_score = -1000000000.0
score_scale = 0.0625
loss_weight = 16.0


def layer_norm(values, norm_gain, norm_shift):
    centred = values - jnp.mean(values, axis=-1, keepdims=True)
    spread = jnp.mean(centred * centred, axis=-1, keepdims=True)
    return centred * lax.rsqrt(spread + norm_eps) * norm_gain + norm_shift


def gelu_exact(values):
    return jax.nn.gelu(values, approximate=False)


def attention_inputs(inputs, lengths, w_joined, vectors):
    num_seq, seq_len, model_width = inputs.shape
    token_rows = inputs.reshape(num_seq * seq_len, model_width)
    joined_proj = jnp.dot(token_rows, w_joined, preferred_element_type=jnp.float32)
    head_shape = (num_seq, seq_len, HEADS, HDIM)
    queries = (joined_proj[:, :model_width] + vectors[0]).astype(jnp.bfloat16).reshape(head_shape)
    key_rows = (
        joined_proj[:, model_width : 2 * model_width].astype(jnp.bfloat16).reshape(head_shape)
    )
    value_rows = (
        (joined_proj[:, 2 * model_width :] + vectors[1]).astype(jnp.bfloat16).reshape(head_shape)
    )
    scores = jnp.einsum(
        "sqhd,skhd->shqk", queries, key_rows, preferred_element_type=jnp.float32
    ) * HDIM ** (-0.5)
    valid_slots = jnp.arange(seq_len, dtype=jnp.int32)[None, :] < lengths[:, None]
    scores = jnp.where(valid_slots[:, None, None, :], scores, masked_score)
    return (token_rows, queries, key_rows, value_rows, scores, valid_slots)


def dense_part(token_rows, attn_probs, value_rows, params):
    w_joined, w_output, w_expand, w_reduce, vectors, b_expand = params
    model_width = token_rows.shape[1]
    context = jnp.einsum(
        "shqk,skhd->sqhd",
        attn_probs.astype(jnp.bfloat16),
        value_rows,
        preferred_element_type=jnp.float32,
    )
    context = context.reshape(-1, model_width).astype(jnp.bfloat16)
    attended = jnp.dot(context, w_output, preferred_element_type=jnp.float32) + vectors[2]
    first_sum = token_rows.astype(jnp.float32) + attended
    mid_norm = layer_norm(first_sum, vectors[3], vectors[4])
    mid_low = mid_norm.astype(jnp.bfloat16)
    expanded = jnp.dot(mid_low, w_expand, preferred_element_type=jnp.float32) + b_expand
    active = gelu_exact(expanded).astype(jnp.bfloat16)
    reduced = jnp.dot(active, w_reduce, preferred_element_type=jnp.float32) + vectors[5]
    return (context, first_sum, mid_low, expanded, active, mid_norm + reduced)


def tower_forward(inputs, lengths, params):
    vectors = params[4]
    token_rows, queries, key_rows, value_rows, scores, valid_slots = attention_inputs(
        inputs, lengths, params[0], vectors
    )
    maxima = jnp.max(scores, axis=-1, keepdims=True)
    exp_scores = jnp.exp(scores - maxima)
    totals = jnp.sum(exp_scores, axis=-1, keepdims=True)
    attn_probs = exp_scores / totals
    log_total = maxima + jnp.log(totals)
    second_sum = dense_part(token_rows, attn_probs, value_rows, params)[5]
    row_mask = valid_slots.reshape(-1, 1).astype(jnp.float32)
    outputs = layer_norm(second_sum, vectors[6], vectors[7]) * row_mask
    return (outputs.astype(jnp.bfloat16).reshape(inputs.shape), log_total)


def tower_backward(inputs, lengths, params, log_total, grad_out):
    w_joined, w_output, w_expand, w_reduce, vectors, b_expand = params
    token_rows, queries, key_rows, value_rows, scores, valid_slots = attention_inputs(
        inputs, lengths, w_joined, vectors
    )
    attn_probs = jnp.exp(scores - log_total)
    context, first_sum, mid_low, expanded, active, second_sum = dense_part(
        token_rows, attn_probs, value_rows, params
    )
    model_width = token_rows.shape[1]
    head_scale = HDIM ** (-0.5)
    row_mask = valid_slots.reshape(-1, 1).astype(jnp.float32)
    grad_rows = grad_out.reshape(-1, model_width) * row_mask
    unused_two, norm_two = jax.vjp(
        layer_norm, second_sum, vectors[6].astype(jnp.float32), vectors[7].astype(jnp.float32)
    )
    grad_second, grad_gain_two, grad_shift_two = norm_two(grad_rows)
    grad_reduced = grad_second.astype(jnp.bfloat16)
    grad_bias_reduce = jnp.sum(grad_reduced.astype(jnp.float32), axis=0)
    grad_active = jnp.einsum(
        "rd,fd->rf", grad_reduced, w_reduce, preferred_element_type=jnp.float32
    )
    unused_act, gelu_pull = jax.vjp(gelu_exact, expanded)
    grad_expanded = gelu_pull(grad_active)[0].astype(jnp.bfloat16)
    grad_bias_expand = jnp.sum(grad_expanded.astype(jnp.float32), axis=0)
    grad_mid = grad_second + jnp.einsum(
        "rf,df->rd", grad_expanded, w_expand, preferred_element_type=jnp.float32
    )
    unused_one, norm_one = jax.vjp(
        layer_norm, first_sum, vectors[3].astype(jnp.float32), vectors[4].astype(jnp.float32)
    )
    grad_first, grad_gain_one, grad_shift_one = norm_one(grad_mid)
    grad_attended = grad_first.astype(jnp.bfloat16)
    grad_bias_output = jnp.sum(grad_attended.astype(jnp.float32), axis=0)
    grad_context = jnp.einsum(
        "rd,cd->rc", grad_attended, w_output, preferred_element_type=jnp.float32
    )
    grad_context = grad_context.astype(jnp.bfloat16).reshape(queries.shape)
    grad_probs = jnp.einsum(
        "sqhd,skhd->shqk", grad_context, value_rows, preferred_element_type=jnp.float32
    )
    grad_values = jnp.einsum(
        "shqk,sqhd->skhd",
        attn_probs.astype(jnp.bfloat16),
        grad_context,
        preferred_element_type=jnp.float32,
    ).astype(jnp.bfloat16)
    row_dot = jnp.sum(grad_probs * attn_probs, axis=-1, keepdims=True)
    grad_scores = (attn_probs * (grad_probs - row_dot)).astype(jnp.bfloat16)
    grad_queries = (
        (
            jnp.einsum("shqk,skhd->sqhd", grad_scores, key_rows, preferred_element_type=jnp.float32)
            * head_scale
        )
        .astype(jnp.bfloat16)
        .reshape(-1, model_width)
    )
    grad_keys = (
        (
            jnp.einsum("shqk,sqhd->skhd", grad_scores, queries, preferred_element_type=jnp.float32)
            * head_scale
        )
        .astype(jnp.bfloat16)
        .reshape(-1, model_width)
    )
    grad_values = grad_values.reshape(-1, model_width)
    grad_joined_rows = jnp.concatenate([grad_queries, grad_keys, grad_values], axis=1)
    grad_inputs = grad_first + jnp.einsum(
        "re,de->rd", grad_joined_rows, w_joined, preferred_element_type=jnp.float32
    )
    grad_vector_rows = jnp.stack(
        [
            jnp.sum(grad_queries.astype(jnp.float32), axis=0),
            jnp.sum(grad_values.astype(jnp.float32), axis=0),
            grad_bias_output,
            grad_gain_one,
            grad_shift_one,
            grad_bias_reduce,
            grad_gain_two,
            grad_shift_two,
        ]
    )
    kept_rows = (
        token_rows,
        grad_joined_rows,
        context,
        grad_attended,
        mid_low,
        grad_expanded,
        active,
        grad_reduced,
        grad_vector_rows,
        grad_bias_expand,
    )
    return (grad_inputs.reshape(inputs.shape), kept_rows)


def gradient_rows(kept_rows, count):
    (
        token_rows,
        grad_joined_rows,
        context,
        grad_attended,
        mid_low,
        grad_expanded,
        active,
        grad_reduced,
        grad_vector_rows,
        grad_bias_expand,
    ) = kept_rows
    grad_w_joined = jnp.einsum(
        "rd,re->de", token_rows, grad_joined_rows, preferred_element_type=jnp.float32
    )
    grad_w_output = jnp.einsum(
        "rc,rd->cd", context, grad_attended, preferred_element_type=jnp.float32
    )
    grad_w_expand = jnp.einsum(
        "rd,rf->df", mid_low, grad_expanded, preferred_element_type=jnp.float32
    )
    grad_w_reduce = jnp.einsum(
        "rf,rd->fd", active, grad_reduced, preferred_element_type=jnp.float32
    ).reshape(count, -1)
    vector_part = grad_vector_rows.T
    bias_part = grad_bias_expand.reshape(count, 4)
    return jnp.concatenate(
        [grad_w_joined, grad_w_output, grad_w_expand, grad_w_reduce, vector_part, bias_part], axis=1
    )


def split_rows(block):
    local_rows = block.shape[0]
    model_width = D
    cuts = [
        0,
        3 * model_width,
        4 * model_width,
        4 * model_width + FF,
        8 * model_width + FF,
        8 * model_width + FF + 8,
        8 * model_width + FF + 12,
    ]
    pieces = [block[:, cuts[index] : cuts[index + 1]] for index in range(6)]
    return (
        pieces[0],
        pieces[1],
        pieces[2],
        pieces[3].reshape(4 * local_rows, model_width),
        pieces[4].T,
        pieces[5].reshape(4 * local_rows),
    )


def per_device(
    question_in,
    passage_in,
    question_len,
    passage_len,
    positive,
    question_cot,
    passage_cot,
    w_joined,
    w_output,
    w_expand,
    w_reduce,
    vectors,
    b_expand,
):
    gathered = (
        lax.all_gather(w_joined, ("pb", "pa"), axis=1, tiled=True),
        lax.all_gather(w_output, ("pb", "pa"), axis=1, tiled=True),
        lax.all_gather(w_expand, ("pb", "pa"), axis=1, tiled=True),
        lax.all_gather(w_reduce, ("pb", "pa"), axis=1, tiled=True),
        lax.all_gather(vectors, ("pb", "pa"), axis=2, tiled=True),
        lax.all_gather(b_expand, ("pb", "pa"), axis=1, tiled=True),
    )
    tower_q = tuple((weight_piece[0] for weight_piece in gathered))
    tower_p = tuple((weight_piece[1] for weight_piece in gathered))
    question_out, question_lse = tower_forward(question_in, question_len, tower_q)
    passage_out, passage_lse = tower_forward(passage_in, passage_len, tower_p)
    cls_rows = lax.all_gather(question_out[:, 0, :], "pa", axis=0, tiled=True)
    cls_cols = lax.all_gather(passage_out[:, 0, :], "pb", axis=0, tiled=True)
    similarity = (
        jnp.einsum("qd,pd->qp", cls_rows, cls_cols, preferred_element_type=jnp.float32)
        * score_scale
    )
    mine_pa = lax.axis_index("pa")
    span_pa = lax.axis_size("pa")
    per_dev = passage_in.shape[0]
    owner_dev = positive // per_dev
    column_idx = owner_dev // span_pa * per_dev + positive % per_dev
    is_local = owner_dev % span_pa == mine_pa
    cols_iota = jnp.arange(similarity.shape[1], dtype=jnp.int32)
    target_hot = jnp.where(
        (cols_iota[None, :] == column_idx[:, None]) & is_local[:, None], 1.0, 0.0
    )
    pos_part = jnp.sum(similarity * target_hot, axis=1)
    local_max = jnp.max(similarity, axis=1)
    row_max = lax.pmax(local_max, "pa")
    exp_sim = jnp.exp(similarity - row_max[:, None])
    row_total, pos_score = lax.psum((jnp.sum(exp_sim, axis=1), pos_part), "pa")
    row_loss = row_max + jnp.log(row_total) - pos_score
    grad_sim = (loss_weight * (exp_sim / row_total[:, None] - target_hot)).astype(jnp.bfloat16)
    grad_rows_q = jnp.dot(grad_sim, cls_cols, preferred_element_type=jnp.float32) * score_scale
    grad_cols_p = (
        jnp.einsum("qp,qd->pd", grad_sim, cls_rows, preferred_element_type=jnp.float32)
        * score_scale
    )
    grad_cls_q = lax.psum_scatter(
        grad_rows_q.astype(jnp.bfloat16), "pa", scatter_dimension=0, tiled=True
    ).astype(jnp.float32)
    grad_cls_p = lax.psum_scatter(
        grad_cols_p.astype(jnp.bfloat16), "pb", scatter_dimension=0, tiled=True
    ).astype(jnp.float32)
    quota_rows = question_in.shape[0]
    question_loss = lax.dynamic_slice_in_dim(row_loss, mine_pa * quota_rows, quota_rows)
    grad_q_out = question_cot.astype(jnp.float32).at[:, 0, :].add(grad_cls_q)
    grad_p_out = passage_cot.astype(jnp.float32).at[:, 0, :].add(grad_cls_p)
    back_weights = (
        lax.all_gather(w_joined, ("pb", "pa"), axis=1, tiled=True),
        lax.all_gather(w_output, ("pb", "pa"), axis=1, tiled=True),
        lax.all_gather(w_expand, ("pb", "pa"), axis=1, tiled=True),
        lax.all_gather(w_reduce, ("pb", "pa"), axis=1, tiled=True),
        lax.all_gather(vectors, ("pb", "pa"), axis=2, tiled=True),
        lax.all_gather(b_expand, ("pb", "pa"), axis=1, tiled=True),
    )
    back_q = tuple((weight_piece[0] for weight_piece in back_weights))
    back_p = tuple((weight_piece[1] for weight_piece in back_weights))
    share_rows = vectors.shape[2]
    question_grad, kept_q = tower_backward(
        question_in, question_len, back_q, question_lse, grad_q_out
    )
    passage_grad, kept_p = tower_backward(passage_in, passage_len, back_p, passage_lse, grad_p_out)
    block_both = lax.psum_scatter(
        jnp.concatenate(
            [
                gradient_rows(kept_q, share_rows * lax.axis_size(("pb", "pa"))),
                gradient_rows(kept_p, share_rows * lax.axis_size(("pb", "pa"))),
            ],
            axis=1,
        ),
        ("pb", "pa"),
        scatter_dimension=0,
        tiled=True,
    )
    half_width = block_both.shape[1] // 2
    block_q = block_both[:, :half_width]
    block_p = block_both[:, half_width:]
    parts_q = split_rows(block_q)
    parts_p = split_rows(block_p)
    summed = tuple(
        (jnp.stack([first_part, second_part]) for first_part, second_part in zip(parts_q, parts_p))
    )
    return (
        question_out,
        passage_out,
        question_loss,
        question_grad,
        passage_grad,
        summed[0],
        summed[1],
        summed[2],
        summed[3],
        summed[4],
        summed[5],
    )


def solution(mesh):
    in_specs = (
        P(("pb", "pa"), None, None),
        P(("pb", "pa"), None, None),
        P(("pb", "pa")),
        P(("pb", "pa")),
        P("pb"),
        P(("pb", "pa"), None, None),
        P(("pb", "pa"), None, None),
        P(None, ("pb", "pa"), None),
        P(None, ("pb", "pa"), None),
        P(None, ("pb", "pa"), None),
        P(None, ("pb", "pa"), None),
        P(None, None, ("pb", "pa")),
        P(None, ("pb", "pa")),
    )
    out_specs = (
        P(("pb", "pa"), None, None),
        P(("pb", "pa"), None, None),
        P(("pb", "pa")),
        P(("pb", "pa"), None, None),
        P(("pb", "pa"), None, None),
        P(None, ("pb", "pa"), None),
        P(None, ("pb", "pa"), None),
        P(None, ("pb", "pa"), None),
        P(None, ("pb", "pa"), None),
        P(None, None, ("pb", "pa")),
        P(None, ("pb", "pa")),
    )
    return jax.shard_map(
        per_device, mesh=mesh, in_specs=in_specs, out_specs=out_specs, check_vma=False
    )
```

profile of v0, /device:TPU:0, one launch (start us, length us, event | category | flops | bytes accessed | tf_op | source)
XLA Modules:
  0.0 1551.4 jit_solution(14005218799001369578)
XLA Ops:
  12.8 43.5 %all-gather.2 = bf16[32,96,2]{1,2,0:T(2,128)(2,1)S(1)} all-gather(bf16[1,96,2]{1,2,0:T(2,128)(2,1)} %bitcast.326), channel_id=1, replica_groups=mesh['pb'=4,'pa'=8] {'pb','pa'}, dimensions={0}, use_global_device_ids=true | all-gather | bytes 12672 | tf_op jit(solution)/shard_map/all_gather | solution.py:257
  60.4 40.1 %all_gather.31 = bf16[2,8,768]{1,0,2:T(2,128)(2,1)S(1)} all-gather(bf16[2,8,24]{1,0,2:T(2,128)(2,1)S(1)} %copy.202), channel_id=1, replica_groups=mesh['pb'=4,'pa'=8] {'pb','pa'}, dimensions={2}, use_global_device_ids=true | all-gather | bytes 25344 | tf_op jit(solution)/shard_map/all_gather | solution.py:256
  102.2 3.1 copy_convert_fusion
  107.0 40.4 %fusion.178 = (f32[768]{0:T(1024)}, f32[768]{0:T(1024)}, f32[768]{0:T(1024)S(1)}, f32[768]{0:T(1024)S(1)}, f32[768]{0:T(1024)S(1)}, /*index=5*/f32[768]{0:T(1024...) fusion(bf16[2,8,768]{1,0,2:T(2,128)(2,1)S(1)} %all_gather.31), kind=kLoop, calls=%fused_computation.309 | loop fusion | flops 12288 | bytes 73728 | tf_op jit(solution)/shard_map/convert_element_type | solution.py:21
  147.4 4.0 fusion.108
  156.3 2.9 copy.232
  159.2 3.8 reshape.689
  165.4 2.9 fusion.292
  174.4 3.6 convert_element_type.451
  178.0 4.3 fusion.110
  187.6 2.9 reshape.634
  190.5 3.3 fusion.114
  196.1 2.9 reshape.633
  201.3 3.1 reshape.632
  204.4 2.8 fusion.297
  230.5 82.6 %all-gather.12.cloned.1.call-done = bf16[2,768,3072]{2,1,0:T(8,128)(2,1)} async-done(((bf16[2,24,3072]{2,1,0:T(8,128)(2,1)}), bf16[2,768,3072]{2,1,0:T(8,128)(2,1)}) %all-gather.12.cloned.1.call-update) | async-done | bytes 9437200 | tf_op jit(solution)/shard_map/all_gather | solution.py:254
  313.2 22.0 %fusion.294 = (f32[512]{0:T(512)S(1)}, f32[512,768]{1,0:T(8,128)S(1)}) fusion(f32[768]{0:T(1024)S(1)} %get-tuple-element.77, bf16[2,3072,768]{2,1,0:T(8,128)(2,1)} %all-gather.14.cloned.1.call-done, bf16[2,768,3072]{2,1,0:T(8,128)(2,1)} %all-gather.12.cloned.1.call-done, f32[3072]{0:T(1024)S(1)} %bitcast.320, f32[512,768]{1,0:T(8,128)} %copy-done.51, ...), kind=kOutput, calls=%fused_computation.494 | convolution fusion | flops 4940365312 | bytes 14198784 | tf_op jit(solution)/shard_map/dot_general | solution.py:64
  335.5 22.5 %fusion.299 = (f32[512]{0:T(512)S(1)}, f32[512,768]{1,0:T(8,128)}) fusion(f32[768]{0:T(1024)S(1)} %get-tuple-element.69, bf16[2,3072,768]{2,1,0:T(8,128)(2,1)} %all-gather.14.cloned.1.call-done, bf16[2,768,3072]{2,1,0:T(8,128)(2,1)} %all-gather.12.cloned.1.call-done, f32[3072]{0:T(1024)S(1)} %bitcast.323, f32[512,768]{1,0:T(8,128)S(1)} %copy-done.50, ...), kind=kOutput, calls=%fused_computation.497 | convolution fusion | flops 4940365312 | bytes 14198784 | tf_op jit(solution)/shard_map/dot_general | solution.py:64
  361.8 8.2 all-gather.1
  371.2 13.9 all-gather
  385.2 15.4 pmax.7
  400.7 14.1 all-reduce.2
  415.8 15.0 all-reduce
  431.0 20.7 %multiply_convert_fusion.1 = (bf16[512,3072]{1,0:T(8,128)(2,1)S(1)}, f32[512,3072]{1,0:T(8,128)}, f32[512,3072]{1,0:T(8,128)}) fusion(f32[3072]{0:T(1024)S(1)} %bitcast.324, bf16[2,768,3072]{2,1,0:T(8,128)(2,1)} %all-gather.12.cloned.1.call-done, f32[512,768]{1,0:T(8,128)} %copy-done.24, f32[512]{0:T(512)S(1)} %fusion.210, f32[512]{0:T(512)S(1)} %copy-done.81, ...), kind=kOutput, calls=%fused_computation.17 | convolution fusion | flops 2521694208 | bytes 22042624 | tf_op jit(solution)/shard_map/dot_general | solution.py:62
  451.7 5.1 fusion.306
  458.7 5.2 fusion.310
  463.9 9.0 convert_reduce_fusion
  472.9 7.3 fusion.278
  480.3 4.1 multiply_reduce_fusion.4
  484.6 20.4 %multiply_convert_fusion.2 = (bf16[512,3072]{1,0:T(8,128)(2,1)S(1)}, f32[512,3072]{1,0:T(8,128)}, f32[512,3072]{1,0:T(8,128)}) fusion(f32[3072]{0:T(1024)S(1)} %bitcast.321, bf16[2,768,3072]{2,1,0:T(8,128)(2,1)} %all-gather.12.cloned.1.call-done, f32[512,768]{1,0:T(8,128)S(1)} %copy-done.21, f32[512]{0:T(512)S(1)} %copy-done.94, f32[512]{0:T(512)S(1)} %copy-done.79, ...), kind=kOutput, calls=%fused_computation.32 | convolution fusion | flops 2521694208 | bytes 22042624 | tf_op jit(solution)/shard_map/dot_general | solution.py:62
  504.9 7.3 fusion.304
  512.2 11.7 reshape.656
  533.4 9.7 convert_reduce_fusion.1
  543.1 3.1 multiply_reduce_fusion.7
  552.1 3.9 reshape.690
  556.1 3.5 multiply_reduce_fusion.1
  571.2 2.8 reshape.645
  574.0 5.0 multiply_reduce_fusion
  588.5 5.6 fusion.281
  594.1 5.1 fusion.308
  617.9 4.8 convolution_bitcast_fusion.1
  622.7 8.0 copy.260
  630.7 11.6 reshape.650
  646.7 6.8 convolution_bitcast_fusion
  657.9 71.8 %concatenate.15 = f32[768,18456]{1,0:T(8,128)} concatenate(f32[768,2304]{1,0:T(8,128)} %copy.260, f32[768,768]{1,0:T(8,128)S(1)} %copy-done.12, f32[768,3072]{1,0:T(8,128)} %fusion.281, f32[768,3072]{1,0:T(8,128)} %reshape.650, f32[768,8]{1,0:T(8,128)S(1)} %bitcast.305, f32[768,4]{1,0:T(8,128)S(1)} %copy-done.54, f32[768,2304]{1,0:T(8,128)} %convolution_bitcast_fusion, ...), dimensions={1} | concatenate | bytes 113393664 | tf_op jit(solution)/shard_map/concatenate | solution.py:317
  731.2 7.0 add_add_fusion.10
  738.2 5.4 add_add_fusion.8
  743.6 790.4 %all-reduce.5.cloned.1.call-done = f32[768,18456]{1,0:T(8,128)} async-done(((f32[768,18456]{1,0:T(8,128)}), f32[768,18456]{1,0:T(8,128)}) %all-reduce.5.cloned.1.call-update) | async-done | bytes 56696848
  (439 shorter events, 142.4 us)
Async XLA Ops:
  7.2 98.2 %copy-start.60 = (bf16[8,64,768]{2,1,0:T(8,128)(2,1)S(1)}, bf16[8,64,768]{2,1,0:T(8,128)(2,1)}, u32[]{:S(2)}) copy-start(bf16[8,64,768]{2,1,0:T(8,128)(2,1)} %param.22) | copy-start | bytes 2359300
  7.2 140.2 %all-gather.8.cloned.1.call-start = ((), (), s32[]{:S(2)}) async-start(), calls=%async_computation.1 | async-start | bytes 7299072 | tf_op jit(solution)/shard_map/all_gather | solution.py:252
  7.9 210.7 %all-gather.10.cloned.1.call-start = ((), (), s32[]{:S(2)}) async-start(), calls=%async_computation.2 | async-start | bytes 2433024 | tf_op jit(solution)/shard_map/all_gather | solution.py:253
  8.7 221.9 %all-gather.14.cloned.1.call-start = ((), (), s32[]{:S(2)}) async-start(), calls=%async_computation.4 | async-start | bytes 9732096 | tf_op jit(solution)/shard_map/all_gather | solution.py:255
  9.4 303.8 %all-gather.12.cloned.1.call-start = ((), (), s32[]{:S(2)}) async-start(), calls=%async_computation.3 | async-start | bytes 9732096 | tf_op jit(solution)/shard_map/all_gather | solution.py:254
  10.0 520.5 %reduce-scatter.2.cloned.1.call-start = ((), (), s32[]{:S(2)}) async-start(), calls=%async_computation.5 | async-start | bytes 110592 | tf_op jit(solution)/shard_map/reduce_scatter | solution.py:291
  107.0 206.2 %copy-start.86 = (f32[1,3072]{1,0:T(1,128)}, f32[1,3072]{1,0:T(1,128)S(1)}, u32[]{:S(2)}) copy-start(f32[1,3072]{1,0:T(1,128)S(1)} %get-tuple-element.126) | copy-start | bytes 36868
  107.0 40.4 %copy-start.64 = (bf16[8,64,768]{2,1,0:T(8,128)(2,1)S(1)}, bf16[8,64,768]{2,1,0:T(8,128)(2,1)}, u32[]{:S(2)}) copy-start(bf16[8,64,768]{2,1,0:T(8,128)(2,1)} %param.17) | copy-start | bytes 2359300
  147.4 165.8 %copy-start.82 = (f32[768]{0:T(1024)}, f32[768]{0:T(1024)S(1)}, u32[]{:S(2)}) copy-start(f32[768]{0:T(1024)S(1)} %get-tuple-element.79) | copy-start | bytes 9220
  147.4 165.8 %copy-start.99 = (f32[768]{0:T(1024)}, f32[768]{0:T(1024)S(1)}, u32[]{:S(2)}) copy-start(f32[768]{0:T(1024)S(1)} %get-tuple-element.78) | copy-start | bytes 9220
  147.4 165.8 %copy-start.101 = (f32[768]{0:T(1024)}, f32[768]{0:T(1024)S(1)}, u32[]{:S(2)}) copy-start(f32[768]{0:T(1024)S(1)} %get-tuple-element.77) | copy-start | bytes 9220
  168.3 46.8 %copy-start.1 = (f32[8,12,64,64]{2,3,1,0:T(8,128)}, f32[8,12,64,64]{2,3,1,0:T(8,128)S(1)}, u32[]{:S(2)}) copy-start(f32[8,12,64,64]{2,3,1,0:T(8,128)S(1)} %get-tuple-element.133) | copy-start | bytes 4718596
  218.6 8.4 copy-start.40
  313.2 22.3 %copy-start.50 = (f32[512,768]{1,0:T(8,128)S(1)}, f32[512,768]{1,0:T(8,128)}, u32[]{:S(2)}) copy-start(f32[512,768]{1,0:T(8,128)} %copy-done.49) | copy-start | bytes 4718596
  335.5 24.4 %copy-start.71 = (f32[768]{0:T(1024)S(1)}, f32[768]{0:T(1024)}, u32[]{:S(2)}) copy-start(f32[768]{0:T(1024)} %get-tuple-element.67) | copy-start | bytes 9220
  335.5 24.4 %copy-start.73 = (f32[1,2,2,128]{3,1,2,0:T(2,128)S(1)}, f32[1,2,2,128]{3,1,2,0:T(2,128)}, u32[]{:S(2)}) copy-start(f32[1,2,2,128]{3,1,2,0:T(2,128)} %copy.289) | copy-start | bytes 6148
  335.5 24.4 %copy-start.85 = (f32[768]{0:T(1024)S(1)}, f32[768]{0:T(1024)}, u32[]{:S(2)}) copy-start(f32[768]{0:T(1024)} %get-tuple-element.68) | copy-start | bytes 9220
  358.0 11.9 copy-start.70
  358.0 11.9 copy-start.72
  358.0 11.9 copy-start.84
  358.0 42.6 %copy-start.97 = (s32[64]{0:T(128)S(1)}, s32[64]{0:T(128)}, u32[]{:S(2)}) copy-start(s32[64]{0:T(128)} %get-tuple-element.107) | copy-start | bytes 772
  358.0 42.6 %copy-start.98 = (pred[64]{0:T(512)(128)(4,1)S(1)}, pred[64]{0:T(512)(128)(4,1)}, u32[]{:S(2)}) copy-start(pred[64]{0:T(512)(128)(4,1)} %fusion.213) | copy-start | bytes 196
  358.1 72.8 %copy-start.6 = (f32[2,256,768]{2,0,1:T(2,128)S(1)}, f32[2,256,768]{2,0,1:T(2,128)}, u32[]{:S(2)}) copy-start(f32[2,256,768]{2,0,1:T(2,128)} %copy_convert_fusion) | copy-start | bytes 4718596
  361.7 8.2 copy-start.58
  361.7 69.2 %copy-start.81 = (f32[512]{0:T(512)S(1)}, f32[512]{0:T(512)}, u32[]{:S(2)}) copy-start(f32[512]{0:T(512)} %copy-done.80) | copy-start | bytes 6148
  400.6 51.0 %copy-start.88 = (f32[64]{0:T(128)}, f32[64]{0:T(128)S(1)}, u32[]{:S(2)}) copy-start(f32[64]{0:T(128)S(1)} %pmax.7) | copy-start | bytes 772
  414.8 36.9 %copy-start.95 = (f32[64]{0:T(128)}, f32[64]{0:T(128)S(1)}, u32[]{:S(2)}) copy-start(f32[64]{0:T(128)S(1)} %get-tuple-element.86) | copy-start | bytes 772
  431.0 20.7 %copy-start.25 = (f32[512,768]{1,0:T(8,128)S(1)}, f32[512,768]{1,0:T(8,128)}, u32[]{:S(2)}) copy-start(f32[512,768]{1,0:T(8,128)} %copy-done.24) | copy-start | bytes 4718596
  458.7 21.5 %slice-start.2 = ((s8[9437184]{0:T(1024)(128)(4,1)}), s8[4194304]{0:T(1024)(128)(4,1)S(1)}, s32[]{:S(2)}) async-start(s8[9437184]{0:T(1024)(128)(4,1)} %bitcast.327), calls=%async_computation.9 | async-start | bytes 8388608
  463.9 16.3 %slice-start.3 = ((s8[9437184]{0:T(1024)(128)(4,1)}), s8[4194304]{0:T(1024)(128)(4,1)S(1)}, s32[]{:S(2)}) async-start(s8[9437184]{0:T(1024)(128)(4,1)} %bitcast.327), calls=%async_computation.10 | async-start | bytes 8388608
  463.9 16.3 %slice-start.4 = ((s8[9437184]{0:T(1024)(128)(4,1)}), s8[1048576]{0:T(1024)(128)(4,1)S(1)}, s32[]{:S(2)}) async-start(s8[9437184]{0:T(1024)(128)(4,1)} %bitcast.327), calls=%async_computation.11 | async-start | bytes 2097152
  472.9 7.3 copy-start.113
  484.5 20.5 %copy-start.102 = (f32[768]{0:T(1024)S(1)}, f32[768]{0:T(1024)}, u32[]{:S(2)}) copy-start(f32[768]{0:T(1024)} %copy-done.101) | copy-start | bytes 9220
  484.5 1049.5 %all-reduce.5.cloned.1.call-start = ((), (), s32[]{:S(2)}) async-start(), calls=%async_computation.6 | async-start | bytes 114032640
  504.9 7.3 copy-start.109
  512.2 14.1 copy-start.67
  532.4 10.7 slice-start.5
  533.3 9.7 copy-start.61
  533.3 9.7 copy-start.22
  533.3 9.7 slice-start.6
  533.4 9.7 slice-start.7
  548.4 7.7 copy-start.90
  571.2 7.8 slice-start
  630.7 11.8 copy-start.5
  630.7 11.8 copy-start.69
  646.7 11.2 copy-start.12
  646.7 11.2 copy-start.53
  646.7 11.2 copy-start.54
  (83 other events, 255.7 us)
Sparse Core Ops, SparseCore 0:
  11.2 75.0 all-gather.7
  89.4 56.9 all-gather.9
  149.6 80.3 all-gather.13
  233.1 80.0 all-gather.11
  484.6 26.8 reduce-scatter.1
  729.9 803.9 all-reduce.4
where the time goes:
time: 1560 us; the launch traced here: 1550 us
  waiting for transfers between devices  876 us (56%)
  matrix products  223 us (14%)
  local copies, waits for them, and re-layouts  208 us (13%)
  blocking collectives  150 us (10%)
  other arithmetic  77.6 us (5%)
  between operations  16.7 us (1%)
    unnamed x7, waiting for transfers between devices  793 us
    all_gather x1, waiting for transfers between devices, per_device(): lax.all_gather(w_expand, ('pb', 'pa'), axis=1, tiled=True)  82.6 us
    concatenate x1, local copies, waits for them, and re-layouts, per_device(): jnp.concatenate([gradient_rows(kept_q, share_rows * lax.axis_size(('pb',...  71.8 us
    dot_general x4, matrix products, dense_part(): jnp.dot(active, w_reduce, preferred_element_type=jnp.float32) + vectors[5]  56.8 us
    all_gather x1, blocking collectives, per_device(): lax.all_gather(b_expand, ('pb', 'pa'), axis=1, tiled=True)  43.5 us
    dot_general x2, matrix products, dense_part(): jnp.dot(mid_low, w_expand, preferred_element_type=jnp.float32) + b_expand  41.1 us
    convert_element_type x1, other arithmetic, layer_norm(): return centred * lax.rsqrt(spread + norm_eps) * norm_gain + norm_shift  40.4 us
    all_gather x1, blocking collectives, per_device(): lax.all_gather(vectors, ('pb', 'pa'), axis=2, tiled=True)  40.1 us
  transfers between devices with their start and end apart: 6, of which 2 were waited for; matrix products, arithmetic and copies ran while one was open for 12% of the time, Pallas kernels for 0%

commit v1 on v0

v1 whole, which is shorter than its diff:
```python
import functools

import jax
import jax.numpy as jnp
from jax import lax
from jax.experimental import pallas as pl
from jax.experimental.pallas import tpu as pltpu
from jax.sharding import PartitionSpec as P

D = 768
HEADS = 12
HDIM = 64
FF = 3072
AXES = ("pb", "pa")
BLOCK = 256

norm_eps = 1e-06
masked_score = -1000000000.0
score_scale = 0.0625
loss_weight = 16.0
head_scale = HDIM ** (-0.5)
F32 = jnp.float32
BF16 = jnp.bfloat16
VMEM_LIMIT = 56 * 1024 * 1024


def bits_of(count):
    return [1 << shift for shift in range(count.bit_length() - 1)]


class Places:
    def __init__(self, mesh):
        self.pb_n = mesh.shape["pb"]
        self.pa_n = mesh.shape["pa"]
        self.nz = self.pa_n // 2
        self.half = self.nz // 2
        self.chips = self.pb_n * self.nz
        pb_bits = bits_of(self.pb_n)
        turn = len(pb_bits) // 2
        low_z = [("z", bit) for bit in bits_of(self.half)]
        first = [("pb", bit) for bit in pb_bits]
        second = first[turn:] + first[:turn]
        self.orders = ([("z", self.half)] + low_z + first, [("z", self.half)] + low_z + second)
        self.steps = len(self.orders[0])

    def chip_mask(self, move):
        axis, bit = move
        return bit * self.nz if axis == "pb" else bit

    def stack_masks(self, core):
        masks = [0]
        for move in self.orders[core]:
            masks = masks + [mask ^ self.chip_mask(move) for mask in masks]
        return masks

    def pairs(self, step):
        out = []
        for pb in range(self.pb_n):
            for pa in range(self.pa_n):
                axis, bit = self.orders[pa % 2][step]
                to_pb, to_pa = (pb ^ bit, pa) if axis == "pb" else (pb, pa ^ (2 * bit))
                out.append((pb * self.pa_n + pa, to_pb * self.pa_n + to_pa))
        return out

    def swap(self, values, step):
        return lax.ppermute(values, AXES, self.pairs(step))

    def swap_core(self, values):
        return lax.ppermute(values, "pa", [(i, i ^ 1) for i in range(self.pa_n)])

    def swap_tower(self, values):
        return lax.ppermute(values, "pa", [(i, i ^ (2 * self.half)) for i in range(self.pa_n)])


def dot(left, right, dims=((1,), (0,))):
    return lax.dot_general(left, right, (dims, ((), ())), preferred_element_type=F32)


def assemble_kernel(segments, rows, idx_ref, *refs):
    count = len(segments)
    sources, outs = refs[:4], refs[4 : 4 + count]
    buffer, in_sem, out_sem = refs[4 + count :]
    core = idx_ref[1, 0]
    part = sources[0].shape[0]
    loads = [
        pltpu.make_async_copy(source, buffer.at[pl.ds(k * part, part)], in_sem.at[k])
        for k, source in enumerate(sources)
    ]
    for load in loads:
        load.start()
    stores = []
    for k in range(4):
        loads[k].wait()
        half = core if k < 2 else 1 - core
        for j in range(part):
            slot = k * part + j
            place = idx_ref[0, slot]
            for s, (start, width, both) in enumerate(segments):
                if both and k >= 2:
                    continue
                column = 0 if both else pl.multiple_of(half * width, 128)
                store = pltpu.make_async_copy(
                    buffer.at[slot, :, pl.ds(start, width)],
                    outs[s].at[place, :, pl.ds(column, width)],
                    out_sem.at[s, slot],
                )
                store.start()
                stores.append(store)
    for store in stores:
        store.wait()


def assemble(parts, table, segments):
    part, rows, width = parts[0].shape
    chips = 2 * part
    shapes = [
        jax.ShapeDtypeStruct((chips, rows, w if both else 2 * w), BF16) for _, w, both in segments
    ]
    return pl.pallas_call(
        functools.partial(assemble_kernel, segments, rows),
        out_shape=shapes,
        in_specs=[pl.BlockSpec(memory_space=pltpu.SMEM)] + [pl.BlockSpec(memory_space=pl.ANY)] * 4,
        out_specs=[pl.BlockSpec(memory_space=pl.ANY)] * len(segments),
        scratch_shapes=[
            pltpu.VMEM((2 * chips, rows, width), BF16),
            pltpu.SemaphoreType.DMA((4,)),
            pltpu.SemaphoreType.DMA((len(segments), 2 * chips)),
        ],
        compiler_params=pltpu.CompilerParams(vmem_limit_bytes=VMEM_LIMIT),
        cost_estimate=pl.CostEstimate(
            flops=0, bytes_accessed=4 * 2 * chips * rows * width, transcendentals=0
        ),
        name="assemble",
    )(table, *parts)


def assemble_plain(parts, table, segments, core):
    own = jnp.concatenate(parts[:2], axis=0)
    other = jnp.concatenate(parts[2:], axis=0)
    chips, rows, width = own.shape
    own_order = jnp.argsort(table[0, :chips])
    other_order = jnp.argsort(table[0, chips:])
    own = jnp.take(own, own_order, axis=0)
    other = jnp.take(other, other_order, axis=0)
    left = jnp.where(core == 0, own, other)
    right = jnp.where(core == 0, other, own)
    outs = []
    for start, w, both in segments:
        if both:
            outs.append(left[:, :, start : start + w])
        else:
            outs.append(
                jnp.concatenate(
                    [left[:, :, start : start + w], right[:, :, start : start + w]], axis=2
                )
            )
    return outs


def fold_kernel(widths, idx_ref, core_ref, *refs):
    count = len(widths)
    ins, (keep_ref, send_ref) = refs[: 4 * count], refs[4 * count :]
    column = 0
    for s, width in enumerate(widths):
        mine, got, theirs, also = ins[4 * s : 4 * s + 4]
        keep_ref[:, :, column : column + width] = mine[...] + got[...].astype(F32)
        send_ref[:, :, column : column + width] = (theirs[...] + also[...].astype(F32)).astype(BF16)
        column += width


def fold(fulls, received, idx, core):
    chips, rows = received[0].shape[:2]
    steps = chips // 2
    widths = [r.shape[2] for r in received]
    in_specs, operands = [], []
    for full, got in zip(fulls, received):
        width = got.shape[2]
        wide = full.shape[2] != width
        for offset in (0, steps):
            in_specs.append(
                pl.BlockSpec(
                    (1, rows, width),
                    lambda i, idx, core, o=offset, w=wide: (idx[i + o], 0, core[0] if w else 0),
                )
            )
            in_specs.append(
                pl.BlockSpec((1, rows, width), lambda i, idx, core, o=offset: (idx[i + o], 0, 0))
            )
            operands += [full, got]
    total = sum(widths)
    return pl.pallas_call(
        functools.partial(fold_kernel, widths),
        grid_spec=pltpu.PrefetchScalarGridSpec(
            num_scalar_prefetch=2,
            grid=(steps,),
            in_specs=in_specs,
            out_specs=[
                pl.BlockSpec((1, rows, total), lambda i, idx, core: (i, 0, 0)),
                pl.BlockSpec((1, rows, total), lambda i, idx, core: (i, 0, 0)),
            ],
        ),
        out_shape=[
            jax.ShapeDtypeStruct((steps, rows, total), F32),
            jax.ShapeDtypeStruct((steps, rows, total), BF16),
        ],
        compiler_params=pltpu.CompilerParams(vmem_limit_bytes=VMEM_LIMIT),
        cost_estimate=pl.CostEstimate(
            flops=0, bytes_accessed=chips * rows * total * 9, transcendentals=0
        ),
        name="fold",
    )(idx, core, *operands)


def attention_kernel(qkv_ref, qid_ref, kid_ref, context_ref, probs_ref):
    allowed = qid_ref[...] == kid_ref[0]
    lane = lax.broadcasted_iota(jnp.int32, (BLOCK, 128), 1)
    zero = jnp.zeros((BLOCK, 128), BF16)
    for pair in range(HEADS // 2):
        queries = qkv_ref[:, pair * 128 : pair * 128 + 128]
        keys = qkv_ref[:, D + pair * 128 : D + pair * 128 + 128]
        values = qkv_ref[:, 2 * D + pair * 128 : 2 * D + pair * 128 + 128]
        outs = []
        for side in range(2):
            mine = (lane < HDIM) if side == 0 else (lane >= HDIM)
            scores = dot(queries, jnp.where(mine, keys, zero), ((1,), (1,))) * head_scale
            scores = jnp.where(allowed, scores, masked_score)
            top = jnp.max(scores, axis=1, keepdims=True)
            grown = jnp.exp(scores - top)
            total = jnp.sum(grown, axis=1, keepdims=True)
            probs = (grown * (1.0 / total)).astype(BF16)
            probs_ref[0, 2 * pair + side] = probs
            outs.append(dot(probs, values))
        context_ref[:, pair * 128 : pair * 128 + 128] = jnp.where(
            lane < HDIM, outs[0], outs[1]
        ).astype(BF16)


def attention(qkv, qid, kid):
    rows = qkv.shape[0]
    blocks = rows // BLOCK
    return pl.pallas_call(
        attention_kernel,
        grid=(blocks,),
        in_specs=[
            pl.BlockSpec((BLOCK, 3 * D), lambda i: (i, 0)),
            pl.BlockSpec((BLOCK, 1), lambda i: (i, 0)),
            pl.BlockSpec((1, 1, BLOCK), lambda i: (i, 0, 0)),
        ],
        out_specs=[
            pl.BlockSpec((BLOCK, D), lambda i: (i, 0)),
            pl.BlockSpec((1, HEADS, BLOCK, BLOCK), lambda i: (i, 0, 0, 0)),
        ],
        out_shape=[
            jax.ShapeDtypeStruct((rows, D), BF16),
            jax.ShapeDtypeStruct((blocks, HEADS, BLOCK, BLOCK), BF16),
        ],
        compiler_params=pltpu.CompilerParams(vmem_limit_bytes=VMEM_LIMIT),
        cost_estimate=pl.CostEstimate(
            flops=4 * rows * BLOCK * D * 2,
            bytes_accessed=rows * (4 * D + HEADS * BLOCK) * 2,
            transcendentals=rows * HEADS * BLOCK,
        ),
        name="attention",
    )(qkv, qid, kid)


def attention_back_kernel(qkv_ref, probs_ref, grad_ref, out_ref):
    lane = lax.broadcasted_iota(jnp.int32, (BLOCK, 128), 1)
    zero = jnp.zeros((BLOCK, 128), BF16)
    for pair in range(HEADS // 2):
        cols = slice(pair * 128, pair * 128 + 128)
        queries = qkv_ref[:, pair * 128 : pair * 128 + 128]
        keys = qkv_ref[:, D + pair * 128 : D + pair * 128 + 128]
        values = qkv_ref[:, 2 * D + pair * 128 : 2 * D + pair * 128 + 128]
        grad = grad_ref[:, cols]
        d_q, d_k, d_v = [], [], []
        for side in range(2):
            mine = (lane < HDIM) if side == 0 else (lane >= HDIM)
            low = probs_ref[0, 2 * pair + side]
            d_probs = dot(jnp.where(mine, grad, zero), values, ((1,), (1,)))
            d_v.append(dot(low, grad, ((0,), (0,))))
            probs = low.astype(F32)
            row_dot = jnp.sum(d_probs * probs, axis=1, keepdims=True)
            d_scores = (probs * (d_probs - row_dot)).astype(BF16)
            d_q.append(dot(d_scores, keys))
            d_k.append(dot(d_scores, queries, ((0,), (0,))))
        first = lane < HDIM
        out_ref[:, pair * 128 : pair * 128 + 128] = (
            jnp.where(first, d_q[0], d_q[1]) * head_scale
        ).astype(BF16)
        out_ref[:, D + pair * 128 : D + pair * 128 + 128] = (
            jnp.where(first, d_k[0], d_k[1]) * head_scale
        ).astype(BF16)
        out_ref[:, 2 * D + pair * 128 : 2 * D + pair * 128 + 128] = jnp.where(
            first, d_v[0], d_v[1]
        ).astype(BF16)


def attention_back(qkv, probs, grad_context):
    rows = qkv.shape[0]
    blocks = rows // BLOCK
    return pl.pallas_call(
        attention_back_kernel,
        grid=(blocks,),
        in_specs=[
            pl.BlockSpec((BLOCK, 3 * D), lambda i: (i, 0)),
            pl.BlockSpec((1, HEADS, BLOCK, BLOCK), lambda i: (i, 0, 0, 0)),
            pl.BlockSpec((BLOCK, D), lambda i: (i, 0)),
        ],
        out_specs=pl.BlockSpec((BLOCK, 3 * D), lambda i: (i, 0)),
        out_shape=jax.ShapeDtypeStruct((rows, 3 * D), BF16),
        compiler_params=pltpu.CompilerParams(vmem_limit_bytes=VMEM_LIMIT),
        cost_estimate=pl.CostEstimate(
            flops=8 * rows * BLOCK * D * 2,
            bytes_accessed=rows * (7 * D + HEADS * BLOCK) * 2,
            transcendentals=0,
        ),
        name="attention_back",
    )(qkv, probs, grad_context)


def expand_kernel(mid_ref, w_ref, b_ref, active_ref, slope_ref):
    expanded = dot(mid_ref[...], w_ref[...]) + b_ref[...]
    phi = 0.5 + 0.5 * lax.erf(expanded * 0.7071067811865476)
    density = jnp.exp(expanded * expanded * -0.5) * 0.3989422804014327
    active_ref[...] = (expanded * phi).astype(BF16)
    slope_ref[...] = (phi + expanded * density).astype(BF16)


def expand(mid_low, w_expand, b_expand):
    rows = mid_low.shape[0]
    tile_r, tile_f = 256, 1024
    return pl.pallas_call(
        expand_kernel,
        grid=(FF // tile_f, rows // tile_r),
        in_specs=[
            pl.BlockSpec((tile_r, D), lambda j, i: (i, 0)),
            pl.BlockSpec((D, tile_f), lambda j, i: (0, j)),
            pl.BlockSpec((1, tile_f), lambda j, i: (0, j)),
        ],
        out_specs=[
            pl.BlockSpec((tile_r, tile_f), lambda j, i: (i, j)),
            pl.BlockSpec((tile_r, tile_f), lambda j, i: (i, j)),
        ],
        out_shape=[jax.ShapeDtypeStruct((rows, FF), BF16)] * 2,
        compiler_params=pltpu.CompilerParams(vmem_limit_bytes=VMEM_LIMIT),
        cost_estimate=pl.CostEstimate(
            flops=2 * rows * D * FF,
            bytes_accessed=2 * (rows * D + D * FF + 2 * rows * FF),
            transcendentals=2 * rows * FF,
        ),
        name="expand",
    )(mid_low, w_expand, b_expand)


def normalized(values):
    centred = values - jnp.mean(values, axis=-1, keepdims=True)
    spread = jnp.mean(centred * centred, axis=-1, keepdims=True)
    inverse = lax.rsqrt(spread + norm_eps)
    return centred * inverse, inverse


def norm_back(grad, gain, norm, inverse):
    scaled = grad * gain
    return inverse * (
        scaled
        - jnp.mean(scaled, axis=-1, keepdims=True)
        - norm * jnp.mean(scaled * norm, axis=-1, keepdims=True)
    )


def column_halves(values, core):
    width = values.shape[-1] // 2
    left, right = values[..., :width], values[..., width:]
    return jnp.where(core == 0, left, right), jnp.where(core == 0, right, left)


def per_device(places, *args):
    (
        question_in,
        passage_in,
        question_len,
        passage_len,
        positive,
        question_cot,
        passage_cot,
        w_joined,
        w_output,
        w_expand,
        w_reduce,
        vectors,
        b_expand,
    ) = args
    pb, pa = lax.axis_index("pb"), lax.axis_index("pa")
    z, core = pa // 2, pa % 2
    tower = z // places.half
    is_q = tower == 0
    chip = pb * places.nz + z
    masks = jnp.array([places.stack_masks(0), places.stack_masks(1)], jnp.int32)
    order = lax.dynamic_index_in_dim(masks, core, 0, keepdims=False) ^ chip
    other_order = lax.dynamic_index_in_dim(masks, 1 - core, 0, keepdims=False) ^ chip
    table = jnp.stack(
        [jnp.concatenate([order, other_order]), jnp.full((2 * places.chips,), core, jnp.int32)]
    ).astype(jnp.int32)
    core_arr = jnp.full((1,), core, jnp.int32)
    share = w_joined.shape[1]

    def start(own_half, other_half):
        got = places.swap_core(other_half)
        return jnp.concatenate(
            [jnp.where(core == 0, own_half, got), jnp.where(core == 0, got, own_half)], axis=1
        )

    small = jnp.concatenate(
        [
            vectors.transpose(0, 2, 1),
            b_expand.reshape(2, share, 4),
            jnp.zeros((2, share, 116), BF16),
        ],
        axis=2,
    )
    j_own, j_other = column_halves(w_joined, core)
    o_own, o_other = column_halves(w_output, core)
    e_own, e_other = column_halves(w_expand, core)
    r_own, r_other = column_halves(w_reduce, core)
    first = start(
        jnp.concatenate([j_own, o_own, small], axis=2),
        jnp.concatenate([j_other, o_other, small], axis=2),
    )
    second = start(e_own, e_other)
    third = start(r_own, r_other)

    def gather(piece):
        mine = lax.dynamic_index_in_dim(piece, tower, 0, keepdims=True)
        theirs = lax.dynamic_index_in_dim(piece, 1 - tower, 0, keepdims=True)
        stack = jnp.concatenate([mine, places.swap(theirs, 0)], axis=0)
        for step in range(1, places.steps - 1):
            stack = jnp.concatenate([stack, places.swap(stack, step)], axis=0)
        last = places.swap(stack, places.steps - 1)
        return [stack, last, places.swap_core(stack), places.swap_core(last)]

    def weights(piece, segments):
        parts = gather(piece)
        if parts[0].shape[1] % 8 == 0:
            return assemble(parts, table, segments)
        return assemble_plain(parts, table, segments, core)

    jw, ow = w_joined.shape[2] // 2, D // 2
    full_j, full_o, full_small = weights(
        first, [(0, jw, False), (jw, ow, False), (jw + ow, 128, True)]
    )
    (full_e,) = weights(second, [(0, FF // 2, False)])
    (full_r,) = weights(third, [(0, D // 2, False)])
    wj = full_j.reshape(D, 3 * D)
    wo = full_o.reshape(D, D)
    we = full_e.reshape(D, FF)
    wr = full_r.reshape(FF, D)
    small = full_small.reshape(D, 128).astype(F32)
    vec = small[:, :8].T
    bias_e = small[:, 8:12].reshape(1, FF)

    rows_q = question_in.reshape(-1, D)
    rows_p = passage_in.reshape(-1, D)
    own_rows = rows_q.shape[0]

    def exchange(q_side, p_side):
        mine = jnp.where(is_q, q_side, p_side)
        theirs = jnp.where(is_q, p_side, q_side)
        return jnp.concatenate([mine, places.swap_tower(theirs)], axis=0)

    def give_back(both):
        mine, theirs = both[:own_rows], places.swap_tower(both[own_rows:])
        return jnp.where(is_q, mine, theirs), jnp.where(is_q, theirs, mine)

    lq, lp = question_in.shape[1], passage_in.shape[1]
    valid_q = (jnp.arange(lq, dtype=jnp.int32)[None, :] < question_len[:, None]).astype(jnp.int32)
    valid_p = (jnp.arange(lp, dtype=jnp.int32)[None, :] < passage_len[:, None]).astype(jnp.int32)
    valid = exchange(valid_q.reshape(-1), valid_p.reshape(-1))
    tokens = exchange(rows_q, rows_p)
    cot = exchange(question_cot.reshape(-1, D), passage_cot.reshape(-1, D))
    rows = tokens.shape[0]
    row_ids = jnp.arange(rows, dtype=jnp.int32)
    seq = jnp.where(is_q, row_ids // lq, row_ids // lp)
    qid = seq.reshape(rows, 1)
    kid = jnp.where(valid > 0, seq, -1).reshape(rows // BLOCK, 1, BLOCK)
    row_mask = valid.reshape(rows, 1).astype(F32)

    bias_j = jnp.concatenate([vec[0], jnp.zeros((D,), F32), vec[1]])
    qkv = (dot(tokens, wj) + bias_j).astype(BF16)
    context, probs = attention(qkv, qid, kid)
    attended = dot(context, wo) + vec[2]
    norm_one, inverse_one = normalized(tokens.astype(F32) + attended)
    mid = norm_one * vec[3] + vec[4]
    mid_low = mid.astype(BF16)
    active, slope = expand(mid_low, we, bias_e)
    norm_two, inverse_two = normalized(mid + dot(active, wr) + vec[5])
    out = ((norm_two * vec[6] + vec[7]) * row_mask).astype(BF16)

    per_q = rows // lq
    every = lp // lq
    per_p = rows // lp
    slots = out.reshape(per_q, lq, D)[:, 0, :]
    others = places.swap_tower(slots)
    cls_q = jnp.where(is_q, slots, others)
    cls_p = jnp.where(is_q, others, slots)[::every]
    pad = (-(per_q + per_p)) % 8
    stack = jnp.concatenate([cls_q, cls_p, jnp.zeros((pad, D), BF16)], axis=0)[None]
    pair_masks = [0]
    for bit in bits_of(places.half):
        got = lax.ppermute(stack, "pa", [(i, i ^ (2 * bit)) for i in range(places.pa_n)])
        stack = jnp.concatenate([stack, got], axis=0)
        pair_masks = pair_masks + [m ^ (2 * bit) for m in pair_masks]
    for bit in bits_of(places.pb_n):
        got = lax.ppermute(stack, "pb", [(i, i ^ bit) for i in range(places.pb_n)])
        stack = jnp.concatenate([stack, got], axis=0)
        pair_masks = pair_masks + [m ^ (bit * places.pa_n) for m in pair_masks]
    stack = jnp.concatenate([stack, places.swap_core(stack)], axis=0)
    pair_masks = pair_masks + [m ^ 1 for m in pair_masks]
    groups = len(pair_masks)
    me = pb * places.pa_n + (pa % (2 * places.half))
    place = jnp.array(pair_masks, jnp.int32) ^ me
    shift = 2 * places.half
    dev_q = jnp.stack([place, place + shift], axis=1)
    dev_p = jnp.stack([place + shift, place], axis=1)
    nq, np_ = question_in.shape[0], passage_in.shape[0]
    q_ids = (dev_q[:, :, None] * nq + jnp.arange(nq, dtype=jnp.int32)).reshape(-1)
    p_ids = (dev_p[:, :, None] * np_ + jnp.arange(np_, dtype=jnp.int32)).reshape(-1)
    wanted = positive
    pos_masks = [0]
    for bit in bits_of(places.pb_n):
        got = lax.ppermute(wanted, "pb", [(i, i ^ bit) for i in range(places.pb_n)])
        wanted = jnp.concatenate([wanted, got])
        pos_masks = pos_masks + [m ^ bit for m in pos_masks]
    per_pb = positive.shape[0]
    slot_of_pb = jnp.zeros((places.pb_n,), jnp.int32)
    slot_of_pb = slot_of_pb.at[jnp.array(pos_masks, jnp.int32) ^ pb].set(
        jnp.arange(places.pb_n, dtype=jnp.int32)
    )
    wanted = jnp.take(wanted, slot_of_pb[q_ids // per_pb] * per_pb + q_ids % per_pb)

    all_q = stack[:, :per_q].reshape(groups * per_q, D)
    all_p = stack[:, per_q : per_q + per_p].reshape(groups * per_p, D)
    similarity = dot(all_q, all_p, ((1,), (1,))) * score_scale
    hot = (wanted[:, None] == p_ids[None, :]).astype(F32)
    top = jnp.max(similarity, axis=1, keepdims=True)
    grown = jnp.exp(similarity - top)
    total = jnp.sum(grown, axis=1, keepdims=True)
    own_sim = similarity[:per_q]
    loss = top[:per_q, 0] + jnp.log(total[:per_q, 0]) - jnp.sum(own_sim * hot[:per_q], axis=1)
    question_loss = lax.dynamic_slice_in_dim(loss, tower * nq, nq)
    d_sim = (loss_weight * (grown / total - hot)).astype(BF16)
    d_q = dot(d_sim[:per_q], all_p) * score_scale
    d_p = dot(d_sim[:, :per_p], all_q, ((0,), (0,))) * score_scale
    d_p = jnp.concatenate(
        [d_p.reshape(per_p, 1, D), jnp.zeros((per_p, every - 1, D), F32)], axis=1
    ).reshape(per_q, D)
    d_slot = jnp.where(is_q, d_q, d_p)

    d_out = cot.astype(F32).reshape(per_q, lq, D)
    at_slot = jnp.arange(lq, dtype=jnp.int32)[None, :, None] == 0
    d_out = d_out + jnp.where(at_slot, d_slot[:, None, :], 0.0)
    d_out = d_out.reshape(rows, D) * row_mask
    d_second = norm_back(d_out, vec[6], norm_two, inverse_two)
    g_gain_two = jnp.sum(d_out * norm_two, axis=0)
    g_shift_two = jnp.sum(d_out, axis=0)
    d_reduced = d_second.astype(BF16)
    g_bias_reduce = jnp.sum(d_reduced.astype(F32), axis=0)

    def as_pieces(values):
        return values.reshape(places.chips, values.shape[0] // places.chips, values.shape[1])

    def other_half(full):
        width = full.shape[2] // 2
        return lax.dynamic_slice_in_dim(full, (1 - core) * width, width, axis=2).astype(BF16)

    def scatter(fulls):
        fulls = [as_pieces(full) for full in fulls]
        received = [
            places.swap_core(full.astype(BF16) if full.shape[2] == 128 else other_half(full))
            for full in fulls
        ]
        keep, send = fold(fulls, received, order, core_arr)
        for step in range(places.steps - 1, 0, -1):
            got = places.swap(send, step)
            both = keep.shape[0] // 2
            if step > 1:
                send = (keep[both:] + got[both:].astype(F32)).astype(BF16)
                keep = keep[:both] + got[:both].astype(F32)
            else:
                total = keep + got.astype(F32)
                keep, send = total[0:1], total[1:2].astype(BF16)
        got = places.swap(send, 0)
        mine = keep.astype(BF16)
        towers = jnp.where(
            is_q, jnp.concatenate([mine, got], axis=0), jnp.concatenate([got, mine], axis=0)
        )
        count = towers.shape[1] // 2
        keep_rows = lax.dynamic_slice_in_dim(towers, core * count, count, axis=1)
        send_rows = lax.dynamic_slice_in_dim(towers, (1 - core) * count, count, axis=1)
        got_rows = places.swap_core(send_rows)
        outs, column = [], 0
        for full in fulls:
            if full.shape[2] == 128:
                outs.append(keep_rows[:, :, column : column + 128].astype(F32))
                column += 128
                continue
            width = full.shape[2] // 2
            mine = keep_rows[:, :, column : column + width]
            theirs = got_rows[:, :, column : column + width]
            outs.append(
                jnp.concatenate(
                    [jnp.where(core == 0, mine, theirs), jnp.where(core == 0, theirs, mine)],
                    axis=2,
                ).astype(F32)
            )
            column += width
        return outs

    (grad_reduce,) = scatter([dot(active, d_reduced, ((0,), (0,)))])
    d_active = dot(d_reduced, wr, ((1,), (1,)))
    d_expanded = (d_active * slope.astype(F32)).astype(BF16)
    g_bias_expand = jnp.sum(d_expanded.astype(F32), axis=0)
    (grad_expand,) = scatter([dot(mid_low, d_expanded, ((0,), (0,)))])
    d_mid = d_second + dot(d_expanded, we, ((1,), (1,)))
    d_first = norm_back(d_mid, vec[3], norm_one, inverse_one)
    g_gain_one = jnp.sum(d_mid * norm_one, axis=0)
    g_shift_one = jnp.sum(d_mid, axis=0)
    d_attended = d_first.astype(BF16)
    g_bias_output = jnp.sum(d_attended.astype(F32), axis=0)
    (grad_output,) = scatter([dot(context, d_attended, ((0,), (0,)))])
    d_context = dot(d_attended, wo, ((1,), (1,))).astype(BF16)
    d_joined = attention_back(qkv, probs, d_context)
    d_tokens = d_first + dot(d_joined, wj, ((1,), (1,)))
    g_joined_bias = jnp.sum(d_joined.astype(F32), axis=0)
    g_vec = jnp.stack(
        [
            g_joined_bias[:D],
            g_joined_bias[2 * D :],
            g_bias_output,
            g_gain_one,
            g_shift_one,
            g_bias_reduce,
            g_gain_two,
            g_shift_two,
        ]
    )
    g_small = jnp.concatenate(
        [g_vec.T, g_bias_expand.reshape(D, 4), jnp.zeros((D, 116), F32)], axis=1
    )
    grad_joined, grad_small = scatter([dot(tokens, d_joined, ((0,), (0,))), g_small])
    grad_vectors = grad_small[:, :, :8].transpose(0, 2, 1)
    grad_b_expand = grad_small[:, :, 8:12].reshape(2, 4 * share)

    out_q, out_p = give_back(out)
    grad_q, grad_p = give_back(d_tokens.astype(BF16))
    return (
        out_q.reshape(question_in.shape),
        out_p.reshape(passage_in.shape),
        question_loss,
        grad_q.astype(F32).reshape(question_in.shape),
        grad_p.astype(F32).reshape(passage_in.shape),
        grad_joined,
        grad_output,
        grad_expand,
        grad_reduce,
        grad_vectors,
        grad_b_expand,
    )


def solution(mesh):
    in_specs = (
        P(("pb", "pa"), None, None),
        P(("pb", "pa"), None, None),
        P(("pb", "pa")),
        P(("pb", "pa")),
        P("pb"),
        P(("pb", "pa"), None, None),
        P(("pb", "pa"), None, None),
        P(None, ("pb", "pa"), None),
        P(None, ("pb", "pa"), None),
        P(None, ("pb", "pa"), None),
        P(None, ("pb", "pa"), None),
        P(None, None, ("pb", "pa")),
        P(None, ("pb", "pa")),
    )
    out_specs = (
        P(("pb", "pa"), None, None),
        P(("pb", "pa"), None, None),
        P(("pb", "pa")),
        P(("pb", "pa"), None, None),
        P(("pb", "pa"), None, None),
        P(None, ("pb", "pa"), None),
        P(None, ("pb", "pa"), None),
        P(None, ("pb", "pa"), None),
        P(None, ("pb", "pa"), None),
        P(None, None, ("pb", "pa")),
        P(None, ("pb", "pa")),
    )
    return jax.shard_map(
        functools.partial(per_device, Places(mesh)),
        mesh=mesh,
        in_specs=in_specs,
        out_specs=out_specs,
        check_vma=False,
    )
```

time: 1560 us -> 495 us (0.32)
  waiting for transfers between devices: 876 us -> 181 us
  local copies, waits for them, and re-layouts: 208 us -> 39.3 us
  matrix products: 223 us -> 70.5 us
  blocking collectives: 150 us -> 0 us
  Pallas kernels: 0 us -> 90.2 us
  starting transfers between devices: 0.23 us -> 46.5 us
  other arithmetic: 77.6 us -> 59 us
    unnamed x7 -> x0, waiting for transfers between devices: 793 us -> none
    ppermute x0 -> x58, waiting for transfers between devices: none -> 181 us  [the longest x28 95.2 us: swap(): return lax.ppermute(values, AXES, self.pairs(step))]
    dot_general x45 -> x14, matrix products: 223 us -> 70.5 us  [dot(): lax.dot_general(left, right, (dims, ((), ())), preferred_element_type=F32)]
    all_gather x4 -> x0, blocking collectives: 106 us -> none  [the longest x1 43.5 us: per_device(): lax.all_gather(b_expand, ('pb', 'pa'), axis=1, tiled=True)]
    pallas_call x0 -> x10, Pallas kernels: none -> 90.2 us  [the longest x4 29 us: fold(): pl.pallas_call(functools.partial(fold_kernel, widths), grid_spec=pltpu.Pr...]
    all_gather x4 -> x0, waiting for transfers between devices: 82.7 us -> none  [the longest x1 82.6 us: per_device(): lax.all_gather(w_expand, ('pb', 'pa'), axis=1, tiled=True)]
    concatenate x3 -> x8, local copies, waits for them, and re-layouts: 72.9 us -> 1.91 us  [the longest x2 1.03 us: per_device(): jnp.concatenate([g_vec.T, g_bias_expand.reshape(D, 4), jnp.zeros((D, 116)...]
    reshape x24 -> x5, local copies, waits for them, and re-layouts: 60.6 us -> 3.84 us  [the longest x1 1.56 us: per_device(): all_p = stack[:, per_q:per_q + per_p].reshape(groups * per_p, D)]
  transfers between devices with their start and end apart: 6 -> 58, of which waited for: 2 -> 27; matrix products, arithmetic and copies ran while one was open for 12% -> 32% of each run, Pallas kernels for 0% -> 18%
where the time goes in v1:
time: 495 us; the launch traced here: 489 us
  waiting for transfers between devices  181 us (37%)
  Pallas kernels  90.2 us (18%)
  matrix products  70.5 us (14%)
  other arithmetic  59 us (12%)
  starting transfers between devices  46.5 us (9%)
  local copies, waits for them, and re-layouts  39.3 us (8%)
    ppermute x28, waiting for transfers between devices, swap(): return lax.ppermute(values, AXES, self.pairs(step))  95.2 us
    dot_general x14, matrix products, dot(): lax.dot_general(left, right, (dims, ((), ())), preferred_element_type=F32)  70.5 us
    ppermute x6, waiting for transfers between devices, swap_tower(): lax.ppermute(values, 'pa', [(i, i ^ 2 * self.half) for i in range(self.pa...  52.4 us
    pallas_call x4, Pallas kernels, fold(): pl.pallas_call(functools.partial(fold_kernel, widths), grid_spec=pltpu.Pr...  29 us
    ppermute x28, starting transfers between devices, swap(): return lax.ppermute(values, AXES, self.pairs(step))  28.1 us
    ppermute x2, waiting for transfers between devices, per_device(): got = lax.ppermute(wanted, 'pb', [(i, i ^ bit) for i in range(places.pb_n)])  23.7 us
    pallas_call x1, Pallas kernels, attention_back(): pl.pallas_call(attention_back_kernel, grid=(blocks,), in_specs=[pl.BlockS...  18 us
    pallas_call x1, Pallas kernels, expand(): pl.pallas_call(expand_kernel, grid=(FF // tile_f, rows // tile_r), in_spe...  17.2 us
  transfers between devices with their start and end apart: 58, of which 27 were waited for; matrix products, arithmetic and copies ran while one was open for 32% of the time, Pallas kernels for 18%

profile of v1, /device:TPU:0, one launch (start us, length us, event | category | flops | bytes accessed | tf_op | source)
XLA Modules:
  0.0 489.0 jit_solution(7349884853073135371)
XLA Ops:
  17.2 2.7 collective-permute-start.2
  19.9 11.5 %collective-permute-done.10 = bf16[1,48,1536]{2,1,0:T(8,128)(2,1)S(1)} collective-permute-done((bf16[1,48,1536]{2,1,0:T(8,128)(2,1)S(1)}, bf16[1,48,1536]{2,1,0:T(8,128)(2,1)S(1)}, u32[]{:S(2)}, u32[]{:S(2)}) %collective-permute-start.10) | collective-permute-done | bytes 147488 | tf_op jit(solution)/shard_map/ppermute | solution.py:66
  31.5 5.8 %collective-permute-done.2 = bf16[1,48,1664]{2,1,0:T(8,128)(2,1)S(1)} collective-permute-done((bf16[1,48,1664]{2,1,0:T(8,128)(2,1)S(1)}, bf16[1,48,1664]{2,1,0:T(8,128)(2,1)S(1)}, u32[]{:S(2)}, u32[]{:S(2)}) %collective-permute-start.2) | collective-permute-done | bytes 159776 | tf_op jit(solution)/shard_map/ppermute | solution.py:66
  39.5 4.1 collective-permute-done.11
  44.2 6.2 %collective-permute-done.3 = bf16[2,48,1664]{2,1,0:T(8,128)(2,1)S(1)} collective-permute-done((bf16[2,48,1664]{2,1,0:T(8,128)(2,1)S(1)}, bf16[2,48,1664]{2,1,0:T(8,128)(2,1)S(1)}, u32[]{:S(2)}, u32[]{:S(2)}) %collective-permute-start.3) | collective-permute-done | bytes 319520 | tf_op jit(solution)/shard_map/ppermute | solution.py:66
  52.5 4.1 collective-permute-done.18
  57.3 3.2 compare_select_fusion.1
  65.2 6.2 %collective-permute-done.19 = bf16[4,192,384]{2,1,0:T(8,128)(2,1)S(1)} collective-permute-done((bf16[4,192,384]{2,1,0:T(8,128)(2,1)S(1)}, bf16[4,192,384]{2,1,0:T(8,128)(2,1)S(1)}, u32[]{:S(2)}, u32[]{:S(2)}) %collective-permute-start.19) | collective-permute-done | bytes 589856 | tf_op jit(solution)/shard_map/ppermute | solution.py:66
  82.8 23.7 %collective-permute-done.30 = s32[128]{0:T(128)S(1)} collective-permute-done((s32[128]{0:T(128)S(1)}, s32[128]{0:T(128)S(1)}, u32[]{:S(2)}, u32[]{:S(2)}) %collective-permute-start.30) | collective-permute-done | bytes 544 | tf_op jit(solution)/shard_map/ppermute | solution.py:531
  107.9 3.0 collective-permute-done.8
  123.2 3.1 gather_fusion
  126.9 4.8 assemble.4
  133.2 4.8 assemble.5
  138.0 5.7 %assemble.3 = (bf16[16,48,2304]{2,1,0:T(8,128)(2,1)}, bf16[16,48,768]{2,1,0:T(8,128)(2,1)}, bf16[16,48,128]{2,1,0:T(8,128)(2,1)}) custom-call(s32[2,32]{1,0:T(2,128)} %stack.48.idx_ref, bf16[8,48,1664]{2,1,0:T(8,128)(2,1)} %copy-done.11, bf16[8,48,1664]{2,1,0:T(8,128)(2,1)} %collective-permute-done.5.refs_1_, ...), custom_call_target="tpu_custom_call" | custom-call | bytes 10223616 | tf_op jit(solution)/shard_map/assemble/pallas_call | solution.py:119
  145.6 31.4 %collective-permute-done = bf16[512,768]{1,0:T(8,128)(2,1)} collective-permute-done((bf16[512,768]{1,0:T(8,128)(2,1)}, bf16[512,768]{1,0:T(8,128)(2,1)}, u32[]{:S(2)}, u32[]{:S(2)}) %collective-permute-start) | collective-permute-done | bytes 786464 | tf_op jit(solution)/shard_map/ppermute | solution.py:72
  177.0 8.3 %add_convert_fusion.qkv_ref = bf16[1024,2304]{1,0:T(8,128)(2,1)} fusion(bf16[768,2304]{1,0:T(8,128)(2,1)} %bitcast.157, f32[2304]{0:T(1024)S(1)} %pad_maximum_fusion.16, bf16[512,768]{1,0:T(8,128)(2,1)} %collective-permute-done, bf16[512,768]{1,0:T(8,128)(2,1)S(1)} %copy-done.25), kind=kOutput, calls=%fused_computation.5 | convolution fusion | flops 3631742976 | bytes 9839616 | tf_op jit(solution)/shard_map/dot_general | solution.py:76
  185.3 10.8 %attention.1 = (bf16[1024,768]{1,0:T(8,128)(2,1)}, bf16[4,12,256,256]{3,2,1,0:T(8,128)(2,1)}) custom-call(bf16[1024,2304]{1,0:T(8,128)(2,1)} %add_convert_fusion.qkv_ref, s32[1024,1]{1,0:T(8,128)} %fusion.14.qid_ref, s32[4,1,256]{2,1,0:T(1,128)} %compare_select_fusion.kid_ref), custom_call_target="tpu_custom_call" | custom-call | flops 1610612736 | bytes 12582912 | tf_op jit(solution)/shard_map/attention/pallas_call | solution.py:241
  196.1 3.1 fusion.68
  204.0 17.2 %expand.1 = (bf16[1024,3072]{1,0:T(8,128)(2,1)}, bf16[1024,3072]{1,0:T(8,128)(2,1)}) custom-call(bf16[1024,768]{1,0:T(8,128)(2,1)} %fusion.5.mid_ref, bf16[768,3072]{1,0:T(8,128)(2,1)} %bitcast.131, f32[1,3072]{1,0:T(1,128)} %reshape.732.b_ref), custom_call_target="tpu_custom_call" | custom-call | flops 4831838208 | bytes 18874368 | tf_op jit(solution)/shard_map/expand/pallas_call | solution.py:333
  221.3 9.0 %fusion.69 = (f32[1024]{0:T(1024)S(1)}, f32[1024,768]{1,0:T(8,128)S(1)}) fusion(f32[768]{0:T(1024)S(1)} %copy-done.47, bf16[1024,3072]{1,0:T(8,128)(2,1)} %get-tuple-element.30, bf16[3072,768]{1,0:T(8,128)(2,1)} %bitcast.135, f32[768]{0:T(1024)S(1)} %copy-done.37, f32[768]{0:T(1024)S(1)} %get-tuple-element.75, f32[1024]{0:T(1024)S(1)} %copy-done.33, ...), kind=kOutput, calls=%fused_computation.275 | convolution fusion | flops 4837342208 | bytes 17323008 | tf_op jit(solution)/shard_map/dot_general | solution.py:76
  233.2 4.6 collective-permute-done.24
  238.7 3.2 collective-permute-done.25
  248.1 3.5 collective-permute-done.27
  260.5 4.2 multiply_reduce_fusion
  264.8 3.7 convert_reduce_fusion.2
  268.5 8.8 %convert_reduce_fusion = (f32[3072]{0:T(1024)S(1)}, bf16[1024,3072]{1,0:T(8,128)(2,1)S(1)}) fusion(bf16[1024,3072]{1,0:T(8,128)(2,1)} %get-tuple-element.31, bf16[3072,768]{1,0:T(8,128)(2,1)} %bitcast.136, f32[1024,768]{1,0:T(8,128)S(1)} %get-tuple-element.82), kind=kOutput, calls=%fused_computation.2 | convolution fusion | flops 4848350208 | bytes 20459520 | tf_op jit(solution)/shard_map/dot_general | solution.py:76
  277.4 6.1 %multiply_reduce_fusion.1 = (f32[768]{0:T(1024)S(1)}, f32[1024]{0:T(1024)S(1)}, f32[1024]{0:T(1024)S(1)}, f32[768]{0:T(1024)S(1)}, f32[1024,768]{1,0:T(8,128)S(1)}) fusion(f32[1024,768]{1,0:T(8,128)S(1)} %copy-done.3, f32[1024]{0:T(1024)S(1)} %copy-done.34, f32[1024]{0:T(1024)S(1)} %broadcast_multiply_fusion.5, f32[768]{0:T(1024)S(1)} %copy-done.32, ...), kind=kOutput, calls=%fused_computation.13 | convolution fusion | flops 4839698432 | bytes 20472832 | tf_op jit(solution)/shard_map/dot_general | solution.py:76
  289.1 7.6 %fusion.71 = f32[768,3072]{1,0:T(8,128)} fusion(bf16[1024,768]{1,0:T(8,128)(2,1)S(1)} %copy-done.17, bf16[1024,3072]{1,0:T(8,128)(2,1)S(1)} %bitcast.162), kind=kOutput, calls=%fused_computation.277 | convolution fusion | flops 4831838208 | bytes 17301504 | tf_op jit(solution)/shard_map/dot_general | solution.py:76
  296.7 7.8 %fusion.57 = f32[3072,768]{1,0:T(8,128)} fusion(bf16[1024,3072]{1,0:T(8,128)(2,1)S(1)} %bitcast.164, f32[1024,768]{1,0:T(8,128)S(1)} %get-tuple-element.82), kind=kOutput, calls=%fused_computation.264 | convolution fusion | flops 4832624640 | bytes 18874368 | tf_op jit(solution)/shard_map/dot_general | solution.py:76
  304.6 18.0 %attention_back.1 = bf16[1024,2304]{1,0:T(8,128)(2,1)} custom-call(bf16[1024,2304]{1,0:T(8,128)(2,1)} %add_convert_fusion.qkv_ref, bf16[4,12,256,256]{3,2,1,0:T(8,128)(2,1)} %get-tuple-element.32.probs_ref, bf16[1024,768]{1,0:T(8,128)(2,1)} %convolution_convert_fusion.grad_ref), custom_call_target="tpu_custom_call" | custom-call | flops 3221225472 | bytes 17301504 | tf_op jit(solution)/shard_map/attention_back/pallas_call | solution.py:302
  322.6 7.4 %add_convert_fusion.1 = bf16[1024,768]{1,0:T(8,128)(2,1)S(1)} fusion(f32[1024,768]{1,0:T(8,128)S(1)} %get-tuple-element.84, bf16[1024,2304]{1,0:T(8,128)(2,1)} %attention_back.1, bf16[768,2304]{1,0:T(8,128)(2,1)} %bitcast.158), kind=kOutput, calls=%fused_computation.15 | convolution fusion | flops 3625451520 | bytes 12976128 | tf_op jit(solution)/shard_map/dot_general | solution.py:76
  330.0 5.7 %fusion.23 = f32[768,2304]{1,0:T(8,128)S(1)} fusion(bf16[1024,2304]{1,0:T(8,128)(2,1)S(1)} %copy-done.4, bf16[512,768]{1,0:T(8,128)(2,1)} %collective-permute-done, bf16[512,768]{1,0:T(8,128)(2,1)S(1)} %copy-done.27), kind=kOutput, calls=%fused_computation.93 | convolution fusion | flops 3627024384 | bytes 13369344 | tf_op jit(solution)/shard_map/dot_general | solution.py:76
  335.8 2.9 copy-done
  343.7 4.1 dynamic-slice_convert_fusion.1
  349.0 6.0 %fold.5 = (f32[8,48,384]{2,1,0:T(8,128)}, bf16[8,48,384]{2,1,0:T(8,128)(2,1)}) custom-call(s32[16]{0:T(128)} %copy-done.39, s32[1]{0:T(128)} %bitcast.36.core_ref, f32[16,48,768]{2,1,0:T(8,128)} %bitcast.128, bf16[16,48,384]{2,1,0:T(8,128)(2,1)} %copy-done.13, f32[16,48,768]{2,1,0:T(8,128)} %bitcast.129, bf16[16,48,384]{2,1,0:T(8,128)(2,1)} %copy-done.13), custom_call_target="tpu_custom_call" | custom-call | bytes 2654208 | tf_op jit(solution)/shard_map/fold/pallas_call | solution.py:191
  357.2 4.8 collective-permute-done.41
  363.6 4.1 dynamic-slice_convert_fusion
  367.8 2.8 collective-permute-start.32
  370.6 7.4 %fold.4 = (f32[8,48,1280]{2,1,0:T(8,128)}, bf16[8,48,1280]{2,1,0:T(8,128)(2,1)}) custom-call(s32[16]{0:T(128)} %copy-done.39, s32[1]{0:T(128)} %bitcast.36.core_ref, f32[16,48,2304]{2,1,0:T(8,128)} %bitcast.125, bf16[16,48,1152]{2,1,0:T(8,128)(2,1)} %collective-permute-done.33.refs_1_.refs_3_, f32[16,48,2304]{2,1,0:T(8,128)} %bitcast.126, ...), custom_call_target="tpu_custom_call" | custom-call | bytes 8847360 | tf_op jit(solution)/shard_map/fold/pallas_call | solution.py:191
  382.1 6.3 %collective-permute-done.43 = bf16[2,48,384]{2,1,0:T(8,128)(2,1)S(1)} collective-permute-done((bf16[2,48,384]{2,1,0:T(8,128)(2,1)S(1)}, bf16[2,48,384]{2,1,0:T(8,128)(2,1)S(1)}, u32[]{:S(2)}, u32[]{:S(2)}) %collective-permute-start.43) | collective-permute-done | bytes 73760 | tf_op jit(solution)/shard_map/ppermute | solution.py:66
  393.1 13.4 %collective-permute-done.32 = bf16[512,768]{1,0:T(8,128)(2,1)} collective-permute-done((bf16[512,768]{1,0:T(8,128)(2,1)}, bf16[512,768]{1,0:T(8,128)(2,1)}, u32[]{:S(2)}, u32[]{:S(2)}) %collective-permute-start.32) | collective-permute-done | bytes 786464 | tf_op jit(solution)/shard_map/ppermute | solution.py:72
  411.9 7.7 %fold.6 = (f32[8,48,1536]{2,1,0:T(8,128)}, bf16[8,48,1536]{2,1,0:T(8,128)(2,1)}) custom-call(s32[16]{0:T(128)} %copy-done.39, s32[1]{0:T(128)} %bitcast.36.core_ref, f32[16,48,3072]{2,1,0:T(8,128)} %bitcast.122, bf16[16,48,1536]{2,1,0:T(8,128)(2,1)} %copy-done.6, f32[16,48,3072]{2,1,0:T(8,128)} %bitcast.123, bf16[16,48,1536]{2,1,0:T(8,128)(2,1)} %copy-done.6), custom_call_target="tpu_custom_call" | custom-call | bytes 10616832 | tf_op jit(solution)/shard_map/fold/pallas_call | solution.py:191
  422.4 8.0 %fold.7 = (f32[8,192,384]{2,1,0:T(8,128)}, bf16[8,192,384]{2,1,0:T(8,128)(2,1)}) custom-call(s32[16]{0:T(128)} %copy-done.39, s32[1]{0:T(128)} %bitcast.36.core_ref, f32[16,192,768]{2,1,0:T(8,128)} %bitcast.119, bf16[16,192,384]{2,1,0:T(8,128)(2,1)} %copy-done.7, f32[16,192,768]{2,1,0:T(8,128)} %bitcast.120, bf16[16,192,384]{2,1,0:T(8,128)(2,1)} %copy-done.7), custom_call_target="tpu_custom_call" | custom-call | bytes 10616832 | tf_op jit(solution)/shard_map/fold/pallas_call | solution.py:191
  437.8 17.2 %collective-permute-done.53 = bf16[8,192,384]{2,1,0:T(8,128)(2,1)S(1)} collective-permute-done((bf16[8,192,384]{2,1,0:T(8,128)(2,1)}, bf16[8,192,384]{2,1,0:T(8,128)(2,1)S(1)}, u32[]{:S(2)}, u32[]{:S(2)}) %collective-permute-start.53) | collective-permute-done | bytes 1179680 | tf_op jit(solution)/shard_map/ppermute | solution.py:66
  460.4 5.8 %collective-permute-done.54 = bf16[4,192,384]{2,1,0:T(8,128)(2,1)S(1)} collective-permute-done((bf16[4,192,384]{2,1,0:T(8,128)(2,1)}, bf16[4,192,384]{2,1,0:T(8,128)(2,1)S(1)}, u32[]{:S(2)}, u32[]{:S(2)}) %collective-permute-start.54) | collective-permute-done | bytes 589856 | tf_op jit(solution)/shard_map/ppermute | solution.py:66
  466.5 2.9 collective-permute-done.49
  471.2 6.2 %collective-permute-done.55 = bf16[2,192,384]{2,1,0:T(8,128)(2,1)S(1)} collective-permute-done((bf16[2,192,384]{2,1,0:T(8,128)(2,1)S(1)}, bf16[2,192,384]{2,1,0:T(8,128)(2,1)S(1)}, u32[]{:S(2)}, u32[]{:S(2)}) %collective-permute-start.55) | collective-permute-done | bytes 294944 | tf_op jit(solution)/shard_map/ppermute | solution.py:66
  479.8 6.5 %collective-permute-done.56 = bf16[1,192,384]{2,1,0:T(8,128)(2,1)S(1)} collective-permute-done((bf16[1,192,384]{2,1,0:T(8,128)(2,1)S(1)}, bf16[1,192,384]{2,1,0:T(8,128)(2,1)S(1)}, u32[]{:S(2)}, u32[]{:S(2)}) %collective-permute-start.56) | collective-permute-done | bytes 147488 | tf_op jit(solution)/shard_map/ppermute | solution.py:66
  (410 shorter events, 131.5 us)
Async XLA Ops:
  4.1 13.0 %collective-permute-start.1 = (bf16[2,24,1664]{2,1,0:T(8,128)(2,1)S(1)}, bf16[2,24,1664]{2,1,0:T(8,128)(2,1)S(1)}, u32[]{:S(2)}, u32[]{:S(2)}) collective-permute-start(bf16[2,24,1664]{2,1,0:T(8,128)(2,1)S(1)} %concatenate.170), channel_id=1, source_target_pairs={{0,1},{1,0},{2,3},{3,2},{4,5},{5,4},{6,7},{7,6},{8,9},{9,8},{10,11... | collective-permute-start | bytes 479240 | tf_op jit(solution)/shard_map/ppermute | solution.py:69
  5.7 7.2 %collective-permute-start.9 = (bf16[2,24,1536]{2,1,0:T(8,128)(2,1)S(1)}, bf16[2,24,1536]{2,1,0:T(8,128)(2,1)S(1)}, u32[]{:S(2)}, u32[]{:S(2)}) collective-permute-start(bf16[2,24,1536]{2,1,0:T(8,128)(2,1)S(1)} %broadcast_select_fusion.16), channel_id=1, source_target_pairs={{0,1},{1,0},{2,3},{3,2},{4,5},{5,4},{6,7},{7,6},{8,9},{9,8},{10,11... | collective-permute-start | bytes 442376 | tf_op jit(solution)/shard_map/ppermute | solution.py:69
  6.8 9.8 %collective-permute-start.16 = (bf16[2,96,384]{2,1,0:T(8,128)(2,1)S(1)}, bf16[2,96,384]{2,1,0:T(8,128)(2,1)S(1)}, u32[]{:S(2)}, u32[]{:S(2)}) collective-permute-start(bf16[2,96,384]{2,1,0:T(8,128)(2,1)S(1)} %broadcast_select_fusion.10), channel_id=1, source_target_pairs={{0,1},{1,0},{2,3},{3,2},{4,5},{5,4},{6,7},{7,6},{8,9},{9,8},{10,11... | collective-permute-start | bytes 442376 | tf_op jit(solution)/shard_map/ppermute | solution.py:69
  7.3 73.8 %collective-permute-start.29 = (s32[64]{0:T(128)}, s32[64]{0:T(128)S(1)}, u32[]{:S(2)}, u32[]{:S(2)}) collective-permute-start(s32[64]{0:T(128)} %param.20), channel_id=1, source_target_pairs={{0,8},{8,0},{16,24},{24,16},{1,9},{9,1},{17,25},{25,17},{2,10},{10... | collective-permute-start | bytes 776 | tf_op jit(solution)/shard_map/ppermute | solution.py:531
  14.0 17.4 %collective-permute-start.10 = (bf16[1,48,1536]{2,1,0:T(8,128)(2,1)S(1)}, bf16[1,48,1536]{2,1,0:T(8,128)(2,1)S(1)}, u32[]{:S(2)}, u32[]{:S(2)}) collective-permute-start(bf16[1,48,1536]{2,1,0:T(8,128)(2,1)S(1)} %get-tuple-element.124), channel_id=1, source_target_pairs={{0,4},{1,5},{2,6},{3,7},{4,0},{5,1},{6,2},{7,3},{8,12},{9,13},{10,... | collective-permute-start | bytes 442376 | tf_op jit(solution)/shard_map/ppermute | solution.py:66
  16.7 21.3 %collective-permute-start.17 = (bf16[1,192,384]{2,1,0:T(8,128)(2,1)S(1)}, bf16[1,192,384]{2,1,0:T(8,128)(2,1)S(1)}, u32[]{:S(2)}, u32[]{:S(2)}) collective-permute-start(bf16[1,192,384]{2,1,0:T(8,128)(2,1)S(1)} %get-tuple-element.122), channel_id=1, source_target_pairs={{0,4},{1,5},{2,6},{3,7},{4,0},{5,1},{6,2},{7,3},{8,12},{9,13},{10,... | collective-permute-start | bytes 442376 | tf_op jit(solution)/shard_map/ppermute | solution.py:66
  17.2 20.0 %collective-permute-start.2 = (bf16[1,48,1664]{2,1,0:T(8,128)(2,1)S(1)}, bf16[1,48,1664]{2,1,0:T(8,128)(2,1)S(1)}, u32[]{:S(2)}, u32[]{:S(2)}) collective-permute-start(bf16[1,48,1664]{2,1,0:T(8,128)(2,1)S(1)} %get-tuple-element.114), channel_id=1, source_target_pairs={{0,4},{1,5},{2,6},{3,7},{4,0},{5,1},{6,2},{7,3},{8,12},{9,13},{10,... | collective-permute-start | bytes 479240 | tf_op jit(solution)/shard_map/ppermute | solution.py:66
  31.4 12.1 %collective-permute-start.11 = (bf16[2,48,1536]{2,1,0:T(8,128)(2,1)S(1)}, bf16[2,48,1536]{2,1,0:T(8,128)(2,1)S(1)}, u32[]{:S(2)}, u32[]{:S(2)}) collective-permute-start(bf16[2,48,1536]{2,1,0:T(8,128)(2,1)S(1)} %pad_maximum_fusion.11), channel_id=1, source_target_pairs={{0,2},{1,3},{2,0},{3,1},{4,6},{5,7},{6,4},{7,5},{8,10},{9,11},{10,... | collective-permute-start | bytes 884744 | tf_op jit(solution)/shard_map/ppermute | solution.py:66
  37.3 13.1 %collective-permute-start.3 = (bf16[2,48,1664]{2,1,0:T(8,128)(2,1)S(1)}, bf16[2,48,1664]{2,1,0:T(8,128)(2,1)S(1)}, u32[]{:S(2)}, u32[]{:S(2)}) collective-permute-start(bf16[2,48,1664]{2,1,0:T(8,128)(2,1)S(1)} %pad_maximum_fusion.10), channel_id=1, source_target_pairs={{0,2},{1,3},{2,0},{3,1},{4,6},{5,7},{6,4},{7,5},{8,10},{9,11},{10,... | collective-permute-start | bytes 958472 | tf_op jit(solution)/shard_map/ppermute | solution.py:66
  38.0 18.6 %collective-permute-start.18 = (bf16[2,192,384]{2,1,0:T(8,128)(2,1)S(1)}, bf16[2,192,384]{2,1,0:T(8,128)(2,1)S(1)}, u32[]{:S(2)}, u32[]{:S(2)}) collective-permute-start(bf16[2,192,384]{2,1,0:T(8,128)(2,1)S(1)} %pad_maximum_fusion.12), channel_id=1, source_target_pairs={{0,2},{1,3},{2,0},{3,1},{4,6},{5,7},{6,4},{7,5},{8,10},{9,11},{10,... | collective-permute-start | bytes 884744 | tf_op jit(solution)/shard_map/ppermute | solution.py:66
  43.6 16.8 %collective-permute-start.12 = (bf16[4,48,1536]{2,1,0:T(8,128)(2,1)S(1)}, bf16[4,48,1536]{2,1,0:T(8,128)(2,1)}, u32[]{:S(2)}, u32[]{:S(2)}) collective-permute-start(bf16[4,48,1536]{2,1,0:T(8,128)(2,1)S(1)} %pad_maximum_fusion.6), channel_id=1, source_target_pairs={{0,8},{1,17},{2,10},{3,19},{4,12},{5,21},{6,14},{7,23},{8,0},{9,25... | collective-permute-start | bytes 1769480 | tf_op jit(solution)/shard_map/ppermute | solution.py:66
  51.3 12.0 %collective-permute-start.4 = (bf16[4,48,1664]{2,1,0:T(8,128)(2,1)}, bf16[4,48,1664]{2,1,0:T(8,128)(2,1)}, u32[]{:S(2)}, u32[]{:S(2)}) collective-permute-start(bf16[4,48,1664]{2,1,0:T(8,128)(2,1)} %pad_maximum_fusion.5), channel_id=1, source_target_pairs={{0,8},{1,17},{2,10},{3,19},{4,12},{5,21},{6,14},{7,23},{8,0},{9,25... | collective-permute-start | bytes 1916936 | tf_op jit(solution)/shard_map/ppermute | solution.py:66
  56.7 14.6 %collective-permute-start.19 = (bf16[4,192,384]{2,1,0:T(8,128)(2,1)S(1)}, bf16[4,192,384]{2,1,0:T(8,128)(2,1)S(1)}, u32[]{:S(2)}, u32[]{:S(2)}) collective-permute-start(bf16[4,192,384]{2,1,0:T(8,128)(2,1)S(1)} %pad_maximum_fusion.7), channel_id=1, source_target_pairs={{0,8},{1,17},{2,10},{3,19},{4,12},{5,21},{6,14},{7,23},{8,0},{9,25... | collective-permute-start | bytes 1769480 | tf_op jit(solution)/shard_map/ppermute | solution.py:66
  61.7 18.4 %collective-permute-start.13 = (bf16[8,48,1536]{2,1,0:T(8,128)(2,1)S(1)}, bf16[8,48,1536]{2,1,0:T(8,128)(2,1)}, u32[]{:S(2)}, u32[]{:S(2)}) collective-permute-start(bf16[8,48,1536]{2,1,0:T(8,128)(2,1)S(1)} %pad_maximum_fusion.3.refs_0_), channel_id=1, source_target_pairs={{0,16},{1,9},{2,18},{3,11},{4,20},{5,13},{6,22},{7,15},{8,24},{9,1... | collective-permute-start | bytes 3538952 | tf_op jit(solution)/shard_map/ppermute | solution.py:66
  63.4 47.6 %collective-permute-start.14 = (bf16[8,48,1536]{2,1,0:T(8,128)(2,1)S(1)}, bf16[8,48,1536]{2,1,0:T(8,128)(2,1)}, u32[]{:S(2)}, u32[]{:S(2)}) collective-permute-start(bf16[8,48,1536]{2,1,0:T(8,128)(2,1)S(1)} %pad_maximum_fusion.3.refs_0_), channel_id=1, source_target_pairs={{0,1},{1,0},{2,3},{3,2},{4,5},{5,4},{6,7},{7,6},{8,9},{9,8},{10,11... | collective-permute-start | bytes 3538952 | tf_op jit(solution)/shard_map/ppermute | solution.py:69
  64.6 46.9 %collective-permute-start.5 = (bf16[8,48,1664]{2,1,0:T(8,128)(2,1)S(1)}, bf16[8,48,1664]{2,1,0:T(8,128)(2,1)}, u32[]{:S(2)}, u32[]{:S(2)}) collective-permute-start(bf16[8,48,1664]{2,1,0:T(8,128)(2,1)S(1)} %pad_maximum_fusion.2.refs_0_), channel_id=1, source_target_pairs={{0,16},{1,9},{2,18},{3,11},{4,20},{5,13},{6,22},{7,15},{8,24},{9,1... | collective-permute-start | bytes 3833864 | tf_op jit(solution)/shard_map/ppermute | solution.py:66
  73.5 38.0 %collective-permute-start.20 = (bf16[8,192,384]{2,1,0:T(8,128)(2,1)}, bf16[8,192,384]{2,1,0:T(8,128)(2,1)}, u32[]{:S(2)}, u32[]{:S(2)}) collective-permute-start(bf16[8,192,384]{2,1,0:T(8,128)(2,1)} %pad_maximum_fusion.4.refs_0_), channel_id=1, source_target_pairs={{0,16},{1,9},{2,18},{3,11},{4,20},{5,13},{6,22},{7,15},{8,24},{9,1... | collective-permute-start | bytes 3538952 | tf_op jit(solution)/shard_map/ppermute | solution.py:66
  80.1 41.6 %collective-permute-start.15 = (bf16[8,48,1536]{2,1,0:T(8,128)(2,1)}, bf16[8,48,1536]{2,1,0:T(8,128)(2,1)}, u32[]{:S(2)}, u32[]{:S(2)}) collective-permute-start(bf16[8,48,1536]{2,1,0:T(8,128)(2,1)} %collective-permute-done.13.refs_1_), channel_id=1, source_target_pairs={{0,1},{1,0},{2,3},{3,2},{4,5},{5,4},{6,7},{7,6},{8,9},{9,8},{10,11... | collective-permute-start | bytes 3538952 | tf_op jit(solution)/shard_map/ppermute | solution.py:69
  81.2 25.2 %collective-permute-start.30 = (s32[128]{0:T(128)S(1)}, s32[128]{0:T(128)S(1)}, u32[]{:S(2)}, u32[]{:S(2)}) collective-permute-start(s32[128]{0:T(128)S(1)} %pad_add_fusion.1), channel_id=1, source_target_pairs={{0,16},{8,24},{16,0},{24,8},{1,17},{9,25},{17,1},{25,9},{2,18},{10... | collective-permute-start | bytes 1544 | tf_op jit(solution)/shard_map/ppermute | solution.py:531
  110.9 20.8 %collective-permute-start.21 = (bf16[8,192,384]{2,1,0:T(8,128)(2,1)}, bf16[8,192,384]{2,1,0:T(8,128)(2,1)}, u32[]{:S(2)}, u32[]{:S(2)}) collective-permute-start(bf16[8,192,384]{2,1,0:T(8,128)(2,1)} %pad_maximum_fusion.4.refs_0_), channel_id=1, source_target_pairs={{0,1},{1,0},{2,3},{3,2},{4,5},{5,4},{6,7},{7,6},{8,9},{9,8},{10,11... | collective-permute-start | bytes 3538952 | tf_op jit(solution)/shard_map/ppermute | solution.py:69
  110.9 27.1 %collective-permute-start.6 = (bf16[8,48,1664]{2,1,0:T(8,128)(2,1)S(1)}, bf16[8,48,1664]{2,1,0:T(8,128)(2,1)}, u32[]{:S(2)}, u32[]{:S(2)}) collective-permute-start(bf16[8,48,1664]{2,1,0:T(8,128)(2,1)S(1)} %pad_maximum_fusion.2.refs_0_), channel_id=1, source_target_pairs={{0,1},{1,0},{2,3},{3,2},{4,5},{5,4},{6,7},{7,6},{8,9},{9,8},{10,11... | collective-permute-start | bytes 3833864 | tf_op jit(solution)/shard_map/ppermute | solution.py:69
  111.4 21.8 %collective-permute-start.22 = (bf16[8,192,384]{2,1,0:T(8,128)(2,1)}, bf16[8,192,384]{2,1,0:T(8,128)(2,1)}, u32[]{:S(2)}, u32[]{:S(2)}) collective-permute-start(bf16[8,192,384]{2,1,0:T(8,128)(2,1)} %collective-permute-done.20.refs_1_), channel_id=1, source_target_pairs={{0,1},{1,0},{2,3},{3,2},{4,5},{5,4},{6,7},{7,6},{8,9},{9,8},{10,11... | collective-permute-start | bytes 3538952 | tf_op jit(solution)/shard_map/ppermute | solution.py:69
  111.5 26.5 %collective-permute-start.7 = (bf16[8,48,1664]{2,1,0:T(8,128)(2,1)}, bf16[8,48,1664]{2,1,0:T(8,128)(2,1)}, u32[]{:S(2)}, u32[]{:S(2)}) collective-permute-start(bf16[8,48,1664]{2,1,0:T(8,128)(2,1)} %collective-permute-done.5.refs_1_), channel_id=1, source_target_pairs={{0,1},{1,0},{2,3},{3,2},{4,5},{5,4},{6,7},{7,6},{8,9},{9,8},{10,11... | collective-permute-start | bytes 3833864 | tf_op jit(solution)/shard_map/ppermute | solution.py:69
  121.7 55.3 %collective-permute-start = (bf16[512,768]{1,0:T(8,128)(2,1)}, bf16[512,768]{1,0:T(8,128)(2,1)}, u32[]{:S(2)}, u32[]{:S(2)}) collective-permute-start(bf16[512,768]{1,0:T(8,128)(2,1)} %get-tuple-element.100), channel_id=1, source_target_pairs={{0,4},{1,5},{2,6},{3,7},{4,0},{5,1},{6,2},{7,3},{8,12},{9,13},{10,... | collective-permute-start | bytes 2359304 | tf_op jit(solution)/shard_map/ppermute | solution.py:72
  131.7 128.8 %collective-permute-start.31 = (bf16[512,768]{1,0:T(8,128)(2,1)}, bf16[512,768]{1,0:T(8,128)(2,1)}, u32[]{:S(2)}, u32[]{:S(2)}) collective-permute-start(bf16[512,768]{1,0:T(8,128)(2,1)} %get-tuple-element.98), channel_id=1, source_target_pairs={{0,4},{1,5},{2,6},{3,7},{4,0},{5,1},{6,2},{7,3},{8,12},{9,13},{10,... | collective-permute-start | bytes 2359304 | tf_op jit(solution)/shard_map/ppermute | solution.py:72
  245.2 134.4 %collective-permute-start.23 = (bf16[512,768]{1,0:T(8,128)(2,1)}, bf16[512,768]{1,0:T(8,128)(2,1)}, u32[]{:S(2)}, u32[]{:S(2)}) collective-permute-start(bf16[512,768]{1,0:T(8,128)(2,1)} %slice.346), channel_id=1, source_target_pairs={{0,4},{1,5},{2,6},{3,7},{4,0},{5,1},{6,2},{7,3},{8,12},{9,13},{10,... | collective-permute-start | bytes 2359304 | tf_op jit(solution)/shard_map/ppermute | solution.py:72
  338.8 31.7 %collective-permute-start.33 = (bf16[16,48,1152]{2,1,0:T(8,128)(2,1)S(1)}, bf16[16,48,1152]{2,1,0:T(8,128)(2,1)}, u32[]{:S(2)}, u32[]{:S(2)}) collective-permute-start(bf16[16,48,1152]{2,1,0:T(8,128)(2,1)S(1)} %dynamic-slice_convert_fusion.2), channel_id=1, source_target_pairs={{0,1},{1,0},{2,3},{3,2},{4,5},{5,4},{6,7},{7,6},{8,9},{9,8},{10,11... | collective-permute-start | bytes 5308424 | tf_op jit(solution)/shard_map/ppermute | solution.py:69
  339.9 8.3 %collective-permute-start.40 = (bf16[16,48,384]{2,1,0:T(8,128)(2,1)}, bf16[16,48,384]{2,1,0:T(8,128)(2,1)S(1)}, u32[]{:S(2)}, u32[]{:S(2)}) collective-permute-start(bf16[16,48,384]{2,1,0:T(8,128)(2,1)} %dynamic-slice_convert_fusion.3), channel_id=1, source_target_pairs={{0,1},{1,0},{2,3},{3,2},{4,5},{5,4},{6,7},{7,6},{8,9},{9,8},{10,11... | collective-permute-start | bytes 1769480 | tf_op jit(solution)/shard_map/ppermute | solution.py:69
  343.6 24.2 %collective-permute-start.34 = (bf16[16,48,128]{2,1,0:T(8,128)(2,1)S(1)}, bf16[16,48,128]{2,1,0:T(8,128)(2,1)S(1)}, u32[]{:S(2)}, u32[]{:S(2)}) collective-permute-start(bf16[16,48,128]{2,1,0:T(8,128)(2,1)S(1)} %get-tuple-element.79), channel_id=1, source_target_pairs={{0,1},{1,0},{2,3},{3,2},{4,5},{5,4},{6,7},{7,6},{8,9},{9,8},{10,11... | collective-permute-start | bytes 589832 | tf_op jit(solution)/shard_map/ppermute | solution.py:69
  347.8 62.7 %collective-permute-start.46 = (bf16[16,48,1536]{2,1,0:T(8,128)(2,1)}, bf16[16,48,1536]{2,1,0:T(8,128)(2,1)S(1)}, u32[]{:S(2)}, u32[]{:S(2)}) collective-permute-start(bf16[16,48,1536]{2,1,0:T(8,128)(2,1)} %dynamic-slice_convert_fusion.1), channel_id=1, source_target_pairs={{0,1},{1,0},{2,3},{3,2},{4,5},{5,4},{6,7},{7,6},{8,9},{9,8},{10,11... | collective-permute-start | bytes 7077896 | tf_op jit(solution)/shard_map/ppermute | solution.py:69
  363.1 14.9 %collective-permute-start.42 = (bf16[4,48,384]{2,1,0:T(8,128)(2,1)S(1)}, bf16[4,48,384]{2,1,0:T(8,128)(2,1)S(1)}, u32[]{:S(2)}, u32[]{:S(2)}) collective-permute-start(bf16[4,48,384]{2,1,0:T(8,128)(2,1)S(1)} %get-tuple-element.101), channel_id=1, source_target_pairs={{0,8},{1,17},{2,10},{3,19},{4,12},{5,21},{6,14},{7,23},{8,0},{9,25... | collective-permute-start | bytes 442376 | tf_op jit(solution)/shard_map/ppermute | solution.py:66
  367.8 38.7 %collective-permute-start.32 = (bf16[512,768]{1,0:T(8,128)(2,1)}, bf16[512,768]{1,0:T(8,128)(2,1)}, u32[]{:S(2)}, u32[]{:S(2)}) collective-permute-start(bf16[512,768]{1,0:T(8,128)(2,1)} %slice.355), channel_id=1, source_target_pairs={{0,4},{1,5},{2,6},{3,7},{4,0},{5,1},{6,2},{7,3},{8,12},{9,13},{10,... | collective-permute-start | bytes 2359304 | tf_op jit(solution)/shard_map/ppermute | solution.py:72
  370.5 50.4 %collective-permute-start.52 = (bf16[16,192,384]{2,1,0:T(8,128)(2,1)}, bf16[16,192,384]{2,1,0:T(8,128)(2,1)S(1)}, u32[]{:S(2)}, u32[]{:S(2)}) collective-permute-start(bf16[16,192,384]{2,1,0:T(8,128)(2,1)} %dynamic-slice_convert_fusion), channel_id=1, source_target_pairs={{0,1},{1,0},{2,3},{3,2},{4,5},{5,4},{6,7},{7,6},{8,9},{9,8},{10,11... | collective-permute-start | bytes 7077896 | tf_op jit(solution)/shard_map/ppermute | solution.py:69
  378.0 14.4 %collective-permute-start.35 = (bf16[8,48,1280]{2,1,0:T(8,128)(2,1)}, bf16[8,48,1280]{2,1,0:T(8,128)(2,1)S(1)}, u32[]{:S(2)}, u32[]{:S(2)}) collective-permute-start(bf16[8,48,1280]{2,1,0:T(8,128)(2,1)} %get-tuple-element.34), channel_id=1, source_target_pairs={{0,16},{1,9},{2,18},{3,11},{4,20},{5,13},{6,22},{7,15},{8,24},{9,1... | collective-permute-start | bytes 2949128 | tf_op jit(solution)/shard_map/ppermute | solution.py:66
  379.6 8.8 %collective-permute-start.43 = (bf16[2,48,384]{2,1,0:T(8,128)(2,1)S(1)}, bf16[2,48,384]{2,1,0:T(8,128)(2,1)S(1)}, u32[]{:S(2)}, u32[]{:S(2)}) collective-permute-start(bf16[2,48,384]{2,1,0:T(8,128)(2,1)S(1)} %fusion.30), channel_id=1, source_target_pairs={{0,2},{1,3},{2,0},{3,1},{4,6},{5,7},{6,4},{7,5},{8,10},{9,11},{10,... | collective-permute-start | bytes 221192 | tf_op jit(solution)/shard_map/ppermute | solution.py:66
  388.4 21.9 %collective-permute-start.44 = (bf16[1,48,384]{2,1,0:T(8,128)(2,1)S(1)}, bf16[1,48,384]{2,1,0:T(8,128)(2,1)S(1)}, u32[]{:S(2)}, u32[]{:S(2)}) collective-permute-start(bf16[1,48,384]{2,1,0:T(8,128)(2,1)S(1)} %get-tuple-element.132), channel_id=1, source_target_pairs={{0,4},{1,5},{2,6},{3,7},{4,0},{5,1},{6,2},{7,3},{8,12},{9,13},{10,... | collective-permute-start | bytes 110600 | tf_op jit(solution)/shard_map/ppermute | solution.py:66
  392.6 27.6 %collective-permute-start.36 = (bf16[4,48,1280]{2,1,0:T(8,128)(2,1)S(1)}, bf16[4,48,1280]{2,1,0:T(8,128)(2,1)S(1)}, u32[]{:S(2)}, u32[]{:S(2)}) collective-permute-start(bf16[4,48,1280]{2,1,0:T(8,128)(2,1)S(1)} %get-tuple-element.91), channel_id=1, source_target_pairs={{0,8},{1,17},{2,10},{3,19},{4,12},{5,21},{6,14},{7,23},{8,0},{9,25... | collective-permute-start | bytes 1474568 | tf_op jit(solution)/shard_map/ppermute | solution.py:66
  410.4 9.8 %collective-permute-start.45 = (bf16[2,24,384]{2,1,0:T(8,128)(2,1)S(1)}, bf16[2,24,384]{2,1,0:T(8,128)(2,1)S(1)}, u32[]{:S(2)}, u32[]{:S(2)}) collective-permute-start(bf16[2,24,384]{2,1,0:T(8,128)(2,1)S(1)} %constant_dynamic-slice_fusion.2), channel_id=1, source_target_pairs={{0,1},{1,0},{2,3},{3,2},{4,5},{5,4},{6,7},{7,6},{8,9},{9,8},{10,11... | collective-permute-start | bytes 110600 | tf_op jit(solution)/shard_map/ppermute | solution.py:69
  419.6 16.4 %collective-permute-start.47 = (bf16[8,48,1536]{2,1,0:T(8,128)(2,1)}, bf16[8,48,1536]{2,1,0:T(8,128)(2,1)S(1)}, u32[]{:S(2)}, u32[]{:S(2)}) collective-permute-start(bf16[8,48,1536]{2,1,0:T(8,128)(2,1)} %get-tuple-element.38), channel_id=1, source_target_pairs={{0,16},{1,9},{2,18},{3,11},{4,20},{5,13},{6,22},{7,15},{8,24},{9,1... | collective-permute-start | bytes 3538952 | tf_op jit(solution)/shard_map/ppermute | solution.py:66
  420.2 11.8 %collective-permute-start.37 = (bf16[2,48,1280]{2,1,0:T(8,128)(2,1)S(1)}, bf16[2,48,1280]{2,1,0:T(8,128)(2,1)S(1)}, u32[]{:S(2)}, u32[]{:S(2)}) collective-permute-start(bf16[2,48,1280]{2,1,0:T(8,128)(2,1)S(1)} %fusion.20), channel_id=1, source_target_pairs={{0,2},{1,3},{2,0},{3,1},{4,6},{5,7},{6,4},{7,5},{8,10},{9,11},{10,... | collective-permute-start | bytes 737288 | tf_op jit(solution)/shard_map/ppermute | solution.py:66
  430.3 24.6 %collective-permute-start.53 = (bf16[8,192,384]{2,1,0:T(8,128)(2,1)}, bf16[8,192,384]{2,1,0:T(8,128)(2,1)S(1)}, u32[]{:S(2)}, u32[]{:S(2)}) collective-permute-start(bf16[8,192,384]{2,1,0:T(8,128)(2,1)} %get-tuple-element.40), channel_id=1, source_target_pairs={{0,16},{1,9},{2,18},{3,11},{4,20},{5,13},{6,22},{7,15},{8,24},{9,1... | collective-permute-start | bytes 3538952 | tf_op jit(solution)/shard_map/ppermute | solution.py:66
  432.1 24.7 %collective-permute-start.38 = (bf16[1,48,1280]{2,1,0:T(8,128)(2,1)S(1)}, bf16[1,48,1280]{2,1,0:T(8,128)(2,1)S(1)}, u32[]{:S(2)}, u32[]{:S(2)}) collective-permute-start(bf16[1,48,1280]{2,1,0:T(8,128)(2,1)S(1)} %get-tuple-element.126), channel_id=1, source_target_pairs={{0,4},{1,5},{2,6},{3,7},{4,0},{5,1},{6,2},{7,3},{8,12},{9,13},{10,... | collective-permute-start | bytes 368648 | tf_op jit(solution)/shard_map/ppermute | solution.py:66
  437.2 21.2 %collective-permute-start.48 = (bf16[4,48,1536]{2,1,0:T(8,128)(2,1)}, bf16[4,48,1536]{2,1,0:T(8,128)(2,1)}, u32[]{:S(2)}, u32[]{:S(2)}) collective-permute-start(bf16[4,48,1536]{2,1,0:T(8,128)(2,1)} %get-tuple-element.89), channel_id=1, source_target_pairs={{0,8},{1,17},{2,10},{3,19},{4,12},{5,21},{6,14},{7,23},{8,0},{9,25... | collective-permute-start | bytes 1769480 | tf_op jit(solution)/shard_map/ppermute | solution.py:66
  456.1 10.1 %collective-permute-start.54 = (bf16[4,192,384]{2,1,0:T(8,128)(2,1)}, bf16[4,192,384]{2,1,0:T(8,128)(2,1)S(1)}, u32[]{:S(2)}, u32[]{:S(2)}) collective-permute-start(bf16[4,192,384]{2,1,0:T(8,128)(2,1)} %get-tuple-element.87), channel_id=1, source_target_pairs={{0,8},{1,17},{2,10},{3,19},{4,12},{5,21},{6,14},{7,23},{8,0},{9,25... | collective-permute-start | bytes 1769480 | tf_op jit(solution)/shard_map/ppermute | solution.py:66
  459.4 9.9 %collective-permute-start.49 = (bf16[2,48,1536]{2,1,0:T(8,128)(2,1)S(1)}, bf16[2,48,1536]{2,1,0:T(8,128)(2,1)S(1)}, u32[]{:S(2)}, u32[]{:S(2)}) collective-permute-start(bf16[2,48,1536]{2,1,0:T(8,128)(2,1)S(1)} %fusion.11), channel_id=1, source_target_pairs={{0,2},{1,3},{2,0},{3,1},{4,6},{5,7},{6,4},{7,5},{8,10},{9,11},{10,... | collective-permute-start | bytes 884744 | tf_op jit(solution)/shard_map/ppermute | solution.py:66
  466.3 11.1 %collective-permute-start.55 = (bf16[2,192,384]{2,1,0:T(8,128)(2,1)S(1)}, bf16[2,192,384]{2,1,0:T(8,128)(2,1)S(1)}, u32[]{:S(2)}, u32[]{:S(2)}) collective-permute-start(bf16[2,192,384]{2,1,0:T(8,128)(2,1)S(1)} %fusion.8), channel_id=1, source_target_pairs={{0,2},{1,3},{2,0},{3,1},{4,6},{5,7},{6,4},{7,5},{8,10},{9,11},{10,... | collective-permute-start | bytes 884744 | tf_op jit(solution)/shard_map/ppermute | solution.py:66
  470.4 9.3 %collective-permute-start.50 = (bf16[1,48,1536]{2,1,0:T(8,128)(2,1)S(1)}, bf16[1,48,1536]{2,1,0:T(8,128)(2,1)S(1)}, u32[]{:S(2)}, u32[]{:S(2)}) collective-permute-start(bf16[1,48,1536]{2,1,0:T(8,128)(2,1)S(1)} %get-tuple-element.120), channel_id=1, source_target_pairs={{0,4},{1,5},{2,6},{3,7},{4,0},{5,1},{6,2},{7,3},{8,12},{9,13},{10,... | collective-permute-start | bytes 442376 | tf_op jit(solution)/shard_map/ppermute | solution.py:66
  477.5 8.8 %collective-permute-start.56 = (bf16[1,192,384]{2,1,0:T(8,128)(2,1)S(1)}, bf16[1,192,384]{2,1,0:T(8,128)(2,1)S(1)}, u32[]{:S(2)}, u32[]{:S(2)}) collective-permute-start(bf16[1,192,384]{2,1,0:T(8,128)(2,1)S(1)} %get-tuple-element.118), channel_id=1, source_target_pairs={{0,4},{1,5},{2,6},{3,7},{4,0},{5,1},{6,2},{7,3},{8,12},{9,13},{10,... | collective-permute-start | bytes 442376 | tf_op jit(solution)/shard_map/ppermute | solution.py:66
  (77 other events, 869.8 us)

commit v2 on v1

--- a/solution.py
+++ b/solution.py
@@ -76,11 +76,15 @@
     return lax.dot_general(left, right, (dims, ((), ())), preferred_element_type=F32)
 
 
-def assemble_kernel(segments, rows, idx_ref, *refs):
+def tie(*values):
+    return lax.optimization_barrier(values)
+
+
+def assemble_kernel(segments, idx_ref, *refs):
     count = len(segments)
     sources, outs = refs[:4], refs[4 : 4 + count]
     buffer, in_sem, out_sem = refs[4 + count :]
-    core = idx_ref[1, 0]
+    core = idx_ref[2, 0]
     part = sources[0].shape[0]
     loads = [
         pltpu.make_async_copy(source, buffer.at[pl.ds(k * part, part)], in_sem.at[k])
@@ -94,14 +98,11 @@
         half = core if k < 2 else 1 - core
         for j in range(part):
             slot = k * part + j
-            place = idx_ref[0, slot]
-            for s, (start, width, both) in enumerate(segments):
-                if both and k >= 2:
-                    continue
-                column = 0 if both else pl.multiple_of(half * width, 128)
+            place = idx_ref[k // 2, (k % 2) * part + j]
+            for s, (start, width) in enumerate(segments):
                 store = pltpu.make_async_copy(
                     buffer.at[slot, :, pl.ds(start, width)],
-                    outs[s].at[place, :, pl.ds(column, width)],
+                    outs[s].at[place, half],
                     out_sem.at[s, slot],
                 )
                 store.start()
@@ -113,11 +114,9 @@
 def assemble(parts, table, segments):
     part, rows, width = parts[0].shape
     chips = 2 * part
-    shapes = [
-        jax.ShapeDtypeStruct((chips, rows, w if both else 2 * w), BF16) for _, w, both in segments
-    ]
+    shapes = [jax.ShapeDtypeStruct((chips, 2, rows, w), BF16) for _, w in segments]
     return pl.pallas_call(
-        functools.partial(assemble_kernel, segments, rows),
+        functools.partial(assemble_kernel, segments),
         out_shape=shapes,
         in_specs=[pl.BlockSpec(memory_space=pltpu.SMEM)] + [pl.BlockSpec(memory_space=pl.ANY)] * 4,
         out_specs=[pl.BlockSpec(memory_space=pl.ANY)] * len(segments),
@@ -134,81 +133,164 @@
     )(table, *parts)
 
 
-def assemble_plain(parts, table, segments, core):
-    own = jnp.concatenate(parts[:2], axis=0)
-    other = jnp.concatenate(parts[2:], axis=0)
-    chips, rows, width = own.shape
-    own_order = jnp.argsort(table[0, :chips])
-    other_order = jnp.argsort(table[0, chips:])
-    own = jnp.take(own, own_order, axis=0)
-    other = jnp.take(other, other_order, axis=0)
-    left = jnp.where(core == 0, own, other)
-    right = jnp.where(core == 0, other, own)
-    outs = []
-    for start, w, both in segments:
-        if both:
-            outs.append(left[:, :, start : start + w])
-        else:
-            outs.append(
-                jnp.concatenate(
-                    [left[:, :, start : start + w], right[:, :, start : start + w]], axis=2
-                )
-            )
-    return outs
-
-
-def fold_kernel(widths, idx_ref, core_ref, *refs):
-    count = len(widths)
-    ins, (keep_ref, send_ref) = refs[: 4 * count], refs[4 * count :]
-    column = 0
-    for s, width in enumerate(widths):
-        mine, got, theirs, also = ins[4 * s : 4 * s + 4]
-        keep_ref[:, :, column : column + width] = mine[...] + got[...].astype(F32)
-        send_ref[:, :, column : column + width] = (theirs[...] + also[...].astype(F32)).astype(BF16)
-        column += width
-
-
-def fold(fulls, received, idx, core):
-    chips, rows = received[0].shape[:2]
-    steps = chips // 2
-    widths = [r.shape[2] for r in received]
-    in_specs, operands = [], []
-    for full, got in zip(fulls, received):
-        width = got.shape[2]
-        wide = full.shape[2] != width
-        for offset in (0, steps):
-            in_specs.append(
-                pl.BlockSpec(
-                    (1, rows, width),
-                    lambda i, idx, core, o=offset, w=wide: (idx[i + o], 0, core[0] if w else 0),
-                )
-            )
-            in_specs.append(
-                pl.BlockSpec((1, rows, width), lambda i, idx, core, o=offset: (idx[i + o], 0, 0))
-            )
-            operands += [full, got]
-    total = sum(widths)
+def assemble_plain(parts, table, segments):
+    own = jnp.take(jnp.concatenate(parts[:2], axis=0), jnp.argsort(table[0]), axis=0)
+    other = jnp.take(jnp.concatenate(parts[2:], axis=0), jnp.argsort(table[1]), axis=0)
+    first = table[2, 0] == 0
+    both = jnp.stack([jnp.where(first, own, other), jnp.where(first, other, own)], axis=1)
+    return [both[..., start : start + w] for start, w in segments]
+
+
+def split_slabs(acc, core, chips, mine_ref, theirs_ref, cols, within):
+    rows = acc.shape[0] // (2 * chips)
+    for s in range(chips):
+        low = acc[2 * s * rows : (2 * s + 1) * rows]
+        high = acc[(2 * s + 1) * rows : (2 * s + 2) * rows]
+        mine, theirs = within(s)
+        mine_ref[mine, :, cols] = jnp.where(core == 0, low, high).astype(BF16)
+        theirs_ref[theirs, :, cols] = jnp.where(core == 0, high, low).astype(BF16)
+
+
+def weight_grad_kernel(chips, extra, table_ref, left_ref, right_ref, *refs):
+    mine_ref, theirs_ref = refs[-2:]
+    core = table_ref[2, 0]
+    acc = dot(left_ref[...], right_ref[...], ((0,), (0,)))
+    width = acc.shape[1]
+
+    def within(s):
+        return table_ref[0, s], table_ref[1, s]
+
+    if not extra:
+        split_slabs(acc, core, chips, mine_ref, theirs_ref, slice(None), within)
+        return
+    step = pl.program_id(0)
+    cols = pl.ds(pl.multiple_of(step * width, 128), width)
+    split_slabs(acc, core, chips, mine_ref, theirs_ref, cols, within)
+
+    @pl.when(step == 0)
+    def _():
+        tail = pl.ds(mine_ref.shape[2] - 128, 128)
+        split_slabs(refs[0][...], core, chips, mine_ref, theirs_ref, tail, within)
+
+
+def weight_grad(left, right, slots, tile, extra=None):
+    rows, height = left.shape
+    width = right.shape[1]
+    chips = slots.shape[1]
+    slab = height // (2 * chips)
+    total = width + (0 if extra is None else extra.shape[1])
+    block = (chips, slab, total if extra is not None else tile)
+    place = (lambda j, t: (0, 0, 0)) if extra is not None else (lambda j, t: (0, 0, j))
     return pl.pallas_call(
-        functools.partial(fold_kernel, widths),
+        functools.partial(weight_grad_kernel, chips, extra is not None),
         grid_spec=pltpu.PrefetchScalarGridSpec(
-            num_scalar_prefetch=2,
-            grid=(steps,),
-            in_specs=in_specs,
+            num_scalar_prefetch=1,
+            grid=(width // tile,),
+            in_specs=[
+                pl.BlockSpec((rows, height), lambda j, t: (0, 0)),
+                pl.BlockSpec((rows, tile), lambda j, t: (0, j)),
+            ]
+            + ([] if extra is None else [pl.BlockSpec((height, 128), lambda j, t: (0, 0))]),
+            out_specs=[pl.BlockSpec(block, place)] * 2,
+        ),
+        out_shape=[jax.ShapeDtypeStruct((chips, slab, total), BF16)] * 2,
+        compiler_params=pltpu.CompilerParams(vmem_limit_bytes=VMEM_LIMIT),
+        cost_estimate=pl.CostEstimate(
+            flops=2 * rows * height * width,
+            bytes_accessed=2 * (rows * (height + width) + height * width),
+            transcendentals=0,
+        ),
+        name="weight_grad",
+    )(slots, left, right, *([] if extra is None else [extra]))
+
+
+def tall_grad_kernel(chips, table_ref, left_ref, right_ref, mine_ref, theirs_ref):
+    core = table_ref[2, 0]
+    acc = dot(left_ref[...], right_ref[...], ((0,), (0,)))
+    base = pl.program_id(0) * chips
+
+    def within(s):
+        return table_ref[0, base + s] % chips, table_ref[1, base + s] % chips
+
+    split_slabs(acc, core, chips, mine_ref, theirs_ref, slice(None), within)
+
+
+def tall_grad(left, right, slots, column):
+    rows, height = left.shape
+    width = right.shape[1]
+    chips = slots.shape[1]
+    slab = height // (2 * chips)
+    tile = height // chips * column
+    return pl.pallas_call(
+        functools.partial(tall_grad_kernel, column),
+        grid_spec=pltpu.PrefetchScalarGridSpec(
+            num_scalar_prefetch=1,
+            grid=(chips // column,),
+            in_specs=[
+                pl.BlockSpec((rows, tile), lambda i, t: (0, i)),
+                pl.BlockSpec((rows, width), lambda i, t: (0, 0)),
+            ],
             out_specs=[
-                pl.BlockSpec((1, rows, total), lambda i, idx, core: (i, 0, 0)),
-                pl.BlockSpec((1, rows, total), lambda i, idx, core: (i, 0, 0)),
+                pl.BlockSpec((column, slab, width), lambda i, t: (t[0, i * column] // column, 0, 0)),
+                pl.BlockSpec((column, slab, width), lambda i, t: (t[1, i * column] // column, 0, 0)),
             ],
         ),
-        out_shape=[
-            jax.ShapeDtypeStruct((steps, rows, total), F32),
-            jax.ShapeDtypeStruct((steps, rows, total), BF16),
-        ],
+        out_shape=[jax.ShapeDtypeStruct((chips, slab, width), BF16)] * 2,
         compiler_params=pltpu.CompilerParams(vmem_limit_bytes=VMEM_LIMIT),
         cost_estimate=pl.CostEstimate(
-            flops=0, bytes_accessed=chips * rows * total * 9, transcendentals=0
+            flops=2 * rows * height * width,
+            bytes_accessed=2 * (rows * (height + width) + height * width),
+            transcendentals=0,
         ),
-        name="fold",
-    )(idx, core, *operands)
+        name="tall_grad",
+    )(slots, left, right)
+
+
+def grad_plain(left, right, table, extra=None):
+    full = dot(left, right, ((0,), (0,)))
+    if extra is not None:
+        full = jnp.concatenate([full, extra], axis=1)
+    chips = table.shape[1]
+    full = full.astype(BF16).reshape(chips, 2, full.shape[0] // (2 * chips), full.shape[1])
+    core = table[2, 0]
+    mine = lax.dynamic_index_in_dim(full, core, 1, keepdims=False)
+    theirs = lax.dynamic_index_in_dim(full, 1 - core, 1, keepdims=False)
+    return jnp.take(mine, table[0], axis=0), jnp.take(theirs, table[1], axis=0)
+
+
+def hidden_grad_kernel(grad_ref, w_ref, slope_ref, out_ref, sum_ref):
+    grad = dot(grad_ref[...], w_ref[...], ((1,), (1,))) * slope_ref[...].astype(F32)
+    low = grad.astype(BF16)
+    out_ref[...] = low
+    sum_ref[...] = jnp.sum(low.astype(F32), axis=0, keepdims=True)
+
+
+def hidden_grad(grad, w_reduce, slope):
+    rows, tile = grad.shape[0], 512
+    return pl.pallas_call(
+        hidden_grad_kernel,
+        grid=(FF // tile,),
+        in_specs=[
+            pl.BlockSpec((rows, D), lambda j: (0, 0)),
+            pl.BlockSpec((tile, D), lambda j: (j, 0)),
+            pl.BlockSpec((rows, tile), lambda j: (0, j)),
+        ],
+        out_specs=[
+            pl.BlockSpec((rows, tile), lambda j: (0, j)),
+            pl.BlockSpec((1, tile), lambda j: (0, j)),
+        ],
+        out_shape=[
+            jax.ShapeDtypeStruct((rows, FF), BF16),
+            jax.ShapeDtypeStruct((1, FF), F32),
+        ],
+        compiler_params=pltpu.CompilerParams(vmem_limit_bytes=VMEM_LIMIT),
+        cost_estimate=pl.CostEstimate(
+            flops=2 * rows * D * FF,
+            bytes_accessed=2 * (rows * D + D * FF + 2 * rows * FF),
+            transcendentals=0,
+        ),
+        name="hidden_grad",
+    )(grad, w_reduce, slope)
 
 
 def attention_kernel(qkv_ref, qid_ref, kid_ref, context_ref, probs_ref):
@@ -264,7 +346,7 @@
     )(qkv, qid, kid)
 
 
-def attention_back_kernel(qkv_ref, probs_ref, grad_ref, out_ref):
+def attention_back_kernel(qkv_ref, probs_ref, grad_ref, out_ref, sum_ref):
     lane = lax.broadcasted_iota(jnp.int32, (BLOCK, 128), 1)
     zero = jnp.zeros((BLOCK, 128), BF16)
     for pair in range(HEADS // 2):
@@ -294,29 +376,50 @@
         out_ref[:, 2 * D + pair * 128 : 2 * D + pair * 128 + 128] = jnp.where(
             first, d_v[0], d_v[1]
         ).astype(BF16)
-
-
-def attention_back(qkv, probs, grad_context):
+    sums = jnp.sum(out_ref[...].astype(F32), axis=0, keepdims=True)
+
+    @pl.when(pl.program_id(0) == 0)
+    def _():
+        sum_ref[...] = sums
+
+    @pl.when(pl.program_id(0) > 0)
+    def _():
+        sum_ref[...] += sums
+
+
+def attention_back_more_kernel(qkv_ref, probs_ref, grad_ref, _, out_ref, sum_ref):
+    attention_back_kernel(qkv_ref, probs_ref, grad_ref, out_ref, sum_ref)
+
+
+def attention_back(qkv, probs, grad_context, start, count, into=None):
     rows = qkv.shape[0]
-    blocks = rows // BLOCK
+    more = into is not None
     return pl.pallas_call(
-        attention_back_kernel,
-        grid=(blocks,),
+        attention_back_more_kernel if more else attention_back_kernel,
+        grid=(count,),
         in_specs=[
-            pl.BlockSpec((BLOCK, 3 * D), lambda i: (i, 0)),
-            pl.BlockSpec((1, HEADS, BLOCK, BLOCK), lambda i: (i, 0, 0, 0)),
-            pl.BlockSpec((BLOCK, D), lambda i: (i, 0)),
-        ],
-        out_specs=pl.BlockSpec((BLOCK, 3 * D), lambda i: (i, 0)),
-        out_shape=jax.ShapeDtypeStruct((rows, 3 * D), BF16),
+            pl.BlockSpec((BLOCK, 3 * D), lambda i: (i + start, 0)),
+            pl.BlockSpec((1, HEADS, BLOCK, BLOCK), lambda i: (i + start, 0, 0, 0)),
+            pl.BlockSpec((BLOCK, D), lambda i: (i + start, 0)),
+        ]
+        + ([pl.BlockSpec(memory_space=pl.ANY)] if more else []),
+        out_specs=[
+            pl.BlockSpec((BLOCK, 3 * D), lambda i: (i + start, 0)),
+            pl.BlockSpec((1, 3 * D), lambda i: (0, 0)),
+        ],
+        out_shape=[
+            jax.ShapeDtypeStruct((rows, 3 * D), BF16),
+            jax.ShapeDtypeStruct((1, 3 * D), F32),
+        ],
+        input_output_aliases={3: 0} if more else {},
         compiler_params=pltpu.CompilerParams(vmem_limit_bytes=VMEM_LIMIT),
         cost_estimate=pl.CostEstimate(
-            flops=8 * rows * BLOCK * D * 2,
-            bytes_accessed=rows * (7 * D + HEADS * BLOCK) * 2,
+            flops=8 * count * BLOCK * BLOCK * D * 2,
+            bytes_accessed=count * BLOCK * (7 * D + HEADS * BLOCK) * 2,
             transcendentals=0,
         ),
         name="attention_back",
-    )(qkv, probs, grad_context)
+    )(qkv, probs, grad_context, *([into] if more else []))
 
 
 def expand_kernel(mid_ref, w_ref, b_ref, active_ref, slope_ref):
@@ -367,12 +470,6 @@
         - jnp.mean(scaled, axis=-1, keepdims=True)
         - norm * jnp.mean(scaled * norm, axis=-1, keepdims=True)
     )
-
-
-def column_halves(values, core):
-    width = values.shape[-1] // 2
-    left, right = values[..., :width], values[..., width:]
-    return jnp.where(core == 0, left, right), jnp.where(core == 0, right, left)
 
 
 def per_device(places, *args):
@@ -396,20 +493,21 @@
     tower = z // places.half
     is_q = tower == 0
     chip = pb * places.nz + z
-    masks = jnp.array([places.stack_masks(0), places.stack_masks(1)], jnp.int32)
-    order = lax.dynamic_index_in_dim(masks, core, 0, keepdims=False) ^ chip
-    other_order = lax.dynamic_index_in_dim(masks, 1 - core, 0, keepdims=False) ^ chip
-    table = jnp.stack(
-        [jnp.concatenate([order, other_order]), jnp.full((2 * places.chips,), core, jnp.int32)]
-    ).astype(jnp.int32)
-    core_arr = jnp.full((1,), core, jnp.int32)
+    masks = [places.stack_masks(side) for side in range(2)]
+    slots_of = [sorted(range(places.chips), key=side.__getitem__) for side in masks]
+
+    def of_core(rows_of):
+        both = jnp.array(rows_of, jnp.int32)
+        return (
+            lax.dynamic_index_in_dim(both, core, 0, keepdims=False),
+            lax.dynamic_index_in_dim(both, 1 - core, 0, keepdims=False),
+        )
+
+    side = jnp.full((places.chips,), core, jnp.int32)
+    table = jnp.stack([x ^ chip for x in of_core(masks)] + [side]).astype(jnp.int32)
+    away = jnp.arange(places.chips, dtype=jnp.int32) ^ chip
+    slots = jnp.stack([jnp.take(x, away) for x in of_core(slots_of)] + [side]).astype(jnp.int32)
     share = w_joined.shape[1]
-
-    def start(own_half, other_half):
-        got = places.swap_core(other_half)
-        return jnp.concatenate(
-            [jnp.where(core == 0, own_half, got), jnp.where(core == 0, got, own_half)], axis=1
-        )
 
     small = jnp.concatenate(
         [
@@ -419,90 +517,153 @@
         ],
         axis=2,
     )
-    j_own, j_other = column_halves(w_joined, core)
-    o_own, o_other = column_halves(w_output, core)
-    e_own, e_other = column_halves(w_expand, core)
-    r_own, r_other = column_halves(w_reduce, core)
-    first = start(
-        jnp.concatenate([j_own, o_own, small], axis=2),
-        jnp.concatenate([j_other, o_other, small], axis=2),
-    )
-    second = start(e_own, e_other)
-    third = start(r_own, r_other)
-
-    def gather(piece):
-        mine = lax.dynamic_index_in_dim(piece, tower, 0, keepdims=True)
-        theirs = lax.dynamic_index_in_dim(piece, 1 - tower, 0, keepdims=True)
-        stack = jnp.concatenate([mine, places.swap(theirs, 0)], axis=0)
-        for step in range(1, places.steps - 1):
-            stack = jnp.concatenate([stack, places.swap(stack, step)], axis=0)
-        last = places.swap(stack, places.steps - 1)
-        return [stack, last, places.swap_core(stack), places.swap_core(last)]
-
-    def weights(piece, segments):
-        parts = gather(piece)
-        if parts[0].shape[1] % 8 == 0:
-            return assemble(parts, table, segments)
-        return assemble_plain(parts, table, segments, core)
-
-    jw, ow = w_joined.shape[2] // 2, D // 2
-    full_j, full_o, full_small = weights(
-        first, [(0, jw, False), (jw, ow, False), (jw + ow, 128, True)]
-    )
-    (full_e,) = weights(second, [(0, FF // 2, False)])
-    (full_r,) = weights(third, [(0, D // 2, False)])
-    wj = full_j.reshape(D, 3 * D)
-    wo = full_o.reshape(D, D)
-    we = full_e.reshape(D, FF)
-    wr = full_r.reshape(FF, D)
-    small = full_small.reshape(D, 128).astype(F32)
-    vec = small[:, :8].T
-    bias_e = small[:, 8:12].reshape(1, FF)
+    first = jnp.concatenate([w_joined, w_output, small], axis=2)
+    second, third = w_expand, w_reduce
+
+    class Gather:
+        def __init__(self, piece):
+            self.stack = lax.dynamic_index_in_dim(piece, tower, 0, keepdims=True)
+            self.send = lax.dynamic_index_in_dim(piece, 1 - tower, 0, keepdims=True)
+            self.held = None
+
+        def join(self, got):
+            self.stack = jnp.concatenate([self.stack, got], axis=0)
+            self.send = self.stack
+
+        def move(self, first, last):
+            for step in range(first, last):
+                self.join(places.swap(self.send, step))
+
+        def mid(self):
+            self.move(0, 1)
+
+        def along_z(self):
+            self.move(1, z_steps)
+
+        def pb_first(self):
+            self.move(z_steps, places.steps - 1)
+
+        def pb_last(self):
+            self.held = places.swap(self.send, places.steps - 1)
+
+        def core_stack(self):
+            self.other = places.swap_core(self.stack)
+
+        def core_held(self):
+            self.parts = [self.stack, self.held, self.other, places.swap_core(self.held)]
+
+        def whole(self, segments):
+            if self.stack.shape[1] % 8 == 0:
+                return assemble(self.parts, table, segments)
+            return assemble_plain(self.parts, table, segments)
+
+    z_steps = 1 + len(bits_of(places.half))
 
     rows_q = question_in.reshape(-1, D)
     rows_p = passage_in.reshape(-1, D)
     own_rows = rows_q.shape[0]
 
-    def exchange(q_side, p_side):
-        mine = jnp.where(is_q, q_side, p_side)
-        theirs = jnp.where(is_q, p_side, q_side)
-        return jnp.concatenate([mine, places.swap_tower(theirs)], axis=0)
-
-    def give_back(both):
-        mine, theirs = both[:own_rows], places.swap_tower(both[own_rows:])
-        return jnp.where(is_q, mine, theirs), jnp.where(is_q, theirs, mine)
+    def sides(q_side, p_side):
+        return jnp.where(is_q, q_side, p_side), jnp.where(is_q, p_side, q_side)
 
     lq, lp = question_in.shape[1], passage_in.shape[1]
     valid_q = (jnp.arange(lq, dtype=jnp.int32)[None, :] < question_len[:, None]).astype(jnp.int32)
     valid_p = (jnp.arange(lp, dtype=jnp.int32)[None, :] < passage_len[:, None]).astype(jnp.int32)
-    valid = exchange(valid_q.reshape(-1), valid_p.reshape(-1))
-    tokens = exchange(rows_q, rows_p)
-    cot = exchange(question_cot.reshape(-1, D), passage_cot.reshape(-1, D))
-    rows = tokens.shape[0]
+    my_valid, send_valid = sides(valid_q.reshape(-1), valid_p.reshape(-1))
+    valid = jnp.concatenate([my_valid, places.swap_tower(send_valid)])
+    my_tokens, send_tokens = sides(rows_q, rows_p)
+    my_cot, send_cot = sides(question_cot.reshape(-1, D), passage_cot.reshape(-1, D))
+    rows = 2 * own_rows
     row_ids = jnp.arange(rows, dtype=jnp.int32)
     seq = jnp.where(is_q, row_ids // lq, row_ids // lp)
     qid = seq.reshape(rows, 1)
     kid = jnp.where(valid > 0, seq, -1).reshape(rows // BLOCK, 1, BLOCK)
     row_mask = valid.reshape(rows, 1).astype(F32)
 
+    def chunked(values):
+        step = values.shape[0] // 4
+        return [values[i * step : (i + 1) * step] for i in range(4)]
+
+    def hand(values):
+        return [places.swap_tower(x) for x in values]
+
+    g1, g2, g3 = Gather(first), Gather(second), Gather(third)
+    tokens_out, cot_out = chunked(send_tokens), chunked(send_cot)
+    g1.mid()
+    g1.send, g2.send = tie(g1.send, g2.send)
+    g1.along_z()
+    g2.mid()
+    g1.send, g2.send, g3.send = tie(g1.send, g2.send, g3.send)
+    g1.pb_first()
+    g2.along_z()
+    g3.mid()
+    g1.stack, g2.send, g3.send, tokens_out = tie(g1.stack, g2.send, g3.send, tokens_out)
+    g1.send = g1.stack
+    g1.pb_last()
+    g1.core_stack()
+    g3.along_z()
+    tokens_in = hand(tokens_out[:2])
+    g1.held, g1.other, g2.send, g3.send, tokens_in, tokens_out = tie(
+        g1.held, g1.other, g2.send, g3.send, tokens_in, tokens_out
+    )
+    g1.core_held()
+    g2.pb_first()
+    tokens_in = tokens_in + hand(tokens_out[2:3])
+    g1.parts, g2.stack, g3.send, tokens_in, tokens_out = tie(
+        g1.parts, g2.stack, g3.send, tokens_in, tokens_out
+    )
+    g2.send = g2.stack
+    g2.pb_last()
+    g2.core_stack()
+    tokens_in = tokens_in + hand(tokens_out[3:])
+    full_j, full_o, full_small = g1.whole([(0, 3 * D), (3 * D, D), (4 * D, 128)])
+    wj = full_j.reshape(D, 3 * D)
+    wo = full_o.reshape(D, D)
+    small = full_small.reshape(D, 128).astype(F32)
+    vec = small[:, :8].T
+    bias_e = small[:, 8:12].reshape(1, FF)
     bias_j = jnp.concatenate([vec[0], jnp.zeros((D,), F32), vec[1]])
+    tokens = jnp.concatenate([my_tokens] + tokens_in, axis=0)
+    wj, tokens, cot_out = tie(wj, tokens, cot_out)
+    cot_in = hand(cot_out[:1])
     qkv = (dot(tokens, wj) + bias_j).astype(BF16)
+    qkv, g2.held, g2.other, g2.stack, g3.send, cot_in, cot_out = tie(
+        qkv, g2.held, g2.other, g2.stack, g3.send, cot_in, cot_out
+    )
+    g3.pb_first()
+    g2.core_held()
+    cot_in = cot_in + hand(cot_out[1:2])
     context, probs = attention(qkv, qid, kid)
+    context, g2.parts, g3.stack, cot_in, cot_out = tie(context, g2.parts, g3.stack, cot_in, cot_out)
+    g3.send = g3.stack
+    g3.pb_last()
+    g3.core_stack()
+    cot_in = cot_in + hand(cot_out[2:3])
+    (full_e,) = g2.whole([(0, FF)])
+    we = full_e.reshape(D, FF)
     attended = dot(context, wo) + vec[2]
     norm_one, inverse_one = normalized(tokens.astype(F32) + attended)
     mid = norm_one * vec[3] + vec[4]
     mid_low = mid.astype(BF16)
+    mid_low, we, g3.held, g3.other, g3.stack, cot_in, cot_out = tie(
+        mid_low, we, g3.held, g3.other, g3.stack, cot_in, cot_out
+    )
+    g3.core_held()
+    cot_in = cot_in + hand(cot_out[3:])
     active, slope = expand(mid_low, we, bias_e)
+    active, g3.parts, cot_in = tie(active, g3.parts, cot_in)
+    (full_r,) = g3.whole([(0, D)])
+    wr = full_r.reshape(FF, D)
     norm_two, inverse_two = normalized(mid + dot(active, wr) + vec[5])
     out = ((norm_two * vec[6] + vec[7]) * row_mask).astype(BF16)
 
     per_q = rows // lq
     every = lp // lq
     per_p = rows // lp
-    slots = out.reshape(per_q, lq, D)[:, 0, :]
-    others = places.swap_tower(slots)
-    cls_q = jnp.where(is_q, slots, others)
-    cls_p = jnp.where(is_q, others, slots)[::every]
+    firsts = out.reshape(per_q, lq, D)[:, 0, :]
+    others = places.swap_tower(firsts)
+    cls_q = jnp.where(is_q, firsts, others)
+    cls_p = jnp.where(is_q, others, firsts)[::every]
     pad = (-(per_q + per_p)) % 8
     stack = jnp.concatenate([cls_q, cls_p, jnp.zeros((pad, D), BF16)], axis=0)[None]
     pair_masks = [0]
@@ -556,6 +717,7 @@
     ).reshape(per_q, D)
     d_slot = jnp.where(is_q, d_q, d_p)
 
+    cot = jnp.concatenate([my_cot] + cot_in, axis=0)
     d_out = cot.astype(F32).reshape(per_q, lq, D)
     at_slot = jnp.arange(lq, dtype=jnp.int32)[None, :, None] == 0
     d_out = d_out + jnp.where(at_slot, d_slot[:, None, :], 0.0)
@@ -566,72 +728,104 @@
     d_reduced = d_second.astype(BF16)
     g_bias_reduce = jnp.sum(d_reduced.astype(F32), axis=0)
 
-    def as_pieces(values):
-        return values.reshape(places.chips, values.shape[0] // places.chips, values.shape[1])
-
-    def other_half(full):
-        width = full.shape[2] // 2
-        return lax.dynamic_slice_in_dim(full, (1 - core) * width, width, axis=2).astype(BF16)
-
-    def scatter(fulls):
-        fulls = [as_pieces(full) for full in fulls]
-        received = [
-            places.swap_core(full.astype(BF16) if full.shape[2] == 128 else other_half(full))
-            for full in fulls
-        ]
-        keep, send = fold(fulls, received, order, core_arr)
-        for step in range(places.steps - 1, 0, -1):
-            got = places.swap(send, step)
-            both = keep.shape[0] // 2
-            if step > 1:
-                send = (keep[both:] + got[both:].astype(F32)).astype(BF16)
-                keep = keep[:both] + got[:both].astype(F32)
-            else:
-                total = keep + got.astype(F32)
-                keep, send = total[0:1], total[1:2].astype(BF16)
-        got = places.swap(send, 0)
-        mine = keep.astype(BF16)
-        towers = jnp.where(
-            is_q, jnp.concatenate([mine, got], axis=0), jnp.concatenate([got, mine], axis=0)
-        )
-        count = towers.shape[1] // 2
-        keep_rows = lax.dynamic_slice_in_dim(towers, core * count, count, axis=1)
-        send_rows = lax.dynamic_slice_in_dim(towers, (1 - core) * count, count, axis=1)
-        got_rows = places.swap_core(send_rows)
-        outs, column = [], 0
-        for full in fulls:
-            if full.shape[2] == 128:
-                outs.append(keep_rows[:, :, column : column + 128].astype(F32))
-                column += 128
-                continue
-            width = full.shape[2] // 2
-            mine = keep_rows[:, :, column : column + width]
-            theirs = got_rows[:, :, column : column + width]
-            outs.append(
-                jnp.concatenate(
-                    [jnp.where(core == 0, mine, theirs), jnp.where(core == 0, theirs, mine)],
-                    axis=2,
-                ).astype(F32)
+    even = share % 8 == 0
+
+    def gradient(left, right, tile, extra=None):
+        if not even:
+            return grad_plain(left, right, table, extra)
+        if left.shape[1] > D:
+            return tall_grad(left, right, slots, places.nz)
+        return weight_grad(left, right, slots, tile, extra)
+
+    class Scatter:
+        def __init__(self, mine, theirs):
+            self.parts, self.theirs = [mine], theirs
+            self.count = mine.shape[0]
+
+        def cores(self):
+            self.parts = self.parts + [places.swap_core(self.theirs)]
+
+        def total(self, start, stop):
+            out = self.parts[0][start:stop].astype(F32)
+            for part in self.parts[1:]:
+                out = out + part[start:stop].astype(F32)
+            return out
+
+        def move(self, step):
+            half = self.count // 2
+            send = self.total(half, self.count).astype(BF16)
+            self.parts = self.parts + [places.swap(send, step)]
+            self.count = half
+
+        def pb_first(self):
+            self.move(places.steps - 1)
+
+        def pb_rest(self):
+            for step in range(places.steps - 2, z_steps - 1, -1):
+                self.move(step)
+
+        def along_z(self):
+            for step in range(z_steps - 1, 0, -1):
+                self.move(step)
+
+        def mid(self):
+            got = places.swap(self.total(1, 2).astype(BF16), 0).astype(F32)
+            keep = self.total(0, 1)
+            self.out = jnp.concatenate(
+                [jnp.where(is_q, keep, got), jnp.where(is_q, got, keep)], axis=0
             )
-            column += width
-        return outs
-
-    (grad_reduce,) = scatter([dot(active, d_reduced, ((0,), (0,)))])
-    d_active = dot(d_reduced, wr, ((1,), (1,)))
-    d_expanded = (d_active * slope.astype(F32)).astype(BF16)
-    g_bias_expand = jnp.sum(d_expanded.astype(F32), axis=0)
-    (grad_expand,) = scatter([dot(mid_low, d_expanded, ((0,), (0,)))])
+
+    send_out = chunked(out[own_rows:])
+    sr = Scatter(*gradient(active, d_reduced, D))
+    sr.parts, sr.theirs, d_reduced, send_out = tie(sr.parts, sr.theirs, d_reduced, send_out)
+    sr.cores()
+    got_out = hand(send_out[:1])
+    d_expanded, g_bias_expand = hidden_grad(d_reduced, wr, slope)
+    sr.parts, d_expanded, got_out, send_out = tie(sr.parts, d_expanded, got_out, send_out)
+    sr.pb_first()
+    got_out = got_out + hand(send_out[1:2])
+    se = Scatter(*gradient(mid_low, d_expanded, 1024))
+    se.parts, se.theirs, d_expanded, got_out, send_out = tie(
+        se.parts, se.theirs, d_expanded, got_out, send_out
+    )
+    se.cores()
+    got_out = got_out + hand(send_out[2:3])
     d_mid = d_second + dot(d_expanded, we, ((1,), (1,)))
+    sr.parts, se.parts, d_mid, got_out, send_out = tie(
+        sr.parts, se.parts, d_mid, got_out, send_out
+    )
+    sr.pb_rest()
+    got_out = got_out + hand(send_out[3:])
     d_first = norm_back(d_mid, vec[3], norm_one, inverse_one)
     g_gain_one = jnp.sum(d_mid * norm_one, axis=0)
     g_shift_one = jnp.sum(d_mid, axis=0)
     d_attended = d_first.astype(BF16)
     g_bias_output = jnp.sum(d_attended.astype(F32), axis=0)
-    (grad_output,) = scatter([dot(context, d_attended, ((0,), (0,)))])
+    so = Scatter(*gradient(context, d_attended, D))
     d_context = dot(d_attended, wo, ((1,), (1,))).astype(BF16)
-    d_joined = attention_back(qkv, probs, d_context)
-    d_tokens = d_first + dot(d_joined, wj, ((1,), (1,)))
-    g_joined_bias = jnp.sum(d_joined.astype(F32), axis=0)
+    sr.parts, se.parts, so.parts, so.theirs, d_context, got_out = tie(
+        sr.parts, se.parts, so.parts, so.theirs, d_context, got_out
+    )
+    se.pb_first()
+    sr.along_z()
+    so.cores()
+    blocks = rows // BLOCK
+    d_joined, sums_one = attention_back(qkv, probs, d_context, 0, blocks // 2)
+    sr.parts, so.parts, d_joined = tie(sr.parts, so.parts, d_joined)
+    sr.mid()
+    d_joined, sums_two = attention_back(
+        qkv, probs, d_context, blocks // 2, blocks - blocks // 2, d_joined
+    )
+    sr.out, se.parts, so.parts, d_joined = tie(sr.out, se.parts, so.parts, d_joined)
+    se.pb_rest()
+    so.pb_first()
+    send_grad = (d_first[own_rows:] + dot(d_joined[own_rows:], wj, ((1,), (1,)))).astype(BF16)
+    send_grad = chunked(send_grad)
+    se.parts, so.parts, d_joined, send_grad = tie(se.parts, so.parts, d_joined, send_grad)
+    se.along_z()
+    so.pb_rest()
+    got_grad = hand(send_grad[:1])
+    g_joined_bias = (sums_one + sums_two)[0]
     g_vec = jnp.stack(
         [
             g_joined_bias[:D],
@@ -647,18 +841,40 @@
     g_small = jnp.concatenate(
         [g_vec.T, g_bias_expand.reshape(D, 4), jnp.zeros((D, 116), F32)], axis=1
     )
-    grad_joined, grad_small = scatter([dot(tokens, d_joined, ((0,), (0,))), g_small])
-    grad_vectors = grad_small[:, :, :8].transpose(0, 2, 1)
-    grad_b_expand = grad_small[:, :, 8:12].reshape(2, 4 * share)
-
-    out_q, out_p = give_back(out)
-    grad_q, grad_p = give_back(d_tokens.astype(BF16))
+    sj = Scatter(*gradient(tokens, d_joined, D, g_small))
+    se.parts, so.parts, sj.parts, sj.theirs, d_joined, got_grad, send_grad = tie(
+        se.parts, so.parts, sj.parts, sj.theirs, d_joined, got_grad, send_grad
+    )
+    sj.cores()
+    so.along_z()
+    se.mid()
+    got_grad = got_grad + hand(send_grad[1:2])
+    own_grad = d_first[:own_rows] + dot(d_joined[:own_rows], wj, ((1,), (1,)))
+    sj.parts, so.parts, own_grad, got_grad, send_grad = tie(
+        sj.parts, so.parts, own_grad, got_grad, send_grad
+    )
+    sj.pb_first()
+    so.mid()
+    got_grad = got_grad + hand(send_grad[2:3])
+    sj.parts, got_grad, send_grad = tie(sj.parts, got_grad, send_grad)
+    sj.pb_rest()
+    got_grad = got_grad + hand(send_grad[3:])
+    sj.along_z()
+    sj.mid()
+    grad_joined = sj.out[:, :, : 3 * D]
+    grad_output, grad_expand, grad_reduce = so.out, se.out, sr.out
+    extra = sj.out[:, :, 3 * D :]
+    grad_vectors = extra[:, :, :8].transpose(0, 2, 1)
+    grad_b_expand = extra[:, :, 8:12].reshape(2, 4 * share)
+
+    out_q, out_p = sides(out[:own_rows], jnp.concatenate(got_out, axis=0))
+    grad_q, grad_p = sides(own_grad, jnp.concatenate(got_grad, axis=0).astype(F32))
     return (
         out_q.reshape(question_in.shape),
         out_p.reshape(passage_in.shape),
         question_loss,
-        grad_q.astype(F32).reshape(question_in.shape),
-        grad_p.astype(F32).reshape(passage_in.shape),
+        grad_q.reshape(question_in.shape),
+        grad_p.reshape(passage_in.shape),
         grad_joined,
         grad_output,
         grad_expand,

time: 495 us -> 465 us (0.939)
  waiting for transfers between devices: 181 us -> 104 us
  matrix products: 70.5 us -> 42.4 us
  other arithmetic: 59 us -> 80.9 us
  Pallas kernels: 90.2 us -> 110 us
  local copies, waits for them, and re-layouts: 39.3 us -> 58.8 us
  starting transfers between devices: 46.5 us -> 58 us
    ppermute x28, waiting for transfers between devices: 95.2 us -> 51.2 us  [swap(): return lax.ppermute(values, AXES, self.pairs(step))]
    dot_general x14 -> x10, matrix products: 70.5 us -> 42.4 us  [dot(): lax.dot_general(left, right, (dims, ((), ())), preferred_element_type=F32)]
    ppermute x2, waiting for transfers between devices: 23.7 us -> 0.01 us  [per_device(): got = lax.ppermute(wanted, 'pb', [(i, i ^ bit) for i in range(places.pb_n)])]
    pallas_call x8 -> x10, Pallas kernels: 62.2 us -> 82.3 us  [the longest x3 24 us: weight_grad(): pl.pallas_call(functools.partial(weight_grad_kernel, chips, extra is not...]
    ppermute x6 -> x18, starting transfers between devices: 7.45 us -> 24.3 us  [swap_tower(): lax.ppermute(values, 'pa', [(i, i ^ 2 * self.half) for i in range(self.pa...]
    ppermute x6 -> x18, waiting for transfers between devices: 52.4 us -> 41.9 us  [swap_tower(): lax.ppermute(values, 'pa', [(i, i ^ 2 * self.half) for i in range(self.pa...]
    convert_element_type x14 -> x16, other arithmetic: 8.78 us -> 18.9 us  [the longest x12 14.6 us: move(): send = self.total(half, self.count).astype(BF16)]
    unnamed x144 -> x221, local copies, waits for them, and re-layouts: 11.3 us -> 20.8 us
  transfers between devices with their start and end apart: 58 -> 62, of which waited for: 27 -> 26; matrix products, arithmetic and copies ran while one was open for 32% -> 31% of each run, Pallas kernels for 18% -> 21%
where the time goes in v2:
time: 465 us; the launch traced here: 457 us
  Pallas kernels  110 us (24%)
  waiting for transfers between devices  104 us (22%)
  other arithmetic  80.9 us (17%)
  local copies, waits for them, and re-layouts  58.8 us (13%)
  starting transfers between devices  58 us (12%)
  matrix products  42.4 us (9%)
    ppermute x28, waiting for transfers between devices, swap(): return lax.ppermute(values, AXES, self.pairs(step))  51.2 us
    dot_general x10, matrix products, dot(): lax.dot_general(left, right, (dims, ((), ())), preferred_element_type=F32)  42.4 us
    ppermute x18, waiting for transfers between devices, swap_tower(): lax.ppermute(values, 'pa', [(i, i ^ 2 * self.half) for i in range(self.pa...  41.9 us
    ppermute x28, starting transfers between devices, swap(): return lax.ppermute(values, AXES, self.pairs(step))  29.6 us
    ppermute x18, starting transfers between devices, swap_tower(): lax.ppermute(values, 'pa', [(i, i ^ 2 * self.half) for i in range(self.pa...  24.3 us
    pallas_call x3, Pallas kernels, weight_grad(): pl.pallas_call(functools.partial(weight_grad_kernel, chips, extra is not...  24 us
    pallas_call x2, Pallas kernels, attention_back(): pl.pallas_call(attention_back_more_kernel if more else attention_back_ker...  21.5 us
    unnamed x221, local copies, waits for them, and re-layouts  20.8 us
  transfers between devices with their start and end apart: 62, of which 26 were waited for; matrix products, arithmetic and copies ran while one was open for 31% of the time, Pallas kernels for 21%

profile of v2, /device:TPU:0, one launch (start us, length us, event | category | flops | bytes accessed | tf_op | source)
XLA Modules:
  0.0 456.9 jit_solution(3929122308639159709)
XLA Ops:
  3.4 4.1 collective-permute-start
  10.6 2.7 bitcast_select_fusion.1
  19.8 4.1 collective-permute-start.1
  24.1 7.0 %collective-permute-done.1 = bf16[2,24,3200]{2,1,0:T(8,128)(2,1)S(1)} collective-permute-done((bf16[2,24,3200]{2,1,0:T(8,128)(2,1)S(1)}, bf16[2,24,3200]{2,1,0:T(8,128)(2,1)S(1)}, u32[]{:S(2)}, u32[]{:S(2)}) %collective-permute-start.1) | collective-permute-done | bytes 307232 | tf_op jit(solution)/shard_map/ppermute | solution.py:66
  34.8 5.4 %collective-permute-done.5 = bf16[1,96,768]{2,1,0:T(8,128)(2,1)S(1)} collective-permute-done((bf16[1,96,768]{2,1,0:T(8,128)(2,1)S(1)}, bf16[1,96,768]{2,1,0:T(8,128)(2,1)S(1)}, u32[]{:S(2)}, u32[]{:S(2)}) %collective-permute-start.5) | collective-permute-done | bytes 147488 | tf_op jit(solution)/shard_map/ppermute | solution.py:66
  49.1 3.7 collective-permute-start.9
  55.0 6.9 %collective-permute-done.8 = bf16[2,96,768]{2,1,0:T(8,128)(2,1)S(1)} collective-permute-done((bf16[2,96,768]{2,1,0:T(8,128)(2,1)}, bf16[2,96,768]{2,1,0:T(8,128)(2,1)S(1)}, u32[]{:S(2)}, u32[]{:S(2)}) %collective-permute-start.8) | collective-permute-done | bytes 294944 | tf_op jit(solution)/shard_map/ppermute | solution.py:66
  63.3 7.3 %collective-permute-done.10 = bf16[128,768]{1,0:T(8,128)(2,1)S(1)} collective-permute-done((bf16[128,768]{1,0:T(8,128)(2,1)}, bf16[128,768]{1,0:T(8,128)(2,1)S(1)}, u32[]{:S(2)}, u32[]{:S(2)}) %collective-permute-start.10) | collective-permute-done | bytes 196640 | tf_op jit(solution)/shard_map/ppermute | solution.py:72
  76.3 6.5 %collective-permute-done.12 = bf16[4,24,3072]{2,1,0:T(8,128)(2,1)} collective-permute-done((bf16[4,24,3072]{2,1,0:T(8,128)(2,1)}, bf16[4,24,3072]{2,1,0:T(8,128)(2,1)}, u32[]{:S(2)}, u32[]{:S(2)}) %collective-permute-start.12) | collective-permute-done | bytes 589856 | tf_op jit(solution)/shard_map/ppermute | solution.py:66
  84.0 4.8 %collective-permute-done.13 = bf16[128,768]{1,0:T(8,128)(2,1)S(1)} collective-permute-done((bf16[128,768]{1,0:T(8,128)(2,1)}, bf16[128,768]{1,0:T(8,128)(2,1)S(1)}, u32[]{:S(2)}, u32[]{:S(2)}) %collective-permute-start.13) | collective-permute-done | bytes 196640 | tf_op jit(solution)/shard_map/ppermute | solution.py:72
  90.4 5.4 %assemble.3 = (bf16[16,2,24,2304]{3,2,1,0:T(8,128)(2,1)}, bf16[16,2,24,768]{3,2,1,0:T(8,128)(2,1)}, bf16[16,2,24,128]{3,2,1,0:T(8,128)(2,1)}) custom-call(s32[3,16]{1,0:T(4,128)} %get-tuple-element.527.idx_ref, bf16[8,24,3200]{2,1,0:T(8,128)(2,1)} %copy-done.4, bf16[8,24,3200]{2,1,0:T(8,128)(2,1)} %collective-permute-done.6.refs_1_, ...), custom_call_target="tpu_custom_call" | custom-call | bytes 9830400 | tf_op jit(solution)/shard_map/assemble/pallas_call | solution.py:118
  104.0 2.9 collective-permute-start.17
  106.9 8.5 %add_convert_fusion.qkv_ref = bf16[1024,2304]{1,0:T(8,128)(2,1)} fusion(bf16[1024,768]{1,0:T(8,128)(2,1)} %constant_dynamic-update-slice_fusion.left_ref, bf16[768,2304]{1,0:T(8,128)(2,1)} %bitcast.135, f32[2304]{0:T(1024)S(1)} %pad_maximum_fusion.17), kind=kOutput, calls=%fused_computation.4 | convolution fusion | flops 3628597248 | bytes 9839616 | tf_op jit(solution)/shard_map/dot_general | solution.py:76
  118.8 3.1 compare_select_fusion.1
  123.1 11.1 %attention.1 = (bf16[1024,768]{1,0:T(8,128)(2,1)}, bf16[4,12,256,256]{3,2,1,0:T(8,128)(2,1)}) custom-call(bf16[1024,2304]{1,0:T(8,128)(2,1)} %add_convert_fusion.qkv_ref, s32[1024,1]{1,0:T(8,128)} %fusion.13.qid_ref, s32[4,1,256]{2,1,0:T(1,128)} %compare_select_fusion.kid_ref), custom_call_target="tpu_custom_call" | custom-call | flops 1610612736 | bytes 12582912 | tf_op jit(solution)/shard_map/attention/pallas_call | solution.py:323
  136.1 2.8 collective-permute-start.24
  138.9 3.3 fusion.48
  142.2 4.8 %assemble.4 = bf16[16,2,24,3072]{3,2,1,0:T(8,128)(2,1)} custom-call(s32[3,16]{1,0:T(4,128)} %get-tuple-element.527.idx_ref, bf16[8,24,3072]{2,1,0:T(8,128)(2,1)} %copy-done.5, bf16[8,24,3072]{2,1,0:T(8,128)(2,1)} %collective-permute-done.15.refs_1_, bf16[8,24,3072]{2,1,0:T(8,128)(2,1)} %copy-done.19, bf16[8,24,3072]{2,1,0:T(8,128)(2,1)} %copy-done.21), custom_call_target="tpu_custom_call" | custom-call | bytes 9437184 | tf_op jit(solution)/shard_map/assemble/pallas_call | solution.py:118
  167.7 2.8 collective-permute-start.26
  170.4 17.0 %expand.1 = (bf16[1024,3072]{1,0:T(8,128)(2,1)}, bf16[1024,3072]{1,0:T(8,128)(2,1)}) custom-call(bf16[1024,768]{1,0:T(8,128)(2,1)} %fusion.5.mid_ref.left_ref, bf16[768,3072]{1,0:T(8,128)(2,1)} %bitcast.111, f32[1,3072]{1,0:T(1,128)} %reshape.718.b_ref), custom_call_target="tpu_custom_call" | custom-call | flops 4831838208 | bytes 18874368 | tf_op jit(solution)/shard_map/expand/pallas_call | solution.py:436
  187.5 4.9 %assemble.5 = bf16[16,2,96,768]{3,2,1,0:T(8,128)(2,1)} custom-call(s32[3,16]{1,0:T(4,128)} %get-tuple-element.527.idx_ref, bf16[8,96,768]{2,1,0:T(8,128)(2,1)} %copy-done.6, bf16[8,96,768]{2,1,0:T(8,128)(2,1)} %collective-permute-done.22.refs_1_, bf16[8,96,768]{2,1,0:T(8,128)(2,1)} %copy-done.20, bf16[8,96,768]{2,1,0:T(8,128)(2,1)} %collective-permute-done.25.refs_3_), custom_call_target="tpu_custom_call" | custom-call | bytes 9437184 | tf_op jit(solution)/shard_map/assemble/pallas_call | solution.py:118
  192.4 8.8 %fusion.49 = (f32[1024]{0:T(1024)S(1)}, f32[1024,768]{1,0:T(8,128)S(1)}) fusion(f32[768]{0:T(1024)S(1)} %copy-done.90, bf16[1024,3072]{1,0:T(8,128)(2,1)} %get-tuple-element.281.left_ref, bf16[3072,768]{1,0:T(8,128)(2,1)} %bitcast.113, f32[768]{0:T(1024)S(1)} %copy-done.77, f32[768]{0:T(1024)S(1)} %copy-done.64, f32[1024]{0:T(1024)S(1)} %copy-done.67, ...), kind=kOutput, calls=%fused_computation.248 | convolution fusion | flops 4837342208 | bytes 17323008 | tf_op jit(solution)/shard_map/dot_general | solution.py:76
  206.0 3.2 collective-permute-done.27
  210.0 3.2 collective-permute-done.28
  219.0 4.0 collective-permute-done.30
  231.8 4.5 multiply_reduce_fusion
  236.4 4.2 convert_reduce_fusion
  240.6 10.1 %tall_grad.1 = (bf16[16,96,768]{2,1,0:T(8,128)(2,1)}, bf16[16,96,768]{2,1,0:T(8,128)(2,1)}) custom-call(s32[3,16]{1,0:T(4,128)} %get-tuple-element.528.table_ref, bf16[1024,3072]{1,0:T(8,128)(2,1)} %get-tuple-element.281.left_ref, bf16[1024,768]{1,0:T(8,128)(2,1)} %get-tuple-element.294.right_ref.grad_ref), custom_call_target="tpu_custom_call" | custom-call | flops 4831838208 | bytes 12582912 | tf_op jit(solution)/shard_map/tall_grad/pallas_call | solution.py:224
  251.0 11.7 %hidden_grad.1 = (bf16[1024,3072]{1,0:T(8,128)(2,1)}, f32[1,3072]{1,0:T(1,128)}) custom-call(bf16[1024,768]{1,0:T(8,128)(2,1)} %get-tuple-element.294.right_ref.grad_ref, bf16[3072,768]{1,0:T(8,128)(2,1)} %bitcast.114, bf16[1024,3072]{1,0:T(8,128)(2,1)} %get-tuple-element.295.slope_ref), custom_call_target="tpu_custom_call" | custom-call | flops 4831838208 | bytes 18874368 | tf_op jit(solution)/shard_map/hidden_grad/pallas_call | solution.py:270
  262.8 2.8 collective-permute-start.37
  265.7 9.8 %weight_grad.3 = (bf16[16,24,3072]{2,1,0:T(8,128)(2,1)}, bf16[16,24,3072]{2,1,0:T(8,128)(2,1)}) custom-call(s32[3,16]{1,0:T(4,128)} %get-tuple-element.528.table_ref, bf16[1024,768]{1,0:T(8,128)(2,1)} %fusion.5.mid_ref.left_ref, bf16[1024,3072]{1,0:T(8,128)(2,1)} %get-tuple-element.312.right_ref), custom_call_target="tpu_custom_call" | custom-call | flops 4831838208 | bytes 12582912 | tf_op jit(solution)/shard_map/weight_grad/pallas_call | solution.py:184
  287.2 8.6 %convolution_add_fusion = f32[1024,768]{1,0:T(8,128)S(1)} fusion(f32[1024,768]{1,0:T(8,128)S(1)} %copy-done.9, bf16[1024,3072]{1,0:T(8,128)(2,1)} %get-tuple-element.312.right_ref, bf16[768,3072]{1,0:T(8,128)(2,1)} %bitcast.112), kind=kOutput, calls=%fused_computation.39 | convolution fusion | flops 4832624640 | bytes 17301504 | tf_op jit(solution)/shard_map/dot_general | solution.py:76
  298.4 3.6 collective-permute-done.36
  313.8 5.1 %weight_grad.4 = (bf16[16,24,768]{2,1,0:T(8,128)(2,1)}, bf16[16,24,768]{2,1,0:T(8,128)(2,1)}) custom-call(s32[3,16]{1,0:T(4,128)} %get-tuple-element.528.table_ref, bf16[1024,768]{1,0:T(8,128)(2,1)} %get-tuple-element.260.left_ref, bf16[1024,768]{1,0:T(8,128)(2,1)} %copy-done.13), custom_call_target="tpu_custom_call" | custom-call | flops 1207959552 | bytes 4325376 | tf_op jit(solution)/shard_map/weight_grad/pallas_call | solution.py:184
  326.9 10.5 %attention_back.2 = (bf16[1024,2304]{1,0:T(8,128)(2,1)}, f32[1,2304]{1,0:T(1,128)}) custom-call(bf16[1024,2304]{1,0:T(8,128)(2,1)} %add_convert_fusion.qkv_ref, bf16[4,12,256,256]{3,2,1,0:T(8,128)(2,1)} %get-tuple-element.339.probs_ref, bf16[1024,768]{1,0:T(8,128)(2,1)} %convolution_convert_fusion.grad_ref), custom_call_target="tpu_custom_call" | custom-call | flops 1610612736 | bytes 8650752 | tf_op jit(solution)/shard_map/attention_back/pallas_call | solution.py:397
  340.4 11.0 %attention_back.3 = (bf16[1024,2304]{1,0:T(8,128)(2,1)}, f32[1,2304]{1,0:T(1,128)}) custom-call(bf16[1024,2304]{1,0:T(8,128)(2,1)} %add_convert_fusion.qkv_ref, bf16[4,12,256,256]{3,2,1,0:T(8,128)(2,1)} %get-tuple-element.339.probs_ref, bf16[1024,768]{1,0:T(8,128)(2,1)} %convolution_convert_fusion.grad_ref, ...), custom_call_target="tpu_custom_call", output_to_operand_aliasing={{0}: (3, {})} | custom-call | flops 1610612736 | bytes 8650752 | tf_op jit(solution)/shard_map/attention_back/pallas_call | solution.py:397
  364.0 4.0 fusion.10
  369.0 3.9 collective-permute-done.46
  379.1 9.0 %weight_grad.5 = (bf16[16,24,2432]{2,1,0:T(8,128)(2,1)}, bf16[16,24,2432]{2,1,0:T(8,128)(2,1)}) custom-call(s32[3,16]{1,0:T(4,128)} %get-tuple-element.528.table_ref, bf16[1024,768]{1,0:T(8,128)(2,1)} %constant_dynamic-update-slice_fusion.left_ref, bf16[1024,2304]{1,0:T(8,128)(2,1)} %get-tuple-element.382.right_ref, f32[768,128]{1,0:T(8,128)} %maximum_maximum_fusion.refs_0_), custom_call_target="tpu_custom_call" | custom-call | flops 3623878656 | bytes 9830400 | tf_op jit(solution)/shard_map/weight_grad/pallas_call | solution.py:184
  396.4 2.9 collective-permute-start.53
  400.6 4.2 slice_add_fusion
  404.9 7.9 %collective-permute-done.53 = bf16[128,768]{1,0:T(8,128)(2,1)S(1)} collective-permute-done((bf16[128,768]{1,0:T(8,128)(2,1)}, bf16[128,768]{1,0:T(8,128)(2,1)S(1)}, u32[]{:S(2)}, u32[]{:S(2)}) %collective-permute-start.53) | collective-permute-done | bytes 196640 | tf_op jit(solution)/shard_map/ppermute | solution.py:72
  416.7 9.1 %collective-permute-done.55 = bf16[128,768]{1,0:T(8,128)(2,1)S(1)} collective-permute-done((bf16[128,768]{1,0:T(8,128)(2,1)S(1)}, bf16[128,768]{1,0:T(8,128)(2,1)S(1)}, u32[]{:S(2)}, u32[]{:S(2)}) %collective-permute-start.55) | collective-permute-done | bytes 196640 | tf_op jit(solution)/shard_map/ppermute | solution.py:72
  429.8 5.7 %collective-permute-done.57 = bf16[4,24,2432]{2,1,0:T(8,128)(2,1)S(1)} collective-permute-done((bf16[4,24,2432]{2,1,0:T(8,128)(2,1)S(1)}, bf16[4,24,2432]{2,1,0:T(8,128)(2,1)S(1)}, u32[]{:S(2)}, u32[]{:S(2)}) %collective-permute-start.57) | collective-permute-done | bytes 466976 | tf_op jit(solution)/shard_map/ppermute | solution.py:66
  437.2 2.9 collective-permute-start.56
  440.1 4.6 %collective-permute-done.58 = bf16[2,24,2432]{2,1,0:T(8,128)(2,1)S(1)} collective-permute-done((bf16[2,24,2432]{2,1,0:T(8,128)(2,1)S(1)}, bf16[2,24,2432]{2,1,0:T(8,128)(2,1)S(1)}, u32[]{:S(2)}, u32[]{:S(2)}) %collective-permute-start.58) | collective-permute-done | bytes 233504 | tf_op jit(solution)/shard_map/ppermute | solution.py:66
  444.9 6.4 %collective-permute-done.56 = bf16[128,768]{1,0:T(8,128)(2,1)S(1)} collective-permute-done((bf16[128,768]{1,0:T(8,128)(2,1)S(1)}, bf16[128,768]{1,0:T(8,128)(2,1)S(1)}, u32[]{:S(2)}, u32[]{:S(2)}) %collective-permute-start.56) | collective-permute-done | bytes 196640 | tf_op jit(solution)/shard_map/ppermute | solution.py:72
  451.2 2.8 convert_select_fusion
  (479 shorter events, 170.7 us)
Async XLA Ops:
  3.4 11.4 %collective-permute-start = (bf16[1,24,3200]{2,1,0:T(8,128)(2,1)S(1)}, bf16[1,24,3200]{2,1,0:T(8,128)(2,1)S(1)}, u32[]{:S(2)}, u32[]{:S(2)}) collective-permute-start(bf16[1,24,3200]{2,1,0:T(8,128)(2,1)S(1)} %get-tuple-element.502), channel_id=1, source_target_pairs={{0,4},{1,5},{2,6},{3,7},{4,0},{5,1},{6,2},{7,3},{8,12},{9,13},{10,... | collective-permute-start | bytes 460808 | tf_op jit(solution)/shard_map/ppermute | solution.py:66
  19.8 11.3 %collective-permute-start.1 = (bf16[2,24,3200]{2,1,0:T(8,128)(2,1)S(1)}, bf16[2,24,3200]{2,1,0:T(8,128)(2,1)S(1)}, u32[]{:S(2)}, u32[]{:S(2)}) collective-permute-start(bf16[2,24,3200]{2,1,0:T(8,128)(2,1)S(1)} %pad_maximum_fusion.9), channel_id=1, source_target_pairs={{0,2},{1,3},{2,0},{3,1},{4,6},{5,7},{6,4},{7,5},{8,10},{9,11},{10,... | collective-permute-start | bytes 921608 | tf_op jit(solution)/shard_map/ppermute | solution.py:66
  31.5 11.0 %collective-permute-start.4 = (bf16[2,24,3072]{2,1,0:T(8,128)(2,1)S(1)}, bf16[2,24,3072]{2,1,0:T(8,128)(2,1)S(1)}, u32[]{:S(2)}, u32[]{:S(2)}) collective-permute-start(bf16[2,24,3072]{2,1,0:T(8,128)(2,1)S(1)} %pad_maximum_fusion.10), channel_id=1, source_target_pairs={{0,2},{1,3},{2,0},{3,1},{4,6},{5,7},{6,4},{7,5},{8,10},{9,11},{10,... | collective-permute-start | bytes 884744 | tf_op jit(solution)/shard_map/ppermute | solution.py:66
  33.3 10.2 %collective-permute-start.3 = (bf16[4,24,3200]{2,1,0:T(8,128)(2,1)S(1)}, bf16[4,24,3200]{2,1,0:T(8,128)(2,1)S(1)}, u32[]{:S(2)}, u32[]{:S(2)}) collective-permute-start(bf16[4,24,3200]{2,1,0:T(8,128)(2,1)S(1)} %pad_maximum_fusion.4), channel_id=1, source_target_pairs={{0,8},{1,17},{2,10},{3,19},{4,12},{5,21},{6,14},{7,23},{8,0},{9,25... | collective-permute-start | bytes 1843208 | tf_op jit(solution)/shard_map/ppermute | solution.py:66
  43.6 27.0 %collective-permute-start.7 = (bf16[8,24,3200]{2,1,0:T(8,128)(2,1)S(1)}, bf16[8,24,3200]{2,1,0:T(8,128)(2,1)}, u32[]{:S(2)}, u32[]{:S(2)}) collective-permute-start(bf16[8,24,3200]{2,1,0:T(8,128)(2,1)S(1)} %pad_maximum_fusion.refs_0_), channel_id=1, source_target_pairs={{0,1},{1,0},{2,3},{3,2},{4,5},{5,4},{6,7},{7,6},{8,9},{9,8},{10,11... | collective-permute-start | bytes 3686408 | tf_op jit(solution)/shard_map/ppermute | solution.py:69
  43.7 26.9 %collective-permute-start.6 = (bf16[8,24,3200]{2,1,0:T(8,128)(2,1)S(1)}, bf16[8,24,3200]{2,1,0:T(8,128)(2,1)}, u32[]{:S(2)}, u32[]{:S(2)}) collective-permute-start(bf16[8,24,3200]{2,1,0:T(8,128)(2,1)S(1)} %pad_maximum_fusion.refs_0_), channel_id=1, source_target_pairs={{0,16},{1,9},{2,18},{3,11},{4,20},{5,13},{6,22},{7,15},{8,24},{9,1... | collective-permute-start | bytes 3686408 | tf_op jit(solution)/shard_map/ppermute | solution.py:66
  47.5 14.4 %collective-permute-start.8 = (bf16[2,96,768]{2,1,0:T(8,128)(2,1)}, bf16[2,96,768]{2,1,0:T(8,128)(2,1)S(1)}, u32[]{:S(2)}, u32[]{:S(2)}) collective-permute-start(bf16[2,96,768]{2,1,0:T(8,128)(2,1)} %pad_maximum_fusion.11), channel_id=1, source_target_pairs={{0,2},{1,3},{2,0},{3,1},{4,6},{5,7},{6,4},{7,5},{8,10},{9,11},{10,... | collective-permute-start | bytes 884744 | tf_op jit(solution)/shard_map/ppermute | solution.py:66
  49.1 14.2 %collective-permute-start.9 = (bf16[128,768]{1,0:T(8,128)(2,1)}, bf16[128,768]{1,0:T(8,128)(2,1)S(1)}, u32[]{:S(2)}, u32[]{:S(2)}) collective-permute-start(bf16[128,768]{1,0:T(8,128)(2,1)} %get-tuple-element.220), channel_id=1, source_target_pairs={{0,4},{1,5},{2,6},{3,7},{4,0},{5,1},{6,2},{7,3},{8,12},{9,13},{10,... | collective-permute-start | bytes 589832 | tf_op jit(solution)/shard_map/ppermute | solution.py:72
  52.8 17.8 %collective-permute-start.10 = (bf16[128,768]{1,0:T(8,128)(2,1)}, bf16[128,768]{1,0:T(8,128)(2,1)S(1)}, u32[]{:S(2)}, u32[]{:S(2)}) collective-permute-start(bf16[128,768]{1,0:T(8,128)(2,1)} %get-tuple-element.221), channel_id=1, source_target_pairs={{0,4},{1,5},{2,6},{3,7},{4,0},{5,1},{6,2},{7,3},{8,12},{9,13},{10,... | collective-permute-start | bytes 589832 | tf_op jit(solution)/shard_map/ppermute | solution.py:72
  61.9 89.5 %collective-permute-start.32 = (s32[64]{0:T(128)}, s32[64]{0:T(128)}, u32[]{:S(2)}, u32[]{:S(2)}) collective-permute-start(s32[64]{0:T(128)} %param.23), channel_id=1, source_target_pairs={{0,8},{8,0},{16,24},{24,16},{1,9},{9,1},{17,25},{25,17},{2,10},{10... | collective-permute-start | bytes 776 | tf_op jit(solution)/shard_map/ppermute | solution.py:692
  63.3 59.1 %collective-permute-start.18 = (s32[512]{0:T(512)}, s32[512]{0:T(512)S(1)}, u32[]{:S(2)}, u32[]{:S(2)}) collective-permute-start(s32[512]{0:T(512)} %get-tuple-element.512), channel_id=1, source_target_pairs={{0,4},{1,5},{2,6},{3,7},{4,0},{5,1},{6,2},{7,3},{8,12},{9,13},{10,... | collective-permute-start | bytes 6152 | tf_op jit(solution)/shard_map/ppermute | solution.py:72
  70.7 18.8 %collective-permute-start.11 = (bf16[8,24,3200]{2,1,0:T(8,128)(2,1)}, bf16[8,24,3200]{2,1,0:T(8,128)(2,1)}, u32[]{:S(2)}, u32[]{:S(2)}) collective-permute-start(bf16[8,24,3200]{2,1,0:T(8,128)(2,1)} %collective-permute-done.6.refs_1_), channel_id=1, source_target_pairs={{0,1},{1,0},{2,3},{3,2},{4,5},{5,4},{6,7},{7,6},{8,9},{9,8},{10,11... | collective-permute-start | bytes 3686408 | tf_op jit(solution)/shard_map/ppermute | solution.py:69
  72.5 10.2 %collective-permute-start.12 = (bf16[4,24,3072]{2,1,0:T(8,128)(2,1)}, bf16[4,24,3072]{2,1,0:T(8,128)(2,1)}, u32[]{:S(2)}, u32[]{:S(2)}) collective-permute-start(bf16[4,24,3072]{2,1,0:T(8,128)(2,1)} %pad_maximum_fusion.5), channel_id=1, source_target_pairs={{0,8},{1,17},{2,10},{3,19},{4,12},{5,21},{6,14},{7,23},{8,0},{9,25... | collective-permute-start | bytes 1769480 | tf_op jit(solution)/shard_map/ppermute | solution.py:66
  75.8 13.0 %collective-permute-start.13 = (bf16[128,768]{1,0:T(8,128)(2,1)}, bf16[128,768]{1,0:T(8,128)(2,1)S(1)}, u32[]{:S(2)}, u32[]{:S(2)}) collective-permute-start(bf16[128,768]{1,0:T(8,128)(2,1)} %get-tuple-element.230), channel_id=1, source_target_pairs={{0,4},{1,5},{2,6},{3,7},{4,0},{5,1},{6,2},{7,3},{8,12},{9,13},{10,... | collective-permute-start | bytes 589832 | tf_op jit(solution)/shard_map/ppermute | solution.py:72
  89.5 26.7 %collective-permute-start.16 = (bf16[8,24,3072]{2,1,0:T(8,128)(2,1)S(1)}, bf16[8,24,3072]{2,1,0:T(8,128)(2,1)S(1)}, u32[]{:S(2)}, u32[]{:S(2)}) collective-permute-start(bf16[8,24,3072]{2,1,0:T(8,128)(2,1)S(1)} %pad_maximum_fusion.1.refs_0_), channel_id=1, source_target_pairs={{0,1},{1,0},{2,3},{3,2},{4,5},{5,4},{6,7},{7,6},{8,9},{9,8},{10,11... | collective-permute-start | bytes 3538952 | tf_op jit(solution)/shard_map/ppermute | solution.py:69
  89.5 26.7 %collective-permute-start.15 = (bf16[8,24,3072]{2,1,0:T(8,128)(2,1)S(1)}, bf16[8,24,3072]{2,1,0:T(8,128)(2,1)}, u32[]{:S(2)}, u32[]{:S(2)}) collective-permute-start(bf16[8,24,3072]{2,1,0:T(8,128)(2,1)S(1)} %pad_maximum_fusion.1.refs_0_), channel_id=1, source_target_pairs={{0,16},{1,9},{2,18},{3,11},{4,20},{5,13},{6,22},{7,15},{8,24},{9,1... | collective-permute-start | bytes 3538952 | tf_op jit(solution)/shard_map/ppermute | solution.py:66
  90.4 12.0 %collective-permute-start.14 = (bf16[128,768]{1,0:T(8,128)(2,1)}, bf16[128,768]{1,0:T(8,128)(2,1)}, u32[]{:S(2)}, u32[]{:S(2)}) collective-permute-start(bf16[128,768]{1,0:T(8,128)(2,1)} %get-tuple-element.240), channel_id=1, source_target_pairs={{0,4},{1,5},{2,6},{3,7},{4,0},{5,1},{6,2},{7,3},{8,12},{9,13},{10,... | collective-permute-start | bytes 589832 | tf_op jit(solution)/shard_map/ppermute | solution.py:72
  104.0 12.2 %collective-permute-start.17 = (bf16[128,768]{1,0:T(8,128)(2,1)S(1)}, bf16[128,768]{1,0:T(8,128)(2,1)S(1)}, u32[]{:S(2)}, u32[]{:S(2)}) collective-permute-start(bf16[128,768]{1,0:T(8,128)(2,1)S(1)} %get-tuple-element.246), channel_id=1, source_target_pairs={{0,4},{1,5},{2,6},{3,7},{4,0},{5,1},{6,2},{7,3},{8,12},{9,13},{10,... | collective-permute-start | bytes 589832 | tf_op jit(solution)/shard_map/ppermute | solution.py:72
  116.2 18.2 %collective-permute-start.19 = (bf16[8,24,3072]{2,1,0:T(8,128)(2,1)}, bf16[8,24,3072]{2,1,0:T(8,128)(2,1)S(1)}, u32[]{:S(2)}, u32[]{:S(2)}) collective-permute-start(bf16[8,24,3072]{2,1,0:T(8,128)(2,1)} %collective-permute-done.15.refs_1_), channel_id=1, source_target_pairs={{0,1},{1,0},{2,3},{3,2},{4,5},{5,4},{6,7},{7,6},{8,9},{9,8},{10,11... | collective-permute-start | bytes 3538952 | tf_op jit(solution)/shard_map/ppermute | solution.py:69
  117.7 16.6 %collective-permute-start.20 = (bf16[4,96,768]{2,1,0:T(8,128)(2,1)S(1)}, bf16[4,96,768]{2,1,0:T(8,128)(2,1)S(1)}, u32[]{:S(2)}, u32[]{:S(2)}) collective-permute-start(bf16[4,96,768]{2,1,0:T(8,128)(2,1)S(1)} %copy-done.31), channel_id=1, source_target_pairs={{0,8},{1,17},{2,10},{3,19},{4,12},{5,21},{6,14},{7,23},{8,0},{9,25... | collective-permute-start | bytes 1769480 | tf_op jit(solution)/shard_map/ppermute | solution.py:66
  123.1 11.3 %collective-permute-start.21 = (bf16[128,768]{1,0:T(8,128)(2,1)S(1)}, bf16[128,768]{1,0:T(8,128)(2,1)S(1)}, u32[]{:S(2)}, u32[]{:S(2)}) collective-permute-start(bf16[128,768]{1,0:T(8,128)(2,1)S(1)} %get-tuple-element.257), channel_id=1, source_target_pairs={{0,4},{1,5},{2,6},{3,7},{4,0},{5,1},{6,2},{7,3},{8,12},{9,13},{10,... | collective-permute-start | bytes 589832 | tf_op jit(solution)/shard_map/ppermute | solution.py:72
  135.1 14.2 %collective-permute-start.23 = (bf16[8,96,768]{2,1,0:T(8,128)(2,1)S(1)}, bf16[8,96,768]{2,1,0:T(8,128)(2,1)S(1)}, u32[]{:S(2)}, u32[]{:S(2)}) collective-permute-start(bf16[8,96,768]{2,1,0:T(8,128)(2,1)S(1)} %pad_maximum_fusion.2.refs_0_), channel_id=1, source_target_pairs={{0,1},{1,0},{2,3},{3,2},{4,5},{5,4},{6,7},{7,6},{8,9},{9,8},{10,11... | collective-permute-start | bytes 3538952 | tf_op jit(solution)/shard_map/ppermute | solution.py:69
  135.1 16.3 %collective-permute-start.22 = (bf16[8,96,768]{2,1,0:T(8,128)(2,1)S(1)}, bf16[8,96,768]{2,1,0:T(8,128)(2,1)}, u32[]{:S(2)}, u32[]{:S(2)}) collective-permute-start(bf16[8,96,768]{2,1,0:T(8,128)(2,1)S(1)} %pad_maximum_fusion.2.refs_0_), channel_id=1, source_target_pairs={{0,16},{1,9},{2,18},{3,11},{4,20},{5,13},{6,22},{7,15},{8,24},{9,1... | collective-permute-start | bytes 3538952 | tf_op jit(solution)/shard_map/ppermute | solution.py:66
  136.1 13.1 %collective-permute-start.24 = (bf16[128,768]{1,0:T(8,128)(2,1)}, bf16[128,768]{1,0:T(8,128)(2,1)S(1)}, u32[]{:S(2)}, u32[]{:S(2)}) collective-permute-start(bf16[128,768]{1,0:T(8,128)(2,1)} %get-tuple-element.269), channel_id=1, source_target_pairs={{0,4},{1,5},{2,6},{3,7},{4,0},{5,1},{6,2},{7,3},{8,12},{9,13},{10,... | collective-permute-start | bytes 589832 | tf_op jit(solution)/shard_map/ppermute | solution.py:72
  151.4 36.0 %collective-permute-start.25 = (bf16[8,96,768]{2,1,0:T(8,128)(2,1)}, bf16[8,96,768]{2,1,0:T(8,128)(2,1)}, u32[]{:S(2)}, u32[]{:S(2)}) collective-permute-start(bf16[8,96,768]{2,1,0:T(8,128)(2,1)} %collective-permute-done.22.refs_1_), channel_id=1, source_target_pairs={{0,1},{1,0},{2,3},{3,2},{4,5},{5,4},{6,7},{7,6},{8,9},{9,8},{10,11... | collective-permute-start | bytes 3538952 | tf_op jit(solution)/shard_map/ppermute | solution.py:69
  167.7 19.7 %collective-permute-start.26 = (bf16[128,768]{1,0:T(8,128)(2,1)}, bf16[128,768]{1,0:T(8,128)(2,1)S(1)}, u32[]{:S(2)}, u32[]{:S(2)}) collective-permute-start(bf16[128,768]{1,0:T(8,128)(2,1)} %get-tuple-element.280), channel_id=1, source_target_pairs={{0,4},{1,5},{2,6},{3,7},{4,0},{5,1},{6,2},{7,3},{8,12},{9,13},{10,... | collective-permute-start | bytes 589832 | tf_op jit(solution)/shard_map/ppermute | solution.py:72
  250.7 12.0 %collective-permute-start.34 = (bf16[16,96,768]{2,1,0:T(8,128)(2,1)}, bf16[16,96,768]{2,1,0:T(8,128)(2,1)S(1)}, u32[]{:S(2)}, u32[]{:S(2)}) collective-permute-start(bf16[16,96,768]{2,1,0:T(8,128)(2,1)} %get-tuple-element.293), channel_id=1, source_target_pairs={{0,1},{1,0},{2,3},{3,2},{4,5},{5,4},{6,7},{7,6},{8,9},{9,8},{10,11... | collective-permute-start | bytes 7077896 | tf_op jit(solution)/shard_map/ppermute | solution.py:69
  250.9 11.9 %collective-permute-start.35 = (bf16[128,768]{1,0:T(8,128)(2,1)S(1)}, bf16[128,768]{1,0:T(8,128)(2,1)S(1)}, u32[]{:S(2)}, u32[]{:S(2)}) collective-permute-start(bf16[128,768]{1,0:T(8,128)(2,1)S(1)} %copy-done.42), channel_id=1, source_target_pairs={{0,4},{1,5},{2,6},{3,7},{4,0},{5,1},{6,2},{7,3},{8,12},{9,13},{10,... | collective-permute-start | bytes 589832 | tf_op jit(solution)/shard_map/ppermute | solution.py:72
  262.8 12.6 %collective-permute-start.37 = (bf16[128,768]{1,0:T(8,128)(2,1)S(1)}, bf16[128,768]{1,0:T(8,128)(2,1)S(1)}, u32[]{:S(2)}, u32[]{:S(2)}) collective-permute-start(bf16[128,768]{1,0:T(8,128)(2,1)S(1)} %copy-done.41), channel_id=1, source_target_pairs={{0,4},{1,5},{2,6},{3,7},{4,0},{5,1},{6,2},{7,3},{8,12},{9,13},{10,... | collective-permute-start | bytes 589832 | tf_op jit(solution)/shard_map/ppermute | solution.py:72
  276.1 25.9 %collective-permute-start.38 = (bf16[16,24,3072]{2,1,0:T(8,128)(2,1)}, bf16[16,24,3072]{2,1,0:T(8,128)(2,1)}, u32[]{:S(2)}, u32[]{:S(2)}) collective-permute-start(bf16[16,24,3072]{2,1,0:T(8,128)(2,1)} %get-tuple-element.311), channel_id=1, source_target_pairs={{0,1},{1,0},{2,3},{3,2},{4,5},{5,4},{6,7},{7,6},{8,9},{9,8},{10,11... | collective-permute-start | bytes 7077896 | tf_op jit(solution)/shard_map/ppermute | solution.py:69
  285.8 16.3 %collective-permute-start.36 = (bf16[8,96,768]{2,1,0:T(8,128)(2,1)S(1)}, bf16[8,96,768]{2,1,0:T(8,128)(2,1)S(1)}, u32[]{:S(2)}, u32[]{:S(2)}) collective-permute-start(bf16[8,96,768]{2,1,0:T(8,128)(2,1)S(1)} %add_convert_fusion.2), channel_id=1, source_target_pairs={{0,16},{1,9},{2,18},{3,11},{4,20},{5,13},{6,22},{7,15},{8,24},{9,1... | collective-permute-start | bytes 3538952 | tf_op jit(solution)/shard_map/ppermute | solution.py:66
  286.9 11.5 %collective-permute-start.39 = (bf16[128,768]{1,0:T(8,128)(2,1)S(1)}, bf16[128,768]{1,0:T(8,128)(2,1)S(1)}, u32[]{:S(2)}, u32[]{:S(2)}) collective-permute-start(bf16[128,768]{1,0:T(8,128)(2,1)S(1)} %copy-done.39), channel_id=1, source_target_pairs={{0,4},{1,5},{2,6},{3,7},{4,0},{5,1},{6,2},{7,3},{8,12},{9,13},{10,... | collective-permute-start | bytes 589832 | tf_op jit(solution)/shard_map/ppermute | solution.py:72
  303.9 15.1 %collective-permute-start.41 = (bf16[128,768]{1,0:T(8,128)(2,1)S(1)}, bf16[128,768]{1,0:T(8,128)(2,1)}, u32[]{:S(2)}, u32[]{:S(2)}) collective-permute-start(bf16[128,768]{1,0:T(8,128)(2,1)S(1)} %copy-done.38), channel_id=1, source_target_pairs={{0,4},{1,5},{2,6},{3,7},{4,0},{5,1},{6,2},{7,3},{8,12},{9,13},{10,... | collective-permute-start | bytes 589832 | tf_op jit(solution)/shard_map/ppermute | solution.py:72
  306.5 12.5 %collective-permute-start.40 = (bf16[4,96,768]{2,1,0:T(8,128)(2,1)}, bf16[4,96,768]{2,1,0:T(8,128)(2,1)S(1)}, u32[]{:S(2)}, u32[]{:S(2)}) collective-permute-start(bf16[4,96,768]{2,1,0:T(8,128)(2,1)} %add_convert_fusion.5), channel_id=1, source_target_pairs={{0,8},{1,17},{2,10},{3,19},{4,12},{5,21},{6,14},{7,23},{8,0},{9,25... | collective-permute-start | bytes 1769480 | tf_op jit(solution)/shard_map/ppermute | solution.py:66
  320.5 17.0 %collective-permute-start.42 = (bf16[2,96,768]{2,1,0:T(8,128)(2,1)S(1)}, bf16[2,96,768]{2,1,0:T(8,128)(2,1)S(1)}, u32[]{:S(2)}, u32[]{:S(2)}) collective-permute-start(bf16[2,96,768]{2,1,0:T(8,128)(2,1)S(1)} %add_convert_fusion.9), channel_id=1, source_target_pairs={{0,2},{1,3},{2,0},{3,1},{4,6},{5,7},{6,4},{7,5},{8,10},{9,11},{10,... | collective-permute-start | bytes 884744 | tf_op jit(solution)/shard_map/ppermute | solution.py:66
  322.4 15.1 %collective-permute-start.43 = (bf16[16,24,768]{2,1,0:T(8,128)(2,1)}, bf16[16,24,768]{2,1,0:T(8,128)(2,1)S(1)}, u32[]{:S(2)}, u32[]{:S(2)}) collective-permute-start(bf16[16,24,768]{2,1,0:T(8,128)(2,1)} %get-tuple-element.338), channel_id=1, source_target_pairs={{0,1},{1,0},{2,3},{3,2},{4,5},{5,4},{6,7},{7,6},{8,9},{9,8},{10,11... | collective-permute-start | bytes 1769480 | tf_op jit(solution)/shard_map/ppermute | solution.py:69
  325.1 35.0 %collective-permute-start.45 = (bf16[8,24,3072]{2,1,0:T(8,128)(2,1)}, bf16[8,24,3072]{2,1,0:T(8,128)(2,1)}, u32[]{:S(2)}, u32[]{:S(2)}) collective-permute-start(bf16[8,24,3072]{2,1,0:T(8,128)(2,1)} %add_convert_fusion.1), channel_id=1, source_target_pairs={{0,16},{1,9},{2,18},{3,11},{4,20},{5,13},{6,22},{7,15},{8,24},{9,1... | collective-permute-start | bytes 3538952 | tf_op jit(solution)/shard_map/ppermute | solution.py:66
  339.6 18.1 %collective-permute-start.44 = (bf16[1,96,768]{2,1,0:T(8,128)(2,1)}, bf16[1,96,768]{2,1,0:T(8,128)(2,1)}, u32[]{:S(2)}, u32[]{:S(2)}) collective-permute-start(bf16[1,96,768]{2,1,0:T(8,128)(2,1)} %add_convert_fusion.13), channel_id=1, source_target_pairs={{0,4},{1,5},{2,6},{3,7},{4,0},{5,1},{6,2},{7,3},{8,12},{9,13},{10,... | collective-permute-start | bytes 442376 | tf_op jit(solution)/shard_map/ppermute | solution.py:66
  362.9 9.9 %collective-permute-start.46 = (bf16[4,24,3072]{2,1,0:T(8,128)(2,1)S(1)}, bf16[4,24,3072]{2,1,0:T(8,128)(2,1)S(1)}, u32[]{:S(2)}, u32[]{:S(2)}) collective-permute-start(bf16[4,24,3072]{2,1,0:T(8,128)(2,1)S(1)} %add_convert_fusion.4), channel_id=1, source_target_pairs={{0,8},{1,17},{2,10},{3,19},{4,12},{5,21},{6,14},{7,23},{8,0},{9,25... | collective-permute-start | bytes 1769480 | tf_op jit(solution)/shard_map/ppermute | solution.py:66
  373.7 14.5 %collective-permute-start.49 = (bf16[4,24,768]{2,1,0:T(8,128)(2,1)}, bf16[4,24,768]{2,1,0:T(8,128)(2,1)}, u32[]{:S(2)}, u32[]{:S(2)}) collective-permute-start(bf16[4,24,768]{2,1,0:T(8,128)(2,1)} %add_convert_fusion.12), channel_id=1, source_target_pairs={{0,8},{1,17},{2,10},{3,19},{4,12},{5,21},{6,14},{7,23},{8,0},{9,25... | collective-permute-start | bytes 442376 | tf_op jit(solution)/shard_map/ppermute | solution.py:66
  374.7 13.4 %collective-permute-start.50 = (bf16[128,768]{1,0:T(8,128)(2,1)}, bf16[128,768]{1,0:T(8,128)(2,1)}, u32[]{:S(2)}, u32[]{:S(2)}) collective-permute-start(bf16[128,768]{1,0:T(8,128)(2,1)} %get-tuple-element.372), channel_id=1, source_target_pairs={{0,4},{1,5},{2,6},{3,7},{4,0},{5,1},{6,2},{7,3},{8,12},{9,13},{10,... | collective-permute-start | bytes 589832 | tf_op jit(solution)/shard_map/ppermute | solution.py:72
  379.0 11.5 %collective-permute-start.48 = (bf16[2,24,3072]{2,1,0:T(8,128)(2,1)}, bf16[2,24,3072]{2,1,0:T(8,128)(2,1)S(1)}, u32[]{:S(2)}, u32[]{:S(2)}) collective-permute-start(bf16[2,24,3072]{2,1,0:T(8,128)(2,1)} %add_convert_fusion.7), channel_id=1, source_target_pairs={{0,2},{1,3},{2,0},{3,1},{4,6},{5,7},{6,4},{7,5},{8,10},{9,11},{10,... | collective-permute-start | bytes 884744 | tf_op jit(solution)/shard_map/ppermute | solution.py:66
  390.5 22.3 %collective-permute-start.51 = (bf16[16,24,2432]{2,1,0:T(8,128)(2,1)}, bf16[16,24,2432]{2,1,0:T(8,128)(2,1)S(1)}, u32[]{:S(2)}, u32[]{:S(2)}) collective-permute-start(bf16[16,24,2432]{2,1,0:T(8,128)(2,1)} %get-tuple-element.377), channel_id=1, source_target_pairs={{0,1},{1,0},{2,3},{3,2},{4,5},{5,4},{6,7},{7,6},{8,9},{9,8},{10,11... | collective-permute-start | bytes 5603336 | tf_op jit(solution)/shard_map/ppermute | solution.py:69
  396.4 16.4 %collective-permute-start.53 = (bf16[128,768]{1,0:T(8,128)(2,1)}, bf16[128,768]{1,0:T(8,128)(2,1)S(1)}, u32[]{:S(2)}, u32[]{:S(2)}) collective-permute-start(bf16[128,768]{1,0:T(8,128)(2,1)} %get-tuple-element.384), channel_id=1, source_target_pairs={{0,4},{1,5},{2,6},{3,7},{4,0},{5,1},{6,2},{7,3},{8,12},{9,13},{10,... | collective-permute-start | bytes 589832 | tf_op jit(solution)/shard_map/ppermute | solution.py:72
  404.7 10.7 %collective-permute-start.61 = (bf16[1,24,3072]{2,1,0:T(8,128)(2,1)S(1)}, bf16[1,24,3072]{2,1,0:T(8,128)(2,1)S(1)}, u32[]{:S(2)}, u32[]{:S(2)}) collective-permute-start(bf16[1,24,3072]{2,1,0:T(8,128)(2,1)S(1)} %add_convert_fusion.11), channel_id=1, source_target_pairs={{0,4},{1,5},{2,6},{3,7},{4,0},{5,1},{6,2},{7,3},{8,12},{9,13},{10,... | collective-permute-start | bytes 442376 | tf_op jit(solution)/shard_map/ppermute | solution.py:66
  413.0 13.6 %collective-permute-start.54 = (bf16[8,24,2432]{2,1,0:T(8,128)(2,1)S(1)}, bf16[8,24,2432]{2,1,0:T(8,128)(2,1)S(1)}, u32[]{:S(2)}, u32[]{:S(2)}) collective-permute-start(bf16[8,24,2432]{2,1,0:T(8,128)(2,1)S(1)} %add_convert_fusion.3), channel_id=1, source_target_pairs={{0,16},{1,9},{2,18},{3,11},{4,20},{5,13},{6,22},{7,15},{8,24},{9,1... | collective-permute-start | bytes 2801672 | tf_op jit(solution)/shard_map/ppermute | solution.py:66
  415.5 10.3 %collective-permute-start.55 = (bf16[128,768]{1,0:T(8,128)(2,1)S(1)}, bf16[128,768]{1,0:T(8,128)(2,1)S(1)}, u32[]{:S(2)}, u32[]{:S(2)}) collective-permute-start(bf16[128,768]{1,0:T(8,128)(2,1)S(1)} %copy-done.43), channel_id=1, source_target_pairs={{0,4},{1,5},{2,6},{3,7},{4,0},{5,1},{6,2},{7,3},{8,12},{9,13},{10,... | collective-permute-start | bytes 589832 | tf_op jit(solution)/shard_map/ppermute | solution.py:72
  437.2 14.0 %collective-permute-start.56 = (bf16[128,768]{1,0:T(8,128)(2,1)S(1)}, bf16[128,768]{1,0:T(8,128)(2,1)S(1)}, u32[]{:S(2)}, u32[]{:S(2)}) collective-permute-start(bf16[128,768]{1,0:T(8,128)(2,1)S(1)} %copy-done.40), channel_id=1, source_target_pairs={{0,4},{1,5},{2,6},{3,7},{4,0},{5,1},{6,2},{7,3},{8,12},{9,13},{10,... | collective-permute-start | bytes 589832 | tf_op jit(solution)/shard_map/ppermute | solution.py:72
  (114 other events, 1092.9 us)

commit v3 on v2

--- a/solution.py
+++ b/solution.py
@@ -422,6 +422,182 @@
     )(qkv, probs, grad_context, *([into] if more else []))
 
 
+def join_kernel(*refs):
+    count = len(refs) - 2
+    sources, out, sem = refs[:count], refs[count], refs[count + 1]
+    copies, row = [], 0
+    for k, source in enumerate(sources):
+        rows = source.shape[0]
+        copies.append(
+            pltpu.make_async_copy(source, out.at[pl.ds(row, rows)], sem.at[k])
+        )
+        copies[-1].start()
+        row += rows
+    for copy in copies:
+        copy.wait()
+
+
+def join(pieces):
+    rows, width = sum(x.shape[0] for x in pieces), pieces[0].shape[1]
+    return pl.pallas_call(
+        join_kernel,
+        in_specs=[pl.BlockSpec(memory_space=pl.ANY)] * len(pieces),
+        out_specs=pl.BlockSpec(memory_space=pl.ANY),
+        out_shape=jax.ShapeDtypeStruct((rows, width), pieces[0].dtype),
+        scratch_shapes=[pltpu.SemaphoreType.DMA((len(pieces),))],
+        cost_estimate=pl.CostEstimate(
+            flops=0, bytes_accessed=4 * rows * width, transcendentals=0
+        ),
+        name="join",
+    )(*pieces)
+
+
+def deal_kernel(tower_ref, own_ref, *refs):
+    pieces, (q_ref, p_ref) = refs[:-2], refs[-2:]
+
+    def give(own_out, other_out):
+        own_out[...] = own_ref[...]
+        row = 0
+        for piece in pieces:
+            rows = piece.shape[0]
+            other_out[row : row + rows, :] = piece[...].astype(other_out.dtype)
+            row += rows
+
+    @pl.when(tower_ref[0] == 0)
+    def _():
+        give(q_ref, p_ref)
+
+    @pl.when(tower_ref[0] != 0)
+    def _():
+        give(p_ref, q_ref)
+
+
+def deal(tower, own, pieces):
+    rows, width = sum(x.shape[0] for x in pieces), own.shape[1]
+    shape = jax.ShapeDtypeStruct((rows, width), own.dtype)
+    return pl.pallas_call(
+        deal_kernel,
+        grid=(1,),
+        in_specs=[
+            pl.BlockSpec(memory_space=pltpu.SMEM),
+            pl.BlockSpec((rows, width), lambda i: (0, 0)),
+        ]
+        + [pl.BlockSpec(x.shape, lambda i: (0, 0)) for x in pieces],
+        out_specs=[pl.BlockSpec((rows, width), lambda i: (0, 0))] * 2,
+        out_shape=[shape] * 2,
+        compiler_params=pltpu.CompilerParams(vmem_limit_bytes=VMEM_LIMIT),
+        cost_estimate=pl.CostEstimate(
+            flops=0, bytes_accessed=12 * rows * width, transcendentals=0
+        ),
+        name="deal",
+    )(tower, own, *pieces)
+
+
+def add_sums(sum_ref, values):
+    total = jnp.concatenate(
+        [jnp.sum(x, axis=0, keepdims=True) for x in values]
+        + [jnp.zeros((8 - len(values), values[0].shape[1]), F32)],
+        axis=0,
+    )
+
+    @pl.when(pl.program_id(0) == 0)
+    def _():
+        sum_ref[...] = total
+
+    @pl.when(pl.program_id(0) > 0)
+    def _():
+        sum_ref[...] += total
+
+
+def second_back_kernel(
+    cot_ref, slot_ref, mask_ref, norm_ref, inverse_ref, gain_ref, grad_ref, low_ref, sum_ref
+):
+    group = slot_ref.shape[1]
+    cot = cot_ref[...].astype(F32).reshape(group, BLOCK // group, D)
+    first = lax.broadcasted_iota(jnp.int32, cot.shape, 1) == 0
+    grad = cot + jnp.where(first, slot_ref[0][:, None, :], 0.0)
+    grad = grad.reshape(BLOCK, D) * mask_ref[...]
+    norm = norm_ref[...]
+    second = norm_back(grad, gain_ref[...], norm, inverse_ref[...])
+    low = second.astype(BF16)
+    grad_ref[...] = second
+    low_ref[...] = low
+    add_sums(sum_ref, [grad * norm, grad, low.astype(F32)])
+
+
+def second_back(cot, d_slot, mask, norm, inverse, gain):
+    rows = cot.shape[0]
+    blocks = rows // BLOCK
+    wide = pl.BlockSpec((BLOCK, D), lambda i: (i, 0))
+    thin = pl.BlockSpec((BLOCK, 1), lambda i: (i, 0))
+    group = d_slot.shape[0] // blocks
+    return pl.pallas_call(
+        second_back_kernel,
+        grid=(blocks,),
+        in_specs=[
+            wide,
+            pl.BlockSpec((1, group, D), lambda i: (i, 0, 0)),
+            thin,
+            wide,
+            thin,
+            pl.BlockSpec((1, D), lambda i: (0, 0)),
+        ],
+        out_specs=[wide, wide, pl.BlockSpec((8, D), lambda i: (0, 0))],
+        out_shape=[
+            jax.ShapeDtypeStruct((rows, D), F32),
+            jax.ShapeDtypeStruct((rows, D), BF16),
+            jax.ShapeDtypeStruct((8, D), F32),
+        ],
+        compiler_params=pltpu.CompilerParams(vmem_limit_bytes=VMEM_LIMIT),
+        cost_estimate=pl.CostEstimate(
+            flops=20 * rows * D, bytes_accessed=12 * rows * D, transcendentals=0
+        ),
+        name="second_back",
+    )(cot, d_slot.reshape(blocks, group, D), mask, norm, inverse, gain)
+
+
+def first_back_kernel(
+    hidden_ref, w_ref, second_ref, norm_ref, inverse_ref, gain_ref, grad_ref, low_ref, sum_ref
+):
+    grad = second_ref[...] + dot(hidden_ref[...], w_ref[...], ((1,), (1,)))
+    norm = norm_ref[...]
+    first = norm_back(grad, gain_ref[...], norm, inverse_ref[...])
+    low = first.astype(BF16)
+    grad_ref[...] = first
+    low_ref[...] = low
+    add_sums(sum_ref, [grad * norm, grad, low.astype(F32)])
+
+
+def first_back(d_expanded, w_expand, d_second, norm, inverse, gain):
+    rows = d_expanded.shape[0]
+    wide = pl.BlockSpec((BLOCK, D), lambda i: (i, 0))
+    return pl.pallas_call(
+        first_back_kernel,
+        grid=(rows // BLOCK,),
+        in_specs=[
+            pl.BlockSpec((BLOCK, FF), lambda i: (i, 0)),
+            pl.BlockSpec((D, FF), lambda i: (0, 0)),
+            wide,
+            wide,
+            pl.BlockSpec((BLOCK, 1), lambda i: (i, 0)),
+            pl.BlockSpec((1, D), lambda i: (0, 0)),
+        ],
+        out_specs=[wide, wide, pl.BlockSpec((8, D), lambda i: (0, 0))],
+        out_shape=[
+            jax.ShapeDtypeStruct((rows, D), F32),
+            jax.ShapeDtypeStruct((rows, D), BF16),
+            jax.ShapeDtypeStruct((8, D), F32),
+        ],
+        compiler_params=pltpu.CompilerParams(vmem_limit_bytes=VMEM_LIMIT),
+        cost_estimate=pl.CostEstimate(
+            flops=2 * rows * D * FF,
+            bytes_accessed=2 * (rows * FF + D * FF) + 14 * rows * D,
+            transcendentals=0,
+        ),
+        name="first_back",
+    )(d_expanded, w_expand, d_second, norm, inverse, gain)
+
+
 def expand_kernel(mid_ref, w_ref, b_ref, active_ref, slope_ref):
     expanded = dot(mid_ref[...], w_ref[...]) + b_ref[...]
     phi = 0.5 + 0.5 * lax.erf(expanded * 0.7071067811865476)
@@ -505,8 +681,8 @@
 
     side = jnp.full((places.chips,), core, jnp.int32)
     table = jnp.stack([x ^ chip for x in of_core(masks)] + [side]).astype(jnp.int32)
-    away = jnp.arange(places.chips, dtype=jnp.int32) ^ chip
-    slots = jnp.stack([jnp.take(x, away) for x in of_core(slots_of)] + [side]).astype(jnp.int32)
+    slots = [x ^ lax.dynamic_index_in_dim(x, chip, 0, keepdims=False) for x in of_core(slots_of)]
+    slots = jnp.stack(slots + [side]).astype(jnp.int32)
     share = w_joined.shape[1]
 
     small = jnp.concatenate(
@@ -567,44 +743,55 @@
         return jnp.where(is_q, q_side, p_side), jnp.where(is_q, p_side, q_side)
 
     lq, lp = question_in.shape[1], passage_in.shape[1]
-    valid_q = (jnp.arange(lq, dtype=jnp.int32)[None, :] < question_len[:, None]).astype(jnp.int32)
-    valid_p = (jnp.arange(lp, dtype=jnp.int32)[None, :] < passage_len[:, None]).astype(jnp.int32)
-    my_valid, send_valid = sides(valid_q.reshape(-1), valid_p.reshape(-1))
-    valid = jnp.concatenate([my_valid, places.swap_tower(send_valid)])
-    my_tokens, send_tokens = sides(rows_q, rows_p)
-    my_cot, send_cot = sides(question_cot.reshape(-1, D), passage_cot.reshape(-1, D))
     rows = 2 * own_rows
-    row_ids = jnp.arange(rows, dtype=jnp.int32)
-    seq = jnp.where(is_q, row_ids // lq, row_ids // lp)
-    qid = seq.reshape(rows, 1)
-    kid = jnp.where(valid > 0, seq, -1).reshape(rows // BLOCK, 1, BLOCK)
-    row_mask = valid.reshape(rows, 1).astype(F32)
-
-    def chunked(values):
-        step = values.shape[0] // 4
-        return [values[i * step : (i + 1) * step] for i in range(4)]
+
+    def chunked(values, sixteenths):
+        out, row = [], 0
+        for part in sixteenths:
+            step = values.shape[0] * part // 16
+            out.append(values[row : row + step])
+            row += step
+        return out
 
     def hand(values):
         return [places.swap_tower(x) for x in values]
 
     g1, g2, g3 = Gather(first), Gather(second), Gather(third)
-    tokens_out, cot_out = chunked(send_tokens), chunked(send_cot)
+    my_tokens, send_tokens = sides(rows_q, rows_p)
+    tokens_out = chunked(send_tokens, (4, 6, 4, 2))
     g1.mid()
-    g1.send, g2.send = tie(g1.send, g2.send)
+    g1.send, tokens_out = tie(g1.send, tokens_out)
     g1.along_z()
+    tokens_in = hand(tokens_out[:1])
+    g1.send, g2.send, tokens_in = tie(g1.send, g2.send, tokens_in)
+    g1.pb_first()
     g2.mid()
-    g1.send, g2.send, g3.send = tie(g1.send, g2.send, g3.send)
-    g1.pb_first()
-    g2.along_z()
-    g3.mid()
-    g1.stack, g2.send, g3.send, tokens_out = tie(g1.stack, g2.send, g3.send, tokens_out)
+    g1.stack, g2.send, tokens_out = tie(g1.stack, g2.send, tokens_out)
     g1.send = g1.stack
     g1.pb_last()
     g1.core_stack()
-    g3.along_z()
-    tokens_in = hand(tokens_out[:2])
-    g1.held, g1.other, g2.send, g3.send, tokens_in, tokens_out = tie(
-        g1.held, g1.other, g2.send, g3.send, tokens_in, tokens_out
+    g2.along_z()
+    tokens_in = tokens_in + hand(tokens_out[1:2])
+    (
+        g1.held,
+        g2.send,
+        tokens_in,
+        tokens_out,
+        question_len,
+        passage_len,
+        positive,
+        question_cot,
+        passage_cot,
+    ) = tie(
+        g1.held,
+        g2.send,
+        tokens_in,
+        tokens_out,
+        question_len,
+        passage_len,
+        positive,
+        question_cot,
+        passage_cot,
     )
     g1.core_held()
     g2.pb_first()
@@ -623,35 +810,45 @@
     vec = small[:, :8].T
     bias_e = small[:, 8:12].reshape(1, FF)
     bias_j = jnp.concatenate([vec[0], jnp.zeros((D,), F32), vec[1]])
-    tokens = jnp.concatenate([my_tokens] + tokens_in, axis=0)
-    wj, tokens, cot_out = tie(wj, tokens, cot_out)
+    wj, tokens_in, g3.send = tie(wj, tokens_in, g3.send)
+    g3.mid()
+    tokens = join([my_tokens] + tokens_in)
+    qkv = (dot(tokens, wj) + bias_j).astype(BF16)
+
+    my_cot, send_cot = sides(question_cot.reshape(-1, D), passage_cot.reshape(-1, D))
+    cot_out = chunked(send_cot, (4, 6, 6))
+    valid_q = (jnp.arange(lq, dtype=jnp.int32)[None, :] < question_len[:, None]).astype(jnp.int32)
+    valid_p = (jnp.arange(lp, dtype=jnp.int32)[None, :] < passage_len[:, None]).astype(jnp.int32)
+    my_valid, send_valid = sides(valid_q.reshape(-1), valid_p.reshape(-1))
+    valid = jnp.concatenate([my_valid, places.swap_tower(send_valid)])
+    row_ids = jnp.arange(rows, dtype=jnp.int32)
+    seq = jnp.where(is_q, row_ids // lq, row_ids // lp)
+    qid = seq.reshape(rows, 1)
+    kid = jnp.where(valid > 0, seq, -1).reshape(rows // BLOCK, 1, BLOCK)
+    row_mask = valid.reshape(rows, 1).astype(F32)
+
+    qkv, g2.held, g3.send, cot_out = tie(qkv, g2.held, g3.send, cot_out)
+    g2.core_held()
+    g3.along_z()
     cot_in = hand(cot_out[:1])
-    qkv = (dot(tokens, wj) + bias_j).astype(BF16)
-    qkv, g2.held, g2.other, g2.stack, g3.send, cot_in, cot_out = tie(
-        qkv, g2.held, g2.other, g2.stack, g3.send, cot_in, cot_out
-    )
+    context, probs = attention(qkv, qid, kid)
+    context, g2.parts, g3.send, cot_in, cot_out = tie(context, g2.parts, g3.send, cot_in, cot_out)
     g3.pb_first()
-    g2.core_held()
-    cot_in = cot_in + hand(cot_out[1:2])
-    context, probs = attention(qkv, qid, kid)
-    context, g2.parts, g3.stack, cot_in, cot_out = tie(context, g2.parts, g3.stack, cot_in, cot_out)
-    g3.send = g3.stack
-    g3.pb_last()
-    g3.core_stack()
-    cot_in = cot_in + hand(cot_out[2:3])
     (full_e,) = g2.whole([(0, FF)])
     we = full_e.reshape(D, FF)
     attended = dot(context, wo) + vec[2]
     norm_one, inverse_one = normalized(tokens.astype(F32) + attended)
     mid = norm_one * vec[3] + vec[4]
     mid_low = mid.astype(BF16)
-    mid_low, we, g3.held, g3.other, g3.stack, cot_in, cot_out = tie(
-        mid_low, we, g3.held, g3.other, g3.stack, cot_in, cot_out
-    )
+    mid_low, we, g3.stack, cot_in, cot_out = tie(mid_low, we, g3.stack, cot_in, cot_out)
+    g3.send = g3.stack
+    g3.pb_last()
+    g3.core_stack()
+    cot_in = cot_in + hand(cot_out[1:2])
+    active, slope = expand(mid_low, we, bias_e)
+    active, g3.held, g3.other, cot_in, cot_out = tie(active, g3.held, g3.other, cot_in, cot_out)
     g3.core_held()
-    cot_in = cot_in + hand(cot_out[3:])
-    active, slope = expand(mid_low, we, bias_e)
-    active, g3.parts, cot_in = tie(active, g3.parts, cot_in)
+    cot_in = cot_in + hand(cot_out[2:])
     (full_r,) = g3.whole([(0, D)])
     wr = full_r.reshape(FF, D)
     norm_two, inverse_two = normalized(mid + dot(active, wr) + vec[5])
@@ -717,17 +914,9 @@
     ).reshape(per_q, D)
     d_slot = jnp.where(is_q, d_q, d_p)
 
-    cot = jnp.concatenate([my_cot] + cot_in, axis=0)
-    d_out = cot.astype(F32).reshape(per_q, lq, D)
-    at_slot = jnp.arange(lq, dtype=jnp.int32)[None, :, None] == 0
-    d_out = d_out + jnp.where(at_slot, d_slot[:, None, :], 0.0)
-    d_out = d_out.reshape(rows, D) * row_mask
-    d_second = norm_back(d_out, vec[6], norm_two, inverse_two)
-    g_gain_two = jnp.sum(d_out * norm_two, axis=0)
-    g_shift_two = jnp.sum(d_out, axis=0)
-    d_reduced = d_second.astype(BF16)
-    g_bias_reduce = jnp.sum(d_reduced.astype(F32), axis=0)
-
+    d_second, d_reduced, sums_second = second_back(
+        join([my_cot] + cot_in), d_slot, row_mask, norm_two, inverse_two, vec[6][None, :]
+    )
     even = share % 8 == 0
 
     def gradient(left, right, tile, extra=None):
@@ -775,7 +964,7 @@
                 [jnp.where(is_q, keep, got), jnp.where(is_q, got, keep)], axis=0
             )
 
-    send_out = chunked(out[own_rows:])
+    send_out = chunked(out[own_rows:], (5, 6, 5))
     sr = Scatter(*gradient(active, d_reduced, D))
     sr.parts, sr.theirs, d_reduced, send_out = tie(sr.parts, sr.theirs, d_reduced, send_out)
     sr.cores()
@@ -785,22 +974,16 @@
     sr.pb_first()
     got_out = got_out + hand(send_out[1:2])
     se = Scatter(*gradient(mid_low, d_expanded, 1024))
-    se.parts, se.theirs, d_expanded, got_out, send_out = tie(
-        se.parts, se.theirs, d_expanded, got_out, send_out
-    )
+    se.parts, se.theirs, d_expanded = tie(se.parts, se.theirs, d_expanded)
     se.cores()
-    got_out = got_out + hand(send_out[2:3])
-    d_mid = d_second + dot(d_expanded, we, ((1,), (1,)))
-    sr.parts, se.parts, d_mid, got_out, send_out = tie(
-        sr.parts, se.parts, d_mid, got_out, send_out
+    d_first, d_attended, sums_first = first_back(
+        d_expanded, we, d_second, norm_one, inverse_one, vec[3][None, :]
+    )
+    sr.parts, se.parts, d_attended, got_out, send_out = tie(
+        sr.parts, se.parts, d_attended, got_out, send_out
     )
     sr.pb_rest()
-    got_out = got_out + hand(send_out[3:])
-    d_first = norm_back(d_mid, vec[3], norm_one, inverse_one)
-    g_gain_one = jnp.sum(d_mid * norm_one, axis=0)
-    g_shift_one = jnp.sum(d_mid, axis=0)
-    d_attended = d_first.astype(BF16)
-    g_bias_output = jnp.sum(d_attended.astype(F32), axis=0)
+    got_out = got_out + hand(send_out[2:])
     so = Scatter(*gradient(context, d_attended, D))
     d_context = dot(d_attended, wo, ((1,), (1,))).astype(BF16)
     sr.parts, se.parts, so.parts, so.theirs, d_context, got_out = tie(
@@ -810,56 +993,58 @@
     sr.along_z()
     so.cores()
     blocks = rows // BLOCK
-    d_joined, sums_one = attention_back(qkv, probs, d_context, 0, blocks // 2)
+    later = blocks // 2
+    d_joined, sums_one = attention_back(qkv, probs, d_context, later, blocks - later)
     sr.parts, so.parts, d_joined = tie(sr.parts, so.parts, d_joined)
     sr.mid()
-    d_joined, sums_two = attention_back(
-        qkv, probs, d_context, blocks // 2, blocks - blocks // 2, d_joined
-    )
-    sr.out, se.parts, so.parts, d_joined = tie(sr.out, se.parts, so.parts, d_joined)
+    send_grad = (d_first[own_rows:] + dot(d_joined[own_rows:], wj, ((1,), (1,)))).astype(BF16)
+    se.parts, sr.out, d_joined, send_grad = tie(
+        se.parts, sr.out, d_joined, chunked(send_grad, (5, 5, 6))
+    )
     se.pb_rest()
     so.pb_first()
-    send_grad = (d_first[own_rows:] + dot(d_joined[own_rows:], wj, ((1,), (1,)))).astype(BF16)
-    send_grad = chunked(send_grad)
-    se.parts, so.parts, d_joined, send_grad = tie(se.parts, so.parts, d_joined, send_grad)
+    got_grad = hand(send_grad[:1])
+    d_joined, sums_two = attention_back(qkv, probs, d_context, 0, later, d_joined)
+    se.parts, so.parts, d_joined, got_grad, send_grad = tie(
+        se.parts, so.parts, d_joined, got_grad, send_grad
+    )
     se.along_z()
     so.pb_rest()
-    got_grad = hand(send_grad[:1])
+    got_grad = got_grad + hand(send_grad[1:2])
     g_joined_bias = (sums_one + sums_two)[0]
-    g_vec = jnp.stack(
+    g_vec = jnp.concatenate(
         [
-            g_joined_bias[:D],
-            g_joined_bias[2 * D :],
-            g_bias_output,
-            g_gain_one,
-            g_shift_one,
-            g_bias_reduce,
-            g_gain_two,
-            g_shift_two,
+            g_joined_bias[None, :D],
+            g_joined_bias[None, 2 * D :],
+            sums_first[2:3],
+            sums_first[:2],
+            sums_second[2:3],
+            sums_second[:2],
         ]
     )
     g_small = jnp.concatenate(
         [g_vec.T, g_bias_expand.reshape(D, 4), jnp.zeros((D, 116), F32)], axis=1
     )
     sj = Scatter(*gradient(tokens, d_joined, D, g_small))
-    se.parts, so.parts, sj.parts, sj.theirs, d_joined, got_grad, send_grad = tie(
-        se.parts, so.parts, sj.parts, sj.theirs, d_joined, got_grad, send_grad
+    se.parts, so.parts, sj.parts, sj.theirs, d_joined = tie(
+        se.parts, so.parts, sj.parts, sj.theirs, d_joined
     )
     sj.cores()
     so.along_z()
-    se.mid()
-    got_grad = got_grad + hand(send_grad[1:2])
     own_grad = d_first[:own_rows] + dot(d_joined[:own_rows], wj, ((1,), (1,)))
     sj.parts, so.parts, own_grad, got_grad, send_grad = tie(
         sj.parts, so.parts, own_grad, got_grad, send_grad
     )
     sj.pb_first()
+    got_grad = got_grad + hand(send_grad[2:])
+    out_q, out_p = deal(tower.reshape(1), out, got_out)
+    sj.parts, se.parts, so.parts = tie(sj.parts, se.parts, so.parts)
+    sj.pb_rest()
+    se.mid()
     so.mid()
-    got_grad = got_grad + hand(send_grad[2:3])
-    sj.parts, got_grad, send_grad = tie(sj.parts, got_grad, send_grad)
-    sj.pb_rest()
-    got_grad = got_grad + hand(send_grad[3:])
+    sj.parts, se.out, so.out, got_grad = tie(sj.parts, se.out, so.out, got_grad)
     sj.along_z()
+    grad_q, grad_p = deal(tower.reshape(1), own_grad, got_grad)
     sj.mid()
     grad_joined = sj.out[:, :, : 3 * D]
     grad_output, grad_expand, grad_reduce = so.out, se.out, sr.out
@@ -867,8 +1052,6 @@
     grad_vectors = extra[:, :, :8].transpose(0, 2, 1)
     grad_b_expand = extra[:, :, 8:12].reshape(2, 4 * share)
 
-    out_q, out_p = sides(out[:own_rows], jnp.concatenate(got_out, axis=0))
-    grad_q, grad_p = sides(own_grad, jnp.concatenate(got_grad, axis=0).astype(F32))
     return (
         out_q.reshape(question_in.shape),
         out_p.reshape(passage_in.shape),

time: 465 us -> 532 us (1.14)
  Pallas kernels: 110 us -> 233 us
  other arithmetic: 80.9 us -> 54.8 us
  local copies, waits for them, and re-layouts: 58.8 us -> 35.1 us
  matrix products: 42.4 us -> 36.1 us
    pallas_call x0 -> x6, Pallas kernels: none -> 123 us  [the longest x2 97.6 us: join(): pl.pallas_call(join_kernel, in_specs=[pl.BlockSpec(memory_space=pl.ANY)]...]
    reduce_sum x4 -> x0, other arithmetic: 13 us -> none  [the longest x1 4.52 us: per_device(): g_gain_two = jnp.sum(d_out * norm_two, axis=0)]
    unnamed x221 -> x129, local copies, waits for them, and re-layouts: 20.8 us -> 7.85 us
    ppermute x18 -> x15, waiting for transfers between devices: 41.9 us -> 51.4 us  [swap_tower(): lax.ppermute(values, 'pa', [(i, i ^ 2 * self.half) for i in range(self.pa...]
    ppermute x18 -> x15, starting transfers between devices: 24.3 us -> 15.4 us  [swap_tower(): lax.ppermute(values, 'pa', [(i, i ^ 2 * self.half) for i in range(self.pa...]
    dot_general x10 -> x9, matrix products: 42.4 us -> 36.1 us  [dot(): lax.dot_general(left, right, (dims, ((), ())), preferred_element_type=F32)]
    ppermute x28, starting transfers between devices: 29.6 us -> 35.6 us  [swap(): return lax.ppermute(values, AXES, self.pairs(step))]
    slice x5 -> x14, local copies, waits for them, and re-layouts: 4.07 us -> 9.69 us  [the longest x9 6.63 us: chunked(): out.append(values[row:row + step])]
  transfers between devices with their start and end apart: 62 -> 59, of which waited for: 26 -> 24; matrix products, arithmetic and copies ran while one was open for 31% -> 17% of each run, Pallas kernels for 21% -> 38%
where the time goes in v3:
time: 532 us; the launch traced here: 525 us
  Pallas kernels  233 us (44%)
  waiting for transfers between devices  107 us (20%)
  starting transfers between devices  56.3 us (11%)
  other arithmetic  54.8 us (10%)
  matrix products  36.1 us (7%)
  local copies, waits for them, and re-layouts  35.1 us (7%)
    pallas_call x2, Pallas kernels, join(): pl.pallas_call(join_kernel, in_specs=[pl.BlockSpec(memory_space=pl.ANY)]...  97.6 us
    ppermute x15, waiting for transfers between devices, swap_tower(): lax.ppermute(values, 'pa', [(i, i ^ 2 * self.half) for i in range(self.pa...  51.4 us
    ppermute x28, waiting for transfers between devices, swap(): return lax.ppermute(values, AXES, self.pairs(step))  46.3 us
    dot_general x9, matrix products, dot(): lax.dot_general(left, right, (dims, ((), ())), preferred_element_type=F32)  36.1 us
    ppermute x28, starting transfers between devices, swap(): return lax.ppermute(values, AXES, self.pairs(step))  35.6 us
    pallas_call x3, Pallas kernels, weight_grad(): pl.pallas_call(functools.partial(weight_grad_kernel, chips, extra is not...  24.6 us
    pallas_call x2, Pallas kernels, attention_back(): pl.pallas_call(attention_back_more_kernel if more else attention_back_ker...  21.3 us
    pallas_call x1, Pallas kernels, expand(): pl.pallas_call(expand_kernel, grid=(FF // tile_f, rows // tile_r), in_spe...  17 us
  transfers between devices with their start and end apart: 59, of which 24 were waited for; matrix products, arithmetic and copies ran while one was open for 17% of the time, Pallas kernels for 38%

profile of v3, /device:TPU:0, one launch (start us, length us, event | category | flops | bytes accessed | tf_op | source)
XLA Modules:
  0.0 524.6 jit_solution(6134020433648717057)
XLA Ops:
  3.4 4.1 collective-permute-start
  7.5 2.4 bitcast_select_fusion.3
  12.0 2.8 collective-permute-done
  15.6 3.4 collective-permute-start.2
  19.1 8.5 %collective-permute-done.1 = bf16[2,24,3200]{2,1,0:T(8,128)(2,1)S(1)} collective-permute-done((bf16[2,24,3200]{2,1,0:T(8,128)(2,1)S(1)}, bf16[2,24,3200]{2,1,0:T(8,128)(2,1)S(1)}, u32[]{:S(2)}, u32[]{:S(2)}) %collective-permute-start.1) | collective-permute-done | bytes 307232 | tf_op jit(solution)/shard_map/ppermute | solution.py:66
  29.0 2.6 collective-permute-start.4
  31.6 6.6 %collective-permute-done.4 = bf16[1,24,3072]{2,1,0:T(8,128)(2,1)S(1)} collective-permute-done((bf16[1,24,3072]{2,1,0:T(8,128)(2,1)S(1)}, bf16[1,24,3072]{2,1,0:T(8,128)(2,1)S(1)}, u32[]{:S(2)}, u32[]{:S(2)}) %collective-permute-start.4) | collective-permute-done | bytes 147488 | tf_op jit(solution)/shard_map/ppermute | solution.py:66
  49.1 13.1 %collective-permute-done.7.refs_2_ = bf16[192,768]{1,0:T(8,128)(2,1)S(1)} collective-permute-done((bf16[192,768]{1,0:T(8,128)(2,1)}, bf16[192,768]{1,0:T(8,128)(2,1)S(1)}, u32[]{:S(2)}, u32[]{:S(2)}) %collective-permute-start.7) | collective-permute-done | bytes 294944 | tf_op jit(solution)/shard_map/ppermute | solution.py:72
  65.8 2.4 bitcast_select_fusion
  70.4 2.7 collective-permute-done.10
  77.7 5.5 %assemble.3 = (bf16[16,2,24,2304]{3,2,1,0:T(8,128)(2,1)}, bf16[16,2,24,768]{3,2,1,0:T(8,128)(2,1)}, bf16[16,2,24,128]{3,2,1,0:T(8,128)(2,1)}) custom-call(s32[3,16]{1,0:T(4,128)} %get-tuple-element.530.idx_ref, bf16[8,24,3200]{2,1,0:T(8,128)(2,1)} %copy-done.1, bf16[8,24,3200]{2,1,0:T(8,128)(2,1)} %collective-permute-done.5.refs_1_, ...), custom_call_target="tpu_custom_call" | custom-call | bytes 9830400 | tf_op jit(solution)/shard_map/assemble/pallas_call | solution.py:118
  85.6 8.0 %collective-permute-done.12.refs_4_ = bf16[64,768]{1,0:T(8,128)(2,1)S(1)} collective-permute-done((bf16[64,768]{1,0:T(8,128)(2,1)S(1)}, bf16[64,768]{1,0:T(8,128)(2,1)S(1)}, u32[]{:S(2)}, u32[]{:S(2)}) %collective-permute-start.12) | collective-permute-done | bytes 98336 | tf_op jit(solution)/shard_map/ppermute | solution.py:72
  94.3 48.8 %join.2.left_ref = bf16[1024,768]{1,0:T(8,128)(2,1)} custom-call(bf16[512,768]{1,0:T(8,128)(2,1)} %get-tuple-element.493.refs_0_, bf16[128,768]{1,0:T(8,128)(2,1)} %copy-done.37, bf16[192,768]{1,0:T(8,128)(2,1)} %copy-done.24, bf16[128,768]{1,0:T(8,128)(2,1)} %copy-done.38, bf16[64,768]{1,0:T(8,128)(2,1)} %copy-done.39), custom_call_target="tpu_custom_call" | custom-call | bytes 3145728 | tf_op jit(solution)/shard_map/join/pallas_call | solution.py:442
  143.1 8.5 %add_convert_fusion.qkv_ref = bf16[1024,2304]{1,0:T(8,128)(2,1)} fusion(bf16[1024,768]{1,0:T(8,128)(2,1)} %join.2.left_ref, bf16[768,2304]{1,0:T(8,128)(2,1)} %bitcast.100, f32[2304]{0:T(1024)S(1)} %pad_maximum_fusion.16), kind=kOutput, calls=%fused_computation.2 | convolution fusion | flops 3628597248 | bytes 9839616 | tf_op jit(solution)/shard_map/dot_general | solution.py:76
  160.0 11.1 %attention.1 = (bf16[1024,768]{1,0:T(8,128)(2,1)}, bf16[4,12,256,256]{3,2,1,0:T(8,128)(2,1)}) custom-call(bf16[1024,2304]{1,0:T(8,128)(2,1)} %add_convert_fusion.qkv_ref, s32[1024,1]{1,0:T(8,128)} %fusion.11.qid_ref, s32[4,1,256]{2,1,0:T(1,128)} %compare_select_fusion.kid_ref), custom_call_target="tpu_custom_call" | custom-call | flops 1610612736 | bytes 12582912 | tf_op jit(solution)/shard_map/attention/pallas_call | solution.py:323
  172.7 3.3 fusion.46
  177.3 4.7 assemble.4
  182.1 2.7 fusion
  188.4 17.0 %expand.1 = (bf16[1024,3072]{1,0:T(8,128)(2,1)}, bf16[1024,3072]{1,0:T(8,128)(2,1)}) custom-call(bf16[1024,768]{1,0:T(8,128)(2,1)} %get-tuple-element.275.mid_ref.left_ref, bf16[768,3072]{1,0:T(8,128)(2,1)} %bitcast.79, f32[1,3072]{1,0:T(1,128)} %reshape.653.b_ref), custom_call_target="tpu_custom_call" | custom-call | flops 4831838208 | bytes 18874368 | tf_op jit(solution)/shard_map/expand/pallas_call | solution.py:612
  208.9 2.6 compare_select_fusion.1
  218.4 4.9 assemble.5
  223.3 8.7 %fusion.47 = (f32[1024]{0:T(1024)S(1)}, f32[1024,768]{1,0:T(8,128)S(1)}) fusion(f32[768]{0:T(1024)S(1)} %copy-done.48, bf16[1024,3072]{1,0:T(8,128)(2,1)} %get-tuple-element.282.left_ref, bf16[3072,768]{1,0:T(8,128)(2,1)} %bitcast.81, f32[768]{0:T(1024)S(1)} %copy-done.43, f32[1024,768]{1,0:T(8,128)S(1)} %copy-done.4, f32[768]{0:T(1024)S(1)} %get-tuple-element.468), kind=kOutput, calls=%fused_computation.198 | convolution fusion | flops 4835769344 | bytes 17314816 | tf_op jit(solution)/shard_map/dot_general | solution.py:76
  237.9 7.9 %collective-permute-done.26 = bf16[16,768]{1,0:T(8,128)(2,1)S(1)} collective-permute-done((bf16[16,768]{1,0:T(8,128)(2,1)S(1)}, bf16[16,768]{1,0:T(8,128)(2,1)S(1)}, u32[]{:S(2)}, u32[]{:S(2)}) %collective-permute-start.26) | collective-permute-done | bytes 24608 | tf_op jit(solution)/shard_map/ppermute | solution.py:72
  246.9 5.0 collective-permute-done.25.refs_3_
  252.6 48.8 %join.3.cot_ref = bf16[1024,768]{1,0:T(8,128)(2,1)} custom-call(bf16[512,768]{1,0:T(8,128)(2,1)} %get-tuple-element.491.refs_0_, bf16[128,768]{1,0:T(8,128)(2,1)} %copy-done.36, bf16[192,768]{1,0:T(8,128)(2,1)} %copy-done.23, bf16[192,768]{1,0:T(8,128)(2,1)} %copy-done.26), custom_call_target="tpu_custom_call" | custom-call | bytes 3145728 | tf_op jit(solution)/shard_map/join/pallas_call | solution.py:442
  307.1 4.0 collective-permute-done.29
  314.7 6.5 %second_back.1 = (f32[1024,768]{1,0:T(8,128)}, bf16[1024,768]{1,0:T(8,128)(2,1)}, f32[8,768]{1,0:T(8,128)}) custom-call(bf16[1024,768]{1,0:T(8,128)(2,1)} %join.3.cot_ref, f32[4,4,768]{2,1,0:T(4,128)} %reshape.660.slot_ref, f32[1024,1]{1,0:T(8,128)} %copy.76.mask_ref, f32[1024,768]{1,0:T(8,128)} %get-tuple-element.478.norm_ref, f32[1024,1]{1,0:T(8,128)} %copy.77.inverse_ref, ...), custom_call_target="tpu_custom_call" | custom-call | flops 15728640 | bytes 9437184 | tf_op jit(solution)/shard_map/second_back/pallas_call | solution.py:534
  321.2 9.9 %tall_grad.1 = (bf16[16,96,768]{2,1,0:T(8,128)(2,1)}, bf16[16,96,768]{2,1,0:T(8,128)(2,1)}) custom-call(s32[3,16]{1,0:T(4,128)} %get-tuple-element.529.table_ref, bf16[1024,3072]{1,0:T(8,128)(2,1)} %get-tuple-element.282.left_ref, bf16[1024,768]{1,0:T(8,128)(2,1)} %get-tuple-element.294.right_ref.grad_ref), custom_call_target="tpu_custom_call" | custom-call | flops 4831838208 | bytes 12582912 | tf_op jit(solution)/shard_map/tall_grad/pallas_call | solution.py:224
  331.3 11.6 %hidden_grad.1 = (bf16[1024,3072]{1,0:T(8,128)(2,1)}, f32[1,3072]{1,0:T(1,128)}) custom-call(bf16[1024,768]{1,0:T(8,128)(2,1)} %get-tuple-element.294.right_ref.grad_ref, bf16[3072,768]{1,0:T(8,128)(2,1)} %bitcast.82, bf16[1024,3072]{1,0:T(8,128)(2,1)} %get-tuple-element.295.slope_ref), custom_call_target="tpu_custom_call" | custom-call | flops 4831838208 | bytes 18874368 | tf_op jit(solution)/shard_map/hidden_grad/pallas_call | solution.py:270
  345.2 10.7 %weight_grad.3 = (bf16[16,24,3072]{2,1,0:T(8,128)(2,1)}, bf16[16,24,3072]{2,1,0:T(8,128)(2,1)}) custom-call(s32[3,16]{1,0:T(4,128)} %get-tuple-element.529.table_ref, bf16[1024,768]{1,0:T(8,128)(2,1)} %get-tuple-element.275.mid_ref.left_ref, bf16[1024,3072]{1,0:T(8,128)(2,1)} %get-tuple-element.307.right_ref.hidden_ref), custom_call_target="tpu_custom_call" | custom-call | flops 4831838208 | bytes 12582912 | tf_op jit(solution)/shard_map/weight_grad/pallas_call | solution.py:184
  359.2 12.5 %first_back.1 = (f32[1024,768]{1,0:T(8,128)}, bf16[1024,768]{1,0:T(8,128)(2,1)}, f32[8,768]{1,0:T(8,128)}) custom-call(bf16[1024,3072]{1,0:T(8,128)(2,1)} %get-tuple-element.307.right_ref.hidden_ref, bf16[768,3072]{1,0:T(8,128)(2,1)} %bitcast.80, f32[1024,768]{1,0:T(8,128)} %get-tuple-element.308.second_ref, f32[1024,768]{1,0:T(8,128)} %get-tuple-element.480.norm_ref, ...), custom_call_target="tpu_custom_call" | custom-call | flops 4831838208 | bytes 22020096 | tf_op jit(solution)/shard_map/first_back/pallas_call | solution.py:574
  371.6 2.8 collective-permute-done.37.refs_1_
  384.2 5.0 weight_grad.4
  389.2 4.1 convolution_convert_fusion.grad_ref
  393.3 4.0 collective-permute-done.39.refs_2_
  401.8 10.6 %attention_back.2 = (bf16[1024,2304]{1,0:T(8,128)(2,1)}, f32[1,2304]{1,0:T(1,128)}) custom-call(bf16[1024,2304]{1,0:T(8,128)(2,1)} %add_convert_fusion.qkv_ref, bf16[4,12,256,256]{3,2,1,0:T(8,128)(2,1)} %get-tuple-element.337.probs_ref, bf16[1024,768]{1,0:T(8,128)(2,1)} %convolution_convert_fusion.grad_ref), custom_call_target="tpu_custom_call" | custom-call | flops 1610612736 | bytes 8650752 | tf_op jit(solution)/shard_map/attention_back/pallas_call | solution.py:397
  413.9 2.8 collective-permute-start.43
  416.7 5.3 %add_convert_fusion.4 = bf16[512,768]{1,0:T(8,128)(2,1)S(1)} fusion(f32[1024,768]{1,0:T(8,128)} %get-tuple-element.346, bf16[768,2304]{1,0:T(8,128)(2,1)} %bitcast.101, bf16[1024,2304]{1,0:T(8,128)(2,1)} %get-tuple-element.352._), kind=kOutput, calls=%fused_computation.21 | convolution fusion | flops 1812725760 | bytes 8257536 | tf_op jit(solution)/shard_map/dot_general | solution.py:76
  431.0 10.8 %attention_back.3 = (bf16[1024,2304]{1,0:T(8,128)(2,1)}, f32[1,2304]{1,0:T(1,128)}) custom-call(bf16[1024,2304]{1,0:T(8,128)(2,1)} %add_convert_fusion.qkv_ref, bf16[4,12,256,256]{3,2,1,0:T(8,128)(2,1)} %get-tuple-element.337.probs_ref, bf16[1024,768]{1,0:T(8,128)(2,1)} %convolution_convert_fusion.grad_ref, ...), custom_call_target="tpu_custom_call", output_to_operand_aliasing={{0}: (3, {})} | custom-call | flops 1610612736 | bytes 8650752 | tf_op jit(solution)/shard_map/attention_back/pallas_call | solution.py:397
  449.5 8.9 %weight_grad.5 = (bf16[16,24,2432]{2,1,0:T(8,128)(2,1)}, bf16[16,24,2432]{2,1,0:T(8,128)(2,1)}) custom-call(s32[3,16]{1,0:T(4,128)} %get-tuple-element.529.table_ref, bf16[1024,768]{1,0:T(8,128)(2,1)} %join.2.left_ref, bf16[1024,2304]{1,0:T(8,128)(2,1)} %get-tuple-element.378.right_ref, f32[768,128]{1,0:T(8,128)} %maximum_maximum_fusion.refs_0_), custom_call_target="tpu_custom_call" | custom-call | flops 3623878656 | bytes 9830400 | tf_op jit(solution)/shard_map/weight_grad/pallas_call | solution.py:184
  462.4 5.7 %slice_add_fusion.own_ref = f32[512,768]{1,0:T(8,128)} fusion(f32[1024,768]{1,0:T(8,128)} %get-tuple-element.346, bf16[768,2304]{1,0:T(8,128)(2,1)} %bitcast.102, bf16[1024,2304]{1,0:T(8,128)(2,1)S(1)} %bitcast.84), kind=kOutput, calls=%fused_computation.20 | convolution fusion | flops 1812332544 | bytes 9043968 | tf_op jit(solution)/shard_map/dot_general | solution.py:76
  468.1 4.5 collective-permute-done.51.refs_1_
  476.6 12.9 %collective-permute-done.52 = bf16[8,24,2432]{2,1,0:T(8,128)(2,1)S(1)} collective-permute-done((bf16[8,24,2432]{2,1,0:T(8,128)(2,1)}, bf16[8,24,2432]{2,1,0:T(8,128)(2,1)S(1)}, u32[]{:S(2)}, u32[]{:S(2)}) %collective-permute-start.52) | collective-permute-done | bytes 933920 | tf_op jit(solution)/shard_map/ppermute | solution.py:66
  494.0 3.0 collective-permute-start.54
  499.4 3.7 collective-permute-done.54
  506.6 5.9 %collective-permute-done.57 = bf16[2,24,2432]{2,1,0:T(8,128)(2,1)S(1)} collective-permute-done((bf16[2,24,2432]{2,1,0:T(8,128)(2,1)S(1)}, bf16[2,24,2432]{2,1,0:T(8,128)(2,1)S(1)}, u32[]{:S(2)}, u32[]{:S(2)}) %collective-permute-start.57) | collective-permute-done | bytes 233504 | tf_op jit(solution)/shard_map/ppermute | solution.py:66
  514.8 2.6 deal.2
  517.4 3.5 deal.3
  (372 shorter events, 135.1 us)
Async XLA Ops:
  3.4 11.4 %collective-permute-start = (bf16[1,24,3200]{2,1,0:T(8,128)(2,1)S(1)}, bf16[1,24,3200]{2,1,0:T(8,128)(2,1)S(1)}, u32[]{:S(2)}, u32[]{:S(2)}) collective-permute-start(bf16[1,24,3200]{2,1,0:T(8,128)(2,1)S(1)} %get-tuple-element.502), channel_id=1, source_target_pairs={{0,4},{1,5},{2,6},{3,7},{4,0},{5,1},{6,2},{7,3},{8,12},{9,13},{10,... | collective-permute-start | bytes 460808 | tf_op jit(solution)/shard_map/ppermute | solution.py:66
  14.8 12.7 %collective-permute-start.1 = (bf16[2,24,3200]{2,1,0:T(8,128)(2,1)S(1)}, bf16[2,24,3200]{2,1,0:T(8,128)(2,1)S(1)}, u32[]{:S(2)}, u32[]{:S(2)}) collective-permute-start(bf16[2,24,3200]{2,1,0:T(8,128)(2,1)S(1)} %pad_maximum_fusion.8), channel_id=1, source_target_pairs={{0,2},{1,3},{2,0},{3,1},{4,6},{5,7},{6,4},{7,5},{8,10},{9,11},{10,... | collective-permute-start | bytes 921608 | tf_op jit(solution)/shard_map/ppermute | solution.py:66
  15.6 12.0 %collective-permute-start.2 = (bf16[128,768]{1,0:T(8,128)(2,1)S(1)}, bf16[128,768]{1,0:T(8,128)(2,1)S(1)}, u32[]{:S(2)}, u32[]{:S(2)}) collective-permute-start(bf16[128,768]{1,0:T(8,128)(2,1)S(1)} %get-tuple-element.218), channel_id=1, source_target_pairs={{0,4},{1,5},{2,6},{3,7},{4,0},{5,1},{6,2},{7,3},{8,12},{9,13},{10,... | collective-permute-start | bytes 589832 | tf_op jit(solution)/shard_map/ppermute | solution.py:72
  27.6 11.3 %collective-permute-start.3 = (bf16[4,24,3200]{2,1,0:T(8,128)(2,1)S(1)}, bf16[4,24,3200]{2,1,0:T(8,128)(2,1)S(1)}, u32[]{:S(2)}, u32[]{:S(2)}) collective-permute-start(bf16[4,24,3200]{2,1,0:T(8,128)(2,1)S(1)} %pad_maximum_fusion.3), channel_id=1, source_target_pairs={{0,8},{1,17},{2,10},{3,19},{4,12},{5,21},{6,14},{7,23},{8,0},{9,25... | collective-permute-start | bytes 1843208 | tf_op jit(solution)/shard_map/ppermute | solution.py:66
  29.0 9.2 %collective-permute-start.4 = (bf16[1,24,3072]{2,1,0:T(8,128)(2,1)S(1)}, bf16[1,24,3072]{2,1,0:T(8,128)(2,1)S(1)}, u32[]{:S(2)}, u32[]{:S(2)}) collective-permute-start(bf16[1,24,3072]{2,1,0:T(8,128)(2,1)S(1)} %get-tuple-element.220), channel_id=1, source_target_pairs={{0,4},{1,5},{2,6},{3,7},{4,0},{5,1},{6,2},{7,3},{8,12},{9,13},{10,... | collective-permute-start | bytes 442376 | tf_op jit(solution)/shard_map/ppermute | solution.py:66
  39.1 23.1 %collective-permute-start.5 = (bf16[8,24,3200]{2,1,0:T(8,128)(2,1)S(1)}, bf16[8,24,3200]{2,1,0:T(8,128)(2,1)}, u32[]{:S(2)}, u32[]{:S(2)}) collective-permute-start(bf16[8,24,3200]{2,1,0:T(8,128)(2,1)S(1)} %pad_maximum_fusion.refs_0_), channel_id=1, source_target_pairs={{0,16},{1,9},{2,18},{3,11},{4,20},{5,13},{6,22},{7,15},{8,24},{9,1... | collective-permute-start | bytes 3686408 | tf_op jit(solution)/shard_map/ppermute | solution.py:66
  45.4 29.0 %collective-permute-start.8 = (bf16[8,24,3200]{2,1,0:T(8,128)(2,1)S(1)}, bf16[8,24,3200]{2,1,0:T(8,128)(2,1)}, u32[]{:S(2)}, u32[]{:S(2)}) collective-permute-start(bf16[8,24,3200]{2,1,0:T(8,128)(2,1)S(1)} %pad_maximum_fusion.refs_0_), channel_id=1, source_target_pairs={{0,1},{1,0},{2,3},{3,2},{4,5},{5,4},{6,7},{7,6},{8,9},{9,8},{10,11... | collective-permute-start | bytes 3686408 | tf_op jit(solution)/shard_map/ppermute | solution.py:69
  45.4 16.8 %collective-permute-start.7 = (bf16[192,768]{1,0:T(8,128)(2,1)}, bf16[192,768]{1,0:T(8,128)(2,1)S(1)}, u32[]{:S(2)}, u32[]{:S(2)}) collective-permute-start(bf16[192,768]{1,0:T(8,128)(2,1)} %slice.509), channel_id=1, source_target_pairs={{0,4},{1,5},{2,6},{3,7},{4,0},{5,1},{6,2},{7,3},{8,12},{9,13},{10,... | collective-permute-start | bytes 884744 | tf_op jit(solution)/shard_map/ppermute | solution.py:72
  62.2 14.0 %collective-permute-start.9 = (bf16[8,24,3200]{2,1,0:T(8,128)(2,1)}, bf16[8,24,3200]{2,1,0:T(8,128)(2,1)}, u32[]{:S(2)}, u32[]{:S(2)}) collective-permute-start(bf16[8,24,3200]{2,1,0:T(8,128)(2,1)} %collective-permute-done.5.refs_1_), channel_id=1, source_target_pairs={{0,1},{1,0},{2,3},{3,2},{4,5},{5,4},{6,7},{7,6},{8,9},{9,8},{10,11... | collective-permute-start | bytes 3686408 | tf_op jit(solution)/shard_map/ppermute | solution.py:69
  63.0 10.2 %collective-permute-start.10 = (bf16[4,24,3072]{2,1,0:T(8,128)(2,1)}, bf16[4,24,3072]{2,1,0:T(8,128)(2,1)}, u32[]{:S(2)}, u32[]{:S(2)}) collective-permute-start(bf16[4,24,3072]{2,1,0:T(8,128)(2,1)} %pad_maximum_fusion.4), channel_id=1, source_target_pairs={{0,8},{1,17},{2,10},{3,19},{4,12},{5,21},{6,14},{7,23},{8,0},{9,25... | collective-permute-start | bytes 1769480 | tf_op jit(solution)/shard_map/ppermute | solution.py:66
  65.8 10.4 %collective-permute-start.11 = (bf16[128,768]{1,0:T(8,128)(2,1)}, bf16[128,768]{1,0:T(8,128)(2,1)S(1)}, u32[]{:S(2)}, u32[]{:S(2)}) collective-permute-start(bf16[128,768]{1,0:T(8,128)(2,1)} %get-tuple-element.234), channel_id=1, source_target_pairs={{0,4},{1,5},{2,6},{3,7},{4,0},{5,1},{6,2},{7,3},{8,12},{9,13},{10,... | collective-permute-start | bytes 589832 | tf_op jit(solution)/shard_map/ppermute | solution.py:72
  76.2 76.1 %collective-permute-start.13 = (bf16[8,24,3072]{2,1,0:T(8,128)(2,1)S(1)}, bf16[8,24,3072]{2,1,0:T(8,128)(2,1)S(1)}, u32[]{:S(2)}, u32[]{:S(2)}) collective-permute-start(bf16[8,24,3072]{2,1,0:T(8,128)(2,1)S(1)} %pad_maximum_fusion.1.refs_0_), channel_id=1, source_target_pairs={{0,16},{1,9},{2,18},{3,11},{4,20},{5,13},{6,22},{7,15},{8,24},{9,1... | collective-permute-start | bytes 3538952 | tf_op jit(solution)/shard_map/ppermute | solution.py:66
  77.7 94.3 %collective-permute-start.16 = (bf16[8,24,3072]{2,1,0:T(8,128)(2,1)S(1)}, bf16[8,24,3072]{2,1,0:T(8,128)(2,1)}, u32[]{:S(2)}, u32[]{:S(2)}) collective-permute-start(bf16[8,24,3072]{2,1,0:T(8,128)(2,1)S(1)} %pad_maximum_fusion.1.refs_0_), channel_id=1, source_target_pairs={{0,1},{1,0},{2,3},{3,2},{4,5},{5,4},{6,7},{7,6},{8,9},{9,8},{10,11... | collective-permute-start | bytes 3538952 | tf_op jit(solution)/shard_map/ppermute | solution.py:69
  93.6 57.9 %collective-permute-start.14 = (bf16[1,96,768]{2,1,0:T(8,128)(2,1)S(1)}, bf16[1,96,768]{2,1,0:T(8,128)(2,1)S(1)}, u32[]{:S(2)}, u32[]{:S(2)}) collective-permute-start(bf16[1,96,768]{2,1,0:T(8,128)(2,1)S(1)} %get-tuple-element.253), channel_id=1, source_target_pairs={{0,4},{1,5},{2,6},{3,7},{4,0},{5,1},{6,2},{7,3},{8,12},{9,13},{10,... | collective-permute-start | bytes 442376 | tf_op jit(solution)/shard_map/ppermute | solution.py:66
  152.3 19.7 %collective-permute-start.17 = (bf16[8,24,3072]{2,1,0:T(8,128)(2,1)S(1)}, bf16[8,24,3072]{2,1,0:T(8,128)(2,1)}, u32[]{:S(2)}, u32[]{:S(2)}) collective-permute-start(bf16[8,24,3072]{2,1,0:T(8,128)(2,1)S(1)} %collective-permute-done.13.refs_1_), channel_id=1, source_target_pairs={{0,1},{1,0},{2,3},{3,2},{4,5},{5,4},{6,7},{7,6},{8,9},{9,8},{10,11... | collective-permute-start | bytes 3538952 | tf_op jit(solution)/shard_map/ppermute | solution.py:69
  155.0 16.1 %collective-permute-start.18 = (bf16[2,96,768]{2,1,0:T(8,128)(2,1)}, bf16[2,96,768]{2,1,0:T(8,128)(2,1)S(1)}, u32[]{:S(2)}, u32[]{:S(2)}) collective-permute-start(bf16[2,96,768]{2,1,0:T(8,128)(2,1)} %pad_maximum_fusion.10), channel_id=1, source_target_pairs={{0,2},{1,3},{2,0},{3,1},{4,6},{5,7},{6,4},{7,5},{8,10},{9,11},{10,... | collective-permute-start | bytes 884744 | tf_op jit(solution)/shard_map/ppermute | solution.py:66
  157.7 14.3 %collective-permute-start.19 = (bf16[128,768]{1,0:T(8,128)(2,1)}, bf16[128,768]{1,0:T(8,128)(2,1)S(1)}, u32[]{:S(2)}, u32[]{:S(2)}) collective-permute-start(bf16[128,768]{1,0:T(8,128)(2,1)} %slice.515), channel_id=1, source_target_pairs={{0,4},{1,5},{2,6},{3,7},{4,0},{5,1},{6,2},{7,3},{8,12},{9,13},{10,... | collective-permute-start | bytes 589832 | tf_op jit(solution)/shard_map/ppermute | solution.py:72
  176.0 10.2 %collective-permute-start.20 = (bf16[4,96,768]{2,1,0:T(8,128)(2,1)}, bf16[4,96,768]{2,1,0:T(8,128)(2,1)S(1)}, u32[]{:S(2)}, u32[]{:S(2)}) collective-permute-start(bf16[4,96,768]{2,1,0:T(8,128)(2,1)} %pad_maximum_fusion.5), channel_id=1, source_target_pairs={{0,8},{1,17},{2,10},{3,19},{4,12},{5,21},{6,14},{7,23},{8,0},{9,25... | collective-permute-start | bytes 1769480 | tf_op jit(solution)/shard_map/ppermute | solution.py:66
  186.3 19.2 %collective-permute-start.21 = (bf16[8,96,768]{2,1,0:T(8,128)(2,1)S(1)}, bf16[8,96,768]{2,1,0:T(8,128)(2,1)S(1)}, u32[]{:S(2)}, u32[]{:S(2)}) collective-permute-start(bf16[8,96,768]{2,1,0:T(8,128)(2,1)S(1)} %pad_maximum_fusion.2.refs_0_), channel_id=1, source_target_pairs={{0,16},{1,9},{2,18},{3,11},{4,20},{5,13},{6,22},{7,15},{8,24},{9,1... | collective-permute-start | bytes 3538952 | tf_op jit(solution)/shard_map/ppermute | solution.py:66
  186.7 18.8 %collective-permute-start.22 = (bf16[8,96,768]{2,1,0:T(8,128)(2,1)S(1)}, bf16[8,96,768]{2,1,0:T(8,128)(2,1)}, u32[]{:S(2)}, u32[]{:S(2)}) collective-permute-start(bf16[8,96,768]{2,1,0:T(8,128)(2,1)S(1)} %pad_maximum_fusion.2.refs_0_), channel_id=1, source_target_pairs={{0,1},{1,0},{2,3},{3,2},{4,5},{5,4},{6,7},{7,6},{8,9},{9,8},{10,11... | collective-permute-start | bytes 3538952 | tf_op jit(solution)/shard_map/ppermute | solution.py:69
  187.8 17.6 %collective-permute-start.23 = (bf16[192,768]{1,0:T(8,128)(2,1)}, bf16[192,768]{1,0:T(8,128)(2,1)S(1)}, u32[]{:S(2)}, u32[]{:S(2)}) collective-permute-start(bf16[192,768]{1,0:T(8,128)(2,1)} %get-tuple-element.280), channel_id=1, source_target_pairs={{0,4},{1,5},{2,6},{3,7},{4,0},{5,1},{6,2},{7,3},{8,12},{9,13},{10,... | collective-permute-start | bytes 884744 | tf_op jit(solution)/shard_map/ppermute | solution.py:72
  205.5 11.9 %collective-permute-start.24 = (bf16[8,96,768]{2,1,0:T(8,128)(2,1)S(1)}, bf16[8,96,768]{2,1,0:T(8,128)(2,1)S(1)}, u32[]{:S(2)}, u32[]{:S(2)}) collective-permute-start(bf16[8,96,768]{2,1,0:T(8,128)(2,1)S(1)} %collective-permute-done.21.refs_1_), channel_id=1, source_target_pairs={{0,1},{1,0},{2,3},{3,2},{4,5},{5,4},{6,7},{7,6},{8,9},{9,8},{10,11... | collective-permute-start | bytes 3538952 | tf_op jit(solution)/shard_map/ppermute | solution.py:69
  234.8 10.9 %collective-permute-start.26 = (bf16[16,768]{1,0:T(8,128)(2,1)S(1)}, bf16[16,768]{1,0:T(8,128)(2,1)S(1)}, u32[]{:S(2)}, u32[]{:S(2)}) collective-permute-start(bf16[16,768]{1,0:T(8,128)(2,1)S(1)} %bitcast.93), channel_id=1, source_target_pairs={{0,4},{1,5},{2,6},{3,7},{4,0},{5,1},{6,2},{7,3},{8,12},{9,13},{10,... | collective-permute-start | bytes 73736 | tf_op jit(solution)/shard_map/ppermute | solution.py:72
  237.1 14.8 %collective-permute-start.25 = (bf16[192,768]{1,0:T(8,128)(2,1)S(1)}, bf16[192,768]{1,0:T(8,128)(2,1)S(1)}, u32[]{:S(2)}, u32[]{:S(2)}) collective-permute-start(bf16[192,768]{1,0:T(8,128)(2,1)S(1)} %copy-done.30), channel_id=1, source_target_pairs={{0,4},{1,5},{2,6},{3,7},{4,0},{5,1},{6,2},{7,3},{8,12},{9,13},{10,... | collective-permute-start | bytes 884744 | tf_op jit(solution)/shard_map/ppermute | solution.py:72
  245.9 55.5 %collective-permute-start.27 = (bf16[1,24,768]{2,1,0:T(8,128)(2,1)S(1)}, bf16[1,24,768]{2,1,0:T(8,128)(2,1)S(1)}, u32[]{:S(2)}, u32[]{:S(2)}) collective-permute-start(bf16[1,24,768]{2,1,0:T(8,128)(2,1)S(1)} %maximum_bitcast_fusion), channel_id=1, source_target_pairs={{0,2},{1,3},{2,0},{3,1},{4,6},{5,7},{6,4},{7,5},{8,10},{9,11},{10,... | collective-permute-start | bytes 110600 | tf_op jit(solution)/shard_map/ppermute | solution.py:868
  331.1 14.1 %collective-permute-start.33 = (bf16[16,96,768]{2,1,0:T(8,128)(2,1)}, bf16[16,96,768]{2,1,0:T(8,128)(2,1)S(1)}, u32[]{:S(2)}, u32[]{:S(2)}) collective-permute-start(bf16[16,96,768]{2,1,0:T(8,128)(2,1)} %get-tuple-element.293), channel_id=1, source_target_pairs={{0,1},{1,0},{2,3},{3,2},{4,5},{5,4},{6,7},{7,6},{8,9},{9,8},{10,11... | collective-permute-start | bytes 7077896 | tf_op jit(solution)/shard_map/ppermute | solution.py:69
  331.3 13.9 %collective-permute-start.34 = (bf16[160,768]{1,0:T(8,128)(2,1)S(1)}, bf16[160,768]{1,0:T(8,128)(2,1)S(1)}, u32[]{:S(2)}, u32[]{:S(2)}) collective-permute-start(bf16[160,768]{1,0:T(8,128)(2,1)S(1)} %get-tuple-element.297), channel_id=1, source_target_pairs={{0,4},{1,5},{2,6},{3,7},{4,0},{5,1},{6,2},{7,3},{8,12},{9,13},{10,... | collective-permute-start | bytes 737288 | tf_op jit(solution)/shard_map/ppermute | solution.py:72
  355.9 18.5 %collective-permute-start.36 = (bf16[16,24,3072]{2,1,0:T(8,128)(2,1)}, bf16[16,24,3072]{2,1,0:T(8,128)(2,1)}, u32[]{:S(2)}, u32[]{:S(2)}) collective-permute-start(bf16[16,24,3072]{2,1,0:T(8,128)(2,1)} %get-tuple-element.306), channel_id=1, source_target_pairs={{0,1},{1,0},{2,3},{3,2},{4,5},{5,4},{6,7},{7,6},{8,9},{9,8},{10,11... | collective-permute-start | bytes 7077896 | tf_op jit(solution)/shard_map/ppermute | solution.py:69
  356.2 18.2 %collective-permute-start.35 = (bf16[8,96,768]{2,1,0:T(8,128)(2,1)S(1)}, bf16[8,96,768]{2,1,0:T(8,128)(2,1)}, u32[]{:S(2)}, u32[]{:S(2)}) collective-permute-start(bf16[8,96,768]{2,1,0:T(8,128)(2,1)S(1)} %add_convert_fusion.2), channel_id=1, source_target_pairs={{0,16},{1,9},{2,18},{3,11},{4,20},{5,13},{6,22},{7,15},{8,24},{9,1... | collective-permute-start | bytes 3538952 | tf_op jit(solution)/shard_map/ppermute | solution.py:66
  358.5 15.9 %collective-permute-start.37 = (bf16[192,768]{1,0:T(8,128)(2,1)}, bf16[192,768]{1,0:T(8,128)(2,1)S(1)}, u32[]{:S(2)}, u32[]{:S(2)}) collective-permute-start(bf16[192,768]{1,0:T(8,128)(2,1)} %slice.531), channel_id=1, source_target_pairs={{0,4},{1,5},{2,6},{3,7},{4,0},{5,1},{6,2},{7,3},{8,12},{9,13},{10,... | collective-permute-start | bytes 884744 | tf_op jit(solution)/shard_map/ppermute | solution.py:72
  377.4 19.9 %collective-permute-start.38 = (bf16[4,96,768]{2,1,0:T(8,128)(2,1)}, bf16[4,96,768]{2,1,0:T(8,128)(2,1)S(1)}, u32[]{:S(2)}, u32[]{:S(2)}) collective-permute-start(bf16[4,96,768]{2,1,0:T(8,128)(2,1)} %add_convert_fusion.6), channel_id=1, source_target_pairs={{0,8},{1,17},{2,10},{3,19},{4,12},{5,21},{6,14},{7,23},{8,0},{9,25... | collective-permute-start | bytes 1769480 | tf_op jit(solution)/shard_map/ppermute | solution.py:66
  384.2 13.1 %collective-permute-start.39 = (bf16[160,768]{1,0:T(8,128)(2,1)}, bf16[160,768]{1,0:T(8,128)(2,1)S(1)}, u32[]{:S(2)}, u32[]{:S(2)}) collective-permute-start(bf16[160,768]{1,0:T(8,128)(2,1)} %get-tuple-element.323), channel_id=1, source_target_pairs={{0,4},{1,5},{2,6},{3,7},{4,0},{5,1},{6,2},{7,3},{8,12},{9,13},{10,... | collective-permute-start | bytes 737288 | tf_op jit(solution)/shard_map/ppermute | solution.py:72
  399.6 12.8 %collective-permute-start.41 = (bf16[2,96,768]{2,1,0:T(8,128)(2,1)}, bf16[2,96,768]{2,1,0:T(8,128)(2,1)}, u32[]{:S(2)}, u32[]{:S(2)}) collective-permute-start(bf16[2,96,768]{2,1,0:T(8,128)(2,1)} %add_convert_fusion.10), channel_id=1, source_target_pairs={{0,2},{1,3},{2,0},{3,1},{4,6},{5,7},{6,4},{7,5},{8,10},{9,11},{10,... | collective-permute-start | bytes 884744 | tf_op jit(solution)/shard_map/ppermute | solution.py:66
  399.6 12.8 %collective-permute-start.42 = (bf16[16,24,768]{2,1,0:T(8,128)(2,1)}, bf16[16,24,768]{2,1,0:T(8,128)(2,1)S(1)}, u32[]{:S(2)}, u32[]{:S(2)}) collective-permute-start(bf16[16,24,768]{2,1,0:T(8,128)(2,1)} %get-tuple-element.336), channel_id=1, source_target_pairs={{0,1},{1,0},{2,3},{3,2},{4,5},{5,4},{6,7},{7,6},{8,9},{9,8},{10,11... | collective-permute-start | bytes 1769480 | tf_op jit(solution)/shard_map/ppermute | solution.py:69
  401.3 26.6 %collective-permute-start.40 = (bf16[8,24,3072]{2,1,0:T(8,128)(2,1)S(1)}, bf16[8,24,3072]{2,1,0:T(8,128)(2,1)S(1)}, u32[]{:S(2)}, u32[]{:S(2)}) collective-permute-start(bf16[8,24,3072]{2,1,0:T(8,128)(2,1)S(1)} %add_convert_fusion.1), channel_id=1, source_target_pairs={{0,16},{1,9},{2,18},{3,11},{4,20},{5,13},{6,22},{7,15},{8,24},{9,1... | collective-permute-start | bytes 3538952 | tf_op jit(solution)/shard_map/ppermute | solution.py:66
  413.9 12.0 %collective-permute-start.43 = (bf16[1,96,768]{2,1,0:T(8,128)(2,1)S(1)}, bf16[1,96,768]{2,1,0:T(8,128)(2,1)S(1)}, u32[]{:S(2)}, u32[]{:S(2)}) collective-permute-start(bf16[1,96,768]{2,1,0:T(8,128)(2,1)S(1)} %add_convert_fusion.14), channel_id=1, source_target_pairs={{0,4},{1,5},{2,6},{3,7},{4,0},{5,1},{6,2},{7,3},{8,12},{9,13},{10,... | collective-permute-start | bytes 442376 | tf_op jit(solution)/shard_map/ppermute | solution.py:66
  423.5 20.1 %collective-permute-start.45 = (bf16[8,24,768]{2,1,0:T(8,128)(2,1)}, bf16[8,24,768]{2,1,0:T(8,128)(2,1)}, u32[]{:S(2)}, u32[]{:S(2)}) collective-permute-start(bf16[8,24,768]{2,1,0:T(8,128)(2,1)} %add_convert_fusion.9), channel_id=1, source_target_pairs={{0,16},{1,9},{2,18},{3,11},{4,20},{5,13},{6,22},{7,15},{8,24},{9,1... | collective-permute-start | bytes 884744 | tf_op jit(solution)/shard_map/ppermute | solution.py:66
  429.7 14.0 %collective-permute-start.44 = (bf16[4,24,3072]{2,1,0:T(8,128)(2,1)S(1)}, bf16[4,24,3072]{2,1,0:T(8,128)(2,1)S(1)}, u32[]{:S(2)}, u32[]{:S(2)}) collective-permute-start(bf16[4,24,3072]{2,1,0:T(8,128)(2,1)S(1)} %add_convert_fusion.5), channel_id=1, source_target_pairs={{0,8},{1,17},{2,10},{3,19},{4,12},{5,21},{6,14},{7,23},{8,0},{9,25... | collective-permute-start | bytes 1769480 | tf_op jit(solution)/shard_map/ppermute | solution.py:66
  430.7 12.9 %collective-permute-start.46 = (bf16[160,768]{1,0:T(8,128)(2,1)}, bf16[160,768]{1,0:T(8,128)(2,1)S(1)}, u32[]{:S(2)}, u32[]{:S(2)}) collective-permute-start(bf16[160,768]{1,0:T(8,128)(2,1)} %get-tuple-element.354), channel_id=1, source_target_pairs={{0,4},{1,5},{2,6},{3,7},{4,0},{5,1},{6,2},{7,3},{8,12},{9,13},{10,... | collective-permute-start | bytes 737288 | tf_op jit(solution)/shard_map/ppermute | solution.py:72
  445.3 13.2 %collective-permute-start.47 = (bf16[2,24,3072]{2,1,0:T(8,128)(2,1)S(1)}, bf16[2,24,3072]{2,1,0:T(8,128)(2,1)S(1)}, u32[]{:S(2)}, u32[]{:S(2)}) collective-permute-start(bf16[2,24,3072]{2,1,0:T(8,128)(2,1)S(1)} %add_convert_fusion.8), channel_id=1, source_target_pairs={{0,2},{1,3},{2,0},{3,1},{4,6},{5,7},{6,4},{7,5},{8,10},{9,11},{10,... | collective-permute-start | bytes 884744 | tf_op jit(solution)/shard_map/ppermute | solution.py:66
  448.4 10.0 %collective-permute-start.48 = (bf16[4,24,768]{2,1,0:T(8,128)(2,1)S(1)}, bf16[4,24,768]{2,1,0:T(8,128)(2,1)S(1)}, u32[]{:S(2)}, u32[]{:S(2)}) collective-permute-start(bf16[4,24,768]{2,1,0:T(8,128)(2,1)S(1)} %add_convert_fusion.13), channel_id=1, source_target_pairs={{0,8},{1,17},{2,10},{3,19},{4,12},{5,21},{6,14},{7,23},{8,0},{9,25... | collective-permute-start | bytes 442376 | tf_op jit(solution)/shard_map/ppermute | solution.py:66
  458.4 14.2 %collective-permute-start.49 = (bf16[16,24,2432]{2,1,0:T(8,128)(2,1)}, bf16[16,24,2432]{2,1,0:T(8,128)(2,1)S(1)}, u32[]{:S(2)}, u32[]{:S(2)}) collective-permute-start(bf16[16,24,2432]{2,1,0:T(8,128)(2,1)} %get-tuple-element.373), channel_id=1, source_target_pairs={{0,1},{1,0},{2,3},{3,2},{4,5},{5,4},{6,7},{7,6},{8,9},{9,8},{10,11... | collective-permute-start | bytes 5603336 | tf_op jit(solution)/shard_map/ppermute | solution.py:69
  458.5 14.1 %collective-permute-start.51 = (bf16[160,768]{1,0:T(8,128)(2,1)S(1)}, bf16[160,768]{1,0:T(8,128)(2,1)S(1)}, u32[]{:S(2)}, u32[]{:S(2)}) collective-permute-start(bf16[160,768]{1,0:T(8,128)(2,1)S(1)} %copy-done.35), channel_id=1, source_target_pairs={{0,4},{1,5},{2,6},{3,7},{4,0},{5,1},{6,2},{7,3},{8,12},{9,13},{10,... | collective-permute-start | bytes 737288 | tf_op jit(solution)/shard_map/ppermute | solution.py:72
  460.4 12.2 %collective-permute-start.50 = (bf16[2,24,768]{2,1,0:T(8,128)(2,1)S(1)}, bf16[2,24,768]{2,1,0:T(8,128)(2,1)S(1)}, u32[]{:S(2)}, u32[]{:S(2)}) collective-permute-start(bf16[2,24,768]{2,1,0:T(8,128)(2,1)S(1)} %add_convert_fusion.16), channel_id=1, source_target_pairs={{0,2},{1,3},{2,0},{3,1},{4,6},{5,7},{6,4},{7,5},{8,10},{9,11},{10,... | collective-permute-start | bytes 221192 | tf_op jit(solution)/shard_map/ppermute | solution.py:66
  475.7 13.8 %collective-permute-start.52 = (bf16[8,24,2432]{2,1,0:T(8,128)(2,1)}, bf16[8,24,2432]{2,1,0:T(8,128)(2,1)S(1)}, u32[]{:S(2)}, u32[]{:S(2)}) collective-permute-start(bf16[8,24,2432]{2,1,0:T(8,128)(2,1)} %add_convert_fusion.3), channel_id=1, source_target_pairs={{0,16},{1,9},{2,18},{3,11},{4,20},{5,13},{6,22},{7,15},{8,24},{9,1... | collective-permute-start | bytes 2801672 | tf_op jit(solution)/shard_map/ppermute | solution.py:66
  476.6 28.6 %collective-permute-start.56 = (bf16[192,768]{1,0:T(8,128)(2,1)}, bf16[192,768]{1,0:T(8,128)(2,1)S(1)}, u32[]{:S(2)}, u32[]{:S(2)}) collective-permute-start(bf16[192,768]{1,0:T(8,128)(2,1)} %slice.537), channel_id=1, source_target_pairs={{0,4},{1,5},{2,6},{3,7},{4,0},{5,1},{6,2},{7,3},{8,12},{9,13},{10,... | collective-permute-start | bytes 884744 | tf_op jit(solution)/shard_map/ppermute | solution.py:72
  490.7 14.5 %collective-permute-start.53 = (bf16[4,24,2432]{2,1,0:T(8,128)(2,1)S(1)}, bf16[4,24,2432]{2,1,0:T(8,128)(2,1)S(1)}, u32[]{:S(2)}, u32[]{:S(2)}) collective-permute-start(bf16[4,24,2432]{2,1,0:T(8,128)(2,1)S(1)} %add_convert_fusion.7), channel_id=1, source_target_pairs={{0,8},{1,17},{2,10},{3,19},{4,12},{5,21},{6,14},{7,23},{8,0},{9,25... | collective-permute-start | bytes 1400840 | tf_op jit(solution)/shard_map/ppermute | solution.py:66
  494.0 9.1 %collective-permute-start.54 = (bf16[1,24,3072]{2,1,0:T(8,128)(2,1)S(1)}, bf16[1,24,3072]{2,1,0:T(8,128)(2,1)S(1)}, u32[]{:S(2)}, u32[]{:S(2)}) collective-permute-start(bf16[1,24,3072]{2,1,0:T(8,128)(2,1)S(1)} %add_convert_fusion.12), channel_id=1, source_target_pairs={{0,4},{1,5},{2,6},{3,7},{4,0},{5,1},{6,2},{7,3},{8,12},{9,13},{10,... | collective-permute-start | bytes 442376 | tf_op jit(solution)/shard_map/ppermute | solution.py:66
  (71 other events, 810.6 us)

commit v4 on v3

--- a/solution.py
+++ b/solution.py
@@ -173,14 +173,18 @@
         split_slabs(refs[0][...], core, chips, mine_ref, theirs_ref, tail, within)
 
 
-def weight_grad(left, right, slots, tile, extra=None):
+def weight_grad(left, right, slots, tile, extra=None, room=0, into=()):
     rows, height = left.shape
     width = right.shape[1]
     chips = slots.shape[1]
     slab = height // (2 * chips)
-    total = width + (0 if extra is None else extra.shape[1])
+    total = width + (room if extra is None else extra.shape[1])
+    first = 0
+    if into:
+        total = into[0].shape[2]
+        first = (total - width) // tile
     block = (chips, slab, total if extra is not None else tile)
-    place = (lambda j, t: (0, 0, 0)) if extra is not None else (lambda j, t: (0, 0, j))
+    place = (lambda j, t: (0, 0, 0)) if extra is not None else (lambda j, t: (0, 0, j + first))
     return pl.pallas_call(
         functools.partial(weight_grad_kernel, chips, extra is not None),
         grid_spec=pltpu.PrefetchScalarGridSpec(
@@ -190,10 +194,12 @@
                 pl.BlockSpec((rows, height), lambda j, t: (0, 0)),
                 pl.BlockSpec((rows, tile), lambda j, t: (0, j)),
             ]
-            + ([] if extra is None else [pl.BlockSpec((height, 128), lambda j, t: (0, 0))]),
+            + ([] if extra is None else [pl.BlockSpec((height, 128), lambda j, t: (0, 0))])
+            + [pl.BlockSpec(memory_space=pl.ANY)] * len(into),
             out_specs=[pl.BlockSpec(block, place)] * 2,
         ),
         out_shape=[jax.ShapeDtypeStruct((chips, slab, total), BF16)] * 2,
+        input_output_aliases={3: 0, 4: 1} if into else {},
         compiler_params=pltpu.CompilerParams(vmem_limit_bytes=VMEM_LIMIT),
         cost_estimate=pl.CostEstimate(
             flops=2 * rows * height * width,
@@ -201,7 +207,7 @@
             transcendentals=0,
         ),
         name="weight_grad",
-    )(slots, left, right, *([] if extra is None else [extra]))
+    )(slots, left, right, *([] if extra is None else [extra]), *into)
 
 
 def tall_grad_kernel(chips, table_ref, left_ref, right_ref, mine_ref, theirs_ref):
@@ -317,33 +323,39 @@
         ).astype(BF16)
 
 
-def attention(qkv, qid, kid):
+def attention_more_kernel(qkv_ref, qid_ref, kid_ref, _, __, context_ref, probs_ref):
+    attention_kernel(qkv_ref, qid_ref, kid_ref, context_ref, probs_ref)
+
+
+def attention(qkv, qid, kid, start, count, into=()):
     rows = qkv.shape[0]
     blocks = rows // BLOCK
     return pl.pallas_call(
-        attention_kernel,
-        grid=(blocks,),
+        attention_more_kernel if into else attention_kernel,
+        grid=(count,),
         in_specs=[
-            pl.BlockSpec((BLOCK, 3 * D), lambda i: (i, 0)),
-            pl.BlockSpec((BLOCK, 1), lambda i: (i, 0)),
-            pl.BlockSpec((1, 1, BLOCK), lambda i: (i, 0, 0)),
-        ],
+            pl.BlockSpec((BLOCK, 3 * D), lambda i: (i + start, 0)),
+            pl.BlockSpec((BLOCK, 1), lambda i: (i + start, 0)),
+            pl.BlockSpec((1, 1, BLOCK), lambda i: (i + start, 0, 0)),
+        ]
+        + [pl.BlockSpec(memory_space=pl.ANY)] * len(into),
         out_specs=[
-            pl.BlockSpec((BLOCK, D), lambda i: (i, 0)),
-            pl.BlockSpec((1, HEADS, BLOCK, BLOCK), lambda i: (i, 0, 0, 0)),
-        ],
+            pl.BlockSpec((BLOCK, D), lambda i: (i + start, 0)),
+            pl.BlockSpec((1, HEADS, BLOCK, BLOCK), lambda i: (i + start, 0, 0, 0)),
+        ],
+        input_output_aliases={3: 0, 4: 1} if into else {},
         out_shape=[
             jax.ShapeDtypeStruct((rows, D), BF16),
             jax.ShapeDtypeStruct((blocks, HEADS, BLOCK, BLOCK), BF16),
         ],
         compiler_params=pltpu.CompilerParams(vmem_limit_bytes=VMEM_LIMIT),
         cost_estimate=pl.CostEstimate(
-            flops=4 * rows * BLOCK * D * 2,
-            bytes_accessed=rows * (4 * D + HEADS * BLOCK) * 2,
-            transcendentals=rows * HEADS * BLOCK,
+            flops=4 * count * BLOCK * BLOCK * D * 2,
+            bytes_accessed=count * BLOCK * (4 * D + HEADS * BLOCK) * 2,
+            transcendentals=count * BLOCK * HEADS * BLOCK,
         ),
         name="attention",
-    )(qkv, qid, kid)
+    )(qkv, qid, kid, *into)
 
 
 def attention_back_kernel(qkv_ref, probs_ref, grad_ref, out_ref, sum_ref):
@@ -423,28 +435,22 @@
 
 
 def join_kernel(*refs):
-    count = len(refs) - 2
-    sources, out, sem = refs[:count], refs[count], refs[count + 1]
-    copies, row = [], 0
-    for k, source in enumerate(sources):
-        rows = source.shape[0]
-        copies.append(
-            pltpu.make_async_copy(source, out.at[pl.ds(row, rows)], sem.at[k])
-        )
-        copies[-1].start()
+    row = 0
+    for piece in refs[:-1]:
+        rows = piece.shape[0]
+        refs[-1][row : row + rows, :] = piece[...]
         row += rows
-    for copy in copies:
-        copy.wait()
 
 
 def join(pieces):
     rows, width = sum(x.shape[0] for x in pieces), pieces[0].shape[1]
     return pl.pallas_call(
         join_kernel,
-        in_specs=[pl.BlockSpec(memory_space=pl.ANY)] * len(pieces),
-        out_specs=pl.BlockSpec(memory_space=pl.ANY),
+        grid=(1,),
+        in_specs=[pl.BlockSpec(x.shape, lambda i: (0, 0)) for x in pieces],
+        out_specs=pl.BlockSpec((rows, width), lambda i: (0, 0)),
         out_shape=jax.ShapeDtypeStruct((rows, width), pieces[0].dtype),
-        scratch_shapes=[pltpu.SemaphoreType.DMA((len(pieces),))],
+        compiler_params=pltpu.CompilerParams(vmem_limit_bytes=VMEM_LIMIT),
         cost_estimate=pl.CostEstimate(
             flops=0, bytes_accessed=4 * rows * width, transcendentals=0
         ),
@@ -606,30 +612,36 @@
     slope_ref[...] = (phi + expanded * density).astype(BF16)
 
 
-def expand(mid_low, w_expand, b_expand):
+def expand_more_kernel(mid_ref, w_ref, b_ref, _, __, active_ref, slope_ref):
+    expand_kernel(mid_ref, w_ref, b_ref, active_ref, slope_ref)
+
+
+def expand(mid_low, w_expand, b_expand, start, count, into=()):
     rows = mid_low.shape[0]
-    tile_r, tile_f = 256, 1024
+    tile_r, tile_f = 256, FF // 4
     return pl.pallas_call(
-        expand_kernel,
-        grid=(FF // tile_f, rows // tile_r),
+        expand_more_kernel if into else expand_kernel,
+        grid=(count, rows // tile_r),
         in_specs=[
             pl.BlockSpec((tile_r, D), lambda j, i: (i, 0)),
-            pl.BlockSpec((D, tile_f), lambda j, i: (0, j)),
-            pl.BlockSpec((1, tile_f), lambda j, i: (0, j)),
-        ],
+            pl.BlockSpec((D, tile_f), lambda j, i: (0, j + start)),
+            pl.BlockSpec((1, tile_f), lambda j, i: (0, j + start)),
+        ]
+        + [pl.BlockSpec(memory_space=pl.ANY)] * len(into),
         out_specs=[
-            pl.BlockSpec((tile_r, tile_f), lambda j, i: (i, j)),
-            pl.BlockSpec((tile_r, tile_f), lambda j, i: (i, j)),
+            pl.BlockSpec((tile_r, tile_f), lambda j, i: (i, j + start)),
+            pl.BlockSpec((tile_r, tile_f), lambda j, i: (i, j + start)),
         ],
         out_shape=[jax.ShapeDtypeStruct((rows, FF), BF16)] * 2,
+        input_output_aliases={3: 0, 4: 1} if into else {},
         compiler_params=pltpu.CompilerParams(vmem_limit_bytes=VMEM_LIMIT),
         cost_estimate=pl.CostEstimate(
-            flops=2 * rows * D * FF,
-            bytes_accessed=2 * (rows * D + D * FF + 2 * rows * FF),
-            transcendentals=2 * rows * FF,
+            flops=2 * rows * D * count * tile_f,
+            bytes_accessed=2 * (rows * D + D * count * tile_f + 2 * rows * count * tile_f),
+            transcendentals=2 * rows * count * tile_f,
         ),
         name="expand",
-    )(mid_low, w_expand, b_expand)
+    )(mid_low, w_expand, b_expand, *into)
 
 
 def normalized(values):
@@ -758,7 +770,7 @@
 
     g1, g2, g3 = Gather(first), Gather(second), Gather(third)
     my_tokens, send_tokens = sides(rows_q, rows_p)
-    tokens_out = chunked(send_tokens, (4, 6, 4, 2))
+    tokens_out = chunked(send_tokens, (5, 6, 5))
     g1.mid()
     g1.send, tokens_out = tie(g1.send, tokens_out)
     g1.along_z()
@@ -795,28 +807,26 @@
     )
     g1.core_held()
     g2.pb_first()
-    tokens_in = tokens_in + hand(tokens_out[2:3])
-    g1.parts, g2.stack, g3.send, tokens_in, tokens_out = tie(
-        g1.parts, g2.stack, g3.send, tokens_in, tokens_out
+    tokens_in = tokens_in + hand(tokens_out[2:])
+    full_j, full_o, full_small = g1.whole([(0, 3 * D), (3 * D, D), (4 * D, 128)])
+    full_j, full_o, full_small, g2.stack, g3.send, tokens_in = tie(
+        full_j, full_o, full_small, g2.stack, g3.send, tokens_in
     )
     g2.send = g2.stack
     g2.pb_last()
     g2.core_stack()
-    tokens_in = tokens_in + hand(tokens_out[3:])
-    full_j, full_o, full_small = g1.whole([(0, 3 * D), (3 * D, D), (4 * D, 128)])
+    g3.mid()
     wj = full_j.reshape(D, 3 * D)
     wo = full_o.reshape(D, D)
     small = full_small.reshape(D, 128).astype(F32)
     vec = small[:, :8].T
     bias_e = small[:, 8:12].reshape(1, FF)
     bias_j = jnp.concatenate([vec[0], jnp.zeros((D,), F32), vec[1]])
-    wj, tokens_in, g3.send = tie(wj, tokens_in, g3.send)
-    g3.mid()
     tokens = join([my_tokens] + tokens_in)
     qkv = (dot(tokens, wj) + bias_j).astype(BF16)
 
     my_cot, send_cot = sides(question_cot.reshape(-1, D), passage_cot.reshape(-1, D))
-    cot_out = chunked(send_cot, (4, 6, 6))
+    cot_out = chunked(send_cot, (4, 5, 7))
     valid_q = (jnp.arange(lq, dtype=jnp.int32)[None, :] < question_len[:, None]).astype(jnp.int32)
     valid_p = (jnp.arange(lp, dtype=jnp.int32)[None, :] < passage_len[:, None]).astype(jnp.int32)
     my_valid, send_valid = sides(valid_q.reshape(-1), valid_p.reshape(-1))
@@ -827,28 +837,35 @@
     kid = jnp.where(valid > 0, seq, -1).reshape(rows // BLOCK, 1, BLOCK)
     row_mask = valid.reshape(rows, 1).astype(F32)
 
-    qkv, g2.held, g3.send, cot_out = tie(qkv, g2.held, g3.send, cot_out)
-    g2.core_held()
+    blocks = rows // BLOCK
+    later = blocks // 2
+    qkv, g3.send, cot_out = tie(qkv, g3.send, cot_out)
     g3.along_z()
     cot_in = hand(cot_out[:1])
-    context, probs = attention(qkv, qid, kid)
-    context, g2.parts, g3.send, cot_in, cot_out = tie(context, g2.parts, g3.send, cot_in, cot_out)
+    spread = attention(qkv, qid, kid, 0, later)
+    spread, g2.held, g3.send = tie(spread, g2.held, g3.send)
+    g2.core_held()
     g3.pb_first()
+    context, probs = attention(qkv, qid, kid, later, blocks - later, tuple(spread))
+    context, g2.parts, cot_in, cot_out = tie(context, g2.parts, cot_in, cot_out)
+    cot_in = cot_in + hand(cot_out[1:2])
     (full_e,) = g2.whole([(0, FF)])
     we = full_e.reshape(D, FF)
+    context, we, g3.stack = tie(context, we, g3.stack)
+    g3.send = g3.stack
+    g3.pb_last()
+    g3.core_stack()
     attended = dot(context, wo) + vec[2]
     norm_one, inverse_one = normalized(tokens.astype(F32) + attended)
     mid = norm_one * vec[3] + vec[4]
     mid_low = mid.astype(BF16)
-    mid_low, we, g3.stack, cot_in, cot_out = tie(mid_low, we, g3.stack, cot_in, cot_out)
-    g3.send = g3.stack
-    g3.pb_last()
-    g3.core_stack()
-    cot_in = cot_in + hand(cot_out[1:2])
-    active, slope = expand(mid_low, we, bias_e)
-    active, g3.held, g3.other, cot_in, cot_out = tie(active, g3.held, g3.other, cot_in, cot_out)
+    mid_low, cot_in, cot_out = tie(mid_low, cot_in, cot_out)
+    cot_in = cot_in + hand(cot_out[2:])
+    gelu = expand(mid_low, we, bias_e, 0, 2)
+    gelu, g3.held, g3.other, g3.stack = tie(gelu, g3.held, g3.other, g3.stack)
     g3.core_held()
-    cot_in = cot_in + hand(cot_out[2:])
+    active, slope = expand(mid_low, we, bias_e, 2, 2, tuple(gelu))
+    active, g3.parts, cot_in = tie(active, g3.parts, cot_in)
     (full_r,) = g3.whole([(0, D)])
     wr = full_r.reshape(FF, D)
     norm_two, inverse_two = normalized(mid + dot(active, wr) + vec[5])
@@ -919,12 +936,13 @@
     )
     even = share % 8 == 0
 
-    def gradient(left, right, tile, extra=None):
-        if not even:
-            return grad_plain(left, right, table, extra)
+    def gradient(left, right, **more):
         if left.shape[1] > D:
             return tall_grad(left, right, slots, places.nz)
-        return weight_grad(left, right, slots, tile, extra)
+        return weight_grad(left, right, slots, D, **more)
+
+    def plain(left, right, extra=None):
+        return grad_plain(left, right, table, extra)
 
     class Scatter:
         def __init__(self, mine, theirs):
@@ -965,7 +983,7 @@
             )
 
     send_out = chunked(out[own_rows:], (5, 6, 5))
-    sr = Scatter(*gradient(active, d_reduced, D))
+    sr = Scatter(*(gradient if even else plain)(active, d_reduced))
     sr.parts, sr.theirs, d_reduced, send_out = tie(sr.parts, sr.theirs, d_reduced, send_out)
     sr.cores()
     got_out = hand(send_out[:1])
@@ -973,43 +991,43 @@
     sr.parts, d_expanded, got_out, send_out = tie(sr.parts, d_expanded, got_out, send_out)
     sr.pb_first()
     got_out = got_out + hand(send_out[1:2])
-    se = Scatter(*gradient(mid_low, d_expanded, 1024))
-    se.parts, se.theirs, d_expanded = tie(se.parts, se.theirs, d_expanded)
-    se.cores()
+    if even:
+        partial = gradient(mid_low, d_expanded, room=D)
+    else:
+        partial = plain(mid_low, d_expanded)
+    partial, d_expanded = tie(partial, d_expanded)
     d_first, d_attended, sums_first = first_back(
         d_expanded, we, d_second, norm_one, inverse_one, vec[3][None, :]
     )
-    sr.parts, se.parts, d_attended, got_out, send_out = tie(
-        sr.parts, se.parts, d_attended, got_out, send_out
+    sr.parts, partial, d_attended, got_out, send_out = tie(
+        sr.parts, partial, d_attended, got_out, send_out
     )
     sr.pb_rest()
     got_out = got_out + hand(send_out[2:])
-    so = Scatter(*gradient(context, d_attended, D))
+    if even:
+        partial = gradient(context, d_attended, into=tuple(partial))
+    else:
+        also = plain(context, d_attended)
+        partial = [jnp.concatenate(x, axis=2) for x in zip(partial, also)]
+    se = Scatter(*partial)
+    se.parts, se.theirs, d_attended = tie(se.parts, se.theirs, d_attended)
+    se.cores()
     d_context = dot(d_attended, wo, ((1,), (1,))).astype(BF16)
-    sr.parts, se.parts, so.parts, so.theirs, d_context, got_out = tie(
-        sr.parts, se.parts, so.parts, so.theirs, d_context, got_out
-    )
+    sr.parts, se.parts, d_context, got_out = tie(sr.parts, se.parts, d_context, got_out)
     se.pb_first()
     sr.along_z()
-    so.cores()
-    blocks = rows // BLOCK
-    later = blocks // 2
     d_joined, sums_one = attention_back(qkv, probs, d_context, later, blocks - later)
-    sr.parts, so.parts, d_joined = tie(sr.parts, so.parts, d_joined)
+    sr.parts, d_joined = tie(sr.parts, d_joined)
     sr.mid()
     send_grad = (d_first[own_rows:] + dot(d_joined[own_rows:], wj, ((1,), (1,)))).astype(BF16)
     se.parts, sr.out, d_joined, send_grad = tie(
         se.parts, sr.out, d_joined, chunked(send_grad, (5, 5, 6))
     )
     se.pb_rest()
-    so.pb_first()
     got_grad = hand(send_grad[:1])
     d_joined, sums_two = attention_back(qkv, probs, d_context, 0, later, d_joined)
-    se.parts, so.parts, d_joined, got_grad, send_grad = tie(
-        se.parts, so.parts, d_joined, got_grad, send_grad
-    )
+    se.parts, d_joined, got_grad, send_grad = tie(se.parts, d_joined, got_grad, send_grad)
     se.along_z()
-    so.pb_rest()
     got_grad = got_grad + hand(send_grad[1:2])
     g_joined_bias = (sums_one + sums_two)[0]
     g_vec = jnp.concatenate(
@@ -1025,29 +1043,25 @@
     g_small = jnp.concatenate(
         [g_vec.T, g_bias_expand.reshape(D, 4), jnp.zeros((D, 116), F32)], axis=1
     )
-    sj = Scatter(*gradient(tokens, d_joined, D, g_small))
-    se.parts, so.parts, sj.parts, sj.theirs, d_joined = tie(
-        se.parts, so.parts, sj.parts, sj.theirs, d_joined
+    sj = Scatter(*(gradient if even else plain)(tokens, d_joined, extra=g_small))
+    se.parts, sj.parts, sj.theirs, d_joined, got_grad, send_grad = tie(
+        se.parts, sj.parts, sj.theirs, d_joined, got_grad, send_grad
     )
     sj.cores()
-    so.along_z()
+    got_grad = got_grad + hand(send_grad[2:])
     own_grad = d_first[:own_rows] + dot(d_joined[:own_rows], wj, ((1,), (1,)))
-    sj.parts, so.parts, own_grad, got_grad, send_grad = tie(
-        sj.parts, so.parts, own_grad, got_grad, send_grad
-    )
+    sj.parts, own_grad = tie(sj.parts, own_grad)
     sj.pb_first()
-    got_grad = got_grad + hand(send_grad[2:])
+    se.mid()
     out_q, out_p = deal(tower.reshape(1), out, got_out)
-    sj.parts, se.parts, so.parts = tie(sj.parts, se.parts, so.parts)
+    sj.parts, se.out, got_grad = tie(sj.parts, se.out, got_grad)
     sj.pb_rest()
-    se.mid()
-    so.mid()
-    sj.parts, se.out, so.out, got_grad = tie(sj.parts, se.out, so.out, got_grad)
+    grad_q, grad_p = deal(tower.reshape(1), own_grad, got_grad)
+    sj.parts, grad_q, grad_p = tie(sj.parts, grad_q, grad_p)
     sj.along_z()
-    grad_q, grad_p = deal(tower.reshape(1), own_grad, got_grad)
     sj.mid()
     grad_joined = sj.out[:, :, : 3 * D]
-    grad_output, grad_expand, grad_reduce = so.out, se.out, sr.out
+    grad_expand, grad_output, grad_reduce = se.out[:, :, :FF], se.out[:, :, FF:], sr.out
     extra = sj.out[:, :, 3 * D :]
     grad_vectors = extra[:, :, :8].transpose(0, 2, 1)
     grad_b_expand = extra[:, :, 8:12].reshape(2, 4 * share)

time: 532 us -> 446 us (0.84)
  Pallas kernels: 233 us -> 147 us
  waiting for transfers between devices: 107 us -> 119 us
  other arithmetic: 54.8 us -> 47.6 us
  starting transfers between devices: 56.3 us -> 50.6 us
    pallas_call x4 -> x6, Pallas kernels: 126 us -> 39.1 us  [the longest x2 20.3 us: expand(): pl.pallas_call(expand_more_kernel if into else expand_kernel, grid=(count...]
    ppermute x28 -> x24, waiting for transfers between devices: 46.3 us -> 53.4 us  [swap(): return lax.ppermute(values, AXES, self.pairs(step))]
    convert_element_type x12 -> x9, other arithmetic: 16.1 us -> 11 us  [move(): send = self.total(half, self.count).astype(BF16)]
    ppermute x28 -> x24, starting transfers between devices: 35.6 us -> 31.1 us  [swap(): return lax.ppermute(values, AXES, self.pairs(step))]
    ppermute x15 -> x14, waiting for transfers between devices: 51.4 us -> 54.4 us  [swap_tower(): lax.ppermute(values, 'pa', [(i, i ^ 2 * self.half) for i in range(self.pa...]
    ppermute x15 -> x14, starting transfers between devices: 15.4 us -> 14 us  [swap_tower(): lax.ppermute(values, 'pa', [(i, i ^ 2 * self.half) for i in range(self.pa...]
  transfers between devices with their start and end apart: 59 -> 53, of which waited for: 24 -> 25; matrix products, arithmetic and copies ran while one was open for 17% -> 19% of each run, Pallas kernels for 38% -> 26%
where the time goes in v4:
time: 446 us; the launch traced here: 437 us
  Pallas kernels  147 us (33%)
  waiting for transfers between devices  119 us (27%)
  starting transfers between devices  50.6 us (11%)
  other arithmetic  47.6 us (11%)
  matrix products  35.5 us (8%)
  local copies, waits for them, and re-layouts  35.1 us (8%)
    ppermute x14, waiting for transfers between devices, swap_tower(): lax.ppermute(values, 'pa', [(i, i ^ 2 * self.half) for i in range(self.pa...  54.4 us
    ppermute x24, waiting for transfers between devices, swap(): return lax.ppermute(values, AXES, self.pairs(step))  53.4 us
    dot_general x9, matrix products, dot(): lax.dot_general(left, right, (dims, ((), ())), preferred_element_type=F32)  35.5 us
    ppermute x24, starting transfers between devices, swap(): return lax.ppermute(values, AXES, self.pairs(step))  31.1 us
    pallas_call x3, Pallas kernels, weight_grad(): pl.pallas_call(functools.partial(weight_grad_kernel, chips, extra is not...  24.3 us
    pallas_call x2, Pallas kernels, attention_back(): pl.pallas_call(attention_back_more_kernel if more else attention_back_ker...  21.3 us
    pallas_call x2, Pallas kernels, expand(): pl.pallas_call(expand_more_kernel if into else expand_kernel, grid=(count...  20.3 us
    pallas_call x3, Pallas kernels, assemble(): pl.pallas_call(functools.partial(assemble_kernel, segments), out_shape=sh...  15.8 us
  transfers between devices with their start and end apart: 53, of which 25 were waited for; matrix products, arithmetic and copies ran while one was open for 19% of the time, Pallas kernels for 26%

profile of v4, /device:TPU:0, one launch (start us, length us, event | category | flops | bytes accessed | tf_op | source)
XLA Modules:
  0.0 436.9 jit_solution(3321410158333528387)
XLA Ops:
  3.4 4.1 collective-permute-start
  10.7 4.1 collective-permute-done
  15.6 3.4 collective-permute-start.2
  19.1 9.5 %collective-permute-done.1 = bf16[2,24,3200]{2,1,0:T(8,128)(2,1)S(1)} collective-permute-done((bf16[2,24,3200]{2,1,0:T(8,128)(2,1)S(1)}, bf16[2,24,3200]{2,1,0:T(8,128)(2,1)S(1)}, u32[]{:S(2)}, u32[]{:S(2)}) %collective-permute-start.1) | collective-permute-done | bytes 307232 | tf_op jit(solution)/shard_map/ppermute | solution.py:66
  32.6 6.7 %collective-permute-done.4 = bf16[1,24,3072]{2,1,0:T(8,128)(2,1)S(1)} collective-permute-done((bf16[1,24,3072]{2,1,0:T(8,128)(2,1)S(1)}, bf16[1,24,3072]{2,1,0:T(8,128)(2,1)S(1)}, u32[]{:S(2)}, u32[]{:S(2)}) %collective-permute-start.4) | collective-permute-done | bytes 147488 | tf_op jit(solution)/shard_map/ppermute | solution.py:66
  52.3 12.3 %collective-permute-done.7.refs_2_ = bf16[192,768]{1,0:T(8,128)(2,1)S(1)} collective-permute-done((bf16[192,768]{1,0:T(8,128)(2,1)S(1)}, bf16[192,768]{1,0:T(8,128)(2,1)S(1)}, u32[]{:S(2)}, u32[]{:S(2)}) %collective-permute-start.7) | collective-permute-done | bytes 294944 | tf_op jit(solution)/shard_map/ppermute | solution.py:72
  71.5 2.9 collective-permute-start.13
  74.4 5.6 %collective-permute-done.10 = bf16[4,24,3072]{2,1,0:T(8,128)(2,1)} collective-permute-done((bf16[4,24,3072]{2,1,0:T(8,128)(2,1)}, bf16[4,24,3072]{2,1,0:T(8,128)(2,1)}, u32[]{:S(2)}, u32[]{:S(2)}) %collective-permute-start.10) | collective-permute-done | bytes 589856 | tf_op jit(solution)/shard_map/ppermute | solution.py:66
  81.2 5.6 %assemble.3 = (bf16[16,2,24,2304]{3,2,1,0:T(8,128)(2,1)}, bf16[16,2,24,768]{3,2,1,0:T(8,128)(2,1)}, bf16[16,2,24,128]{3,2,1,0:T(8,128)(2,1)}) custom-call(s32[3,16]{1,0:T(4,128)} %get-tuple-element.488.idx_ref, bf16[8,24,3200]{2,1,0:T(8,128)(2,1)} %copy-done.4, bf16[8,24,3200]{2,1,0:T(8,128)(2,1)} %collective-permute-done.5.refs_1_, ...), custom_call_target="tpu_custom_call" | custom-call | bytes 9830400 | tf_op jit(solution)/shard_map/assemble/pallas_call | solution.py:118
  89.1 2.6 join.2.left_ref
  91.7 8.4 %add_convert_fusion.qkv_ref = bf16[1024,2304]{1,0:T(8,128)(2,1)} fusion(bf16[1024,768]{1,0:T(8,128)(2,1)} %join.2.left_ref, bf16[768,2304]{1,0:T(8,128)(2,1)} %bitcast.101, f32[2304]{0:T(1024)S(1)} %pad_maximum_fusion.15), kind=kOutput, calls=%fused_computation.2 | convolution fusion | flops 3628597248 | bytes 9839616 | tf_op jit(solution)/shard_map/dot_general | solution.py:76
  103.0 6.6 %attention.2 = (bf16[1024,768]{1,0:T(8,128)(2,1)}, bf16[4,12,256,256]{3,2,1,0:T(8,128)(2,1)}) custom-call(bf16[1024,2304]{1,0:T(8,128)(2,1)} %add_convert_fusion.qkv_ref, s32[1024,1]{1,0:T(8,128)} %fusion.11.qid_ref, s32[4,1,256]{2,1,0:T(1,128)} %compare_select_fusion.kid_ref), custom_call_target="tpu_custom_call" | custom-call | flops 805306368 | bytes 6291456 | tf_op jit(solution)/shard_map/attention/pallas_call | solution.py:333
  115.7 7.0 %attention.3 = (bf16[1024,768]{1,0:T(8,128)(2,1)}, bf16[4,12,256,256]{3,2,1,0:T(8,128)(2,1)}) custom-call(bf16[1024,2304]{1,0:T(8,128)(2,1)} %add_convert_fusion.qkv_ref, s32[1024,1]{1,0:T(8,128)} %fusion.11.qid_ref, s32[4,1,256]{2,1,0:T(1,128)} %compare_select_fusion.kid_ref, ...), custom_call_target="tpu_custom_call", output_to_operand_aliasing={{0}: (3, {}), {1}: (4, {})} | custom-call | flops 805306368 | bytes 6291456 | tf_op jit(solution)/shard_map/attention/pallas_call | solution.py:333
  126.4 5.0 %assemble.4 = bf16[16,2,24,3072]{3,2,1,0:T(8,128)(2,1)} custom-call(s32[3,16]{1,0:T(4,128)} %get-tuple-element.488.idx_ref, bf16[8,24,3072]{2,1,0:T(8,128)(2,1)} %copy-done.5, bf16[8,24,3072]{2,1,0:T(8,128)(2,1)} %copy-done.15, bf16[8,24,3072]{2,1,0:T(8,128)(2,1)} %collective-permute-done.16.refs_2_, bf16[8,24,3072]{2,1,0:T(8,128)(2,1)} %collective-permute-done.17.refs_3_), custom_call_target="tpu_custom_call" | custom-call | bytes 9437184 | tf_op jit(solution)/shard_map/assemble/pallas_call | solution.py:118
  132.3 2.8 fusion.45
  136.1 2.7 fusion
  138.8 10.5 %collective-permute-done.20.refs_2_ = bf16[160,768]{1,0:T(8,128)(2,1)S(1)} collective-permute-done((bf16[160,768]{1,0:T(8,128)(2,1)S(1)}, bf16[160,768]{1,0:T(8,128)(2,1)S(1)}, u32[]{:S(2)}, u32[]{:S(2)}) %collective-permute-start.20) | collective-permute-done | bytes 245792 | tf_op jit(solution)/shard_map/ppermute | solution.py:72
  149.3 10.2 %expand.2 = (bf16[1024,3072]{1,0:T(8,128)(2,1)}, bf16[1024,3072]{1,0:T(8,128)(2,1)}) custom-call(bf16[1024,768]{1,0:T(8,128)(2,1)} %get-tuple-element.250.mid_ref.left_ref, bf16[768,3072]{1,0:T(8,128)(2,1)} %bitcast.78, f32[1,3072]{1,0:T(1,128)} %reshape.653.b_ref), custom_call_target="tpu_custom_call" | custom-call | flops 2415919104 | bytes 10223616 | tf_op jit(solution)/shard_map/expand/pallas_call | solution.py:622
  171.1 10.1 %expand.3 = (bf16[1024,3072]{1,0:T(8,128)(2,1)}, bf16[1024,3072]{1,0:T(8,128)(2,1)}) custom-call(bf16[1024,768]{1,0:T(8,128)(2,1)} %get-tuple-element.250.mid_ref.left_ref, bf16[768,3072]{1,0:T(8,128)(2,1)} %bitcast.79, f32[1,3072]{1,0:T(1,128)} %reshape.653.b_ref, ...), custom_call_target="tpu_custom_call", output_to_operand_aliasing={{0}: (3, {}), {1}: (4, {})} | custom-call | flops 2415919104 | bytes 10223616 | tf_op jit(solution)/shard_map/expand/pallas_call | solution.py:622
  181.2 2.8 collective-permute-done.24.refs_3_
  185.0 5.2 %assemble.5 = bf16[16,2,96,768]{3,2,1,0:T(8,128)(2,1)} custom-call(s32[3,16]{1,0:T(4,128)} %get-tuple-element.488.idx_ref, bf16[8,96,768]{2,1,0:T(8,128)(2,1)} %copy-done.6, bf16[8,96,768]{2,1,0:T(8,128)(2,1)} %copy-done.16, bf16[8,96,768]{2,1,0:T(8,128)(2,1)} %copy-done.17, bf16[8,96,768]{2,1,0:T(8,128)(2,1)} %copy-done.18), custom_call_target="tpu_custom_call" | custom-call | bytes 9437184 | tf_op jit(solution)/shard_map/assemble/pallas_call | solution.py:118
  190.9 8.7 %fusion.46 = (f32[1024]{0:T(1024)S(1)}, f32[1024,768]{1,0:T(8,128)S(1)}) fusion(f32[768]{0:T(1024)S(1)} %get-tuple-element.432, bf16[1024,3072]{1,0:T(8,128)(2,1)S(1)} %copy-done.3, bf16[3072,768]{1,0:T(8,128)(2,1)} %bitcast.82, f32[768]{0:T(1024)S(1)} %get-tuple-element.433, f32[1024,768]{1,0:T(8,128)} %get-tuple-element.442.norm_ref, ...), kind=kOutput, calls=%fused_computation.189 | convolution fusion | flops 4835769344 | bytes 17314816 | tf_op jit(solution)/shard_map/dot_general | solution.py:76
  202.6 4.7 %collective-permute-done.25 = bf16[16,768]{1,0:T(8,128)(2,1)S(1)} collective-permute-done((bf16[16,768]{1,0:T(8,128)(2,1)S(1)}, bf16[16,768]{1,0:T(8,128)(2,1)S(1)}, u32[]{:S(2)}, u32[]{:S(2)}) %collective-permute-start.25) | collective-permute-done | bytes 24608 | tf_op jit(solution)/shard_map/ppermute | solution.py:72
  208.5 2.9 collective-permute-done.26
  215.0 2.7 join.3.cot_ref
  218.7 4.2 collective-permute-done.28
  226.5 6.5 %second_back.1 = (f32[1024,768]{1,0:T(8,128)}, bf16[1024,768]{1,0:T(8,128)(2,1)}, f32[8,768]{1,0:T(8,128)}) custom-call(bf16[1024,768]{1,0:T(8,128)(2,1)} %join.3.cot_ref, f32[4,4,768]{2,1,0:T(4,128)} %reshape.660.slot_ref, f32[1024,1]{1,0:T(8,128)} %copy.82.mask_ref, f32[1024,768]{1,0:T(8,128)} %get-tuple-element.440.norm_ref, f32[1024,1]{1,0:T(8,128)} %copy.83.inverse_ref, ...), custom_call_target="tpu_custom_call" | custom-call | flops 15728640 | bytes 9437184 | tf_op jit(solution)/shard_map/second_back/pallas_call | solution.py:540
  233.0 10.0 %tall_grad.1 = (bf16[16,96,768]{2,1,0:T(8,128)(2,1)}, bf16[16,96,768]{2,1,0:T(8,128)(2,1)}) custom-call(s32[3,16]{1,0:T(4,128)} %get-tuple-element.487.table_ref, bf16[1024,3072]{1,0:T(8,128)(2,1)} %get-tuple-element.264.left_ref, bf16[1024,768]{1,0:T(8,128)(2,1)} %get-tuple-element.278.right_ref.grad_ref), custom_call_target="tpu_custom_call" | custom-call | flops 4831838208 | bytes 12582912 | tf_op jit(solution)/shard_map/tall_grad/pallas_call | solution.py:230
  243.9 11.7 %hidden_grad.1 = (bf16[1024,3072]{1,0:T(8,128)(2,1)}, f32[1,3072]{1,0:T(1,128)}) custom-call(bf16[1024,768]{1,0:T(8,128)(2,1)} %get-tuple-element.278.right_ref.grad_ref, bf16[3072,768]{1,0:T(8,128)(2,1)} %bitcast.83, bf16[1024,3072]{1,0:T(8,128)(2,1)} %get-tuple-element.279.slope_ref), custom_call_target="tpu_custom_call" | custom-call | flops 4831838208 | bytes 18874368 | tf_op jit(solution)/shard_map/hidden_grad/pallas_call | solution.py:276
  260.6 10.1 %weight_grad.3 = (bf16[16,24,3840]{2,1,0:T(8,128)(2,1)}, bf16[16,24,3840]{2,1,0:T(8,128)(2,1)}) custom-call(s32[3,16]{1,0:T(4,128)} %get-tuple-element.487.table_ref, bf16[1024,768]{1,0:T(8,128)(2,1)} %get-tuple-element.250.mid_ref.left_ref, bf16[1024,3072]{1,0:T(8,128)(2,1)} %get-tuple-element.291.right_ref.hidden_ref), custom_call_target="tpu_custom_call" | custom-call | flops 4831838208 | bytes 12582912 | tf_op jit(solution)/shard_map/weight_grad/pallas_call | solution.py:188
  271.6 12.3 %first_back.1 = (f32[1024,768]{1,0:T(8,128)}, bf16[1024,768]{1,0:T(8,128)(2,1)}, f32[8,768]{1,0:T(8,128)}) custom-call(bf16[1024,3072]{1,0:T(8,128)(2,1)} %get-tuple-element.291.right_ref.hidden_ref, bf16[768,3072]{1,0:T(8,128)(2,1)} %bitcast.80, f32[1024,768]{1,0:T(8,128)} %get-tuple-element.292.second_ref, f32[1024,768]{1,0:T(8,128)} %get-tuple-element.442.norm_ref, ...), custom_call_target="tpu_custom_call" | custom-call | flops 4831838208 | bytes 22020096 | tf_op jit(solution)/shard_map/first_back/pallas_call | solution.py:580
  283.9 2.9 collective-permute-done.35.refs_1_
  286.8 5.1 %weight_grad.4 = (bf16[16,24,3840]{2,1,0:T(8,128)(2,1)}, bf16[16,24,3840]{2,1,0:T(8,128)(2,1)}) custom-call(s32[3,16]{1,0:T(4,128)} %get-tuple-element.487.table_ref, bf16[1024,768]{1,0:T(8,128)(2,1)} %get-tuple-element.245.left_ref, bf16[1024,768]{1,0:T(8,128)(2,1)} %get-tuple-element.307.right_ref, ...), custom_call_target="tpu_custom_call", output_to_operand_aliasing={{0}: (3, {}), {1}: (4, {})} | custom-call | flops 1207959552 | bytes 4325376 | tf_op jit(solution)/shard_map/weight_grad/pallas_call | solution.py:188
  294.8 4.0 convolution_convert_fusion.grad_ref
  298.8 9.2 %collective-permute-done.38.refs_2_ = bf16[160,768]{1,0:T(8,128)(2,1)S(1)} collective-permute-done((bf16[160,768]{1,0:T(8,128)(2,1)S(1)}, bf16[160,768]{1,0:T(8,128)(2,1)S(1)}, u32[]{:S(2)}, u32[]{:S(2)}) %collective-permute-start.38) | collective-permute-done | bytes 245792 | tf_op jit(solution)/shard_map/ppermute | solution.py:72
  313.7 10.8 %attention_back.2 = (bf16[1024,2304]{1,0:T(8,128)(2,1)}, f32[1,2304]{1,0:T(1,128)}) custom-call(bf16[1024,2304]{1,0:T(8,128)(2,1)} %add_convert_fusion.qkv_ref, bf16[4,12,256,256]{3,2,1,0:T(8,128)(2,1)} %get-tuple-element.322.probs_ref, bf16[1024,768]{1,0:T(8,128)(2,1)} %convolution_convert_fusion.grad_ref), custom_call_target="tpu_custom_call" | custom-call | flops 1610612736 | bytes 8650752 | tf_op jit(solution)/shard_map/attention_back/pallas_call | solution.py:409
  324.5 5.3 %add_convert_fusion.4 = bf16[512,768]{1,0:T(8,128)(2,1)S(1)} fusion(f32[1024,768]{1,0:T(8,128)} %get-tuple-element.331, bf16[768,2304]{1,0:T(8,128)(2,1)} %bitcast.102, bf16[1024,2304]{1,0:T(8,128)(2,1)} %get-tuple-element.335._), kind=kOutput, calls=%fused_computation.21 | convolution fusion | flops 1812725760 | bytes 8257536 | tf_op jit(solution)/shard_map/dot_general | solution.py:76
  335.2 6.0 %collective-permute-done.41 = bf16[1,96,768]{2,1,0:T(8,128)(2,1)S(1)} collective-permute-done((bf16[1,96,768]{2,1,0:T(8,128)(2,1)S(1)}, bf16[1,96,768]{2,1,0:T(8,128)(2,1)S(1)}, u32[]{:S(2)}, u32[]{:S(2)}) %collective-permute-start.41) | collective-permute-done | bytes 147488 | tf_op jit(solution)/shard_map/ppermute | solution.py:66
  350.5 10.6 %attention_back.3 = (bf16[1024,2304]{1,0:T(8,128)(2,1)}, f32[1,2304]{1,0:T(1,128)}) custom-call(bf16[1024,2304]{1,0:T(8,128)(2,1)} %add_convert_fusion.qkv_ref, bf16[4,12,256,256]{3,2,1,0:T(8,128)(2,1)} %get-tuple-element.322.probs_ref, bf16[1024,768]{1,0:T(8,128)(2,1)} %convolution_convert_fusion.grad_ref, ...), custom_call_target="tpu_custom_call", output_to_operand_aliasing={{0}: (3, {})} | custom-call | flops 1610612736 | bytes 8650752 | tf_op jit(solution)/shard_map/attention_back/pallas_call | solution.py:409
  369.9 9.1 %weight_grad.5 = (bf16[16,24,2432]{2,1,0:T(8,128)(2,1)}, bf16[16,24,2432]{2,1,0:T(8,128)(2,1)}) custom-call(s32[3,16]{1,0:T(4,128)} %get-tuple-element.487.table_ref, bf16[1024,768]{1,0:T(8,128)(2,1)} %join.2.left_ref, bf16[1024,2304]{1,0:T(8,128)(2,1)} %get-tuple-element.357.right_ref, f32[768,128]{1,0:T(8,128)} %maximum_maximum_fusion.refs_0_), custom_call_target="tpu_custom_call" | custom-call | flops 3623878656 | bytes 9830400 | tf_op jit(solution)/shard_map/weight_grad/pallas_call | solution.py:188
  379.0 3.0 collective-permute-done.45.refs_1_
  386.5 5.6 %slice_add_fusion.own_ref = f32[512,768]{1,0:T(8,128)} fusion(f32[1024,768]{1,0:T(8,128)} %get-tuple-element.331, bf16[768,2304]{1,0:T(8,128)(2,1)} %bitcast.103, bf16[1024,2304]{1,0:T(8,128)(2,1)S(1)} %bitcast.85), kind=kOutput, calls=%fused_computation.20 | convolution fusion | flops 1812332544 | bytes 9043968 | tf_op jit(solution)/shard_map/dot_general | solution.py:76
  393.0 8.4 %collective-permute-done.48 = bf16[1,24,3840]{2,1,0:T(8,128)(2,1)S(1)} collective-permute-done((bf16[1,24,3840]{2,1,0:T(8,128)(2,1)S(1)}, bf16[1,24,3840]{2,1,0:T(8,128)(2,1)S(1)}, u32[]{:S(2)}, u32[]{:S(2)}) %collective-permute-start.48) | collective-permute-done | bytes 184352 | tf_op jit(solution)/shard_map/ppermute | solution.py:66
  402.8 4.8 %collective-permute-done.49.refs_2_ = bf16[192,768]{1,0:T(8,128)(2,1)S(1)} collective-permute-done((bf16[192,768]{1,0:T(8,128)(2,1)S(1)}, bf16[192,768]{1,0:T(8,128)(2,1)S(1)}, u32[]{:S(2)}, u32[]{:S(2)}) %collective-permute-start.49) | collective-permute-done | bytes 294944 | tf_op jit(solution)/shard_map/ppermute | solution.py:72
  409.8 3.6 deal.3
  413.4 3.8 collective-permute-done.50
  418.6 6.7 %collective-permute-done.51 = bf16[2,24,2432]{2,1,0:T(8,128)(2,1)S(1)} collective-permute-done((bf16[2,24,2432]{2,1,0:T(8,128)(2,1)S(1)}, bf16[2,24,2432]{2,1,0:T(8,128)(2,1)S(1)}, u32[]{:S(2)}, u32[]{:S(2)}) %collective-permute-start.51) | collective-permute-done | bytes 233504 | tf_op jit(solution)/shard_map/ppermute | solution.py:66
  427.9 2.6 deal.2
  (352 shorter events, 131.4 us)
Async XLA Ops:
  3.4 11.4 %collective-permute-start = (bf16[1,24,3200]{2,1,0:T(8,128)(2,1)S(1)}, bf16[1,24,3200]{2,1,0:T(8,128)(2,1)S(1)}, u32[]{:S(2)}, u32[]{:S(2)}) collective-permute-start(bf16[1,24,3200]{2,1,0:T(8,128)(2,1)S(1)} %get-tuple-element.460), channel_id=1, source_target_pairs={{0,4},{1,5},{2,6},{3,7},{4,0},{5,1},{6,2},{7,3},{8,12},{9,13},{10,... | collective-permute-start | bytes 460808 | tf_op jit(solution)/shard_map/ppermute | solution.py:66
  14.8 13.8 %collective-permute-start.1 = (bf16[2,24,3200]{2,1,0:T(8,128)(2,1)S(1)}, bf16[2,24,3200]{2,1,0:T(8,128)(2,1)S(1)}, u32[]{:S(2)}, u32[]{:S(2)}) collective-permute-start(bf16[2,24,3200]{2,1,0:T(8,128)(2,1)S(1)} %pad_maximum_fusion.8), channel_id=1, source_target_pairs={{0,2},{1,3},{2,0},{3,1},{4,6},{5,7},{6,4},{7,5},{8,10},{9,11},{10,... | collective-permute-start | bytes 921608 | tf_op jit(solution)/shard_map/ppermute | solution.py:66
  15.6 13.0 %collective-permute-start.2 = (bf16[160,768]{1,0:T(8,128)(2,1)S(1)}, bf16[160,768]{1,0:T(8,128)(2,1)S(1)}, u32[]{:S(2)}, u32[]{:S(2)}) collective-permute-start(bf16[160,768]{1,0:T(8,128)(2,1)S(1)} %get-tuple-element.199), channel_id=1, source_target_pairs={{0,4},{1,5},{2,6},{3,7},{4,0},{5,1},{6,2},{7,3},{8,12},{9,13},{10,... | collective-permute-start | bytes 737288 | tf_op jit(solution)/shard_map/ppermute | solution.py:72
  28.7 11.3 %collective-permute-start.3 = (bf16[4,24,3200]{2,1,0:T(8,128)(2,1)S(1)}, bf16[4,24,3200]{2,1,0:T(8,128)(2,1)S(1)}, u32[]{:S(2)}, u32[]{:S(2)}) collective-permute-start(bf16[4,24,3200]{2,1,0:T(8,128)(2,1)S(1)} %pad_maximum_fusion.4), channel_id=1, source_target_pairs={{0,8},{1,17},{2,10},{3,19},{4,12},{5,21},{6,14},{7,23},{8,0},{9,25... | collective-permute-start | bytes 1843208 | tf_op jit(solution)/shard_map/ppermute | solution.py:66
  30.1 9.2 %collective-permute-start.4 = (bf16[1,24,3072]{2,1,0:T(8,128)(2,1)S(1)}, bf16[1,24,3072]{2,1,0:T(8,128)(2,1)S(1)}, u32[]{:S(2)}, u32[]{:S(2)}) collective-permute-start(bf16[1,24,3072]{2,1,0:T(8,128)(2,1)S(1)} %get-tuple-element.201), channel_id=1, source_target_pairs={{0,4},{1,5},{2,6},{3,7},{4,0},{5,1},{6,2},{7,3},{8,12},{9,13},{10,... | collective-permute-start | bytes 442376 | tf_op jit(solution)/shard_map/ppermute | solution.py:66
  40.2 24.4 %collective-permute-start.5 = (bf16[8,24,3200]{2,1,0:T(8,128)(2,1)S(1)}, bf16[8,24,3200]{2,1,0:T(8,128)(2,1)}, u32[]{:S(2)}, u32[]{:S(2)}) collective-permute-start(bf16[8,24,3200]{2,1,0:T(8,128)(2,1)S(1)} %pad_maximum_fusion.refs_0_), channel_id=1, source_target_pairs={{0,16},{1,9},{2,18},{3,11},{4,20},{5,13},{6,22},{7,15},{8,24},{9,1... | collective-permute-start | bytes 3686408 | tf_op jit(solution)/shard_map/ppermute | solution.py:66
  43.9 7.5 %collective-permute-start.6 = (bf16[2,24,3072]{2,1,0:T(8,128)(2,1)S(1)}, bf16[2,24,3072]{2,1,0:T(8,128)(2,1)S(1)}, u32[]{:S(2)}, u32[]{:S(2)}) collective-permute-start(bf16[2,24,3072]{2,1,0:T(8,128)(2,1)S(1)} %copy-done.34), channel_id=1, source_target_pairs={{0,2},{1,3},{2,0},{3,1},{4,6},{5,7},{6,4},{7,5},{8,10},{9,11},{10,... | collective-permute-start | bytes 884744 | tf_op jit(solution)/shard_map/ppermute | solution.py:66
  47.9 33.3 %collective-permute-start.8 = (bf16[8,24,3200]{2,1,0:T(8,128)(2,1)S(1)}, bf16[8,24,3200]{2,1,0:T(8,128)(2,1)}, u32[]{:S(2)}, u32[]{:S(2)}) collective-permute-start(bf16[8,24,3200]{2,1,0:T(8,128)(2,1)S(1)} %pad_maximum_fusion.refs_0_), channel_id=1, source_target_pairs={{0,1},{1,0},{2,3},{3,2},{4,5},{5,4},{6,7},{7,6},{8,9},{9,8},{10,11... | collective-permute-start | bytes 3686408 | tf_op jit(solution)/shard_map/ppermute | solution.py:69
  47.9 16.6 %collective-permute-start.7 = (bf16[192,768]{1,0:T(8,128)(2,1)S(1)}, bf16[192,768]{1,0:T(8,128)(2,1)S(1)}, u32[]{:S(2)}, u32[]{:S(2)}) collective-permute-start(bf16[192,768]{1,0:T(8,128)(2,1)S(1)} %slice.437), channel_id=1, source_target_pairs={{0,4},{1,5},{2,6},{3,7},{4,0},{5,1},{6,2},{7,3},{8,12},{9,13},{10,... | collective-permute-start | bytes 884744 | tf_op jit(solution)/shard_map/ppermute | solution.py:72
  65.3 16.0 %collective-permute-start.9 = (bf16[8,24,3200]{2,1,0:T(8,128)(2,1)}, bf16[8,24,3200]{2,1,0:T(8,128)(2,1)}, u32[]{:S(2)}, u32[]{:S(2)}) collective-permute-start(bf16[8,24,3200]{2,1,0:T(8,128)(2,1)} %collective-permute-done.5.refs_1_), channel_id=1, source_target_pairs={{0,1},{1,0},{2,3},{3,2},{4,5},{5,4},{6,7},{7,6},{8,9},{9,8},{10,11... | collective-permute-start | bytes 3686408 | tf_op jit(solution)/shard_map/ppermute | solution.py:69
  69.8 10.2 %collective-permute-start.10 = (bf16[4,24,3072]{2,1,0:T(8,128)(2,1)}, bf16[4,24,3072]{2,1,0:T(8,128)(2,1)}, u32[]{:S(2)}, u32[]{:S(2)}) collective-permute-start(bf16[4,24,3072]{2,1,0:T(8,128)(2,1)} %pad_maximum_fusion.5), channel_id=1, source_target_pairs={{0,8},{1,17},{2,10},{3,19},{4,12},{5,21},{6,14},{7,23},{8,0},{9,25... | collective-permute-start | bytes 1769480 | tf_op jit(solution)/shard_map/ppermute | solution.py:66
  71.0 15.9 %collective-permute-start.11 = (bf16[160,768]{1,0:T(8,128)(2,1)}, bf16[160,768]{1,0:T(8,128)(2,1)S(1)}, u32[]{:S(2)}, u32[]{:S(2)}) collective-permute-start(bf16[160,768]{1,0:T(8,128)(2,1)} %get-tuple-element.216), channel_id=1, source_target_pairs={{0,4},{1,5},{2,6},{3,7},{4,0},{5,1},{6,2},{7,3},{8,12},{9,13},{10,... | collective-permute-start | bytes 737288 | tf_op jit(solution)/shard_map/ppermute | solution.py:72
  71.5 30.9 %collective-permute-start.13 = (s32[512]{0:T(512)S(1)}, s32[512]{0:T(512)S(1)}, u32[]{:S(2)}, u32[]{:S(2)}) collective-permute-start(s32[512]{0:T(512)S(1)} %get-tuple-element.472), channel_id=1, source_target_pairs={{0,4},{1,5},{2,6},{3,7},{4,0},{5,1},{6,2},{7,3},{8,12},{9,13},{10,... | collective-permute-start | bytes 6152 | tf_op jit(solution)/shard_map/ppermute | solution.py:72
  88.7 11.5 %collective-permute-start.12 = (bf16[1,96,768]{2,1,0:T(8,128)(2,1)S(1)}, bf16[1,96,768]{2,1,0:T(8,128)(2,1)S(1)}, u32[]{:S(2)}, u32[]{:S(2)}) collective-permute-start(bf16[1,96,768]{2,1,0:T(8,128)(2,1)S(1)} %copy-done.45), channel_id=1, source_target_pairs={{0,4},{1,5},{2,6},{3,7},{4,0},{5,1},{6,2},{7,3},{8,12},{9,13},{10,... | collective-permute-start | bytes 442376 | tf_op jit(solution)/shard_map/ppermute | solution.py:66
  88.7 21.8 %collective-permute-start.14 = (bf16[8,24,3072]{2,1,0:T(8,128)(2,1)S(1)}, bf16[8,24,3072]{2,1,0:T(8,128)(2,1)S(1)}, u32[]{:S(2)}, u32[]{:S(2)}) collective-permute-start(bf16[8,24,3072]{2,1,0:T(8,128)(2,1)S(1)} %pad_maximum_fusion.1.refs_0_), channel_id=1, source_target_pairs={{0,16},{1,9},{2,18},{3,11},{4,20},{5,13},{6,22},{7,15},{8,24},{9,1... | collective-permute-start | bytes 3538952 | tf_op jit(solution)/shard_map/ppermute | solution.py:66
  100.2 9.4 %collective-permute-start.15 = (bf16[2,96,768]{2,1,0:T(8,128)(2,1)S(1)}, bf16[2,96,768]{2,1,0:T(8,128)(2,1)S(1)}, u32[]{:S(2)}, u32[]{:S(2)}) collective-permute-start(bf16[2,96,768]{2,1,0:T(8,128)(2,1)S(1)} %pad_maximum_fusion.10), channel_id=1, source_target_pairs={{0,2},{1,3},{2,0},{3,1},{4,6},{5,7},{6,4},{7,5},{8,10},{9,11},{10,... | collective-permute-start | bytes 884744 | tf_op jit(solution)/shard_map/ppermute | solution.py:66
  103.0 23.3 %collective-permute-start.16 = (bf16[8,24,3072]{2,1,0:T(8,128)(2,1)S(1)}, bf16[8,24,3072]{2,1,0:T(8,128)(2,1)}, u32[]{:S(2)}, u32[]{:S(2)}) collective-permute-start(bf16[8,24,3072]{2,1,0:T(8,128)(2,1)S(1)} %pad_maximum_fusion.1.refs_0_), channel_id=1, source_target_pairs={{0,1},{1,0},{2,3},{3,2},{4,5},{5,4},{6,7},{7,6},{8,9},{9,8},{10,11... | collective-permute-start | bytes 3538952 | tf_op jit(solution)/shard_map/ppermute | solution.py:69
  110.5 15.8 %collective-permute-start.17 = (bf16[8,24,3072]{2,1,0:T(8,128)(2,1)S(1)}, bf16[8,24,3072]{2,1,0:T(8,128)(2,1)}, u32[]{:S(2)}, u32[]{:S(2)}) collective-permute-start(bf16[8,24,3072]{2,1,0:T(8,128)(2,1)S(1)} %collective-permute-done.14.refs_1_), channel_id=1, source_target_pairs={{0,1},{1,0},{2,3},{3,2},{4,5},{5,4},{6,7},{7,6},{8,9},{9,8},{10,11... | collective-permute-start | bytes 3538952 | tf_op jit(solution)/shard_map/ppermute | solution.py:69
  111.0 11.7 %collective-permute-start.19 = (bf16[4,96,768]{2,1,0:T(8,128)(2,1)}, bf16[4,96,768]{2,1,0:T(8,128)(2,1)}, u32[]{:S(2)}, u32[]{:S(2)}) collective-permute-start(bf16[4,96,768]{2,1,0:T(8,128)(2,1)} %pad_maximum_fusion.6), channel_id=1, source_target_pairs={{0,8},{1,17},{2,10},{3,19},{4,12},{5,21},{6,14},{7,23},{8,0},{9,25... | collective-permute-start | bytes 1769480 | tf_op jit(solution)/shard_map/ppermute | solution.py:66
  114.4 12.0 %collective-permute-start.18 = (bf16[128,768]{1,0:T(8,128)(2,1)}, bf16[128,768]{1,0:T(8,128)(2,1)S(1)}, u32[]{:S(2)}, u32[]{:S(2)}) collective-permute-start(bf16[128,768]{1,0:T(8,128)(2,1)} %slice.442), channel_id=1, source_target_pairs={{0,4},{1,5},{2,6},{3,7},{4,0},{5,1},{6,2},{7,3},{8,12},{9,13},{10,... | collective-permute-start | bytes 589832 | tf_op jit(solution)/shard_map/ppermute | solution.py:72
  131.4 28.1 %collective-permute-start.21 = (bf16[8,96,768]{2,1,0:T(8,128)(2,1)S(1)}, bf16[8,96,768]{2,1,0:T(8,128)(2,1)S(1)}, u32[]{:S(2)}, u32[]{:S(2)}) collective-permute-start(bf16[8,96,768]{2,1,0:T(8,128)(2,1)S(1)} %pad_maximum_fusion.2.refs_0_), channel_id=1, source_target_pairs={{0,16},{1,9},{2,18},{3,11},{4,20},{5,13},{6,22},{7,15},{8,24},{9,1... | collective-permute-start | bytes 3538952 | tf_op jit(solution)/shard_map/ppermute | solution.py:66
  131.9 27.5 %collective-permute-start.22 = (bf16[8,96,768]{2,1,0:T(8,128)(2,1)S(1)}, bf16[8,96,768]{2,1,0:T(8,128)(2,1)S(1)}, u32[]{:S(2)}, u32[]{:S(2)}) collective-permute-start(bf16[8,96,768]{2,1,0:T(8,128)(2,1)S(1)} %pad_maximum_fusion.2.refs_0_), channel_id=1, source_target_pairs={{0,1},{1,0},{2,3},{3,2},{4,5},{5,4},{6,7},{7,6},{8,9},{9,8},{10,11... | collective-permute-start | bytes 3538952 | tf_op jit(solution)/shard_map/ppermute | solution.py:69
  135.2 14.1 %collective-permute-start.20 = (bf16[160,768]{1,0:T(8,128)(2,1)S(1)}, bf16[160,768]{1,0:T(8,128)(2,1)S(1)}, u32[]{:S(2)}, u32[]{:S(2)}) collective-permute-start(bf16[160,768]{1,0:T(8,128)(2,1)S(1)} %copy-done.38), channel_id=1, source_target_pairs={{0,4},{1,5},{2,6},{3,7},{4,0},{5,1},{6,2},{7,3},{8,12},{9,13},{10,... | collective-permute-start | bytes 737288 | tf_op jit(solution)/shard_map/ppermute | solution.py:72
  160.6 23.4 %collective-permute-start.23 = (bf16[8,96,768]{2,1,0:T(8,128)(2,1)S(1)}, bf16[8,96,768]{2,1,0:T(8,128)(2,1)S(1)}, u32[]{:S(2)}, u32[]{:S(2)}) collective-permute-start(bf16[8,96,768]{2,1,0:T(8,128)(2,1)S(1)} %collective-permute-done.21.refs_1_), channel_id=1, source_target_pairs={{0,1},{1,0},{2,3},{3,2},{4,5},{5,4},{6,7},{7,6},{8,9},{9,8},{10,11... | collective-permute-start | bytes 3538952 | tf_op jit(solution)/shard_map/ppermute | solution.py:69
  166.8 17.2 %collective-permute-start.24 = (bf16[224,768]{1,0:T(8,128)(2,1)S(1)}, bf16[224,768]{1,0:T(8,128)(2,1)S(1)}, u32[]{:S(2)}, u32[]{:S(2)}) collective-permute-start(bf16[224,768]{1,0:T(8,128)(2,1)S(1)} %copy-done.26), channel_id=1, source_target_pairs={{0,4},{1,5},{2,6},{3,7},{4,0},{5,1},{6,2},{7,3},{8,12},{9,13},{10,... | collective-permute-start | bytes 1032200 | tf_op jit(solution)/shard_map/ppermute | solution.py:72
  211.4 6.2 %collective-permute-start.27 = (bf16[2,24,768]{2,1,0:T(8,128)(2,1)S(1)}, bf16[2,24,768]{2,1,0:T(8,128)(2,1)S(1)}, u32[]{:S(2)}, u32[]{:S(2)}) collective-permute-start(bf16[2,24,768]{2,1,0:T(8,128)(2,1)S(1)} %pad_maximum_fusion.13), channel_id=1, source_target_pairs={{0,8},{8,0},{16,24},{24,16},{1,9},{9,1},{17,25},{25,17},{2,10},{10... | collective-permute-start | bytes 221192 | tf_op jit(solution)/shard_map/ppermute | solution.py:889
  217.7 5.2 %collective-permute-start.28 = (bf16[4,24,768]{2,1,0:T(8,128)(2,1)S(1)}, bf16[4,24,768]{2,1,0:T(8,128)(2,1)S(1)}, u32[]{:S(2)}, u32[]{:S(2)}) collective-permute-start(bf16[4,24,768]{2,1,0:T(8,128)(2,1)S(1)} %pad_maximum_fusion.12), channel_id=1, source_target_pairs={{0,16},{8,24},{16,0},{24,8},{1,17},{9,25},{17,1},{25,9},{2,18},{10... | collective-permute-start | bytes 442376 | tf_op jit(solution)/shard_map/ppermute | solution.py:889
  243.0 14.1 %collective-permute-start.32 = (bf16[16,96,768]{2,1,0:T(8,128)(2,1)}, bf16[16,96,768]{2,1,0:T(8,128)(2,1)S(1)}, u32[]{:S(2)}, u32[]{:S(2)}) collective-permute-start(bf16[16,96,768]{2,1,0:T(8,128)(2,1)} %get-tuple-element.277), channel_id=1, source_target_pairs={{0,1},{1,0},{2,3},{3,2},{4,5},{5,4},{6,7},{7,6},{8,9},{9,8},{10,11... | collective-permute-start | bytes 7077896 | tf_op jit(solution)/shard_map/ppermute | solution.py:69
  243.1 14.0 %collective-permute-start.33 = (bf16[160,768]{1,0:T(8,128)(2,1)S(1)}, bf16[160,768]{1,0:T(8,128)(2,1)S(1)}, u32[]{:S(2)}, u32[]{:S(2)}) collective-permute-start(bf16[160,768]{1,0:T(8,128)(2,1)S(1)} %get-tuple-element.281), channel_id=1, source_target_pairs={{0,4},{1,5},{2,6},{3,7},{4,0},{5,1},{6,2},{7,3},{8,12},{9,13},{10,... | collective-permute-start | bytes 737288 | tf_op jit(solution)/shard_map/ppermute | solution.py:72
  258.8 28.0 %collective-permute-start.34 = (bf16[8,96,768]{2,1,0:T(8,128)(2,1)S(1)}, bf16[8,96,768]{2,1,0:T(8,128)(2,1)}, u32[]{:S(2)}, u32[]{:S(2)}) collective-permute-start(bf16[8,96,768]{2,1,0:T(8,128)(2,1)S(1)} %add_convert_fusion.2), channel_id=1, source_target_pairs={{0,16},{1,9},{2,18},{3,11},{4,20},{5,13},{6,22},{7,15},{8,24},{9,1... | collective-permute-start | bytes 3538952 | tf_op jit(solution)/shard_map/ppermute | solution.py:66
  270.7 16.1 %collective-permute-start.35 = (bf16[192,768]{1,0:T(8,128)(2,1)S(1)}, bf16[192,768]{1,0:T(8,128)(2,1)S(1)}, u32[]{:S(2)}, u32[]{:S(2)}) collective-permute-start(bf16[192,768]{1,0:T(8,128)(2,1)S(1)} %copy-done.33), channel_id=1, source_target_pairs={{0,4},{1,5},{2,6},{3,7},{4,0},{5,1},{6,2},{7,3},{8,12},{9,13},{10,... | collective-permute-start | bytes 884744 | tf_op jit(solution)/shard_map/ppermute | solution.py:72
  291.9 16.0 %collective-permute-start.37 = (bf16[16,24,3840]{2,1,0:T(8,128)(2,1)}, bf16[16,24,3840]{2,1,0:T(8,128)(2,1)S(1)}, u32[]{:S(2)}, u32[]{:S(2)}) collective-permute-start(bf16[16,24,3840]{2,1,0:T(8,128)(2,1)} %get-tuple-element.306), channel_id=1, source_target_pairs={{0,1},{1,0},{2,3},{3,2},{4,5},{5,4},{6,7},{7,6},{8,9},{9,8},{10,11... | collective-permute-start | bytes 8847368 | tf_op jit(solution)/shard_map/ppermute | solution.py:69
  293.6 14.4 %collective-permute-start.36 = (bf16[4,96,768]{2,1,0:T(8,128)(2,1)S(1)}, bf16[4,96,768]{2,1,0:T(8,128)(2,1)S(1)}, u32[]{:S(2)}, u32[]{:S(2)}) collective-permute-start(bf16[4,96,768]{2,1,0:T(8,128)(2,1)S(1)} %add_convert_fusion.6), channel_id=1, source_target_pairs={{0,8},{1,17},{2,10},{3,19},{4,12},{5,21},{6,14},{7,23},{8,0},{9,25... | collective-permute-start | bytes 1769480 | tf_op jit(solution)/shard_map/ppermute | solution.py:66
  294.8 13.2 %collective-permute-start.38 = (bf16[160,768]{1,0:T(8,128)(2,1)S(1)}, bf16[160,768]{1,0:T(8,128)(2,1)S(1)}, u32[]{:S(2)}, u32[]{:S(2)}) collective-permute-start(bf16[160,768]{1,0:T(8,128)(2,1)S(1)} %copy-done.43), channel_id=1, source_target_pairs={{0,4},{1,5},{2,6},{3,7},{4,0},{5,1},{6,2},{7,3},{8,12},{9,13},{10,... | collective-permute-start | bytes 737288 | tf_op jit(solution)/shard_map/ppermute | solution.py:72
  311.3 13.3 %collective-permute-start.40 = (bf16[2,96,768]{2,1,0:T(8,128)(2,1)}, bf16[2,96,768]{2,1,0:T(8,128)(2,1)S(1)}, u32[]{:S(2)}, u32[]{:S(2)}) collective-permute-start(bf16[2,96,768]{2,1,0:T(8,128)(2,1)} %add_convert_fusion.9), channel_id=1, source_target_pairs={{0,2},{1,3},{2,0},{3,1},{4,6},{5,7},{6,4},{7,5},{8,10},{9,11},{10,... | collective-permute-start | bytes 884744 | tf_op jit(solution)/shard_map/ppermute | solution.py:66
  312.7 30.6 %collective-permute-start.39 = (bf16[8,24,3840]{2,1,0:T(8,128)(2,1)}, bf16[8,24,3840]{2,1,0:T(8,128)(2,1)S(1)}, u32[]{:S(2)}, u32[]{:S(2)}) collective-permute-start(bf16[8,24,3840]{2,1,0:T(8,128)(2,1)} %add_convert_fusion.1), channel_id=1, source_target_pairs={{0,16},{1,9},{2,18},{3,11},{4,20},{5,13},{6,22},{7,15},{8,24},{9,1... | collective-permute-start | bytes 4423688 | tf_op jit(solution)/shard_map/ppermute | solution.py:66
  331.7 9.4 %collective-permute-start.41 = (bf16[1,96,768]{2,1,0:T(8,128)(2,1)S(1)}, bf16[1,96,768]{2,1,0:T(8,128)(2,1)S(1)}, u32[]{:S(2)}, u32[]{:S(2)}) collective-permute-start(bf16[1,96,768]{2,1,0:T(8,128)(2,1)S(1)} %add_convert_fusion.12), channel_id=1, source_target_pairs={{0,4},{1,5},{2,6},{3,7},{4,0},{5,1},{6,2},{7,3},{8,12},{9,13},{10,... | collective-permute-start | bytes 442376 | tf_op jit(solution)/shard_map/ppermute | solution.py:66
  344.7 18.3 %collective-permute-start.42 = (bf16[4,24,3840]{2,1,0:T(8,128)(2,1)}, bf16[4,24,3840]{2,1,0:T(8,128)(2,1)}, u32[]{:S(2)}, u32[]{:S(2)}) collective-permute-start(bf16[4,24,3840]{2,1,0:T(8,128)(2,1)} %add_convert_fusion.5), channel_id=1, source_target_pairs={{0,8},{1,17},{2,10},{3,19},{4,12},{5,21},{6,14},{7,23},{8,0},{9,25... | collective-permute-start | bytes 2211848 | tf_op jit(solution)/shard_map/ppermute | solution.py:66
  350.5 12.5 %collective-permute-start.43 = (bf16[160,768]{1,0:T(8,128)(2,1)}, bf16[160,768]{1,0:T(8,128)(2,1)}, u32[]{:S(2)}, u32[]{:S(2)}) collective-permute-start(bf16[160,768]{1,0:T(8,128)(2,1)} %get-tuple-element.337), channel_id=1, source_target_pairs={{0,4},{1,5},{2,6},{3,7},{4,0},{5,1},{6,2},{7,3},{8,12},{9,13},{10,... | collective-permute-start | bytes 737288 | tf_op jit(solution)/shard_map/ppermute | solution.py:72
  365.1 16.9 %collective-permute-start.44 = (bf16[2,24,3840]{2,1,0:T(8,128)(2,1)}, bf16[2,24,3840]{2,1,0:T(8,128)(2,1)}, u32[]{:S(2)}, u32[]{:S(2)}) collective-permute-start(bf16[2,24,3840]{2,1,0:T(8,128)(2,1)} %add_convert_fusion.8), channel_id=1, source_target_pairs={{0,2},{1,3},{2,0},{3,1},{4,6},{5,7},{6,4},{7,5},{8,10},{9,11},{10,... | collective-permute-start | bytes 1105928 | tf_op jit(solution)/shard_map/ppermute | solution.py:66
  369.6 12.4 %collective-permute-start.45 = (bf16[160,768]{1,0:T(8,128)(2,1)}, bf16[160,768]{1,0:T(8,128)(2,1)S(1)}, u32[]{:S(2)}, u32[]{:S(2)}) collective-permute-start(bf16[160,768]{1,0:T(8,128)(2,1)} %get-tuple-element.353), channel_id=1, source_target_pairs={{0,4},{1,5},{2,6},{3,7},{4,0},{5,1},{6,2},{7,3},{8,12},{9,13},{10,... | collective-permute-start | bytes 737288 | tf_op jit(solution)/shard_map/ppermute | solution.py:72
  382.0 10.1 %collective-permute-start.46 = (bf16[16,24,2432]{2,1,0:T(8,128)(2,1)}, bf16[16,24,2432]{2,1,0:T(8,128)(2,1)S(1)}, u32[]{:S(2)}, u32[]{:S(2)}) collective-permute-start(bf16[16,24,2432]{2,1,0:T(8,128)(2,1)} %get-tuple-element.356), channel_id=1, source_target_pairs={{0,1},{1,0},{2,3},{3,2},{4,5},{5,4},{6,7},{7,6},{8,9},{9,8},{10,11... | collective-permute-start | bytes 5603336 | tf_op jit(solution)/shard_map/ppermute | solution.py:69
  383.5 17.9 %collective-permute-start.48 = (bf16[1,24,3840]{2,1,0:T(8,128)(2,1)S(1)}, bf16[1,24,3840]{2,1,0:T(8,128)(2,1)S(1)}, u32[]{:S(2)}, u32[]{:S(2)}) collective-permute-start(bf16[1,24,3840]{2,1,0:T(8,128)(2,1)S(1)} %add_convert_fusion.11), channel_id=1, source_target_pairs={{0,4},{1,5},{2,6},{3,7},{4,0},{5,1},{6,2},{7,3},{8,12},{9,13},{10,... | collective-permute-start | bytes 552968 | tf_op jit(solution)/shard_map/ppermute | solution.py:66
  384.4 23.2 %collective-permute-start.49 = (bf16[192,768]{1,0:T(8,128)(2,1)S(1)}, bf16[192,768]{1,0:T(8,128)(2,1)S(1)}, u32[]{:S(2)}, u32[]{:S(2)}) collective-permute-start(bf16[192,768]{1,0:T(8,128)(2,1)S(1)} %copy-done.32), channel_id=1, source_target_pairs={{0,4},{1,5},{2,6},{3,7},{4,0},{5,1},{6,2},{7,3},{8,12},{9,13},{10,... | collective-permute-start | bytes 884744 | tf_op jit(solution)/shard_map/ppermute | solution.py:72
  392.3 15.3 %collective-permute-start.47 = (bf16[8,24,2432]{2,1,0:T(8,128)(2,1)S(1)}, bf16[8,24,2432]{2,1,0:T(8,128)(2,1)S(1)}, u32[]{:S(2)}, u32[]{:S(2)}) collective-permute-start(bf16[8,24,2432]{2,1,0:T(8,128)(2,1)S(1)} %add_convert_fusion.3), channel_id=1, source_target_pairs={{0,16},{1,9},{2,18},{3,11},{4,20},{5,13},{6,22},{7,15},{8,24},{9,1... | collective-permute-start | bytes 2801672 | tf_op jit(solution)/shard_map/ppermute | solution.py:66
  408.6 8.6 %collective-permute-start.50 = (bf16[4,24,2432]{2,1,0:T(8,128)(2,1)S(1)}, bf16[4,24,2432]{2,1,0:T(8,128)(2,1)S(1)}, u32[]{:S(2)}, u32[]{:S(2)}) collective-permute-start(bf16[4,24,2432]{2,1,0:T(8,128)(2,1)S(1)} %add_convert_fusion.7), channel_id=1, source_target_pairs={{0,8},{1,17},{2,10},{3,19},{4,12},{5,21},{6,14},{7,23},{8,0},{9,25... | collective-permute-start | bytes 1400840 | tf_op jit(solution)/shard_map/ppermute | solution.py:66
  418.4 6.9 %collective-permute-start.51 = (bf16[2,24,2432]{2,1,0:T(8,128)(2,1)S(1)}, bf16[2,24,2432]{2,1,0:T(8,128)(2,1)S(1)}, u32[]{:S(2)}, u32[]{:S(2)}) collective-permute-start(bf16[2,24,2432]{2,1,0:T(8,128)(2,1)S(1)} %add_convert_fusion.10), channel_id=1, source_target_pairs={{0,2},{1,3},{2,0},{3,1},{4,6},{5,7},{6,4},{7,5},{8,10},{9,11},{10,... | collective-permute-start | bytes 700424 | tf_op jit(solution)/shard_map/ppermute | solution.py:66
  426.3 6.9 %collective-permute-start.52 = (bf16[1,24,2432]{2,1,0:T(8,128)(2,1)S(1)}, bf16[1,24,2432]{2,1,0:T(8,128)(2,1)S(1)}, u32[]{:S(2)}, u32[]{:S(2)}) collective-permute-start(bf16[1,24,2432]{2,1,0:T(8,128)(2,1)S(1)} %add_convert_fusion.13), channel_id=1, source_target_pairs={{0,4},{1,5},{2,6},{3,7},{4,0},{5,1},{6,2},{7,3},{8,12},{9,13},{10,... | collective-permute-start | bytes 350216 | tf_op jit(solution)/shard_map/ppermute | solution.py:66
  (62 other events, 646.6 us)

commit v5 on v4

--- a/solution.py
+++ b/solution.py
@@ -618,7 +618,7 @@
 
 def expand(mid_low, w_expand, b_expand, start, count, into=()):
     rows = mid_low.shape[0]
-    tile_r, tile_f = 256, FF // 4
+    tile_r, tile_f = 256, FF // 2
     return pl.pallas_call(
         expand_more_kernel if into else expand_kernel,
         grid=(count, rows // tile_r),
@@ -768,14 +768,25 @@
     def hand(values):
         return [places.swap_tower(x) for x in values]
 
+    per_q = rows // lq
+    every = lp // lq
+    per_p = rows // lp
+    nq, np_ = question_in.shape[0], passage_in.shape[0]
+    shift = 2 * places.half
+    low_pa = pa % shift
     g1, g2, g3 = Gather(first), Gather(second), Gather(third)
     my_tokens, send_tokens = sides(rows_q, rows_p)
     tokens_out = chunked(send_tokens, (5, 6, 5))
     g1.mid()
-    g1.send, tokens_out = tie(g1.send, tokens_out)
+    g1.send, tokens_out, question_cot, passage_cot = tie(
+        g1.send, tokens_out, question_cot, passage_cot
+    )
     g1.along_z()
     tokens_in = hand(tokens_out[:1])
-    g1.send, g2.send, tokens_in = tie(g1.send, g2.send, tokens_in)
+    my_cot, send_cot = sides(question_cot.reshape(-1, D), passage_cot.reshape(-1, D))
+    g1.send, g2.send, tokens_in, my_cot, send_cot = tie(
+        g1.send, g2.send, tokens_in, my_cot, send_cot
+    )
     g1.pb_first()
     g2.mid()
     g1.stack, g2.send, tokens_out = tie(g1.stack, g2.send, tokens_out)
@@ -784,26 +795,8 @@
     g1.core_stack()
     g2.along_z()
     tokens_in = tokens_in + hand(tokens_out[1:2])
-    (
-        g1.held,
-        g2.send,
-        tokens_in,
-        tokens_out,
-        question_len,
-        passage_len,
-        positive,
-        question_cot,
-        passage_cot,
-    ) = tie(
-        g1.held,
-        g2.send,
-        tokens_in,
-        tokens_out,
-        question_len,
-        passage_len,
-        positive,
-        question_cot,
-        passage_cot,
+    g1.held, g2.send, tokens_in, tokens_out, question_len, passage_len, positive = tie(
+        g1.held, g2.send, tokens_in, tokens_out, question_len, passage_len, positive
     )
     g1.core_held()
     g2.pb_first()
@@ -825,8 +818,12 @@
     tokens = join([my_tokens] + tokens_in)
     qkv = (dot(tokens, wj) + bias_j).astype(BF16)
 
-    my_cot, send_cot = sides(question_cot.reshape(-1, D), passage_cot.reshape(-1, D))
-    cot_out = chunked(send_cot, (4, 5, 7))
+    cot_out = chunked(send_cot, (3, 3, 3, 4, 3))
+    by_pa = positive.reshape(places.pa_n, nq)
+    pair = [lax.dynamic_index_in_dim(by_pa, low_pa + k, 0, keepdims=False) for k in (0, shift)]
+    pair = jnp.concatenate(pair)[None]
+    wanted_rows = jnp.concatenate([pair // 16, pair % 16], axis=0).astype(BF16)
+    wanted_rows = jnp.pad(wanted_rows, ((0, 0), (0, D - per_q)))
     valid_q = (jnp.arange(lq, dtype=jnp.int32)[None, :] < question_len[:, None]).astype(jnp.int32)
     valid_p = (jnp.arange(lp, dtype=jnp.int32)[None, :] < passage_len[:, None]).astype(jnp.int32)
     my_valid, send_valid = sides(valid_q.reshape(-1), valid_p.reshape(-1))
@@ -843,43 +840,43 @@
     g3.along_z()
     cot_in = hand(cot_out[:1])
     spread = attention(qkv, qid, kid, 0, later)
-    spread, g2.held, g3.send = tie(spread, g2.held, g3.send)
+    spread, g2.held, g3.send, cot_in, cot_out = tie(spread, g2.held, g3.send, cot_in, cot_out)
     g2.core_held()
     g3.pb_first()
+    cot_in = cot_in + hand(cot_out[1:2])
     context, probs = attention(qkv, qid, kid, later, blocks - later, tuple(spread))
-    context, g2.parts, cot_in, cot_out = tie(context, g2.parts, cot_in, cot_out)
-    cot_in = cot_in + hand(cot_out[1:2])
-    (full_e,) = g2.whole([(0, FF)])
-    we = full_e.reshape(D, FF)
-    context, we, g3.stack = tie(context, we, g3.stack)
+    context, g2.parts, g3.stack, cot_in, cot_out = tie(context, g2.parts, g3.stack, cot_in, cot_out)
     g3.send = g3.stack
     g3.pb_last()
     g3.core_stack()
+    cot_in = cot_in + hand(cot_out[2:3])
+    (full_e,) = g2.whole([(0, FF)])
+    we = full_e.reshape(D, FF)
     attended = dot(context, wo) + vec[2]
     norm_one, inverse_one = normalized(tokens.astype(F32) + attended)
     mid = norm_one * vec[3] + vec[4]
     mid_low = mid.astype(BF16)
-    mid_low, cot_in, cot_out = tie(mid_low, cot_in, cot_out)
-    cot_in = cot_in + hand(cot_out[2:])
-    gelu = expand(mid_low, we, bias_e, 0, 2)
-    gelu, g3.held, g3.other, g3.stack = tie(gelu, g3.held, g3.other, g3.stack)
+    mid_low, we, cot_in, cot_out = tie(mid_low, we, cot_in, cot_out)
+    cot_in = cot_in + hand(cot_out[3:4])
+    gelu = expand(mid_low, we, bias_e, 0, 1)
+    gelu, g3.held, g3.other, g3.stack, cot_in, cot_out = tie(
+        gelu, g3.held, g3.other, g3.stack, cot_in, cot_out
+    )
     g3.core_held()
-    active, slope = expand(mid_low, we, bias_e, 2, 2, tuple(gelu))
+    cot_in = cot_in + hand(cot_out[4:])
+    active, slope = expand(mid_low, we, bias_e, 1, 1, tuple(gelu))
     active, g3.parts, cot_in = tie(active, g3.parts, cot_in)
     (full_r,) = g3.whole([(0, D)])
     wr = full_r.reshape(FF, D)
     norm_two, inverse_two = normalized(mid + dot(active, wr) + vec[5])
     out = ((norm_two * vec[6] + vec[7]) * row_mask).astype(BF16)
 
-    per_q = rows // lq
-    every = lp // lq
-    per_p = rows // lp
     firsts = out.reshape(per_q, lq, D)[:, 0, :]
     others = places.swap_tower(firsts)
     cls_q = jnp.where(is_q, firsts, others)
     cls_p = jnp.where(is_q, others, firsts)[::every]
-    pad = (-(per_q + per_p)) % 8
-    stack = jnp.concatenate([cls_q, cls_p, jnp.zeros((pad, D), BF16)], axis=0)[None]
+    pad = (-(per_q + per_p + 2)) % 8
+    stack = jnp.concatenate([cls_q, cls_p, wanted_rows, jnp.zeros((pad, D), BF16)], axis=0)[None]
     pair_masks = [0]
     for bit in bits_of(places.half):
         got = lax.ppermute(stack, "pa", [(i, i ^ (2 * bit)) for i in range(places.pa_n)])
@@ -892,26 +889,12 @@
     stack = jnp.concatenate([stack, places.swap_core(stack)], axis=0)
     pair_masks = pair_masks + [m ^ 1 for m in pair_masks]
     groups = len(pair_masks)
-    me = pb * places.pa_n + (pa % (2 * places.half))
+    me = pb * places.pa_n + low_pa
     place = jnp.array(pair_masks, jnp.int32) ^ me
-    shift = 2 * places.half
-    dev_q = jnp.stack([place, place + shift], axis=1)
     dev_p = jnp.stack([place + shift, place], axis=1)
-    nq, np_ = question_in.shape[0], passage_in.shape[0]
-    q_ids = (dev_q[:, :, None] * nq + jnp.arange(nq, dtype=jnp.int32)).reshape(-1)
     p_ids = (dev_p[:, :, None] * np_ + jnp.arange(np_, dtype=jnp.int32)).reshape(-1)
-    wanted = positive
-    pos_masks = [0]
-    for bit in bits_of(places.pb_n):
-        got = lax.ppermute(wanted, "pb", [(i, i ^ bit) for i in range(places.pb_n)])
-        wanted = jnp.concatenate([wanted, got])
-        pos_masks = pos_masks + [m ^ bit for m in pos_masks]
-    per_pb = positive.shape[0]
-    slot_of_pb = jnp.zeros((places.pb_n,), jnp.int32)
-    slot_of_pb = slot_of_pb.at[jnp.array(pos_masks, jnp.int32) ^ pb].set(
-        jnp.arange(places.pb_n, dtype=jnp.int32)
-    )
-    wanted = jnp.take(wanted, slot_of_pb[q_ids // per_pb] * per_pb + q_ids % per_pb)
+    digits = stack[:, per_q + per_p : per_q + per_p + 2, :per_q].astype(jnp.int32)
+    wanted = (digits[:, 0] * 16 + digits[:, 1]).reshape(-1)
 
     all_q = stack[:, :per_q].reshape(groups * per_q, D)
     all_p = stack[:, per_q : per_q + per_p].reshape(groups * per_p, D)
@@ -982,28 +965,30 @@
                 [jnp.where(is_q, keep, got), jnp.where(is_q, got, keep)], axis=0
             )
 
-    send_out = chunked(out[own_rows:], (5, 6, 5))
+    send_out = chunked(out[own_rows:], (4, 4, 4, 4))
+    d_reduced, send_out = tie(d_reduced, send_out)
+    got_out = hand(send_out[:1])
     sr = Scatter(*(gradient if even else plain)(active, d_reduced))
-    sr.parts, sr.theirs, d_reduced, send_out = tie(sr.parts, sr.theirs, d_reduced, send_out)
+    sr.parts, sr.theirs, d_reduced, got_out, send_out = tie(
+        sr.parts, sr.theirs, d_reduced, got_out, send_out
+    )
     sr.cores()
-    got_out = hand(send_out[:1])
+    got_out = got_out + hand(send_out[1:2])
     d_expanded, g_bias_expand = hidden_grad(d_reduced, wr, slope)
     sr.parts, d_expanded, got_out, send_out = tie(sr.parts, d_expanded, got_out, send_out)
     sr.pb_first()
-    got_out = got_out + hand(send_out[1:2])
+    got_out = got_out + hand(send_out[2:3])
     if even:
         partial = gradient(mid_low, d_expanded, room=D)
     else:
         partial = plain(mid_low, d_expanded)
-    partial, d_expanded = tie(partial, d_expanded)
+    partial, d_expanded, got_out, send_out = tie(partial, d_expanded, got_out, send_out)
+    got_out = got_out + hand(send_out[3:])
     d_first, d_attended, sums_first = first_back(
         d_expanded, we, d_second, norm_one, inverse_one, vec[3][None, :]
     )
-    sr.parts, partial, d_attended, got_out, send_out = tie(
-        sr.parts, partial, d_attended, got_out, send_out
-    )
+    sr.parts, partial, d_attended, got_out = tie(sr.parts, partial, d_attended, got_out)
     sr.pb_rest()
-    got_out = got_out + hand(send_out[2:])
     if even:
         partial = gradient(context, d_attended, into=tuple(partial))
     else:
@@ -1013,21 +998,16 @@
     se.parts, se.theirs, d_attended = tie(se.parts, se.theirs, d_attended)
     se.cores()
     d_context = dot(d_attended, wo, ((1,), (1,))).astype(BF16)
-    sr.parts, se.parts, d_context, got_out = tie(sr.parts, se.parts, d_context, got_out)
+    d_joined, sums_one = attention_back(qkv, probs, d_context, later, blocks - later)
+    sr.parts, se.parts, d_joined = tie(sr.parts, se.parts, d_joined)
     se.pb_first()
     sr.along_z()
-    d_joined, sums_one = attention_back(qkv, probs, d_context, later, blocks - later)
-    sr.parts, d_joined = tie(sr.parts, d_joined)
-    sr.mid()
     send_grad = (d_first[own_rows:] + dot(d_joined[own_rows:], wj, ((1,), (1,)))).astype(BF16)
-    se.parts, sr.out, d_joined, send_grad = tie(
-        se.parts, sr.out, d_joined, chunked(send_grad, (5, 5, 6))
-    )
-    se.pb_rest()
+    d_joined, send_grad = tie(d_joined, chunked(send_grad, (4, 4, 2, 6)))
     got_grad = hand(send_grad[:1])
     d_joined, sums_two = attention_back(qkv, probs, d_context, 0, later, d_joined)
-    se.parts, d_joined, got_grad, send_grad = tie(se.parts, d_joined, got_grad, send_grad)
-    se.along_z()
+    sr.parts, d_joined, got_grad, send_grad = tie(sr.parts, d_joined, got_grad, send_grad)
+    sr.mid()
     got_grad = got_grad + hand(send_grad[1:2])
     g_joined_bias = (sums_one + sums_two)[0]
     g_vec = jnp.concatenate(
@@ -1044,21 +1024,25 @@
         [g_vec.T, g_bias_expand.reshape(D, 4), jnp.zeros((D, 116), F32)], axis=1
     )
     sj = Scatter(*(gradient if even else plain)(tokens, d_joined, extra=g_small))
-    se.parts, sj.parts, sj.theirs, d_joined, got_grad, send_grad = tie(
-        se.parts, sj.parts, sj.theirs, d_joined, got_grad, send_grad
+    se.parts, sj.parts, sj.theirs, d_joined, sr.out, got_grad, send_grad = tie(
+        se.parts, sj.parts, sj.theirs, d_joined, sr.out, got_grad, send_grad
     )
     sj.cores()
-    got_grad = got_grad + hand(send_grad[2:])
+    se.pb_rest()
+    got_grad = got_grad + hand(send_grad[2:3])
     own_grad = d_first[:own_rows] + dot(d_joined[:own_rows], wj, ((1,), (1,)))
-    sj.parts, own_grad = tie(sj.parts, own_grad)
+    sj.parts, own_grad, got_grad, send_grad = tie(sj.parts, own_grad, got_grad, send_grad)
     sj.pb_first()
-    se.mid()
+    got_grad = got_grad + hand(send_grad[3:])
     out_q, out_p = deal(tower.reshape(1), out, got_out)
-    sj.parts, se.out, got_grad = tie(sj.parts, se.out, got_grad)
+    sj.parts, se.parts, got_grad = tie(sj.parts, se.parts, got_grad)
+    se.along_z()
     sj.pb_rest()
     grad_q, grad_p = deal(tower.reshape(1), own_grad, got_grad)
-    sj.parts, grad_q, grad_p = tie(sj.parts, grad_q, grad_p)
+    sj.parts, se.parts, grad_q, grad_p = tie(sj.parts, se.parts, grad_q, grad_p)
     sj.along_z()
+    se.mid()
+    sj.parts, se.out = tie(sj.parts, se.out)
     sj.mid()
     grad_joined = sj.out[:, :, : 3 * D]
     grad_expand, grad_output, grad_reduce = se.out[:, :, :FF], se.out[:, :, FF:], sr.out

time: 446 us -> 421 us (0.944)
  waiting for transfers between devices: 119 us -> 103 us
  starting transfers between devices: 50.6 us -> 57.8 us
  other arithmetic: 47.6 us -> 42.4 us
  local copies, waits for them, and re-layouts: 35.1 us -> 30.1 us
    ppermute x14 -> x18, waiting for transfers between devices: 54.4 us -> 29.9 us  [swap_tower(): lax.ppermute(values, 'pa', [(i, i ^ 2 * self.half) for i in range(self.pa...]
    ppermute x14 -> x18, starting transfers between devices: 14 us -> 26.3 us  [swap_tower(): lax.ppermute(values, 'pa', [(i, i ^ 2 * self.half) for i in range(self.pa...]
    ppermute x24, waiting for transfers between devices: 53.4 us -> 65.6 us  [swap(): return lax.ppermute(values, AXES, self.pairs(step))]
  transfers between devices with their start and end apart: 53 -> 55, of which waited for: 25 -> 27; matrix products, arithmetic and copies ran while one was open for 19% -> 17% of each run, Pallas kernels for 26% -> 28%
where the time goes in v5:
time: 421 us; the launch traced here: 414 us
  Pallas kernels  143 us (34%)
  waiting for transfers between devices  103 us (24%)
  starting transfers between devices  57.8 us (14%)
  other arithmetic  42.4 us (10%)
  matrix products  36 us (9%)
  local copies, waits for them, and re-layouts  30.1 us (7%)
    ppermute x24, waiting for transfers between devices, swap(): return lax.ppermute(values, AXES, self.pairs(step))  65.6 us
    dot_general x9, matrix products, dot(): lax.dot_general(left, right, (dims, ((), ())), preferred_element_type=F32)  36 us
    ppermute x18, waiting for transfers between devices, swap_tower(): lax.ppermute(values, 'pa', [(i, i ^ 2 * self.half) for i in range(self.pa...  29.9 us
    ppermute x24, starting transfers between devices, swap(): return lax.ppermute(values, AXES, self.pairs(step))  27.7 us
    ppermute x18, starting transfers between devices, swap_tower(): lax.ppermute(values, 'pa', [(i, i ^ 2 * self.half) for i in range(self.pa...  26.3 us
    pallas_call x3, Pallas kernels, weight_grad(): pl.pallas_call(functools.partial(weight_grad_kernel, chips, extra is not...  24 us
    pallas_call x2, Pallas kernels, attention_back(): pl.pallas_call(attention_back_more_kernel if more else attention_back_ker...  21.7 us
    pallas_call x2, Pallas kernels, expand(): pl.pallas_call(expand_more_kernel if into else expand_kernel, grid=(count...  16.1 us
  transfers between devices with their start and end apart: 55, of which 27 were waited for; matrix products, arithmetic and copies ran while one was open for 17% of the time, Pallas kernels for 28%

profile of v5, /device:TPU:0, one launch (start us, length us, event | category | flops | bytes accessed | tf_op | source)
XLA Modules:
  0.0 414.5 jit_solution(14635338230798320271)
XLA Ops:
  3.4 4.1 collective-permute-start
  7.5 2.5 bitcast_select_fusion.3
  11.5 3.3 collective-permute-done
  15.6 3.4 collective-permute-start.2
  20.2 8.4 %collective-permute-done.1 = bf16[2,24,3200]{2,1,0:T(8,128)(2,1)S(1)} collective-permute-done((bf16[2,24,3200]{2,1,0:T(8,128)(2,1)S(1)}, bf16[2,24,3200]{2,1,0:T(8,128)(2,1)S(1)}, u32[]{:S(2)}, u32[]{:S(2)}) %collective-permute-start.1) | collective-permute-done | bytes 307232 | tf_op jit(solution)/shard_map/ppermute | solution.py:66
  30.0 2.5 collective-permute-start.4
  32.6 6.7 %collective-permute-done.4 = bf16[1,24,3072]{2,1,0:T(8,128)(2,1)S(1)} collective-permute-done((bf16[1,24,3072]{2,1,0:T(8,128)(2,1)S(1)}, bf16[1,24,3072]{2,1,0:T(8,128)(2,1)S(1)}, u32[]{:S(2)}, u32[]{:S(2)}) %collective-permute-start.4) | collective-permute-done | bytes 147488 | tf_op jit(solution)/shard_map/ppermute | solution.py:66
  42.5 2.8 collective-permute-start.6
  50.8 13.7 %collective-permute-done.7.refs_2_ = bf16[192,768]{1,0:T(8,128)(2,1)S(1)} collective-permute-done((bf16[192,768]{1,0:T(8,128)(2,1)}, bf16[192,768]{1,0:T(8,128)(2,1)S(1)}, u32[]{:S(2)}, u32[]{:S(2)}) %collective-permute-start.7) | collective-permute-done | bytes 294944 | tf_op jit(solution)/shard_map/ppermute | solution.py:72
  67.1 2.9 collective-permute-start.13
  70.1 5.2 %collective-permute-done.10 = bf16[4,24,3072]{2,1,0:T(8,128)(2,1)S(1)} collective-permute-done((bf16[4,24,3072]{2,1,0:T(8,128)(2,1)S(1)}, bf16[4,24,3072]{2,1,0:T(8,128)(2,1)S(1)}, u32[]{:S(2)}, u32[]{:S(2)}) %collective-permute-start.10) | collective-permute-done | bytes 589856 | tf_op jit(solution)/shard_map/ppermute | solution.py:66
  76.4 5.5 %assemble.3 = (bf16[16,2,24,2304]{3,2,1,0:T(8,128)(2,1)}, bf16[16,2,24,768]{3,2,1,0:T(8,128)(2,1)}, bf16[16,2,24,128]{3,2,1,0:T(8,128)(2,1)}) custom-call(s32[3,16]{1,0:T(4,128)} %get-tuple-element.570.idx_ref, bf16[8,24,3200]{2,1,0:T(8,128)(2,1)} %copy-done.4, bf16[8,24,3200]{2,1,0:T(8,128)(2,1)} %collective-permute-done.5.refs_1_, ...), custom_call_target="tpu_custom_call" | custom-call | bytes 9830400 | tf_op jit(solution)/shard_map/assemble/pallas_call | solution.py:118
  84.2 2.6 join.2.left_ref
  86.9 8.5 %add_convert_fusion.qkv_ref = bf16[1024,2304]{1,0:T(8,128)(2,1)} fusion(bf16[1024,768]{1,0:T(8,128)(2,1)} %join.2.left_ref, bf16[768,2304]{1,0:T(8,128)(2,1)} %bitcast.93, f32[2304]{0:T(1024)S(1)} %pad_maximum_fusion.15), kind=kOutput, calls=%fused_computation | convolution fusion | flops 3628597248 | bytes 9839616 | tf_op jit(solution)/shard_map/dot_general | solution.py:76
  99.1 7.0 %attention.2 = (bf16[1024,768]{1,0:T(8,128)(2,1)}, bf16[4,12,256,256]{3,2,1,0:T(8,128)(2,1)}) custom-call(bf16[1024,2304]{1,0:T(8,128)(2,1)} %add_convert_fusion.qkv_ref, s32[1024,1]{1,0:T(8,128)} %fusion.11.qid_ref, s32[4,1,256]{2,1,0:T(1,128)} %compare_select_fusion.kid_ref), custom_call_target="tpu_custom_call" | custom-call | flops 805306368 | bytes 6291456 | tf_op jit(solution)/shard_map/attention/pallas_call | solution.py:333
  113.0 6.7 %attention.3 = (bf16[1024,768]{1,0:T(8,128)(2,1)}, bf16[4,12,256,256]{3,2,1,0:T(8,128)(2,1)}) custom-call(bf16[1024,2304]{1,0:T(8,128)(2,1)} %add_convert_fusion.qkv_ref, s32[1024,1]{1,0:T(8,128)} %fusion.11.qid_ref, s32[4,1,256]{2,1,0:T(1,128)} %compare_select_fusion.kid_ref, ...), custom_call_target="tpu_custom_call", output_to_operand_aliasing={{0}: (3, {}), {1}: (4, {})} | custom-call | flops 805306368 | bytes 6291456 | tf_op jit(solution)/shard_map/attention/pallas_call | solution.py:333
  123.6 2.8 fusion.44
  128.8 2.7 fusion
  131.5 4.8 %assemble.4 = bf16[16,2,24,3072]{3,2,1,0:T(8,128)(2,1)} custom-call(s32[3,16]{1,0:T(4,128)} %get-tuple-element.570.idx_ref, bf16[8,24,3072]{2,1,0:T(8,128)(2,1)} %pad_maximum_fusion.1.refs_0_, bf16[8,24,3072]{2,1,0:T(8,128)(2,1)} %copy-done.13, bf16[8,24,3072]{2,1,0:T(8,128)(2,1)} %copy-done.16, bf16[8,24,3072]{2,1,0:T(8,128)(2,1)} %collective-permute-done.18.refs_3_), custom_call_target="tpu_custom_call" | custom-call | bytes 9437184 | tf_op jit(solution)/shard_map/assemble/pallas_call | solution.py:118
  137.7 7.9 %expand.2 = (bf16[1024,3072]{1,0:T(8,128)(2,1)}, bf16[1024,3072]{1,0:T(8,128)(2,1)}) custom-call(bf16[1024,768]{1,0:T(8,128)(2,1)} %get-tuple-element.299.mid_ref.left_ref, bf16[768,3072]{1,0:T(8,128)(2,1)} %bitcast.72, f32[1,3072]{1,0:T(1,128)} %reshape.714.b_ref), custom_call_target="tpu_custom_call" | custom-call | flops 2415919104 | bytes 10223616 | tf_op jit(solution)/shard_map/expand/pallas_call | solution.py:622
  145.6 3.0 collective-permute-done.24.refs_4_
  150.5 8.2 %expand.3 = (bf16[1024,3072]{1,0:T(8,128)(2,1)}, bf16[1024,3072]{1,0:T(8,128)(2,1)}) custom-call(bf16[1024,768]{1,0:T(8,128)(2,1)} %get-tuple-element.299.mid_ref.left_ref, bf16[768,3072]{1,0:T(8,128)(2,1)} %bitcast.73, f32[1,3072]{1,0:T(1,128)} %reshape.714.b_ref, ...), custom_call_target="tpu_custom_call", output_to_operand_aliasing={{0}: (3, {}), {1}: (4, {})} | custom-call | flops 2415919104 | bytes 10223616 | tf_op jit(solution)/shard_map/expand/pallas_call | solution.py:622
  161.3 5.2 %assemble.5 = bf16[16,2,96,768]{3,2,1,0:T(8,128)(2,1)} custom-call(s32[3,16]{1,0:T(4,128)} %get-tuple-element.570.idx_ref, bf16[8,96,768]{2,1,0:T(8,128)(2,1)} %copy-done.5, bf16[8,96,768]{2,1,0:T(8,128)(2,1)} %copy-done.14, bf16[8,96,768]{2,1,0:T(8,128)(2,1)} %copy-done.15, bf16[8,96,768]{2,1,0:T(8,128)(2,1)} %copy-done.17), custom_call_target="tpu_custom_call" | custom-call | bytes 9437184 | tf_op jit(solution)/shard_map/assemble/pallas_call | solution.py:118
  167.2 8.6 %fusion.45 = (f32[1024]{0:T(1024)S(1)}, f32[1024,768]{1,0:T(8,128)S(1)}) fusion(f32[768]{0:T(1024)S(1)} %get-tuple-element.512, bf16[1024,3072]{1,0:T(8,128)(2,1)S(1)} %copy-done.3, bf16[3072,768]{1,0:T(8,128)(2,1)} %bitcast.76, f32[768]{0:T(1024)S(1)} %get-tuple-element.513, f32[1024,768]{1,0:T(8,128)} %get-tuple-element.522.norm_ref, ...), kind=kOutput, calls=%fused_computation.178 | convolution fusion | flops 4835769344 | bytes 17314816 | tf_op jit(solution)/shard_map/dot_general | solution.py:76
  180.1 3.4 collective-permute-done.27
  189.9 2.6 join.3.cot_ref
  193.8 3.9 collective-permute-done.30
  201.2 6.5 %second_back.1 = (f32[1024,768]{1,0:T(8,128)}, bf16[1024,768]{1,0:T(8,128)(2,1)}, f32[8,768]{1,0:T(8,128)}) custom-call(bf16[1024,768]{1,0:T(8,128)(2,1)} %join.3.cot_ref, f32[4,4,768]{2,1,0:T(4,128)} %reshape.722.slot_ref, f32[1024,1]{1,0:T(8,128)} %copy.77.mask_ref, f32[1024,768]{1,0:T(8,128)} %get-tuple-element.520.norm_ref, f32[1024,1]{1,0:T(8,128)} %copy.78.inverse_ref, ...), custom_call_target="tpu_custom_call" | custom-call | flops 15728640 | bytes 9437184 | tf_op jit(solution)/shard_map/second_back/pallas_call | solution.py:540
  209.0 9.9 %tall_grad.1 = (bf16[16,96,768]{2,1,0:T(8,128)(2,1)}, bf16[16,96,768]{2,1,0:T(8,128)(2,1)}) custom-call(s32[3,16]{1,0:T(4,128)} %get-tuple-element.569.table_ref, bf16[1024,3072]{1,0:T(8,128)(2,1)} %get-tuple-element.320.left_ref, bf16[1024,768]{1,0:T(8,128)(2,1)} %get-tuple-element.342.right_ref.grad_ref), custom_call_target="tpu_custom_call" | custom-call | flops 4831838208 | bytes 12582912 | tf_op jit(solution)/shard_map/tall_grad/pallas_call | solution.py:230
  220.9 11.8 %hidden_grad.1 = (bf16[1024,3072]{1,0:T(8,128)(2,1)}, f32[1,3072]{1,0:T(1,128)}) custom-call(bf16[1024,768]{1,0:T(8,128)(2,1)} %get-tuple-element.342.right_ref.grad_ref, bf16[3072,768]{1,0:T(8,128)(2,1)} %bitcast.77, bf16[1024,3072]{1,0:T(8,128)(2,1)} %get-tuple-element.343.slope_ref), custom_call_target="tpu_custom_call" | custom-call | flops 4831838208 | bytes 18874368 | tf_op jit(solution)/shard_map/hidden_grad/pallas_call | solution.py:276
  238.9 9.9 %weight_grad.3 = (bf16[16,24,3840]{2,1,0:T(8,128)(2,1)}, bf16[16,24,3840]{2,1,0:T(8,128)(2,1)}) custom-call(s32[3,16]{1,0:T(4,128)} %get-tuple-element.569.table_ref, bf16[1024,768]{1,0:T(8,128)(2,1)} %get-tuple-element.299.mid_ref.left_ref, bf16[1024,3072]{1,0:T(8,128)(2,1)} %get-tuple-element.360.right_ref.hidden_ref), custom_call_target="tpu_custom_call" | custom-call | flops 4831838208 | bytes 12582912 | tf_op jit(solution)/shard_map/weight_grad/pallas_call | solution.py:188
  249.9 12.5 %first_back.1 = (f32[1024,768]{1,0:T(8,128)}, bf16[1024,768]{1,0:T(8,128)(2,1)}, f32[8,768]{1,0:T(8,128)}) custom-call(bf16[1024,3072]{1,0:T(8,128)(2,1)} %get-tuple-element.360.right_ref.hidden_ref, bf16[768,3072]{1,0:T(8,128)(2,1)} %bitcast.74, f32[1024,768]{1,0:T(8,128)} %get-tuple-element.361.second_ref, f32[1024,768]{1,0:T(8,128)} %get-tuple-element.522.norm_ref, ...), custom_call_target="tpu_custom_call" | custom-call | flops 4831838208 | bytes 22020096 | tf_op jit(solution)/shard_map/first_back/pallas_call | solution.py:580
  262.4 5.2 %weight_grad.4 = (bf16[16,24,3840]{2,1,0:T(8,128)(2,1)}, bf16[16,24,3840]{2,1,0:T(8,128)(2,1)}) custom-call(s32[3,16]{1,0:T(4,128)} %get-tuple-element.569.table_ref, bf16[1024,768]{1,0:T(8,128)(2,1)} %get-tuple-element.288.left_ref, bf16[1024,768]{1,0:T(8,128)(2,1)} %get-tuple-element.384.right_ref, ...), custom_call_target="tpu_custom_call", output_to_operand_aliasing={{0}: (3, {}), {1}: (4, {})} | custom-call | flops 1207959552 | bytes 4325376 | tf_op jit(solution)/shard_map/weight_grad/pallas_call | solution.py:188
  267.6 2.4 add_convert_fusion.6
  275.4 4.3 %convolution_convert_fusion.grad_ref = bf16[1024,768]{1,0:T(8,128)(2,1)} fusion(bf16[1024,768]{1,0:T(8,128)(2,1)} %get-tuple-element.384.right_ref, bf16[768,768]{1,0:T(8,128)(2,1)} %bitcast.99), kind=kOutput, calls=%fused_computation.17 | convolution fusion | flops 1208745984 | bytes 4325376 | tf_op jit(solution)/shard_map/dot_general | solution.py:76
  279.7 10.7 %attention_back.2 = (bf16[1024,2304]{1,0:T(8,128)(2,1)}, f32[1,2304]{1,0:T(1,128)}) custom-call(bf16[1024,2304]{1,0:T(8,128)(2,1)} %add_convert_fusion.qkv_ref, bf16[4,12,256,256]{3,2,1,0:T(8,128)(2,1)} %get-tuple-element.383.probs_ref, bf16[1024,768]{1,0:T(8,128)(2,1)} %convolution_convert_fusion.grad_ref), custom_call_target="tpu_custom_call" | custom-call | flops 1610612736 | bytes 8650752 | tf_op jit(solution)/shard_map/attention_back/pallas_call | solution.py:409
  290.4 5.2 %add_convert_fusion.4 = bf16[512,768]{1,0:T(8,128)(2,1)S(1)} fusion(f32[1024,768]{1,0:T(8,128)} %get-tuple-element.393, bf16[768,2304]{1,0:T(8,128)(2,1)S(1)} %bitcast.95, bf16[1024,2304]{1,0:T(8,128)(2,1)} %get-tuple-element.394._), kind=kOutput, calls=%fused_computation.19 | convolution fusion | flops 1812725760 | bytes 8257536 | tf_op jit(solution)/shard_map/dot_general | solution.py:76
  297.8 11.0 %attention_back.3 = (bf16[1024,2304]{1,0:T(8,128)(2,1)}, f32[1,2304]{1,0:T(1,128)}) custom-call(bf16[1024,2304]{1,0:T(8,128)(2,1)} %add_convert_fusion.qkv_ref, bf16[4,12,256,256]{3,2,1,0:T(8,128)(2,1)} %get-tuple-element.383.probs_ref, bf16[1024,768]{1,0:T(8,128)(2,1)} %convolution_convert_fusion.grad_ref, ...), custom_call_target="tpu_custom_call", output_to_operand_aliasing={{0}: (3, {})} | custom-call | flops 1610612736 | bytes 8650752 | tf_op jit(solution)/shard_map/attention_back/pallas_call | solution.py:409
  318.7 2.9 collective-permute-done.42.refs_0_
  321.6 6.2 %collective-permute-done.41 = bf16[2,96,768]{2,1,0:T(8,128)(2,1)} collective-permute-done((bf16[2,96,768]{2,1,0:T(8,128)(2,1)}, bf16[2,96,768]{2,1,0:T(8,128)(2,1)}, u32[]{:S(2)}, u32[]{:S(2)}) %collective-permute-start.41) | collective-permute-done | bytes 294944 | tf_op jit(solution)/shard_map/ppermute | solution.py:66
  329.4 2.9 collective-permute-start.44
  332.3 8.9 %weight_grad.5 = (bf16[16,24,2432]{2,1,0:T(8,128)(2,1)}, bf16[16,24,2432]{2,1,0:T(8,128)(2,1)}) custom-call(s32[3,16]{1,0:T(4,128)} %get-tuple-element.569.table_ref, bf16[1024,768]{1,0:T(8,128)(2,1)} %join.2.left_ref, bf16[1024,2304]{1,0:T(8,128)(2,1)} %get-tuple-element.419.right_ref, f32[768,128]{1,0:T(8,128)} %maximum_maximum_fusion.refs_0_), custom_call_target="tpu_custom_call" | custom-call | flops 3623878656 | bytes 9830400 | tf_op jit(solution)/shard_map/weight_grad/pallas_call | solution.py:188
  346.8 5.8 %slice_add_fusion.own_ref = f32[512,768]{1,0:T(8,128)} fusion(f32[1024,768]{1,0:T(8,128)} %get-tuple-element.393, bf16[768,2304]{1,0:T(8,128)(2,1)} %bitcast.94, bf16[1024,2304]{1,0:T(8,128)(2,1)S(1)} %bitcast.79), kind=kOutput, calls=%fused_computation.18 | convolution fusion | flops 1812332544 | bytes 9043968 | tf_op jit(solution)/shard_map/dot_general | solution.py:76
  359.5 15.8 %collective-permute-done.48 = bf16[4,24,3840]{2,1,0:T(8,128)(2,1)S(1)} collective-permute-done((bf16[4,24,3840]{2,1,0:T(8,128)(2,1)S(1)}, bf16[4,24,3840]{2,1,0:T(8,128)(2,1)S(1)}, u32[]{:S(2)}, u32[]{:S(2)}) %collective-permute-start.48) | collective-permute-done | bytes 737312 | tf_op jit(solution)/shard_map/ppermute | solution.py:66
  380.0 3.6 deal.3
  383.6 5.6 %collective-permute-done.51 = bf16[2,24,3840]{2,1,0:T(8,128)(2,1)} collective-permute-done((bf16[2,24,3840]{2,1,0:T(8,128)(2,1)S(1)}, bf16[2,24,3840]{2,1,0:T(8,128)(2,1)}, u32[]{:S(2)}, u32[]{:S(2)}) %collective-permute-start.51) | collective-permute-done | bytes 368672 | tf_op jit(solution)/shard_map/ppermute | solution.py:66
  394.3 6.3 %collective-permute-done.53 = bf16[1,24,3840]{2,1,0:T(8,128)(2,1)S(1)} collective-permute-done((bf16[1,24,3840]{2,1,0:T(8,128)(2,1)S(1)}, bf16[1,24,3840]{2,1,0:T(8,128)(2,1)S(1)}, u32[]{:S(2)}, u32[]{:S(2)}) %collective-permute-start.53) | collective-permute-done | bytes 184352 | tf_op jit(solution)/shard_map/ppermute | solution.py:66
  404.5 2.7 deal.2
  (373 shorter events, 122.8 us)
Async XLA Ops:
  3.4 11.4 %collective-permute-start = (bf16[1,24,3200]{2,1,0:T(8,128)(2,1)S(1)}, bf16[1,24,3200]{2,1,0:T(8,128)(2,1)S(1)}, u32[]{:S(2)}, u32[]{:S(2)}) collective-permute-start(bf16[1,24,3200]{2,1,0:T(8,128)(2,1)S(1)} %get-tuple-element.546), channel_id=1, source_target_pairs={{0,4},{1,5},{2,6},{3,7},{4,0},{5,1},{6,2},{7,3},{8,12},{9,13},{10,... | collective-permute-start | bytes 460808 | tf_op jit(solution)/shard_map/ppermute | solution.py:66
  14.8 13.8 %collective-permute-start.1 = (bf16[2,24,3200]{2,1,0:T(8,128)(2,1)S(1)}, bf16[2,24,3200]{2,1,0:T(8,128)(2,1)S(1)}, u32[]{:S(2)}, u32[]{:S(2)}) collective-permute-start(bf16[2,24,3200]{2,1,0:T(8,128)(2,1)S(1)} %pad_maximum_fusion.8), channel_id=1, source_target_pairs={{0,2},{1,3},{2,0},{3,1},{4,6},{5,7},{6,4},{7,5},{8,10},{9,11},{10,... | collective-permute-start | bytes 921608 | tf_op jit(solution)/shard_map/ppermute | solution.py:66
  15.6 13.0 %collective-permute-start.2 = (bf16[160,768]{1,0:T(8,128)(2,1)S(1)}, bf16[160,768]{1,0:T(8,128)(2,1)S(1)}, u32[]{:S(2)}, u32[]{:S(2)}) collective-permute-start(bf16[160,768]{1,0:T(8,128)(2,1)S(1)} %get-tuple-element.239), channel_id=1, source_target_pairs={{0,4},{1,5},{2,6},{3,7},{4,0},{5,1},{6,2},{7,3},{8,12},{9,13},{10,... | collective-permute-start | bytes 737288 | tf_op jit(solution)/shard_map/ppermute | solution.py:72
  28.7 10.6 %collective-permute-start.3 = (bf16[4,24,3200]{2,1,0:T(8,128)(2,1)S(1)}, bf16[4,24,3200]{2,1,0:T(8,128)(2,1)S(1)}, u32[]{:S(2)}, u32[]{:S(2)}) collective-permute-start(bf16[4,24,3200]{2,1,0:T(8,128)(2,1)S(1)} %pad_maximum_fusion.4), channel_id=1, source_target_pairs={{0,8},{1,17},{2,10},{3,19},{4,12},{5,21},{6,14},{7,23},{8,0},{9,25... | collective-permute-start | bytes 1843208 | tf_op jit(solution)/shard_map/ppermute | solution.py:66
  30.0 9.2 %collective-permute-start.4 = (bf16[1,24,3072]{2,1,0:T(8,128)(2,1)S(1)}, bf16[1,24,3072]{2,1,0:T(8,128)(2,1)S(1)}, u32[]{:S(2)}, u32[]{:S(2)}) collective-permute-start(bf16[1,24,3072]{2,1,0:T(8,128)(2,1)S(1)} %get-tuple-element.243), channel_id=1, source_target_pairs={{0,4},{1,5},{2,6},{3,7},{4,0},{5,1},{6,2},{7,3},{8,12},{9,13},{10,... | collective-permute-start | bytes 442376 | tf_op jit(solution)/shard_map/ppermute | solution.py:66
  39.5 25.0 %collective-permute-start.5 = (bf16[8,24,3200]{2,1,0:T(8,128)(2,1)S(1)}, bf16[8,24,3200]{2,1,0:T(8,128)(2,1)}, u32[]{:S(2)}, u32[]{:S(2)}) collective-permute-start(bf16[8,24,3200]{2,1,0:T(8,128)(2,1)S(1)} %pad_maximum_fusion.refs_0_), channel_id=1, source_target_pairs={{0,16},{1,9},{2,18},{3,11},{4,20},{5,13},{6,22},{7,15},{8,24},{9,1... | collective-permute-start | bytes 3686408 | tf_op jit(solution)/shard_map/ppermute | solution.py:66
  42.5 8.2 %collective-permute-start.6 = (bf16[2,24,3072]{2,1,0:T(8,128)(2,1)S(1)}, bf16[2,24,3072]{2,1,0:T(8,128)(2,1)S(1)}, u32[]{:S(2)}, u32[]{:S(2)}) collective-permute-start(bf16[2,24,3072]{2,1,0:T(8,128)(2,1)S(1)} %pad_maximum_fusion.9), channel_id=1, source_target_pairs={{0,2},{1,3},{2,0},{3,1},{4,6},{5,7},{6,4},{7,5},{8,10},{9,11},{10,... | collective-permute-start | bytes 884744 | tf_op jit(solution)/shard_map/ppermute | solution.py:66
  47.9 28.5 %collective-permute-start.8 = (bf16[8,24,3200]{2,1,0:T(8,128)(2,1)S(1)}, bf16[8,24,3200]{2,1,0:T(8,128)(2,1)}, u32[]{:S(2)}, u32[]{:S(2)}) collective-permute-start(bf16[8,24,3200]{2,1,0:T(8,128)(2,1)S(1)} %pad_maximum_fusion.refs_0_), channel_id=1, source_target_pairs={{0,1},{1,0},{2,3},{3,2},{4,5},{5,4},{6,7},{7,6},{8,9},{9,8},{10,11... | collective-permute-start | bytes 3686408 | tf_op jit(solution)/shard_map/ppermute | solution.py:69
  47.9 16.6 %collective-permute-start.7 = (bf16[192,768]{1,0:T(8,128)(2,1)}, bf16[192,768]{1,0:T(8,128)(2,1)S(1)}, u32[]{:S(2)}, u32[]{:S(2)}) collective-permute-start(bf16[192,768]{1,0:T(8,128)(2,1)} %slice.459), channel_id=1, source_target_pairs={{0,4},{1,5},{2,6},{3,7},{4,0},{5,1},{6,2},{7,3},{8,12},{9,13},{10,... | collective-permute-start | bytes 884744 | tf_op jit(solution)/shard_map/ppermute | solution.py:72
  64.5 11.9 %collective-permute-start.9 = (bf16[8,24,3200]{2,1,0:T(8,128)(2,1)}, bf16[8,24,3200]{2,1,0:T(8,128)(2,1)}, u32[]{:S(2)}, u32[]{:S(2)}) collective-permute-start(bf16[8,24,3200]{2,1,0:T(8,128)(2,1)} %collective-permute-done.5.refs_1_), channel_id=1, source_target_pairs={{0,1},{1,0},{2,3},{3,2},{4,5},{5,4},{6,7},{7,6},{8,9},{9,8},{10,11... | collective-permute-start | bytes 3686408 | tf_op jit(solution)/shard_map/ppermute | solution.py:69
  65.4 9.9 %collective-permute-start.10 = (bf16[4,24,3072]{2,1,0:T(8,128)(2,1)S(1)}, bf16[4,24,3072]{2,1,0:T(8,128)(2,1)S(1)}, u32[]{:S(2)}, u32[]{:S(2)}) collective-permute-start(bf16[4,24,3072]{2,1,0:T(8,128)(2,1)S(1)} %pad_maximum_fusion.5), channel_id=1, source_target_pairs={{0,8},{1,17},{2,10},{3,19},{4,12},{5,21},{6,14},{7,23},{8,0},{9,25... | collective-permute-start | bytes 1769480 | tf_op jit(solution)/shard_map/ppermute | solution.py:66
  66.6 15.3 %collective-permute-start.11 = (bf16[160,768]{1,0:T(8,128)(2,1)}, bf16[160,768]{1,0:T(8,128)(2,1)}, u32[]{:S(2)}, u32[]{:S(2)}) collective-permute-start(bf16[160,768]{1,0:T(8,128)(2,1)} %get-tuple-element.258), channel_id=1, source_target_pairs={{0,4},{1,5},{2,6},{3,7},{4,0},{5,1},{6,2},{7,3},{8,12},{9,13},{10,... | collective-permute-start | bytes 737288 | tf_op jit(solution)/shard_map/ppermute | solution.py:72
  67.1 30.6 %collective-permute-start.13 = (s32[512]{0:T(512)S(1)}, s32[512]{0:T(512)S(1)}, u32[]{:S(2)}, u32[]{:S(2)}) collective-permute-start(s32[512]{0:T(512)S(1)} %get-tuple-element.560), channel_id=1, source_target_pairs={{0,4},{1,5},{2,6},{3,7},{4,0},{5,1},{6,2},{7,3},{8,12},{9,13},{10,... | collective-permute-start | bytes 6152 | tf_op jit(solution)/shard_map/ppermute | solution.py:72
  83.7 11.7 %collective-permute-start.12 = (bf16[1,96,768]{2,1,0:T(8,128)(2,1)S(1)}, bf16[1,96,768]{2,1,0:T(8,128)(2,1)S(1)}, u32[]{:S(2)}, u32[]{:S(2)}) collective-permute-start(bf16[1,96,768]{2,1,0:T(8,128)(2,1)S(1)} %get-tuple-element.264), channel_id=1, source_target_pairs={{0,4},{1,5},{2,6},{3,7},{4,0},{5,1},{6,2},{7,3},{8,12},{9,13},{10,... | collective-permute-start | bytes 442376 | tf_op jit(solution)/shard_map/ppermute | solution.py:66
  83.7 25.3 %collective-permute-start.14 = (bf16[8,24,3072]{2,1,0:T(8,128)(2,1)}, bf16[8,24,3072]{2,1,0:T(8,128)(2,1)S(1)}, u32[]{:S(2)}, u32[]{:S(2)}) collective-permute-start(bf16[8,24,3072]{2,1,0:T(8,128)(2,1)} %pad_maximum_fusion.1.refs_0_), channel_id=1, source_target_pairs={{0,16},{1,9},{2,18},{3,11},{4,20},{5,13},{6,22},{7,15},{8,24},{9,1... | collective-permute-start | bytes 3538952 | tf_op jit(solution)/shard_map/ppermute | solution.py:66
  95.4 12.7 %collective-permute-start.15 = (bf16[2,96,768]{2,1,0:T(8,128)(2,1)S(1)}, bf16[2,96,768]{2,1,0:T(8,128)(2,1)S(1)}, u32[]{:S(2)}, u32[]{:S(2)}) collective-permute-start(bf16[2,96,768]{2,1,0:T(8,128)(2,1)S(1)} %pad_maximum_fusion.10), channel_id=1, source_target_pairs={{0,2},{1,3},{2,0},{3,1},{4,6},{5,7},{6,4},{7,5},{8,10},{9,11},{10,... | collective-permute-start | bytes 884744 | tf_op jit(solution)/shard_map/ppermute | solution.py:66
  98.4 22.8 %collective-permute-start.17 = (bf16[8,24,3072]{2,1,0:T(8,128)(2,1)}, bf16[8,24,3072]{2,1,0:T(8,128)(2,1)S(1)}, u32[]{:S(2)}, u32[]{:S(2)}) collective-permute-start(bf16[8,24,3072]{2,1,0:T(8,128)(2,1)} %pad_maximum_fusion.1.refs_0_), channel_id=1, source_target_pairs={{0,1},{1,0},{2,3},{3,2},{4,5},{5,4},{6,7},{7,6},{8,9},{9,8},{10,11... | collective-permute-start | bytes 3538952 | tf_op jit(solution)/shard_map/ppermute | solution.py:69
  98.4 10.6 %collective-permute-start.16 = (bf16[96,768]{1,0:T(8,128)(2,1)S(1)}, bf16[96,768]{1,0:T(8,128)(2,1)S(1)}, u32[]{:S(2)}, u32[]{:S(2)}) collective-permute-start(bf16[96,768]{1,0:T(8,128)(2,1)S(1)} %copy-done.45), channel_id=1, source_target_pairs={{0,4},{1,5},{2,6},{3,7},{4,0},{5,1},{6,2},{7,3},{8,12},{9,13},{10,... | collective-permute-start | bytes 442376 | tf_op jit(solution)/shard_map/ppermute | solution.py:72
  109.7 11.6 %collective-permute-start.18 = (bf16[8,24,3072]{2,1,0:T(8,128)(2,1)S(1)}, bf16[8,24,3072]{2,1,0:T(8,128)(2,1)}, u32[]{:S(2)}, u32[]{:S(2)}) collective-permute-start(bf16[8,24,3072]{2,1,0:T(8,128)(2,1)S(1)} %collective-permute-done.14.refs_1_), channel_id=1, source_target_pairs={{0,1},{1,0},{2,3},{3,2},{4,5},{5,4},{6,7},{7,6},{8,9},{9,8},{10,11... | collective-permute-start | bytes 3538952 | tf_op jit(solution)/shard_map/ppermute | solution.py:69
  109.7 10.2 %collective-permute-start.19 = (bf16[4,96,768]{2,1,0:T(8,128)(2,1)}, bf16[4,96,768]{2,1,0:T(8,128)(2,1)}, u32[]{:S(2)}, u32[]{:S(2)}) collective-permute-start(bf16[4,96,768]{2,1,0:T(8,128)(2,1)} %pad_maximum_fusion.6), channel_id=1, source_target_pairs={{0,8},{1,17},{2,10},{3,19},{4,12},{5,21},{6,14},{7,23},{8,0},{9,25... | collective-permute-start | bytes 1769480 | tf_op jit(solution)/shard_map/ppermute | solution.py:66
  111.3 10.0 %collective-permute-start.20 = (bf16[96,768]{1,0:T(8,128)(2,1)}, bf16[96,768]{1,0:T(8,128)(2,1)S(1)}, u32[]{:S(2)}, u32[]{:S(2)}) collective-permute-start(bf16[96,768]{1,0:T(8,128)(2,1)} %get-tuple-element.284), channel_id=1, source_target_pairs={{0,4},{1,5},{2,6},{3,7},{4,0},{5,1},{6,2},{7,3},{8,12},{9,13},{10,... | collective-permute-start | bytes 442376 | tf_op jit(solution)/shard_map/ppermute | solution.py:72
  122.3 26.3 %collective-permute-start.22 = (bf16[8,96,768]{2,1,0:T(8,128)(2,1)S(1)}, bf16[8,96,768]{2,1,0:T(8,128)(2,1)S(1)}, u32[]{:S(2)}, u32[]{:S(2)}) collective-permute-start(bf16[8,96,768]{2,1,0:T(8,128)(2,1)S(1)} %pad_maximum_fusion.2.refs_0_), channel_id=1, source_target_pairs={{0,16},{1,9},{2,18},{3,11},{4,20},{5,13},{6,22},{7,15},{8,24},{9,1... | collective-permute-start | bytes 3538952 | tf_op jit(solution)/shard_map/ppermute | solution.py:66
  123.6 25.0 %collective-permute-start.23 = (bf16[8,96,768]{2,1,0:T(8,128)(2,1)S(1)}, bf16[8,96,768]{2,1,0:T(8,128)(2,1)S(1)}, u32[]{:S(2)}, u32[]{:S(2)}) collective-permute-start(bf16[8,96,768]{2,1,0:T(8,128)(2,1)S(1)} %pad_maximum_fusion.2.refs_0_), channel_id=1, source_target_pairs={{0,1},{1,0},{2,3},{3,2},{4,5},{5,4},{6,7},{7,6},{8,9},{9,8},{10,11... | collective-permute-start | bytes 3538952 | tf_op jit(solution)/shard_map/ppermute | solution.py:69
  126.5 10.4 %collective-permute-start.21 = (bf16[96,768]{1,0:T(8,128)(2,1)S(1)}, bf16[96,768]{1,0:T(8,128)(2,1)S(1)}, u32[]{:S(2)}, u32[]{:S(2)}) collective-permute-start(bf16[96,768]{1,0:T(8,128)(2,1)S(1)} %copy-done.42), channel_id=1, source_target_pairs={{0,4},{1,5},{2,6},{3,7},{4,0},{5,1},{6,2},{7,3},{8,12},{9,13},{10,... | collective-permute-start | bytes 442376 | tf_op jit(solution)/shard_map/ppermute | solution.py:72
  136.9 11.7 %collective-permute-start.24 = (bf16[128,768]{1,0:T(8,128)(2,1)S(1)}, bf16[128,768]{1,0:T(8,128)(2,1)S(1)}, u32[]{:S(2)}, u32[]{:S(2)}) collective-permute-start(bf16[128,768]{1,0:T(8,128)(2,1)S(1)} %copy-done.39), channel_id=1, source_target_pairs={{0,4},{1,5},{2,6},{3,7},{4,0},{5,1},{6,2},{7,3},{8,12},{9,13},{10,... | collective-permute-start | bytes 589832 | tf_op jit(solution)/shard_map/ppermute | solution.py:72
  149.8 10.5 %collective-permute-start.25 = (bf16[8,96,768]{2,1,0:T(8,128)(2,1)S(1)}, bf16[8,96,768]{2,1,0:T(8,128)(2,1)S(1)}, u32[]{:S(2)}, u32[]{:S(2)}) collective-permute-start(bf16[8,96,768]{2,1,0:T(8,128)(2,1)S(1)} %collective-permute-done.22.refs_1_), channel_id=1, source_target_pairs={{0,1},{1,0},{2,3},{3,2},{4,5},{5,4},{6,7},{7,6},{8,9},{9,8},{10,11... | collective-permute-start | bytes 3538952 | tf_op jit(solution)/shard_map/ppermute | solution.py:69
  150.4 9.9 %collective-permute-start.26 = (bf16[96,768]{1,0:T(8,128)(2,1)S(1)}, bf16[96,768]{1,0:T(8,128)(2,1)S(1)}, u32[]{:S(2)}, u32[]{:S(2)}) collective-permute-start(bf16[96,768]{1,0:T(8,128)(2,1)S(1)} %copy-done.40), channel_id=1, source_target_pairs={{0,4},{1,5},{2,6},{3,7},{4,0},{5,1},{6,2},{7,3},{8,12},{9,13},{10,... | collective-permute-start | bytes 442376 | tf_op jit(solution)/shard_map/ppermute | solution.py:72
  207.8 12.1 %collective-permute-start.32 = (bf16[128,768]{1,0:T(8,128)(2,1)S(1)}, bf16[128,768]{1,0:T(8,128)(2,1)S(1)}, u32[]{:S(2)}, u32[]{:S(2)}) collective-permute-start(bf16[128,768]{1,0:T(8,128)(2,1)S(1)} %get-tuple-element.336), channel_id=1, source_target_pairs={{0,4},{1,5},{2,6},{3,7},{4,0},{5,1},{6,2},{7,3},{8,12},{9,13},{10,... | collective-permute-start | bytes 589832 | tf_op jit(solution)/shard_map/ppermute | solution.py:72
  219.9 12.8 %collective-permute-start.33 = (bf16[16,96,768]{2,1,0:T(8,128)(2,1)}, bf16[16,96,768]{2,1,0:T(8,128)(2,1)S(1)}, u32[]{:S(2)}, u32[]{:S(2)}) collective-permute-start(bf16[16,96,768]{2,1,0:T(8,128)(2,1)} %get-tuple-element.341), channel_id=1, source_target_pairs={{0,1},{1,0},{2,3},{3,2},{4,5},{5,4},{6,7},{7,6},{8,9},{9,8},{10,11... | collective-permute-start | bytes 7077896 | tf_op jit(solution)/shard_map/ppermute | solution.py:69
  219.9 12.8 %collective-permute-start.34 = (bf16[128,768]{1,0:T(8,128)(2,1)S(1)}, bf16[128,768]{1,0:T(8,128)(2,1)S(1)}, u32[]{:S(2)}, u32[]{:S(2)}) collective-permute-start(bf16[128,768]{1,0:T(8,128)(2,1)S(1)} %get-tuple-element.346), channel_id=1, source_target_pairs={{0,4},{1,5},{2,6},{3,7},{4,0},{5,1},{6,2},{7,3},{8,12},{9,13},{10,... | collective-permute-start | bytes 589832 | tf_op jit(solution)/shard_map/ppermute | solution.py:72
  234.7 27.6 %collective-permute-start.35 = (bf16[8,96,768]{2,1,0:T(8,128)(2,1)S(1)}, bf16[8,96,768]{2,1,0:T(8,128)(2,1)S(1)}, u32[]{:S(2)}, u32[]{:S(2)}) collective-permute-start(bf16[8,96,768]{2,1,0:T(8,128)(2,1)S(1)} %add_convert_fusion.2), channel_id=1, source_target_pairs={{0,16},{1,9},{2,18},{3,11},{4,20},{5,13},{6,22},{7,15},{8,24},{9,1... | collective-permute-start | bytes 3538952 | tf_op jit(solution)/shard_map/ppermute | solution.py:66
  236.9 11.9 %collective-permute-start.36 = (bf16[128,768]{1,0:T(8,128)(2,1)S(1)}, bf16[128,768]{1,0:T(8,128)(2,1)S(1)}, u32[]{:S(2)}, u32[]{:S(2)}) collective-permute-start(bf16[128,768]{1,0:T(8,128)(2,1)S(1)} %get-tuple-element.356), channel_id=1, source_target_pairs={{0,4},{1,5},{2,6},{3,7},{4,0},{5,1},{6,2},{7,3},{8,12},{9,13},{10,... | collective-permute-start | bytes 589832 | tf_op jit(solution)/shard_map/ppermute | solution.py:72
  248.8 13.5 %collective-permute-start.37 = (bf16[128,768]{1,0:T(8,128)(2,1)S(1)}, bf16[128,768]{1,0:T(8,128)(2,1)S(1)}, u32[]{:S(2)}, u32[]{:S(2)}) collective-permute-start(bf16[128,768]{1,0:T(8,128)(2,1)S(1)} %get-tuple-element.366), channel_id=1, source_target_pairs={{0,4},{1,5},{2,6},{3,7},{4,0},{5,1},{6,2},{7,3},{8,12},{9,13},{10,... | collective-permute-start | bytes 589832 | tf_op jit(solution)/shard_map/ppermute | solution.py:72
  267.6 22.9 %collective-permute-start.39 = (bf16[16,24,3840]{2,1,0:T(8,128)(2,1)}, bf16[16,24,3840]{2,1,0:T(8,128)(2,1)S(1)}, u32[]{:S(2)}, u32[]{:S(2)}) collective-permute-start(bf16[16,24,3840]{2,1,0:T(8,128)(2,1)} %get-tuple-element.382), channel_id=1, source_target_pairs={{0,1},{1,0},{2,3},{3,2},{4,5},{5,4},{6,7},{7,6},{8,9},{9,8},{10,11... | collective-permute-start | bytes 8847368 | tf_op jit(solution)/shard_map/ppermute | solution.py:69
  270.1 20.3 %collective-permute-start.38 = (bf16[4,96,768]{2,1,0:T(8,128)(2,1)}, bf16[4,96,768]{2,1,0:T(8,128)(2,1)}, u32[]{:S(2)}, u32[]{:S(2)}) collective-permute-start(bf16[4,96,768]{2,1,0:T(8,128)(2,1)} %add_convert_fusion.6), channel_id=1, source_target_pairs={{0,8},{1,17},{2,10},{3,19},{4,12},{5,21},{6,14},{7,23},{8,0},{9,25... | collective-permute-start | bytes 1769480 | tf_op jit(solution)/shard_map/ppermute | solution.py:66
  308.8 12.8 %collective-permute-start.42 = (bf16[128,768]{1,0:T(8,128)(2,1)}, bf16[128,768]{1,0:T(8,128)(2,1)}, u32[]{:S(2)}, u32[]{:S(2)}) collective-permute-start(bf16[128,768]{1,0:T(8,128)(2,1)} %get-tuple-element.396), channel_id=1, source_target_pairs={{0,4},{1,5},{2,6},{3,7},{4,0},{5,1},{6,2},{7,3},{8,12},{9,13},{10,... | collective-permute-start | bytes 589832 | tf_op jit(solution)/shard_map/ppermute | solution.py:72
  312.3 34.3 %collective-permute-start.40 = (bf16[8,24,3840]{2,1,0:T(8,128)(2,1)}, bf16[8,24,3840]{2,1,0:T(8,128)(2,1)}, u32[]{:S(2)}, u32[]{:S(2)}) collective-permute-start(bf16[8,24,3840]{2,1,0:T(8,128)(2,1)} %add_convert_fusion.1), channel_id=1, source_target_pairs={{0,16},{1,9},{2,18},{3,11},{4,20},{5,13},{6,22},{7,15},{8,24},{9,1... | collective-permute-start | bytes 4423688 | tf_op jit(solution)/shard_map/ppermute | solution.py:66
  315.6 12.3 %collective-permute-start.41 = (bf16[2,96,768]{2,1,0:T(8,128)(2,1)}, bf16[2,96,768]{2,1,0:T(8,128)(2,1)}, u32[]{:S(2)}, u32[]{:S(2)}) collective-permute-start(bf16[2,96,768]{2,1,0:T(8,128)(2,1)} %add_convert_fusion.9), channel_id=1, source_target_pairs={{0,2},{1,3},{2,0},{3,1},{4,6},{5,7},{6,4},{7,5},{8,10},{9,11},{10,... | collective-permute-start | bytes 884744 | tf_op jit(solution)/shard_map/ppermute | solution.py:66
  329.3 13.2 %collective-permute-start.43 = (bf16[1,96,768]{2,1,0:T(8,128)(2,1)S(1)}, bf16[1,96,768]{2,1,0:T(8,128)(2,1)S(1)}, u32[]{:S(2)}, u32[]{:S(2)}) collective-permute-start(bf16[1,96,768]{2,1,0:T(8,128)(2,1)S(1)} %add_convert_fusion.12), channel_id=1, source_target_pairs={{0,4},{1,5},{2,6},{3,7},{4,0},{5,1},{6,2},{7,3},{8,12},{9,13},{10,... | collective-permute-start | bytes 442376 | tf_op jit(solution)/shard_map/ppermute | solution.py:66
  329.4 17.2 %collective-permute-start.44 = (bf16[128,768]{1,0:T(8,128)(2,1)}, bf16[128,768]{1,0:T(8,128)(2,1)S(1)}, u32[]{:S(2)}, u32[]{:S(2)}) collective-permute-start(bf16[128,768]{1,0:T(8,128)(2,1)} %get-tuple-element.414), channel_id=1, source_target_pairs={{0,4},{1,5},{2,6},{3,7},{4,0},{5,1},{6,2},{7,3},{8,12},{9,13},{10,... | collective-permute-start | bytes 589832 | tf_op jit(solution)/shard_map/ppermute | solution.py:72
  346.6 7.8 %collective-permute-start.45 = (bf16[16,24,2432]{2,1,0:T(8,128)(2,1)S(1)}, bf16[16,24,2432]{2,1,0:T(8,128)(2,1)S(1)}, u32[]{:S(2)}, u32[]{:S(2)}) collective-permute-start(bf16[16,24,2432]{2,1,0:T(8,128)(2,1)S(1)} %copy-done.66), channel_id=1, source_target_pairs={{0,1},{1,0},{2,3},{3,2},{4,5},{5,4},{6,7},{7,6},{8,9},{9,8},{10,11... | collective-permute-start | bytes 5603336 | tf_op jit(solution)/shard_map/ppermute | solution.py:69
  354.7 21.5 %collective-permute-start.47 = (bf16[8,24,2432]{2,1,0:T(8,128)(2,1)S(1)}, bf16[8,24,2432]{2,1,0:T(8,128)(2,1)S(1)}, u32[]{:S(2)}, u32[]{:S(2)}) collective-permute-start(bf16[8,24,2432]{2,1,0:T(8,128)(2,1)S(1)} %add_convert_fusion.3), channel_id=1, source_target_pairs={{0,16},{1,9},{2,18},{3,11},{4,20},{5,13},{6,22},{7,15},{8,24},{9,1... | collective-permute-start | bytes 2801672 | tf_op jit(solution)/shard_map/ppermute | solution.py:66
  356.7 18.5 %collective-permute-start.48 = (bf16[4,24,3840]{2,1,0:T(8,128)(2,1)S(1)}, bf16[4,24,3840]{2,1,0:T(8,128)(2,1)S(1)}, u32[]{:S(2)}, u32[]{:S(2)}) collective-permute-start(bf16[4,24,3840]{2,1,0:T(8,128)(2,1)S(1)} %add_convert_fusion.5), channel_id=1, source_target_pairs={{0,8},{1,17},{2,10},{3,19},{4,12},{5,21},{6,14},{7,23},{8,0},{9,25... | collective-permute-start | bytes 2211848 | tf_op jit(solution)/shard_map/ppermute | solution.py:66
  358.3 17.0 %collective-permute-start.49 = (bf16[192,768]{1,0:T(8,128)(2,1)S(1)}, bf16[192,768]{1,0:T(8,128)(2,1)S(1)}, u32[]{:S(2)}, u32[]{:S(2)}) collective-permute-start(bf16[192,768]{1,0:T(8,128)(2,1)S(1)} %copy-done.31), channel_id=1, source_target_pairs={{0,4},{1,5},{2,6},{3,7},{4,0},{5,1},{6,2},{7,3},{8,12},{9,13},{10,... | collective-permute-start | bytes 884744 | tf_op jit(solution)/shard_map/ppermute | solution.py:72
  377.3 11.9 %collective-permute-start.50 = (bf16[4,24,2432]{2,1,0:T(8,128)(2,1)}, bf16[4,24,2432]{2,1,0:T(8,128)(2,1)}, u32[]{:S(2)}, u32[]{:S(2)}) collective-permute-start(bf16[4,24,2432]{2,1,0:T(8,128)(2,1)} %add_convert_fusion.7), channel_id=1, source_target_pairs={{0,8},{1,17},{2,10},{3,19},{4,12},{5,21},{6,14},{7,23},{8,0},{9,25... | collective-permute-start | bytes 1400840 | tf_op jit(solution)/shard_map/ppermute | solution.py:66
  379.1 10.2 %collective-permute-start.51 = (bf16[2,24,3840]{2,1,0:T(8,128)(2,1)S(1)}, bf16[2,24,3840]{2,1,0:T(8,128)(2,1)}, u32[]{:S(2)}, u32[]{:S(2)}) collective-permute-start(bf16[2,24,3840]{2,1,0:T(8,128)(2,1)S(1)} %add_convert_fusion.8), channel_id=1, source_target_pairs={{0,2},{1,3},{2,0},{3,1},{4,6},{5,7},{6,4},{7,5},{8,10},{9,11},{10,... | collective-permute-start | bytes 1105928 | tf_op jit(solution)/shard_map/ppermute | solution.py:66
  390.5 10.1 %collective-permute-start.53 = (bf16[1,24,3840]{2,1,0:T(8,128)(2,1)S(1)}, bf16[1,24,3840]{2,1,0:T(8,128)(2,1)S(1)}, u32[]{:S(2)}, u32[]{:S(2)}) collective-permute-start(bf16[1,24,3840]{2,1,0:T(8,128)(2,1)S(1)} %add_convert_fusion.11), channel_id=1, source_target_pairs={{0,4},{1,5},{2,6},{3,7},{4,0},{5,1},{6,2},{7,3},{8,12},{9,13},{10,... | collective-permute-start | bytes 552968 | tf_op jit(solution)/shard_map/ppermute | solution.py:66
  392.9 9.8 %collective-permute-start.52 = (bf16[2,24,2432]{2,1,0:T(8,128)(2,1)S(1)}, bf16[2,24,2432]{2,1,0:T(8,128)(2,1)S(1)}, u32[]{:S(2)}, u32[]{:S(2)}) collective-permute-start(bf16[2,24,2432]{2,1,0:T(8,128)(2,1)S(1)} %add_convert_fusion.10), channel_id=1, source_target_pairs={{0,2},{1,3},{2,0},{3,1},{4,6},{5,7},{6,4},{7,5},{8,10},{9,11},{10,... | collective-permute-start | bytes 700424 | tf_op jit(solution)/shard_map/ppermute | solution.py:66
  (76 other events, 748.2 us)

commit v6 on v5

--- a/solution.py
+++ b/solution.py
@@ -297,6 +297,36 @@
         ),
         name="hidden_grad",
     )(grad, w_reduce, slope)
+
+
+def project_kernel(tokens_ref, w_ref, b_ref, *refs):
+    refs[-1][...] = (dot(tokens_ref[...], w_ref[...]) + b_ref[...]).astype(BF16)
+
+
+def project(tokens, weight, bias, rows, start, into=()):
+    width = weight.shape[1]
+    count = tokens.shape[0] // BLOCK - (start if into else 0)
+    first = start if into else 0
+    return pl.pallas_call(
+        project_kernel,
+        grid=(count,),
+        in_specs=[
+            pl.BlockSpec((BLOCK, D), lambda i: (i + first, 0)),
+            pl.BlockSpec((D, width), lambda i: (0, 0)),
+            pl.BlockSpec((1, width), lambda i: (0, 0)),
+        ]
+        + [pl.BlockSpec(memory_space=pl.ANY)] * len(into),
+        out_specs=pl.BlockSpec((BLOCK, width), lambda i: (i + start, 0)),
+        out_shape=jax.ShapeDtypeStruct((rows, width), BF16),
+        input_output_aliases={3: 0} if into else {},
+        compiler_params=pltpu.CompilerParams(vmem_limit_bytes=VMEM_LIMIT),
+        cost_estimate=pl.CostEstimate(
+            flops=2 * count * BLOCK * D * width,
+            bytes_accessed=2 * (count * BLOCK * (D + width) + D * width),
+            transcendentals=0,
+        ),
+        name="project",
+    )(tokens, weight, bias, *into)
 
 
 def attention_kernel(qkv_ref, qid_ref, kid_ref, context_ref, probs_ref):
@@ -802,22 +832,23 @@
     g2.pb_first()
     tokens_in = tokens_in + hand(tokens_out[2:])
     full_j, full_o, full_small = g1.whole([(0, 3 * D), (3 * D, D), (4 * D, 128)])
-    full_j, full_o, full_small, g2.stack, g3.send, tokens_in = tie(
-        full_j, full_o, full_small, g2.stack, g3.send, tokens_in
-    )
-    g2.send = g2.stack
-    g2.pb_last()
-    g2.core_stack()
-    g3.mid()
     wj = full_j.reshape(D, 3 * D)
     wo = full_o.reshape(D, D)
     small = full_small.reshape(D, 128).astype(F32)
     vec = small[:, :8].T
     bias_e = small[:, 8:12].reshape(1, FF)
-    bias_j = jnp.concatenate([vec[0], jnp.zeros((D,), F32), vec[1]])
+    bias_j = jnp.concatenate([vec[0], jnp.zeros((D,), F32), vec[1]])[None]
+    wj, wo, vec, bias_e, bias_j, g2.stack, g3.send = tie(
+        wj, wo, vec, bias_e, bias_j, g2.stack, g3.send
+    )
+    g2.send = g2.stack
+    g2.pb_last()
+    g2.core_stack()
+    qkv = project(my_tokens, wj, bias_j, rows, 0)
+    qkv, tokens_in, g3.send = tie(qkv, tokens_in, g3.send)
+    g3.mid()
     tokens = join([my_tokens] + tokens_in)
-    qkv = (dot(tokens, wj) + bias_j).astype(BF16)
-
+    qkv = project(tokens, wj, bias_j, rows, own_rows // BLOCK, (qkv,))
     cot_out = chunked(send_cot, (3, 3, 3, 4, 3))
     by_pa = positive.reshape(places.pa_n, nq)
     pair = [lax.dynamic_index_in_dim(by_pa, low_pa + k, 0, keepdims=False) for k in (0, shift)]
@@ -929,23 +960,35 @@
 
     class Scatter:
         def __init__(self, mine, theirs):
-            self.parts, self.theirs = [mine], theirs
-            self.count = mine.shape[0]
-
-        def cores(self):
-            self.parts = self.parts + [places.swap_core(self.theirs)]
+            self.groups, self.theirs, self.parts = [], [], []
+            self.send = self.keep = self.out = None
+            self.count = places.chips
+            self.add(mine, theirs)
+
+        def add(self, mine, theirs):
+            self.groups = self.groups + [[mine]]
+            self.theirs = self.theirs + [theirs]
+
+        def cores(self, k=0):
+            got = places.swap_core(self.theirs[k])
+            self.groups = [g + [got] if i == k else g for i, g in enumerate(self.groups)]
 
         def total(self, start, stop):
-            out = self.parts[0][start:stop].astype(F32)
-            for part in self.parts[1:]:
+            sums = [sum(x[start:stop].astype(F32) for x in group) for group in self.groups]
+            out = sums[0] if len(sums) == 1 else jnp.concatenate(sums, axis=2)
+            for part in self.parts:
                 out = out + part[start:stop].astype(F32)
             return out
 
+        def prepare(self):
+            self.send = self.total(self.count // 2, self.count).astype(BF16)
+
         def move(self, step):
-            half = self.count // 2
-            send = self.total(half, self.count).astype(BF16)
-            self.parts = self.parts + [places.swap(send, step)]
-            self.count = half
+            if self.send is None:
+                self.prepare()
+            self.parts = self.parts + [places.swap(self.send, step)]
+            self.send = None
+            self.count = self.count // 2
 
         def pb_first(self):
             self.move(places.steps - 1)
@@ -958,62 +1001,80 @@
             for step in range(z_steps - 1, 0, -1):
                 self.move(step)
 
+        def prepare_mid(self):
+            self.keep = self.total(0, 1)
+            self.send = self.total(1, 2).astype(BF16)
+
         def mid(self):
-            got = places.swap(self.total(1, 2).astype(BF16), 0).astype(F32)
-            keep = self.total(0, 1)
+            got = places.swap(self.send, 0).astype(F32)
             self.out = jnp.concatenate(
-                [jnp.where(is_q, keep, got), jnp.where(is_q, got, keep)], axis=0
+                [jnp.where(is_q, self.keep, got), jnp.where(is_q, got, self.keep)], axis=0
             )
-
+            self.groups = self.theirs = self.parts = []
+            self.send = self.keep = None
+
+    def hold(chains, *values):
+        names = ("groups", "theirs", "parts", "send", "keep", "out")
+        states, values = tie([[getattr(c, n) for n in names] for c in chains], values)
+        for chain, state in zip(chains, states):
+            for name, value in zip(names, state):
+                setattr(chain, name, value)
+        return values
+
+    make = gradient if even else plain
     send_out = chunked(out[own_rows:], (4, 4, 4, 4))
     d_reduced, send_out = tie(d_reduced, send_out)
     got_out = hand(send_out[:1])
-    sr = Scatter(*(gradient if even else plain)(active, d_reduced))
-    sr.parts, sr.theirs, d_reduced, got_out, send_out = tie(
-        sr.parts, sr.theirs, d_reduced, got_out, send_out
-    )
+    sr = Scatter(*make(active, d_reduced))
+    d_reduced, got_out, send_out = hold([sr], d_reduced, got_out, send_out)
     sr.cores()
     got_out = got_out + hand(send_out[1:2])
     d_expanded, g_bias_expand = hidden_grad(d_reduced, wr, slope)
-    sr.parts, d_expanded, got_out, send_out = tie(sr.parts, d_expanded, got_out, send_out)
+    d_expanded, got_out, send_out = hold([sr], d_expanded, got_out, send_out)
+    sr.prepare()
+    d_expanded, send_out = hold([sr], d_expanded, send_out)
     sr.pb_first()
     got_out = got_out + hand(send_out[2:3])
-    if even:
-        partial = gradient(mid_low, d_expanded, room=D)
-    else:
-        partial = plain(mid_low, d_expanded)
-    partial, d_expanded, got_out, send_out = tie(partial, d_expanded, got_out, send_out)
+    se = Scatter(*make(mid_low, d_expanded))
+    d_expanded, got_out, send_out = hold([se], d_expanded, got_out, send_out)
+    se.cores()
     got_out = got_out + hand(send_out[3:])
     d_first, d_attended, sums_first = first_back(
         d_expanded, we, d_second, norm_one, inverse_one, vec[3][None, :]
     )
-    sr.parts, partial, d_attended, got_out = tie(sr.parts, partial, d_attended, got_out)
+    d_attended, got_out = hold([sr, se], d_attended, got_out)
+    sr.prepare()
+    (d_attended,) = hold([sr], d_attended)
     sr.pb_rest()
-    if even:
-        partial = gradient(context, d_attended, into=tuple(partial))
-    else:
-        also = plain(context, d_attended)
-        partial = [jnp.concatenate(x, axis=2) for x in zip(partial, also)]
-    se = Scatter(*partial)
-    se.parts, se.theirs, d_attended = tie(se.parts, se.theirs, d_attended)
-    se.cores()
+    se.add(*make(context, d_attended))
+    (d_attended,) = hold([se], d_attended)
+    se.cores(1)
     d_context = dot(d_attended, wo, ((1,), (1,))).astype(BF16)
-    d_joined, sums_one = attention_back(qkv, probs, d_context, later, blocks - later)
-    sr.parts, se.parts, d_joined = tie(sr.parts, se.parts, d_joined)
+    (d_context,) = hold([sr, se], d_context)
+    se.prepare()
+    sr.prepare()
+    (d_context,) = hold([sr, se], d_context)
     se.pb_first()
     sr.along_z()
+    d_joined, sums_one = attention_back(qkv, probs, d_context, later, blocks - later)
+    (d_joined,) = hold([sr], d_joined)
+    sr.prepare_mid()
+    (d_joined,) = hold([sr], d_joined)
+    sr.mid()
     send_grad = (d_first[own_rows:] + dot(d_joined[own_rows:], wj, ((1,), (1,)))).astype(BF16)
-    d_joined, send_grad = tie(d_joined, chunked(send_grad, (4, 4, 2, 6)))
+    d_joined, send_grad = hold([sr, se], d_joined, chunked(send_grad, (4, 3, 6, 3)))
+    se.prepare()
+    d_joined, send_grad = hold([se], d_joined, send_grad)
+    se.pb_rest()
     got_grad = hand(send_grad[:1])
     d_joined, sums_two = attention_back(qkv, probs, d_context, 0, later, d_joined)
-    sr.parts, d_joined, got_grad, send_grad = tie(sr.parts, d_joined, got_grad, send_grad)
-    sr.mid()
-    got_grad = got_grad + hand(send_grad[1:2])
-    g_joined_bias = (sums_one + sums_two)[0]
+    d_joined, sums_two, got_grad, send_grad = hold([se], d_joined, sums_two, got_grad, send_grad)
+    se.prepare()
+    g_joined_bias = sums_one + sums_two
     g_vec = jnp.concatenate(
         [
-            g_joined_bias[None, :D],
-            g_joined_bias[None, 2 * D :],
+            g_joined_bias[:, :D],
+            g_joined_bias[:, 2 * D :],
             sums_first[2:3],
             sums_first[:2],
             sums_second[2:3],
@@ -1023,26 +1084,34 @@
     g_small = jnp.concatenate(
         [g_vec.T, g_bias_expand.reshape(D, 4), jnp.zeros((D, 116), F32)], axis=1
     )
-    sj = Scatter(*(gradient if even else plain)(tokens, d_joined, extra=g_small))
-    se.parts, sj.parts, sj.theirs, d_joined, sr.out, got_grad, send_grad = tie(
-        se.parts, sj.parts, sj.theirs, d_joined, sr.out, got_grad, send_grad
-    )
+    d_joined, g_small, send_grad = hold([se], d_joined, g_small, send_grad)
+    se.along_z()
+    got_grad = got_grad + hand(send_grad[1:2])
+    sj = Scatter(*make(tokens, d_joined, extra=g_small))
+    d_joined, got_grad, send_grad = hold([se, sj], d_joined, got_grad, send_grad)
     sj.cores()
-    se.pb_rest()
+    se.prepare_mid()
+    (d_joined,) = hold([se], d_joined)
+    se.mid()
+    own_grad = d_first[:own_rows] + dot(d_joined[:own_rows], wj, ((1,), (1,)))
+    own_grad, send_grad = hold([sj], own_grad, send_grad)
+    sj.prepare()
+    send_grad = hold([sj], send_grad)[0]
+    sj.pb_first()
     got_grad = got_grad + hand(send_grad[2:3])
-    own_grad = d_first[:own_rows] + dot(d_joined[:own_rows], wj, ((1,), (1,)))
-    sj.parts, own_grad, got_grad, send_grad = tie(sj.parts, own_grad, got_grad, send_grad)
-    sj.pb_first()
+    out_q, out_p = deal(tower.reshape(1), out, got_out)
+    got_grad, send_grad, out_q, out_p = hold([sj, se], got_grad, send_grad, out_q, out_p)
+    sj.prepare()
+    send_grad = hold([sj], send_grad)[0]
+    sj.pb_rest()
     got_grad = got_grad + hand(send_grad[3:])
-    out_q, out_p = deal(tower.reshape(1), out, got_out)
-    sj.parts, se.parts, got_grad = tie(sj.parts, se.parts, got_grad)
-    se.along_z()
-    sj.pb_rest()
+    got_grad = hold([sj], got_grad)[0]
+    sj.prepare()
+    got_grad = hold([sj], got_grad)[0]
+    sj.along_z()
     grad_q, grad_p = deal(tower.reshape(1), own_grad, got_grad)
-    sj.parts, se.parts, grad_q, grad_p = tie(sj.parts, se.parts, grad_q, grad_p)
-    sj.along_z()
-    se.mid()
-    sj.parts, se.out = tie(sj.parts, se.out)
+    grad_q, grad_p = hold([sj], grad_q, grad_p)
+    sj.prepare_mid()
     sj.mid()
     grad_joined = sj.out[:, :, : 3 * D]
     grad_expand, grad_output, grad_reduce = se.out[:, :, :FF], se.out[:, :, FF:], sr.out

time: 421 us -> 438 us (1.040)
  matrix products: 36 us -> 24.2 us
  Pallas kernels: 143 us -> 154 us
  local copies, waits for them, and re-layouts: 30.1 us -> 39.2 us
  other arithmetic: 42.4 us -> 48.3 us
  waiting for transfers between devices: 103 us -> 108 us
    ppermute x18, waiting for transfers between devices: 29.9 us -> 45.7 us  [swap_tower(): lax.ppermute(values, 'pa', [(i, i ^ 2 * self.half) for i in range(self.pa...]
    dot_general x9 -> x8, matrix products: 36 us -> 24.2 us  [dot(): lax.dot_general(left, right, (dims, ((), ())), preferred_element_type=F32)]
    pallas_call x0 -> x2, Pallas kernels: none -> 11.2 us  [project(): pl.pallas_call(project_kernel, grid=(count,), in_specs=[pl.BlockSpec((BLO...]
    ppermute x24, waiting for transfers between devices: 65.6 us -> 55.3 us  [swap(): return lax.ppermute(values, AXES, self.pairs(step))]
    add x1 -> x9, other arithmetic: 0.01 us -> 10.1 us  [the longest x6 6.44 us: total(): sum((x[start:stop].astype(F32) for x in group))]
    ppermute x18, starting transfers between devices: 26.3 us -> 19 us  [swap_tower(): lax.ppermute(values, 'pa', [(i, i ^ 2 * self.half) for i in range(self.pa...]
    ppermute x24, starting transfers between devices: 27.7 us -> 34.4 us  [swap(): return lax.ppermute(values, AXES, self.pairs(step))]
    convert_element_type x12 -> x9, other arithmetic: 15.7 us -> 11.2 us  [the longest x8 10.2 us: prepare(): self.send = self.total(self.count // 2, self.count).astype(BF16)]
  transfers between devices with their start and end apart: 55 -> 56, of which waited for: 27 -> 25; matrix products, arithmetic and copies ran while one was open for 17% -> 15% of each run, Pallas kernels for 28% -> 32%
where the time goes in v6:
time: 438 us; the launch traced here: 432 us
  Pallas kernels  154 us (35%)
  waiting for transfers between devices  108 us (25%)
  starting transfers between devices  56.3 us (13%)
  other arithmetic  48.3 us (11%)
  local copies, waits for them, and re-layouts  39.2 us (9%)
  matrix products  24.2 us (6%)
    ppermute x24, waiting for transfers between devices, swap(): return lax.ppermute(values, AXES, self.pairs(step))  55.3 us
    ppermute x18, waiting for transfers between devices, swap_tower(): lax.ppermute(values, 'pa', [(i, i ^ 2 * self.half) for i in range(self.pa...  45.7 us
    ppermute x24, starting transfers between devices, swap(): return lax.ppermute(values, AXES, self.pairs(step))  34.4 us
    dot_general x8, matrix products, dot(): lax.dot_general(left, right, (dims, ((), ())), preferred_element_type=F32)  24.2 us
    pallas_call x3, Pallas kernels, weight_grad(): pl.pallas_call(functools.partial(weight_grad_kernel, chips, extra is not...  23.9 us
    pallas_call x2, Pallas kernels, attention_back(): pl.pallas_call(attention_back_more_kernel if more else attention_back_ker...  21.5 us
    ppermute x18, starting transfers between devices, swap_tower(): lax.ppermute(values, 'pa', [(i, i ^ 2 * self.half) for i in range(self.pa...  19 us
    pallas_call x2, Pallas kernels, expand(): pl.pallas_call(expand_more_kernel if into else expand_kernel, grid=(count...  16.1 us
  transfers between devices with their start and end apart: 56, of which 25 were waited for; matrix products, arithmetic and copies ran while one was open for 15% of the time, Pallas kernels for 32%

profile of v6, /device:TPU:0, one launch (start us, length us, event | category | flops | bytes accessed | tf_op | source)
XLA Modules:
  0.0 432.4 jit_solution(13365241135663460885)
XLA Ops:
  3.4 4.1 collective-permute-start
  11.2 3.6 collective-permute-done
  15.7 3.4 collective-permute-start.2
  20.2 8.4 %collective-permute-done.1 = bf16[2,24,3200]{2,1,0:T(8,128)(2,1)S(1)} collective-permute-done((bf16[2,24,3200]{2,1,0:T(8,128)(2,1)S(1)}, bf16[2,24,3200]{2,1,0:T(8,128)(2,1)S(1)}, u32[]{:S(2)}, u32[]{:S(2)}) %collective-permute-start.1) | collective-permute-done | bytes 307232 | tf_op jit(solution)/shard_map/ppermute | solution.py:66
  30.1 2.5 collective-permute-start.4
  32.6 6.7 %collective-permute-done.4 = bf16[1,24,3072]{2,1,0:T(8,128)(2,1)S(1)} collective-permute-done((bf16[1,24,3072]{2,1,0:T(8,128)(2,1)S(1)}, bf16[1,24,3072]{2,1,0:T(8,128)(2,1)S(1)}, u32[]{:S(2)}, u32[]{:S(2)}) %collective-permute-start.4) | collective-permute-done | bytes 147488 | tf_op jit(solution)/shard_map/ppermute | solution.py:66
  50.9 12.3 %collective-permute-done.7.refs_2_ = bf16[192,768]{1,0:T(8,128)(2,1)S(1)} collective-permute-done((bf16[192,768]{1,0:T(8,128)(2,1)}, bf16[192,768]{1,0:T(8,128)(2,1)S(1)}, u32[]{:S(2)}, u32[]{:S(2)}) %collective-permute-start.7) | collective-permute-done | bytes 294944 | tf_op jit(solution)/shard_map/ppermute | solution.py:72
  68.9 7.9 %collective-permute-done.10 = bf16[4,24,3072]{2,1,0:T(8,128)(2,1)} collective-permute-done((bf16[4,24,3072]{2,1,0:T(8,128)(2,1)}, bf16[4,24,3072]{2,1,0:T(8,128)(2,1)}, u32[]{:S(2)}, u32[]{:S(2)}) %collective-permute-start.10) | collective-permute-done | bytes 589856 | tf_op jit(solution)/shard_map/ppermute | solution.py:66
  78.0 5.4 %assemble.3 = (bf16[16,2,24,2304]{3,2,1,0:T(8,128)(2,1)}, bf16[16,2,24,768]{3,2,1,0:T(8,128)(2,1)}, bf16[16,2,24,128]{3,2,1,0:T(8,128)(2,1)}) custom-call(s32[3,16]{1,0:T(4,128)} %get-tuple-element.763.idx_ref, bf16[8,24,3200]{2,1,0:T(8,128)(2,1)} %copy-done.4, bf16[8,24,3200]{2,1,0:T(8,128)(2,1)} %collective-permute-done.5.refs_1_, ...), custom_call_target="tpu_custom_call" | custom-call | bytes 9830400 | tf_op jit(solution)/shard_map/assemble/pallas_call | solution.py:118
  86.8 5.8 %project.2.refs_0_ = bf16[1024,2304]{1,0:T(8,128)(2,1)} custom-call(bf16[512,768]{1,0:T(8,128)(2,1)} %get-tuple-element.715.tokens_ref.refs_0_, bf16[768,2304]{1,0:T(8,128)(2,1)} %bitcast.73, f32[1,2304]{1,0:T(1,128)} %broadcast_in_dim.16.b_ref), custom_call_target="tpu_custom_call" | custom-call | flops 1811939328 | bytes 6684672 | tf_op jit(solution)/shard_map/project/pallas_call | solution.py:310
  92.6 3.0 collective-permute-start.12
  95.6 2.6 join.2.tokens_ref.left_ref
  98.3 5.4 %project.3.qkv_ref = bf16[1024,2304]{1,0:T(8,128)(2,1)} custom-call(bf16[1024,768]{1,0:T(8,128)(2,1)} %join.2.tokens_ref.left_ref, bf16[768,2304]{1,0:T(8,128)(2,1)} %bitcast.74, f32[1,2304]{1,0:T(1,128)} %broadcast_in_dim.16.b_ref, bf16[1024,2304]{1,0:T(8,128)(2,1)} %project.2.refs_0_), custom_call_target="tpu_custom_call", output_to_operand_aliasing={{}: (3, {})} | custom-call | flops 1811939328 | bytes 6684672 | tf_op jit(solution)/shard_map/project/pallas_call | solution.py:310
  106.7 6.6 %attention.2 = (bf16[1024,768]{1,0:T(8,128)(2,1)}, bf16[4,12,256,256]{3,2,1,0:T(8,128)(2,1)}) custom-call(bf16[1024,2304]{1,0:T(8,128)(2,1)} %project.3.qkv_ref, s32[1024,1]{1,0:T(8,128)} %fusion.14.qid_ref, s32[4,1,256]{2,1,0:T(1,128)} %compare_select_fusion.kid_ref), custom_call_target="tpu_custom_call" | custom-call | flops 805306368 | bytes 6291456 | tf_op jit(solution)/shard_map/attention/pallas_call | solution.py:363
  120.3 6.6 %attention.3 = (bf16[1024,768]{1,0:T(8,128)(2,1)}, bf16[4,12,256,256]{3,2,1,0:T(8,128)(2,1)}) custom-call(bf16[1024,2304]{1,0:T(8,128)(2,1)} %project.3.qkv_ref, s32[1024,1]{1,0:T(8,128)} %fusion.14.qid_ref, s32[4,1,256]{2,1,0:T(1,128)} %compare_select_fusion.kid_ref, ...), custom_call_target="tpu_custom_call", output_to_operand_aliasing={{0}: (3, {}), {1}: (4, {})} | custom-call | flops 805306368 | bytes 6291456 | tf_op jit(solution)/shard_map/attention/pallas_call | solution.py:363
  131.1 3.3 fusion.53
  136.1 2.7 fusion
  138.8 4.9 %assemble.4 = bf16[16,2,24,3072]{3,2,1,0:T(8,128)(2,1)} custom-call(s32[3,16]{1,0:T(4,128)} %get-tuple-element.763.idx_ref, bf16[8,24,3072]{2,1,0:T(8,128)(2,1)} %copy-done.5, bf16[8,24,3072]{2,1,0:T(8,128)(2,1)} %copy-done.14, bf16[8,24,3072]{2,1,0:T(8,128)(2,1)} %collective-permute-done.17.refs_2_, bf16[8,24,3072]{2,1,0:T(8,128)(2,1)} %collective-permute-done.18.refs_3_), custom_call_target="tpu_custom_call" | custom-call | bytes 9437184 | tf_op jit(solution)/shard_map/assemble/pallas_call | solution.py:118
  145.6 7.9 %expand.2 = (bf16[1024,3072]{1,0:T(8,128)(2,1)}, bf16[1024,3072]{1,0:T(8,128)(2,1)}) custom-call(bf16[1024,768]{1,0:T(8,128)(2,1)} %get-tuple-element.392.mid_ref.left_ref, bf16[768,3072]{1,0:T(8,128)(2,1)} %bitcast.70, f32[1,3072]{1,0:T(1,128)} %reshape.707.b_ref), custom_call_target="tpu_custom_call" | custom-call | flops 2415919104 | bytes 10223616 | tf_op jit(solution)/shard_map/expand/pallas_call | solution.py:652
  153.5 3.2 collective-permute-done.24.refs_4_
  158.6 8.2 %expand.3 = (bf16[1024,3072]{1,0:T(8,128)(2,1)}, bf16[1024,3072]{1,0:T(8,128)(2,1)}) custom-call(bf16[1024,768]{1,0:T(8,128)(2,1)} %get-tuple-element.392.mid_ref.left_ref, bf16[768,3072]{1,0:T(8,128)(2,1)} %bitcast.71, f32[1,3072]{1,0:T(1,128)} %reshape.707.b_ref, ...), custom_call_target="tpu_custom_call", output_to_operand_aliasing={{0}: (3, {}), {1}: (4, {})} | custom-call | flops 2415919104 | bytes 10223616 | tf_op jit(solution)/shard_map/expand/pallas_call | solution.py:652
  169.1 5.3 %assemble.5 = bf16[16,2,96,768]{3,2,1,0:T(8,128)(2,1)} custom-call(s32[3,16]{1,0:T(4,128)} %get-tuple-element.763.idx_ref, bf16[8,96,768]{2,1,0:T(8,128)(2,1)} %copy-done.6, bf16[8,96,768]{2,1,0:T(8,128)(2,1)} %copy-done.15, bf16[8,96,768]{2,1,0:T(8,128)(2,1)} %copy-done.16, bf16[8,96,768]{2,1,0:T(8,128)(2,1)} %copy-done.17), custom_call_target="tpu_custom_call" | custom-call | bytes 9437184 | tf_op jit(solution)/shard_map/assemble/pallas_call | solution.py:118
  175.0 8.6 %fusion.54 = (f32[1024]{0:T(1024)S(1)}, f32[1024,768]{1,0:T(8,128)S(1)}) fusion(f32[768]{0:T(1024)S(1)} %copy-done.63, bf16[1024,3072]{1,0:T(8,128)(2,1)S(1)} %copy-done.3, bf16[3072,768]{1,0:T(8,128)(2,1)} %bitcast.78, f32[768]{0:T(1024)S(1)} %copy-done.51, f32[1024,768]{1,0:T(8,128)} %get-tuple-element.702.norm_ref, f32[768]{0:T(1024)S(1)} %copy-done.53), kind=kOutput, calls=%fused_computation.196 | convolution fusion | flops 4835769344 | bytes 17314816 | tf_op jit(solution)/shard_map/dot_general | solution.py:76
  188.3 3.2 collective-permute-done.27
  197.7 2.6 join.3.cot_ref
  201.7 3.9 collective-permute-done.30
  209.3 6.6 %second_back.1 = (f32[1024,768]{1,0:T(8,128)}, bf16[1024,768]{1,0:T(8,128)(2,1)}, f32[8,768]{1,0:T(8,128)}) custom-call(bf16[1024,768]{1,0:T(8,128)(2,1)} %join.3.cot_ref, f32[4,4,768]{2,1,0:T(4,128)} %reshape.716.slot_ref, f32[1024,1]{1,0:T(8,128)} %copy.76.mask_ref, f32[1024,768]{1,0:T(8,128)} %get-tuple-element.698.norm_ref, f32[1024,1]{1,0:T(8,128)} %copy.77.inverse_ref, ...), custom_call_target="tpu_custom_call" | custom-call | flops 15728640 | bytes 9437184 | tf_op jit(solution)/shard_map/second_back/pallas_call | solution.py:570
  217.8 10.0 %tall_grad.1 = (bf16[16,96,768]{2,1,0:T(8,128)(2,1)}, bf16[16,96,768]{2,1,0:T(8,128)(2,1)}) custom-call(s32[3,16]{1,0:T(4,128)} %get-tuple-element.764.table_ref, bf16[1024,3072]{1,0:T(8,128)(2,1)} %get-tuple-element.414.left_ref, bf16[1024,768]{1,0:T(8,128)(2,1)} %get-tuple-element.436.right_ref.grad_ref), custom_call_target="tpu_custom_call" | custom-call | flops 4831838208 | bytes 12582912 | tf_op jit(solution)/shard_map/tall_grad/pallas_call | solution.py:230
  229.0 11.8 %hidden_grad.1 = (bf16[1024,3072]{1,0:T(8,128)(2,1)}, f32[1,3072]{1,0:T(1,128)}) custom-call(bf16[1024,768]{1,0:T(8,128)(2,1)} %get-tuple-element.436.right_ref.grad_ref, bf16[3072,768]{1,0:T(8,128)(2,1)} %bitcast.79, bf16[1024,3072]{1,0:T(8,128)(2,1)} %get-tuple-element.437.slope_ref), custom_call_target="tpu_custom_call" | custom-call | flops 4831838208 | bytes 18874368 | tf_op jit(solution)/shard_map/hidden_grad/pallas_call | solution.py:276
  243.2 10.0 %weight_grad.3 = (bf16[16,24,3072]{2,1,0:T(8,128)(2,1)}, bf16[16,24,3072]{2,1,0:T(8,128)(2,1)}) custom-call(s32[3,16]{1,0:T(4,128)} %get-tuple-element.764.table_ref, bf16[1024,768]{1,0:T(8,128)(2,1)} %get-tuple-element.392.mid_ref.left_ref, bf16[1024,3072]{1,0:T(8,128)(2,1)} %get-tuple-element.460.right_ref.hidden_ref), custom_call_target="tpu_custom_call" | custom-call | flops 4831838208 | bytes 12582912 | tf_op jit(solution)/shard_map/weight_grad/pallas_call | solution.py:188
  257.1 12.6 %first_back.1 = (f32[1024,768]{1,0:T(8,128)}, bf16[1024,768]{1,0:T(8,128)(2,1)}, f32[8,768]{1,0:T(8,128)}) custom-call(bf16[1024,3072]{1,0:T(8,128)(2,1)} %get-tuple-element.460.right_ref.hidden_ref, bf16[768,3072]{1,0:T(8,128)(2,1)} %bitcast.72, f32[1024,768]{1,0:T(8,128)} %get-tuple-element.461.second_ref, f32[1024,768]{1,0:T(8,128)} %get-tuple-element.702.norm_ref, ...), custom_call_target="tpu_custom_call" | custom-call | flops 4831838208 | bytes 22020096 | tf_op jit(solution)/shard_map/first_back/pallas_call | solution.py:610
  272.6 5.0 %weight_grad.4 = (bf16[16,24,768]{2,1,0:T(8,128)(2,1)}, bf16[16,24,768]{2,1,0:T(8,128)(2,1)}) custom-call(s32[3,16]{1,0:T(4,128)} %get-tuple-element.764.table_ref, bf16[1024,768]{1,0:T(8,128)(2,1)} %get-tuple-element.380.left_ref, bf16[1024,768]{1,0:T(8,128)(2,1)} %get-tuple-element.484.right_ref), custom_call_target="tpu_custom_call" | custom-call | flops 1207959552 | bytes 4325376 | tf_op jit(solution)/shard_map/weight_grad/pallas_call | solution.py:188
  279.4 4.3 convolution_convert_fusion.grad_ref
  283.7 3.9 collective-permute-done.39
  293.4 10.7 %attention_back.2 = (bf16[1024,2304]{1,0:T(8,128)(2,1)}, f32[1,2304]{1,0:T(1,128)}) custom-call(bf16[1024,2304]{1,0:T(8,128)(2,1)} %project.3.qkv_ref, bf16[4,12,256,256]{3,2,1,0:T(8,128)(2,1)} %get-tuple-element.499.probs_ref, bf16[1024,768]{1,0:T(8,128)(2,1)} %convolution_convert_fusion.grad_ref), custom_call_target="tpu_custom_call" | custom-call | flops 1610612736 | bytes 8650752 | tf_op jit(solution)/shard_map/attention_back/pallas_call | solution.py:439
  305.7 4.1 add_convert_fusion.3
  313.6 6.5 %collective-permute-done.42 = bf16[1,96,768]{2,1,0:T(8,128)(2,1)S(1)} collective-permute-done((bf16[1,96,768]{2,1,0:T(8,128)(2,1)S(1)}, bf16[1,96,768]{2,1,0:T(8,128)(2,1)S(1)}, u32[]{:S(2)}, u32[]{:S(2)}) %collective-permute-start.42) | collective-permute-done | bytes 147488 | tf_op jit(solution)/shard_map/ppermute | solution.py:66
  334.8 10.8 %attention_back.3 = (bf16[1024,2304]{1,0:T(8,128)(2,1)}, f32[1,2304]{1,0:T(1,128)}) custom-call(bf16[1024,2304]{1,0:T(8,128)(2,1)} %project.3.qkv_ref, bf16[4,12,256,256]{3,2,1,0:T(8,128)(2,1)} %get-tuple-element.499.probs_ref, bf16[1024,768]{1,0:T(8,128)(2,1)} %convolution_convert_fusion.grad_ref, ...), custom_call_target="tpu_custom_call", output_to_operand_aliasing={{0}: (3, {})} | custom-call | flops 1610612736 | bytes 8650752 | tf_op jit(solution)/shard_map/attention_back/pallas_call | solution.py:439
  358.3 2.8 deal.2
  361.7 8.8 %weight_grad.5 = (bf16[16,24,2432]{2,1,0:T(8,128)(2,1)}, bf16[16,24,2432]{2,1,0:T(8,128)(2,1)}) custom-call(s32[3,16]{1,0:T(4,128)} %get-tuple-element.764.table_ref, bf16[1024,768]{1,0:T(8,128)(2,1)} %join.2.tokens_ref.left_ref, bf16[1024,2304]{1,0:T(8,128)(2,1)} %get-tuple-element.580.right_ref, f32[768,128]{1,0:T(8,128)} %maximum_maximum_fusion.refs_0_), custom_call_target="tpu_custom_call" | custom-call | flops 3623878656 | bytes 9830400 | tf_op jit(solution)/shard_map/weight_grad/pallas_call | solution.py:188
  374.3 2.5 collective-permute-start.50
  376.7 3.2 slice_add_fusion.own_ref
  381.0 5.1 %collective-permute-done.50 = bf16[1,24,3840]{2,1,0:T(8,128)(2,1)S(1)} collective-permute-done((bf16[1,24,3840]{2,1,0:T(8,128)(2,1)S(1)}, bf16[1,24,3840]{2,1,0:T(8,128)(2,1)S(1)}, u32[]{:S(2)}, u32[]{:S(2)}) %collective-permute-start.50) | collective-permute-done | bytes 184352 | tf_op jit(solution)/shard_map/ppermute | solution.py:66
  386.3 14.7 %collective-permute-done.51.refs_2_ = bf16[192,768]{1,0:T(8,128)(2,1)S(1)} collective-permute-done((bf16[192,768]{1,0:T(8,128)(2,1)S(1)}, bf16[192,768]{1,0:T(8,128)(2,1)S(1)}, u32[]{:S(2)}, u32[]{:S(2)}) %collective-permute-start.51) | collective-permute-done | bytes 294944 | tf_op jit(solution)/shard_map/ppermute | solution.py:72
  402.4 8.7 %collective-permute-done.53.refs_3_ = bf16[96,768]{1,0:T(8,128)(2,1)S(1)} collective-permute-done((bf16[96,768]{1,0:T(8,128)(2,1)S(1)}, bf16[96,768]{1,0:T(8,128)(2,1)S(1)}, u32[]{:S(2)}, u32[]{:S(2)}) %collective-permute-start.53) | collective-permute-done | bytes 147488 | tf_op jit(solution)/shard_map/ppermute | solution.py:72
  412.6 3.5 deal.3
  416.1 4.0 collective-permute-done.54
  424.0 4.9 %collective-permute-done.55 = bf16[1,24,2432]{2,1,0:T(8,128)(2,1)S(1)} collective-permute-done((bf16[1,24,2432]{2,1,0:T(8,128)(2,1)S(1)}, bf16[1,24,2432]{2,1,0:T(8,128)(2,1)S(1)}, u32[]{:S(2)}, u32[]{:S(2)}) %collective-permute-start.55) | collective-permute-done | bytes 116768 | tf_op jit(solution)/shard_map/ppermute | solution.py:66
  (392 shorter events, 137.8 us)
Async XLA Ops:
  3.4 11.4 %collective-permute-start = (bf16[1,24,3200]{2,1,0:T(8,128)(2,1)S(1)}, bf16[1,24,3200]{2,1,0:T(8,128)(2,1)S(1)}, u32[]{:S(2)}, u32[]{:S(2)}) collective-permute-start(bf16[1,24,3200]{2,1,0:T(8,128)(2,1)S(1)} %get-tuple-element.734), channel_id=1, source_target_pairs={{0,4},{1,5},{2,6},{3,7},{4,0},{5,1},{6,2},{7,3},{8,12},{9,13},{10,... | collective-permute-start | bytes 460808 | tf_op jit(solution)/shard_map/ppermute | solution.py:66
  14.9 13.8 %collective-permute-start.1 = (bf16[2,24,3200]{2,1,0:T(8,128)(2,1)S(1)}, bf16[2,24,3200]{2,1,0:T(8,128)(2,1)S(1)}, u32[]{:S(2)}, u32[]{:S(2)}) collective-permute-start(bf16[2,24,3200]{2,1,0:T(8,128)(2,1)S(1)} %pad_maximum_fusion.9), channel_id=1, source_target_pairs={{0,2},{1,3},{2,0},{3,1},{4,6},{5,7},{6,4},{7,5},{8,10},{9,11},{10,... | collective-permute-start | bytes 921608 | tf_op jit(solution)/shard_map/ppermute | solution.py:66
  15.7 13.0 %collective-permute-start.2 = (bf16[160,768]{1,0:T(8,128)(2,1)S(1)}, bf16[160,768]{1,0:T(8,128)(2,1)S(1)}, u32[]{:S(2)}, u32[]{:S(2)}) collective-permute-start(bf16[160,768]{1,0:T(8,128)(2,1)S(1)} %get-tuple-element.329), channel_id=1, source_target_pairs={{0,4},{1,5},{2,6},{3,7},{4,0},{5,1},{6,2},{7,3},{8,12},{9,13},{10,... | collective-permute-start | bytes 737288 | tf_op jit(solution)/shard_map/ppermute | solution.py:72
  28.8 11.3 %collective-permute-start.3 = (bf16[4,24,3200]{2,1,0:T(8,128)(2,1)S(1)}, bf16[4,24,3200]{2,1,0:T(8,128)(2,1)S(1)}, u32[]{:S(2)}, u32[]{:S(2)}) collective-permute-start(bf16[4,24,3200]{2,1,0:T(8,128)(2,1)S(1)} %pad_maximum_fusion.5), channel_id=1, source_target_pairs={{0,8},{1,17},{2,10},{3,19},{4,12},{5,21},{6,14},{7,23},{8,0},{9,25... | collective-permute-start | bytes 1843208 | tf_op jit(solution)/shard_map/ppermute | solution.py:66
  30.1 9.2 %collective-permute-start.4 = (bf16[1,24,3072]{2,1,0:T(8,128)(2,1)S(1)}, bf16[1,24,3072]{2,1,0:T(8,128)(2,1)S(1)}, u32[]{:S(2)}, u32[]{:S(2)}) collective-permute-start(bf16[1,24,3072]{2,1,0:T(8,128)(2,1)S(1)} %get-tuple-element.333), channel_id=1, source_target_pairs={{0,4},{1,5},{2,6},{3,7},{4,0},{5,1},{6,2},{7,3},{8,12},{9,13},{10,... | collective-permute-start | bytes 442376 | tf_op jit(solution)/shard_map/ppermute | solution.py:66
  40.2 23.0 %collective-permute-start.5 = (bf16[8,24,3200]{2,1,0:T(8,128)(2,1)S(1)}, bf16[8,24,3200]{2,1,0:T(8,128)(2,1)}, u32[]{:S(2)}, u32[]{:S(2)}) collective-permute-start(bf16[8,24,3200]{2,1,0:T(8,128)(2,1)S(1)} %pad_maximum_fusion.1.refs_0_), channel_id=1, source_target_pairs={{0,16},{1,9},{2,18},{3,11},{4,20},{5,13},{6,22},{7,15},{8,24},{9,1... | collective-permute-start | bytes 3686408 | tf_op jit(solution)/shard_map/ppermute | solution.py:66
  46.3 31.7 %collective-permute-start.8 = (bf16[8,24,3200]{2,1,0:T(8,128)(2,1)S(1)}, bf16[8,24,3200]{2,1,0:T(8,128)(2,1)}, u32[]{:S(2)}, u32[]{:S(2)}) collective-permute-start(bf16[8,24,3200]{2,1,0:T(8,128)(2,1)S(1)} %pad_maximum_fusion.1.refs_0_), channel_id=1, source_target_pairs={{0,1},{1,0},{2,3},{3,2},{4,5},{5,4},{6,7},{7,6},{8,9},{9,8},{10,11... | collective-permute-start | bytes 3686408 | tf_op jit(solution)/shard_map/ppermute | solution.py:69
  46.3 16.8 %collective-permute-start.7 = (bf16[192,768]{1,0:T(8,128)(2,1)}, bf16[192,768]{1,0:T(8,128)(2,1)S(1)}, u32[]{:S(2)}, u32[]{:S(2)}) collective-permute-start(bf16[192,768]{1,0:T(8,128)(2,1)} %slice.497), channel_id=1, source_target_pairs={{0,4},{1,5},{2,6},{3,7},{4,0},{5,1},{6,2},{7,3},{8,12},{9,13},{10,... | collective-permute-start | bytes 884744 | tf_op jit(solution)/shard_map/ppermute | solution.py:72
  63.2 14.9 %collective-permute-start.9 = (bf16[8,24,3200]{2,1,0:T(8,128)(2,1)}, bf16[8,24,3200]{2,1,0:T(8,128)(2,1)}, u32[]{:S(2)}, u32[]{:S(2)}) collective-permute-start(bf16[8,24,3200]{2,1,0:T(8,128)(2,1)} %collective-permute-done.5.refs_1_), channel_id=1, source_target_pairs={{0,1},{1,0},{2,3},{3,2},{4,5},{5,4},{6,7},{7,6},{8,9},{9,8},{10,11... | collective-permute-start | bytes 3686408 | tf_op jit(solution)/shard_map/ppermute | solution.py:69
  66.6 10.2 %collective-permute-start.10 = (bf16[4,24,3072]{2,1,0:T(8,128)(2,1)}, bf16[4,24,3072]{2,1,0:T(8,128)(2,1)}, u32[]{:S(2)}, u32[]{:S(2)}) collective-permute-start(bf16[4,24,3072]{2,1,0:T(8,128)(2,1)} %pad_maximum_fusion.6), channel_id=1, source_target_pairs={{0,8},{1,17},{2,10},{3,19},{4,12},{5,21},{6,14},{7,23},{8,0},{9,25... | collective-permute-start | bytes 1769480 | tf_op jit(solution)/shard_map/ppermute | solution.py:66
  68.7 23.9 %collective-permute-start.11 = (bf16[160,768]{1,0:T(8,128)(2,1)}, bf16[160,768]{1,0:T(8,128)(2,1)}, u32[]{:S(2)}, u32[]{:S(2)}) collective-permute-start(bf16[160,768]{1,0:T(8,128)(2,1)} %get-tuple-element.350), channel_id=1, source_target_pairs={{0,4},{1,5},{2,6},{3,7},{4,0},{5,1},{6,2},{7,3},{8,12},{9,13},{10,... | collective-permute-start | bytes 737288 | tf_op jit(solution)/shard_map/ppermute | solution.py:72
  86.2 29.3 %collective-permute-start.14 = (bf16[8,24,3072]{2,1,0:T(8,128)(2,1)S(1)}, bf16[8,24,3072]{2,1,0:T(8,128)(2,1)S(1)}, u32[]{:S(2)}, u32[]{:S(2)}) collective-permute-start(bf16[8,24,3072]{2,1,0:T(8,128)(2,1)S(1)} %pad_maximum_fusion.2.refs_0_), channel_id=1, source_target_pairs={{0,16},{1,9},{2,18},{3,11},{4,20},{5,13},{6,22},{7,15},{8,24},{9,1... | collective-permute-start | bytes 3538952 | tf_op jit(solution)/shard_map/ppermute | solution.py:66
  86.6 17.2 %collective-permute-start.13 = (s32[512]{0:T(512)S(1)}, s32[512]{0:T(512)S(1)}, u32[]{:S(2)}, u32[]{:S(2)}) collective-permute-start(s32[512]{0:T(512)S(1)} %get-tuple-element.752), channel_id=1, source_target_pairs={{0,4},{1,5},{2,6},{3,7},{4,0},{5,1},{6,2},{7,3},{8,12},{9,13},{10,... | collective-permute-start | bytes 6152 | tf_op jit(solution)/shard_map/ppermute | solution.py:72
  92.6 11.0 %collective-permute-start.12 = (bf16[1,96,768]{2,1,0:T(8,128)(2,1)S(1)}, bf16[1,96,768]{2,1,0:T(8,128)(2,1)S(1)}, u32[]{:S(2)}, u32[]{:S(2)}) collective-permute-start(bf16[1,96,768]{2,1,0:T(8,128)(2,1)S(1)} %copy-done.46), channel_id=1, source_target_pairs={{0,4},{1,5},{2,6},{3,7},{4,0},{5,1},{6,2},{7,3},{8,12},{9,13},{10,... | collective-permute-start | bytes 442376 | tf_op jit(solution)/shard_map/ppermute | solution.py:66
  103.7 11.7 %collective-permute-start.15 = (bf16[2,96,768]{2,1,0:T(8,128)(2,1)S(1)}, bf16[2,96,768]{2,1,0:T(8,128)(2,1)S(1)}, u32[]{:S(2)}, u32[]{:S(2)}) collective-permute-start(bf16[2,96,768]{2,1,0:T(8,128)(2,1)S(1)} %pad_maximum_fusion.11), channel_id=1, source_target_pairs={{0,2},{1,3},{2,0},{3,1},{4,6},{5,7},{6,4},{7,5},{8,10},{9,11},{10,... | collective-permute-start | bytes 884744 | tf_op jit(solution)/shard_map/ppermute | solution.py:66
  104.5 23.7 %collective-permute-start.17 = (bf16[8,24,3072]{2,1,0:T(8,128)(2,1)S(1)}, bf16[8,24,3072]{2,1,0:T(8,128)(2,1)}, u32[]{:S(2)}, u32[]{:S(2)}) collective-permute-start(bf16[8,24,3072]{2,1,0:T(8,128)(2,1)S(1)} %pad_maximum_fusion.2.refs_0_), channel_id=1, source_target_pairs={{0,1},{1,0},{2,3},{3,2},{4,5},{5,4},{6,7},{7,6},{8,9},{9,8},{10,11... | collective-permute-start | bytes 3538952 | tf_op jit(solution)/shard_map/ppermute | solution.py:69
  104.5 11.0 %collective-permute-start.16 = (bf16[96,768]{1,0:T(8,128)(2,1)S(1)}, bf16[96,768]{1,0:T(8,128)(2,1)S(1)}, u32[]{:S(2)}, u32[]{:S(2)}) collective-permute-start(bf16[96,768]{1,0:T(8,128)(2,1)S(1)} %copy-done.42), channel_id=1, source_target_pairs={{0,4},{1,5},{2,6},{3,7},{4,0},{5,1},{6,2},{7,3},{8,12},{9,13},{10,... | collective-permute-start | bytes 442376 | tf_op jit(solution)/shard_map/ppermute | solution.py:72
  116.2 12.9 %collective-permute-start.18 = (bf16[8,24,3072]{2,1,0:T(8,128)(2,1)S(1)}, bf16[8,24,3072]{2,1,0:T(8,128)(2,1)}, u32[]{:S(2)}, u32[]{:S(2)}) collective-permute-start(bf16[8,24,3072]{2,1,0:T(8,128)(2,1)S(1)} %collective-permute-done.14.refs_1_), channel_id=1, source_target_pairs={{0,1},{1,0},{2,3},{3,2},{4,5},{5,4},{6,7},{7,6},{8,9},{9,8},{10,11... | collective-permute-start | bytes 3538952 | tf_op jit(solution)/shard_map/ppermute | solution.py:69
  116.2 10.7 %collective-permute-start.19 = (bf16[4,96,768]{2,1,0:T(8,128)(2,1)S(1)}, bf16[4,96,768]{2,1,0:T(8,128)(2,1)}, u32[]{:S(2)}, u32[]{:S(2)}) collective-permute-start(bf16[4,96,768]{2,1,0:T(8,128)(2,1)S(1)} %pad_maximum_fusion.7), channel_id=1, source_target_pairs={{0,8},{1,17},{2,10},{3,19},{4,12},{5,21},{6,14},{7,23},{8,0},{9,25... | collective-permute-start | bytes 1769480 | tf_op jit(solution)/shard_map/ppermute | solution.py:66
  119.1 10.0 %collective-permute-start.20 = (bf16[96,768]{1,0:T(8,128)(2,1)}, bf16[96,768]{1,0:T(8,128)(2,1)S(1)}, u32[]{:S(2)}, u32[]{:S(2)}) collective-permute-start(bf16[96,768]{1,0:T(8,128)(2,1)} %get-tuple-element.376), channel_id=1, source_target_pairs={{0,4},{1,5},{2,6},{3,7},{4,0},{5,1},{6,2},{7,3},{8,12},{9,13},{10,... | collective-permute-start | bytes 442376 | tf_op jit(solution)/shard_map/ppermute | solution.py:72
  129.7 27.0 %collective-permute-start.22 = (bf16[8,96,768]{2,1,0:T(8,128)(2,1)S(1)}, bf16[8,96,768]{2,1,0:T(8,128)(2,1)S(1)}, u32[]{:S(2)}, u32[]{:S(2)}) collective-permute-start(bf16[8,96,768]{2,1,0:T(8,128)(2,1)S(1)} %pad_maximum_fusion.3.refs_0_), channel_id=1, source_target_pairs={{0,16},{1,9},{2,18},{3,11},{4,20},{5,13},{6,22},{7,15},{8,24},{9,1... | collective-permute-start | bytes 3538952 | tf_op jit(solution)/shard_map/ppermute | solution.py:66
  131.1 25.7 %collective-permute-start.23 = (bf16[8,96,768]{2,1,0:T(8,128)(2,1)S(1)}, bf16[8,96,768]{2,1,0:T(8,128)(2,1)S(1)}, u32[]{:S(2)}, u32[]{:S(2)}) collective-permute-start(bf16[8,96,768]{2,1,0:T(8,128)(2,1)S(1)} %pad_maximum_fusion.3.refs_0_), channel_id=1, source_target_pairs={{0,1},{1,0},{2,3},{3,2},{4,5},{5,4},{6,7},{7,6},{8,9},{9,8},{10,11... | collective-permute-start | bytes 3538952 | tf_op jit(solution)/shard_map/ppermute | solution.py:69
  134.4 10.3 %collective-permute-start.21 = (bf16[96,768]{1,0:T(8,128)(2,1)S(1)}, bf16[96,768]{1,0:T(8,128)(2,1)S(1)}, u32[]{:S(2)}, u32[]{:S(2)}) collective-permute-start(bf16[96,768]{1,0:T(8,128)(2,1)S(1)} %copy-done.39), channel_id=1, source_target_pairs={{0,4},{1,5},{2,6},{3,7},{4,0},{5,1},{6,2},{7,3},{8,12},{9,13},{10,... | collective-permute-start | bytes 442376 | tf_op jit(solution)/shard_map/ppermute | solution.py:72
  144.7 12.0 %collective-permute-start.24 = (bf16[128,768]{1,0:T(8,128)(2,1)S(1)}, bf16[128,768]{1,0:T(8,128)(2,1)S(1)}, u32[]{:S(2)}, u32[]{:S(2)}) collective-permute-start(bf16[128,768]{1,0:T(8,128)(2,1)S(1)} %copy-done.36), channel_id=1, source_target_pairs={{0,4},{1,5},{2,6},{3,7},{4,0},{5,1},{6,2},{7,3},{8,12},{9,13},{10,... | collective-permute-start | bytes 589832 | tf_op jit(solution)/shard_map/ppermute | solution.py:72
  157.8 10.3 %collective-permute-start.25 = (bf16[8,96,768]{2,1,0:T(8,128)(2,1)S(1)}, bf16[8,96,768]{2,1,0:T(8,128)(2,1)S(1)}, u32[]{:S(2)}, u32[]{:S(2)}) collective-permute-start(bf16[8,96,768]{2,1,0:T(8,128)(2,1)S(1)} %collective-permute-done.22.refs_1_), channel_id=1, source_target_pairs={{0,1},{1,0},{2,3},{3,2},{4,5},{5,4},{6,7},{7,6},{8,9},{9,8},{10,11... | collective-permute-start | bytes 3538952 | tf_op jit(solution)/shard_map/ppermute | solution.py:69
  158.5 9.6 %collective-permute-start.26 = (bf16[96,768]{1,0:T(8,128)(2,1)S(1)}, bf16[96,768]{1,0:T(8,128)(2,1)S(1)}, u32[]{:S(2)}, u32[]{:S(2)}) collective-permute-start(bf16[96,768]{1,0:T(8,128)(2,1)S(1)} %copy-done.37), channel_id=1, source_target_pairs={{0,4},{1,5},{2,6},{3,7},{4,0},{5,1},{6,2},{7,3},{8,12},{9,13},{10,... | collective-permute-start | bytes 442376 | tf_op jit(solution)/shard_map/ppermute | solution.py:72
  215.9 12.1 %collective-permute-start.32 = (bf16[128,768]{1,0:T(8,128)(2,1)S(1)}, bf16[128,768]{1,0:T(8,128)(2,1)S(1)}, u32[]{:S(2)}, u32[]{:S(2)}) collective-permute-start(bf16[128,768]{1,0:T(8,128)(2,1)S(1)} %get-tuple-element.430), channel_id=1, source_target_pairs={{0,4},{1,5},{2,6},{3,7},{4,0},{5,1},{6,2},{7,3},{8,12},{9,13},{10,... | collective-permute-start | bytes 589832 | tf_op jit(solution)/shard_map/ppermute | solution.py:72
  228.0 12.8 %collective-permute-start.33 = (bf16[16,96,768]{2,1,0:T(8,128)(2,1)}, bf16[16,96,768]{2,1,0:T(8,128)(2,1)S(1)}, u32[]{:S(2)}, u32[]{:S(2)}) collective-permute-start(bf16[16,96,768]{2,1,0:T(8,128)(2,1)} %get-tuple-element.435), channel_id=1, source_target_pairs={{0,1},{1,0},{2,3},{3,2},{4,5},{5,4},{6,7},{7,6},{8,9},{9,8},{10,11... | collective-permute-start | bytes 7077896 | tf_op jit(solution)/shard_map/ppermute | solution.py:69
  228.0 12.8 %collective-permute-start.34 = (bf16[128,768]{1,0:T(8,128)(2,1)S(1)}, bf16[128,768]{1,0:T(8,128)(2,1)S(1)}, u32[]{:S(2)}, u32[]{:S(2)}) collective-permute-start(bf16[128,768]{1,0:T(8,128)(2,1)S(1)} %get-tuple-element.440), channel_id=1, source_target_pairs={{0,4},{1,5},{2,6},{3,7},{4,0},{5,1},{6,2},{7,3},{8,12},{9,13},{10,... | collective-permute-start | bytes 589832 | tf_op jit(solution)/shard_map/ppermute | solution.py:72
  241.2 12.1 %collective-permute-start.36 = (bf16[128,768]{1,0:T(8,128)(2,1)S(1)}, bf16[128,768]{1,0:T(8,128)(2,1)S(1)}, u32[]{:S(2)}, u32[]{:S(2)}) collective-permute-start(bf16[128,768]{1,0:T(8,128)(2,1)S(1)} %get-tuple-element.456), channel_id=1, source_target_pairs={{0,4},{1,5},{2,6},{3,7},{4,0},{5,1},{6,2},{7,3},{8,12},{9,13},{10,... | collective-permute-start | bytes 589832 | tf_op jit(solution)/shard_map/ppermute | solution.py:72
  254.0 16.3 %collective-permute-start.37 = (bf16[16,24,3072]{2,1,0:T(8,128)(2,1)}, bf16[16,24,3072]{2,1,0:T(8,128)(2,1)S(1)}, u32[]{:S(2)}, u32[]{:S(2)}) collective-permute-start(bf16[16,24,3072]{2,1,0:T(8,128)(2,1)} %get-tuple-element.459), channel_id=1, source_target_pairs={{0,1},{1,0},{2,3},{3,2},{4,5},{5,4},{6,7},{7,6},{8,9},{9,8},{10,11... | collective-permute-start | bytes 7077896 | tf_op jit(solution)/shard_map/ppermute | solution.py:69
  254.0 16.3 %collective-permute-start.35 = (bf16[8,96,768]{2,1,0:T(8,128)(2,1)S(1)}, bf16[8,96,768]{2,1,0:T(8,128)(2,1)}, u32[]{:S(2)}, u32[]{:S(2)}) collective-permute-start(bf16[8,96,768]{2,1,0:T(8,128)(2,1)S(1)} %add_convert_fusion.1), channel_id=1, source_target_pairs={{0,16},{1,9},{2,18},{3,11},{4,20},{5,13},{6,22},{7,15},{8,24},{9,1... | collective-permute-start | bytes 3538952 | tf_op jit(solution)/shard_map/ppermute | solution.py:66
  256.2 13.5 %collective-permute-start.38 = (bf16[128,768]{1,0:T(8,128)(2,1)}, bf16[128,768]{1,0:T(8,128)(2,1)S(1)}, u32[]{:S(2)}, u32[]{:S(2)}) collective-permute-start(bf16[128,768]{1,0:T(8,128)(2,1)} %get-tuple-element.466), channel_id=1, source_target_pairs={{0,4},{1,5},{2,6},{3,7},{4,0},{5,1},{6,2},{7,3},{8,12},{9,13},{10,... | collective-permute-start | bytes 589832 | tf_op jit(solution)/shard_map/ppermute | solution.py:72
  277.6 9.9 %collective-permute-start.39 = (bf16[4,96,768]{2,1,0:T(8,128)(2,1)S(1)}, bf16[4,96,768]{2,1,0:T(8,128)(2,1)S(1)}, u32[]{:S(2)}, u32[]{:S(2)}) collective-permute-start(bf16[4,96,768]{2,1,0:T(8,128)(2,1)S(1)} %add_convert_fusion.4), channel_id=1, source_target_pairs={{0,8},{1,17},{2,10},{3,19},{4,12},{5,21},{6,14},{7,23},{8,0},{9,25... | collective-permute-start | bytes 1769480 | tf_op jit(solution)/shard_map/ppermute | solution.py:66
  291.2 12.9 %collective-permute-start.41 = (bf16[2,96,768]{2,1,0:T(8,128)(2,1)}, bf16[2,96,768]{2,1,0:T(8,128)(2,1)}, u32[]{:S(2)}, u32[]{:S(2)}) collective-permute-start(bf16[2,96,768]{2,1,0:T(8,128)(2,1)} %add_convert_fusion.7), channel_id=1, source_target_pairs={{0,2},{1,3},{2,0},{3,1},{4,6},{5,7},{6,4},{7,5},{8,10},{9,11},{10,... | collective-permute-start | bytes 884744 | tf_op jit(solution)/shard_map/ppermute | solution.py:66
  292.7 28.3 %collective-permute-start.43 = (bf16[8,24,3840]{2,1,0:T(8,128)(2,1)}, bf16[8,24,3840]{2,1,0:T(8,128)(2,1)}, u32[]{:S(2)}, u32[]{:S(2)}) collective-permute-start(bf16[8,24,3840]{2,1,0:T(8,128)(2,1)} %pad_maximum_fusion), channel_id=1, source_target_pairs={{0,16},{1,9},{2,18},{3,11},{4,20},{5,13},{6,22},{7,15},{8,24},{9,1... | collective-permute-start | bytes 4423688 | tf_op jit(solution)/shard_map/ppermute | solution.py:66
  311.3 8.8 %collective-permute-start.42 = (bf16[1,96,768]{2,1,0:T(8,128)(2,1)S(1)}, bf16[1,96,768]{2,1,0:T(8,128)(2,1)S(1)}, u32[]{:S(2)}, u32[]{:S(2)}) collective-permute-start(bf16[1,96,768]{2,1,0:T(8,128)(2,1)S(1)} %get-tuple-element.509), channel_id=1, source_target_pairs={{0,4},{1,5},{2,6},{3,7},{4,0},{5,1},{6,2},{7,3},{8,12},{9,13},{10,... | collective-permute-start | bytes 442376 | tf_op jit(solution)/shard_map/ppermute | solution.py:66
  325.3 20.2 %collective-permute-start.44 = (bf16[4,24,3840]{2,1,0:T(8,128)(2,1)}, bf16[4,24,3840]{2,1,0:T(8,128)(2,1)}, u32[]{:S(2)}, u32[]{:S(2)}) collective-permute-start(bf16[4,24,3840]{2,1,0:T(8,128)(2,1)} %fusion.5), channel_id=1, source_target_pairs={{0,8},{1,17},{2,10},{3,19},{4,12},{5,21},{6,14},{7,23},{8,0},{9,25... | collective-permute-start | bytes 2211848 | tf_op jit(solution)/shard_map/ppermute | solution.py:66
  326.4 19.2 %collective-permute-start.45 = (bf16[128,768]{1,0:T(8,128)(2,1)}, bf16[128,768]{1,0:T(8,128)(2,1)}, u32[]{:S(2)}, u32[]{:S(2)}) collective-permute-start(bf16[128,768]{1,0:T(8,128)(2,1)} %slice.515), channel_id=1, source_target_pairs={{0,4},{1,5},{2,6},{3,7},{4,0},{5,1},{6,2},{7,3},{8,12},{9,13},{10,... | collective-permute-start | bytes 589832 | tf_op jit(solution)/shard_map/ppermute | solution.py:72
  355.9 14.6 %collective-permute-start.46 = (bf16[2,24,3840]{2,1,0:T(8,128)(2,1)}, bf16[2,24,3840]{2,1,0:T(8,128)(2,1)}, u32[]{:S(2)}, u32[]{:S(2)}) collective-permute-start(bf16[2,24,3840]{2,1,0:T(8,128)(2,1)} %fusion.13), channel_id=1, source_target_pairs={{0,2},{1,3},{2,0},{3,1},{4,6},{5,7},{6,4},{7,5},{8,10},{9,11},{10,... | collective-permute-start | bytes 1105928 | tf_op jit(solution)/shard_map/ppermute | solution.py:66
  361.1 9.4 %collective-permute-start.47 = (bf16[96,768]{1,0:T(8,128)(2,1)}, bf16[96,768]{1,0:T(8,128)(2,1)}, u32[]{:S(2)}, u32[]{:S(2)}) collective-permute-start(bf16[96,768]{1,0:T(8,128)(2,1)} %get-tuple-element.567), channel_id=1, source_target_pairs={{0,4},{1,5},{2,6},{3,7},{4,0},{5,1},{6,2},{7,3},{8,12},{9,13},{10,... | collective-permute-start | bytes 442376 | tf_op jit(solution)/shard_map/ppermute | solution.py:72
  370.5 9.4 %collective-permute-start.48 = (bf16[16,24,2432]{2,1,0:T(8,128)(2,1)}, bf16[16,24,2432]{2,1,0:T(8,128)(2,1)S(1)}, u32[]{:S(2)}, u32[]{:S(2)}) collective-permute-start(bf16[16,24,2432]{2,1,0:T(8,128)(2,1)} %get-tuple-element.571), channel_id=1, source_target_pairs={{0,1},{1,0},{2,3},{3,2},{4,5},{5,4},{6,7},{7,6},{8,9},{9,8},{10,11... | collective-permute-start | bytes 5603336 | tf_op jit(solution)/shard_map/ppermute | solution.py:69
  374.3 11.8 %collective-permute-start.50 = (bf16[1,24,3840]{2,1,0:T(8,128)(2,1)S(1)}, bf16[1,24,3840]{2,1,0:T(8,128)(2,1)S(1)}, u32[]{:S(2)}, u32[]{:S(2)}) collective-permute-start(bf16[1,24,3840]{2,1,0:T(8,128)(2,1)S(1)} %get-tuple-element.591), channel_id=1, source_target_pairs={{0,4},{1,5},{2,6},{3,7},{4,0},{5,1},{6,2},{7,3},{8,12},{9,13},{10,... | collective-permute-start | bytes 552968 | tf_op jit(solution)/shard_map/ppermute | solution.py:66
  380.1 20.9 %collective-permute-start.49 = (bf16[8,24,2432]{2,1,0:T(8,128)(2,1)S(1)}, bf16[8,24,2432]{2,1,0:T(8,128)(2,1)S(1)}, u32[]{:S(2)}, u32[]{:S(2)}) collective-permute-start(bf16[8,24,2432]{2,1,0:T(8,128)(2,1)S(1)} %add_convert_fusion.2), channel_id=1, source_target_pairs={{0,16},{1,9},{2,18},{3,11},{4,20},{5,13},{6,22},{7,15},{8,24},{9,1... | collective-permute-start | bytes 2801672 | tf_op jit(solution)/shard_map/ppermute | solution.py:66
  386.1 14.9 %collective-permute-start.51 = (bf16[192,768]{1,0:T(8,128)(2,1)S(1)}, bf16[192,768]{1,0:T(8,128)(2,1)S(1)}, u32[]{:S(2)}, u32[]{:S(2)}) collective-permute-start(bf16[192,768]{1,0:T(8,128)(2,1)S(1)} %copy-done.29), channel_id=1, source_target_pairs={{0,4},{1,5},{2,6},{3,7},{4,0},{5,1},{6,2},{7,3},{8,12},{9,13},{10,... | collective-permute-start | bytes 884744 | tf_op jit(solution)/shard_map/ppermute | solution.py:72
  401.2 10.0 %collective-permute-start.52 = (bf16[4,24,2432]{2,1,0:T(8,128)(2,1)S(1)}, bf16[4,24,2432]{2,1,0:T(8,128)(2,1)S(1)}, u32[]{:S(2)}, u32[]{:S(2)}) collective-permute-start(bf16[4,24,2432]{2,1,0:T(8,128)(2,1)S(1)} %add_convert_fusion.5), channel_id=1, source_target_pairs={{0,8},{1,17},{2,10},{3,19},{4,12},{5,21},{6,14},{7,23},{8,0},{9,25... | collective-permute-start | bytes 1400840 | tf_op jit(solution)/shard_map/ppermute | solution.py:66
  402.4 8.7 %collective-permute-start.53 = (bf16[96,768]{1,0:T(8,128)(2,1)S(1)}, bf16[96,768]{1,0:T(8,128)(2,1)S(1)}, u32[]{:S(2)}, u32[]{:S(2)}) collective-permute-start(bf16[96,768]{1,0:T(8,128)(2,1)S(1)} %copy-done.45), channel_id=1, source_target_pairs={{0,4},{1,5},{2,6},{3,7},{4,0},{5,1},{6,2},{7,3},{8,12},{9,13},{10,... | collective-permute-start | bytes 442376 | tf_op jit(solution)/shard_map/ppermute | solution.py:72
  421.1 7.7 %collective-permute-start.55 = (bf16[1,24,2432]{2,1,0:T(8,128)(2,1)S(1)}, bf16[1,24,2432]{2,1,0:T(8,128)(2,1)S(1)}, u32[]{:S(2)}, u32[]{:S(2)}) collective-permute-start(bf16[1,24,2432]{2,1,0:T(8,128)(2,1)S(1)} %add_convert_fusion.10), channel_id=1, source_target_pairs={{0,4},{1,5},{2,6},{3,7},{4,0},{5,1},{6,2},{7,3},{8,12},{9,13},{10,... | collective-permute-start | bytes 350216 | tf_op jit(solution)/shard_map/ppermute | solution.py:66
  (80 other events, 833.3 us)

commit v7 on v5

--- a/solution.py
+++ b/solution.py
@@ -303,24 +303,33 @@
     allowed = qid_ref[...] == kid_ref[0]
     lane = lax.broadcasted_iota(jnp.int32, (BLOCK, 128), 1)
     zero = jnp.zeros((BLOCK, 128), BF16)
-    for pair in range(HEADS // 2):
-        queries = qkv_ref[:, pair * 128 : pair * 128 + 128]
-        keys = qkv_ref[:, D + pair * 128 : D + pair * 128 + 128]
-        values = qkv_ref[:, 2 * D + pair * 128 : 2 * D + pair * 128 + 128]
-        outs = []
-        for side in range(2):
-            mine = (lane < HDIM) if side == 0 else (lane >= HDIM)
-            scores = dot(queries, jnp.where(mine, keys, zero), ((1,), (1,))) * head_scale
-            scores = jnp.where(allowed, scores, masked_score)
-            top = jnp.max(scores, axis=1, keepdims=True)
-            grown = jnp.exp(scores - top)
-            total = jnp.sum(grown, axis=1, keepdims=True)
-            probs = (grown * (1.0 / total)).astype(BF16)
-            probs_ref[0, 2 * pair + side] = probs
-            outs.append(dot(probs, values))
-        context_ref[:, pair * 128 : pair * 128 + 128] = jnp.where(
-            lane < HDIM, outs[0], outs[1]
-        ).astype(BF16)
+
+    def at(pair, start=0):
+        return pl.ds(pl.multiple_of(start + pair * 128, 128), 128)
+
+    def some(step, carry):
+        for k in range(1):
+            pair = step * 1 + k
+            queries = qkv_ref[:, at(pair)]
+            keys = qkv_ref[:, at(pair, D)]
+            values = qkv_ref[:, at(pair, 2 * D)]
+            outs = []
+            for side in range(2):
+                mine = (lane < HDIM) if side == 0 else (lane >= HDIM)
+                scores = dot(queries, jnp.where(mine, keys, zero), ((1,), (1,))) * head_scale
+                scores = jnp.where(allowed, scores, masked_score)
+                top = jnp.max(scores, axis=1, keepdims=True)
+                grown = jnp.exp(scores - top)
+                total = jnp.sum(grown, axis=1, keepdims=True)
+                probs = (grown * (1.0 / total)).astype(BF16)
+                probs_ref[0, 2 * pair + side] = probs
+                outs.append(dot(probs, values))
+            context_ref[:, at(pair)] = jnp.where(
+                lane < HDIM, outs[0], outs[1]
+            ).astype(BF16)
+        return carry
+
+    lax.fori_loop(0, HEADS // 2 // 1, some, 0)
 
 
 def attention_more_kernel(qkv_ref, qid_ref, kid_ref, _, __, context_ref, probs_ref):
@@ -361,33 +370,42 @@
 def attention_back_kernel(qkv_ref, probs_ref, grad_ref, out_ref, sum_ref):
     lane = lax.broadcasted_iota(jnp.int32, (BLOCK, 128), 1)
     zero = jnp.zeros((BLOCK, 128), BF16)
-    for pair in range(HEADS // 2):
-        cols = slice(pair * 128, pair * 128 + 128)
-        queries = qkv_ref[:, pair * 128 : pair * 128 + 128]
-        keys = qkv_ref[:, D + pair * 128 : D + pair * 128 + 128]
-        values = qkv_ref[:, 2 * D + pair * 128 : 2 * D + pair * 128 + 128]
-        grad = grad_ref[:, cols]
-        d_q, d_k, d_v = [], [], []
-        for side in range(2):
-            mine = (lane < HDIM) if side == 0 else (lane >= HDIM)
-            low = probs_ref[0, 2 * pair + side]
-            d_probs = dot(jnp.where(mine, grad, zero), values, ((1,), (1,)))
-            d_v.append(dot(low, grad, ((0,), (0,))))
-            probs = low.astype(F32)
-            row_dot = jnp.sum(d_probs * probs, axis=1, keepdims=True)
-            d_scores = (probs * (d_probs - row_dot)).astype(BF16)
-            d_q.append(dot(d_scores, keys))
-            d_k.append(dot(d_scores, queries, ((0,), (0,))))
-        first = lane < HDIM
-        out_ref[:, pair * 128 : pair * 128 + 128] = (
-            jnp.where(first, d_q[0], d_q[1]) * head_scale
-        ).astype(BF16)
-        out_ref[:, D + pair * 128 : D + pair * 128 + 128] = (
-            jnp.where(first, d_k[0], d_k[1]) * head_scale
-        ).astype(BF16)
-        out_ref[:, 2 * D + pair * 128 : 2 * D + pair * 128 + 128] = jnp.where(
-            first, d_v[0], d_v[1]
-        ).astype(BF16)
+
+    def at(pair, start=0):
+        return pl.ds(pl.multiple_of(start + pair * 128, 128), 128)
+
+    def some(step, carry):
+        for k in range(1):
+            pair = step * 1 + k
+            cols = at(pair)
+            queries = qkv_ref[:, at(pair)]
+            keys = qkv_ref[:, at(pair, D)]
+            values = qkv_ref[:, at(pair, 2 * D)]
+            grad = grad_ref[:, cols]
+            d_q, d_k, d_v = [], [], []
+            for side in range(2):
+                mine = (lane < HDIM) if side == 0 else (lane >= HDIM)
+                low = probs_ref[0, 2 * pair + side]
+                d_probs = dot(jnp.where(mine, grad, zero), values, ((1,), (1,)))
+                d_v.append(dot(low, grad, ((0,), (0,))))
+                probs = low.astype(F32)
+                row_dot = jnp.sum(d_probs * probs, axis=1, keepdims=True)
+                d_scores = (probs * (d_probs - row_dot)).astype(BF16)
+                d_q.append(dot(d_scores, keys))
+                d_k.append(dot(d_scores, queries, ((0,), (0,))))
+            first = lane < HDIM
+            out_ref[:, at(pair)] = (
+                jnp.where(first, d_q[0], d_q[1]) * head_scale
+            ).astype(BF16)
+            out_ref[:, at(pair, D)] = (
+                jnp.where(first, d_k[0], d_k[1]) * head_scale
+            ).astype(BF16)
+            out_ref[:, at(pair, 2 * D)] = jnp.where(
+                first, d_v[0], d_v[1]
+            ).astype(BF16)
+        return carry
+
+    lax.fori_loop(0, HEADS // 2 // 1, some, 0)
     sums = jnp.sum(out_ref[...].astype(F32), axis=0, keepdims=True)
 
     @pl.when(pl.program_id(0) == 0)
@@ -642,6 +660,79 @@
         ),
         name="expand",
     )(mid_low, w_expand, b_expand, *into)
+
+
+def project_kernel(tokens_ref, w_ref, b_ref, out_ref):
+    out_ref[...] = (dot(tokens_ref[...], w_ref[...]) + b_ref[...]).astype(BF16)
+
+
+def project(tokens, weight, bias):
+    rows, width = tokens.shape[0], weight.shape[1]
+    return pl.pallas_call(
+        project_kernel,
+        grid=(rows // BLOCK,),
+        in_specs=[
+            pl.BlockSpec((BLOCK, D), lambda i: (i, 0)),
+            pl.BlockSpec((D, width), lambda i: (0, 0)),
+            pl.BlockSpec((1, width), lambda i: (0, 0)),
+        ],
+        out_specs=pl.BlockSpec((BLOCK, width), lambda i: (i, 0)),
+        out_shape=jax.ShapeDtypeStruct((rows, width), BF16),
+        compiler_params=pltpu.CompilerParams(vmem_limit_bytes=VMEM_LIMIT),
+        cost_estimate=pl.CostEstimate(
+            flops=2 * rows * D * width,
+            bytes_accessed=2 * (rows * (D + width) + D * width),
+            transcendentals=0,
+        ),
+        name="project",
+    )(tokens, weight, bias)
+
+
+def add_norm_kernel(
+    rows_of, left_ref, w_ref, base_ref, mask_ref, vec_ref, norm_ref, inverse_ref, low_ref, *more
+):
+    bias, gain, shift = (vec_ref[k : k + 1, :] for k in rows_of)
+    norm, inverse = normalized(base_ref[...].astype(F32) + dot(left_ref[...], w_ref[...]) + bias)
+    value = norm * gain + shift
+    norm_ref[...] = norm
+    inverse_ref[...] = inverse
+    if more:
+        more[0][...] = value
+        low_ref[...] = value.astype(BF16)
+    else:
+        low_ref[...] = (value * mask_ref[...]).astype(BF16)
+
+
+def add_norm(left, weight, base, mask, vec, rows_of, keep):
+    rows, depth = left.shape
+    wide = pl.BlockSpec((BLOCK, D), lambda i: (i, 0))
+    thin = pl.BlockSpec((BLOCK, 1), lambda i: (i, 0))
+    shape = jax.ShapeDtypeStruct((rows, D), F32)
+    return pl.pallas_call(
+        functools.partial(add_norm_kernel, rows_of),
+        grid=(rows // BLOCK,),
+        in_specs=[
+            pl.BlockSpec((BLOCK, depth), lambda i: (i, 0)),
+            pl.BlockSpec((depth, D), lambda i: (0, 0)),
+            wide,
+            thin,
+            pl.BlockSpec((8, D), lambda i: (0, 0)),
+        ],
+        out_specs=[wide, thin, wide] + [wide] * keep,
+        out_shape=[
+            shape,
+            jax.ShapeDtypeStruct((rows, 1), F32),
+            jax.ShapeDtypeStruct((rows, D), BF16),
+        ]
+        + [shape] * keep,
+        compiler_params=pltpu.CompilerParams(vmem_limit_bytes=VMEM_LIMIT),
+        cost_estimate=pl.CostEstimate(
+            flops=2 * rows * D * depth,
+            bytes_accessed=2 * (rows + D) * depth + 12 * rows * D,
+            transcendentals=0,
+        ),
+        name="add_norm",
+    )(left, weight, base, mask, vec)
 
 
 def normalized(values):
@@ -816,7 +907,7 @@
     bias_e = small[:, 8:12].reshape(1, FF)
     bias_j = jnp.concatenate([vec[0], jnp.zeros((D,), F32), vec[1]])
     tokens = join([my_tokens] + tokens_in)
-    qkv = (dot(tokens, wj) + bias_j).astype(BF16)
+    qkv = project(tokens, wj, bias_j[None])
 
     cot_out = chunked(send_cot, (3, 3, 3, 4, 3))
     by_pa = positive.reshape(places.pa_n, nq)
@@ -852,10 +943,9 @@
     cot_in = cot_in + hand(cot_out[2:3])
     (full_e,) = g2.whole([(0, FF)])
     we = full_e.reshape(D, FF)
-    attended = dot(context, wo) + vec[2]
-    norm_one, inverse_one = normalized(tokens.astype(F32) + attended)
-    mid = norm_one * vec[3] + vec[4]
-    mid_low = mid.astype(BF16)
+    norm_one, inverse_one, mid_low, mid = add_norm(
+        context, wo, tokens, row_mask, vec, (2, 3, 4), True
+    )
     mid_low, we, cot_in, cot_out = tie(mid_low, we, cot_in, cot_out)
     cot_in = cot_in + hand(cot_out[3:4])
     gelu = expand(mid_low, we, bias_e, 0, 1)
@@ -868,8 +958,7 @@
     active, g3.parts, cot_in = tie(active, g3.parts, cot_in)
     (full_r,) = g3.whole([(0, D)])
     wr = full_r.reshape(FF, D)
-    norm_two, inverse_two = normalized(mid + dot(active, wr) + vec[5])
-    out = ((norm_two * vec[6] + vec[7]) * row_mask).astype(BF16)
+    norm_two, inverse_two, out = add_norm(active, wr, mid, row_mask, vec, (5, 6, 7), False)
 
     firsts = out.reshape(per_q, lq, D)[:, 0, :]
     others = places.swap_tower(firsts)
@@ -929,7 +1018,7 @@
 
     class Scatter:
         def __init__(self, mine, theirs):
-            self.parts, self.theirs = [mine], theirs
+            self.parts, self.theirs, self.send = [mine], theirs, None
             self.count = mine.shape[0]
 
         def cores(self):
@@ -941,11 +1030,15 @@
                 out = out + part[start:stop].astype(F32)
             return out
 
+        def prepare(self):
+            self.send = self.total(self.count // 2, self.count).astype(BF16)
+
         def move(self, step):
-            half = self.count // 2
-            send = self.total(half, self.count).astype(BF16)
-            self.parts = self.parts + [places.swap(send, step)]
-            self.count = half
+            if self.send is None:
+                self.prepare()
+            self.parts = self.parts + [places.swap(self.send, step)]
+            self.send = None
+            self.count = self.count // 2
 
         def pb_first(self):
             self.move(places.steps - 1)
@@ -1000,13 +1093,23 @@
     d_context = dot(d_attended, wo, ((1,), (1,))).astype(BF16)
     d_joined, sums_one = attention_back(qkv, probs, d_context, later, blocks - later)
     sr.parts, se.parts, d_joined = tie(sr.parts, se.parts, d_joined)
+    se.prepare()
+    sr.prepare()
+    sr.send, sr.parts, se.send, se.parts, d_joined = tie(
+        sr.send, sr.parts, se.send, se.parts, d_joined
+    )
     se.pb_first()
     sr.along_z()
     send_grad = (d_first[own_rows:] + dot(d_joined[own_rows:], wj, ((1,), (1,)))).astype(BF16)
-    d_joined, send_grad = tie(d_joined, chunked(send_grad, (4, 4, 2, 6)))
+    d_joined, send_grad = tie(d_joined, chunked(send_grad, (4, 3, 2, 7)))
     got_grad = hand(send_grad[:1])
     d_joined, sums_two = attention_back(qkv, probs, d_context, 0, later, d_joined)
-    sr.parts, d_joined, got_grad, send_grad = tie(sr.parts, d_joined, got_grad, send_grad)
+    sr.parts, se.parts, d_joined, sums_two, got_grad, send_grad = tie(
+        sr.parts, se.parts, d_joined, sums_two, got_grad, send_grad
+    )
+    se.prepare()
+    se.send, se.parts, d_joined, send_grad = tie(se.send, se.parts, d_joined, send_grad)
+    se.pb_rest()
     sr.mid()
     got_grad = got_grad + hand(send_grad[1:2])
     g_joined_bias = (sums_one + sums_two)[0]
@@ -1024,25 +1127,24 @@
         [g_vec.T, g_bias_expand.reshape(D, 4), jnp.zeros((D, 116), F32)], axis=1
     )
     sj = Scatter(*(gradient if even else plain)(tokens, d_joined, extra=g_small))
-    se.parts, sj.parts, sj.theirs, d_joined, sr.out, got_grad, send_grad = tie(
-        se.parts, sj.parts, sj.theirs, d_joined, sr.out, got_grad, send_grad
+    se.parts, sj.parts, sj.theirs, d_joined, got_grad, send_grad = tie(
+        se.parts, sj.parts, sj.theirs, d_joined, got_grad, send_grad
     )
     sj.cores()
-    se.pb_rest()
+    se.along_z()
     got_grad = got_grad + hand(send_grad[2:3])
     own_grad = d_first[:own_rows] + dot(d_joined[:own_rows], wj, ((1,), (1,)))
     sj.parts, own_grad, got_grad, send_grad = tie(sj.parts, own_grad, got_grad, send_grad)
     sj.pb_first()
     got_grad = got_grad + hand(send_grad[3:])
     out_q, out_p = deal(tower.reshape(1), out, got_out)
-    sj.parts, se.parts, got_grad = tie(sj.parts, se.parts, got_grad)
-    se.along_z()
+    sj.parts, se.parts, out_q, out_p = tie(sj.parts, se.parts, out_q, out_p)
     sj.pb_rest()
+    se.mid()
+    sj.parts, se.out, sr.out, got_grad = tie(sj.parts, se.out, sr.out, got_grad)
+    sj.along_z()
     grad_q, grad_p = deal(tower.reshape(1), own_grad, got_grad)
-    sj.parts, se.parts, grad_q, grad_p = tie(sj.parts, se.parts, grad_q, grad_p)
-    sj.along_z()
-    se.mid()
-    sj.parts, se.out = tie(sj.parts, se.out)
+    sj.parts, grad_q, grad_p = tie(sj.parts, grad_q, grad_p)
     sj.mid()
     grad_joined = sj.out[:, :, : 3 * D]
     grad_expand, grad_output, grad_reduce = se.out[:, :, :FF], se.out[:, :, FF:], sr.out

time: 421 us -> 425 us (level); the launches traced: 414 us -> 423 us
  Pallas kernels: 143 us -> 189 us
  matrix products: 36 us -> 15.3 us
  waiting for transfers between devices: 103 us -> 87.9 us
    pallas_call x0 -> x3, Pallas kernels: none -> 27.2 us  [the longest x2 19.1 us: add_norm(): pl.pallas_call(functools.partial(add_norm_kernel, rows_of), grid=(rows //...]
    dot_general x9 -> x6, matrix products: 36 us -> 15.3 us  [dot(): lax.dot_general(left, right, (dims, ((), ())), preferred_element_type=F32)]
    pallas_call x2, Pallas kernels: 13.7 us -> 28.1 us  [attention(): pl.pallas_call(attention_more_kernel if into else attention_kernel, grid=...]
    ppermute x24, waiting for transfers between devices: 65.6 us -> 52.4 us  [swap(): return lax.ppermute(values, AXES, self.pairs(step))]
    pallas_call x2, Pallas kernels: 21.7 us -> 26.1 us  [attention_back(): pl.pallas_call(attention_back_more_kernel if more else attention_back_ker...]
    convert_element_type x11 -> x9, other arithmetic: 16.9 us -> 14.2 us  [prepare(): self.send = self.total(self.count // 2, self.count).astype(BF16)]
  transfers between devices with their start and end apart: 55 -> 55, of which waited for: 27 -> 19; matrix products, arithmetic and copies ran while one was open for 17% -> 15% of each run, Pallas kernels for 28% -> 38%
where the time goes in v7:
time: 425 us; the launch traced here: 423 us
  Pallas kernels  189 us (44%)
  waiting for transfers between devices  87.9 us (21%)
  starting transfers between devices  58.4 us (14%)
  other arithmetic  38.8 us (9%)
  local copies, waits for them, and re-layouts  31.9 us (8%)
  matrix products  15.3 us (4%)
    ppermute x24, waiting for transfers between devices, swap(): return lax.ppermute(values, AXES, self.pairs(step))  52.4 us
    pallas_call x2, Pallas kernels, attention(): pl.pallas_call(attention_more_kernel if into else attention_kernel, grid=...  28.1 us
    ppermute x24, starting transfers between devices, swap(): return lax.ppermute(values, AXES, self.pairs(step))  27.9 us
    ppermute x18, starting transfers between devices, swap_tower(): lax.ppermute(values, 'pa', [(i, i ^ 2 * self.half) for i in range(self.pa...  27.7 us
    ppermute x18, waiting for transfers between devices, swap_tower(): lax.ppermute(values, 'pa', [(i, i ^ 2 * self.half) for i in range(self.pa...  26.4 us
    pallas_call x2, Pallas kernels, attention_back(): pl.pallas_call(attention_back_more_kernel if more else attention_back_ker...  26.1 us
    pallas_call x3, Pallas kernels, weight_grad(): pl.pallas_call(functools.partial(weight_grad_kernel, chips, extra is not...  23.9 us
    pallas_call x2, Pallas kernels, add_norm(): pl.pallas_call(functools.partial(add_norm_kernel, rows_of), grid=(rows //...  19.1 us
  transfers between devices with their start and end apart: 55, of which 19 were waited for; matrix products, arithmetic and copies ran while one was open for 15% of the time, Pallas kernels for 38%

profile of v7, /device:TPU:0, one launch (start us, length us, event | category | flops | bytes accessed | tf_op | source)
XLA Modules:
  0.0 422.8 jit_solution(1638364699159679414)
XLA Ops:
  3.4 4.1 collective-permute-start
  11.2 3.6 collective-permute-done
  15.7 3.4 collective-permute-start.2
  20.2 8.4 %collective-permute-done.1 = bf16[2,24,3200]{2,1,0:T(8,128)(2,1)S(1)} collective-permute-done((bf16[2,24,3200]{2,1,0:T(8,128)(2,1)S(1)}, bf16[2,24,3200]{2,1,0:T(8,128)(2,1)S(1)}, u32[]{:S(2)}, u32[]{:S(2)}) %collective-permute-start.1) | collective-permute-done | bytes 307232 | tf_op jit(solution)/shard_map/ppermute | solution.py:66
  30.8 2.6 collective-permute-start.4
  33.3 6.6 %collective-permute-done.4 = bf16[1,24,3072]{2,1,0:T(8,128)(2,1)S(1)} collective-permute-done((bf16[1,24,3072]{2,1,0:T(8,128)(2,1)S(1)}, bf16[1,24,3072]{2,1,0:T(8,128)(2,1)S(1)}, u32[]{:S(2)}, u32[]{:S(2)}) %collective-permute-start.4) | collective-permute-done | bytes 147488 | tf_op jit(solution)/shard_map/ppermute | solution.py:66
  53.2 13.0 %collective-permute-done.7.refs_2_ = bf16[192,768]{1,0:T(8,128)(2,1)S(1)} collective-permute-done((bf16[192,768]{1,0:T(8,128)(2,1)}, bf16[192,768]{1,0:T(8,128)(2,1)S(1)}, u32[]{:S(2)}, u32[]{:S(2)}) %collective-permute-start.7) | collective-permute-done | bytes 294944 | tf_op jit(solution)/shard_map/ppermute | solution.py:72
  69.2 2.9 collective-permute-start.13
  72.3 5.0 %collective-permute-done.10 = bf16[4,24,3072]{2,1,0:T(8,128)(2,1)} collective-permute-done((bf16[4,24,3072]{2,1,0:T(8,128)(2,1)}, bf16[4,24,3072]{2,1,0:T(8,128)(2,1)}, u32[]{:S(2)}, u32[]{:S(2)}) %collective-permute-start.10) | collective-permute-done | bytes 589856 | tf_op jit(solution)/shard_map/ppermute | solution.py:66
  78.5 5.5 %assemble.3 = (bf16[16,2,24,2304]{3,2,1,0:T(8,128)(2,1)}, bf16[16,2,24,768]{3,2,1,0:T(8,128)(2,1)}, bf16[16,2,24,128]{3,2,1,0:T(8,128)(2,1)}) custom-call(s32[3,16]{1,0:T(4,128)} %get-tuple-element.602.idx_ref, bf16[8,24,3200]{2,1,0:T(8,128)(2,1)} %copy-done.1, bf16[8,24,3200]{2,1,0:T(8,128)(2,1)} %collective-permute-done.5.refs_1_, ...), custom_call_target="tpu_custom_call" | custom-call | bytes 9830400 | tf_op jit(solution)/shard_map/assemble/pallas_call | solution.py:118
  86.7 2.6 join.2.tokens_ref.base_ref.left_ref
  89.4 8.1 %project.1.qkv_ref = bf16[1024,2304]{1,0:T(8,128)(2,1)} custom-call(bf16[1024,768]{1,0:T(8,128)(2,1)} %join.2.tokens_ref.base_ref.left_ref, bf16[768,2304]{1,0:T(8,128)(2,1)} %bitcast.85, f32[1,2304]{1,0:T(1,128)} %broadcast_in_dim.16.b_ref), custom_call_target="tpu_custom_call" | custom-call | flops 3623878656 | bytes 9830400 | tf_op jit(solution)/shard_map/project/pallas_call | solution.py:671
  101.3 14.0 %attention.2 = (bf16[1024,768]{1,0:T(8,128)(2,1)}, bf16[4,12,256,256]{3,2,1,0:T(8,128)(2,1)}) custom-call(bf16[1024,2304]{1,0:T(8,128)(2,1)} %project.1.qkv_ref, s32[1024,1]{1,0:T(8,128)} %fusion.10.qid_ref, s32[4,1,256]{2,1,0:T(1,128)} %compare_select_fusion.kid_ref), custom_call_target="tpu_custom_call" | custom-call | flops 805306368 | bytes 6291456 | tf_op jit(solution)/shard_map/attention/pallas_call | solution.py:342
  117.5 2.3 collective-permute-start.20
  119.8 14.0 %attention.3 = (bf16[1024,768]{1,0:T(8,128)(2,1)}, bf16[4,12,256,256]{3,2,1,0:T(8,128)(2,1)}) custom-call(bf16[1024,2304]{1,0:T(8,128)(2,1)} %project.1.qkv_ref, s32[1024,1]{1,0:T(8,128)} %fusion.10.qid_ref, s32[4,1,256]{2,1,0:T(1,128)} %compare_select_fusion.kid_ref, ...), custom_call_target="tpu_custom_call", output_to_operand_aliasing={{0}: (3, {}), {1}: (4, {})} | custom-call | flops 805306368 | bytes 6291456 | tf_op jit(solution)/shard_map/attention/pallas_call | solution.py:342
  138.5 4.7 %assemble.4 = bf16[16,2,24,3072]{3,2,1,0:T(8,128)(2,1)} custom-call(s32[3,16]{1,0:T(4,128)} %get-tuple-element.602.idx_ref, bf16[8,24,3072]{2,1,0:T(8,128)(2,1)} %copy-done.2, bf16[8,24,3072]{2,1,0:T(8,128)(2,1)} %copy-done.10, bf16[8,24,3072]{2,1,0:T(8,128)(2,1)} %copy-done.12, bf16[8,24,3072]{2,1,0:T(8,128)(2,1)} %copy-done.13), custom_call_target="tpu_custom_call" | custom-call | bytes 9437184 | tf_op jit(solution)/shard_map/assemble/pallas_call | solution.py:118
  143.3 7.5 %add_norm.2 = (f32[1024,768]{1,0:T(8,128)}, f32[1024,1]{1,0:T(8,128)}, bf16[1024,768]{1,0:T(8,128)(2,1)}, f32[1024,768]{1,0:T(8,128)}) custom-call(bf16[1024,768]{1,0:T(8,128)(2,1)} %get-tuple-element.315.left_ref, bf16[768,768]{1,0:T(8,128)(2,1)} %bitcast.74, bf16[1024,768]{1,0:T(8,128)(2,1)} %join.2.tokens_ref.base_ref.left_ref, ...), custom_call_target="tpu_custom_call" | custom-call | flops 1207959552 | bytes 12189696 | tf_op jit(solution)/shard_map/add_norm/pallas_call | solution.py:711
  153.0 7.9 %expand.2 = (bf16[1024,3072]{1,0:T(8,128)(2,1)}, bf16[1024,3072]{1,0:T(8,128)(2,1)}) custom-call(bf16[1024,768]{1,0:T(8,128)(2,1)} %get-tuple-element.327.mid_ref.left_ref, bf16[768,3072]{1,0:T(8,128)(2,1)} %bitcast.64, f32[1,3072]{1,0:T(1,128)} %reshape.658.b_ref), custom_call_target="tpu_custom_call" | custom-call | flops 2415919104 | bytes 10223616 | tf_op jit(solution)/shard_map/expand/pallas_call | solution.py:640
  163.6 7.9 %expand.3 = (bf16[1024,3072]{1,0:T(8,128)(2,1)}, bf16[1024,3072]{1,0:T(8,128)(2,1)}) custom-call(bf16[1024,768]{1,0:T(8,128)(2,1)} %get-tuple-element.327.mid_ref.left_ref, bf16[768,3072]{1,0:T(8,128)(2,1)} %bitcast.65, f32[1,3072]{1,0:T(1,128)} %reshape.658.b_ref, ...), custom_call_target="tpu_custom_call", output_to_operand_aliasing={{0}: (3, {}), {1}: (4, {})} | custom-call | flops 2415919104 | bytes 10223616 | tf_op jit(solution)/shard_map/expand/pallas_call | solution.py:640
  174.0 4.7 %assemble.5 = bf16[16,2,96,768]{3,2,1,0:T(8,128)(2,1)} custom-call(s32[3,16]{1,0:T(4,128)} %get-tuple-element.602.idx_ref, bf16[8,96,768]{2,1,0:T(8,128)(2,1)} %copy-done.3, bf16[8,96,768]{2,1,0:T(8,128)(2,1)} %collective-permute-done.22.refs_1_, bf16[8,96,768]{2,1,0:T(8,128)(2,1)} %collective-permute-done.23.refs_2_, bf16[8,96,768]{2,1,0:T(8,128)(2,1)} %copy-done.11), custom_call_target="tpu_custom_call" | custom-call | bytes 9437184 | tf_op jit(solution)/shard_map/assemble/pallas_call | solution.py:118
  178.8 11.6 %add_norm.3 = (f32[1024,768]{1,0:T(8,128)}, f32[1024,1]{1,0:T(8,128)}, bf16[1024,768]{1,0:T(8,128)(2,1)}) custom-call(bf16[1024,3072]{1,0:T(8,128)(2,1)} %get-tuple-element.348.left_ref, bf16[3072,768]{1,0:T(8,128)(2,1)} %bitcast.67, f32[1024,768]{1,0:T(8,128)} %get-tuple-element.359.base_ref, f32[1024,1]{1,0:T(8,128)} %convert_element_type.293.mask_ref, ...), custom_call_target="tpu_custom_call" | custom-call | flops 4831838208 | bytes 20447232 | tf_op jit(solution)/shard_map/add_norm/pallas_call | solution.py:711
  192.9 3.3 collective-permute-done.27
  197.4 2.9 collective-permute-done.28
  203.1 2.6 join.3.cot_ref
  206.2 4.7 %collective-permute-done.30 = bf16[4,24,768]{2,1,0:T(8,128)(2,1)S(1)} collective-permute-done((bf16[4,24,768]{2,1,0:T(8,128)(2,1)S(1)}, bf16[4,24,768]{2,1,0:T(8,128)(2,1)S(1)}, u32[]{:S(2)}, u32[]{:S(2)}) %collective-permute-start.30) | collective-permute-done | bytes 147488 | tf_op jit(solution)/shard_map/ppermute | solution.py:975
  215.5 6.5 %second_back.1 = (f32[1024,768]{1,0:T(8,128)}, bf16[1024,768]{1,0:T(8,128)(2,1)}, f32[8,768]{1,0:T(8,128)}) custom-call(bf16[1024,768]{1,0:T(8,128)(2,1)} %join.3.cot_ref, f32[4,4,768]{2,1,0:T(4,128)} %reshape.666.slot_ref, f32[1024,1]{1,0:T(8,128)} %convert_element_type.293.mask_ref, f32[1024,768]{1,0:T(8,128)} %get-tuple-element.362.norm_ref, ...), custom_call_target="tpu_custom_call" | custom-call | flops 15728640 | bytes 9437184 | tf_op jit(solution)/shard_map/second_back/pallas_call | solution.py:558
  223.6 10.3 %tall_grad.1 = (bf16[16,96,768]{2,1,0:T(8,128)(2,1)}, bf16[16,96,768]{2,1,0:T(8,128)(2,1)}) custom-call(s32[3,16]{1,0:T(4,128)} %get-tuple-element.603.table_ref, bf16[1024,3072]{1,0:T(8,128)(2,1)} %get-tuple-element.348.left_ref, bf16[1024,768]{1,0:T(8,128)(2,1)} %get-tuple-element.374.right_ref.grad_ref), custom_call_target="tpu_custom_call" | custom-call | flops 4831838208 | bytes 12582912 | tf_op jit(solution)/shard_map/tall_grad/pallas_call | solution.py:230
  235.5 11.8 %hidden_grad.1 = (bf16[1024,3072]{1,0:T(8,128)(2,1)}, f32[1,3072]{1,0:T(1,128)}) custom-call(bf16[1024,768]{1,0:T(8,128)(2,1)} %get-tuple-element.374.right_ref.grad_ref, bf16[3072,768]{1,0:T(8,128)(2,1)} %bitcast.68, bf16[1024,3072]{1,0:T(8,128)(2,1)} %get-tuple-element.375.slope_ref), custom_call_target="tpu_custom_call" | custom-call | flops 4831838208 | bytes 18874368 | tf_op jit(solution)/shard_map/hidden_grad/pallas_call | solution.py:276
  249.9 9.9 %weight_grad.3 = (bf16[16,24,3840]{2,1,0:T(8,128)(2,1)}, bf16[16,24,3840]{2,1,0:T(8,128)(2,1)}) custom-call(s32[3,16]{1,0:T(4,128)} %get-tuple-element.603.table_ref, bf16[1024,768]{1,0:T(8,128)(2,1)} %get-tuple-element.327.mid_ref.left_ref, bf16[1024,3072]{1,0:T(8,128)(2,1)} %get-tuple-element.392.right_ref.hidden_ref), custom_call_target="tpu_custom_call" | custom-call | flops 4831838208 | bytes 12582912 | tf_op jit(solution)/shard_map/weight_grad/pallas_call | solution.py:188
  261.3 12.4 %first_back.1 = (f32[1024,768]{1,0:T(8,128)}, bf16[1024,768]{1,0:T(8,128)(2,1)}, f32[8,768]{1,0:T(8,128)}) custom-call(bf16[1024,3072]{1,0:T(8,128)(2,1)} %get-tuple-element.392.right_ref.hidden_ref, bf16[768,3072]{1,0:T(8,128)(2,1)} %bitcast.66, f32[1024,768]{1,0:T(8,128)} %get-tuple-element.393.second_ref, f32[1024,768]{1,0:T(8,128)} %get-tuple-element.394.norm_ref, ...), custom_call_target="tpu_custom_call" | custom-call | flops 4831838208 | bytes 22020096 | tf_op jit(solution)/shard_map/first_back/pallas_call | solution.py:598
  273.7 5.1 %weight_grad.4 = (bf16[16,24,3840]{2,1,0:T(8,128)(2,1)}, bf16[16,24,3840]{2,1,0:T(8,128)(2,1)}) custom-call(s32[3,16]{1,0:T(4,128)} %get-tuple-element.603.table_ref, bf16[1024,768]{1,0:T(8,128)(2,1)} %get-tuple-element.315.left_ref, bf16[1024,768]{1,0:T(8,128)(2,1)} %get-tuple-element.412.right_ref, ...), custom_call_target="tpu_custom_call", output_to_operand_aliasing={{0}: (3, {}), {1}: (4, {})} | custom-call | flops 1207959552 | bytes 4325376 | tf_op jit(solution)/shard_map/weight_grad/pallas_call | solution.py:188
  279.1 2.2 add_convert_fusion.5
  282.4 3.8 convolution_convert_fusion.grad_ref
  286.2 13.2 %attention_back.2 = (bf16[1024,2304]{1,0:T(8,128)(2,1)}, f32[1,2304]{1,0:T(1,128)}) custom-call(bf16[1024,2304]{1,0:T(8,128)(2,1)} %project.1.qkv_ref, bf16[4,12,256,256]{3,2,1,0:T(8,128)(2,1)} %get-tuple-element.411.probs_ref, bf16[1024,768]{1,0:T(8,128)(2,1)} %convolution_convert_fusion.grad_ref), custom_call_target="tpu_custom_call" | custom-call | flops 1610612736 | bytes 8650752 | tf_op jit(solution)/shard_map/attention_back/pallas_call | solution.py:427
  302.0 2.7 add_convert_fusion.8
  307.6 4.5 %add_convert_fusion.3 = bf16[512,768]{1,0:T(8,128)(2,1)S(1)} fusion(f32[1024,768]{1,0:T(8,128)} %get-tuple-element.430, bf16[768,2304]{1,0:T(8,128)(2,1)} %bitcast.86, bf16[1024,2304]{1,0:T(8,128)(2,1)S(1)} %copy-done.4), kind=kOutput, calls=%fused_computation.9 | convolution fusion | flops 1812725760 | bytes 8257536 | tf_op jit(solution)/shard_map/dot_general | solution.py:76
  321.3 13.0 %attention_back.3 = (bf16[1024,2304]{1,0:T(8,128)(2,1)}, f32[1,2304]{1,0:T(1,128)}) custom-call(bf16[1024,2304]{1,0:T(8,128)(2,1)} %project.1.qkv_ref, bf16[4,12,256,256]{3,2,1,0:T(8,128)(2,1)} %get-tuple-element.411.probs_ref, bf16[1024,768]{1,0:T(8,128)(2,1)} %convolution_convert_fusion.grad_ref, ...), custom_call_target="tpu_custom_call", output_to_operand_aliasing={{0}: (3, {})} | custom-call | flops 1610612736 | bytes 8650752 | tf_op jit(solution)/shard_map/attention_back/pallas_call | solution.py:427
  334.3 2.5 add_convert_fusion.4
  342.1 8.9 %weight_grad.5 = (bf16[16,24,2432]{2,1,0:T(8,128)(2,1)}, bf16[16,24,2432]{2,1,0:T(8,128)(2,1)}) custom-call(s32[3,16]{1,0:T(4,128)} %get-tuple-element.603.table_ref, bf16[1024,768]{1,0:T(8,128)(2,1)} %join.2.tokens_ref.base_ref.left_ref, bf16[1024,2304]{1,0:T(8,128)(2,1)} %get-tuple-element.463.right_ref, f32[768,128]{1,0:T(8,128)} %maximum_maximum_fusion.refs_0_), custom_call_target="tpu_custom_call" | custom-call | flops 3623878656 | bytes 9830400 | tf_op jit(solution)/shard_map/weight_grad/pallas_call | solution.py:188
  351.1 2.7 deal.2
  358.1 6.3 %slice_add_fusion.own_ref = f32[512,768]{1,0:T(8,128)} fusion(f32[1024,768]{1,0:T(8,128)} %get-tuple-element.430, bf16[768,2304]{1,0:T(8,128)(2,1)} %bitcast.87, bf16[1024,2304]{1,0:T(8,128)(2,1)} %get-tuple-element.463.right_ref), kind=kOutput, calls=%fused_computation.8 | convolution fusion | flops 1812332544 | bytes 9043968 | tf_op jit(solution)/shard_map/dot_general | solution.py:76
  364.4 5.2 %collective-permute-done.46.refs_2_ = bf16[64,768]{1,0:T(8,128)(2,1)S(1)} collective-permute-done((bf16[64,768]{1,0:T(8,128)(2,1)S(1)}, bf16[64,768]{1,0:T(8,128)(2,1)S(1)}, u32[]{:S(2)}, u32[]{:S(2)}) %collective-permute-start.46) | collective-permute-done | bytes 98336 | tf_op jit(solution)/shard_map/ppermute | solution.py:72
  375.7 2.4 collective-permute-start.52
  378.1 10.5 %collective-permute-done.48 = bf16[2,24,3840]{2,1,0:T(8,128)(2,1)S(1)} collective-permute-done((bf16[2,24,3840]{2,1,0:T(8,128)(2,1)S(1)}, bf16[2,24,3840]{2,1,0:T(8,128)(2,1)S(1)}, u32[]{:S(2)}, u32[]{:S(2)}) %collective-permute-start.48) | collective-permute-done | bytes 368672 | tf_op jit(solution)/shard_map/ppermute | solution.py:66
  392.4 9.3 %collective-permute-done.50 = bf16[1,24,3840]{2,1,0:T(8,128)(2,1)S(1)} collective-permute-done((bf16[1,24,3840]{2,1,0:T(8,128)(2,1)S(1)}, bf16[1,24,3840]{2,1,0:T(8,128)(2,1)S(1)}, u32[]{:S(2)}, u32[]{:S(2)}) %collective-permute-start.50) | collective-permute-done | bytes 184352 | tf_op jit(solution)/shard_map/ppermute | solution.py:66
  405.3 3.5 deal.3
  408.8 3.0 collective-permute-done.53
  415.0 4.6 %collective-permute-done.54 = bf16[1,24,2432]{2,1,0:T(8,128)(2,1)S(1)} collective-permute-done((bf16[1,24,2432]{2,1,0:T(8,128)(2,1)S(1)}, bf16[1,24,2432]{2,1,0:T(8,128)(2,1)S(1)}, u32[]{:S(2)}, u32[]{:S(2)}) %collective-permute-start.54) | collective-permute-done | bytes 116768 | tf_op jit(solution)/shard_map/ppermute | solution.py:66
  (354 shorter events, 112.2 us)
Async XLA Ops:
  3.4 11.4 %collective-permute-start = (bf16[1,24,3200]{2,1,0:T(8,128)(2,1)S(1)}, bf16[1,24,3200]{2,1,0:T(8,128)(2,1)S(1)}, u32[]{:S(2)}, u32[]{:S(2)}) collective-permute-start(bf16[1,24,3200]{2,1,0:T(8,128)(2,1)S(1)} %get-tuple-element.577), channel_id=1, source_target_pairs={{0,4},{1,5},{2,6},{3,7},{4,0},{5,1},{6,2},{7,3},{8,12},{9,13},{10,... | collective-permute-start | bytes 460808 | tf_op jit(solution)/shard_map/ppermute | solution.py:66
  14.9 13.8 %collective-permute-start.1 = (bf16[2,24,3200]{2,1,0:T(8,128)(2,1)S(1)}, bf16[2,24,3200]{2,1,0:T(8,128)(2,1)S(1)}, u32[]{:S(2)}, u32[]{:S(2)}) collective-permute-start(bf16[2,24,3200]{2,1,0:T(8,128)(2,1)S(1)} %pad_maximum_fusion.8), channel_id=1, source_target_pairs={{0,2},{1,3},{2,0},{3,1},{4,6},{5,7},{6,4},{7,5},{8,10},{9,11},{10,... | collective-permute-start | bytes 921608 | tf_op jit(solution)/shard_map/ppermute | solution.py:66
  15.7 13.1 %collective-permute-start.2 = (bf16[160,768]{1,0:T(8,128)(2,1)S(1)}, bf16[160,768]{1,0:T(8,128)(2,1)S(1)}, u32[]{:S(2)}, u32[]{:S(2)}) collective-permute-start(bf16[160,768]{1,0:T(8,128)(2,1)S(1)} %get-tuple-element.266), channel_id=1, source_target_pairs={{0,4},{1,5},{2,6},{3,7},{4,0},{5,1},{6,2},{7,3},{8,12},{9,13},{10,... | collective-permute-start | bytes 737288 | tf_op jit(solution)/shard_map/ppermute | solution.py:72
  29.5 11.2 %collective-permute-start.3 = (bf16[4,24,3200]{2,1,0:T(8,128)(2,1)S(1)}, bf16[4,24,3200]{2,1,0:T(8,128)(2,1)S(1)}, u32[]{:S(2)}, u32[]{:S(2)}) collective-permute-start(bf16[4,24,3200]{2,1,0:T(8,128)(2,1)S(1)} %pad_maximum_fusion.4), channel_id=1, source_target_pairs={{0,8},{1,17},{2,10},{3,19},{4,12},{5,21},{6,14},{7,23},{8,0},{9,25... | collective-permute-start | bytes 1843208 | tf_op jit(solution)/shard_map/ppermute | solution.py:66
  30.8 9.2 %collective-permute-start.4 = (bf16[1,24,3072]{2,1,0:T(8,128)(2,1)S(1)}, bf16[1,24,3072]{2,1,0:T(8,128)(2,1)S(1)}, u32[]{:S(2)}, u32[]{:S(2)}) collective-permute-start(bf16[1,24,3072]{2,1,0:T(8,128)(2,1)S(1)} %get-tuple-element.270), channel_id=1, source_target_pairs={{0,4},{1,5},{2,6},{3,7},{4,0},{5,1},{6,2},{7,3},{8,12},{9,13},{10,... | collective-permute-start | bytes 442376 | tf_op jit(solution)/shard_map/ppermute | solution.py:66
  40.9 25.3 %collective-permute-start.5 = (bf16[8,24,3200]{2,1,0:T(8,128)(2,1)S(1)}, bf16[8,24,3200]{2,1,0:T(8,128)(2,1)}, u32[]{:S(2)}, u32[]{:S(2)}) collective-permute-start(bf16[8,24,3200]{2,1,0:T(8,128)(2,1)S(1)} %pad_maximum_fusion.refs_0_), channel_id=1, source_target_pairs={{0,16},{1,9},{2,18},{3,11},{4,20},{5,13},{6,22},{7,15},{8,24},{9,1... | collective-permute-start | bytes 3686408 | tf_op jit(solution)/shard_map/ppermute | solution.py:66
  44.6 7.7 %collective-permute-start.6 = (bf16[2,24,3072]{2,1,0:T(8,128)(2,1)}, bf16[2,24,3072]{2,1,0:T(8,128)(2,1)S(1)}, u32[]{:S(2)}, u32[]{:S(2)}) collective-permute-start(bf16[2,24,3072]{2,1,0:T(8,128)(2,1)} %pad_maximum_fusion.9), channel_id=1, source_target_pairs={{0,2},{1,3},{2,0},{3,1},{4,6},{5,7},{6,4},{7,5},{8,10},{9,11},{10,... | collective-permute-start | bytes 884744 | tf_op jit(solution)/shard_map/ppermute | solution.py:66
  49.3 29.1 %collective-permute-start.8 = (bf16[8,24,3200]{2,1,0:T(8,128)(2,1)S(1)}, bf16[8,24,3200]{2,1,0:T(8,128)(2,1)}, u32[]{:S(2)}, u32[]{:S(2)}) collective-permute-start(bf16[8,24,3200]{2,1,0:T(8,128)(2,1)S(1)} %pad_maximum_fusion.refs_0_), channel_id=1, source_target_pairs={{0,1},{1,0},{2,3},{3,2},{4,5},{5,4},{6,7},{7,6},{8,9},{9,8},{10,11... | collective-permute-start | bytes 3686408 | tf_op jit(solution)/shard_map/ppermute | solution.py:69
  49.3 16.8 %collective-permute-start.7 = (bf16[192,768]{1,0:T(8,128)(2,1)}, bf16[192,768]{1,0:T(8,128)(2,1)S(1)}, u32[]{:S(2)}, u32[]{:S(2)}) collective-permute-start(bf16[192,768]{1,0:T(8,128)(2,1)} %slice.441), channel_id=1, source_target_pairs={{0,4},{1,5},{2,6},{3,7},{4,0},{5,1},{6,2},{7,3},{8,12},{9,13},{10,... | collective-permute-start | bytes 884744 | tf_op jit(solution)/shard_map/ppermute | solution.py:72
  66.2 12.3 %collective-permute-start.9 = (bf16[8,24,3200]{2,1,0:T(8,128)(2,1)}, bf16[8,24,3200]{2,1,0:T(8,128)(2,1)}, u32[]{:S(2)}, u32[]{:S(2)}) collective-permute-start(bf16[8,24,3200]{2,1,0:T(8,128)(2,1)} %collective-permute-done.5.refs_1_), channel_id=1, source_target_pairs={{0,1},{1,0},{2,3},{3,2},{4,5},{5,4},{6,7},{7,6},{8,9},{9,8},{10,11... | collective-permute-start | bytes 3686408 | tf_op jit(solution)/shard_map/ppermute | solution.py:69
  67.1 10.2 %collective-permute-start.10 = (bf16[4,24,3072]{2,1,0:T(8,128)(2,1)}, bf16[4,24,3072]{2,1,0:T(8,128)(2,1)}, u32[]{:S(2)}, u32[]{:S(2)}) collective-permute-start(bf16[4,24,3072]{2,1,0:T(8,128)(2,1)} %pad_maximum_fusion.5), channel_id=1, source_target_pairs={{0,8},{1,17},{2,10},{3,19},{4,12},{5,21},{6,14},{7,23},{8,0},{9,25... | collective-permute-start | bytes 1769480 | tf_op jit(solution)/shard_map/ppermute | solution.py:66
  68.3 15.8 %collective-permute-start.11 = (bf16[160,768]{1,0:T(8,128)(2,1)}, bf16[160,768]{1,0:T(8,128)(2,1)}, u32[]{:S(2)}, u32[]{:S(2)}) collective-permute-start(bf16[160,768]{1,0:T(8,128)(2,1)} %get-tuple-element.285), channel_id=1, source_target_pairs={{0,4},{1,5},{2,6},{3,7},{4,0},{5,1},{6,2},{7,3},{8,12},{9,13},{10,... | collective-permute-start | bytes 737288 | tf_op jit(solution)/shard_map/ppermute | solution.py:72
  69.2 30.6 %collective-permute-start.13 = (s32[512]{0:T(512)}, s32[512]{0:T(512)S(1)}, u32[]{:S(2)}, u32[]{:S(2)}) collective-permute-start(s32[512]{0:T(512)} %get-tuple-element.593), channel_id=1, source_target_pairs={{0,4},{1,5},{2,6},{3,7},{4,0},{5,1},{6,2},{7,3},{8,12},{9,13},{10,... | collective-permute-start | bytes 6152 | tf_op jit(solution)/shard_map/ppermute | solution.py:72
  85.1 30.3 %collective-permute-start.14 = (bf16[8,24,3072]{2,1,0:T(8,128)(2,1)S(1)}, bf16[8,24,3072]{2,1,0:T(8,128)(2,1)S(1)}, u32[]{:S(2)}, u32[]{:S(2)}) collective-permute-start(bf16[8,24,3072]{2,1,0:T(8,128)(2,1)S(1)} %pad_maximum_fusion.1.refs_0_), channel_id=1, source_target_pairs={{0,16},{1,9},{2,18},{3,11},{4,20},{5,13},{6,22},{7,15},{8,24},{9,1... | collective-permute-start | bytes 3538952 | tf_op jit(solution)/shard_map/ppermute | solution.py:66
  86.7 10.8 %collective-permute-start.12 = (bf16[1,96,768]{2,1,0:T(8,128)(2,1)S(1)}, bf16[1,96,768]{2,1,0:T(8,128)(2,1)S(1)}, u32[]{:S(2)}, u32[]{:S(2)}) collective-permute-start(bf16[1,96,768]{2,1,0:T(8,128)(2,1)S(1)} %copy-done.44), channel_id=1, source_target_pairs={{0,4},{1,5},{2,6},{3,7},{4,0},{5,1},{6,2},{7,3},{8,12},{9,13},{10,... | collective-permute-start | bytes 442376 | tf_op jit(solution)/shard_map/ppermute | solution.py:66
  97.5 17.8 %collective-permute-start.15 = (bf16[2,96,768]{2,1,0:T(8,128)(2,1)S(1)}, bf16[2,96,768]{2,1,0:T(8,128)(2,1)S(1)}, u32[]{:S(2)}, u32[]{:S(2)}) collective-permute-start(bf16[2,96,768]{2,1,0:T(8,128)(2,1)S(1)} %pad_maximum_fusion.10), channel_id=1, source_target_pairs={{0,2},{1,3},{2,0},{3,1},{4,6},{5,7},{6,4},{7,5},{8,10},{9,11},{10,... | collective-permute-start | bytes 884744 | tf_op jit(solution)/shard_map/ppermute | solution.py:66
  100.4 33.6 %collective-permute-start.17 = (bf16[8,24,3072]{2,1,0:T(8,128)(2,1)S(1)}, bf16[8,24,3072]{2,1,0:T(8,128)(2,1)S(1)}, u32[]{:S(2)}, u32[]{:S(2)}) collective-permute-start(bf16[8,24,3072]{2,1,0:T(8,128)(2,1)S(1)} %pad_maximum_fusion.1.refs_0_), channel_id=1, source_target_pairs={{0,1},{1,0},{2,3},{3,2},{4,5},{5,4},{6,7},{7,6},{8,9},{9,8},{10,11... | collective-permute-start | bytes 3538952 | tf_op jit(solution)/shard_map/ppermute | solution.py:69
  100.4 15.0 %collective-permute-start.16 = (bf16[96,768]{1,0:T(8,128)(2,1)S(1)}, bf16[96,768]{1,0:T(8,128)(2,1)S(1)}, u32[]{:S(2)}, u32[]{:S(2)}) collective-permute-start(bf16[96,768]{1,0:T(8,128)(2,1)S(1)} %copy-done.42), channel_id=1, source_target_pairs={{0,4},{1,5},{2,6},{3,7},{4,0},{5,1},{6,2},{7,3},{8,12},{9,13},{10,... | collective-permute-start | bytes 442376 | tf_op jit(solution)/shard_map/ppermute | solution.py:72
  116.1 18.0 %collective-permute-start.18 = (bf16[8,24,3072]{2,1,0:T(8,128)(2,1)S(1)}, bf16[8,24,3072]{2,1,0:T(8,128)(2,1)S(1)}, u32[]{:S(2)}, u32[]{:S(2)}) collective-permute-start(bf16[8,24,3072]{2,1,0:T(8,128)(2,1)S(1)} %collective-permute-done.14.refs_1_), channel_id=1, source_target_pairs={{0,1},{1,0},{2,3},{3,2},{4,5},{5,4},{6,7},{7,6},{8,9},{9,8},{10,11... | collective-permute-start | bytes 3538952 | tf_op jit(solution)/shard_map/ppermute | solution.py:69
  116.2 17.6 %collective-permute-start.19 = (bf16[4,96,768]{2,1,0:T(8,128)(2,1)S(1)}, bf16[4,96,768]{2,1,0:T(8,128)(2,1)S(1)}, u32[]{:S(2)}, u32[]{:S(2)}) collective-permute-start(bf16[4,96,768]{2,1,0:T(8,128)(2,1)S(1)} %pad_maximum_fusion.6), channel_id=1, source_target_pairs={{0,8},{1,17},{2,10},{3,19},{4,12},{5,21},{6,14},{7,23},{8,0},{9,25... | collective-permute-start | bytes 1769480 | tf_op jit(solution)/shard_map/ppermute | solution.py:66
  117.5 16.5 %collective-permute-start.20 = (bf16[96,768]{1,0:T(8,128)(2,1)}, bf16[96,768]{1,0:T(8,128)(2,1)S(1)}, u32[]{:S(2)}, u32[]{:S(2)}) collective-permute-start(bf16[96,768]{1,0:T(8,128)(2,1)} %get-tuple-element.311), channel_id=1, source_target_pairs={{0,4},{1,5},{2,6},{3,7},{4,0},{5,1},{6,2},{7,3},{8,12},{9,13},{10,... | collective-permute-start | bytes 442376 | tf_op jit(solution)/shard_map/ppermute | solution.py:72
  134.0 29.0 %collective-permute-start.22 = (bf16[8,96,768]{2,1,0:T(8,128)(2,1)S(1)}, bf16[8,96,768]{2,1,0:T(8,128)(2,1)}, u32[]{:S(2)}, u32[]{:S(2)}) collective-permute-start(bf16[8,96,768]{2,1,0:T(8,128)(2,1)S(1)} %pad_maximum_fusion.2.refs_0_), channel_id=1, source_target_pairs={{0,16},{1,9},{2,18},{3,11},{4,20},{5,13},{6,22},{7,15},{8,24},{9,1... | collective-permute-start | bytes 3538952 | tf_op jit(solution)/shard_map/ppermute | solution.py:66
  135.7 27.4 %collective-permute-start.23 = (bf16[8,96,768]{2,1,0:T(8,128)(2,1)S(1)}, bf16[8,96,768]{2,1,0:T(8,128)(2,1)}, u32[]{:S(2)}, u32[]{:S(2)}) collective-permute-start(bf16[8,96,768]{2,1,0:T(8,128)(2,1)S(1)} %pad_maximum_fusion.2.refs_0_), channel_id=1, source_target_pairs={{0,1},{1,0},{2,3},{3,2},{4,5},{5,4},{6,7},{7,6},{8,9},{9,8},{10,11... | collective-permute-start | bytes 3538952 | tf_op jit(solution)/shard_map/ppermute | solution.py:69
  135.7 15.1 %collective-permute-start.21 = (bf16[96,768]{1,0:T(8,128)(2,1)}, bf16[96,768]{1,0:T(8,128)(2,1)S(1)}, u32[]{:S(2)}, u32[]{:S(2)}) collective-permute-start(bf16[96,768]{1,0:T(8,128)(2,1)} %get-tuple-element.324), channel_id=1, source_target_pairs={{0,4},{1,5},{2,6},{3,7},{4,0},{5,1},{6,2},{7,3},{8,12},{9,13},{10,... | collective-permute-start | bytes 442376 | tf_op jit(solution)/shard_map/ppermute | solution.py:72
  150.8 12.2 %collective-permute-start.24 = (bf16[128,768]{1,0:T(8,128)(2,1)S(1)}, bf16[128,768]{1,0:T(8,128)(2,1)S(1)}, u32[]{:S(2)}, u32[]{:S(2)}) collective-permute-start(bf16[128,768]{1,0:T(8,128)(2,1)S(1)} %copy-done.35), channel_id=1, source_target_pairs={{0,4},{1,5},{2,6},{3,7},{4,0},{5,1},{6,2},{7,3},{8,12},{9,13},{10,... | collective-permute-start | bytes 589832 | tf_op jit(solution)/shard_map/ppermute | solution.py:72
  163.0 10.0 %collective-permute-start.25 = (bf16[8,96,768]{2,1,0:T(8,128)(2,1)}, bf16[8,96,768]{2,1,0:T(8,128)(2,1)S(1)}, u32[]{:S(2)}, u32[]{:S(2)}) collective-permute-start(bf16[8,96,768]{2,1,0:T(8,128)(2,1)} %collective-permute-done.22.refs_1_), channel_id=1, source_target_pairs={{0,1},{1,0},{2,3},{3,2},{4,5},{5,4},{6,7},{7,6},{8,9},{9,8},{10,11... | collective-permute-start | bytes 3538952 | tf_op jit(solution)/shard_map/ppermute | solution.py:69
  163.5 9.5 %collective-permute-start.26 = (bf16[96,768]{1,0:T(8,128)(2,1)S(1)}, bf16[96,768]{1,0:T(8,128)(2,1)S(1)}, u32[]{:S(2)}, u32[]{:S(2)}) collective-permute-start(bf16[96,768]{1,0:T(8,128)(2,1)S(1)} %copy-done.37), channel_id=1, source_target_pairs={{0,4},{1,5},{2,6},{3,7},{4,0},{5,1},{6,2},{7,3},{8,12},{9,13},{10,... | collective-permute-start | bytes 442376 | tf_op jit(solution)/shard_map/ppermute | solution.py:72
  222.0 12.1 %collective-permute-start.32 = (bf16[128,768]{1,0:T(8,128)(2,1)S(1)}, bf16[128,768]{1,0:T(8,128)(2,1)S(1)}, u32[]{:S(2)}, u32[]{:S(2)}) collective-permute-start(bf16[128,768]{1,0:T(8,128)(2,1)S(1)} %get-tuple-element.368), channel_id=1, source_target_pairs={{0,4},{1,5},{2,6},{3,7},{4,0},{5,1},{6,2},{7,3},{8,12},{9,13},{10,... | collective-permute-start | bytes 589832 | tf_op jit(solution)/shard_map/ppermute | solution.py:72
  234.1 13.2 %collective-permute-start.33 = (bf16[16,96,768]{2,1,0:T(8,128)(2,1)}, bf16[16,96,768]{2,1,0:T(8,128)(2,1)S(1)}, u32[]{:S(2)}, u32[]{:S(2)}) collective-permute-start(bf16[16,96,768]{2,1,0:T(8,128)(2,1)} %get-tuple-element.373), channel_id=1, source_target_pairs={{0,1},{1,0},{2,3},{3,2},{4,5},{5,4},{6,7},{7,6},{8,9},{9,8},{10,11... | collective-permute-start | bytes 7077896 | tf_op jit(solution)/shard_map/ppermute | solution.py:69
  234.1 13.1 %collective-permute-start.34 = (bf16[128,768]{1,0:T(8,128)(2,1)S(1)}, bf16[128,768]{1,0:T(8,128)(2,1)S(1)}, u32[]{:S(2)}, u32[]{:S(2)}) collective-permute-start(bf16[128,768]{1,0:T(8,128)(2,1)S(1)} %copy-done.34), channel_id=1, source_target_pairs={{0,4},{1,5},{2,6},{3,7},{4,0},{5,1},{6,2},{7,3},{8,12},{9,13},{10,... | collective-permute-start | bytes 589832 | tf_op jit(solution)/shard_map/ppermute | solution.py:72
  248.0 25.7 %collective-permute-start.35 = (bf16[8,96,768]{2,1,0:T(8,128)(2,1)S(1)}, bf16[8,96,768]{2,1,0:T(8,128)(2,1)S(1)}, u32[]{:S(2)}, u32[]{:S(2)}) collective-permute-start(bf16[8,96,768]{2,1,0:T(8,128)(2,1)S(1)} %add_convert_fusion.1), channel_id=1, source_target_pairs={{0,16},{1,9},{2,18},{3,11},{4,20},{5,13},{6,22},{7,15},{8,24},{9,1... | collective-permute-start | bytes 3538952 | tf_op jit(solution)/shard_map/ppermute | solution.py:66
  248.3 12.7 %collective-permute-start.36 = (bf16[128,768]{1,0:T(8,128)(2,1)S(1)}, bf16[128,768]{1,0:T(8,128)(2,1)S(1)}, u32[]{:S(2)}, u32[]{:S(2)}) collective-permute-start(bf16[128,768]{1,0:T(8,128)(2,1)S(1)} %get-tuple-element.388), channel_id=1, source_target_pairs={{0,4},{1,5},{2,6},{3,7},{4,0},{5,1},{6,2},{7,3},{8,12},{9,13},{10,... | collective-permute-start | bytes 589832 | tf_op jit(solution)/shard_map/ppermute | solution.py:72
  261.1 12.6 %collective-permute-start.37 = (bf16[128,768]{1,0:T(8,128)(2,1)S(1)}, bf16[128,768]{1,0:T(8,128)(2,1)S(1)}, u32[]{:S(2)}, u32[]{:S(2)}) collective-permute-start(bf16[128,768]{1,0:T(8,128)(2,1)S(1)} %copy-done.33), channel_id=1, source_target_pairs={{0,4},{1,5},{2,6},{3,7},{4,0},{5,1},{6,2},{7,3},{8,12},{9,13},{10,... | collective-permute-start | bytes 589832 | tf_op jit(solution)/shard_map/ppermute | solution.py:72
  278.8 20.7 %collective-permute-start.39 = (bf16[16,24,3840]{2,1,0:T(8,128)(2,1)}, bf16[16,24,3840]{2,1,0:T(8,128)(2,1)S(1)}, u32[]{:S(2)}, u32[]{:S(2)}) collective-permute-start(bf16[16,24,3840]{2,1,0:T(8,128)(2,1)} %get-tuple-element.410), channel_id=1, source_target_pairs={{0,1},{1,0},{2,3},{3,2},{4,5},{5,4},{6,7},{7,6},{8,9},{9,8},{10,11... | collective-permute-start | bytes 8847368 | tf_op jit(solution)/shard_map/ppermute | solution.py:69
  281.3 18.1 %collective-permute-start.38 = (bf16[4,96,768]{2,1,0:T(8,128)(2,1)}, bf16[4,96,768]{2,1,0:T(8,128)(2,1)S(1)}, u32[]{:S(2)}, u32[]{:S(2)}) collective-permute-start(bf16[4,96,768]{2,1,0:T(8,128)(2,1)} %add_convert_fusion.5), channel_id=1, source_target_pairs={{0,8},{1,17},{2,10},{3,19},{4,12},{5,21},{6,14},{7,23},{8,0},{9,25... | collective-permute-start | bytes 1769480 | tf_op jit(solution)/shard_map/ppermute | solution.py:66
  304.7 29.7 %collective-permute-start.41 = (bf16[8,24,3840]{2,1,0:T(8,128)(2,1)}, bf16[8,24,3840]{2,1,0:T(8,128)(2,1)}, u32[]{:S(2)}, u32[]{:S(2)}) collective-permute-start(bf16[8,24,3840]{2,1,0:T(8,128)(2,1)} %add_convert_fusion), channel_id=1, source_target_pairs={{0,16},{1,9},{2,18},{3,11},{4,20},{5,13},{6,22},{7,15},{8,24},{9,1... | collective-permute-start | bytes 4423688 | tf_op jit(solution)/shard_map/ppermute | solution.py:66
  306.3 28.0 %collective-permute-start.40 = (bf16[2,96,768]{2,1,0:T(8,128)(2,1)}, bf16[2,96,768]{2,1,0:T(8,128)(2,1)}, u32[]{:S(2)}, u32[]{:S(2)}) collective-permute-start(bf16[2,96,768]{2,1,0:T(8,128)(2,1)} %add_convert_fusion.8), channel_id=1, source_target_pairs={{0,2},{1,3},{2,0},{3,1},{4,6},{5,7},{6,4},{7,5},{8,10},{9,11},{10,... | collective-permute-start | bytes 884744 | tf_op jit(solution)/shard_map/ppermute | solution.py:66
  314.9 19.4 %collective-permute-start.42 = (bf16[128,768]{1,0:T(8,128)(2,1)}, bf16[128,768]{1,0:T(8,128)(2,1)}, u32[]{:S(2)}, u32[]{:S(2)}) collective-permute-start(bf16[128,768]{1,0:T(8,128)(2,1)} %slice.457), channel_id=1, source_target_pairs={{0,4},{1,5},{2,6},{3,7},{4,0},{5,1},{6,2},{7,3},{8,12},{9,13},{10,... | collective-permute-start | bytes 589832 | tf_op jit(solution)/shard_map/ppermute | solution.py:72
  336.8 14.2 %collective-permute-start.43 = (bf16[4,24,3840]{2,1,0:T(8,128)(2,1)}, bf16[4,24,3840]{2,1,0:T(8,128)(2,1)}, u32[]{:S(2)}, u32[]{:S(2)}) collective-permute-start(bf16[4,24,3840]{2,1,0:T(8,128)(2,1)} %add_convert_fusion.4), channel_id=1, source_target_pairs={{0,8},{1,17},{2,10},{3,19},{4,12},{5,21},{6,14},{7,23},{8,0},{9,25... | collective-permute-start | bytes 2211848 | tf_op jit(solution)/shard_map/ppermute | solution.py:66
  338.6 12.4 %collective-permute-start.44 = (bf16[96,768]{1,0:T(8,128)(2,1)}, bf16[96,768]{1,0:T(8,128)(2,1)S(1)}, u32[]{:S(2)}, u32[]{:S(2)}) collective-permute-start(bf16[96,768]{1,0:T(8,128)(2,1)} %slice.458), channel_id=1, source_target_pairs={{0,4},{1,5},{2,6},{3,7},{4,0},{5,1},{6,2},{7,3},{8,12},{9,13},{10,... | collective-permute-start | bytes 442376 | tf_op jit(solution)/shard_map/ppermute | solution.py:72
  351.0 18.6 %collective-permute-start.45 = (bf16[16,24,2432]{2,1,0:T(8,128)(2,1)}, bf16[16,24,2432]{2,1,0:T(8,128)(2,1)}, u32[]{:S(2)}, u32[]{:S(2)}) collective-permute-start(bf16[16,24,2432]{2,1,0:T(8,128)(2,1)} %get-tuple-element.462), channel_id=1, source_target_pairs={{0,1},{1,0},{2,3},{3,2},{4,5},{5,4},{6,7},{7,6},{8,9},{9,8},{10,11... | collective-permute-start | bytes 5603336 | tf_op jit(solution)/shard_map/ppermute | solution.py:69
  355.1 18.5 %collective-permute-start.51 = (bf16[1,96,768]{2,1,0:T(8,128)(2,1)S(1)}, bf16[1,96,768]{2,1,0:T(8,128)(2,1)S(1)}, u32[]{:S(2)}, u32[]{:S(2)}) collective-permute-start(bf16[1,96,768]{2,1,0:T(8,128)(2,1)S(1)} %add_convert_fusion.11), channel_id=1, source_target_pairs={{0,4},{1,5},{2,6},{3,7},{4,0},{5,1},{6,2},{7,3},{8,12},{9,13},{10,... | collective-permute-start | bytes 442376 | tf_op jit(solution)/shard_map/ppermute | solution.py:66
  356.4 13.2 %collective-permute-start.46 = (bf16[64,768]{1,0:T(8,128)(2,1)S(1)}, bf16[64,768]{1,0:T(8,128)(2,1)S(1)}, u32[]{:S(2)}, u32[]{:S(2)}) collective-permute-start(bf16[64,768]{1,0:T(8,128)(2,1)S(1)} %copy-done.46), channel_id=1, source_target_pairs={{0,4},{1,5},{2,6},{3,7},{4,0},{5,1},{6,2},{7,3},{8,12},{9,13},{10,... | collective-permute-start | bytes 294920 | tf_op jit(solution)/shard_map/ppermute | solution.py:72
  371.1 17.6 %collective-permute-start.47 = (bf16[8,24,2432]{2,1,0:T(8,128)(2,1)S(1)}, bf16[8,24,2432]{2,1,0:T(8,128)(2,1)S(1)}, u32[]{:S(2)}, u32[]{:S(2)}) collective-permute-start(bf16[8,24,2432]{2,1,0:T(8,128)(2,1)S(1)} %add_convert_fusion.2), channel_id=1, source_target_pairs={{0,16},{1,9},{2,18},{3,11},{4,20},{5,13},{6,22},{7,15},{8,24},{9,1... | collective-permute-start | bytes 2801672 | tf_op jit(solution)/shard_map/ppermute | solution.py:66
  373.5 15.2 %collective-permute-start.48 = (bf16[2,24,3840]{2,1,0:T(8,128)(2,1)S(1)}, bf16[2,24,3840]{2,1,0:T(8,128)(2,1)S(1)}, u32[]{:S(2)}, u32[]{:S(2)}) collective-permute-start(bf16[2,24,3840]{2,1,0:T(8,128)(2,1)S(1)} %add_convert_fusion.7), channel_id=1, source_target_pairs={{0,2},{1,3},{2,0},{3,1},{4,6},{5,7},{6,4},{7,5},{8,10},{9,11},{10,... | collective-permute-start | bytes 1105928 | tf_op jit(solution)/shard_map/ppermute | solution.py:66
  375.7 27.4 %collective-permute-start.52 = (bf16[224,768]{1,0:T(8,128)(2,1)S(1)}, bf16[224,768]{1,0:T(8,128)(2,1)S(1)}, u32[]{:S(2)}, u32[]{:S(2)}) collective-permute-start(bf16[224,768]{1,0:T(8,128)(2,1)S(1)} %copy-done.23), channel_id=1, source_target_pairs={{0,4},{1,5},{2,6},{3,7},{4,0},{5,1},{6,2},{7,3},{8,12},{9,13},{10,... | collective-permute-start | bytes 1032200 | tf_op jit(solution)/shard_map/ppermute | solution.py:72
  389.9 11.9 %collective-permute-start.50 = (bf16[1,24,3840]{2,1,0:T(8,128)(2,1)S(1)}, bf16[1,24,3840]{2,1,0:T(8,128)(2,1)S(1)}, u32[]{:S(2)}, u32[]{:S(2)}) collective-permute-start(bf16[1,24,3840]{2,1,0:T(8,128)(2,1)S(1)} %add_convert_fusion.10), channel_id=1, source_target_pairs={{0,4},{1,5},{2,6},{3,7},{4,0},{5,1},{6,2},{7,3},{8,12},{9,13},{10,... | collective-permute-start | bytes 552968 | tf_op jit(solution)/shard_map/ppermute | solution.py:66
  391.5 11.6 %collective-permute-start.49 = (bf16[4,24,2432]{2,1,0:T(8,128)(2,1)S(1)}, bf16[4,24,2432]{2,1,0:T(8,128)(2,1)S(1)}, u32[]{:S(2)}, u32[]{:S(2)}) collective-permute-start(bf16[4,24,2432]{2,1,0:T(8,128)(2,1)S(1)} %add_convert_fusion.6), channel_id=1, source_target_pairs={{0,8},{1,17},{2,10},{3,19},{4,12},{5,21},{6,14},{7,23},{8,0},{9,25... | collective-permute-start | bytes 1400840 | tf_op jit(solution)/shard_map/ppermute | solution.py:66
  (71 other events, 570.3 us)

commit v8 on v7

--- a/solution.py
+++ b/solution.py
@@ -303,68 +303,53 @@
     allowed = qid_ref[...] == kid_ref[0]
     lane = lax.broadcasted_iota(jnp.int32, (BLOCK, 128), 1)
     zero = jnp.zeros((BLOCK, 128), BF16)
-
-    def at(pair, start=0):
-        return pl.ds(pl.multiple_of(start + pair * 128, 128), 128)
-
-    def some(step, carry):
-        for k in range(1):
-            pair = step * 1 + k
-            queries = qkv_ref[:, at(pair)]
-            keys = qkv_ref[:, at(pair, D)]
-            values = qkv_ref[:, at(pair, 2 * D)]
-            outs = []
-            for side in range(2):
-                mine = (lane < HDIM) if side == 0 else (lane >= HDIM)
-                scores = dot(queries, jnp.where(mine, keys, zero), ((1,), (1,))) * head_scale
-                scores = jnp.where(allowed, scores, masked_score)
-                top = jnp.max(scores, axis=1, keepdims=True)
-                grown = jnp.exp(scores - top)
-                total = jnp.sum(grown, axis=1, keepdims=True)
-                probs = (grown * (1.0 / total)).astype(BF16)
-                probs_ref[0, 2 * pair + side] = probs
-                outs.append(dot(probs, values))
-            context_ref[:, at(pair)] = jnp.where(
-                lane < HDIM, outs[0], outs[1]
-            ).astype(BF16)
-        return carry
-
-    lax.fori_loop(0, HEADS // 2 // 1, some, 0)
-
-
-def attention_more_kernel(qkv_ref, qid_ref, kid_ref, _, __, context_ref, probs_ref):
-    attention_kernel(qkv_ref, qid_ref, kid_ref, context_ref, probs_ref)
-
-
-def attention(qkv, qid, kid, start, count, into=()):
+    for pair in range(HEADS // 2):
+        queries = qkv_ref[:, pair * 128 : pair * 128 + 128]
+        keys = qkv_ref[:, D + pair * 128 : D + pair * 128 + 128]
+        values = qkv_ref[:, 2 * D + pair * 128 : 2 * D + pair * 128 + 128]
+        outs = []
+        for side in range(2):
+            mine = (lane < HDIM) if side == 0 else (lane >= HDIM)
+            scores = dot(queries, jnp.where(mine, keys, zero), ((1,), (1,))) * head_scale
+            scores = jnp.where(allowed, scores, masked_score)
+            top = jnp.max(scores, axis=1, keepdims=True)
+            grown = jnp.exp(scores - top)
+            total = jnp.sum(grown, axis=1, keepdims=True)
+            probs = (grown * (1.0 / total)).astype(BF16)
+            probs_ref[0, 2 * pair + side] = probs
+            outs.append(dot(probs, values))
+        context_ref[:, pair * 128 : pair * 128 + 128] = jnp.where(
+            lane < HDIM, outs[0], outs[1]
+        ).astype(BF16)
+
+
+def attention(qkv, qid, kid):
     rows = qkv.shape[0]
     blocks = rows // BLOCK
     return pl.pallas_call(
-        attention_more_kernel if into else attention_kernel,
-        grid=(count,),
+        attention_kernel,
+        grid=(blocks,),
         in_specs=[
-            pl.BlockSpec((BLOCK, 3 * D), lambda i: (i + start, 0)),
-            pl.BlockSpec((BLOCK, 1), lambda i: (i + start, 0)),
-            pl.BlockSpec((1, 1, BLOCK), lambda i: (i + start, 0, 0)),
-        ]
-        + [pl.BlockSpec(memory_space=pl.ANY)] * len(into),
+            pl.BlockSpec((BLOCK, 3 * D), lambda i: (i, 0)),
+            pl.BlockSpec((BLOCK, 1), lambda i: (i, 0)),
+            pl.BlockSpec((1, 1, BLOCK), lambda i: (i, 0, 0)),
+        ],
         out_specs=[
-            pl.BlockSpec((BLOCK, D), lambda i: (i + start, 0)),
-            pl.BlockSpec((1, HEADS, BLOCK, BLOCK), lambda i: (i + start, 0, 0, 0)),
-        ],
-        input_output_aliases={3: 0, 4: 1} if into else {},
+            pl.BlockSpec((BLOCK, D), lambda i: (i, 0)),
+            pl.BlockSpec((1, HEADS, BLOCK, BLOCK), lambda i: (i, 0, 0, 0)),
+        ],
         out_shape=[
             jax.ShapeDtypeStruct((rows, D), BF16),
             jax.ShapeDtypeStruct((blocks, HEADS, BLOCK, BLOCK), BF16),
         ],
         compiler_params=pltpu.CompilerParams(vmem_limit_bytes=VMEM_LIMIT),
         cost_estimate=pl.CostEstimate(
-            flops=4 * count * BLOCK * BLOCK * D * 2,
-            bytes_accessed=count * BLOCK * (4 * D + HEADS * BLOCK) * 2,
-            transcendentals=count * BLOCK * HEADS * BLOCK,
+            flops=4 * rows * BLOCK * D * 2,
+            bytes_accessed=rows * (4 * D + HEADS * BLOCK) * 2,
+            transcendentals=rows * HEADS * BLOCK,
         ),
         name="attention",
-    )(qkv, qid, kid, *into)
+    )(qkv, qid, kid)
 
 
 def attention_back_kernel(qkv_ref, probs_ref, grad_ref, out_ref, sum_ref):
@@ -375,8 +360,8 @@
         return pl.ds(pl.multiple_of(start + pair * 128, 128), 128)
 
     def some(step, carry):
-        for k in range(1):
-            pair = step * 1 + k
+        for k in range(2):
+            pair = step * 2 + k
             cols = at(pair)
             queries = qkv_ref[:, at(pair)]
             keys = qkv_ref[:, at(pair, D)]
@@ -405,7 +390,7 @@
             ).astype(BF16)
         return carry
 
-    lax.fori_loop(0, HEADS // 2 // 1, some, 0)
+    lax.fori_loop(0, HEADS // 2 // 2, some, 0)
     sums = jnp.sum(out_ref[...].astype(F32), axis=0, keepdims=True)
 
     @pl.when(pl.program_id(0) == 0)
@@ -660,6 +645,45 @@
         ),
         name="expand",
     )(mid_low, w_expand, b_expand, *into)
+
+
+def token_grad_kernel(grad_ref, w_ref, first_ref, *outs):
+    block = first_ref[...] + dot(grad_ref[...], w_ref[...], ((1,), (1,)))
+    block = block.astype(outs[0].dtype)
+    step, start = pl.program_id(0), 0
+    for out in outs:
+        stop = start + out.shape[0]
+        for k in range(start // BLOCK, (stop - 1) // BLOCK + 1):
+            low, high = max(start, k * BLOCK), min(stop, (k + 1) * BLOCK)
+
+            @pl.when(step == k)
+            def _(out=out, k=k, low=low, high=high, start=start):
+                out[low - start : high - start, :] = block[low - k * BLOCK : high - k * BLOCK]
+
+        start = stop
+
+
+def token_grad(d_joined, weight, d_first, start, pieces, dtype):
+    width = weight.shape[1]
+    first, count = start // BLOCK, sum(pieces) // BLOCK
+    return pl.pallas_call(
+        token_grad_kernel,
+        grid=(count,),
+        in_specs=[
+            pl.BlockSpec((BLOCK, width), lambda i: (i + first, 0)),
+            pl.BlockSpec((D, width), lambda i: (0, 0)),
+            pl.BlockSpec((BLOCK, D), lambda i: (i + first, 0)),
+        ],
+        out_specs=[pl.BlockSpec((n, D), lambda i: (0, 0)) for n in pieces],
+        out_shape=[jax.ShapeDtypeStruct((n, D), dtype) for n in pieces],
+        compiler_params=pltpu.CompilerParams(vmem_limit_bytes=VMEM_LIMIT),
+        cost_estimate=pl.CostEstimate(
+            flops=2 * count * BLOCK * D * width,
+            bytes_accessed=2 * D * width + count * BLOCK * (2 * width + 6 * D),
+            transcendentals=0,
+        ),
+        name="token_grad",
+    )(d_joined, weight, d_first)
 
 
 def project_kernel(tokens_ref, w_ref, b_ref, out_ref):
@@ -909,7 +933,7 @@
     tokens = join([my_tokens] + tokens_in)
     qkv = project(tokens, wj, bias_j[None])
 
-    cot_out = chunked(send_cot, (3, 3, 3, 4, 3))
+    cot_out = chunked(send_cot, (4, 5, 4, 3))
     by_pa = positive.reshape(places.pa_n, nq)
     pair = [lax.dynamic_index_in_dim(by_pa, low_pa + k, 0, keepdims=False) for k in (0, shift)]
     pair = jnp.concatenate(pair)[None]
@@ -930,30 +954,28 @@
     qkv, g3.send, cot_out = tie(qkv, g3.send, cot_out)
     g3.along_z()
     cot_in = hand(cot_out[:1])
-    spread = attention(qkv, qid, kid, 0, later)
-    spread, g2.held, g3.send, cot_in, cot_out = tie(spread, g2.held, g3.send, cot_in, cot_out)
+    context, probs = attention(qkv, qid, kid)
+    context, g2.held, g3.send, cot_in, cot_out = tie(context, g2.held, g3.send, cot_in, cot_out)
     g2.core_held()
     g3.pb_first()
-    cot_in = cot_in + hand(cot_out[1:2])
-    context, probs = attention(qkv, qid, kid, later, blocks - later, tuple(spread))
-    context, g2.parts, g3.stack, cot_in, cot_out = tie(context, g2.parts, g3.stack, cot_in, cot_out)
+    norm_one, inverse_one, mid_low, mid = add_norm(
+        context, wo, tokens, row_mask, vec, (2, 3, 4), True
+    )
+    mid_low, g2.parts, g3.stack, cot_out = tie(mid_low, g2.parts, g3.stack, cot_out)
     g3.send = g3.stack
     g3.pb_last()
     g3.core_stack()
-    cot_in = cot_in + hand(cot_out[2:3])
+    cot_in = cot_in + hand(cot_out[1:2])
     (full_e,) = g2.whole([(0, FF)])
     we = full_e.reshape(D, FF)
-    norm_one, inverse_one, mid_low, mid = add_norm(
-        context, wo, tokens, row_mask, vec, (2, 3, 4), True
-    )
     mid_low, we, cot_in, cot_out = tie(mid_low, we, cot_in, cot_out)
-    cot_in = cot_in + hand(cot_out[3:4])
+    cot_in = cot_in + hand(cot_out[2:3])
     gelu = expand(mid_low, we, bias_e, 0, 1)
     gelu, g3.held, g3.other, g3.stack, cot_in, cot_out = tie(
         gelu, g3.held, g3.other, g3.stack, cot_in, cot_out
     )
     g3.core_held()
-    cot_in = cot_in + hand(cot_out[4:])
+    cot_in = cot_in + hand(cot_out[3:])
     active, slope = expand(mid_low, we, bias_e, 1, 1, tuple(gelu))
     active, g3.parts, cot_in = tie(active, g3.parts, cot_in)
     (full_r,) = g3.whole([(0, D)])
@@ -1100,8 +1122,9 @@
     )
     se.pb_first()
     sr.along_z()
-    send_grad = (d_first[own_rows:] + dot(d_joined[own_rows:], wj, ((1,), (1,)))).astype(BF16)
-    d_joined, send_grad = tie(d_joined, chunked(send_grad, (4, 3, 2, 7)))
+    part = own_rows // 16
+    send_grad = token_grad(d_joined, wj, d_first, own_rows, [5 * part] * 3 + [part], BF16)
+    d_joined, send_grad = tie(d_joined, send_grad)
     got_grad = hand(send_grad[:1])
     d_joined, sums_two = attention_back(qkv, probs, d_context, 0, later, d_joined)
     sr.parts, se.parts, d_joined, sums_two, got_grad, send_grad = tie(
@@ -1132,19 +1155,21 @@
     )
     sj.cores()
     se.along_z()
+    (own_grad,) = token_grad(d_joined, wj, d_first, 0, [own_rows], F32)
+    sj.parts, own_grad, send_grad = tie(sj.parts, own_grad, send_grad)
+    sj.pb_first()
     got_grad = got_grad + hand(send_grad[2:3])
-    own_grad = d_first[:own_rows] + dot(d_joined[:own_rows], wj, ((1,), (1,)))
-    sj.parts, own_grad, got_grad, send_grad = tie(sj.parts, own_grad, got_grad, send_grad)
-    sj.pb_first()
+    sj.parts, se.parts, got_grad, send_grad = tie(sj.parts, se.parts, got_grad, send_grad)
+    sj.pb_rest()
+    se.mid()
+    sj.parts, se.out, sr.out, got_out, out, send_grad = tie(
+        sj.parts, se.out, sr.out, got_out, out, send_grad
+    )
+    sj.along_z()
     got_grad = got_grad + hand(send_grad[3:])
     out_q, out_p = deal(tower.reshape(1), out, got_out)
-    sj.parts, se.parts, out_q, out_p = tie(sj.parts, se.parts, out_q, out_p)
-    sj.pb_rest()
-    se.mid()
-    sj.parts, se.out, sr.out, got_grad = tie(sj.parts, se.out, sr.out, got_grad)
-    sj.along_z()
+    sj.parts, out_q, out_p, got_grad = tie(sj.parts, out_q, out_p, got_grad)
     grad_q, grad_p = deal(tower.reshape(1), own_grad, got_grad)
-    sj.parts, grad_q, grad_p = tie(sj.parts, grad_q, grad_p)
     sj.mid()
     grad_joined = sj.out[:, :, : 3 * D]
     grad_expand, grad_output, grad_reduce = se.out[:, :, :FF], se.out[:, :, FF:], sr.out

time: 425 us -> 400 us (0.941)
  matrix products: 15.3 us -> 4.48 us
  Pallas kernels: 189 us -> 181 us
  local copies, waits for them, and re-layouts: 31.9 us -> 26.3 us
  waiting for transfers between devices: 87.9 us -> 82.4 us
    dot_general x6 -> x4, matrix products: 15.3 us -> 4.48 us  [dot(): lax.dot_general(left, right, (dims, ((), ())), preferred_element_type=F32)]
    ppermute x24, waiting for transfers between devices: 52.4 us -> 43.6 us  [swap(): return lax.ppermute(values, AXES, self.pairs(step))]
    ppermute x24, starting transfers between devices: 27.9 us -> 33.9 us  [swap(): return lax.ppermute(values, AXES, self.pairs(step))]
    pallas_call x2 -> x3, Pallas kernels: 28.1 us -> 23.3 us  [the longest x2 12.7 us: token_grad(): pl.pallas_call(token_grad_kernel, grid=(count,), in_specs=[pl.BlockSpec((...]
    ppermute x18 -> x17, waiting for transfers between devices: 26.4 us -> 29.9 us  [swap_tower(): lax.ppermute(values, 'pa', [(i, i ^ 2 * self.half) for i in range(self.pa...]
    ppermute x18 -> x17, starting transfers between devices: 27.7 us -> 24.4 us  [swap_tower(): lax.ppermute(values, 'pa', [(i, i ^ 2 * self.half) for i in range(self.pa...]
  transfers between devices with their start and end apart: 55 -> 54, of which waited for: 19 -> 21; matrix products, arithmetic and copies ran while one was open for 15% -> 12% of each run, Pallas kernels for 38% -> 39%
where the time goes in v8:
time: 400 us; the launch traced here: 397 us
  Pallas kernels  181 us (45%)
  waiting for transfers between devices  82.4 us (21%)
  starting transfers between devices  61.6 us (15%)
  other arithmetic  39.8 us (10%)
  local copies, waits for them, and re-layouts  26.3 us (7%)
  matrix products  4.48 us (1%)
    ppermute x24, waiting for transfers between devices, swap(): return lax.ppermute(values, AXES, self.pairs(step))  43.6 us
    ppermute x24, starting transfers between devices, swap(): return lax.ppermute(values, AXES, self.pairs(step))  33.9 us
    ppermute x17, waiting for transfers between devices, swap_tower(): lax.ppermute(values, 'pa', [(i, i ^ 2 * self.half) for i in range(self.pa...  29.9 us
    ppermute x17, starting transfers between devices, swap_tower(): lax.ppermute(values, 'pa', [(i, i ^ 2 * self.half) for i in range(self.pa...  24.4 us
    pallas_call x3, Pallas kernels, weight_grad(): pl.pallas_call(functools.partial(weight_grad_kernel, chips, extra is not...  23.9 us
    pallas_call x2, Pallas kernels, attention_back(): pl.pallas_call(attention_back_more_kernel if more else attention_back_ker...  23.6 us
    pallas_call x2, Pallas kernels, add_norm(): pl.pallas_call(functools.partial(add_norm_kernel, rows_of), grid=(rows //...  19 us
    pallas_call x2, Pallas kernels, expand(): pl.pallas_call(expand_more_kernel if into else expand_kernel, grid=(count...  16 us
  transfers between devices with their start and end apart: 54, of which 21 were waited for; matrix products, arithmetic and copies ran while one was open for 12% of the time, Pallas kernels for 39%

profile of v8, /device:TPU:0, one launch (start us, length us, event | category | flops | bytes accessed | tf_op | source)
XLA Modules:
  0.0 397.5 jit_solution(10390170726752820736)
XLA Ops:
  3.4 4.1 %collective-permute-start = (bf16[1,24,3200]{2,1,0:T(8,128)(2,1)S(1)}, bf16[1,24,3200]{2,1,0:T(8,128)(2,1)S(1)}, u32[]{:S(2)}, u32[]{:S(2)}) collective-permute-start(bf16[1,24,3200]{2,1,0:T(8,128)(2,1)S(1)} %get-tuple-element.575), channel_id=1, source_target_pairs={{0,4},{1,5},{2,6},{3,7},{4,0},{5,1},{6,2},{7,3},{8,12},{9,13},{10,... | collective-permute-start | bytes 460808 | tf_op jit(solution)/shard_map/ppermute | solution.py:66
  11.2 3.6 collective-permute-done
  15.7 3.4 collective-permute-start.2
  20.2 8.4 %collective-permute-done.1 = bf16[2,24,3200]{2,1,0:T(8,128)(2,1)S(1)} collective-permute-done((bf16[2,24,3200]{2,1,0:T(8,128)(2,1)S(1)}, bf16[2,24,3200]{2,1,0:T(8,128)(2,1)S(1)}, u32[]{:S(2)}, u32[]{:S(2)}) %collective-permute-start.1) | collective-permute-done | bytes 307232 | tf_op jit(solution)/shard_map/ppermute | solution.py:66
  30.8 2.6 collective-permute-start.4
  33.3 6.6 %collective-permute-done.4 = bf16[1,24,3072]{2,1,0:T(8,128)(2,1)S(1)} collective-permute-done((bf16[1,24,3072]{2,1,0:T(8,128)(2,1)S(1)}, bf16[1,24,3072]{2,1,0:T(8,128)(2,1)S(1)}, u32[]{:S(2)}, u32[]{:S(2)}) %collective-permute-start.4) | collective-permute-done | bytes 147488 | tf_op jit(solution)/shard_map/ppermute | solution.py:66
  53.2 13.2 %collective-permute-done.7.refs_2_ = bf16[192,768]{1,0:T(8,128)(2,1)S(1)} collective-permute-done((bf16[192,768]{1,0:T(8,128)(2,1)S(1)}, bf16[192,768]{1,0:T(8,128)(2,1)S(1)}, u32[]{:S(2)}, u32[]{:S(2)}) %collective-permute-start.7) | collective-permute-done | bytes 294944 | tf_op jit(solution)/shard_map/ppermute | solution.py:72
  69.6 2.9 collective-permute-start.13
  72.6 4.9 %collective-permute-done.10 = bf16[4,24,3072]{2,1,0:T(8,128)(2,1)} collective-permute-done((bf16[4,24,3072]{2,1,0:T(8,128)(2,1)}, bf16[4,24,3072]{2,1,0:T(8,128)(2,1)}, u32[]{:S(2)}, u32[]{:S(2)}) %collective-permute-start.10) | collective-permute-done | bytes 589856 | tf_op jit(solution)/shard_map/ppermute | solution.py:66
  78.7 5.5 %assemble.3 = (bf16[16,2,24,2304]{3,2,1,0:T(8,128)(2,1)}, bf16[16,2,24,768]{3,2,1,0:T(8,128)(2,1)}, bf16[16,2,24,128]{3,2,1,0:T(8,128)(2,1)}) custom-call(s32[3,16]{1,0:T(4,128)} %get-tuple-element.600.idx_ref, bf16[8,24,3200]{2,1,0:T(8,128)(2,1)} %copy-done.1, bf16[8,24,3200]{2,1,0:T(8,128)(2,1)} %collective-permute-done.5.refs_1_, ...), custom_call_target="tpu_custom_call" | custom-call | bytes 9830400 | tf_op jit(solution)/shard_map/assemble/pallas_call | solution.py:118
  87.2 2.6 join.2.tokens_ref.base_ref.left_ref
  89.8 8.1 %project.1.qkv_ref = bf16[1024,2304]{1,0:T(8,128)(2,1)} custom-call(bf16[1024,768]{1,0:T(8,128)(2,1)} %join.2.tokens_ref.base_ref.left_ref, bf16[768,2304]{1,0:T(8,128)(2,1)} %bitcast.65, f32[1,2304]{1,0:T(1,128)} %broadcast_in_dim.16.b_ref), custom_call_target="tpu_custom_call" | custom-call | flops 3623878656 | bytes 9830400 | tf_op jit(solution)/shard_map/project/pallas_call | solution.py:695
  98.0 2.2 collective-permute-start.15
  101.7 10.6 %attention.1 = (bf16[1024,768]{1,0:T(8,128)(2,1)}, bf16[4,12,256,256]{3,2,1,0:T(8,128)(2,1)}) custom-call(bf16[1024,2304]{1,0:T(8,128)(2,1)} %project.1.qkv_ref, s32[1024,1]{1,0:T(8,128)} %fusion.2.qid_ref, s32[4,1,256]{2,1,0:T(1,128)} %compare_select_fusion.kid_ref), custom_call_target="tpu_custom_call" | custom-call | flops 1610612736 | bytes 12582912 | tf_op jit(solution)/shard_map/attention/pallas_call | solution.py:329
  112.7 2.2 collective-permute-start.19
  115.9 7.4 %add_norm.2 = (f32[1024,768]{1,0:T(8,128)}, f32[1024,1]{1,0:T(8,128)}, bf16[1024,768]{1,0:T(8,128)(2,1)}, f32[1024,768]{1,0:T(8,128)}) custom-call(bf16[1024,768]{1,0:T(8,128)(2,1)} %get-tuple-element.303.left_ref, bf16[768,768]{1,0:T(8,128)(2,1)} %bitcast.75, bf16[1024,768]{1,0:T(8,128)(2,1)} %join.2.tokens_ref.base_ref.left_ref, ...), custom_call_target="tpu_custom_call" | custom-call | flops 1207959552 | bytes 12189696 | tf_op jit(solution)/shard_map/add_norm/pallas_call | solution.py:735
  128.6 4.8 %assemble.4 = bf16[16,2,24,3072]{3,2,1,0:T(8,128)(2,1)} custom-call(s32[3,16]{1,0:T(4,128)} %get-tuple-element.600.idx_ref, bf16[8,24,3072]{2,1,0:T(8,128)(2,1)} %copy-done.2, bf16[8,24,3072]{2,1,0:T(8,128)(2,1)} %collective-permute-done.14.refs_1_, bf16[8,24,3072]{2,1,0:T(8,128)(2,1)} %collective-permute-done.17.refs_2_, ...), custom_call_target="tpu_custom_call" | custom-call | bytes 9437184 | tf_op jit(solution)/shard_map/assemble/pallas_call | solution.py:118
  133.5 7.4 %collective-permute-done.20.refs_2_ = bf16[160,768]{1,0:T(8,128)(2,1)S(1)} collective-permute-done((bf16[160,768]{1,0:T(8,128)(2,1)}, bf16[160,768]{1,0:T(8,128)(2,1)S(1)}, u32[]{:S(2)}, u32[]{:S(2)}) %collective-permute-start.20) | collective-permute-done | bytes 245792 | tf_op jit(solution)/shard_map/ppermute | solution.py:72
  141.0 8.0 %expand.2 = (bf16[1024,3072]{1,0:T(8,128)(2,1)}, bf16[1024,3072]{1,0:T(8,128)(2,1)}) custom-call(bf16[1024,768]{1,0:T(8,128)(2,1)} %get-tuple-element.320.mid_ref.left_ref, bf16[768,3072]{1,0:T(8,128)(2,1)} %bitcast.62, f32[1,3072]{1,0:T(1,128)} %reshape.658.b_ref), custom_call_target="tpu_custom_call" | custom-call | flops 2415919104 | bytes 10223616 | tf_op jit(solution)/shard_map/expand/pallas_call | solution.py:625
  149.0 3.3 collective-permute-done.23.refs_3_
  152.9 7.9 %expand.3 = (bf16[1024,3072]{1,0:T(8,128)(2,1)}, bf16[1024,3072]{1,0:T(8,128)(2,1)}) custom-call(bf16[1024,768]{1,0:T(8,128)(2,1)} %get-tuple-element.320.mid_ref.left_ref, bf16[768,3072]{1,0:T(8,128)(2,1)} %bitcast.63, f32[1,3072]{1,0:T(1,128)} %reshape.658.b_ref, ...), custom_call_target="tpu_custom_call", output_to_operand_aliasing={{0}: (3, {}), {1}: (4, {})} | custom-call | flops 2415919104 | bytes 10223616 | tf_op jit(solution)/shard_map/expand/pallas_call | solution.py:625
  163.1 4.7 %assemble.5 = bf16[16,2,96,768]{3,2,1,0:T(8,128)(2,1)} custom-call(s32[3,16]{1,0:T(4,128)} %get-tuple-element.600.idx_ref, bf16[8,96,768]{2,1,0:T(8,128)(2,1)} %copy-done.3, bf16[8,96,768]{2,1,0:T(8,128)(2,1)} %collective-permute-done.21.refs_1_, bf16[8,96,768]{2,1,0:T(8,128)(2,1)} %collective-permute-done.22.refs_2_, bf16[8,96,768]{2,1,0:T(8,128)(2,1)} %copy-done.9), custom_call_target="tpu_custom_call" | custom-call | bytes 9437184 | tf_op jit(solution)/shard_map/assemble/pallas_call | solution.py:118
  167.8 11.6 %add_norm.3 = (f32[1024,768]{1,0:T(8,128)}, f32[1024,1]{1,0:T(8,128)}, bf16[1024,768]{1,0:T(8,128)(2,1)}) custom-call(bf16[1024,3072]{1,0:T(8,128)(2,1)} %get-tuple-element.339.left_ref, bf16[3072,768]{1,0:T(8,128)(2,1)} %bitcast.68, f32[1024,768]{1,0:T(8,128)} %get-tuple-element.349.base_ref, f32[1024,1]{1,0:T(8,128)} %convert_element_type.290.mask_ref, ...), custom_call_target="tpu_custom_call" | custom-call | flops 4831838208 | bytes 20447232 | tf_op jit(solution)/shard_map/add_norm/pallas_call | solution.py:735
  182.2 2.9 collective-permute-done.26
  186.3 2.9 collective-permute-done.27
  192.6 2.6 join.3.cot_ref
  196.0 4.4 %collective-permute-done.29 = bf16[4,24,768]{2,1,0:T(8,128)(2,1)S(1)} collective-permute-done((bf16[4,24,768]{2,1,0:T(8,128)(2,1)S(1)}, bf16[4,24,768]{2,1,0:T(8,128)(2,1)S(1)}, u32[]{:S(2)}, u32[]{:S(2)}) %collective-permute-start.29) | collective-permute-done | bytes 147488 | tf_op jit(solution)/shard_map/ppermute | solution.py:997
  203.9 6.5 %second_back.1 = (f32[1024,768]{1,0:T(8,128)}, bf16[1024,768]{1,0:T(8,128)(2,1)}, f32[8,768]{1,0:T(8,128)}) custom-call(bf16[1024,768]{1,0:T(8,128)(2,1)} %join.3.cot_ref, f32[4,4,768]{2,1,0:T(4,128)} %reshape.666.slot_ref, f32[1024,1]{1,0:T(8,128)} %convert_element_type.290.mask_ref, f32[1024,768]{1,0:T(8,128)} %get-tuple-element.352.norm_ref, ...), custom_call_target="tpu_custom_call" | custom-call | flops 15728640 | bytes 9437184 | tf_op jit(solution)/shard_map/second_back/pallas_call | solution.py:543
  211.9 10.3 %tall_grad.1 = (bf16[16,96,768]{2,1,0:T(8,128)(2,1)}, bf16[16,96,768]{2,1,0:T(8,128)(2,1)}) custom-call(s32[3,16]{1,0:T(4,128)} %get-tuple-element.601.table_ref, bf16[1024,3072]{1,0:T(8,128)(2,1)} %get-tuple-element.339.left_ref, bf16[1024,768]{1,0:T(8,128)(2,1)} %get-tuple-element.364.right_ref.grad_ref), custom_call_target="tpu_custom_call" | custom-call | flops 4831838208 | bytes 12582912 | tf_op jit(solution)/shard_map/tall_grad/pallas_call | solution.py:230
  223.8 11.7 %hidden_grad.1 = (bf16[1024,3072]{1,0:T(8,128)(2,1)}, f32[1,3072]{1,0:T(1,128)}) custom-call(bf16[1024,768]{1,0:T(8,128)(2,1)} %get-tuple-element.364.right_ref.grad_ref, bf16[3072,768]{1,0:T(8,128)(2,1)} %bitcast.69, bf16[1024,3072]{1,0:T(8,128)(2,1)} %get-tuple-element.365.slope_ref), custom_call_target="tpu_custom_call" | custom-call | flops 4831838208 | bytes 18874368 | tf_op jit(solution)/shard_map/hidden_grad/pallas_call | solution.py:276
  238.6 9.9 %weight_grad.3 = (bf16[16,24,3840]{2,1,0:T(8,128)(2,1)}, bf16[16,24,3840]{2,1,0:T(8,128)(2,1)}) custom-call(s32[3,16]{1,0:T(4,128)} %get-tuple-element.601.table_ref, bf16[1024,768]{1,0:T(8,128)(2,1)} %get-tuple-element.320.mid_ref.left_ref, bf16[1024,3072]{1,0:T(8,128)(2,1)} %get-tuple-element.382.right_ref.hidden_ref), custom_call_target="tpu_custom_call" | custom-call | flops 4831838208 | bytes 12582912 | tf_op jit(solution)/shard_map/weight_grad/pallas_call | solution.py:188
  249.9 12.3 %first_back.1 = (f32[1024,768]{1,0:T(8,128)}, bf16[1024,768]{1,0:T(8,128)(2,1)}, f32[8,768]{1,0:T(8,128)}) custom-call(bf16[1024,3072]{1,0:T(8,128)(2,1)} %get-tuple-element.382.right_ref.hidden_ref, bf16[768,3072]{1,0:T(8,128)(2,1)} %bitcast.64, f32[1024,768]{1,0:T(8,128)} %get-tuple-element.383.second_ref, f32[1024,768]{1,0:T(8,128)} %get-tuple-element.384.norm_ref, ...), custom_call_target="tpu_custom_call" | custom-call | flops 4831838208 | bytes 22020096 | tf_op jit(solution)/shard_map/first_back/pallas_call | solution.py:583
  262.2 5.1 %weight_grad.4 = (bf16[16,24,3840]{2,1,0:T(8,128)(2,1)}, bf16[16,24,3840]{2,1,0:T(8,128)(2,1)}) custom-call(s32[3,16]{1,0:T(4,128)} %get-tuple-element.601.table_ref, bf16[1024,768]{1,0:T(8,128)(2,1)} %get-tuple-element.303.left_ref, bf16[1024,768]{1,0:T(8,128)(2,1)} %get-tuple-element.402.right_ref, ...), custom_call_target="tpu_custom_call", output_to_operand_aliasing={{0}: (3, {}), {1}: (4, {})} | custom-call | flops 1207959552 | bytes 4325376 | tf_op jit(solution)/shard_map/weight_grad/pallas_call | solution.py:188
  267.4 2.2 add_convert_fusion.4
  270.6 3.8 convolution_convert_fusion.grad_ref
  274.5 11.9 %attention_back.2 = (bf16[1024,2304]{1,0:T(8,128)(2,1)}, f32[1,2304]{1,0:T(1,128)}) custom-call(bf16[1024,2304]{1,0:T(8,128)(2,1)} %project.1.qkv_ref, bf16[4,12,256,256]{3,2,1,0:T(8,128)(2,1)} %get-tuple-element.401.probs_ref, bf16[1024,768]{1,0:T(8,128)(2,1)} %convolution_convert_fusion.grad_ref), custom_call_target="tpu_custom_call" | custom-call | flops 1610612736 | bytes 8650752 | tf_op jit(solution)/shard_map/attention_back/pallas_call | solution.py:412
  293.5 6.2 %token_grad.2 = (bf16[160,768]{1,0:T(8,128)(2,1)}, bf16[160,768]{1,0:T(8,128)(2,1)}, bf16[160,768]{1,0:T(8,128)(2,1)}, bf16[32,768]{1,0:T(8,128)(2,1)}) custom-call(bf16[1024,2304]{1,0:T(8,128)(2,1)} %get-tuple-element.425.grad_ref._, bf16[768,2304]{1,0:T(8,128)(2,1)} %bitcast.66, f32[1024,768]{1,0:T(8,128)} %get-tuple-element.420.first_ref), custom_call_target="tpu_custom_call" | custom-call | flops 1811939328 | bytes 8257536 | tf_op jit(solution)/shard_map/token_grad/pallas_call | solution.py:669
  305.6 11.7 %attention_back.3 = (bf16[1024,2304]{1,0:T(8,128)(2,1)}, f32[1,2304]{1,0:T(1,128)}) custom-call(bf16[1024,2304]{1,0:T(8,128)(2,1)} %project.1.qkv_ref, bf16[4,12,256,256]{3,2,1,0:T(8,128)(2,1)} %get-tuple-element.401.probs_ref, bf16[1024,768]{1,0:T(8,128)(2,1)} %convolution_convert_fusion.grad_ref, ...), custom_call_target="tpu_custom_call", output_to_operand_aliasing={{0}: (3, {})} | custom-call | flops 1610612736 | bytes 8650752 | tf_op jit(solution)/shard_map/attention_back/pallas_call | solution.py:412
  317.4 2.5 add_convert_fusion.3
  325.2 8.9 %weight_grad.5 = (bf16[16,24,2432]{2,1,0:T(8,128)(2,1)}, bf16[16,24,2432]{2,1,0:T(8,128)(2,1)}) custom-call(s32[3,16]{1,0:T(4,128)} %get-tuple-element.601.table_ref, bf16[1024,768]{1,0:T(8,128)(2,1)} %join.2.tokens_ref.base_ref.left_ref, bf16[1024,2304]{1,0:T(8,128)(2,1)} %get-tuple-element.457.right_ref.grad_ref, f32[768,128]{1,0:T(8,128)} %maximum_maximum_fusion.refs_0_), custom_call_target="tpu_custom_call" | custom-call | flops 3623878656 | bytes 9830400 | tf_op jit(solution)/shard_map/weight_grad/pallas_call | solution.py:188
  336.9 6.5 %token_grad.3.own_ref = f32[512,768]{1,0:T(8,128)} custom-call(bf16[1024,2304]{1,0:T(8,128)(2,1)} %get-tuple-element.457.right_ref.grad_ref, bf16[768,2304]{1,0:T(8,128)(2,1)} %bitcast.67, f32[1024,768]{1,0:T(8,128)} %get-tuple-element.420.first_ref), custom_call_target="tpu_custom_call" | custom-call | flops 1811939328 | bytes 8257536 | tf_op jit(solution)/shard_map/token_grad/pallas_call | solution.py:669
  352.2 11.0 %collective-permute-done.46 = bf16[2,24,3840]{2,1,0:T(8,128)(2,1)S(1)} collective-permute-done((bf16[2,24,3840]{2,1,0:T(8,128)(2,1)S(1)}, bf16[2,24,3840]{2,1,0:T(8,128)(2,1)S(1)}, u32[]{:S(2)}, u32[]{:S(2)}) %collective-permute-start.46) | collective-permute-done | bytes 368672 | tf_op jit(solution)/shard_map/ppermute | solution.py:66
  364.5 2.5 collective-permute-start.49
  369.1 6.3 %collective-permute-done.49 = bf16[1,24,3840]{2,1,0:T(8,128)(2,1)S(1)} collective-permute-done((bf16[1,24,3840]{2,1,0:T(8,128)(2,1)S(1)}, bf16[1,24,3840]{2,1,0:T(8,128)(2,1)S(1)}, u32[]{:S(2)}, u32[]{:S(2)}) %collective-permute-start.49) | collective-permute-done | bytes 184352 | tf_op jit(solution)/shard_map/ppermute | solution.py:66
  378.3 2.4 collective-permute-start.52
  380.8 2.7 deal.2
  384.1 2.2 collective-permute-done.51
  390.7 3.5 deal.3
  (320 shorter events, 106.4 us)
Async XLA Ops:
  3.4 11.4 %collective-permute-start = (bf16[1,24,3200]{2,1,0:T(8,128)(2,1)S(1)}, bf16[1,24,3200]{2,1,0:T(8,128)(2,1)S(1)}, u32[]{:S(2)}, u32[]{:S(2)}) collective-permute-start(bf16[1,24,3200]{2,1,0:T(8,128)(2,1)S(1)} %get-tuple-element.575), channel_id=1, source_target_pairs={{0,4},{1,5},{2,6},{3,7},{4,0},{5,1},{6,2},{7,3},{8,12},{9,13},{10,... | collective-permute-start | bytes 460808 | tf_op jit(solution)/shard_map/ppermute | solution.py:66
  14.9 13.8 %collective-permute-start.1 = (bf16[2,24,3200]{2,1,0:T(8,128)(2,1)S(1)}, bf16[2,24,3200]{2,1,0:T(8,128)(2,1)S(1)}, u32[]{:S(2)}, u32[]{:S(2)}) collective-permute-start(bf16[2,24,3200]{2,1,0:T(8,128)(2,1)S(1)} %pad_maximum_fusion.8), channel_id=1, source_target_pairs={{0,2},{1,3},{2,0},{3,1},{4,6},{5,7},{6,4},{7,5},{8,10},{9,11},{10,... | collective-permute-start | bytes 921608 | tf_op jit(solution)/shard_map/ppermute | solution.py:66
  15.7 13.1 %collective-permute-start.2 = (bf16[160,768]{1,0:T(8,128)(2,1)S(1)}, bf16[160,768]{1,0:T(8,128)(2,1)S(1)}, u32[]{:S(2)}, u32[]{:S(2)}) collective-permute-start(bf16[160,768]{1,0:T(8,128)(2,1)S(1)} %get-tuple-element.266), channel_id=1, source_target_pairs={{0,4},{1,5},{2,6},{3,7},{4,0},{5,1},{6,2},{7,3},{8,12},{9,13},{10,... | collective-permute-start | bytes 737288 | tf_op jit(solution)/shard_map/ppermute | solution.py:72
  29.5 11.2 %collective-permute-start.3 = (bf16[4,24,3200]{2,1,0:T(8,128)(2,1)S(1)}, bf16[4,24,3200]{2,1,0:T(8,128)(2,1)S(1)}, u32[]{:S(2)}, u32[]{:S(2)}) collective-permute-start(bf16[4,24,3200]{2,1,0:T(8,128)(2,1)S(1)} %pad_maximum_fusion.4), channel_id=1, source_target_pairs={{0,8},{1,17},{2,10},{3,19},{4,12},{5,21},{6,14},{7,23},{8,0},{9,25... | collective-permute-start | bytes 1843208 | tf_op jit(solution)/shard_map/ppermute | solution.py:66
  30.8 9.2 %collective-permute-start.4 = (bf16[1,24,3072]{2,1,0:T(8,128)(2,1)S(1)}, bf16[1,24,3072]{2,1,0:T(8,128)(2,1)S(1)}, u32[]{:S(2)}, u32[]{:S(2)}) collective-permute-start(bf16[1,24,3072]{2,1,0:T(8,128)(2,1)S(1)} %get-tuple-element.270), channel_id=1, source_target_pairs={{0,4},{1,5},{2,6},{3,7},{4,0},{5,1},{6,2},{7,3},{8,12},{9,13},{10,... | collective-permute-start | bytes 442376 | tf_op jit(solution)/shard_map/ppermute | solution.py:66
  40.9 25.6 %collective-permute-start.5 = (bf16[8,24,3200]{2,1,0:T(8,128)(2,1)S(1)}, bf16[8,24,3200]{2,1,0:T(8,128)(2,1)}, u32[]{:S(2)}, u32[]{:S(2)}) collective-permute-start(bf16[8,24,3200]{2,1,0:T(8,128)(2,1)S(1)} %pad_maximum_fusion.refs_0_), channel_id=1, source_target_pairs={{0,16},{1,9},{2,18},{3,11},{4,20},{5,13},{6,22},{7,15},{8,24},{9,1... | collective-permute-start | bytes 3686408 | tf_op jit(solution)/shard_map/ppermute | solution.py:66
  44.6 7.7 %collective-permute-start.6 = (bf16[2,24,3072]{2,1,0:T(8,128)(2,1)}, bf16[2,24,3072]{2,1,0:T(8,128)(2,1)S(1)}, u32[]{:S(2)}, u32[]{:S(2)}) collective-permute-start(bf16[2,24,3072]{2,1,0:T(8,128)(2,1)} %pad_maximum_fusion.9), channel_id=1, source_target_pairs={{0,2},{1,3},{2,0},{3,1},{4,6},{5,7},{6,4},{7,5},{8,10},{9,11},{10,... | collective-permute-start | bytes 884744 | tf_op jit(solution)/shard_map/ppermute | solution.py:66
  50.1 28.6 %collective-permute-start.8 = (bf16[8,24,3200]{2,1,0:T(8,128)(2,1)S(1)}, bf16[8,24,3200]{2,1,0:T(8,128)(2,1)}, u32[]{:S(2)}, u32[]{:S(2)}) collective-permute-start(bf16[8,24,3200]{2,1,0:T(8,128)(2,1)S(1)} %pad_maximum_fusion.refs_0_), channel_id=1, source_target_pairs={{0,1},{1,0},{2,3},{3,2},{4,5},{5,4},{6,7},{7,6},{8,9},{9,8},{10,11... | collective-permute-start | bytes 3686408 | tf_op jit(solution)/shard_map/ppermute | solution.py:69
  50.1 16.4 %collective-permute-start.7 = (bf16[192,768]{1,0:T(8,128)(2,1)S(1)}, bf16[192,768]{1,0:T(8,128)(2,1)S(1)}, u32[]{:S(2)}, u32[]{:S(2)}) collective-permute-start(bf16[192,768]{1,0:T(8,128)(2,1)S(1)} %copy-done.20), channel_id=1, source_target_pairs={{0,4},{1,5},{2,6},{3,7},{4,0},{5,1},{6,2},{7,3},{8,12},{9,13},{10,... | collective-permute-start | bytes 884744 | tf_op jit(solution)/shard_map/ppermute | solution.py:72
  66.4 12.3 %collective-permute-start.9 = (bf16[8,24,3200]{2,1,0:T(8,128)(2,1)}, bf16[8,24,3200]{2,1,0:T(8,128)(2,1)}, u32[]{:S(2)}, u32[]{:S(2)}) collective-permute-start(bf16[8,24,3200]{2,1,0:T(8,128)(2,1)} %collective-permute-done.5.refs_1_), channel_id=1, source_target_pairs={{0,1},{1,0},{2,3},{3,2},{4,5},{5,4},{6,7},{7,6},{8,9},{9,8},{10,11... | collective-permute-start | bytes 3686408 | tf_op jit(solution)/shard_map/ppermute | solution.py:69
  67.3 10.2 %collective-permute-start.10 = (bf16[4,24,3072]{2,1,0:T(8,128)(2,1)}, bf16[4,24,3072]{2,1,0:T(8,128)(2,1)}, u32[]{:S(2)}, u32[]{:S(2)}) collective-permute-start(bf16[4,24,3072]{2,1,0:T(8,128)(2,1)} %pad_maximum_fusion.5), channel_id=1, source_target_pairs={{0,8},{1,17},{2,10},{3,19},{4,12},{5,21},{6,14},{7,23},{8,0},{9,25... | collective-permute-start | bytes 1769480 | tf_op jit(solution)/shard_map/ppermute | solution.py:66
  68.7 15.6 %collective-permute-start.11 = (bf16[160,768]{1,0:T(8,128)(2,1)}, bf16[160,768]{1,0:T(8,128)(2,1)}, u32[]{:S(2)}, u32[]{:S(2)}) collective-permute-start(bf16[160,768]{1,0:T(8,128)(2,1)} %get-tuple-element.285), channel_id=1, source_target_pairs={{0,4},{1,5},{2,6},{3,7},{4,0},{5,1},{6,2},{7,3},{8,12},{9,13},{10,... | collective-permute-start | bytes 737288 | tf_op jit(solution)/shard_map/ppermute | solution.py:72
  69.6 30.7 %collective-permute-start.13 = (s32[512]{0:T(512)}, s32[512]{0:T(512)S(1)}, u32[]{:S(2)}, u32[]{:S(2)}) collective-permute-start(s32[512]{0:T(512)} %get-tuple-element.591), channel_id=1, source_target_pairs={{0,4},{1,5},{2,6},{3,7},{4,0},{5,1},{6,2},{7,3},{8,12},{9,13},{10,... | collective-permute-start | bytes 6152 | tf_op jit(solution)/shard_map/ppermute | solution.py:72
  86.0 26.5 %collective-permute-start.14 = (bf16[8,24,3072]{2,1,0:T(8,128)(2,1)S(1)}, bf16[8,24,3072]{2,1,0:T(8,128)(2,1)}, u32[]{:S(2)}, u32[]{:S(2)}) collective-permute-start(bf16[8,24,3072]{2,1,0:T(8,128)(2,1)S(1)} %pad_maximum_fusion.1.refs_0_), channel_id=1, source_target_pairs={{0,16},{1,9},{2,18},{3,11},{4,20},{5,13},{6,22},{7,15},{8,24},{9,1... | collective-permute-start | bytes 3538952 | tf_op jit(solution)/shard_map/ppermute | solution.py:66
  87.2 10.8 %collective-permute-start.12 = (bf16[1,96,768]{2,1,0:T(8,128)(2,1)S(1)}, bf16[1,96,768]{2,1,0:T(8,128)(2,1)S(1)}, u32[]{:S(2)}, u32[]{:S(2)}) collective-permute-start(bf16[1,96,768]{2,1,0:T(8,128)(2,1)S(1)} %copy-done.37), channel_id=1, source_target_pairs={{0,4},{1,5},{2,6},{3,7},{4,0},{5,1},{6,2},{7,3},{8,12},{9,13},{10,... | collective-permute-start | bytes 442376 | tf_op jit(solution)/shard_map/ppermute | solution.py:66
  98.0 14.4 %collective-permute-start.15 = (bf16[2,96,768]{2,1,0:T(8,128)(2,1)S(1)}, bf16[2,96,768]{2,1,0:T(8,128)(2,1)S(1)}, u32[]{:S(2)}, u32[]{:S(2)}) collective-permute-start(bf16[2,96,768]{2,1,0:T(8,128)(2,1)S(1)} %pad_maximum_fusion.10), channel_id=1, source_target_pairs={{0,2},{1,3},{2,0},{3,1},{4,6},{5,7},{6,4},{7,5},{8,10},{9,11},{10,... | collective-permute-start | bytes 884744 | tf_op jit(solution)/shard_map/ppermute | solution.py:66
  100.9 23.7 %collective-permute-start.17 = (bf16[8,24,3072]{2,1,0:T(8,128)(2,1)S(1)}, bf16[8,24,3072]{2,1,0:T(8,128)(2,1)}, u32[]{:S(2)}, u32[]{:S(2)}) collective-permute-start(bf16[8,24,3072]{2,1,0:T(8,128)(2,1)S(1)} %pad_maximum_fusion.1.refs_0_), channel_id=1, source_target_pairs={{0,1},{1,0},{2,3},{3,2},{4,5},{5,4},{6,7},{7,6},{8,9},{9,8},{10,11... | collective-permute-start | bytes 3538952 | tf_op jit(solution)/shard_map/ppermute | solution.py:69
  100.9 11.6 %collective-permute-start.16 = (bf16[128,768]{1,0:T(8,128)(2,1)S(1)}, bf16[128,768]{1,0:T(8,128)(2,1)S(1)}, u32[]{:S(2)}, u32[]{:S(2)}) collective-permute-start(bf16[128,768]{1,0:T(8,128)(2,1)S(1)} %copy-done.33), channel_id=1, source_target_pairs={{0,4},{1,5},{2,6},{3,7},{4,0},{5,1},{6,2},{7,3},{8,12},{9,13},{10,... | collective-permute-start | bytes 589832 | tf_op jit(solution)/shard_map/ppermute | solution.py:72
  112.5 12.1 %collective-permute-start.18 = (bf16[8,24,3072]{2,1,0:T(8,128)(2,1)}, bf16[8,24,3072]{2,1,0:T(8,128)(2,1)}, u32[]{:S(2)}, u32[]{:S(2)}) collective-permute-start(bf16[8,24,3072]{2,1,0:T(8,128)(2,1)} %collective-permute-done.14.refs_1_), channel_id=1, source_target_pairs={{0,1},{1,0},{2,3},{3,2},{4,5},{5,4},{6,7},{7,6},{8,9},{9,8},{10,11... | collective-permute-start | bytes 3538952 | tf_op jit(solution)/shard_map/ppermute | solution.py:69
  112.7 10.6 %collective-permute-start.19 = (bf16[4,96,768]{2,1,0:T(8,128)(2,1)S(1)}, bf16[4,96,768]{2,1,0:T(8,128)(2,1)}, u32[]{:S(2)}, u32[]{:S(2)}) collective-permute-start(bf16[4,96,768]{2,1,0:T(8,128)(2,1)S(1)} %pad_maximum_fusion.6), channel_id=1, source_target_pairs={{0,8},{1,17},{2,10},{3,19},{4,12},{5,21},{6,14},{7,23},{8,0},{9,25... | collective-permute-start | bytes 1769480 | tf_op jit(solution)/shard_map/ppermute | solution.py:66
  124.6 27.8 %collective-permute-start.21 = (bf16[8,96,768]{2,1,0:T(8,128)(2,1)S(1)}, bf16[8,96,768]{2,1,0:T(8,128)(2,1)}, u32[]{:S(2)}, u32[]{:S(2)}) collective-permute-start(bf16[8,96,768]{2,1,0:T(8,128)(2,1)S(1)} %pad_maximum_fusion.2.refs_0_), channel_id=1, source_target_pairs={{0,16},{1,9},{2,18},{3,11},{4,20},{5,13},{6,22},{7,15},{8,24},{9,1... | collective-permute-start | bytes 3538952 | tf_op jit(solution)/shard_map/ppermute | solution.py:66
  126.2 26.2 %collective-permute-start.22 = (bf16[8,96,768]{2,1,0:T(8,128)(2,1)S(1)}, bf16[8,96,768]{2,1,0:T(8,128)(2,1)}, u32[]{:S(2)}, u32[]{:S(2)}) collective-permute-start(bf16[8,96,768]{2,1,0:T(8,128)(2,1)S(1)} %pad_maximum_fusion.2.refs_0_), channel_id=1, source_target_pairs={{0,1},{1,0},{2,3},{3,2},{4,5},{5,4},{6,7},{7,6},{8,9},{9,8},{10,11... | collective-permute-start | bytes 3538952 | tf_op jit(solution)/shard_map/ppermute | solution.py:69
  126.2 14.7 %collective-permute-start.20 = (bf16[160,768]{1,0:T(8,128)(2,1)}, bf16[160,768]{1,0:T(8,128)(2,1)S(1)}, u32[]{:S(2)}, u32[]{:S(2)}) collective-permute-start(bf16[160,768]{1,0:T(8,128)(2,1)} %slice.313), channel_id=1, source_target_pairs={{0,4},{1,5},{2,6},{3,7},{4,0},{5,1},{6,2},{7,3},{8,12},{9,13},{10,... | collective-permute-start | bytes 737288 | tf_op jit(solution)/shard_map/ppermute | solution.py:72
  140.9 11.4 %collective-permute-start.23 = (bf16[128,768]{1,0:T(8,128)(2,1)S(1)}, bf16[128,768]{1,0:T(8,128)(2,1)S(1)}, u32[]{:S(2)}, u32[]{:S(2)}) collective-permute-start(bf16[128,768]{1,0:T(8,128)(2,1)S(1)} %copy-done.32), channel_id=1, source_target_pairs={{0,4},{1,5},{2,6},{3,7},{4,0},{5,1},{6,2},{7,3},{8,12},{9,13},{10,... | collective-permute-start | bytes 589832 | tf_op jit(solution)/shard_map/ppermute | solution.py:72
  152.4 9.7 %collective-permute-start.24 = (bf16[8,96,768]{2,1,0:T(8,128)(2,1)}, bf16[8,96,768]{2,1,0:T(8,128)(2,1)S(1)}, u32[]{:S(2)}, u32[]{:S(2)}) collective-permute-start(bf16[8,96,768]{2,1,0:T(8,128)(2,1)} %collective-permute-done.21.refs_1_), channel_id=1, source_target_pairs={{0,1},{1,0},{2,3},{3,2},{4,5},{5,4},{6,7},{7,6},{8,9},{9,8},{10,11... | collective-permute-start | bytes 3538952 | tf_op jit(solution)/shard_map/ppermute | solution.py:69
  152.9 9.2 %collective-permute-start.25 = (bf16[96,768]{1,0:T(8,128)(2,1)S(1)}, bf16[96,768]{1,0:T(8,128)(2,1)S(1)}, u32[]{:S(2)}, u32[]{:S(2)}) collective-permute-start(bf16[96,768]{1,0:T(8,128)(2,1)S(1)} %copy-done.36), channel_id=1, source_target_pairs={{0,4},{1,5},{2,6},{3,7},{4,0},{5,1},{6,2},{7,3},{8,12},{9,13},{10,... | collective-permute-start | bytes 442376 | tf_op jit(solution)/shard_map/ppermute | solution.py:72
  210.4 12.1 %collective-permute-start.31 = (bf16[128,768]{1,0:T(8,128)(2,1)S(1)}, bf16[128,768]{1,0:T(8,128)(2,1)S(1)}, u32[]{:S(2)}, u32[]{:S(2)}) collective-permute-start(bf16[128,768]{1,0:T(8,128)(2,1)S(1)} %get-tuple-element.358), channel_id=1, source_target_pairs={{0,4},{1,5},{2,6},{3,7},{4,0},{5,1},{6,2},{7,3},{8,12},{9,13},{10,... | collective-permute-start | bytes 589832 | tf_op jit(solution)/shard_map/ppermute | solution.py:72
  222.5 13.1 %collective-permute-start.32 = (bf16[16,96,768]{2,1,0:T(8,128)(2,1)}, bf16[16,96,768]{2,1,0:T(8,128)(2,1)S(1)}, u32[]{:S(2)}, u32[]{:S(2)}) collective-permute-start(bf16[16,96,768]{2,1,0:T(8,128)(2,1)} %get-tuple-element.363), channel_id=1, source_target_pairs={{0,1},{1,0},{2,3},{3,2},{4,5},{5,4},{6,7},{7,6},{8,9},{9,8},{10,11... | collective-permute-start | bytes 7077896 | tf_op jit(solution)/shard_map/ppermute | solution.py:69
  222.5 13.1 %collective-permute-start.33 = (bf16[128,768]{1,0:T(8,128)(2,1)S(1)}, bf16[128,768]{1,0:T(8,128)(2,1)S(1)}, u32[]{:S(2)}, u32[]{:S(2)}) collective-permute-start(bf16[128,768]{1,0:T(8,128)(2,1)S(1)} %copy-done.31), channel_id=1, source_target_pairs={{0,4},{1,5},{2,6},{3,7},{4,0},{5,1},{6,2},{7,3},{8,12},{9,13},{10,... | collective-permute-start | bytes 589832 | tf_op jit(solution)/shard_map/ppermute | solution.py:72
  236.3 25.9 %collective-permute-start.34 = (bf16[8,96,768]{2,1,0:T(8,128)(2,1)S(1)}, bf16[8,96,768]{2,1,0:T(8,128)(2,1)S(1)}, u32[]{:S(2)}, u32[]{:S(2)}) collective-permute-start(bf16[8,96,768]{2,1,0:T(8,128)(2,1)S(1)} %add_convert_fusion.1), channel_id=1, source_target_pairs={{0,16},{1,9},{2,18},{3,11},{4,20},{5,13},{6,22},{7,15},{8,24},{9,1... | collective-permute-start | bytes 3538952 | tf_op jit(solution)/shard_map/ppermute | solution.py:66
  236.9 11.9 %collective-permute-start.35 = (bf16[128,768]{1,0:T(8,128)(2,1)S(1)}, bf16[128,768]{1,0:T(8,128)(2,1)S(1)}, u32[]{:S(2)}, u32[]{:S(2)}) collective-permute-start(bf16[128,768]{1,0:T(8,128)(2,1)S(1)} %get-tuple-element.378), channel_id=1, source_target_pairs={{0,4},{1,5},{2,6},{3,7},{4,0},{5,1},{6,2},{7,3},{8,12},{9,13},{10,... | collective-permute-start | bytes 589832 | tf_op jit(solution)/shard_map/ppermute | solution.py:72
  248.9 13.3 %collective-permute-start.36 = (bf16[128,768]{1,0:T(8,128)(2,1)S(1)}, bf16[128,768]{1,0:T(8,128)(2,1)S(1)}, u32[]{:S(2)}, u32[]{:S(2)}) collective-permute-start(bf16[128,768]{1,0:T(8,128)(2,1)S(1)} %copy-done.30), channel_id=1, source_target_pairs={{0,4},{1,5},{2,6},{3,7},{4,0},{5,1},{6,2},{7,3},{8,12},{9,13},{10,... | collective-permute-start | bytes 589832 | tf_op jit(solution)/shard_map/ppermute | solution.py:72
  267.3 19.1 %collective-permute-start.38 = (bf16[16,24,3840]{2,1,0:T(8,128)(2,1)}, bf16[16,24,3840]{2,1,0:T(8,128)(2,1)S(1)}, u32[]{:S(2)}, u32[]{:S(2)}) collective-permute-start(bf16[16,24,3840]{2,1,0:T(8,128)(2,1)} %get-tuple-element.400), channel_id=1, source_target_pairs={{0,1},{1,0},{2,3},{3,2},{4,5},{5,4},{6,7},{7,6},{8,9},{9,8},{10,11... | collective-permute-start | bytes 8847368 | tf_op jit(solution)/shard_map/ppermute | solution.py:69
  269.6 16.8 %collective-permute-start.37 = (bf16[4,96,768]{2,1,0:T(8,128)(2,1)}, bf16[4,96,768]{2,1,0:T(8,128)(2,1)S(1)}, u32[]{:S(2)}, u32[]{:S(2)}) collective-permute-start(bf16[4,96,768]{2,1,0:T(8,128)(2,1)} %add_convert_fusion.4), channel_id=1, source_target_pairs={{0,8},{1,17},{2,10},{3,19},{4,12},{5,21},{6,14},{7,23},{8,0},{9,25... | collective-permute-start | bytes 1769480 | tf_op jit(solution)/shard_map/ppermute | solution.py:66
  290.7 26.7 %collective-permute-start.40 = (bf16[8,24,3840]{2,1,0:T(8,128)(2,1)}, bf16[8,24,3840]{2,1,0:T(8,128)(2,1)}, u32[]{:S(2)}, u32[]{:S(2)}) collective-permute-start(bf16[8,24,3840]{2,1,0:T(8,128)(2,1)} %add_convert_fusion), channel_id=1, source_target_pairs={{0,16},{1,9},{2,18},{3,11},{4,20},{5,13},{6,22},{7,15},{8,24},{9,1... | collective-permute-start | bytes 4423688 | tf_op jit(solution)/shard_map/ppermute | solution.py:66
  291.9 25.5 %collective-permute-start.39 = (bf16[2,96,768]{2,1,0:T(8,128)(2,1)}, bf16[2,96,768]{2,1,0:T(8,128)(2,1)}, u32[]{:S(2)}, u32[]{:S(2)}) collective-permute-start(bf16[2,96,768]{2,1,0:T(8,128)(2,1)} %add_convert_fusion.7), channel_id=1, source_target_pairs={{0,2},{1,3},{2,0},{3,1},{4,6},{5,7},{6,4},{7,5},{8,10},{9,11},{10,... | collective-permute-start | bytes 884744 | tf_op jit(solution)/shard_map/ppermute | solution.py:66
  299.7 17.7 %collective-permute-start.41 = (bf16[160,768]{1,0:T(8,128)(2,1)}, bf16[160,768]{1,0:T(8,128)(2,1)}, u32[]{:S(2)}, u32[]{:S(2)}) collective-permute-start(bf16[160,768]{1,0:T(8,128)(2,1)} %get-tuple-element.428), channel_id=1, source_target_pairs={{0,4},{1,5},{2,6},{3,7},{4,0},{5,1},{6,2},{7,3},{8,12},{9,13},{10,... | collective-permute-start | bytes 737288 | tf_op jit(solution)/shard_map/ppermute | solution.py:72
  319.9 14.9 %collective-permute-start.42 = (bf16[4,24,3840]{2,1,0:T(8,128)(2,1)}, bf16[4,24,3840]{2,1,0:T(8,128)(2,1)}, u32[]{:S(2)}, u32[]{:S(2)}) collective-permute-start(bf16[4,24,3840]{2,1,0:T(8,128)(2,1)} %add_convert_fusion.3), channel_id=1, source_target_pairs={{0,8},{1,17},{2,10},{3,19},{4,12},{5,21},{6,14},{7,23},{8,0},{9,25... | collective-permute-start | bytes 2211848 | tf_op jit(solution)/shard_map/ppermute | solution.py:66
  321.6 13.1 %collective-permute-start.43 = (bf16[160,768]{1,0:T(8,128)(2,1)}, bf16[160,768]{1,0:T(8,128)(2,1)}, u32[]{:S(2)}, u32[]{:S(2)}) collective-permute-start(bf16[160,768]{1,0:T(8,128)(2,1)} %get-tuple-element.452), channel_id=1, source_target_pairs={{0,4},{1,5},{2,6},{3,7},{4,0},{5,1},{6,2},{7,3},{8,12},{9,13},{10,... | collective-permute-start | bytes 737288 | tf_op jit(solution)/shard_map/ppermute | solution.py:72
  334.7 8.6 %collective-permute-start.44 = (bf16[16,24,2432]{2,1,0:T(8,128)(2,1)}, bf16[16,24,2432]{2,1,0:T(8,128)(2,1)}, u32[]{:S(2)}, u32[]{:S(2)}) collective-permute-start(bf16[16,24,2432]{2,1,0:T(8,128)(2,1)} %get-tuple-element.456), channel_id=1, source_target_pairs={{0,1},{1,0},{2,3},{3,2},{4,5},{5,4},{6,7},{7,6},{8,9},{9,8},{10,11... | collective-permute-start | bytes 5603336 | tf_op jit(solution)/shard_map/ppermute | solution.py:69
  336.0 14.0 %collective-permute-start.50 = (bf16[1,96,768]{2,1,0:T(8,128)(2,1)S(1)}, bf16[1,96,768]{2,1,0:T(8,128)(2,1)S(1)}, u32[]{:S(2)}, u32[]{:S(2)}) collective-permute-start(bf16[1,96,768]{2,1,0:T(8,128)(2,1)S(1)} %add_convert_fusion.10), channel_id=1, source_target_pairs={{0,4},{1,5},{2,6},{3,7},{4,0},{5,1},{6,2},{7,3},{8,12},{9,13},{10,... | collective-permute-start | bytes 442376 | tf_op jit(solution)/shard_map/ppermute | solution.py:66
  344.8 18.4 %collective-permute-start.45 = (bf16[8,24,2432]{2,1,0:T(8,128)(2,1)S(1)}, bf16[8,24,2432]{2,1,0:T(8,128)(2,1)S(1)}, u32[]{:S(2)}, u32[]{:S(2)}) collective-permute-start(bf16[8,24,2432]{2,1,0:T(8,128)(2,1)S(1)} %add_convert_fusion.2), channel_id=1, source_target_pairs={{0,16},{1,9},{2,18},{3,11},{4,20},{5,13},{6,22},{7,15},{8,24},{9,1... | collective-permute-start | bytes 2801672 | tf_op jit(solution)/shard_map/ppermute | solution.py:66
  347.0 16.2 %collective-permute-start.46 = (bf16[2,24,3840]{2,1,0:T(8,128)(2,1)S(1)}, bf16[2,24,3840]{2,1,0:T(8,128)(2,1)S(1)}, u32[]{:S(2)}, u32[]{:S(2)}) collective-permute-start(bf16[2,24,3840]{2,1,0:T(8,128)(2,1)S(1)} %add_convert_fusion.6), channel_id=1, source_target_pairs={{0,2},{1,3},{2,0},{3,1},{4,6},{5,7},{6,4},{7,5},{8,10},{9,11},{10,... | collective-permute-start | bytes 1105928 | tf_op jit(solution)/shard_map/ppermute | solution.py:66
  349.0 14.2 %collective-permute-start.47 = (bf16[160,768]{1,0:T(8,128)(2,1)S(1)}, bf16[160,768]{1,0:T(8,128)(2,1)S(1)}, u32[]{:S(2)}, u32[]{:S(2)}) collective-permute-start(bf16[160,768]{1,0:T(8,128)(2,1)S(1)} %copy-done.48), channel_id=1, source_target_pairs={{0,4},{1,5},{2,6},{3,7},{4,0},{5,1},{6,2},{7,3},{8,12},{9,13},{10,... | collective-permute-start | bytes 737288 | tf_op jit(solution)/shard_map/ppermute | solution.py:72
  364.5 10.9 %collective-permute-start.49 = (bf16[1,24,3840]{2,1,0:T(8,128)(2,1)S(1)}, bf16[1,24,3840]{2,1,0:T(8,128)(2,1)S(1)}, u32[]{:S(2)}, u32[]{:S(2)}) collective-permute-start(bf16[1,24,3840]{2,1,0:T(8,128)(2,1)S(1)} %add_convert_fusion.9), channel_id=1, source_target_pairs={{0,4},{1,5},{2,6},{3,7},{4,0},{5,1},{6,2},{7,3},{8,12},{9,13},{10,... | collective-permute-start | bytes 552968 | tf_op jit(solution)/shard_map/ppermute | solution.py:66
  368.3 8.6 %collective-permute-start.48 = (bf16[4,24,2432]{2,1,0:T(8,128)(2,1)S(1)}, bf16[4,24,2432]{2,1,0:T(8,128)(2,1)S(1)}, u32[]{:S(2)}, u32[]{:S(2)}) collective-permute-start(bf16[4,24,2432]{2,1,0:T(8,128)(2,1)S(1)} %add_convert_fusion.5), channel_id=1, source_target_pairs={{0,8},{1,17},{2,10},{3,19},{4,12},{5,21},{6,14},{7,23},{8,0},{9,25... | collective-permute-start | bytes 1400840 | tf_op jit(solution)/shard_map/ppermute | solution.py:66
  378.1 8.2 %collective-permute-start.51 = (bf16[2,24,2432]{2,1,0:T(8,128)(2,1)S(1)}, bf16[2,24,2432]{2,1,0:T(8,128)(2,1)S(1)}, u32[]{:S(2)}, u32[]{:S(2)}) collective-permute-start(bf16[2,24,2432]{2,1,0:T(8,128)(2,1)S(1)} %add_convert_fusion.8), channel_id=1, source_target_pairs={{0,2},{1,3},{2,0},{3,1},{4,6},{5,7},{6,4},{7,5},{8,10},{9,11},{10,... | collective-permute-start | bytes 700424 | tf_op jit(solution)/shard_map/ppermute | solution.py:66
  387.3 6.9 %collective-permute-start.53 = (bf16[1,24,2432]{2,1,0:T(8,128)(2,1)S(1)}, bf16[1,24,2432]{2,1,0:T(8,128)(2,1)S(1)}, u32[]{:S(2)}, u32[]{:S(2)}) collective-permute-start(bf16[1,24,2432]{2,1,0:T(8,128)(2,1)S(1)} %add_convert_fusion.11), channel_id=1, source_target_pairs={{0,4},{1,5},{2,6},{3,7},{4,0},{5,1},{6,2},{7,3},{8,12},{9,13},{10,... | collective-permute-start | bytes 350216 | tf_op jit(solution)/shard_map/ppermute | solution.py:66
  (56 other events, 480.6 us)

commit v9 on v8

--- a/solution.py
+++ b/solution.py
@@ -160,7 +160,7 @@
     def within(s):
         return table_ref[0, s], table_ref[1, s]
 
-    if not extra:
+    if extra == 0:
         split_slabs(acc, core, chips, mine_ref, theirs_ref, slice(None), within)
         return
     step = pl.program_id(0)
@@ -169,8 +169,21 @@
 
     @pl.when(step == 0)
     def _():
+        one, two, first, second, bias = (ref[...] for ref in refs[:extra])
+        joined = one + two
+        lines = [
+            joined[:, :D],
+            joined[:, 2 * D :],
+            first[2:3],
+            first[:2],
+            second[2:3],
+            second[:2],
+            bias,
+            jnp.zeros((116, D), F32),
+        ]
+        values = jnp.concatenate(lines, axis=0).T
         tail = pl.ds(mine_ref.shape[2] - 128, 128)
-        split_slabs(refs[0][...], core, chips, mine_ref, theirs_ref, tail, within)
+        split_slabs(values, core, chips, mine_ref, theirs_ref, tail, within)
 
 
 def weight_grad(left, right, slots, tile, extra=None, room=0, into=()):
@@ -178,7 +191,7 @@
     width = right.shape[1]
     chips = slots.shape[1]
     slab = height // (2 * chips)
-    total = width + (room if extra is None else extra.shape[1])
+    total = width + (room if extra is None else 128)
     first = 0
     if into:
         total = into[0].shape[2]
@@ -186,7 +199,7 @@
     block = (chips, slab, total if extra is not None else tile)
     place = (lambda j, t: (0, 0, 0)) if extra is not None else (lambda j, t: (0, 0, j + first))
     return pl.pallas_call(
-        functools.partial(weight_grad_kernel, chips, extra is not None),
+        functools.partial(weight_grad_kernel, chips, len(extra or ())),
         grid_spec=pltpu.PrefetchScalarGridSpec(
             num_scalar_prefetch=1,
             grid=(width // tile,),
@@ -194,7 +207,7 @@
                 pl.BlockSpec((rows, height), lambda j, t: (0, 0)),
                 pl.BlockSpec((rows, tile), lambda j, t: (0, j)),
             ]
-            + ([] if extra is None else [pl.BlockSpec((height, 128), lambda j, t: (0, 0))])
+            + [pl.BlockSpec(x.shape, lambda j, t: (0, 0)) for x in extra or ()]
             + [pl.BlockSpec(memory_space=pl.ANY)] * len(into),
             out_specs=[pl.BlockSpec(block, place)] * 2,
         ),
@@ -207,7 +220,7 @@
             transcendentals=0,
         ),
         name="weight_grad",
-    )(slots, left, right, *([] if extra is None else [extra]), *into)
+    )(slots, left, right, *(extra or ()), *into)
 
 
 def tall_grad_kernel(chips, table_ref, left_ref, right_ref, mine_ref, theirs_ref):
@@ -686,30 +699,44 @@
     )(d_joined, weight, d_first)
 
 
-def project_kernel(tokens_ref, w_ref, b_ref, out_ref):
-    out_ref[...] = (dot(tokens_ref[...], w_ref[...]) + b_ref[...]).astype(BF16)
-
-
-def project(tokens, weight, bias):
-    rows, width = tokens.shape[0], weight.shape[1]
+def project_kernel(w_ref, b_ref, *refs):
+    pieces, (tokens_ref, out_ref) = refs[:-2], refs[-2:]
+    step = pl.program_id(0)
+
+    @pl.when(step == 0)
+    def _():
+        join_kernel(*pieces, tokens_ref)
+
+    tokens = tokens_ref[pl.ds(pl.multiple_of(step * BLOCK, BLOCK), BLOCK), :]
+    out_ref[...] = (dot(tokens, w_ref[...]) + b_ref[...]).astype(BF16)
+
+
+def project(pieces, weight, bias):
+    rows, width = sum(x.shape[0] for x in pieces), weight.shape[1]
     return pl.pallas_call(
         project_kernel,
         grid=(rows // BLOCK,),
         in_specs=[
-            pl.BlockSpec((BLOCK, D), lambda i: (i, 0)),
             pl.BlockSpec((D, width), lambda i: (0, 0)),
             pl.BlockSpec((1, width), lambda i: (0, 0)),
-        ],
-        out_specs=pl.BlockSpec((BLOCK, width), lambda i: (i, 0)),
-        out_shape=jax.ShapeDtypeStruct((rows, width), BF16),
+        ]
+        + [pl.BlockSpec(x.shape, lambda i: (0, 0)) for x in pieces],
+        out_specs=[
+            pl.BlockSpec((rows, D), lambda i: (0, 0)),
+            pl.BlockSpec((BLOCK, width), lambda i: (i, 0)),
+        ],
+        out_shape=[
+            jax.ShapeDtypeStruct((rows, D), BF16),
+            jax.ShapeDtypeStruct((rows, width), BF16),
+        ],
         compiler_params=pltpu.CompilerParams(vmem_limit_bytes=VMEM_LIMIT),
         cost_estimate=pl.CostEstimate(
             flops=2 * rows * D * width,
-            bytes_accessed=2 * (rows * (D + width) + D * width),
+            bytes_accessed=2 * (rows * (2 * D + width) + D * width),
             transcendentals=0,
         ),
         name="project",
-    )(tokens, weight, bias)
+    )(weight, bias, *pieces)
 
 
 def add_norm_kernel(
@@ -889,6 +916,9 @@
     nq, np_ = question_in.shape[0], passage_in.shape[0]
     shift = 2 * places.half
     low_pa = pa % shift
+    row_ids = jnp.arange(rows, dtype=jnp.int32)
+    seq = jnp.where(is_q, row_ids // lq, row_ids // lp)
+    qid = seq.reshape(rows, 1)
     g1, g2, g3 = Gather(first), Gather(second), Gather(third)
     my_tokens, send_tokens = sides(rows_q, rows_p)
     tokens_out = chunked(send_tokens, (5, 6, 5))
@@ -899,9 +929,10 @@
     g1.along_z()
     tokens_in = hand(tokens_out[:1])
     my_cot, send_cot = sides(question_cot.reshape(-1, D), passage_cot.reshape(-1, D))
-    g1.send, g2.send, tokens_in, my_cot, send_cot = tie(
-        g1.send, g2.send, tokens_in, my_cot, send_cot
-    )
+    g1.send, g2.send, tokens_in, my_cot, send_cot, table, slots, seq, qid = tie(
+        g1.send, g2.send, tokens_in, my_cot, send_cot, table, slots, seq, qid
+    )
+    g3.send, g3.stack = tie(g3.send, g3.stack)
     g1.pb_first()
     g2.mid()
     g1.stack, g2.send, tokens_out = tie(g1.stack, g2.send, tokens_out)
@@ -930,10 +961,9 @@
     vec = small[:, :8].T
     bias_e = small[:, 8:12].reshape(1, FF)
     bias_j = jnp.concatenate([vec[0], jnp.zeros((D,), F32), vec[1]])
-    tokens = join([my_tokens] + tokens_in)
-    qkv = project(tokens, wj, bias_j[None])
-
-    cot_out = chunked(send_cot, (4, 5, 4, 3))
+    tokens, qkv = project([my_tokens] + tokens_in, wj, bias_j[None])
+
+    cot_out = chunked(send_cot, (5, 3, 3, 2, 3))
     by_pa = positive.reshape(places.pa_n, nq)
     pair = [lax.dynamic_index_in_dim(by_pa, low_pa + k, 0, keepdims=False) for k in (0, shift)]
     pair = jnp.concatenate(pair)[None]
@@ -943,9 +973,6 @@
     valid_p = (jnp.arange(lp, dtype=jnp.int32)[None, :] < passage_len[:, None]).astype(jnp.int32)
     my_valid, send_valid = sides(valid_q.reshape(-1), valid_p.reshape(-1))
     valid = jnp.concatenate([my_valid, places.swap_tower(send_valid)])
-    row_ids = jnp.arange(rows, dtype=jnp.int32)
-    seq = jnp.where(is_q, row_ids // lq, row_ids // lp)
-    qid = seq.reshape(rows, 1)
     kid = jnp.where(valid > 0, seq, -1).reshape(rows // BLOCK, 1, BLOCK)
     row_mask = valid.reshape(rows, 1).astype(F32)
 
@@ -958,29 +985,32 @@
     context, g2.held, g3.send, cot_in, cot_out = tie(context, g2.held, g3.send, cot_in, cot_out)
     g2.core_held()
     g3.pb_first()
+    cot_in = cot_in + hand(cot_out[1:2])
     norm_one, inverse_one, mid_low, mid = add_norm(
         context, wo, tokens, row_mask, vec, (2, 3, 4), True
     )
-    mid_low, g2.parts, g3.stack, cot_out = tie(mid_low, g2.parts, g3.stack, cot_out)
+    mid_low, g2.parts, g3.stack, cot_in, cot_out = tie(mid_low, g2.parts, g3.stack, cot_in, cot_out)
     g3.send = g3.stack
     g3.pb_last()
     g3.core_stack()
-    cot_in = cot_in + hand(cot_out[1:2])
     (full_e,) = g2.whole([(0, FF)])
     we = full_e.reshape(D, FF)
-    mid_low, we, cot_in, cot_out = tie(mid_low, we, cot_in, cot_out)
+    mid_low, we, cot_out = tie(mid_low, we, cot_out)
     cot_in = cot_in + hand(cot_out[2:3])
     gelu = expand(mid_low, we, bias_e, 0, 1)
     gelu, g3.held, g3.other, g3.stack, cot_in, cot_out = tie(
         gelu, g3.held, g3.other, g3.stack, cot_in, cot_out
     )
     g3.core_held()
-    cot_in = cot_in + hand(cot_out[3:])
+    cot_in = cot_in + hand(cot_out[3:4])
     active, slope = expand(mid_low, we, bias_e, 1, 1, tuple(gelu))
-    active, g3.parts, cot_in = tie(active, g3.parts, cot_in)
+    active, g3.parts, cot_in, cot_out = tie(active, g3.parts, cot_in, cot_out)
     (full_r,) = g3.whole([(0, D)])
     wr = full_r.reshape(FF, D)
+    wr, cot_out = tie(wr, cot_out)
+    cot_in = cot_in + hand(cot_out[4:])
     norm_two, inverse_two, out = add_norm(active, wr, mid, row_mask, vec, (5, 6, 7), False)
+    out, cot_in = tie(out, cot_in)
 
     firsts = out.reshape(per_q, lq, D)[:, 0, :]
     others = places.swap_tower(firsts)
@@ -1036,6 +1066,12 @@
         return weight_grad(left, right, slots, D, **more)
 
     def plain(left, right, extra=None):
+        if extra is not None:
+            one, two, first, second, bias = extra
+            joined = one + two
+            lines = [joined[:, :D], joined[:, 2 * D :], first[2:3], first[:2]]
+            lines = lines + [second[2:3], second[:2], bias, jnp.zeros((116, D), F32)]
+            extra = jnp.concatenate(lines, axis=0).T
         return grad_plain(left, right, table, extra)
 
     class Scatter:
@@ -1123,7 +1159,7 @@
     se.pb_first()
     sr.along_z()
     part = own_rows // 16
-    send_grad = token_grad(d_joined, wj, d_first, own_rows, [5 * part] * 3 + [part], BF16)
+    send_grad = token_grad(d_joined, wj, d_first, own_rows, [k * part for k in (5, 3, 3, 5)], BF16)
     d_joined, send_grad = tie(d_joined, send_grad)
     got_grad = hand(send_grad[:1])
     d_joined, sums_two = attention_back(qkv, probs, d_context, 0, later, d_joined)
@@ -1135,38 +1171,24 @@
     se.pb_rest()
     sr.mid()
     got_grad = got_grad + hand(send_grad[1:2])
-    g_joined_bias = (sums_one + sums_two)[0]
-    g_vec = jnp.concatenate(
-        [
-            g_joined_bias[None, :D],
-            g_joined_bias[None, 2 * D :],
-            sums_first[2:3],
-            sums_first[:2],
-            sums_second[2:3],
-            sums_second[:2],
-        ]
-    )
-    g_small = jnp.concatenate(
-        [g_vec.T, g_bias_expand.reshape(D, 4), jnp.zeros((D, 116), F32)], axis=1
-    )
-    sj = Scatter(*(gradient if even else plain)(tokens, d_joined, extra=g_small))
-    se.parts, sj.parts, sj.theirs, d_joined, got_grad, send_grad = tie(
-        se.parts, sj.parts, sj.theirs, d_joined, got_grad, send_grad
+    bias_sums = g_bias_expand.reshape(D, 4).T
+    small_sums = (sums_one, sums_two, sums_first, sums_second, bias_sums)
+    sj = Scatter(*(gradient if even else plain)(tokens, d_joined, extra=small_sums))
+    se.parts, sr.out, sj.parts, sj.theirs, d_joined, got_grad, send_grad = tie(
+        se.parts, sr.out, sj.parts, sj.theirs, d_joined, got_grad, send_grad
     )
     sj.cores()
+    got_grad = got_grad + hand(send_grad[2:3])
+    (own_grad,) = token_grad(d_joined, wj, d_first, 0, [own_rows], F32)
+    sj.parts, own_grad, got_grad, send_grad = tie(sj.parts, own_grad, got_grad, send_grad)
+    sj.pb_first()
     se.along_z()
-    (own_grad,) = token_grad(d_joined, wj, d_first, 0, [own_rows], F32)
-    sj.parts, own_grad, send_grad = tie(sj.parts, own_grad, send_grad)
-    sj.pb_first()
-    got_grad = got_grad + hand(send_grad[2:3])
+    got_grad = got_grad + hand(send_grad[3:])
     sj.parts, se.parts, got_grad, send_grad = tie(sj.parts, se.parts, got_grad, send_grad)
     sj.pb_rest()
     se.mid()
-    sj.parts, se.out, sr.out, got_out, out, send_grad = tie(
-        sj.parts, se.out, sr.out, got_out, out, send_grad
-    )
+    sj.parts, se.out, got_out, out = tie(sj.parts, se.out, got_out, out)
     sj.along_z()
-    got_grad = got_grad + hand(send_grad[3:])
     out_q, out_p = deal(tower.reshape(1), out, got_out)
     sj.parts, out_q, out_p, got_grad = tie(sj.parts, out_q, out_p, got_grad)
     grad_q, grad_p = deal(tower.reshape(1), own_grad, got_grad)

time: 400 us -> 389 us (0.973)
  other arithmetic: 39.8 us -> 35.2 us
    ppermute x24, waiting for transfers between devices: 43.6 us -> 50.2 us  [swap(): return lax.ppermute(values, AXES, self.pairs(step))]
    ppermute x17 -> x18, waiting for transfers between devices: 29.9 us -> 24.6 us  [swap_tower(): lax.ppermute(values, 'pa', [(i, i ^ 2 * self.half) for i in range(self.pa...]
    ppermute x17 -> x18, starting transfers between devices: 24.4 us -> 26.1 us  [swap_tower(): lax.ppermute(values, 'pa', [(i, i ^ 2 * self.half) for i in range(self.pa...]
  transfers between devices with their start and end apart: 54 -> 55, of which waited for: 21 -> 22; matrix products, arithmetic and copies ran while one was open for 12% -> 10% of each run, Pallas kernels for 39% -> 42%
where the time goes in v9:
time: 389 us; the launch traced here: 387 us
  Pallas kernels  179 us (46%)
  waiting for transfers between devices  83.4 us (21%)
  starting transfers between devices  59.9 us (15%)
  other arithmetic  35.2 us (9%)
  local copies, waits for them, and re-layouts  23.5 us (6%)
  matrix products  4.48 us (1%)
    ppermute x24, waiting for transfers between devices, swap(): return lax.ppermute(values, AXES, self.pairs(step))  50.2 us
    ppermute x24, starting transfers between devices, swap(): return lax.ppermute(values, AXES, self.pairs(step))  30.1 us
    ppermute x18, starting transfers between devices, swap_tower(): lax.ppermute(values, 'pa', [(i, i ^ 2 * self.half) for i in range(self.pa...  26.1 us
    ppermute x18, waiting for transfers between devices, swap_tower(): lax.ppermute(values, 'pa', [(i, i ^ 2 * self.half) for i in range(self.pa...  24.6 us
    pallas_call x3, Pallas kernels, weight_grad(): pl.pallas_call(functools.partial(weight_grad_kernel, chips, len(extra or...  24 us
    pallas_call x2, Pallas kernels, attention_back(): pl.pallas_call(attention_back_more_kernel if more else attention_back_ker...  23.7 us
    pallas_call x2, Pallas kernels, add_norm(): pl.pallas_call(functools.partial(add_norm_kernel, rows_of), grid=(rows //...  19 us
    pallas_call x2, Pallas kernels, expand(): pl.pallas_call(expand_more_kernel if into else expand_kernel, grid=(count...  15.8 us
  transfers between devices with their start and end apart: 55, of which 22 were waited for; matrix products, arithmetic and copies ran while one was open for 10% of the time, Pallas kernels for 42%

profile of v9, /device:TPU:0, one launch (start us, length us, event | category | flops | bytes accessed | tf_op | source)
XLA Modules:
  0.0 387.3 jit_solution(12799951330249354905)
XLA Ops:
  3.4 4.1 %collective-permute-start = (bf16[1,24,3200]{2,1,0:T(8,128)(2,1)S(1)}, bf16[1,24,3200]{2,1,0:T(8,128)(2,1)S(1)}, u32[]{:S(2)}, u32[]{:S(2)}) collective-permute-start(bf16[1,24,3200]{2,1,0:T(8,128)(2,1)S(1)} %get-tuple-element.620), channel_id=1, source_target_pairs={{0,4},{1,5},{2,6},{3,7},{4,0},{5,1},{6,2},{7,3},{8,12},{9,13},{10,... | collective-permute-start | bytes 460808 | tf_op jit(solution)/shard_map/ppermute | solution.py:66
  7.7 2.2 bitcast_select_fusion.2
  15.9 3.2 collective-permute-start.2
  20.1 8.5 %collective-permute-done.1 = bf16[2,24,3200]{2,1,0:T(8,128)(2,1)S(1)} collective-permute-done((bf16[2,24,3200]{2,1,0:T(8,128)(2,1)S(1)}, bf16[2,24,3200]{2,1,0:T(8,128)(2,1)S(1)}, u32[]{:S(2)}, u32[]{:S(2)}) %collective-permute-start.1) | collective-permute-done | bytes 307232 | tf_op jit(solution)/shard_map/ppermute | solution.py:66
  30.7 2.6 collective-permute-start.4
  33.3 6.6 %collective-permute-done.4 = bf16[1,24,3072]{2,1,0:T(8,128)(2,1)S(1)} collective-permute-done((bf16[1,24,3072]{2,1,0:T(8,128)(2,1)S(1)}, bf16[1,24,3072]{2,1,0:T(8,128)(2,1)S(1)}, u32[]{:S(2)}, u32[]{:S(2)}) %collective-permute-start.4) | collective-permute-done | bytes 147488 | tf_op jit(solution)/shard_map/ppermute | solution.py:66
  41.6 2.8 collective-permute-start.6
  49.9 12.9 %collective-permute-done.7.refs_2_ = bf16[192,768]{1,0:T(8,128)(2,1)S(1)} collective-permute-done((bf16[192,768]{1,0:T(8,128)(2,1)S(1)}, bf16[192,768]{1,0:T(8,128)(2,1)S(1)}, u32[]{:S(2)}, u32[]{:S(2)}) %collective-permute-start.7) | collective-permute-done | bytes 294944 | tf_op jit(solution)/shard_map/ppermute | solution.py:72
  65.4 2.9 collective-permute-start.13
  68.3 5.3 %collective-permute-done.10 = bf16[4,24,3072]{2,1,0:T(8,128)(2,1)} collective-permute-done((bf16[4,24,3072]{2,1,0:T(8,128)(2,1)S(1)}, bf16[4,24,3072]{2,1,0:T(8,128)(2,1)}, u32[]{:S(2)}, u32[]{:S(2)}) %collective-permute-start.10) | collective-permute-done | bytes 589856 | tf_op jit(solution)/shard_map/ppermute | solution.py:66
  74.9 5.5 %assemble.3 = (bf16[16,2,24,2304]{3,2,1,0:T(8,128)(2,1)}, bf16[16,2,24,768]{3,2,1,0:T(8,128)(2,1)}, bf16[16,2,24,128]{3,2,1,0:T(8,128)(2,1)}) custom-call(s32[3,16]{1,0:T(4,128)} %get-tuple-element.292.idx_ref, bf16[8,24,3200]{2,1,0:T(8,128)(2,1)} %copy-done.1, bf16[8,24,3200]{2,1,0:T(8,128)(2,1)} %collective-permute-done.5.refs_1_, ...), custom_call_target="tpu_custom_call" | custom-call | bytes 9830400 | tf_op jit(solution)/shard_map/assemble/pallas_call | solution.py:118
  83.3 8.5 %project.1 = (bf16[1024,768]{1,0:T(8,128)(2,1)}, bf16[1024,2304]{1,0:T(8,128)(2,1)}) custom-call(bf16[768,2304]{1,0:T(8,128)(2,1)} %bitcast.65, f32[1,2304]{1,0:T(1,128)} %broadcast_in_dim.14.b_ref, bf16[512,768]{1,0:T(8,128)(2,1)} %get-tuple-element.610.refs_0_, bf16[160,768]{1,0:T(8,128)(2,1)} %copy-done.56, bf16[192,768]{1,0:T(8,128)(2,1)} %copy-done.55, ...), custom_call_target="tpu_custom_call" | custom-call | flops 3623878656 | bytes 11403264 | tf_op jit(solution)/shard_map/project/pallas_call | solution.py:716
  96.0 10.6 %attention.1 = (bf16[1024,768]{1,0:T(8,128)(2,1)}, bf16[4,12,256,256]{3,2,1,0:T(8,128)(2,1)}) custom-call(bf16[1024,2304]{1,0:T(8,128)(2,1)} %get-tuple-element.320.qkv_ref, s32[1024,1]{1,0:T(8,128)} %fusion.2.qid_ref, s32[4,1,256]{2,1,0:T(1,128)} %bitcast.85), custom_call_target="tpu_custom_call" | custom-call | flops 1610612736 | bytes 12582912 | tf_op jit(solution)/shard_map/attention/pallas_call | solution.py:342
  106.7 2.4 collective-permute-done.16.refs_1_
  111.7 7.4 %add_norm.2 = (f32[1024,768]{1,0:T(8,128)}, f32[1024,1]{1,0:T(8,128)}, bf16[1024,768]{1,0:T(8,128)(2,1)}, f32[1024,768]{1,0:T(8,128)}) custom-call(bf16[1024,768]{1,0:T(8,128)(2,1)} %get-tuple-element.333.left_ref, bf16[768,768]{1,0:T(8,128)(2,1)} %bitcast.74, bf16[1024,768]{1,0:T(8,128)(2,1)} %get-tuple-element.335.base_ref.left_ref, ...), custom_call_target="tpu_custom_call" | custom-call | flops 1207959552 | bytes 12189696 | tf_op jit(solution)/shard_map/add_norm/pallas_call | solution.py:762
  123.5 4.8 %assemble.4 = bf16[16,2,24,3072]{3,2,1,0:T(8,128)(2,1)} custom-call(s32[3,16]{1,0:T(4,128)} %get-tuple-element.292.idx_ref, bf16[8,24,3072]{2,1,0:T(8,128)(2,1)} %copy-done.2, bf16[8,24,3072]{2,1,0:T(8,128)(2,1)} %collective-permute-done.14.refs_1_, bf16[8,24,3072]{2,1,0:T(8,128)(2,1)} %collective-permute-done.17.refs_2_, ...), custom_call_target="tpu_custom_call" | custom-call | bytes 9437184 | tf_op jit(solution)/shard_map/assemble/pallas_call | solution.py:118
  128.4 2.3 collective-permute-start.23
  130.7 7.9 %expand.2 = (bf16[1024,3072]{1,0:T(8,128)(2,1)}, bf16[1024,3072]{1,0:T(8,128)(2,1)}) custom-call(bf16[1024,768]{1,0:T(8,128)(2,1)} %get-tuple-element.352.mid_ref.left_ref, bf16[768,3072]{1,0:T(8,128)(2,1)} %bitcast.62, f32[1,3072]{1,0:T(1,128)} %reshape.500.b_ref), custom_call_target="tpu_custom_call" | custom-call | flops 2415919104 | bytes 10223616 | tf_op jit(solution)/shard_map/expand/pallas_call | solution.py:638
  140.2 7.9 %expand.3 = (bf16[1024,3072]{1,0:T(8,128)(2,1)}, bf16[1024,3072]{1,0:T(8,128)(2,1)}) custom-call(bf16[1024,768]{1,0:T(8,128)(2,1)} %get-tuple-element.352.mid_ref.left_ref, bf16[768,3072]{1,0:T(8,128)(2,1)} %bitcast.63, f32[1,3072]{1,0:T(1,128)} %reshape.500.b_ref, ...), custom_call_target="tpu_custom_call", output_to_operand_aliasing={{0}: (3, {}), {1}: (4, {})} | custom-call | flops 2415919104 | bytes 10223616 | tf_op jit(solution)/shard_map/expand/pallas_call | solution.py:638
  149.2 4.9 %assemble.5 = bf16[16,2,96,768]{3,2,1,0:T(8,128)(2,1)} custom-call(s32[3,16]{1,0:T(4,128)} %get-tuple-element.292.idx_ref, bf16[8,96,768]{2,1,0:T(8,128)(2,1)} %copy-done.3, bf16[8,96,768]{2,1,0:T(8,128)(2,1)} %collective-permute-done.21.refs_1_, bf16[8,96,768]{2,1,0:T(8,128)(2,1)} %collective-permute-done.22.refs_2_, bf16[8,96,768]{2,1,0:T(8,128)(2,1)} %copy-done.10), custom_call_target="tpu_custom_call" | custom-call | bytes 9437184 | tf_op jit(solution)/shard_map/assemble/pallas_call | solution.py:118
  154.1 2.2 collective-permute-start.26
  156.3 11.6 %add_norm.3 = (f32[1024,768]{1,0:T(8,128)}, f32[1024,1]{1,0:T(8,128)}, bf16[1024,768]{1,0:T(8,128)(2,1)}) custom-call(bf16[1024,3072]{1,0:T(8,128)(2,1)} %get-tuple-element.373.left_ref, bf16[3072,768]{1,0:T(8,128)(2,1)} %bitcast.68, f32[1024,768]{1,0:T(8,128)} %get-tuple-element.381.base_ref, f32[1024,1]{1,0:T(8,128)} %convert_element_type.272.mask_ref, ...), custom_call_target="tpu_custom_call" | custom-call | flops 4831838208 | bytes 20447232 | tf_op jit(solution)/shard_map/add_norm/pallas_call | solution.py:762
  169.7 4.2 %collective-permute-done.27 = bf16[16,768]{1,0:T(8,128)(2,1)S(1)} collective-permute-done((bf16[16,768]{1,0:T(8,128)(2,1)S(1)}, bf16[16,768]{1,0:T(8,128)(2,1)S(1)}, u32[]{:S(2)}, u32[]{:S(2)}) %collective-permute-start.27) | collective-permute-done | bytes 24608 | tf_op jit(solution)/shard_map/ppermute | solution.py:72
  174.7 3.3 collective-permute-done.28
  178.9 2.0 fusion.35
  180.9 2.7 join.1.cot_ref
  185.0 3.8 collective-permute-done.30
  193.4 6.5 %second_back.1 = (f32[1024,768]{1,0:T(8,128)}, bf16[1024,768]{1,0:T(8,128)(2,1)}, f32[8,768]{1,0:T(8,128)}) custom-call(bf16[1024,768]{1,0:T(8,128)(2,1)} %join.1.cot_ref, f32[4,4,768]{2,1,0:T(4,128)} %reshape.508.slot_ref, f32[1024,1]{1,0:T(8,128)} %convert_element_type.272.mask_ref, f32[1024,768]{1,0:T(8,128)} %get-tuple-element.395.norm_ref, ...), custom_call_target="tpu_custom_call" | custom-call | flops 15728640 | bytes 9437184 | tf_op jit(solution)/shard_map/second_back/pallas_call | solution.py:556
  200.7 10.2 %tall_grad.1 = (bf16[16,96,768]{2,1,0:T(8,128)(2,1)}, bf16[16,96,768]{2,1,0:T(8,128)(2,1)}) custom-call(s32[3,16]{1,0:T(4,128)} %get-tuple-element.291.table_ref, bf16[1024,3072]{1,0:T(8,128)(2,1)} %get-tuple-element.373.left_ref, bf16[1024,768]{1,0:T(8,128)(2,1)} %get-tuple-element.407.right_ref.grad_ref), custom_call_target="tpu_custom_call" | custom-call | flops 4831838208 | bytes 12582912 | tf_op jit(solution)/shard_map/tall_grad/pallas_call | solution.py:243
  213.2 11.7 %hidden_grad.1 = (bf16[1024,3072]{1,0:T(8,128)(2,1)}, f32[1,3072]{1,0:T(1,128)}) custom-call(bf16[1024,768]{1,0:T(8,128)(2,1)} %get-tuple-element.407.right_ref.grad_ref, bf16[3072,768]{1,0:T(8,128)(2,1)} %bitcast.69, bf16[1024,3072]{1,0:T(8,128)(2,1)} %get-tuple-element.408.slope_ref), custom_call_target="tpu_custom_call" | custom-call | flops 4831838208 | bytes 18874368 | tf_op jit(solution)/shard_map/hidden_grad/pallas_call | solution.py:289
  228.5 10.0 %weight_grad.3 = (bf16[16,24,3840]{2,1,0:T(8,128)(2,1)}, bf16[16,24,3840]{2,1,0:T(8,128)(2,1)}) custom-call(s32[3,16]{1,0:T(4,128)} %get-tuple-element.291.table_ref, bf16[1024,768]{1,0:T(8,128)(2,1)} %get-tuple-element.352.mid_ref.left_ref, bf16[1024,3072]{1,0:T(8,128)(2,1)} %get-tuple-element.425.right_ref.hidden_ref), custom_call_target="tpu_custom_call" | custom-call | flops 4831838208 | bytes 12582912 | tf_op jit(solution)/shard_map/weight_grad/pallas_call | solution.py:201
  239.9 12.3 %first_back.1 = (f32[1024,768]{1,0:T(8,128)}, bf16[1024,768]{1,0:T(8,128)(2,1)}, f32[8,768]{1,0:T(8,128)}) custom-call(bf16[1024,3072]{1,0:T(8,128)(2,1)} %get-tuple-element.425.right_ref.hidden_ref, bf16[768,3072]{1,0:T(8,128)(2,1)} %bitcast.64, f32[1024,768]{1,0:T(8,128)} %get-tuple-element.426.second_ref, f32[1024,768]{1,0:T(8,128)} %get-tuple-element.427.norm_ref, ...), custom_call_target="tpu_custom_call" | custom-call | flops 4831838208 | bytes 22020096 | tf_op jit(solution)/shard_map/first_back/pallas_call | solution.py:596
  252.3 5.1 %weight_grad.4 = (bf16[16,24,3840]{2,1,0:T(8,128)(2,1)}, bf16[16,24,3840]{2,1,0:T(8,128)(2,1)}) custom-call(s32[3,16]{1,0:T(4,128)} %get-tuple-element.291.table_ref, bf16[1024,768]{1,0:T(8,128)(2,1)} %get-tuple-element.333.left_ref, bf16[1024,768]{1,0:T(8,128)(2,1)} %get-tuple-element.445.right_ref, ...), custom_call_target="tpu_custom_call", output_to_operand_aliasing={{0}: (3, {}), {1}: (4, {})} | custom-call | flops 1207959552 | bytes 4325376 | tf_op jit(solution)/shard_map/weight_grad/pallas_call | solution.py:201
  257.5 2.2 add_convert_fusion.4
  260.4 3.8 convolution_convert_fusion.grad_ref
  264.2 11.9 %attention_back.2 = (bf16[1024,2304]{1,0:T(8,128)(2,1)}, f32[1,2304]{1,0:T(1,128)}) custom-call(bf16[1024,2304]{1,0:T(8,128)(2,1)} %get-tuple-element.320.qkv_ref, bf16[4,12,256,256]{3,2,1,0:T(8,128)(2,1)} %get-tuple-element.444.probs_ref, bf16[1024,768]{1,0:T(8,128)(2,1)} %convolution_convert_fusion.grad_ref), custom_call_target="tpu_custom_call" | custom-call | flops 1610612736 | bytes 8650752 | tf_op jit(solution)/shard_map/attention_back/pallas_call | solution.py:425
  282.9 6.2 %token_grad.2 = (bf16[160,768]{1,0:T(8,128)(2,1)}, bf16[96,768]{1,0:T(8,128)(2,1)}, bf16[96,768]{1,0:T(8,128)(2,1)}, bf16[160,768]{1,0:T(8,128)(2,1)}) custom-call(bf16[1024,2304]{1,0:T(8,128)(2,1)} %get-tuple-element.468.grad_ref._, bf16[768,2304]{1,0:T(8,128)(2,1)} %bitcast.66, f32[1024,768]{1,0:T(8,128)} %get-tuple-element.463.first_ref), custom_call_target="tpu_custom_call" | custom-call | flops 1811939328 | bytes 8257536 | tf_op jit(solution)/shard_map/token_grad/pallas_call | solution.py:682
  292.7 11.7 %attention_back.3 = (bf16[1024,2304]{1,0:T(8,128)(2,1)}, f32[1,2304]{1,0:T(1,128)}) custom-call(bf16[1024,2304]{1,0:T(8,128)(2,1)} %get-tuple-element.320.qkv_ref, bf16[4,12,256,256]{3,2,1,0:T(8,128)(2,1)} %get-tuple-element.444.probs_ref, bf16[1024,768]{1,0:T(8,128)(2,1)} %convolution_convert_fusion.grad_ref, ...), custom_call_target="tpu_custom_call", output_to_operand_aliasing={{0}: (3, {})} | custom-call | flops 1610612736 | bytes 8650752 | tf_op jit(solution)/shard_map/attention_back/pallas_call | solution.py:425
  308.3 2.0 collective-permute-start.44
  311.3 9.0 %weight_grad.5 = (bf16[16,24,2432]{2,1,0:T(8,128)(2,1)}, bf16[16,24,2432]{2,1,0:T(8,128)(2,1)}) custom-call(s32[3,16]{1,0:T(4,128)} %get-tuple-element.291.table_ref, bf16[1024,768]{1,0:T(8,128)(2,1)} %get-tuple-element.335.base_ref.left_ref, bf16[1024,2304]{1,0:T(8,128)(2,1)} %get-tuple-element.505.right_ref.grad_ref, ...), custom_call_target="tpu_custom_call" | custom-call | flops 3623878656 | bytes 9830400 | tf_op jit(solution)/shard_map/weight_grad/pallas_call | solution.py:201
  324.7 6.4 %token_grad.3.own_ref = f32[512,768]{1,0:T(8,128)} custom-call(bf16[1024,2304]{1,0:T(8,128)(2,1)} %get-tuple-element.505.right_ref.grad_ref, bf16[768,2304]{1,0:T(8,128)(2,1)} %bitcast.67, f32[1024,768]{1,0:T(8,128)} %get-tuple-element.463.first_ref), custom_call_target="tpu_custom_call" | custom-call | flops 1811939328 | bytes 8257536 | tf_op jit(solution)/shard_map/token_grad/pallas_call | solution.py:682
  331.1 2.5 collective-permute-done.47.refs_2_
  337.8 2.4 collective-permute-start.50
  340.2 13.3 %collective-permute-done.49 = bf16[2,24,3840]{2,1,0:T(8,128)(2,1)} collective-permute-done((bf16[2,24,3840]{2,1,0:T(8,128)(2,1)S(1)}, bf16[2,24,3840]{2,1,0:T(8,128)(2,1)}, u32[]{:S(2)}, u32[]{:S(2)}) %collective-permute-start.49) | collective-permute-done | bytes 368672 | tf_op jit(solution)/shard_map/ppermute | solution.py:66
  358.4 7.0 %collective-permute-done.52 = bf16[1,24,3840]{2,1,0:T(8,128)(2,1)S(1)} collective-permute-done((bf16[1,24,3840]{2,1,0:T(8,128)(2,1)S(1)}, bf16[1,24,3840]{2,1,0:T(8,128)(2,1)S(1)}, u32[]{:S(2)}, u32[]{:S(2)}) %collective-permute-start.52) | collective-permute-done | bytes 184352 | tf_op jit(solution)/shard_map/ppermute | solution.py:66
  368.8 2.7 deal.2
  371.5 4.3 %collective-permute-done.53 = bf16[2,24,2432]{2,1,0:T(8,128)(2,1)S(1)} collective-permute-done((bf16[2,24,2432]{2,1,0:T(8,128)(2,1)S(1)}, bf16[2,24,2432]{2,1,0:T(8,128)(2,1)S(1)}, u32[]{:S(2)}, u32[]{:S(2)}) %collective-permute-start.53) | collective-permute-done | bytes 233504 | tf_op jit(solution)/shard_map/ppermute | solution.py:66
  379.0 3.5 deal.3
  (323 shorter events, 97.6 us)
Async XLA Ops:
  3.4 11.4 %collective-permute-start = (bf16[1,24,3200]{2,1,0:T(8,128)(2,1)S(1)}, bf16[1,24,3200]{2,1,0:T(8,128)(2,1)S(1)}, u32[]{:S(2)}, u32[]{:S(2)}) collective-permute-start(bf16[1,24,3200]{2,1,0:T(8,128)(2,1)S(1)} %get-tuple-element.620), channel_id=1, source_target_pairs={{0,4},{1,5},{2,6},{3,7},{4,0},{5,1},{6,2},{7,3},{8,12},{9,13},{10,... | collective-permute-start | bytes 460808 | tf_op jit(solution)/shard_map/ppermute | solution.py:66
  14.9 13.8 %collective-permute-start.1 = (bf16[2,24,3200]{2,1,0:T(8,128)(2,1)S(1)}, bf16[2,24,3200]{2,1,0:T(8,128)(2,1)S(1)}, u32[]{:S(2)}, u32[]{:S(2)}) collective-permute-start(bf16[2,24,3200]{2,1,0:T(8,128)(2,1)S(1)} %pad_maximum_fusion.8), channel_id=1, source_target_pairs={{0,2},{1,3},{2,0},{3,1},{4,6},{5,7},{6,4},{7,5},{8,10},{9,11},{10,... | collective-permute-start | bytes 921608 | tf_op jit(solution)/shard_map/ppermute | solution.py:66
  15.9 12.9 %collective-permute-start.2 = (bf16[160,768]{1,0:T(8,128)(2,1)S(1)}, bf16[160,768]{1,0:T(8,128)(2,1)S(1)}, u32[]{:S(2)}, u32[]{:S(2)}) collective-permute-start(bf16[160,768]{1,0:T(8,128)(2,1)S(1)} %copy-done.23), channel_id=1, source_target_pairs={{0,4},{1,5},{2,6},{3,7},{4,0},{5,1},{6,2},{7,3},{8,12},{9,13},{10,... | collective-permute-start | bytes 737288 | tf_op jit(solution)/shard_map/ppermute | solution.py:72
  29.5 10.5 %collective-permute-start.3 = (bf16[4,24,3200]{2,1,0:T(8,128)(2,1)S(1)}, bf16[4,24,3200]{2,1,0:T(8,128)(2,1)S(1)}, u32[]{:S(2)}, u32[]{:S(2)}) collective-permute-start(bf16[4,24,3200]{2,1,0:T(8,128)(2,1)S(1)} %pad_maximum_fusion.4), channel_id=1, source_target_pairs={{0,8},{1,17},{2,10},{3,19},{4,12},{5,21},{6,14},{7,23},{8,0},{9,25... | collective-permute-start | bytes 1843208 | tf_op jit(solution)/shard_map/ppermute | solution.py:66
  30.7 9.2 %collective-permute-start.4 = (bf16[1,24,3072]{2,1,0:T(8,128)(2,1)S(1)}, bf16[1,24,3072]{2,1,0:T(8,128)(2,1)S(1)}, u32[]{:S(2)}, u32[]{:S(2)}) collective-permute-start(bf16[1,24,3072]{2,1,0:T(8,128)(2,1)S(1)} %get-tuple-element.294), channel_id=1, source_target_pairs={{0,4},{1,5},{2,6},{3,7},{4,0},{5,1},{6,2},{7,3},{8,12},{9,13},{10,... | collective-permute-start | bytes 442376 | tf_op jit(solution)/shard_map/ppermute | solution.py:66
  40.2 22.6 %collective-permute-start.5 = (bf16[8,24,3200]{2,1,0:T(8,128)(2,1)S(1)}, bf16[8,24,3200]{2,1,0:T(8,128)(2,1)}, u32[]{:S(2)}, u32[]{:S(2)}) collective-permute-start(bf16[8,24,3200]{2,1,0:T(8,128)(2,1)S(1)} %pad_maximum_fusion.refs_0_), channel_id=1, source_target_pairs={{0,16},{1,9},{2,18},{3,11},{4,20},{5,13},{6,22},{7,15},{8,24},{9,1... | collective-permute-start | bytes 3686408 | tf_op jit(solution)/shard_map/ppermute | solution.py:66
  41.6 8.2 %collective-permute-start.6 = (bf16[2,24,3072]{2,1,0:T(8,128)(2,1)S(1)}, bf16[2,24,3072]{2,1,0:T(8,128)(2,1)S(1)}, u32[]{:S(2)}, u32[]{:S(2)}) collective-permute-start(bf16[2,24,3072]{2,1,0:T(8,128)(2,1)S(1)} %pad_maximum_fusion.9), channel_id=1, source_target_pairs={{0,2},{1,3},{2,0},{3,1},{4,6},{5,7},{6,4},{7,5},{8,10},{9,11},{10,... | collective-permute-start | bytes 884744 | tf_op jit(solution)/shard_map/ppermute | solution.py:66
  46.4 28.4 %collective-permute-start.8 = (bf16[8,24,3200]{2,1,0:T(8,128)(2,1)S(1)}, bf16[8,24,3200]{2,1,0:T(8,128)(2,1)}, u32[]{:S(2)}, u32[]{:S(2)}) collective-permute-start(bf16[8,24,3200]{2,1,0:T(8,128)(2,1)S(1)} %pad_maximum_fusion.refs_0_), channel_id=1, source_target_pairs={{0,1},{1,0},{2,3},{3,2},{4,5},{5,4},{6,7},{7,6},{8,9},{9,8},{10,11... | collective-permute-start | bytes 3686408 | tf_op jit(solution)/shard_map/ppermute | solution.py:69
  46.4 16.4 %collective-permute-start.7 = (bf16[192,768]{1,0:T(8,128)(2,1)S(1)}, bf16[192,768]{1,0:T(8,128)(2,1)S(1)}, u32[]{:S(2)}, u32[]{:S(2)}) collective-permute-start(bf16[192,768]{1,0:T(8,128)(2,1)S(1)} %slice.383), channel_id=1, source_target_pairs={{0,4},{1,5},{2,6},{3,7},{4,0},{5,1},{6,2},{7,3},{8,12},{9,13},{10,... | collective-permute-start | bytes 884744 | tf_op jit(solution)/shard_map/ppermute | solution.py:72
  62.8 12.0 %collective-permute-start.9 = (bf16[8,24,3200]{2,1,0:T(8,128)(2,1)}, bf16[8,24,3200]{2,1,0:T(8,128)(2,1)}, u32[]{:S(2)}, u32[]{:S(2)}) collective-permute-start(bf16[8,24,3200]{2,1,0:T(8,128)(2,1)} %collective-permute-done.5.refs_1_), channel_id=1, source_target_pairs={{0,1},{1,0},{2,3},{3,2},{4,5},{5,4},{6,7},{7,6},{8,9},{9,8},{10,11... | collective-permute-start | bytes 3686408 | tf_op jit(solution)/shard_map/ppermute | solution.py:69
  63.6 10.0 %collective-permute-start.10 = (bf16[4,24,3072]{2,1,0:T(8,128)(2,1)S(1)}, bf16[4,24,3072]{2,1,0:T(8,128)(2,1)}, u32[]{:S(2)}, u32[]{:S(2)}) collective-permute-start(bf16[4,24,3072]{2,1,0:T(8,128)(2,1)S(1)} %pad_maximum_fusion.5), channel_id=1, source_target_pairs={{0,8},{1,17},{2,10},{3,19},{4,12},{5,21},{6,14},{7,23},{8,0},{9,25... | collective-permute-start | bytes 1769480 | tf_op jit(solution)/shard_map/ppermute | solution.py:66
  65.1 15.3 %collective-permute-start.11 = (bf16[160,768]{1,0:T(8,128)(2,1)S(1)}, bf16[160,768]{1,0:T(8,128)(2,1)}, u32[]{:S(2)}, u32[]{:S(2)}) collective-permute-start(bf16[160,768]{1,0:T(8,128)(2,1)S(1)} %copy-done.22), channel_id=1, source_target_pairs={{0,4},{1,5},{2,6},{3,7},{4,0},{5,1},{6,2},{7,3},{8,12},{9,13},{10,... | collective-permute-start | bytes 737288 | tf_op jit(solution)/shard_map/ppermute | solution.py:72
  65.4 28.5 %collective-permute-start.13 = (s32[512]{0:T(512)S(1)}, s32[512]{0:T(512)S(1)}, u32[]{:S(2)}, u32[]{:S(2)}) collective-permute-start(s32[512]{0:T(512)S(1)} %get-tuple-element.634), channel_id=1, source_target_pairs={{0,4},{1,5},{2,6},{3,7},{4,0},{5,1},{6,2},{7,3},{8,12},{9,13},{10,... | collective-permute-start | bytes 6152 | tf_op jit(solution)/shard_map/ppermute | solution.py:72
  81.5 27.6 %collective-permute-start.14 = (bf16[8,24,3072]{2,1,0:T(8,128)(2,1)S(1)}, bf16[8,24,3072]{2,1,0:T(8,128)(2,1)}, u32[]{:S(2)}, u32[]{:S(2)}) collective-permute-start(bf16[8,24,3072]{2,1,0:T(8,128)(2,1)S(1)} %pad_maximum_fusion.1.refs_0_), channel_id=1, source_target_pairs={{0,16},{1,9},{2,18},{3,11},{4,20},{5,13},{6,22},{7,15},{8,24},{9,1... | collective-permute-start | bytes 3538952 | tf_op jit(solution)/shard_map/ppermute | solution.py:66
  83.3 9.1 %collective-permute-start.12 = (bf16[1,96,768]{2,1,0:T(8,128)(2,1)S(1)}, bf16[1,96,768]{2,1,0:T(8,128)(2,1)S(1)}, u32[]{:S(2)}, u32[]{:S(2)}) collective-permute-start(bf16[1,96,768]{2,1,0:T(8,128)(2,1)S(1)} %copy-done.38), channel_id=1, source_target_pairs={{0,4},{1,5},{2,6},{3,7},{4,0},{5,1},{6,2},{7,3},{8,12},{9,13},{10,... | collective-permute-start | bytes 442376 | tf_op jit(solution)/shard_map/ppermute | solution.py:66
  92.4 14.1 %collective-permute-start.15 = (bf16[2,96,768]{2,1,0:T(8,128)(2,1)S(1)}, bf16[2,96,768]{2,1,0:T(8,128)(2,1)S(1)}, u32[]{:S(2)}, u32[]{:S(2)}) collective-permute-start(bf16[2,96,768]{2,1,0:T(8,128)(2,1)S(1)} %pad_maximum_fusion.10), channel_id=1, source_target_pairs={{0,2},{1,3},{2,0},{3,1},{4,6},{5,7},{6,4},{7,5},{8,10},{9,11},{10,... | collective-permute-start | bytes 884744 | tf_op jit(solution)/shard_map/ppermute | solution.py:66
  94.5 25.9 %collective-permute-start.17 = (bf16[8,24,3072]{2,1,0:T(8,128)(2,1)S(1)}, bf16[8,24,3072]{2,1,0:T(8,128)(2,1)}, u32[]{:S(2)}, u32[]{:S(2)}) collective-permute-start(bf16[8,24,3072]{2,1,0:T(8,128)(2,1)S(1)} %pad_maximum_fusion.1.refs_0_), channel_id=1, source_target_pairs={{0,1},{1,0},{2,3},{3,2},{4,5},{5,4},{6,7},{7,6},{8,9},{9,8},{10,11... | collective-permute-start | bytes 3538952 | tf_op jit(solution)/shard_map/ppermute | solution.py:69
  94.5 14.6 %collective-permute-start.16 = (bf16[160,768]{1,0:T(8,128)(2,1)S(1)}, bf16[160,768]{1,0:T(8,128)(2,1)S(1)}, u32[]{:S(2)}, u32[]{:S(2)}) collective-permute-start(bf16[160,768]{1,0:T(8,128)(2,1)S(1)} %copy-done.21), channel_id=1, source_target_pairs={{0,4},{1,5},{2,6},{3,7},{4,0},{5,1},{6,2},{7,3},{8,12},{9,13},{10,... | collective-permute-start | bytes 737288 | tf_op jit(solution)/shard_map/ppermute | solution.py:72
  109.1 12.4 %collective-permute-start.18 = (bf16[8,24,3072]{2,1,0:T(8,128)(2,1)}, bf16[8,24,3072]{2,1,0:T(8,128)(2,1)}, u32[]{:S(2)}, u32[]{:S(2)}) collective-permute-start(bf16[8,24,3072]{2,1,0:T(8,128)(2,1)} %collective-permute-done.14.refs_1_), channel_id=1, source_target_pairs={{0,1},{1,0},{2,3},{3,2},{4,5},{5,4},{6,7},{7,6},{8,9},{9,8},{10,11... | collective-permute-start | bytes 3538952 | tf_op jit(solution)/shard_map/ppermute | solution.py:69
  109.1 10.1 %collective-permute-start.19 = (bf16[4,96,768]{2,1,0:T(8,128)(2,1)S(1)}, bf16[4,96,768]{2,1,0:T(8,128)(2,1)}, u32[]{:S(2)}, u32[]{:S(2)}) collective-permute-start(bf16[4,96,768]{2,1,0:T(8,128)(2,1)S(1)} %pad_maximum_fusion.6), channel_id=1, source_target_pairs={{0,8},{1,17},{2,10},{3,19},{4,12},{5,21},{6,14},{7,23},{8,0},{9,25... | collective-permute-start | bytes 1769480 | tf_op jit(solution)/shard_map/ppermute | solution.py:66
  111.7 9.8 %collective-permute-start.20 = (bf16[96,768]{1,0:T(8,128)(2,1)}, bf16[96,768]{1,0:T(8,128)(2,1)S(1)}, u32[]{:S(2)}, u32[]{:S(2)}) collective-permute-start(bf16[96,768]{1,0:T(8,128)(2,1)} %get-tuple-element.340), channel_id=1, source_target_pairs={{0,4},{1,5},{2,6},{3,7},{4,0},{5,1},{6,2},{7,3},{8,12},{9,13},{10,... | collective-permute-start | bytes 442376 | tf_op jit(solution)/shard_map/ppermute | solution.py:72
  121.5 17.1 %collective-permute-start.21 = (bf16[8,96,768]{2,1,0:T(8,128)(2,1)S(1)}, bf16[8,96,768]{2,1,0:T(8,128)(2,1)}, u32[]{:S(2)}, u32[]{:S(2)}) collective-permute-start(bf16[8,96,768]{2,1,0:T(8,128)(2,1)S(1)} %pad_maximum_fusion.2.refs_0_), channel_id=1, source_target_pairs={{0,16},{1,9},{2,18},{3,11},{4,20},{5,13},{6,22},{7,15},{8,24},{9,1... | collective-permute-start | bytes 3538952 | tf_op jit(solution)/shard_map/ppermute | solution.py:66
  122.0 16.6 %collective-permute-start.22 = (bf16[8,96,768]{2,1,0:T(8,128)(2,1)S(1)}, bf16[8,96,768]{2,1,0:T(8,128)(2,1)}, u32[]{:S(2)}, u32[]{:S(2)}) collective-permute-start(bf16[8,96,768]{2,1,0:T(8,128)(2,1)S(1)} %pad_maximum_fusion.2.refs_0_), channel_id=1, source_target_pairs={{0,1},{1,0},{2,3},{3,2},{4,5},{5,4},{6,7},{7,6},{8,9},{9,8},{10,11... | collective-permute-start | bytes 3538952 | tf_op jit(solution)/shard_map/ppermute | solution.py:69
  128.4 10.2 %collective-permute-start.23 = (bf16[96,768]{1,0:T(8,128)(2,1)S(1)}, bf16[96,768]{1,0:T(8,128)(2,1)S(1)}, u32[]{:S(2)}, u32[]{:S(2)}) collective-permute-start(bf16[96,768]{1,0:T(8,128)(2,1)S(1)} %copy-done.37), channel_id=1, source_target_pairs={{0,4},{1,5},{2,6},{3,7},{4,0},{5,1},{6,2},{7,3},{8,12},{9,13},{10,... | collective-permute-start | bytes 442376 | tf_op jit(solution)/shard_map/ppermute | solution.py:72
  138.6 9.5 %collective-permute-start.24 = (bf16[8,96,768]{2,1,0:T(8,128)(2,1)}, bf16[8,96,768]{2,1,0:T(8,128)(2,1)S(1)}, u32[]{:S(2)}, u32[]{:S(2)}) collective-permute-start(bf16[8,96,768]{2,1,0:T(8,128)(2,1)} %collective-permute-done.21.refs_1_), channel_id=1, source_target_pairs={{0,1},{1,0},{2,3},{3,2},{4,5},{5,4},{6,7},{7,6},{8,9},{9,8},{10,11... | collective-permute-start | bytes 3538952 | tf_op jit(solution)/shard_map/ppermute | solution.py:69
  139.3 8.8 %collective-permute-start.25 = (bf16[64,768]{1,0:T(8,128)(2,1)S(1)}, bf16[64,768]{1,0:T(8,128)(2,1)S(1)}, u32[]{:S(2)}, u32[]{:S(2)}) collective-permute-start(bf16[64,768]{1,0:T(8,128)(2,1)S(1)} %copy-done.40), channel_id=1, source_target_pairs={{0,4},{1,5},{2,6},{3,7},{4,0},{5,1},{6,2},{7,3},{8,12},{9,13},{10,... | collective-permute-start | bytes 294920 | tf_op jit(solution)/shard_map/ppermute | solution.py:72
  154.1 13.8 %collective-permute-start.26 = (bf16[96,768]{1,0:T(8,128)(2,1)S(1)}, bf16[96,768]{1,0:T(8,128)(2,1)S(1)}, u32[]{:S(2)}, u32[]{:S(2)}) collective-permute-start(bf16[96,768]{1,0:T(8,128)(2,1)S(1)} %copy-done.36), channel_id=1, source_target_pairs={{0,4},{1,5},{2,6},{3,7},{4,0},{5,1},{6,2},{7,3},{8,12},{9,13},{10,... | collective-permute-start | bytes 442376 | tf_op jit(solution)/shard_map/ppermute | solution.py:72
  199.9 11.7 %collective-permute-start.32 = (bf16[128,768]{1,0:T(8,128)(2,1)S(1)}, bf16[128,768]{1,0:T(8,128)(2,1)S(1)}, u32[]{:S(2)}, u32[]{:S(2)}) collective-permute-start(bf16[128,768]{1,0:T(8,128)(2,1)S(1)} %get-tuple-element.401), channel_id=1, source_target_pairs={{0,4},{1,5},{2,6},{3,7},{4,0},{5,1},{6,2},{7,3},{8,12},{9,13},{10,... | collective-permute-start | bytes 589832 | tf_op jit(solution)/shard_map/ppermute | solution.py:72
  211.7 13.3 %collective-permute-start.33 = (bf16[16,96,768]{2,1,0:T(8,128)(2,1)}, bf16[16,96,768]{2,1,0:T(8,128)(2,1)S(1)}, u32[]{:S(2)}, u32[]{:S(2)}) collective-permute-start(bf16[16,96,768]{2,1,0:T(8,128)(2,1)} %get-tuple-element.406), channel_id=1, source_target_pairs={{0,1},{1,0},{2,3},{3,2},{4,5},{5,4},{6,7},{7,6},{8,9},{9,8},{10,11... | collective-permute-start | bytes 7077896 | tf_op jit(solution)/shard_map/ppermute | solution.py:69
  211.7 13.3 %collective-permute-start.34 = (bf16[128,768]{1,0:T(8,128)(2,1)S(1)}, bf16[128,768]{1,0:T(8,128)(2,1)S(1)}, u32[]{:S(2)}, u32[]{:S(2)}) collective-permute-start(bf16[128,768]{1,0:T(8,128)(2,1)S(1)} %copy-done.29), channel_id=1, source_target_pairs={{0,4},{1,5},{2,6},{3,7},{4,0},{5,1},{6,2},{7,3},{8,12},{9,13},{10,... | collective-permute-start | bytes 589832 | tf_op jit(solution)/shard_map/ppermute | solution.py:72
  225.7 26.6 %collective-permute-start.35 = (bf16[8,96,768]{2,1,0:T(8,128)(2,1)S(1)}, bf16[8,96,768]{2,1,0:T(8,128)(2,1)S(1)}, u32[]{:S(2)}, u32[]{:S(2)}) collective-permute-start(bf16[8,96,768]{2,1,0:T(8,128)(2,1)S(1)} %add_convert_fusion.1), channel_id=1, source_target_pairs={{0,16},{1,9},{2,18},{3,11},{4,20},{5,13},{6,22},{7,15},{8,24},{9,1... | collective-permute-start | bytes 3538952 | tf_op jit(solution)/shard_map/ppermute | solution.py:66
  227.0 11.7 %collective-permute-start.36 = (bf16[128,768]{1,0:T(8,128)(2,1)S(1)}, bf16[128,768]{1,0:T(8,128)(2,1)S(1)}, u32[]{:S(2)}, u32[]{:S(2)}) collective-permute-start(bf16[128,768]{1,0:T(8,128)(2,1)S(1)} %get-tuple-element.421), channel_id=1, source_target_pairs={{0,4},{1,5},{2,6},{3,7},{4,0},{5,1},{6,2},{7,3},{8,12},{9,13},{10,... | collective-permute-start | bytes 589832 | tf_op jit(solution)/shard_map/ppermute | solution.py:72
  238.7 13.6 %collective-permute-start.37 = (bf16[128,768]{1,0:T(8,128)(2,1)S(1)}, bf16[128,768]{1,0:T(8,128)(2,1)S(1)}, u32[]{:S(2)}, u32[]{:S(2)}) collective-permute-start(bf16[128,768]{1,0:T(8,128)(2,1)S(1)} %copy-done.28), channel_id=1, source_target_pairs={{0,4},{1,5},{2,6},{3,7},{4,0},{5,1},{6,2},{7,3},{8,12},{9,13},{10,... | collective-permute-start | bytes 589832 | tf_op jit(solution)/shard_map/ppermute | solution.py:72
  257.4 18.8 %collective-permute-start.39 = (bf16[16,24,3840]{2,1,0:T(8,128)(2,1)}, bf16[16,24,3840]{2,1,0:T(8,128)(2,1)S(1)}, u32[]{:S(2)}, u32[]{:S(2)}) collective-permute-start(bf16[16,24,3840]{2,1,0:T(8,128)(2,1)} %get-tuple-element.443), channel_id=1, source_target_pairs={{0,1},{1,0},{2,3},{3,2},{4,5},{5,4},{6,7},{7,6},{8,9},{9,8},{10,11... | collective-permute-start | bytes 8847368 | tf_op jit(solution)/shard_map/ppermute | solution.py:69
  259.7 16.5 %collective-permute-start.38 = (bf16[4,96,768]{2,1,0:T(8,128)(2,1)}, bf16[4,96,768]{2,1,0:T(8,128)(2,1)S(1)}, u32[]{:S(2)}, u32[]{:S(2)}) collective-permute-start(bf16[4,96,768]{2,1,0:T(8,128)(2,1)} %add_convert_fusion.4), channel_id=1, source_target_pairs={{0,8},{1,17},{2,10},{3,19},{4,12},{5,21},{6,14},{7,23},{8,0},{9,25... | collective-permute-start | bytes 1769480 | tf_op jit(solution)/shard_map/ppermute | solution.py:66
  280.5 24.0 %collective-permute-start.41 = (bf16[8,24,3840]{2,1,0:T(8,128)(2,1)}, bf16[8,24,3840]{2,1,0:T(8,128)(2,1)}, u32[]{:S(2)}, u32[]{:S(2)}) collective-permute-start(bf16[8,24,3840]{2,1,0:T(8,128)(2,1)} %add_convert_fusion), channel_id=1, source_target_pairs={{0,16},{1,9},{2,18},{3,11},{4,20},{5,13},{6,22},{7,15},{8,24},{9,1... | collective-permute-start | bytes 4423688 | tf_op jit(solution)/shard_map/ppermute | solution.py:66
  281.7 22.8 %collective-permute-start.40 = (bf16[2,96,768]{2,1,0:T(8,128)(2,1)}, bf16[2,96,768]{2,1,0:T(8,128)(2,1)}, u32[]{:S(2)}, u32[]{:S(2)}) collective-permute-start(bf16[2,96,768]{2,1,0:T(8,128)(2,1)} %add_convert_fusion.7), channel_id=1, source_target_pairs={{0,2},{1,3},{2,0},{3,1},{4,6},{5,7},{6,4},{7,5},{8,10},{9,11},{10,... | collective-permute-start | bytes 884744 | tf_op jit(solution)/shard_map/ppermute | solution.py:66
  289.0 15.4 %collective-permute-start.42 = (bf16[160,768]{1,0:T(8,128)(2,1)}, bf16[160,768]{1,0:T(8,128)(2,1)}, u32[]{:S(2)}, u32[]{:S(2)}) collective-permute-start(bf16[160,768]{1,0:T(8,128)(2,1)} %get-tuple-element.471), channel_id=1, source_target_pairs={{0,4},{1,5},{2,6},{3,7},{4,0},{5,1},{6,2},{7,3},{8,12},{9,13},{10,... | collective-permute-start | bytes 737288 | tf_op jit(solution)/shard_map/ppermute | solution.py:72
  306.2 17.6 %collective-permute-start.43 = (bf16[4,24,3840]{2,1,0:T(8,128)(2,1)S(1)}, bf16[4,24,3840]{2,1,0:T(8,128)(2,1)S(1)}, u32[]{:S(2)}, u32[]{:S(2)}) collective-permute-start(bf16[4,24,3840]{2,1,0:T(8,128)(2,1)S(1)} %add_convert_fusion.3), channel_id=1, source_target_pairs={{0,8},{1,17},{2,10},{3,19},{4,12},{5,21},{6,14},{7,23},{8,0},{9,25... | collective-permute-start | bytes 2211848 | tf_op jit(solution)/shard_map/ppermute | solution.py:66
  308.3 12.9 %collective-permute-start.44 = (bf16[1,96,768]{2,1,0:T(8,128)(2,1)S(1)}, bf16[1,96,768]{2,1,0:T(8,128)(2,1)S(1)}, u32[]{:S(2)}, u32[]{:S(2)}) collective-permute-start(bf16[1,96,768]{2,1,0:T(8,128)(2,1)S(1)} %add_convert_fusion.10), channel_id=1, source_target_pairs={{0,4},{1,5},{2,6},{3,7},{4,0},{5,1},{6,2},{7,3},{8,12},{9,13},{10,... | collective-permute-start | bytes 442376 | tf_op jit(solution)/shard_map/ppermute | solution.py:66
  310.4 13.4 %collective-permute-start.45 = (bf16[96,768]{1,0:T(8,128)(2,1)S(1)}, bf16[96,768]{1,0:T(8,128)(2,1)S(1)}, u32[]{:S(2)}, u32[]{:S(2)}) collective-permute-start(bf16[96,768]{1,0:T(8,128)(2,1)S(1)} %copy-done.58), channel_id=1, source_target_pairs={{0,4},{1,5},{2,6},{3,7},{4,0},{5,1},{6,2},{7,3},{8,12},{9,13},{10,... | collective-permute-start | bytes 442376 | tf_op jit(solution)/shard_map/ppermute | solution.py:72
  323.8 9.9 %collective-permute-start.46 = (bf16[16,24,2432]{2,1,0:T(8,128)(2,1)}, bf16[16,24,2432]{2,1,0:T(8,128)(2,1)S(1)}, u32[]{:S(2)}, u32[]{:S(2)}) collective-permute-start(bf16[16,24,2432]{2,1,0:T(8,128)(2,1)} %get-tuple-element.504), channel_id=1, source_target_pairs={{0,1},{1,0},{2,3},{3,2},{4,5},{5,4},{6,7},{7,6},{8,9},{9,8},{10,11... | collective-permute-start | bytes 5603336 | tf_op jit(solution)/shard_map/ppermute | solution.py:69
  323.9 9.8 %collective-permute-start.47 = (bf16[96,768]{1,0:T(8,128)(2,1)S(1)}, bf16[96,768]{1,0:T(8,128)(2,1)S(1)}, u32[]{:S(2)}, u32[]{:S(2)}) collective-permute-start(bf16[96,768]{1,0:T(8,128)(2,1)S(1)} %copy-done.57), channel_id=1, source_target_pairs={{0,4},{1,5},{2,6},{3,7},{4,0},{5,1},{6,2},{7,3},{8,12},{9,13},{10,... | collective-permute-start | bytes 442376 | tf_op jit(solution)/shard_map/ppermute | solution.py:72
  335.2 18.3 %collective-permute-start.48 = (bf16[8,24,2432]{2,1,0:T(8,128)(2,1)}, bf16[8,24,2432]{2,1,0:T(8,128)(2,1)}, u32[]{:S(2)}, u32[]{:S(2)}) collective-permute-start(bf16[8,24,2432]{2,1,0:T(8,128)(2,1)} %add_convert_fusion.2), channel_id=1, source_target_pairs={{0,16},{1,9},{2,18},{3,11},{4,20},{5,13},{6,22},{7,15},{8,24},{9,1... | collective-permute-start | bytes 2801672 | tf_op jit(solution)/shard_map/ppermute | solution.py:66
  337.8 15.8 %collective-permute-start.49 = (bf16[2,24,3840]{2,1,0:T(8,128)(2,1)S(1)}, bf16[2,24,3840]{2,1,0:T(8,128)(2,1)}, u32[]{:S(2)}, u32[]{:S(2)}) collective-permute-start(bf16[2,24,3840]{2,1,0:T(8,128)(2,1)S(1)} %add_convert_fusion.6), channel_id=1, source_target_pairs={{0,2},{1,3},{2,0},{3,1},{4,6},{5,7},{6,4},{7,5},{8,10},{9,11},{10,... | collective-permute-start | bytes 1105928 | tf_op jit(solution)/shard_map/ppermute | solution.py:66
  337.8 15.7 %collective-permute-start.50 = (bf16[160,768]{1,0:T(8,128)(2,1)}, bf16[160,768]{1,0:T(8,128)(2,1)}, u32[]{:S(2)}, u32[]{:S(2)}) collective-permute-start(bf16[160,768]{1,0:T(8,128)(2,1)} %get-tuple-element.519), channel_id=1, source_target_pairs={{0,4},{1,5},{2,6},{3,7},{4,0},{5,1},{6,2},{7,3},{8,12},{9,13},{10,... | collective-permute-start | bytes 737288 | tf_op jit(solution)/shard_map/ppermute | solution.py:72
  354.9 10.5 %collective-permute-start.52 = (bf16[1,24,3840]{2,1,0:T(8,128)(2,1)S(1)}, bf16[1,24,3840]{2,1,0:T(8,128)(2,1)S(1)}, u32[]{:S(2)}, u32[]{:S(2)}) collective-permute-start(bf16[1,24,3840]{2,1,0:T(8,128)(2,1)S(1)} %add_convert_fusion.9), channel_id=1, source_target_pairs={{0,4},{1,5},{2,6},{3,7},{4,0},{5,1},{6,2},{7,3},{8,12},{9,13},{10,... | collective-permute-start | bytes 552968 | tf_op jit(solution)/shard_map/ppermute | solution.py:66
  357.6 9.2 %collective-permute-start.51 = (bf16[4,24,2432]{2,1,0:T(8,128)(2,1)S(1)}, bf16[4,24,2432]{2,1,0:T(8,128)(2,1)S(1)}, u32[]{:S(2)}, u32[]{:S(2)}) collective-permute-start(bf16[4,24,2432]{2,1,0:T(8,128)(2,1)S(1)} %add_convert_fusion.5), channel_id=1, source_target_pairs={{0,8},{1,17},{2,10},{3,19},{4,12},{5,21},{6,14},{7,23},{8,0},{9,25... | collective-permute-start | bytes 1400840 | tf_op jit(solution)/shard_map/ppermute | solution.py:66
  (66 other events, 548.6 us)

commit v10 on v9

--- a/solution.py
+++ b/solution.py
@@ -921,7 +921,7 @@
     qid = seq.reshape(rows, 1)
     g1, g2, g3 = Gather(first), Gather(second), Gather(third)
     my_tokens, send_tokens = sides(rows_q, rows_p)
-    tokens_out = chunked(send_tokens, (5, 6, 5))
+    tokens_out = chunked(send_tokens, (5, 4, 7))
     g1.mid()
     g1.send, tokens_out, question_cot, passage_cot = tie(
         g1.send, tokens_out, question_cot, passage_cot
@@ -963,7 +963,7 @@
     bias_j = jnp.concatenate([vec[0], jnp.zeros((D,), F32), vec[1]])
     tokens, qkv = project([my_tokens] + tokens_in, wj, bias_j[None])
 
-    cot_out = chunked(send_cot, (5, 3, 3, 2, 3))
+    cot_out = chunked(send_cot, (4, 3, 3, 2, 4))
     by_pa = positive.reshape(places.pa_n, nq)
     pair = [lax.dynamic_index_in_dim(by_pa, low_pa + k, 0, keepdims=False) for k in (0, shift)]
     pair = jnp.concatenate(pair)[None]
@@ -1110,7 +1110,10 @@
                 self.move(step)
 
         def mid(self):
-            got = places.swap(self.total(1, 2).astype(BF16), 0).astype(F32)
+            if self.send is None:
+                self.prepare()
+            got = places.swap(self.send, 0).astype(F32)
+            self.send = None
             keep = self.total(0, 1)
             self.out = jnp.concatenate(
                 [jnp.where(is_q, keep, got), jnp.where(is_q, got, keep)], axis=0
@@ -1133,21 +1136,27 @@
         partial = gradient(mid_low, d_expanded, room=D)
     else:
         partial = plain(mid_low, d_expanded)
-    partial, d_expanded, got_out, send_out = tie(partial, d_expanded, got_out, send_out)
+    sr.parts, partial, d_expanded, got_out, send_out = tie(
+        sr.parts, partial, d_expanded, got_out, send_out
+    )
+    sr.pb_rest()
     got_out = got_out + hand(send_out[3:])
     d_first, d_attended, sums_first = first_back(
         d_expanded, we, d_second, norm_one, inverse_one, vec[3][None, :]
     )
     sr.parts, partial, d_attended, got_out = tie(sr.parts, partial, d_attended, got_out)
-    sr.pb_rest()
     if even:
         partial = gradient(context, d_attended, into=tuple(partial))
     else:
         also = plain(context, d_attended)
         partial = [jnp.concatenate(x, axis=2) for x in zip(partial, also)]
     se = Scatter(*partial)
-    se.parts, se.theirs, d_attended = tie(se.parts, se.theirs, d_attended)
+    sr.prepare()
+    se.parts, se.theirs, sr.send, sr.parts, d_attended = tie(
+        se.parts, se.theirs, sr.send, sr.parts, d_attended
+    )
     se.cores()
+    sr.along_z()
     d_context = dot(d_attended, wo, ((1,), (1,))).astype(BF16)
     d_joined, sums_one = attention_back(qkv, probs, d_context, later, blocks - later)
     sr.parts, se.parts, d_joined = tie(sr.parts, se.parts, d_joined)
@@ -1157,38 +1166,37 @@
         sr.send, sr.parts, se.send, se.parts, d_joined
     )
     se.pb_first()
-    sr.along_z()
+    sr.mid()
     part = own_rows // 16
-    send_grad = token_grad(d_joined, wj, d_first, own_rows, [k * part for k in (5, 3, 3, 5)], BF16)
-    d_joined, send_grad = tie(d_joined, send_grad)
+    send_grad = token_grad(d_joined, wj, d_first, own_rows, [k * part for k in (5, 5, 4, 2)], BF16)
+    d_joined, send_grad, sr.out = tie(d_joined, send_grad, sr.out)
     got_grad = hand(send_grad[:1])
     d_joined, sums_two = attention_back(qkv, probs, d_context, 0, later, d_joined)
-    sr.parts, se.parts, d_joined, sums_two, got_grad, send_grad = tie(
-        sr.parts, se.parts, d_joined, sums_two, got_grad, send_grad
+    se.parts, d_joined, sums_two, got_grad, send_grad = tie(
+        se.parts, d_joined, sums_two, got_grad, send_grad
     )
     se.prepare()
     se.send, se.parts, d_joined, send_grad = tie(se.send, se.parts, d_joined, send_grad)
     se.pb_rest()
-    sr.mid()
     got_grad = got_grad + hand(send_grad[1:2])
     bias_sums = g_bias_expand.reshape(D, 4).T
     small_sums = (sums_one, sums_two, sums_first, sums_second, bias_sums)
     sj = Scatter(*(gradient if even else plain)(tokens, d_joined, extra=small_sums))
-    se.parts, sr.out, sj.parts, sj.theirs, d_joined, got_grad, send_grad = tie(
-        se.parts, sr.out, sj.parts, sj.theirs, d_joined, got_grad, send_grad
+    se.parts, sj.parts, sj.theirs, d_joined, got_grad, send_grad = tie(
+        se.parts, sj.parts, sj.theirs, d_joined, got_grad, send_grad
     )
     sj.cores()
+    se.along_z()
+    (own_grad,) = token_grad(d_joined, wj, d_first, 0, [own_rows], F32)
+    sj.parts, se.parts, own_grad, send_grad = tie(sj.parts, se.parts, own_grad, send_grad)
+    sj.pb_first()
     got_grad = got_grad + hand(send_grad[2:3])
-    (own_grad,) = token_grad(d_joined, wj, d_first, 0, [own_rows], F32)
-    sj.parts, own_grad, got_grad, send_grad = tie(sj.parts, own_grad, got_grad, send_grad)
-    sj.pb_first()
-    se.along_z()
-    got_grad = got_grad + hand(send_grad[3:])
     sj.parts, se.parts, got_grad, send_grad = tie(sj.parts, se.parts, got_grad, send_grad)
     sj.pb_rest()
     se.mid()
-    sj.parts, se.out, got_out, out = tie(sj.parts, se.out, got_out, out)
+    sj.parts, se.out, got_out, out, send_grad = tie(sj.parts, se.out, got_out, out, send_grad)
     sj.along_z()
+    got_grad = got_grad + hand(send_grad[3:])
     out_q, out_p = deal(tower.reshape(1), out, got_out)
     sj.parts, out_q, out_p, got_grad = tie(sj.parts, out_q, out_p, got_grad)
     grad_q, grad_p = deal(tower.reshape(1), own_grad, got_grad)

time: 389 us -> 391 us (level)
  waiting for transfers between devices: 83.4 us -> 89.4 us
  other arithmetic: 35.2 us -> 30.7 us
    ppermute x18, waiting for transfers between devices: 24.6 us -> 35.2 us  [swap_tower(): lax.ppermute(values, 'pa', [(i, i ^ 2 * self.half) for i in range(self.pa...]
    ppermute x24, waiting for transfers between devices: 50.2 us -> 45.1 us  [swap(): return lax.ppermute(values, AXES, self.pairs(step))]
    convert_element_type x9 -> x12, other arithmetic: 13.2 us -> 13.5 us  [prepare(): self.send = self.total(self.count // 2, self.count).astype(BF16)]
  transfers between devices with their start and end apart: 55 -> 55, of which waited for: 22 -> 27; matrix products, arithmetic and copies ran while one was open for 10% -> 9% of each run, Pallas kernels for 42% -> 42%
where the time goes in v10:
time: 391 us; the launch traced here: 390 us
  Pallas kernels  179 us (46%)
  waiting for transfers between devices  89.4 us (23%)
  starting transfers between devices  60.4 us (15%)
  other arithmetic  30.7 us (8%)
  local copies, waits for them, and re-layouts  23.6 us (6%)
  matrix products  4.46 us (1%)
    ppermute x24, waiting for transfers between devices, swap(): return lax.ppermute(values, AXES, self.pairs(step))  45.1 us
    ppermute x18, waiting for transfers between devices, swap_tower(): lax.ppermute(values, 'pa', [(i, i ^ 2 * self.half) for i in range(self.pa...  35.2 us
    ppermute x24, starting transfers between devices, swap(): return lax.ppermute(values, AXES, self.pairs(step))  32.4 us
    ppermute x18, starting transfers between devices, swap_tower(): lax.ppermute(values, 'pa', [(i, i ^ 2 * self.half) for i in range(self.pa...  25.4 us
    pallas_call x3, Pallas kernels, weight_grad(): pl.pallas_call(functools.partial(weight_grad_kernel, chips, len(extra or...  24.2 us
    pallas_call x2, Pallas kernels, attention_back(): pl.pallas_call(attention_back_more_kernel if more else attention_back_ker...  23.7 us
    pallas_call x2, Pallas kernels, add_norm(): pl.pallas_call(functools.partial(add_norm_kernel, rows_of), grid=(rows //...  19 us
    pallas_call x2, Pallas kernels, expand(): pl.pallas_call(expand_more_kernel if into else expand_kernel, grid=(count...  15.9 us
  transfers between devices with their start and end apart: 55, of which 27 were waited for; matrix products, arithmetic and copies ran while one was open for 9% of the time, Pallas kernels for 42%

profile of v10, /device:TPU:0, one launch (start us, length us, event | category | flops | bytes accessed | tf_op | source)
XLA Modules:
  0.0 389.7 jit_solution(11816118630568550528)
XLA Ops:
  3.5 4.1 %collective-permute-start = (bf16[1,24,3200]{2,1,0:T(8,128)(2,1)S(1)}, bf16[1,24,3200]{2,1,0:T(8,128)(2,1)S(1)}, u32[]{:S(2)}, u32[]{:S(2)}) collective-permute-start(bf16[1,24,3200]{2,1,0:T(8,128)(2,1)S(1)} %get-tuple-element.639), channel_id=1, source_target_pairs={{0,4},{1,5},{2,6},{3,7},{4,0},{5,1},{6,2},{7,3},{8,12},{9,13},{10,... | collective-permute-start | bytes 460808 | tf_op jit(solution)/shard_map/ppermute | solution.py:66
  12.4 2.5 collective-permute-done
  15.8 3.4 collective-permute-start.2
  20.2 8.5 %collective-permute-done.1 = bf16[2,24,3200]{2,1,0:T(8,128)(2,1)S(1)} collective-permute-done((bf16[2,24,3200]{2,1,0:T(8,128)(2,1)S(1)}, bf16[2,24,3200]{2,1,0:T(8,128)(2,1)S(1)}, u32[]{:S(2)}, u32[]{:S(2)}) %collective-permute-start.1) | collective-permute-done | bytes 307232 | tf_op jit(solution)/shard_map/ppermute | solution.py:66
  30.2 2.6 collective-permute-start.4
  32.8 6.6 %collective-permute-done.4 = bf16[1,24,3072]{2,1,0:T(8,128)(2,1)S(1)} collective-permute-done((bf16[1,24,3072]{2,1,0:T(8,128)(2,1)S(1)}, bf16[1,24,3072]{2,1,0:T(8,128)(2,1)S(1)}, u32[]{:S(2)}, u32[]{:S(2)}) %collective-permute-start.4) | collective-permute-done | bytes 147488 | tf_op jit(solution)/shard_map/ppermute | solution.py:66
  41.0 2.8 collective-permute-start.6
  49.3 8.8 %collective-permute-done.7.refs_2_ = bf16[128,768]{1,0:T(8,128)(2,1)S(1)} collective-permute-done((bf16[128,768]{1,0:T(8,128)(2,1)S(1)}, bf16[128,768]{1,0:T(8,128)(2,1)S(1)}, u32[]{:S(2)}, u32[]{:S(2)}) %collective-permute-start.7) | collective-permute-done | bytes 196640 | tf_op jit(solution)/shard_map/ppermute | solution.py:72
  61.1 2.4 collective-permute-start.13
  63.5 5.3 %collective-permute-done.10 = bf16[4,24,3072]{2,1,0:T(8,128)(2,1)} collective-permute-done((bf16[4,24,3072]{2,1,0:T(8,128)(2,1)S(1)}, bf16[4,24,3072]{2,1,0:T(8,128)(2,1)}, u32[]{:S(2)}, u32[]{:S(2)}) %collective-permute-start.10) | collective-permute-done | bytes 589856 | tf_op jit(solution)/shard_map/ppermute | solution.py:66
  70.0 5.5 %assemble.3 = (bf16[16,2,24,2304]{3,2,1,0:T(8,128)(2,1)}, bf16[16,2,24,768]{3,2,1,0:T(8,128)(2,1)}, bf16[16,2,24,128]{3,2,1,0:T(8,128)(2,1)}) custom-call(s32[3,16]{1,0:T(4,128)} %get-tuple-element.302.idx_ref, bf16[8,24,3200]{2,1,0:T(8,128)(2,1)} %copy-done.1, bf16[8,24,3200]{2,1,0:T(8,128)(2,1)} %collective-permute-done.5.refs_1_, ...), custom_call_target="tpu_custom_call" | custom-call | bytes 9830400 | tf_op jit(solution)/shard_map/assemble/pallas_call | solution.py:118
  75.6 2.4 collective-permute-done.11.refs_3_
  81.9 8.5 %project.1 = (bf16[1024,768]{1,0:T(8,128)(2,1)}, bf16[1024,2304]{1,0:T(8,128)(2,1)}) custom-call(bf16[768,2304]{1,0:T(8,128)(2,1)} %bitcast.65, f32[1,2304]{1,0:T(1,128)} %broadcast_in_dim.14.b_ref, bf16[512,768]{1,0:T(8,128)(2,1)} %get-tuple-element.630.refs_0_, bf16[160,768]{1,0:T(8,128)(2,1)} %copy-done.54, bf16[128,768]{1,0:T(8,128)(2,1)} %copy-done.55, ...), custom_call_target="tpu_custom_call" | custom-call | flops 3623878656 | bytes 11403264 | tf_op jit(solution)/shard_map/project/pallas_call | solution.py:716
  93.9 10.6 %attention.1 = (bf16[1024,768]{1,0:T(8,128)(2,1)}, bf16[4,12,256,256]{3,2,1,0:T(8,128)(2,1)}) custom-call(bf16[1024,2304]{1,0:T(8,128)(2,1)} %get-tuple-element.330.qkv_ref, s32[1024,1]{1,0:T(8,128)} %fusion.2.qid_ref, s32[4,1,256]{2,1,0:T(1,128)} %bitcast.85), custom_call_target="tpu_custom_call" | custom-call | flops 1610612736 | bytes 12582912 | tf_op jit(solution)/shard_map/attention/pallas_call | solution.py:342
  109.4 7.4 %add_norm.2 = (f32[1024,768]{1,0:T(8,128)}, f32[1024,1]{1,0:T(8,128)}, bf16[1024,768]{1,0:T(8,128)(2,1)}, f32[1024,768]{1,0:T(8,128)}) custom-call(bf16[1024,768]{1,0:T(8,128)(2,1)} %get-tuple-element.343.left_ref, bf16[768,768]{1,0:T(8,128)(2,1)} %bitcast.74, bf16[1024,768]{1,0:T(8,128)(2,1)} %get-tuple-element.345.base_ref.left_ref, ...), custom_call_target="tpu_custom_call" | custom-call | flops 1207959552 | bytes 12189696 | tf_op jit(solution)/shard_map/add_norm/pallas_call | solution.py:762
  120.4 4.9 %assemble.4 = bf16[16,2,24,3072]{3,2,1,0:T(8,128)(2,1)} custom-call(s32[3,16]{1,0:T(4,128)} %get-tuple-element.302.idx_ref, bf16[8,24,3072]{2,1,0:T(8,128)(2,1)} %copy-done.2, bf16[8,24,3072]{2,1,0:T(8,128)(2,1)} %collective-permute-done.14.refs_1_, bf16[8,24,3072]{2,1,0:T(8,128)(2,1)} %collective-permute-done.17.refs_2_, ...), custom_call_target="tpu_custom_call" | custom-call | bytes 9437184 | tf_op jit(solution)/shard_map/assemble/pallas_call | solution.py:118
  126.9 7.9 %expand.2 = (bf16[1024,3072]{1,0:T(8,128)(2,1)}, bf16[1024,3072]{1,0:T(8,128)(2,1)}) custom-call(bf16[1024,768]{1,0:T(8,128)(2,1)} %get-tuple-element.362.mid_ref.left_ref, bf16[768,3072]{1,0:T(8,128)(2,1)} %bitcast.62, f32[1,3072]{1,0:T(1,128)} %reshape.500.b_ref), custom_call_target="tpu_custom_call" | custom-call | flops 2415919104 | bytes 10223616 | tf_op jit(solution)/shard_map/expand/pallas_call | solution.py:638
  137.0 8.0 %expand.3 = (bf16[1024,3072]{1,0:T(8,128)(2,1)}, bf16[1024,3072]{1,0:T(8,128)(2,1)}) custom-call(bf16[1024,768]{1,0:T(8,128)(2,1)} %get-tuple-element.362.mid_ref.left_ref, bf16[768,3072]{1,0:T(8,128)(2,1)} %bitcast.63, f32[1,3072]{1,0:T(1,128)} %reshape.500.b_ref, ...), custom_call_target="tpu_custom_call", output_to_operand_aliasing={{0}: (3, {}), {1}: (4, {})} | custom-call | flops 2415919104 | bytes 10223616 | tf_op jit(solution)/shard_map/expand/pallas_call | solution.py:638
  146.0 4.8 %assemble.5 = bf16[16,2,96,768]{3,2,1,0:T(8,128)(2,1)} custom-call(s32[3,16]{1,0:T(4,128)} %get-tuple-element.302.idx_ref, bf16[8,96,768]{2,1,0:T(8,128)(2,1)} %copy-done.3, bf16[8,96,768]{2,1,0:T(8,128)(2,1)} %collective-permute-done.21.refs_1_, bf16[8,96,768]{2,1,0:T(8,128)(2,1)} %collective-permute-done.22.refs_2_, bf16[8,96,768]{2,1,0:T(8,128)(2,1)} %copy-done.11), custom_call_target="tpu_custom_call" | custom-call | bytes 9437184 | tf_op jit(solution)/shard_map/assemble/pallas_call | solution.py:118
  150.8 2.3 collective-permute-start.26
  153.1 11.6 %add_norm.3 = (f32[1024,768]{1,0:T(8,128)}, f32[1024,1]{1,0:T(8,128)}, bf16[1024,768]{1,0:T(8,128)(2,1)}) custom-call(bf16[1024,3072]{1,0:T(8,128)(2,1)} %get-tuple-element.383.left_ref, bf16[3072,768]{1,0:T(8,128)(2,1)} %bitcast.68, f32[1024,768]{1,0:T(8,128)} %get-tuple-element.391.base_ref, f32[1024,1]{1,0:T(8,128)} %convert_element_type.272.mask_ref, ...), custom_call_target="tpu_custom_call" | custom-call | flops 4831838208 | bytes 20447232 | tf_op jit(solution)/shard_map/add_norm/pallas_call | solution.py:762
  166.5 4.0 %collective-permute-done.27 = bf16[16,768]{1,0:T(8,128)(2,1)S(1)} collective-permute-done((bf16[16,768]{1,0:T(8,128)(2,1)S(1)}, bf16[16,768]{1,0:T(8,128)(2,1)S(1)}, u32[]{:S(2)}, u32[]{:S(2)}) %collective-permute-start.27) | collective-permute-done | bytes 24608 | tf_op jit(solution)/shard_map/ppermute | solution.py:72
  171.0 3.6 collective-permute-done.28
  175.6 1.9 fusion.35
  177.5 2.7 join.1.cot_ref
  181.6 3.8 collective-permute-done.30
  189.9 6.5 %second_back.1 = (f32[1024,768]{1,0:T(8,128)}, bf16[1024,768]{1,0:T(8,128)(2,1)}, f32[8,768]{1,0:T(8,128)}) custom-call(bf16[1024,768]{1,0:T(8,128)(2,1)} %join.1.cot_ref, f32[4,4,768]{2,1,0:T(4,128)} %reshape.508.slot_ref, f32[1024,1]{1,0:T(8,128)} %convert_element_type.272.mask_ref, f32[1024,768]{1,0:T(8,128)} %get-tuple-element.405.norm_ref, ...), custom_call_target="tpu_custom_call" | custom-call | flops 15728640 | bytes 9437184 | tf_op jit(solution)/shard_map/second_back/pallas_call | solution.py:556
  197.2 10.2 %tall_grad.1 = (bf16[16,96,768]{2,1,0:T(8,128)(2,1)}, bf16[16,96,768]{2,1,0:T(8,128)(2,1)}) custom-call(s32[3,16]{1,0:T(4,128)} %get-tuple-element.301.table_ref, bf16[1024,3072]{1,0:T(8,128)(2,1)} %get-tuple-element.383.left_ref, bf16[1024,768]{1,0:T(8,128)(2,1)} %get-tuple-element.417.right_ref.grad_ref), custom_call_target="tpu_custom_call" | custom-call | flops 4831838208 | bytes 12582912 | tf_op jit(solution)/shard_map/tall_grad/pallas_call | solution.py:243
  210.3 11.8 %hidden_grad.1 = (bf16[1024,3072]{1,0:T(8,128)(2,1)}, f32[1,3072]{1,0:T(1,128)}) custom-call(bf16[1024,768]{1,0:T(8,128)(2,1)} %get-tuple-element.417.right_ref.grad_ref, bf16[3072,768]{1,0:T(8,128)(2,1)} %bitcast.69, bf16[1024,3072]{1,0:T(8,128)(2,1)} %get-tuple-element.418.slope_ref), custom_call_target="tpu_custom_call" | custom-call | flops 4831838208 | bytes 18874368 | tf_op jit(solution)/shard_map/hidden_grad/pallas_call | solution.py:289
  225.8 10.0 %weight_grad.3 = (bf16[16,24,3840]{2,1,0:T(8,128)(2,1)}, bf16[16,24,3840]{2,1,0:T(8,128)(2,1)}) custom-call(s32[3,16]{1,0:T(4,128)} %get-tuple-element.301.table_ref, bf16[1024,768]{1,0:T(8,128)(2,1)} %get-tuple-element.362.mid_ref.left_ref, bf16[1024,3072]{1,0:T(8,128)(2,1)} %get-tuple-element.438.right_ref.hidden_ref), custom_call_target="tpu_custom_call" | custom-call | flops 4831838208 | bytes 12582912 | tf_op jit(solution)/shard_map/weight_grad/pallas_call | solution.py:201
  236.1 3.2 collective-permute-done.35
  242.1 12.3 %first_back.1 = (f32[1024,768]{1,0:T(8,128)}, bf16[1024,768]{1,0:T(8,128)(2,1)}, f32[8,768]{1,0:T(8,128)}) custom-call(bf16[1024,3072]{1,0:T(8,128)(2,1)} %get-tuple-element.438.right_ref.hidden_ref, bf16[768,3072]{1,0:T(8,128)(2,1)} %bitcast.64, f32[1024,768]{1,0:T(8,128)} %get-tuple-element.439.second_ref, f32[1024,768]{1,0:T(8,128)} %get-tuple-element.440.norm_ref, ...), custom_call_target="tpu_custom_call" | custom-call | flops 4831838208 | bytes 22020096 | tf_op jit(solution)/shard_map/first_back/pallas_call | solution.py:596
  255.2 5.2 %weight_grad.4 = (bf16[16,24,3840]{2,1,0:T(8,128)(2,1)}, bf16[16,24,3840]{2,1,0:T(8,128)(2,1)}) custom-call(s32[3,16]{1,0:T(4,128)} %get-tuple-element.301.table_ref, bf16[1024,768]{1,0:T(8,128)(2,1)} %get-tuple-element.343.left_ref, bf16[1024,768]{1,0:T(8,128)(2,1)} %get-tuple-element.464.right_ref, ...), custom_call_target="tpu_custom_call", output_to_operand_aliasing={{0}: (3, {}), {1}: (4, {})} | custom-call | flops 1207959552 | bytes 4325376 | tf_op jit(solution)/shard_map/weight_grad/pallas_call | solution.py:201
  262.3 3.8 convolution_convert_fusion.grad_ref
  266.1 11.9 %attention_back.2 = (bf16[1024,2304]{1,0:T(8,128)(2,1)}, f32[1,2304]{1,0:T(1,128)}) custom-call(bf16[1024,2304]{1,0:T(8,128)(2,1)} %get-tuple-element.330.qkv_ref, bf16[4,12,256,256]{3,2,1,0:T(8,128)(2,1)} %get-tuple-element.463.probs_ref, bf16[1024,768]{1,0:T(8,128)(2,1)} %convolution_convert_fusion.grad_ref), custom_call_target="tpu_custom_call" | custom-call | flops 1610612736 | bytes 8650752 | tf_op jit(solution)/shard_map/attention_back/pallas_call | solution.py:425
  283.5 6.2 %token_grad.2 = (bf16[160,768]{1,0:T(8,128)(2,1)}, bf16[160,768]{1,0:T(8,128)(2,1)}, bf16[128,768]{1,0:T(8,128)(2,1)}, bf16[64,768]{1,0:T(8,128)(2,1)}) custom-call(bf16[1024,2304]{1,0:T(8,128)(2,1)} %get-tuple-element.489.grad_ref._, bf16[768,2304]{1,0:T(8,128)(2,1)} %bitcast.66, f32[1024,768]{1,0:T(8,128)} %get-tuple-element.478.first_ref), custom_call_target="tpu_custom_call" | custom-call | flops 1811939328 | bytes 8257536 | tf_op jit(solution)/shard_map/token_grad/pallas_call | solution.py:682
  289.7 1.9 collective-permute-done.42
  293.8 11.7 %attention_back.3 = (bf16[1024,2304]{1,0:T(8,128)(2,1)}, f32[1,2304]{1,0:T(1,128)}) custom-call(bf16[1024,2304]{1,0:T(8,128)(2,1)} %get-tuple-element.330.qkv_ref, bf16[4,12,256,256]{3,2,1,0:T(8,128)(2,1)} %get-tuple-element.463.probs_ref, bf16[1024,768]{1,0:T(8,128)(2,1)} %convolution_convert_fusion.grad_ref, ...), custom_call_target="tpu_custom_call", output_to_operand_aliasing={{0}: (3, {})} | custom-call | flops 1610612736 | bytes 8650752 | tf_op jit(solution)/shard_map/attention_back/pallas_call | solution.py:425
  313.3 9.0 %weight_grad.5 = (bf16[16,24,2432]{2,1,0:T(8,128)(2,1)}, bf16[16,24,2432]{2,1,0:T(8,128)(2,1)}) custom-call(s32[3,16]{1,0:T(4,128)} %get-tuple-element.301.table_ref, bf16[1024,768]{1,0:T(8,128)(2,1)} %get-tuple-element.345.base_ref.left_ref, bf16[1024,2304]{1,0:T(8,128)(2,1)} %get-tuple-element.525.right_ref.grad_ref, ...), custom_call_target="tpu_custom_call" | custom-call | flops 3623878656 | bytes 9830400 | tf_op jit(solution)/shard_map/weight_grad/pallas_call | solution.py:201
  322.3 3.2 collective-permute-done.45.refs_1_
  327.7 6.6 %token_grad.3.own_ref = f32[512,768]{1,0:T(8,128)} custom-call(bf16[1024,2304]{1,0:T(8,128)(2,1)} %get-tuple-element.525.right_ref.grad_ref, bf16[768,2304]{1,0:T(8,128)(2,1)} %bitcast.67, f32[1024,768]{1,0:T(8,128)} %get-tuple-element.478.first_ref), custom_call_target="tpu_custom_call" | custom-call | flops 1811939328 | bytes 8257536 | tf_op jit(solution)/shard_map/token_grad/pallas_call | solution.py:682
  334.2 4.4 %collective-permute-done.47 = bf16[2,24,3840]{2,1,0:T(8,128)(2,1)S(1)} collective-permute-done((bf16[2,24,3840]{2,1,0:T(8,128)(2,1)S(1)}, bf16[2,24,3840]{2,1,0:T(8,128)(2,1)S(1)}, u32[]{:S(2)}, u32[]{:S(2)}) %collective-permute-start.47) | collective-permute-done | bytes 368672 | tf_op jit(solution)/shard_map/ppermute | solution.py:66
  341.7 11.0 %collective-permute-done.49.refs_2_ = bf16[128,768]{1,0:T(8,128)(2,1)} collective-permute-done((bf16[128,768]{1,0:T(8,128)(2,1)}, bf16[128,768]{1,0:T(8,128)(2,1)}, u32[]{:S(2)}, u32[]{:S(2)}) %collective-permute-start.49) | collective-permute-done | bytes 196640 | tf_op jit(solution)/shard_map/ppermute | solution.py:72
  358.6 7.1 %collective-permute-done.51 = bf16[1,24,3840]{2,1,0:T(8,128)(2,1)S(1)} collective-permute-done((bf16[1,24,3840]{2,1,0:T(8,128)(2,1)S(1)}, bf16[1,24,3840]{2,1,0:T(8,128)(2,1)S(1)}, u32[]{:S(2)}, u32[]{:S(2)}) %collective-permute-start.51) | collective-permute-done | bytes 184352 | tf_op jit(solution)/shard_map/ppermute | solution.py:66
  371.2 2.7 deal.2
  373.9 2.1 collective-permute-done.53.refs_3_
  375.9 2.2 collective-permute-done.52
  382.6 3.5 deal.3
  (320 shorter events, 104.7 us)
Async XLA Ops:
  3.5 11.4 %collective-permute-start = (bf16[1,24,3200]{2,1,0:T(8,128)(2,1)S(1)}, bf16[1,24,3200]{2,1,0:T(8,128)(2,1)S(1)}, u32[]{:S(2)}, u32[]{:S(2)}) collective-permute-start(bf16[1,24,3200]{2,1,0:T(8,128)(2,1)S(1)} %get-tuple-element.639), channel_id=1, source_target_pairs={{0,4},{1,5},{2,6},{3,7},{4,0},{5,1},{6,2},{7,3},{8,12},{9,13},{10,... | collective-permute-start | bytes 460808 | tf_op jit(solution)/shard_map/ppermute | solution.py:66
  15.0 13.8 %collective-permute-start.1 = (bf16[2,24,3200]{2,1,0:T(8,128)(2,1)S(1)}, bf16[2,24,3200]{2,1,0:T(8,128)(2,1)S(1)}, u32[]{:S(2)}, u32[]{:S(2)}) collective-permute-start(bf16[2,24,3200]{2,1,0:T(8,128)(2,1)S(1)} %pad_maximum_fusion.8), channel_id=1, source_target_pairs={{0,2},{1,3},{2,0},{3,1},{4,6},{5,7},{6,4},{7,5},{8,10},{9,11},{10,... | collective-permute-start | bytes 921608 | tf_op jit(solution)/shard_map/ppermute | solution.py:66
  15.8 13.1 %collective-permute-start.2 = (bf16[160,768]{1,0:T(8,128)(2,1)S(1)}, bf16[160,768]{1,0:T(8,128)(2,1)S(1)}, u32[]{:S(2)}, u32[]{:S(2)}) collective-permute-start(bf16[160,768]{1,0:T(8,128)(2,1)S(1)} %slice.382), channel_id=1, source_target_pairs={{0,4},{1,5},{2,6},{3,7},{4,0},{5,1},{6,2},{7,3},{8,12},{9,13},{10,... | collective-permute-start | bytes 737288 | tf_op jit(solution)/shard_map/ppermute | solution.py:72
  28.9 10.6 %collective-permute-start.3 = (bf16[4,24,3200]{2,1,0:T(8,128)(2,1)S(1)}, bf16[4,24,3200]{2,1,0:T(8,128)(2,1)S(1)}, u32[]{:S(2)}, u32[]{:S(2)}) collective-permute-start(bf16[4,24,3200]{2,1,0:T(8,128)(2,1)S(1)} %pad_maximum_fusion.4), channel_id=1, source_target_pairs={{0,8},{1,17},{2,10},{3,19},{4,12},{5,21},{6,14},{7,23},{8,0},{9,25... | collective-permute-start | bytes 1843208 | tf_op jit(solution)/shard_map/ppermute | solution.py:66
  30.2 9.2 %collective-permute-start.4 = (bf16[1,24,3072]{2,1,0:T(8,128)(2,1)S(1)}, bf16[1,24,3072]{2,1,0:T(8,128)(2,1)S(1)}, u32[]{:S(2)}, u32[]{:S(2)}) collective-permute-start(bf16[1,24,3072]{2,1,0:T(8,128)(2,1)S(1)} %get-tuple-element.304), channel_id=1, source_target_pairs={{0,4},{1,5},{2,6},{3,7},{4,0},{5,1},{6,2},{7,3},{8,12},{9,13},{10,... | collective-permute-start | bytes 442376 | tf_op jit(solution)/shard_map/ppermute | solution.py:66
  39.7 18.4 %collective-permute-start.5 = (bf16[8,24,3200]{2,1,0:T(8,128)(2,1)S(1)}, bf16[8,24,3200]{2,1,0:T(8,128)(2,1)}, u32[]{:S(2)}, u32[]{:S(2)}) collective-permute-start(bf16[8,24,3200]{2,1,0:T(8,128)(2,1)S(1)} %pad_maximum_fusion.refs_0_), channel_id=1, source_target_pairs={{0,16},{1,9},{2,18},{3,11},{4,20},{5,13},{6,22},{7,15},{8,24},{9,1... | collective-permute-start | bytes 3686408 | tf_op jit(solution)/shard_map/ppermute | solution.py:66
  41.0 8.2 %collective-permute-start.6 = (bf16[2,24,3072]{2,1,0:T(8,128)(2,1)S(1)}, bf16[2,24,3072]{2,1,0:T(8,128)(2,1)S(1)}, u32[]{:S(2)}, u32[]{:S(2)}) collective-permute-start(bf16[2,24,3072]{2,1,0:T(8,128)(2,1)S(1)} %pad_maximum_fusion.9), channel_id=1, source_target_pairs={{0,2},{1,3},{2,0},{3,1},{4,6},{5,7},{6,4},{7,5},{8,10},{9,11},{10,... | collective-permute-start | bytes 884744 | tf_op jit(solution)/shard_map/ppermute | solution.py:66
  45.9 24.1 %collective-permute-start.8 = (bf16[8,24,3200]{2,1,0:T(8,128)(2,1)S(1)}, bf16[8,24,3200]{2,1,0:T(8,128)(2,1)}, u32[]{:S(2)}, u32[]{:S(2)}) collective-permute-start(bf16[8,24,3200]{2,1,0:T(8,128)(2,1)S(1)} %pad_maximum_fusion.refs_0_), channel_id=1, source_target_pairs={{0,1},{1,0},{2,3},{3,2},{4,5},{5,4},{6,7},{7,6},{8,9},{9,8},{10,11... | collective-permute-start | bytes 3686408 | tf_op jit(solution)/shard_map/ppermute | solution.py:69
  45.9 12.1 %collective-permute-start.7 = (bf16[128,768]{1,0:T(8,128)(2,1)S(1)}, bf16[128,768]{1,0:T(8,128)(2,1)S(1)}, u32[]{:S(2)}, u32[]{:S(2)}) collective-permute-start(bf16[128,768]{1,0:T(8,128)(2,1)S(1)} %slice.383), channel_id=1, source_target_pairs={{0,4},{1,5},{2,6},{3,7},{4,0},{5,1},{6,2},{7,3},{8,12},{9,13},{10,... | collective-permute-start | bytes 589832 | tf_op jit(solution)/shard_map/ppermute | solution.py:72
  58.1 12.0 %collective-permute-start.9 = (bf16[8,24,3200]{2,1,0:T(8,128)(2,1)}, bf16[8,24,3200]{2,1,0:T(8,128)(2,1)}, u32[]{:S(2)}, u32[]{:S(2)}) collective-permute-start(bf16[8,24,3200]{2,1,0:T(8,128)(2,1)} %collective-permute-done.5.refs_1_), channel_id=1, source_target_pairs={{0,1},{1,0},{2,3},{3,2},{4,5},{5,4},{6,7},{7,6},{8,9},{9,8},{10,11... | collective-permute-start | bytes 3686408 | tf_op jit(solution)/shard_map/ppermute | solution.py:69
  58.8 10.0 %collective-permute-start.10 = (bf16[4,24,3072]{2,1,0:T(8,128)(2,1)S(1)}, bf16[4,24,3072]{2,1,0:T(8,128)(2,1)}, u32[]{:S(2)}, u32[]{:S(2)}) collective-permute-start(bf16[4,24,3072]{2,1,0:T(8,128)(2,1)S(1)} %pad_maximum_fusion.5), channel_id=1, source_target_pairs={{0,8},{1,17},{2,10},{3,19},{4,12},{5,21},{6,14},{7,23},{8,0},{9,25... | collective-permute-start | bytes 1769480 | tf_op jit(solution)/shard_map/ppermute | solution.py:66
  60.3 17.7 %collective-permute-start.11 = (bf16[224,768]{1,0:T(8,128)(2,1)S(1)}, bf16[224,768]{1,0:T(8,128)(2,1)}, u32[]{:S(2)}, u32[]{:S(2)}) collective-permute-start(bf16[224,768]{1,0:T(8,128)(2,1)S(1)} %slice.384), channel_id=1, source_target_pairs={{0,4},{1,5},{2,6},{3,7},{4,0},{5,1},{6,2},{7,3},{8,12},{9,13},{10,... | collective-permute-start | bytes 1032200 | tf_op jit(solution)/shard_map/ppermute | solution.py:72
  61.1 31.2 %collective-permute-start.13 = (s32[512]{0:T(512)S(1)}, s32[512]{0:T(512)S(1)}, u32[]{:S(2)}, u32[]{:S(2)}) collective-permute-start(s32[512]{0:T(512)S(1)} %get-tuple-element.653), channel_id=1, source_target_pairs={{0,4},{1,5},{2,6},{3,7},{4,0},{5,1},{6,2},{7,3},{8,12},{9,13},{10,... | collective-permute-start | bytes 6152 | tf_op jit(solution)/shard_map/ppermute | solution.py:72
  79.1 26.3 %collective-permute-start.14 = (bf16[8,24,3072]{2,1,0:T(8,128)(2,1)S(1)}, bf16[8,24,3072]{2,1,0:T(8,128)(2,1)}, u32[]{:S(2)}, u32[]{:S(2)}) collective-permute-start(bf16[8,24,3072]{2,1,0:T(8,128)(2,1)S(1)} %pad_maximum_fusion.1.refs_0_), channel_id=1, source_target_pairs={{0,16},{1,9},{2,18},{3,11},{4,20},{5,13},{6,22},{7,15},{8,24},{9,1... | collective-permute-start | bytes 3538952 | tf_op jit(solution)/shard_map/ppermute | solution.py:66
  81.9 8.8 %collective-permute-start.12 = (bf16[1,96,768]{2,1,0:T(8,128)(2,1)S(1)}, bf16[1,96,768]{2,1,0:T(8,128)(2,1)S(1)}, u32[]{:S(2)}, u32[]{:S(2)}) collective-permute-start(bf16[1,96,768]{2,1,0:T(8,128)(2,1)S(1)} %copy-done.36), channel_id=1, source_target_pairs={{0,4},{1,5},{2,6},{3,7},{4,0},{5,1},{6,2},{7,3},{8,12},{9,13},{10,... | collective-permute-start | bytes 442376 | tf_op jit(solution)/shard_map/ppermute | solution.py:66
  90.7 13.8 %collective-permute-start.15 = (bf16[2,96,768]{2,1,0:T(8,128)(2,1)S(1)}, bf16[2,96,768]{2,1,0:T(8,128)(2,1)S(1)}, u32[]{:S(2)}, u32[]{:S(2)}) collective-permute-start(bf16[2,96,768]{2,1,0:T(8,128)(2,1)S(1)} %pad_maximum_fusion.10), channel_id=1, source_target_pairs={{0,2},{1,3},{2,0},{3,1},{4,6},{5,7},{6,4},{7,5},{8,10},{9,11},{10,... | collective-permute-start | bytes 884744 | tf_op jit(solution)/shard_map/ppermute | solution.py:66
  92.9 25.2 %collective-permute-start.17 = (bf16[8,24,3072]{2,1,0:T(8,128)(2,1)S(1)}, bf16[8,24,3072]{2,1,0:T(8,128)(2,1)}, u32[]{:S(2)}, u32[]{:S(2)}) collective-permute-start(bf16[8,24,3072]{2,1,0:T(8,128)(2,1)S(1)} %pad_maximum_fusion.1.refs_0_), channel_id=1, source_target_pairs={{0,1},{1,0},{2,3},{3,2},{4,5},{5,4},{6,7},{7,6},{8,9},{9,8},{10,11... | collective-permute-start | bytes 3538952 | tf_op jit(solution)/shard_map/ppermute | solution.py:69
  92.9 12.5 %collective-permute-start.16 = (bf16[128,768]{1,0:T(8,128)(2,1)S(1)}, bf16[128,768]{1,0:T(8,128)(2,1)S(1)}, u32[]{:S(2)}, u32[]{:S(2)}) collective-permute-start(bf16[128,768]{1,0:T(8,128)(2,1)S(1)} %copy-done.31), channel_id=1, source_target_pairs={{0,4},{1,5},{2,6},{3,7},{4,0},{5,1},{6,2},{7,3},{8,12},{9,13},{10,... | collective-permute-start | bytes 589832 | tf_op jit(solution)/shard_map/ppermute | solution.py:72
  105.3 12.7 %collective-permute-start.18 = (bf16[8,24,3072]{2,1,0:T(8,128)(2,1)}, bf16[8,24,3072]{2,1,0:T(8,128)(2,1)}, u32[]{:S(2)}, u32[]{:S(2)}) collective-permute-start(bf16[8,24,3072]{2,1,0:T(8,128)(2,1)} %collective-permute-done.14.refs_1_), channel_id=1, source_target_pairs={{0,1},{1,0},{2,3},{3,2},{4,5},{5,4},{6,7},{7,6},{8,9},{9,8},{10,11... | collective-permute-start | bytes 3538952 | tf_op jit(solution)/shard_map/ppermute | solution.py:69
  105.3 11.5 %collective-permute-start.19 = (bf16[4,96,768]{2,1,0:T(8,128)(2,1)S(1)}, bf16[4,96,768]{2,1,0:T(8,128)(2,1)}, u32[]{:S(2)}, u32[]{:S(2)}) collective-permute-start(bf16[4,96,768]{2,1,0:T(8,128)(2,1)S(1)} %pad_maximum_fusion.6), channel_id=1, source_target_pairs={{0,8},{1,17},{2,10},{3,19},{4,12},{5,21},{6,14},{7,23},{8,0},{9,25... | collective-permute-start | bytes 1769480 | tf_op jit(solution)/shard_map/ppermute | solution.py:66
  107.7 10.4 %collective-permute-start.20 = (bf16[96,768]{1,0:T(8,128)(2,1)}, bf16[96,768]{1,0:T(8,128)(2,1)S(1)}, u32[]{:S(2)}, u32[]{:S(2)}) collective-permute-start(bf16[96,768]{1,0:T(8,128)(2,1)} %get-tuple-element.350), channel_id=1, source_target_pairs={{0,4},{1,5},{2,6},{3,7},{4,0},{5,1},{6,2},{7,3},{8,12},{9,13},{10,... | collective-permute-start | bytes 442376 | tf_op jit(solution)/shard_map/ppermute | solution.py:72
  118.1 17.6 %collective-permute-start.21 = (bf16[8,96,768]{2,1,0:T(8,128)(2,1)S(1)}, bf16[8,96,768]{2,1,0:T(8,128)(2,1)}, u32[]{:S(2)}, u32[]{:S(2)}) collective-permute-start(bf16[8,96,768]{2,1,0:T(8,128)(2,1)S(1)} %pad_maximum_fusion.2.refs_0_), channel_id=1, source_target_pairs={{0,16},{1,9},{2,18},{3,11},{4,20},{5,13},{6,22},{7,15},{8,24},{9,1... | collective-permute-start | bytes 3538952 | tf_op jit(solution)/shard_map/ppermute | solution.py:66
  119.4 16.3 %collective-permute-start.22 = (bf16[8,96,768]{2,1,0:T(8,128)(2,1)S(1)}, bf16[8,96,768]{2,1,0:T(8,128)(2,1)}, u32[]{:S(2)}, u32[]{:S(2)}) collective-permute-start(bf16[8,96,768]{2,1,0:T(8,128)(2,1)S(1)} %pad_maximum_fusion.2.refs_0_), channel_id=1, source_target_pairs={{0,1},{1,0},{2,3},{3,2},{4,5},{5,4},{6,7},{7,6},{8,9},{9,8},{10,11... | collective-permute-start | bytes 3538952 | tf_op jit(solution)/shard_map/ppermute | solution.py:69
  125.3 10.3 %collective-permute-start.23 = (bf16[96,768]{1,0:T(8,128)(2,1)S(1)}, bf16[96,768]{1,0:T(8,128)(2,1)S(1)}, u32[]{:S(2)}, u32[]{:S(2)}) collective-permute-start(bf16[96,768]{1,0:T(8,128)(2,1)S(1)} %copy-done.35), channel_id=1, source_target_pairs={{0,4},{1,5},{2,6},{3,7},{4,0},{5,1},{6,2},{7,3},{8,12},{9,13},{10,... | collective-permute-start | bytes 442376 | tf_op jit(solution)/shard_map/ppermute | solution.py:72
  135.7 9.3 %collective-permute-start.24 = (bf16[8,96,768]{2,1,0:T(8,128)(2,1)}, bf16[8,96,768]{2,1,0:T(8,128)(2,1)S(1)}, u32[]{:S(2)}, u32[]{:S(2)}) collective-permute-start(bf16[8,96,768]{2,1,0:T(8,128)(2,1)} %collective-permute-done.21.refs_1_), channel_id=1, source_target_pairs={{0,1},{1,0},{2,3},{3,2},{4,5},{5,4},{6,7},{7,6},{8,9},{9,8},{10,11... | collective-permute-start | bytes 3538952 | tf_op jit(solution)/shard_map/ppermute | solution.py:69
  136.2 8.8 %collective-permute-start.25 = (bf16[64,768]{1,0:T(8,128)(2,1)S(1)}, bf16[64,768]{1,0:T(8,128)(2,1)S(1)}, u32[]{:S(2)}, u32[]{:S(2)}) collective-permute-start(bf16[64,768]{1,0:T(8,128)(2,1)S(1)} %copy-done.39), channel_id=1, source_target_pairs={{0,4},{1,5},{2,6},{3,7},{4,0},{5,1},{6,2},{7,3},{8,12},{9,13},{10,... | collective-permute-start | bytes 294920 | tf_op jit(solution)/shard_map/ppermute | solution.py:72
  150.8 13.8 %collective-permute-start.26 = (bf16[128,768]{1,0:T(8,128)(2,1)S(1)}, bf16[128,768]{1,0:T(8,128)(2,1)S(1)}, u32[]{:S(2)}, u32[]{:S(2)}) collective-permute-start(bf16[128,768]{1,0:T(8,128)(2,1)S(1)} %copy-done.30), channel_id=1, source_target_pairs={{0,4},{1,5},{2,6},{3,7},{4,0},{5,1},{6,2},{7,3},{8,12},{9,13},{10,... | collective-permute-start | bytes 589832 | tf_op jit(solution)/shard_map/ppermute | solution.py:72
  196.4 11.8 %collective-permute-start.32 = (bf16[128,768]{1,0:T(8,128)(2,1)S(1)}, bf16[128,768]{1,0:T(8,128)(2,1)S(1)}, u32[]{:S(2)}, u32[]{:S(2)}) collective-permute-start(bf16[128,768]{1,0:T(8,128)(2,1)S(1)} %get-tuple-element.411), channel_id=1, source_target_pairs={{0,4},{1,5},{2,6},{3,7},{4,0},{5,1},{6,2},{7,3},{8,12},{9,13},{10,... | collective-permute-start | bytes 589832 | tf_op jit(solution)/shard_map/ppermute | solution.py:72
  208.9 13.1 %collective-permute-start.33 = (bf16[16,96,768]{2,1,0:T(8,128)(2,1)}, bf16[16,96,768]{2,1,0:T(8,128)(2,1)S(1)}, u32[]{:S(2)}, u32[]{:S(2)}) collective-permute-start(bf16[16,96,768]{2,1,0:T(8,128)(2,1)} %get-tuple-element.416), channel_id=1, source_target_pairs={{0,1},{1,0},{2,3},{3,2},{4,5},{5,4},{6,7},{7,6},{8,9},{9,8},{10,11... | collective-permute-start | bytes 7077896 | tf_op jit(solution)/shard_map/ppermute | solution.py:69
  208.9 13.1 %collective-permute-start.34 = (bf16[128,768]{1,0:T(8,128)(2,1)S(1)}, bf16[128,768]{1,0:T(8,128)(2,1)S(1)}, u32[]{:S(2)}, u32[]{:S(2)}) collective-permute-start(bf16[128,768]{1,0:T(8,128)(2,1)S(1)} %get-tuple-element.421), channel_id=1, source_target_pairs={{0,4},{1,5},{2,6},{3,7},{4,0},{5,1},{6,2},{7,3},{8,12},{9,13},{10,... | collective-permute-start | bytes 589832 | tf_op jit(solution)/shard_map/ppermute | solution.py:72
  223.0 16.3 %collective-permute-start.35 = (bf16[8,96,768]{2,1,0:T(8,128)(2,1)S(1)}, bf16[8,96,768]{2,1,0:T(8,128)(2,1)S(1)}, u32[]{:S(2)}, u32[]{:S(2)}) collective-permute-start(bf16[8,96,768]{2,1,0:T(8,128)(2,1)S(1)} %add_convert_fusion.1), channel_id=1, source_target_pairs={{0,16},{1,9},{2,18},{3,11},{4,20},{5,13},{6,22},{7,15},{8,24},{9,1... | collective-permute-start | bytes 3538952 | tf_op jit(solution)/shard_map/ppermute | solution.py:66
  224.3 11.7 %collective-permute-start.36 = (bf16[128,768]{1,0:T(8,128)(2,1)S(1)}, bf16[128,768]{1,0:T(8,128)(2,1)S(1)}, u32[]{:S(2)}, u32[]{:S(2)}) collective-permute-start(bf16[128,768]{1,0:T(8,128)(2,1)S(1)} %get-tuple-element.431), channel_id=1, source_target_pairs={{0,4},{1,5},{2,6},{3,7},{4,0},{5,1},{6,2},{7,3},{8,12},{9,13},{10,... | collective-permute-start | bytes 589832 | tf_op jit(solution)/shard_map/ppermute | solution.py:72
  239.5 15.0 %collective-permute-start.37 = (bf16[4,96,768]{2,1,0:T(8,128)(2,1)S(1)}, bf16[4,96,768]{2,1,0:T(8,128)(2,1)S(1)}, u32[]{:S(2)}, u32[]{:S(2)}) collective-permute-start(bf16[4,96,768]{2,1,0:T(8,128)(2,1)S(1)} %add_convert_fusion.4), channel_id=1, source_target_pairs={{0,8},{1,17},{2,10},{3,19},{4,12},{5,21},{6,14},{7,23},{8,0},{9,25... | collective-permute-start | bytes 1769480 | tf_op jit(solution)/shard_map/ppermute | solution.py:66
  240.7 13.8 %collective-permute-start.38 = (bf16[128,768]{1,0:T(8,128)(2,1)}, bf16[128,768]{1,0:T(8,128)(2,1)S(1)}, u32[]{:S(2)}, u32[]{:S(2)}) collective-permute-start(bf16[128,768]{1,0:T(8,128)(2,1)} %get-tuple-element.446), channel_id=1, source_target_pairs={{0,4},{1,5},{2,6},{3,7},{4,0},{5,1},{6,2},{7,3},{8,12},{9,13},{10,... | collective-permute-start | bytes 589832 | tf_op jit(solution)/shard_map/ppermute | solution.py:72
  261.3 16.8 %collective-permute-start.40 = (bf16[16,24,3840]{2,1,0:T(8,128)(2,1)}, bf16[16,24,3840]{2,1,0:T(8,128)(2,1)S(1)}, u32[]{:S(2)}, u32[]{:S(2)}) collective-permute-start(bf16[16,24,3840]{2,1,0:T(8,128)(2,1)} %get-tuple-element.462), channel_id=1, source_target_pairs={{0,1},{1,0},{2,3},{3,2},{4,5},{5,4},{6,7},{7,6},{8,9},{9,8},{10,11... | collective-permute-start | bytes 8847368 | tf_op jit(solution)/shard_map/ppermute | solution.py:69
  261.3 16.8 %collective-permute-start.39 = (bf16[2,96,768]{2,1,0:T(8,128)(2,1)}, bf16[2,96,768]{2,1,0:T(8,128)(2,1)S(1)}, u32[]{:S(2)}, u32[]{:S(2)}) collective-permute-start(bf16[2,96,768]{2,1,0:T(8,128)(2,1)} %add_convert_fusion.7), channel_id=1, source_target_pairs={{0,2},{1,3},{2,0},{3,1},{4,6},{5,7},{6,4},{7,5},{8,10},{9,11},{10,... | collective-permute-start | bytes 884744 | tf_op jit(solution)/shard_map/ppermute | solution.py:66
  280.9 25.7 %collective-permute-start.41 = (bf16[8,24,3840]{2,1,0:T(8,128)(2,1)}, bf16[8,24,3840]{2,1,0:T(8,128)(2,1)S(1)}, u32[]{:S(2)}, u32[]{:S(2)}) collective-permute-start(bf16[8,24,3840]{2,1,0:T(8,128)(2,1)} %add_convert_fusion), channel_id=1, source_target_pairs={{0,16},{1,9},{2,18},{3,11},{4,20},{5,13},{6,22},{7,15},{8,24},{9,1... | collective-permute-start | bytes 4423688 | tf_op jit(solution)/shard_map/ppermute | solution.py:66
  281.9 9.7 %collective-permute-start.42 = (bf16[1,96,768]{2,1,0:T(8,128)(2,1)S(1)}, bf16[1,96,768]{2,1,0:T(8,128)(2,1)S(1)}, u32[]{:S(2)}, u32[]{:S(2)}) collective-permute-start(bf16[1,96,768]{2,1,0:T(8,128)(2,1)S(1)} %add_convert_fusion.10), channel_id=1, source_target_pairs={{0,4},{1,5},{2,6},{3,7},{4,0},{5,1},{6,2},{7,3},{8,12},{9,13},{10,... | collective-permute-start | bytes 442376 | tf_op jit(solution)/shard_map/ppermute | solution.py:66
  293.7 12.9 %collective-permute-start.43 = (bf16[160,768]{1,0:T(8,128)(2,1)}, bf16[160,768]{1,0:T(8,128)(2,1)S(1)}, u32[]{:S(2)}, u32[]{:S(2)}) collective-permute-start(bf16[160,768]{1,0:T(8,128)(2,1)} %get-tuple-element.492), channel_id=1, source_target_pairs={{0,4},{1,5},{2,6},{3,7},{4,0},{5,1},{6,2},{7,3},{8,12},{9,13},{10,... | collective-permute-start | bytes 737288 | tf_op jit(solution)/shard_map/ppermute | solution.py:72
  308.0 17.5 %collective-permute-start.44 = (bf16[4,24,3840]{2,1,0:T(8,128)(2,1)}, bf16[4,24,3840]{2,1,0:T(8,128)(2,1)}, u32[]{:S(2)}, u32[]{:S(2)}) collective-permute-start(bf16[4,24,3840]{2,1,0:T(8,128)(2,1)} %add_convert_fusion.3), channel_id=1, source_target_pairs={{0,8},{1,17},{2,10},{3,19},{4,12},{5,21},{6,14},{7,23},{8,0},{9,25... | collective-permute-start | bytes 2211848 | tf_op jit(solution)/shard_map/ppermute | solution.py:66
  311.5 14.0 %collective-permute-start.45 = (bf16[160,768]{1,0:T(8,128)(2,1)}, bf16[160,768]{1,0:T(8,128)(2,1)S(1)}, u32[]{:S(2)}, u32[]{:S(2)}) collective-permute-start(bf16[160,768]{1,0:T(8,128)(2,1)} %get-tuple-element.516), channel_id=1, source_target_pairs={{0,4},{1,5},{2,6},{3,7},{4,0},{5,1},{6,2},{7,3},{8,12},{9,13},{10,... | collective-permute-start | bytes 737288 | tf_op jit(solution)/shard_map/ppermute | solution.py:72
  326.2 12.5 %collective-permute-start.46 = (bf16[16,24,2432]{2,1,0:T(8,128)(2,1)}, bf16[16,24,2432]{2,1,0:T(8,128)(2,1)S(1)}, u32[]{:S(2)}, u32[]{:S(2)}) collective-permute-start(bf16[16,24,2432]{2,1,0:T(8,128)(2,1)} %get-tuple-element.520), channel_id=1, source_target_pairs={{0,1},{1,0},{2,3},{3,2},{4,5},{5,4},{6,7},{7,6},{8,9},{9,8},{10,11... | collective-permute-start | bytes 5603336 | tf_op jit(solution)/shard_map/ppermute | solution.py:69
  327.6 11.1 %collective-permute-start.47 = (bf16[2,24,3840]{2,1,0:T(8,128)(2,1)S(1)}, bf16[2,24,3840]{2,1,0:T(8,128)(2,1)S(1)}, u32[]{:S(2)}, u32[]{:S(2)}) collective-permute-start(bf16[2,24,3840]{2,1,0:T(8,128)(2,1)S(1)} %add_convert_fusion.6), channel_id=1, source_target_pairs={{0,2},{1,3},{2,0},{3,1},{4,6},{5,7},{6,4},{7,5},{8,10},{9,11},{10,... | collective-permute-start | bytes 1105928 | tf_op jit(solution)/shard_map/ppermute | solution.py:66
  340.2 13.9 %collective-permute-start.48 = (bf16[8,24,2432]{2,1,0:T(8,128)(2,1)}, bf16[8,24,2432]{2,1,0:T(8,128)(2,1)}, u32[]{:S(2)}, u32[]{:S(2)}) collective-permute-start(bf16[8,24,2432]{2,1,0:T(8,128)(2,1)} %add_convert_fusion.2), channel_id=1, source_target_pairs={{0,16},{1,9},{2,18},{3,11},{4,20},{5,13},{6,22},{7,15},{8,24},{9,1... | collective-permute-start | bytes 2801672 | tf_op jit(solution)/shard_map/ppermute | solution.py:66
  341.0 11.7 %collective-permute-start.49 = (bf16[128,768]{1,0:T(8,128)(2,1)}, bf16[128,768]{1,0:T(8,128)(2,1)}, u32[]{:S(2)}, u32[]{:S(2)}) collective-permute-start(bf16[128,768]{1,0:T(8,128)(2,1)} %get-tuple-element.537), channel_id=1, source_target_pairs={{0,4},{1,5},{2,6},{3,7},{4,0},{5,1},{6,2},{7,3},{8,12},{9,13},{10,... | collective-permute-start | bytes 589832 | tf_op jit(solution)/shard_map/ppermute | solution.py:72
  355.4 10.2 %collective-permute-start.51 = (bf16[1,24,3840]{2,1,0:T(8,128)(2,1)S(1)}, bf16[1,24,3840]{2,1,0:T(8,128)(2,1)S(1)}, u32[]{:S(2)}, u32[]{:S(2)}) collective-permute-start(bf16[1,24,3840]{2,1,0:T(8,128)(2,1)S(1)} %add_convert_fusion.9), channel_id=1, source_target_pairs={{0,4},{1,5},{2,6},{3,7},{4,0},{5,1},{6,2},{7,3},{8,12},{9,13},{10,... | collective-permute-start | bytes 552968 | tf_op jit(solution)/shard_map/ppermute | solution.py:66
  357.8 9.2 %collective-permute-start.50 = (bf16[4,24,2432]{2,1,0:T(8,128)(2,1)S(1)}, bf16[4,24,2432]{2,1,0:T(8,128)(2,1)S(1)}, u32[]{:S(2)}, u32[]{:S(2)}) collective-permute-start(bf16[4,24,2432]{2,1,0:T(8,128)(2,1)S(1)} %add_convert_fusion.5), channel_id=1, source_target_pairs={{0,8},{1,17},{2,10},{3,19},{4,12},{5,21},{6,14},{7,23},{8,0},{9,25... | collective-permute-start | bytes 1400840 | tf_op jit(solution)/shard_map/ppermute | solution.py:66
  368.3 9.8 %collective-permute-start.52 = (bf16[2,24,2432]{2,1,0:T(8,128)(2,1)S(1)}, bf16[2,24,2432]{2,1,0:T(8,128)(2,1)S(1)}, u32[]{:S(2)}, u32[]{:S(2)}) collective-permute-start(bf16[2,24,2432]{2,1,0:T(8,128)(2,1)S(1)} %add_convert_fusion.8), channel_id=1, source_target_pairs={{0,2},{1,3},{2,0},{3,1},{4,6},{5,7},{6,4},{7,5},{8,10},{9,11},{10,... | collective-permute-start | bytes 700424 | tf_op jit(solution)/shard_map/ppermute | solution.py:66
  (64 other events, 571.2 us)

commit v11 on v9

--- a/solution.py
+++ b/solution.py
@@ -921,7 +921,7 @@
     qid = seq.reshape(rows, 1)
     g1, g2, g3 = Gather(first), Gather(second), Gather(third)
     my_tokens, send_tokens = sides(rows_q, rows_p)
-    tokens_out = chunked(send_tokens, (5, 6, 5))
+    tokens_out = chunked(send_tokens, (5, 4, 7))
     g1.mid()
     g1.send, tokens_out, question_cot, passage_cot = tie(
         g1.send, tokens_out, question_cot, passage_cot
@@ -963,7 +963,7 @@
     bias_j = jnp.concatenate([vec[0], jnp.zeros((D,), F32), vec[1]])
     tokens, qkv = project([my_tokens] + tokens_in, wj, bias_j[None])
 
-    cot_out = chunked(send_cot, (5, 3, 3, 2, 3))
+    cot_out = chunked(send_cot, (4, 3, 3, 2, 4))
     by_pa = positive.reshape(places.pa_n, nq)
     pair = [lax.dynamic_index_in_dim(by_pa, low_pa + k, 0, keepdims=False) for k in (0, shift)]
     pair = jnp.concatenate(pair)[None]
@@ -1110,9 +1110,11 @@
                 self.move(step)
 
         def mid(self):
-            got = places.swap(self.total(1, 2).astype(BF16), 0).astype(F32)
-            keep = self.total(0, 1)
-            self.out = jnp.concatenate(
+            self.got = places.swap(self.total(1, 2).astype(BF16), 0)
+
+        def finish(self):
+            got, keep = self.got.astype(F32), self.total(0, 1)
+            return jnp.concatenate(
                 [jnp.where(is_q, keep, got), jnp.where(is_q, got, keep)], axis=0
             )
 
@@ -1174,8 +1176,8 @@
     bias_sums = g_bias_expand.reshape(D, 4).T
     small_sums = (sums_one, sums_two, sums_first, sums_second, bias_sums)
     sj = Scatter(*(gradient if even else plain)(tokens, d_joined, extra=small_sums))
-    se.parts, sr.out, sj.parts, sj.theirs, d_joined, got_grad, send_grad = tie(
-        se.parts, sr.out, sj.parts, sj.theirs, d_joined, got_grad, send_grad
+    se.parts, sr.got, sj.parts, sj.theirs, d_joined, got_grad, send_grad = tie(
+        se.parts, sr.got, sj.parts, sj.theirs, d_joined, got_grad, send_grad
     )
     sj.cores()
     got_grad = got_grad + hand(send_grad[2:3])
@@ -1187,15 +1189,18 @@
     sj.parts, se.parts, got_grad, send_grad = tie(sj.parts, se.parts, got_grad, send_grad)
     sj.pb_rest()
     se.mid()
-    sj.parts, se.out, got_out, out = tie(sj.parts, se.out, got_out, out)
+    sj.parts, se.got, got_out, out = tie(sj.parts, se.got, got_out, out)
     sj.along_z()
     out_q, out_p = deal(tower.reshape(1), out, got_out)
-    sj.parts, out_q, out_p, got_grad = tie(sj.parts, out_q, out_p, got_grad)
+    sj.parts, out_q, out_p, got_grad, sr.got, sr.parts, se.got, se.parts = tie(
+        sj.parts, out_q, out_p, got_grad, sr.got, sr.parts, se.got, se.parts
+    )
     grad_q, grad_p = deal(tower.reshape(1), own_grad, got_grad)
     sj.mid()
-    grad_joined = sj.out[:, :, : 3 * D]
-    grad_expand, grad_output, grad_reduce = se.out[:, :, :FF], se.out[:, :, FF:], sr.out
-    extra = sj.out[:, :, 3 * D :]
+    grad_reduce, both, last = sr.finish(), se.finish(), sj.finish()
+    grad_joined = last[:, :, : 3 * D]
+    grad_expand, grad_output = both[:, :, :FF], both[:, :, FF:]
+    extra = last[:, :, 3 * D :]
     grad_vectors = extra[:, :, :8].transpose(0, 2, 1)
     grad_b_expand = extra[:, :, 8:12].reshape(2, 4 * share)
 

time: 389 us -> 387 us (level)
  transfers between devices with their start and end apart: 55 -> 55, of which waited for: 22 -> 23; matrix products, arithmetic and copies ran while one was open for 10% -> 10% of each run, Pallas kernels for 42% -> 42%
where the time goes in v11:
time: 387 us; the launch traced here: 385 us
  Pallas kernels  180 us (47%)
  waiting for transfers between devices  84.3 us (22%)
  starting transfers between devices  60.5 us (16%)
  other arithmetic  34.8 us (9%)
  local copies, waits for them, and re-layouts  19.7 us (5%)
  matrix products  4.48 us (1%)
    ppermute x24, waiting for transfers between devices, swap(): return lax.ppermute(values, AXES, self.pairs(step))  50.3 us
    ppermute x24, starting transfers between devices, swap(): return lax.ppermute(values, AXES, self.pairs(step))  30.9 us
    ppermute x18, starting transfers between devices, swap_tower(): lax.ppermute(values, 'pa', [(i, i ^ 2 * self.half) for i in range(self.pa...  26.9 us
    ppermute x18, waiting for transfers between devices, swap_tower(): lax.ppermute(values, 'pa', [(i, i ^ 2 * self.half) for i in range(self.pa...  24.9 us
    pallas_call x3, Pallas kernels, weight_grad(): pl.pallas_call(functools.partial(weight_grad_kernel, chips, len(extra or...  24.2 us
    pallas_call x2, Pallas kernels, attention_back(): pl.pallas_call(attention_back_more_kernel if more else attention_back_ker...  23.7 us
    pallas_call x2, Pallas kernels, add_norm(): pl.pallas_call(functools.partial(add_norm_kernel, rows_of), grid=(rows //...  19 us
    pallas_call x2, Pallas kernels, expand(): pl.pallas_call(expand_more_kernel if into else expand_kernel, grid=(count...  15.9 us
  transfers between devices with their start and end apart: 55, of which 23 were waited for; matrix products, arithmetic and copies ran while one was open for 10% of the time, Pallas kernels for 42%

profile of v11, /device:TPU:0, one launch (start us, length us, event | category | flops | bytes accessed | tf_op | source)
XLA Modules:
  0.0 385.0 jit_solution(16042739983816110801)
XLA Ops:
  3.5 4.1 %collective-permute-start = (bf16[1,24,3200]{2,1,0:T(8,128)(2,1)S(1)}, bf16[1,24,3200]{2,1,0:T(8,128)(2,1)S(1)}, u32[]{:S(2)}, u32[]{:S(2)}) collective-permute-start(bf16[1,24,3200]{2,1,0:T(8,128)(2,1)S(1)} %get-tuple-element.643), channel_id=1, source_target_pairs={{0,4},{1,5},{2,6},{3,7},{4,0},{5,1},{6,2},{7,3},{8,12},{9,13},{10,... | collective-permute-start | bytes 460808 | tf_op jit(solution)/shard_map/ppermute | solution.py:66
  12.4 2.5 collective-permute-done
  15.8 3.4 collective-permute-start.2
  20.2 8.5 %collective-permute-done.1 = bf16[2,24,3200]{2,1,0:T(8,128)(2,1)S(1)} collective-permute-done((bf16[2,24,3200]{2,1,0:T(8,128)(2,1)S(1)}, bf16[2,24,3200]{2,1,0:T(8,128)(2,1)S(1)}, u32[]{:S(2)}, u32[]{:S(2)}) %collective-permute-start.1) | collective-permute-done | bytes 307232 | tf_op jit(solution)/shard_map/ppermute | solution.py:66
  30.2 2.6 collective-permute-start.4
  32.8 6.6 %collective-permute-done.4 = bf16[1,24,3072]{2,1,0:T(8,128)(2,1)S(1)} collective-permute-done((bf16[1,24,3072]{2,1,0:T(8,128)(2,1)S(1)}, bf16[1,24,3072]{2,1,0:T(8,128)(2,1)S(1)}, u32[]{:S(2)}, u32[]{:S(2)}) %collective-permute-start.4) | collective-permute-done | bytes 147488 | tf_op jit(solution)/shard_map/ppermute | solution.py:66
  41.0 2.8 collective-permute-start.6
  49.3 8.8 %collective-permute-done.7.refs_2_ = bf16[128,768]{1,0:T(8,128)(2,1)S(1)} collective-permute-done((bf16[128,768]{1,0:T(8,128)(2,1)S(1)}, bf16[128,768]{1,0:T(8,128)(2,1)S(1)}, u32[]{:S(2)}, u32[]{:S(2)}) %collective-permute-start.7) | collective-permute-done | bytes 196640 | tf_op jit(solution)/shard_map/ppermute | solution.py:72
  61.1 2.4 collective-permute-start.13
  63.5 5.3 %collective-permute-done.10 = bf16[4,24,3072]{2,1,0:T(8,128)(2,1)} collective-permute-done((bf16[4,24,3072]{2,1,0:T(8,128)(2,1)S(1)}, bf16[4,24,3072]{2,1,0:T(8,128)(2,1)}, u32[]{:S(2)}, u32[]{:S(2)}) %collective-permute-start.10) | collective-permute-done | bytes 589856 | tf_op jit(solution)/shard_map/ppermute | solution.py:66
  70.0 5.5 %assemble.3 = (bf16[16,2,24,2304]{3,2,1,0:T(8,128)(2,1)}, bf16[16,2,24,768]{3,2,1,0:T(8,128)(2,1)}, bf16[16,2,24,128]{3,2,1,0:T(8,128)(2,1)}) custom-call(s32[3,16]{1,0:T(4,128)} %get-tuple-element.304.idx_ref, bf16[8,24,3200]{2,1,0:T(8,128)(2,1)} %copy-done.1, bf16[8,24,3200]{2,1,0:T(8,128)(2,1)} %collective-permute-done.5.refs_1_, ...), custom_call_target="tpu_custom_call" | custom-call | bytes 9830400 | tf_op jit(solution)/shard_map/assemble/pallas_call | solution.py:118
  75.6 2.4 collective-permute-done.11.refs_3_
  81.9 8.5 %project.1 = (bf16[1024,768]{1,0:T(8,128)(2,1)}, bf16[1024,2304]{1,0:T(8,128)(2,1)}) custom-call(bf16[768,2304]{1,0:T(8,128)(2,1)} %bitcast.65, f32[1,2304]{1,0:T(1,128)} %broadcast_in_dim.14.b_ref, bf16[512,768]{1,0:T(8,128)(2,1)} %get-tuple-element.634.refs_0_, bf16[160,768]{1,0:T(8,128)(2,1)} %copy-done.57, bf16[128,768]{1,0:T(8,128)(2,1)} %copy-done.58, ...), custom_call_target="tpu_custom_call" | custom-call | flops 3623878656 | bytes 11403264 | tf_op jit(solution)/shard_map/project/pallas_call | solution.py:716
  93.9 10.6 %attention.1 = (bf16[1024,768]{1,0:T(8,128)(2,1)}, bf16[4,12,256,256]{3,2,1,0:T(8,128)(2,1)}) custom-call(bf16[1024,2304]{1,0:T(8,128)(2,1)} %get-tuple-element.332.qkv_ref, s32[1024,1]{1,0:T(8,128)} %fusion.2.qid_ref, s32[4,1,256]{2,1,0:T(1,128)} %bitcast.85), custom_call_target="tpu_custom_call" | custom-call | flops 1610612736 | bytes 12582912 | tf_op jit(solution)/shard_map/attention/pallas_call | solution.py:342
  109.4 7.4 %add_norm.2 = (f32[1024,768]{1,0:T(8,128)}, f32[1024,1]{1,0:T(8,128)}, bf16[1024,768]{1,0:T(8,128)(2,1)}, f32[1024,768]{1,0:T(8,128)}) custom-call(bf16[1024,768]{1,0:T(8,128)(2,1)} %get-tuple-element.345.left_ref, bf16[768,768]{1,0:T(8,128)(2,1)} %bitcast.74, bf16[1024,768]{1,0:T(8,128)(2,1)} %get-tuple-element.347.base_ref.left_ref, ...), custom_call_target="tpu_custom_call" | custom-call | flops 1207959552 | bytes 12189696 | tf_op jit(solution)/shard_map/add_norm/pallas_call | solution.py:762
  120.4 4.8 %assemble.4 = bf16[16,2,24,3072]{3,2,1,0:T(8,128)(2,1)} custom-call(s32[3,16]{1,0:T(4,128)} %get-tuple-element.304.idx_ref, bf16[8,24,3072]{2,1,0:T(8,128)(2,1)} %copy-done.2, bf16[8,24,3072]{2,1,0:T(8,128)(2,1)} %collective-permute-done.14.refs_1_, bf16[8,24,3072]{2,1,0:T(8,128)(2,1)} %collective-permute-done.17.refs_2_, ...), custom_call_target="tpu_custom_call" | custom-call | bytes 9437184 | tf_op jit(solution)/shard_map/assemble/pallas_call | solution.py:118
  126.8 7.9 %expand.2 = (bf16[1024,3072]{1,0:T(8,128)(2,1)}, bf16[1024,3072]{1,0:T(8,128)(2,1)}) custom-call(bf16[1024,768]{1,0:T(8,128)(2,1)} %get-tuple-element.364.mid_ref.left_ref, bf16[768,3072]{1,0:T(8,128)(2,1)} %bitcast.62, f32[1,3072]{1,0:T(1,128)} %reshape.500.b_ref), custom_call_target="tpu_custom_call" | custom-call | flops 2415919104 | bytes 10223616 | tf_op jit(solution)/shard_map/expand/pallas_call | solution.py:638
  137.0 8.0 %expand.3 = (bf16[1024,3072]{1,0:T(8,128)(2,1)}, bf16[1024,3072]{1,0:T(8,128)(2,1)}) custom-call(bf16[1024,768]{1,0:T(8,128)(2,1)} %get-tuple-element.364.mid_ref.left_ref, bf16[768,3072]{1,0:T(8,128)(2,1)} %bitcast.63, f32[1,3072]{1,0:T(1,128)} %reshape.500.b_ref, ...), custom_call_target="tpu_custom_call", output_to_operand_aliasing={{0}: (3, {}), {1}: (4, {})} | custom-call | flops 2415919104 | bytes 10223616 | tf_op jit(solution)/shard_map/expand/pallas_call | solution.py:638
  146.0 4.9 %assemble.5 = bf16[16,2,96,768]{3,2,1,0:T(8,128)(2,1)} custom-call(s32[3,16]{1,0:T(4,128)} %get-tuple-element.304.idx_ref, bf16[8,96,768]{2,1,0:T(8,128)(2,1)} %copy-done.3, bf16[8,96,768]{2,1,0:T(8,128)(2,1)} %collective-permute-done.21.refs_1_, bf16[8,96,768]{2,1,0:T(8,128)(2,1)} %collective-permute-done.22.refs_2_, bf16[8,96,768]{2,1,0:T(8,128)(2,1)} %copy-done.11), custom_call_target="tpu_custom_call" | custom-call | bytes 9437184 | tf_op jit(solution)/shard_map/assemble/pallas_call | solution.py:118
  150.9 2.2 collective-permute-start.26
  153.2 11.6 %add_norm.3 = (f32[1024,768]{1,0:T(8,128)}, f32[1024,1]{1,0:T(8,128)}, bf16[1024,768]{1,0:T(8,128)(2,1)}) custom-call(bf16[1024,3072]{1,0:T(8,128)(2,1)} %get-tuple-element.385.left_ref, bf16[3072,768]{1,0:T(8,128)(2,1)} %bitcast.68, f32[1024,768]{1,0:T(8,128)} %get-tuple-element.393.base_ref, f32[1024,1]{1,0:T(8,128)} %convert_element_type.272.mask_ref, ...), custom_call_target="tpu_custom_call" | custom-call | flops 4831838208 | bytes 20447232 | tf_op jit(solution)/shard_map/add_norm/pallas_call | solution.py:762
  166.6 4.0 %collective-permute-done.27 = bf16[16,768]{1,0:T(8,128)(2,1)S(1)} collective-permute-done((bf16[16,768]{1,0:T(8,128)(2,1)S(1)}, bf16[16,768]{1,0:T(8,128)(2,1)S(1)}, u32[]{:S(2)}, u32[]{:S(2)}) %collective-permute-start.27) | collective-permute-done | bytes 24608 | tf_op jit(solution)/shard_map/ppermute | solution.py:72
  171.0 3.6 collective-permute-done.28
  175.6 2.0 fusion.35
  177.6 2.7 join.1.cot_ref
  181.6 3.9 %collective-permute-done.30 = bf16[4,24,768]{2,1,0:T(8,128)(2,1)S(1)} collective-permute-done((bf16[4,24,768]{2,1,0:T(8,128)(2,1)S(1)}, bf16[4,24,768]{2,1,0:T(8,128)(2,1)S(1)}, u32[]{:S(2)}, u32[]{:S(2)}) %collective-permute-start.30) | collective-permute-done | bytes 147488 | tf_op jit(solution)/shard_map/ppermute | solution.py:1027
  190.0 6.5 %second_back.1 = (f32[1024,768]{1,0:T(8,128)}, bf16[1024,768]{1,0:T(8,128)(2,1)}, f32[8,768]{1,0:T(8,128)}) custom-call(bf16[1024,768]{1,0:T(8,128)(2,1)} %join.1.cot_ref, f32[4,4,768]{2,1,0:T(4,128)} %reshape.508.slot_ref, f32[1024,1]{1,0:T(8,128)} %convert_element_type.272.mask_ref, f32[1024,768]{1,0:T(8,128)} %get-tuple-element.407.norm_ref, ...), custom_call_target="tpu_custom_call" | custom-call | flops 15728640 | bytes 9437184 | tf_op jit(solution)/shard_map/second_back/pallas_call | solution.py:556
  197.3 10.2 %tall_grad.1 = (bf16[16,96,768]{2,1,0:T(8,128)(2,1)}, bf16[16,96,768]{2,1,0:T(8,128)(2,1)}) custom-call(s32[3,16]{1,0:T(4,128)} %get-tuple-element.303.table_ref, bf16[1024,3072]{1,0:T(8,128)(2,1)} %get-tuple-element.385.left_ref, bf16[1024,768]{1,0:T(8,128)(2,1)} %get-tuple-element.419.right_ref.grad_ref), custom_call_target="tpu_custom_call" | custom-call | flops 4831838208 | bytes 12582912 | tf_op jit(solution)/shard_map/tall_grad/pallas_call | solution.py:243
  209.8 11.8 %hidden_grad.1 = (bf16[1024,3072]{1,0:T(8,128)(2,1)}, f32[1,3072]{1,0:T(1,128)}) custom-call(bf16[1024,768]{1,0:T(8,128)(2,1)} %get-tuple-element.419.right_ref.grad_ref, bf16[3072,768]{1,0:T(8,128)(2,1)} %bitcast.69, bf16[1024,3072]{1,0:T(8,128)(2,1)} %get-tuple-element.420.slope_ref), custom_call_target="tpu_custom_call" | custom-call | flops 4831838208 | bytes 18874368 | tf_op jit(solution)/shard_map/hidden_grad/pallas_call | solution.py:289
  224.8 9.9 %weight_grad.3 = (bf16[16,24,3840]{2,1,0:T(8,128)(2,1)}, bf16[16,24,3840]{2,1,0:T(8,128)(2,1)}) custom-call(s32[3,16]{1,0:T(4,128)} %get-tuple-element.303.table_ref, bf16[1024,768]{1,0:T(8,128)(2,1)} %get-tuple-element.364.mid_ref.left_ref, bf16[1024,3072]{1,0:T(8,128)(2,1)} %get-tuple-element.437.right_ref.hidden_ref), custom_call_target="tpu_custom_call" | custom-call | flops 4831838208 | bytes 12582912 | tf_op jit(solution)/shard_map/weight_grad/pallas_call | solution.py:201
  236.4 12.3 %first_back.1 = (f32[1024,768]{1,0:T(8,128)}, bf16[1024,768]{1,0:T(8,128)(2,1)}, f32[8,768]{1,0:T(8,128)}) custom-call(bf16[1024,3072]{1,0:T(8,128)(2,1)} %get-tuple-element.437.right_ref.hidden_ref, bf16[768,3072]{1,0:T(8,128)(2,1)} %bitcast.64, f32[1024,768]{1,0:T(8,128)} %get-tuple-element.438.second_ref, f32[1024,768]{1,0:T(8,128)} %get-tuple-element.439.norm_ref, ...), custom_call_target="tpu_custom_call" | custom-call | flops 4831838208 | bytes 22020096 | tf_op jit(solution)/shard_map/first_back/pallas_call | solution.py:596
  248.8 5.2 %weight_grad.4 = (bf16[16,24,3840]{2,1,0:T(8,128)(2,1)}, bf16[16,24,3840]{2,1,0:T(8,128)(2,1)}) custom-call(s32[3,16]{1,0:T(4,128)} %get-tuple-element.303.table_ref, bf16[1024,768]{1,0:T(8,128)(2,1)} %get-tuple-element.345.left_ref, bf16[1024,768]{1,0:T(8,128)(2,1)} %get-tuple-element.457.right_ref, ...), custom_call_target="tpu_custom_call", output_to_operand_aliasing={{0}: (3, {}), {1}: (4, {})} | custom-call | flops 1207959552 | bytes 4325376 | tf_op jit(solution)/shard_map/weight_grad/pallas_call | solution.py:201
  254.0 2.2 add_convert_fusion.4
  257.1 3.8 convolution_convert_fusion.grad_ref
  260.9 11.9 %attention_back.2 = (bf16[1024,2304]{1,0:T(8,128)(2,1)}, f32[1,2304]{1,0:T(1,128)}) custom-call(bf16[1024,2304]{1,0:T(8,128)(2,1)} %get-tuple-element.332.qkv_ref, bf16[4,12,256,256]{3,2,1,0:T(8,128)(2,1)} %get-tuple-element.456.probs_ref, bf16[1024,768]{1,0:T(8,128)(2,1)} %convolution_convert_fusion.grad_ref), custom_call_target="tpu_custom_call" | custom-call | flops 1610612736 | bytes 8650752 | tf_op jit(solution)/shard_map/attention_back/pallas_call | solution.py:425
  278.4 6.2 %token_grad.2 = (bf16[160,768]{1,0:T(8,128)(2,1)}, bf16[96,768]{1,0:T(8,128)(2,1)}, bf16[96,768]{1,0:T(8,128)(2,1)}, bf16[160,768]{1,0:T(8,128)(2,1)}) custom-call(bf16[1024,2304]{1,0:T(8,128)(2,1)} %get-tuple-element.480.grad_ref._, bf16[768,2304]{1,0:T(8,128)(2,1)} %bitcast.66, f32[1024,768]{1,0:T(8,128)} %get-tuple-element.475.first_ref), custom_call_target="tpu_custom_call" | custom-call | flops 1811939328 | bytes 8257536 | tf_op jit(solution)/shard_map/token_grad/pallas_call | solution.py:682
  285.7 11.7 %attention_back.3 = (bf16[1024,2304]{1,0:T(8,128)(2,1)}, f32[1,2304]{1,0:T(1,128)}) custom-call(bf16[1024,2304]{1,0:T(8,128)(2,1)} %get-tuple-element.332.qkv_ref, bf16[4,12,256,256]{3,2,1,0:T(8,128)(2,1)} %get-tuple-element.456.probs_ref, bf16[1024,768]{1,0:T(8,128)(2,1)} %convolution_convert_fusion.grad_ref, ...), custom_call_target="tpu_custom_call", output_to_operand_aliasing={{0}: (3, {})} | custom-call | flops 1610612736 | bytes 8650752 | tf_op jit(solution)/shard_map/attention_back/pallas_call | solution.py:425
  305.4 2.1 collective-permute-start.45
  307.5 9.2 %weight_grad.5 = (bf16[16,24,2432]{2,1,0:T(8,128)(2,1)}, bf16[16,24,2432]{2,1,0:T(8,128)(2,1)}) custom-call(s32[3,16]{1,0:T(4,128)} %get-tuple-element.303.table_ref, bf16[1024,768]{1,0:T(8,128)(2,1)} %get-tuple-element.347.base_ref.left_ref, bf16[1024,2304]{1,0:T(8,128)(2,1)} %get-tuple-element.517.right_ref.grad_ref, ...), custom_call_target="tpu_custom_call" | custom-call | flops 3623878656 | bytes 9830400 | tf_op jit(solution)/shard_map/weight_grad/pallas_call | solution.py:201
  316.7 2.9 collective-permute-done.45.refs_1_
  319.8 6.6 %token_grad.3.own_ref = f32[512,768]{1,0:T(8,128)} custom-call(bf16[1024,2304]{1,0:T(8,128)(2,1)} %get-tuple-element.517.right_ref.grad_ref, bf16[768,2304]{1,0:T(8,128)(2,1)} %bitcast.67, f32[1024,768]{1,0:T(8,128)} %get-tuple-element.475.first_ref), custom_call_target="tpu_custom_call" | custom-call | flops 1811939328 | bytes 8257536 | tf_op jit(solution)/shard_map/token_grad/pallas_call | solution.py:682
  326.4 2.8 collective-permute-done.47.refs_2_
  333.3 2.5 collective-permute-start.50
  335.8 13.0 %collective-permute-done.49 = bf16[2,24,3840]{2,1,0:T(8,128)(2,1)} collective-permute-done((bf16[2,24,3840]{2,1,0:T(8,128)(2,1)S(1)}, bf16[2,24,3840]{2,1,0:T(8,128)(2,1)}, u32[]{:S(2)}, u32[]{:S(2)}) %collective-permute-start.49) | collective-permute-done | bytes 368672 | tf_op jit(solution)/shard_map/ppermute | solution.py:66
  354.0 8.7 %collective-permute-done.52 = bf16[1,24,3840]{2,1,0:T(8,128)(2,1)S(1)} collective-permute-done((bf16[1,24,3840]{2,1,0:T(8,128)(2,1)S(1)}, bf16[1,24,3840]{2,1,0:T(8,128)(2,1)S(1)}, u32[]{:S(2)}, u32[]{:S(2)}) %collective-permute-start.52) | collective-permute-done | bytes 184352 | tf_op jit(solution)/shard_map/ppermute | solution.py:66
  364.7 2.7 deal.2
  367.3 3.8 collective-permute-done.53
  377.5 3.5 deal.3
  (325 shorter events, 96.7 us)
Async XLA Ops:
  3.5 11.4 %collective-permute-start = (bf16[1,24,3200]{2,1,0:T(8,128)(2,1)S(1)}, bf16[1,24,3200]{2,1,0:T(8,128)(2,1)S(1)}, u32[]{:S(2)}, u32[]{:S(2)}) collective-permute-start(bf16[1,24,3200]{2,1,0:T(8,128)(2,1)S(1)} %get-tuple-element.643), channel_id=1, source_target_pairs={{0,4},{1,5},{2,6},{3,7},{4,0},{5,1},{6,2},{7,3},{8,12},{9,13},{10,... | collective-permute-start | bytes 460808 | tf_op jit(solution)/shard_map/ppermute | solution.py:66
  15.0 13.8 %collective-permute-start.1 = (bf16[2,24,3200]{2,1,0:T(8,128)(2,1)S(1)}, bf16[2,24,3200]{2,1,0:T(8,128)(2,1)S(1)}, u32[]{:S(2)}, u32[]{:S(2)}) collective-permute-start(bf16[2,24,3200]{2,1,0:T(8,128)(2,1)S(1)} %pad_maximum_fusion.8), channel_id=1, source_target_pairs={{0,2},{1,3},{2,0},{3,1},{4,6},{5,7},{6,4},{7,5},{8,10},{9,11},{10,... | collective-permute-start | bytes 921608 | tf_op jit(solution)/shard_map/ppermute | solution.py:66
  15.8 13.1 %collective-permute-start.2 = (bf16[160,768]{1,0:T(8,128)(2,1)S(1)}, bf16[160,768]{1,0:T(8,128)(2,1)S(1)}, u32[]{:S(2)}, u32[]{:S(2)}) collective-permute-start(bf16[160,768]{1,0:T(8,128)(2,1)S(1)} %slice.382), channel_id=1, source_target_pairs={{0,4},{1,5},{2,6},{3,7},{4,0},{5,1},{6,2},{7,3},{8,12},{9,13},{10,... | collective-permute-start | bytes 737288 | tf_op jit(solution)/shard_map/ppermute | solution.py:72
  28.9 10.6 %collective-permute-start.3 = (bf16[4,24,3200]{2,1,0:T(8,128)(2,1)S(1)}, bf16[4,24,3200]{2,1,0:T(8,128)(2,1)S(1)}, u32[]{:S(2)}, u32[]{:S(2)}) collective-permute-start(bf16[4,24,3200]{2,1,0:T(8,128)(2,1)S(1)} %pad_maximum_fusion.3), channel_id=1, source_target_pairs={{0,8},{1,17},{2,10},{3,19},{4,12},{5,21},{6,14},{7,23},{8,0},{9,25... | collective-permute-start | bytes 1843208 | tf_op jit(solution)/shard_map/ppermute | solution.py:66
  30.2 9.2 %collective-permute-start.4 = (bf16[1,24,3072]{2,1,0:T(8,128)(2,1)S(1)}, bf16[1,24,3072]{2,1,0:T(8,128)(2,1)S(1)}, u32[]{:S(2)}, u32[]{:S(2)}) collective-permute-start(bf16[1,24,3072]{2,1,0:T(8,128)(2,1)S(1)} %get-tuple-element.306), channel_id=1, source_target_pairs={{0,4},{1,5},{2,6},{3,7},{4,0},{5,1},{6,2},{7,3},{8,12},{9,13},{10,... | collective-permute-start | bytes 442376 | tf_op jit(solution)/shard_map/ppermute | solution.py:66
  39.7 18.4 %collective-permute-start.5 = (bf16[8,24,3200]{2,1,0:T(8,128)(2,1)S(1)}, bf16[8,24,3200]{2,1,0:T(8,128)(2,1)}, u32[]{:S(2)}, u32[]{:S(2)}) collective-permute-start(bf16[8,24,3200]{2,1,0:T(8,128)(2,1)S(1)} %pad_maximum_fusion.refs_0_), channel_id=1, source_target_pairs={{0,16},{1,9},{2,18},{3,11},{4,20},{5,13},{6,22},{7,15},{8,24},{9,1... | collective-permute-start | bytes 3686408 | tf_op jit(solution)/shard_map/ppermute | solution.py:66
  45.9 24.1 %collective-permute-start.8 = (bf16[8,24,3200]{2,1,0:T(8,128)(2,1)S(1)}, bf16[8,24,3200]{2,1,0:T(8,128)(2,1)}, u32[]{:S(2)}, u32[]{:S(2)}) collective-permute-start(bf16[8,24,3200]{2,1,0:T(8,128)(2,1)S(1)} %pad_maximum_fusion.refs_0_), channel_id=1, source_target_pairs={{0,1},{1,0},{2,3},{3,2},{4,5},{5,4},{6,7},{7,6},{8,9},{9,8},{10,11... | collective-permute-start | bytes 3686408 | tf_op jit(solution)/shard_map/ppermute | solution.py:69
  45.9 12.1 %collective-permute-start.7 = (bf16[128,768]{1,0:T(8,128)(2,1)S(1)}, bf16[128,768]{1,0:T(8,128)(2,1)S(1)}, u32[]{:S(2)}, u32[]{:S(2)}) collective-permute-start(bf16[128,768]{1,0:T(8,128)(2,1)S(1)} %slice.383), channel_id=1, source_target_pairs={{0,4},{1,5},{2,6},{3,7},{4,0},{5,1},{6,2},{7,3},{8,12},{9,13},{10,... | collective-permute-start | bytes 589832 | tf_op jit(solution)/shard_map/ppermute | solution.py:72
  58.1 12.0 %collective-permute-start.9 = (bf16[8,24,3200]{2,1,0:T(8,128)(2,1)}, bf16[8,24,3200]{2,1,0:T(8,128)(2,1)}, u32[]{:S(2)}, u32[]{:S(2)}) collective-permute-start(bf16[8,24,3200]{2,1,0:T(8,128)(2,1)} %collective-permute-done.5.refs_1_), channel_id=1, source_target_pairs={{0,1},{1,0},{2,3},{3,2},{4,5},{5,4},{6,7},{7,6},{8,9},{9,8},{10,11... | collective-permute-start | bytes 3686408 | tf_op jit(solution)/shard_map/ppermute | solution.py:69
  58.8 10.0 %collective-permute-start.10 = (bf16[4,24,3072]{2,1,0:T(8,128)(2,1)S(1)}, bf16[4,24,3072]{2,1,0:T(8,128)(2,1)}, u32[]{:S(2)}, u32[]{:S(2)}) collective-permute-start(bf16[4,24,3072]{2,1,0:T(8,128)(2,1)S(1)} %pad_maximum_fusion.5), channel_id=1, source_target_pairs={{0,8},{1,17},{2,10},{3,19},{4,12},{5,21},{6,14},{7,23},{8,0},{9,25... | collective-permute-start | bytes 1769480 | tf_op jit(solution)/shard_map/ppermute | solution.py:66
  60.3 17.6 %collective-permute-start.11 = (bf16[224,768]{1,0:T(8,128)(2,1)S(1)}, bf16[224,768]{1,0:T(8,128)(2,1)}, u32[]{:S(2)}, u32[]{:S(2)}) collective-permute-start(bf16[224,768]{1,0:T(8,128)(2,1)S(1)} %slice.384), channel_id=1, source_target_pairs={{0,4},{1,5},{2,6},{3,7},{4,0},{5,1},{6,2},{7,3},{8,12},{9,13},{10,... | collective-permute-start | bytes 1032200 | tf_op jit(solution)/shard_map/ppermute | solution.py:72
  61.1 31.2 %collective-permute-start.13 = (s32[512]{0:T(512)S(1)}, s32[512]{0:T(512)S(1)}, u32[]{:S(2)}, u32[]{:S(2)}) collective-permute-start(s32[512]{0:T(512)S(1)} %get-tuple-element.657), channel_id=1, source_target_pairs={{0,4},{1,5},{2,6},{3,7},{4,0},{5,1},{6,2},{7,3},{8,12},{9,13},{10,... | collective-permute-start | bytes 6152 | tf_op jit(solution)/shard_map/ppermute | solution.py:72
  79.0 26.3 %collective-permute-start.14 = (bf16[8,24,3072]{2,1,0:T(8,128)(2,1)S(1)}, bf16[8,24,3072]{2,1,0:T(8,128)(2,1)}, u32[]{:S(2)}, u32[]{:S(2)}) collective-permute-start(bf16[8,24,3072]{2,1,0:T(8,128)(2,1)S(1)} %pad_maximum_fusion.1.refs_0_), channel_id=1, source_target_pairs={{0,16},{1,9},{2,18},{3,11},{4,20},{5,13},{6,22},{7,15},{8,24},{9,1... | collective-permute-start | bytes 3538952 | tf_op jit(solution)/shard_map/ppermute | solution.py:66
  81.8 8.8 %collective-permute-start.12 = (bf16[1,96,768]{2,1,0:T(8,128)(2,1)S(1)}, bf16[1,96,768]{2,1,0:T(8,128)(2,1)S(1)}, u32[]{:S(2)}, u32[]{:S(2)}) collective-permute-start(bf16[1,96,768]{2,1,0:T(8,128)(2,1)S(1)} %copy-done.40), channel_id=1, source_target_pairs={{0,4},{1,5},{2,6},{3,7},{4,0},{5,1},{6,2},{7,3},{8,12},{9,13},{10,... | collective-permute-start | bytes 442376 | tf_op jit(solution)/shard_map/ppermute | solution.py:66
  90.7 13.8 %collective-permute-start.15 = (bf16[2,96,768]{2,1,0:T(8,128)(2,1)S(1)}, bf16[2,96,768]{2,1,0:T(8,128)(2,1)S(1)}, u32[]{:S(2)}, u32[]{:S(2)}) collective-permute-start(bf16[2,96,768]{2,1,0:T(8,128)(2,1)S(1)} %pad_maximum_fusion.10), channel_id=1, source_target_pairs={{0,2},{1,3},{2,0},{3,1},{4,6},{5,7},{6,4},{7,5},{8,10},{9,11},{10,... | collective-permute-start | bytes 884744 | tf_op jit(solution)/shard_map/ppermute | solution.py:66
  92.8 25.2 %collective-permute-start.17 = (bf16[8,24,3072]{2,1,0:T(8,128)(2,1)S(1)}, bf16[8,24,3072]{2,1,0:T(8,128)(2,1)}, u32[]{:S(2)}, u32[]{:S(2)}) collective-permute-start(bf16[8,24,3072]{2,1,0:T(8,128)(2,1)S(1)} %pad_maximum_fusion.1.refs_0_), channel_id=1, source_target_pairs={{0,1},{1,0},{2,3},{3,2},{4,5},{5,4},{6,7},{7,6},{8,9},{9,8},{10,11... | collective-permute-start | bytes 3538952 | tf_op jit(solution)/shard_map/ppermute | solution.py:69
  92.9 12.5 %collective-permute-start.16 = (bf16[128,768]{1,0:T(8,128)(2,1)S(1)}, bf16[128,768]{1,0:T(8,128)(2,1)S(1)}, u32[]{:S(2)}, u32[]{:S(2)}) collective-permute-start(bf16[128,768]{1,0:T(8,128)(2,1)S(1)} %copy-done.31), channel_id=1, source_target_pairs={{0,4},{1,5},{2,6},{3,7},{4,0},{5,1},{6,2},{7,3},{8,12},{9,13},{10,... | collective-permute-start | bytes 589832 | tf_op jit(solution)/shard_map/ppermute | solution.py:72
  105.3 12.7 %collective-permute-start.18 = (bf16[8,24,3072]{2,1,0:T(8,128)(2,1)}, bf16[8,24,3072]{2,1,0:T(8,128)(2,1)}, u32[]{:S(2)}, u32[]{:S(2)}) collective-permute-start(bf16[8,24,3072]{2,1,0:T(8,128)(2,1)} %collective-permute-done.14.refs_1_), channel_id=1, source_target_pairs={{0,1},{1,0},{2,3},{3,2},{4,5},{5,4},{6,7},{7,6},{8,9},{9,8},{10,11... | collective-permute-start | bytes 3538952 | tf_op jit(solution)/shard_map/ppermute | solution.py:69
  105.3 11.5 %collective-permute-start.19 = (bf16[4,96,768]{2,1,0:T(8,128)(2,1)S(1)}, bf16[4,96,768]{2,1,0:T(8,128)(2,1)}, u32[]{:S(2)}, u32[]{:S(2)}) collective-permute-start(bf16[4,96,768]{2,1,0:T(8,128)(2,1)S(1)} %pad_maximum_fusion.6), channel_id=1, source_target_pairs={{0,8},{1,17},{2,10},{3,19},{4,12},{5,21},{6,14},{7,23},{8,0},{9,25... | collective-permute-start | bytes 1769480 | tf_op jit(solution)/shard_map/ppermute | solution.py:66
  107.6 10.4 %collective-permute-start.20 = (bf16[96,768]{1,0:T(8,128)(2,1)}, bf16[96,768]{1,0:T(8,128)(2,1)S(1)}, u32[]{:S(2)}, u32[]{:S(2)}) collective-permute-start(bf16[96,768]{1,0:T(8,128)(2,1)} %get-tuple-element.352), channel_id=1, source_target_pairs={{0,4},{1,5},{2,6},{3,7},{4,0},{5,1},{6,2},{7,3},{8,12},{9,13},{10,... | collective-permute-start | bytes 442376 | tf_op jit(solution)/shard_map/ppermute | solution.py:72
  118.0 17.6 %collective-permute-start.21 = (bf16[8,96,768]{2,1,0:T(8,128)(2,1)S(1)}, bf16[8,96,768]{2,1,0:T(8,128)(2,1)}, u32[]{:S(2)}, u32[]{:S(2)}) collective-permute-start(bf16[8,96,768]{2,1,0:T(8,128)(2,1)S(1)} %pad_maximum_fusion.2.refs_0_), channel_id=1, source_target_pairs={{0,16},{1,9},{2,18},{3,11},{4,20},{5,13},{6,22},{7,15},{8,24},{9,1... | collective-permute-start | bytes 3538952 | tf_op jit(solution)/shard_map/ppermute | solution.py:66
  119.4 16.3 %collective-permute-start.22 = (bf16[8,96,768]{2,1,0:T(8,128)(2,1)S(1)}, bf16[8,96,768]{2,1,0:T(8,128)(2,1)}, u32[]{:S(2)}, u32[]{:S(2)}) collective-permute-start(bf16[8,96,768]{2,1,0:T(8,128)(2,1)S(1)} %pad_maximum_fusion.2.refs_0_), channel_id=1, source_target_pairs={{0,1},{1,0},{2,3},{3,2},{4,5},{5,4},{6,7},{7,6},{8,9},{9,8},{10,11... | collective-permute-start | bytes 3538952 | tf_op jit(solution)/shard_map/ppermute | solution.py:69
  125.3 10.4 %collective-permute-start.23 = (bf16[96,768]{1,0:T(8,128)(2,1)S(1)}, bf16[96,768]{1,0:T(8,128)(2,1)S(1)}, u32[]{:S(2)}, u32[]{:S(2)}) collective-permute-start(bf16[96,768]{1,0:T(8,128)(2,1)S(1)} %copy-done.37), channel_id=1, source_target_pairs={{0,4},{1,5},{2,6},{3,7},{4,0},{5,1},{6,2},{7,3},{8,12},{9,13},{10,... | collective-permute-start | bytes 442376 | tf_op jit(solution)/shard_map/ppermute | solution.py:72
  135.7 9.3 %collective-permute-start.24 = (bf16[8,96,768]{2,1,0:T(8,128)(2,1)}, bf16[8,96,768]{2,1,0:T(8,128)(2,1)S(1)}, u32[]{:S(2)}, u32[]{:S(2)}) collective-permute-start(bf16[8,96,768]{2,1,0:T(8,128)(2,1)} %collective-permute-done.21.refs_1_), channel_id=1, source_target_pairs={{0,1},{1,0},{2,3},{3,2},{4,5},{5,4},{6,7},{7,6},{8,9},{9,8},{10,11... | collective-permute-start | bytes 3538952 | tf_op jit(solution)/shard_map/ppermute | solution.py:69
  136.2 8.8 %collective-permute-start.25 = (bf16[64,768]{1,0:T(8,128)(2,1)S(1)}, bf16[64,768]{1,0:T(8,128)(2,1)S(1)}, u32[]{:S(2)}, u32[]{:S(2)}) collective-permute-start(bf16[64,768]{1,0:T(8,128)(2,1)S(1)} %copy-done.42), channel_id=1, source_target_pairs={{0,4},{1,5},{2,6},{3,7},{4,0},{5,1},{6,2},{7,3},{8,12},{9,13},{10,... | collective-permute-start | bytes 294920 | tf_op jit(solution)/shard_map/ppermute | solution.py:72
  150.9 13.8 %collective-permute-start.26 = (bf16[128,768]{1,0:T(8,128)(2,1)S(1)}, bf16[128,768]{1,0:T(8,128)(2,1)S(1)}, u32[]{:S(2)}, u32[]{:S(2)}) collective-permute-start(bf16[128,768]{1,0:T(8,128)(2,1)S(1)} %copy-done.30), channel_id=1, source_target_pairs={{0,4},{1,5},{2,6},{3,7},{4,0},{5,1},{6,2},{7,3},{8,12},{9,13},{10,... | collective-permute-start | bytes 589832 | tf_op jit(solution)/shard_map/ppermute | solution.py:72
  196.5 11.9 %collective-permute-start.32 = (bf16[128,768]{1,0:T(8,128)(2,1)S(1)}, bf16[128,768]{1,0:T(8,128)(2,1)S(1)}, u32[]{:S(2)}, u32[]{:S(2)}) collective-permute-start(bf16[128,768]{1,0:T(8,128)(2,1)S(1)} %get-tuple-element.413), channel_id=1, source_target_pairs={{0,4},{1,5},{2,6},{3,7},{4,0},{5,1},{6,2},{7,3},{8,12},{9,13},{10,... | collective-permute-start | bytes 589832 | tf_op jit(solution)/shard_map/ppermute | solution.py:72
  208.4 13.3 %collective-permute-start.33 = (bf16[16,96,768]{2,1,0:T(8,128)(2,1)}, bf16[16,96,768]{2,1,0:T(8,128)(2,1)S(1)}, u32[]{:S(2)}, u32[]{:S(2)}) collective-permute-start(bf16[16,96,768]{2,1,0:T(8,128)(2,1)} %get-tuple-element.418), channel_id=1, source_target_pairs={{0,1},{1,0},{2,3},{3,2},{4,5},{5,4},{6,7},{7,6},{8,9},{9,8},{10,11... | collective-permute-start | bytes 7077896 | tf_op jit(solution)/shard_map/ppermute | solution.py:69
  208.4 13.2 %collective-permute-start.34 = (bf16[128,768]{1,0:T(8,128)(2,1)S(1)}, bf16[128,768]{1,0:T(8,128)(2,1)S(1)}, u32[]{:S(2)}, u32[]{:S(2)}) collective-permute-start(bf16[128,768]{1,0:T(8,128)(2,1)S(1)} %copy-done.28), channel_id=1, source_target_pairs={{0,4},{1,5},{2,6},{3,7},{4,0},{5,1},{6,2},{7,3},{8,12},{9,13},{10,... | collective-permute-start | bytes 589832 | tf_op jit(solution)/shard_map/ppermute | solution.py:72
  222.3 26.5 %collective-permute-start.35 = (bf16[8,96,768]{2,1,0:T(8,128)(2,1)S(1)}, bf16[8,96,768]{2,1,0:T(8,128)(2,1)S(1)}, u32[]{:S(2)}, u32[]{:S(2)}) collective-permute-start(bf16[8,96,768]{2,1,0:T(8,128)(2,1)S(1)} %add_convert_fusion.1), channel_id=1, source_target_pairs={{0,16},{1,9},{2,18},{3,11},{4,20},{5,13},{6,22},{7,15},{8,24},{9,1... | collective-permute-start | bytes 3538952 | tf_op jit(solution)/shard_map/ppermute | solution.py:66
  223.5 11.7 %collective-permute-start.36 = (bf16[128,768]{1,0:T(8,128)(2,1)S(1)}, bf16[128,768]{1,0:T(8,128)(2,1)S(1)}, u32[]{:S(2)}, u32[]{:S(2)}) collective-permute-start(bf16[128,768]{1,0:T(8,128)(2,1)S(1)} %get-tuple-element.433), channel_id=1, source_target_pairs={{0,4},{1,5},{2,6},{3,7},{4,0},{5,1},{6,2},{7,3},{8,12},{9,13},{10,... | collective-permute-start | bytes 589832 | tf_op jit(solution)/shard_map/ppermute | solution.py:72
  235.2 13.6 %collective-permute-start.37 = (bf16[128,768]{1,0:T(8,128)(2,1)S(1)}, bf16[128,768]{1,0:T(8,128)(2,1)S(1)}, u32[]{:S(2)}, u32[]{:S(2)}) collective-permute-start(bf16[128,768]{1,0:T(8,128)(2,1)S(1)} %copy-done.27), channel_id=1, source_target_pairs={{0,4},{1,5},{2,6},{3,7},{4,0},{5,1},{6,2},{7,3},{8,12},{9,13},{10,... | collective-permute-start | bytes 589832 | tf_op jit(solution)/shard_map/ppermute | solution.py:72
  254.0 18.9 %collective-permute-start.39 = (bf16[16,24,3840]{2,1,0:T(8,128)(2,1)}, bf16[16,24,3840]{2,1,0:T(8,128)(2,1)S(1)}, u32[]{:S(2)}, u32[]{:S(2)}) collective-permute-start(bf16[16,24,3840]{2,1,0:T(8,128)(2,1)} %get-tuple-element.455), channel_id=1, source_target_pairs={{0,1},{1,0},{2,3},{3,2},{4,5},{5,4},{6,7},{7,6},{8,9},{9,8},{10,11... | collective-permute-start | bytes 8847368 | tf_op jit(solution)/shard_map/ppermute | solution.py:69
  256.2 16.6 %collective-permute-start.38 = (bf16[4,96,768]{2,1,0:T(8,128)(2,1)}, bf16[4,96,768]{2,1,0:T(8,128)(2,1)S(1)}, u32[]{:S(2)}, u32[]{:S(2)}) collective-permute-start(bf16[4,96,768]{2,1,0:T(8,128)(2,1)} %add_convert_fusion.4), channel_id=1, source_target_pairs={{0,8},{1,17},{2,10},{3,19},{4,12},{5,21},{6,14},{7,23},{8,0},{9,25... | collective-permute-start | bytes 1769480 | tf_op jit(solution)/shard_map/ppermute | solution.py:66
  275.9 22.7 %collective-permute-start.41 = (bf16[8,24,3840]{2,1,0:T(8,128)(2,1)}, bf16[8,24,3840]{2,1,0:T(8,128)(2,1)S(1)}, u32[]{:S(2)}, u32[]{:S(2)}) collective-permute-start(bf16[8,24,3840]{2,1,0:T(8,128)(2,1)} %add_convert_fusion), channel_id=1, source_target_pairs={{0,16},{1,9},{2,18},{3,11},{4,20},{5,13},{6,22},{7,15},{8,24},{9,1... | collective-permute-start | bytes 4423688 | tf_op jit(solution)/shard_map/ppermute | solution.py:66
  277.1 21.4 %collective-permute-start.40 = (bf16[2,96,768]{2,1,0:T(8,128)(2,1)S(1)}, bf16[2,96,768]{2,1,0:T(8,128)(2,1)S(1)}, u32[]{:S(2)}, u32[]{:S(2)}) collective-permute-start(bf16[2,96,768]{2,1,0:T(8,128)(2,1)S(1)} %add_convert_fusion.7), channel_id=1, source_target_pairs={{0,2},{1,3},{2,0},{3,1},{4,6},{5,7},{6,4},{7,5},{8,10},{9,11},{10,... | collective-permute-start | bytes 884744 | tf_op jit(solution)/shard_map/ppermute | solution.py:66
  284.6 13.9 %collective-permute-start.42 = (bf16[160,768]{1,0:T(8,128)(2,1)}, bf16[160,768]{1,0:T(8,128)(2,1)}, u32[]{:S(2)}, u32[]{:S(2)}) collective-permute-start(bf16[160,768]{1,0:T(8,128)(2,1)} %get-tuple-element.483), channel_id=1, source_target_pairs={{0,4},{1,5},{2,6},{3,7},{4,0},{5,1},{6,2},{7,3},{8,12},{9,13},{10,... | collective-permute-start | bytes 737288 | tf_op jit(solution)/shard_map/ppermute | solution.py:72
  299.9 19.7 %collective-permute-start.43 = (bf16[4,24,3840]{2,1,0:T(8,128)(2,1)}, bf16[4,24,3840]{2,1,0:T(8,128)(2,1)}, u32[]{:S(2)}, u32[]{:S(2)}) collective-permute-start(bf16[4,24,3840]{2,1,0:T(8,128)(2,1)} %add_convert_fusion.3), channel_id=1, source_target_pairs={{0,8},{1,17},{2,10},{3,19},{4,12},{5,21},{6,14},{7,23},{8,0},{9,25... | collective-permute-start | bytes 2211848 | tf_op jit(solution)/shard_map/ppermute | solution.py:66
  304.5 12.2 %collective-permute-start.44 = (bf16[1,96,768]{2,1,0:T(8,128)(2,1)S(1)}, bf16[1,96,768]{2,1,0:T(8,128)(2,1)S(1)}, u32[]{:S(2)}, u32[]{:S(2)}) collective-permute-start(bf16[1,96,768]{2,1,0:T(8,128)(2,1)S(1)} %add_convert_fusion.10), channel_id=1, source_target_pairs={{0,4},{1,5},{2,6},{3,7},{4,0},{5,1},{6,2},{7,3},{8,12},{9,13},{10,... | collective-permute-start | bytes 442376 | tf_op jit(solution)/shard_map/ppermute | solution.py:66
  305.4 14.2 %collective-permute-start.45 = (bf16[96,768]{1,0:T(8,128)(2,1)}, bf16[96,768]{1,0:T(8,128)(2,1)S(1)}, u32[]{:S(2)}, u32[]{:S(2)}) collective-permute-start(bf16[96,768]{1,0:T(8,128)(2,1)} %get-tuple-element.512), channel_id=1, source_target_pairs={{0,4},{1,5},{2,6},{3,7},{4,0},{5,1},{6,2},{7,3},{8,12},{9,13},{10,... | collective-permute-start | bytes 442376 | tf_op jit(solution)/shard_map/ppermute | solution.py:72
  319.6 9.6 %collective-permute-start.46 = (bf16[16,24,2432]{2,1,0:T(8,128)(2,1)}, bf16[16,24,2432]{2,1,0:T(8,128)(2,1)S(1)}, u32[]{:S(2)}, u32[]{:S(2)}) collective-permute-start(bf16[16,24,2432]{2,1,0:T(8,128)(2,1)} %get-tuple-element.516), channel_id=1, source_target_pairs={{0,1},{1,0},{2,3},{3,2},{4,5},{5,4},{6,7},{7,6},{8,9},{9,8},{10,11... | collective-permute-start | bytes 5603336 | tf_op jit(solution)/shard_map/ppermute | solution.py:69
  319.7 9.5 %collective-permute-start.47 = (bf16[96,768]{1,0:T(8,128)(2,1)S(1)}, bf16[96,768]{1,0:T(8,128)(2,1)S(1)}, u32[]{:S(2)}, u32[]{:S(2)}) collective-permute-start(bf16[96,768]{1,0:T(8,128)(2,1)S(1)} %copy-done.59), channel_id=1, source_target_pairs={{0,4},{1,5},{2,6},{3,7},{4,0},{5,1},{6,2},{7,3},{8,12},{9,13},{10,... | collective-permute-start | bytes 442376 | tf_op jit(solution)/shard_map/ppermute | solution.py:72
  330.6 18.2 %collective-permute-start.48 = (bf16[8,24,2432]{2,1,0:T(8,128)(2,1)}, bf16[8,24,2432]{2,1,0:T(8,128)(2,1)}, u32[]{:S(2)}, u32[]{:S(2)}) collective-permute-start(bf16[8,24,2432]{2,1,0:T(8,128)(2,1)} %add_convert_fusion.2), channel_id=1, source_target_pairs={{0,16},{1,9},{2,18},{3,11},{4,20},{5,13},{6,22},{7,15},{8,24},{9,1... | collective-permute-start | bytes 2801672 | tf_op jit(solution)/shard_map/ppermute | solution.py:66
  333.3 15.6 %collective-permute-start.49 = (bf16[2,24,3840]{2,1,0:T(8,128)(2,1)S(1)}, bf16[2,24,3840]{2,1,0:T(8,128)(2,1)}, u32[]{:S(2)}, u32[]{:S(2)}) collective-permute-start(bf16[2,24,3840]{2,1,0:T(8,128)(2,1)S(1)} %add_convert_fusion.6), channel_id=1, source_target_pairs={{0,2},{1,3},{2,0},{3,1},{4,6},{5,7},{6,4},{7,5},{8,10},{9,11},{10,... | collective-permute-start | bytes 1105928 | tf_op jit(solution)/shard_map/ppermute | solution.py:66
  333.3 15.5 %collective-permute-start.50 = (bf16[160,768]{1,0:T(8,128)(2,1)}, bf16[160,768]{1,0:T(8,128)(2,1)}, u32[]{:S(2)}, u32[]{:S(2)}) collective-permute-start(bf16[160,768]{1,0:T(8,128)(2,1)} %get-tuple-element.531), channel_id=1, source_target_pairs={{0,4},{1,5},{2,6},{3,7},{4,0},{5,1},{6,2},{7,3},{8,12},{9,13},{10,... | collective-permute-start | bytes 737288 | tf_op jit(solution)/shard_map/ppermute | solution.py:72
  350.3 12.3 %collective-permute-start.51 = (bf16[4,24,2432]{2,1,0:T(8,128)(2,1)S(1)}, bf16[4,24,2432]{2,1,0:T(8,128)(2,1)S(1)}, u32[]{:S(2)}, u32[]{:S(2)}) collective-permute-start(bf16[4,24,2432]{2,1,0:T(8,128)(2,1)S(1)} %add_convert_fusion.5), channel_id=1, source_target_pairs={{0,8},{1,17},{2,10},{3,19},{4,12},{5,21},{6,14},{7,23},{8,0},{9,25... | collective-permute-start | bytes 1400840 | tf_op jit(solution)/shard_map/ppermute | solution.py:66
  352.7 10.0 %collective-permute-start.52 = (bf16[1,24,3840]{2,1,0:T(8,128)(2,1)S(1)}, bf16[1,24,3840]{2,1,0:T(8,128)(2,1)S(1)}, u32[]{:S(2)}, u32[]{:S(2)}) collective-permute-start(bf16[1,24,3840]{2,1,0:T(8,128)(2,1)S(1)} %add_convert_fusion.9), channel_id=1, source_target_pairs={{0,4},{1,5},{2,6},{3,7},{4,0},{5,1},{6,2},{7,3},{8,12},{9,13},{10,... | collective-permute-start | bytes 552968 | tf_op jit(solution)/shard_map/ppermute | solution.py:66
  372.3 9.4 %collective-permute-start.54 = (bf16[1,24,2432]{2,1,0:T(8,128)(2,1)S(1)}, bf16[1,24,2432]{2,1,0:T(8,128)(2,1)S(1)}, u32[]{:S(2)}, u32[]{:S(2)}) collective-permute-start(bf16[1,24,2432]{2,1,0:T(8,128)(2,1)S(1)} %add_convert_fusion.11), channel_id=1, source_target_pairs={{0,4},{1,5},{2,6},{3,7},{4,0},{5,1},{6,2},{7,3},{8,12},{9,13},{10,... | collective-permute-start | bytes 350216 | tf_op jit(solution)/shard_map/ppermute | solution.py:66
  (67 other events, 620.3 us)

commit v12 on v11

--- a/solution.py
+++ b/solution.py
@@ -1186,18 +1186,20 @@
     sj.pb_first()
     se.along_z()
     got_grad = got_grad + hand(send_grad[3:])
-    sj.parts, se.parts, got_grad, send_grad = tie(sj.parts, se.parts, got_grad, send_grad)
+    out_q, out_p = deal(tower.reshape(1), out, got_out)
+    grad_reduce = sr.finish()
+    sj.parts, se.parts, got_grad, out_q, out_p, grad_reduce = tie(
+        sj.parts, se.parts, got_grad, out_q, out_p, grad_reduce
+    )
     sj.pb_rest()
     se.mid()
-    sj.parts, se.got, got_out, out = tie(sj.parts, se.got, got_out, out)
+    grad_q, grad_p = deal(tower.reshape(1), own_grad, got_grad)
+    sj.parts, se.got, se.parts, grad_q, grad_p = tie(sj.parts, se.got, se.parts, grad_q, grad_p)
     sj.along_z()
-    out_q, out_p = deal(tower.reshape(1), out, got_out)
-    sj.parts, out_q, out_p, got_grad, sr.got, sr.parts, se.got, se.parts = tie(
-        sj.parts, out_q, out_p, got_grad, sr.got, sr.parts, se.got, se.parts
-    )
-    grad_q, grad_p = deal(tower.reshape(1), own_grad, got_grad)
+    both = se.finish()
+    sj.parts, both = tie(sj.parts, both)
     sj.mid()
-    grad_reduce, both, last = sr.finish(), se.finish(), sj.finish()
+    last = sj.finish()
     grad_joined = last[:, :, : 3 * D]
     grad_expand, grad_output = both[:, :, :FF], both[:, :, FF:]
     extra = last[:, :, 3 * D :]

time: 387 us -> 388 us (level)
  transfers between devices with their start and end apart: 55 -> 55, of which waited for: 23 -> 24; matrix products, arithmetic and copies ran while one was open for 10% -> 9% of each run, Pallas kernels for 42% -> 42%
where the time goes in v12:
time: 388 us; the launch traced here: 386 us
  Pallas kernels  179 us (46%)
  waiting for transfers between devices  86.3 us (22%)
  starting transfers between devices  60 us (15%)
  other arithmetic  32.3 us (8%)
  local copies, waits for them, and re-layouts  22.3 us (6%)
  matrix products  4.48 us (1%)
    ppermute x24, waiting for transfers between devices, swap(): return lax.ppermute(values, AXES, self.pairs(step))  52 us
    ppermute x24, starting transfers between devices, swap(): return lax.ppermute(values, AXES, self.pairs(step))  30.8 us
    ppermute x18, starting transfers between devices, swap_tower(): lax.ppermute(values, 'pa', [(i, i ^ 2 * self.half) for i in range(self.pa...  26.6 us
    ppermute x18, waiting for transfers between devices, swap_tower(): lax.ppermute(values, 'pa', [(i, i ^ 2 * self.half) for i in range(self.pa...  25.3 us
    pallas_call x3, Pallas kernels, weight_grad(): pl.pallas_call(functools.partial(weight_grad_kernel, chips, len(extra or...  24 us
    pallas_call x2, Pallas kernels, attention_back(): pl.pallas_call(attention_back_more_kernel if more else attention_back_ker...  23.7 us
    pallas_call x2, Pallas kernels, add_norm(): pl.pallas_call(functools.partial(add_norm_kernel, rows_of), grid=(rows //...  19 us
    pallas_call x2, Pallas kernels, expand(): pl.pallas_call(expand_more_kernel if into else expand_kernel, grid=(count...  15.8 us
  transfers between devices with their start and end apart: 55, of which 24 were waited for; matrix products, arithmetic and copies ran while one was open for 9% of the time, Pallas kernels for 42%

profile of v12, /device:TPU:0, one launch (start us, length us, event | category | flops | bytes accessed | tf_op | source)
XLA Modules:
  0.0 386.5 jit_solution(8620369881304494508)
XLA Ops:
  3.5 4.1 %collective-permute-start = (bf16[1,24,3200]{2,1,0:T(8,128)(2,1)S(1)}, bf16[1,24,3200]{2,1,0:T(8,128)(2,1)S(1)}, u32[]{:S(2)}, u32[]{:S(2)}) collective-permute-start(bf16[1,24,3200]{2,1,0:T(8,128)(2,1)S(1)} %get-tuple-element.619), channel_id=1, source_target_pairs={{0,4},{1,5},{2,6},{3,7},{4,0},{5,1},{6,2},{7,3},{8,12},{9,13},{10,... | collective-permute-start | bytes 460808 | tf_op jit(solution)/shard_map/ppermute | solution.py:66
  12.3 2.6 collective-permute-done
  15.8 3.4 collective-permute-start.2
  20.2 8.5 %collective-permute-done.1 = bf16[2,24,3200]{2,1,0:T(8,128)(2,1)S(1)} collective-permute-done((bf16[2,24,3200]{2,1,0:T(8,128)(2,1)S(1)}, bf16[2,24,3200]{2,1,0:T(8,128)(2,1)S(1)}, u32[]{:S(2)}, u32[]{:S(2)}) %collective-permute-start.1) | collective-permute-done | bytes 307232 | tf_op jit(solution)/shard_map/ppermute | solution.py:66
  30.2 2.6 collective-permute-start.4
  32.8 6.6 %collective-permute-done.4 = bf16[1,24,3072]{2,1,0:T(8,128)(2,1)S(1)} collective-permute-done((bf16[1,24,3072]{2,1,0:T(8,128)(2,1)S(1)}, bf16[1,24,3072]{2,1,0:T(8,128)(2,1)S(1)}, u32[]{:S(2)}, u32[]{:S(2)}) %collective-permute-start.4) | collective-permute-done | bytes 147488 | tf_op jit(solution)/shard_map/ppermute | solution.py:66
  41.0 2.8 collective-permute-start.6
  49.3 8.8 %collective-permute-done.7.refs_2_ = bf16[128,768]{1,0:T(8,128)(2,1)S(1)} collective-permute-done((bf16[128,768]{1,0:T(8,128)(2,1)S(1)}, bf16[128,768]{1,0:T(8,128)(2,1)S(1)}, u32[]{:S(2)}, u32[]{:S(2)}) %collective-permute-start.7) | collective-permute-done | bytes 196640 | tf_op jit(solution)/shard_map/ppermute | solution.py:72
  61.0 2.5 collective-permute-start.13
  63.5 5.3 %collective-permute-done.10 = bf16[4,24,3072]{2,1,0:T(8,128)(2,1)} collective-permute-done((bf16[4,24,3072]{2,1,0:T(8,128)(2,1)S(1)}, bf16[4,24,3072]{2,1,0:T(8,128)(2,1)}, u32[]{:S(2)}, u32[]{:S(2)}) %collective-permute-start.10) | collective-permute-done | bytes 589856 | tf_op jit(solution)/shard_map/ppermute | solution.py:66
  70.1 5.5 %assemble.3 = (bf16[16,2,24,2304]{3,2,1,0:T(8,128)(2,1)}, bf16[16,2,24,768]{3,2,1,0:T(8,128)(2,1)}, bf16[16,2,24,128]{3,2,1,0:T(8,128)(2,1)}) custom-call(s32[3,16]{1,0:T(4,128)} %get-tuple-element.292.idx_ref, bf16[8,24,3200]{2,1,0:T(8,128)(2,1)} %copy-done.1, bf16[8,24,3200]{2,1,0:T(8,128)(2,1)} %collective-permute-done.5.refs_1_, ...), custom_call_target="tpu_custom_call" | custom-call | bytes 9830400 | tf_op jit(solution)/shard_map/assemble/pallas_call | solution.py:118
  75.6 2.4 collective-permute-done.11.refs_3_
  81.9 8.5 %project.1 = (bf16[1024,768]{1,0:T(8,128)(2,1)}, bf16[1024,2304]{1,0:T(8,128)(2,1)}) custom-call(bf16[768,2304]{1,0:T(8,128)(2,1)} %bitcast.65, f32[1,2304]{1,0:T(1,128)} %broadcast_in_dim.14.b_ref, bf16[512,768]{1,0:T(8,128)(2,1)} %get-tuple-element.610.refs_0_, bf16[160,768]{1,0:T(8,128)(2,1)} %copy-done.61, bf16[128,768]{1,0:T(8,128)(2,1)} %copy-done.63, ...), custom_call_target="tpu_custom_call" | custom-call | flops 3623878656 | bytes 11403264 | tf_op jit(solution)/shard_map/project/pallas_call | solution.py:716
  93.9 10.6 %attention.1 = (bf16[1024,768]{1,0:T(8,128)(2,1)}, bf16[4,12,256,256]{3,2,1,0:T(8,128)(2,1)}) custom-call(bf16[1024,2304]{1,0:T(8,128)(2,1)} %get-tuple-element.320.qkv_ref, s32[1024,1]{1,0:T(8,128)} %fusion.2.qid_ref, s32[4,1,256]{2,1,0:T(1,128)} %bitcast.85), custom_call_target="tpu_custom_call" | custom-call | flops 1610612736 | bytes 12582912 | tf_op jit(solution)/shard_map/attention/pallas_call | solution.py:342
  109.4 7.4 %add_norm.2 = (f32[1024,768]{1,0:T(8,128)}, f32[1024,1]{1,0:T(8,128)}, bf16[1024,768]{1,0:T(8,128)(2,1)}, f32[1024,768]{1,0:T(8,128)}) custom-call(bf16[1024,768]{1,0:T(8,128)(2,1)} %get-tuple-element.333.left_ref, bf16[768,768]{1,0:T(8,128)(2,1)} %bitcast.74, bf16[1024,768]{1,0:T(8,128)(2,1)} %get-tuple-element.335.base_ref.left_ref, ...), custom_call_target="tpu_custom_call" | custom-call | flops 1207959552 | bytes 12189696 | tf_op jit(solution)/shard_map/add_norm/pallas_call | solution.py:762
  120.4 4.8 %assemble.4 = bf16[16,2,24,3072]{3,2,1,0:T(8,128)(2,1)} custom-call(s32[3,16]{1,0:T(4,128)} %get-tuple-element.292.idx_ref, bf16[8,24,3072]{2,1,0:T(8,128)(2,1)} %copy-done.2, bf16[8,24,3072]{2,1,0:T(8,128)(2,1)} %collective-permute-done.14.refs_1_, bf16[8,24,3072]{2,1,0:T(8,128)(2,1)} %collective-permute-done.17.refs_2_, ...), custom_call_target="tpu_custom_call" | custom-call | bytes 9437184 | tf_op jit(solution)/shard_map/assemble/pallas_call | solution.py:118
  126.9 7.9 %expand.2 = (bf16[1024,3072]{1,0:T(8,128)(2,1)}, bf16[1024,3072]{1,0:T(8,128)(2,1)}) custom-call(bf16[1024,768]{1,0:T(8,128)(2,1)} %get-tuple-element.352.mid_ref.left_ref, bf16[768,3072]{1,0:T(8,128)(2,1)} %bitcast.62, f32[1,3072]{1,0:T(1,128)} %reshape.500.b_ref), custom_call_target="tpu_custom_call" | custom-call | flops 2415919104 | bytes 10223616 | tf_op jit(solution)/shard_map/expand/pallas_call | solution.py:638
  137.0 7.9 %expand.3 = (bf16[1024,3072]{1,0:T(8,128)(2,1)}, bf16[1024,3072]{1,0:T(8,128)(2,1)}) custom-call(bf16[1024,768]{1,0:T(8,128)(2,1)} %get-tuple-element.352.mid_ref.left_ref, bf16[768,3072]{1,0:T(8,128)(2,1)} %bitcast.63, f32[1,3072]{1,0:T(1,128)} %reshape.500.b_ref, ...), custom_call_target="tpu_custom_call", output_to_operand_aliasing={{0}: (3, {}), {1}: (4, {})} | custom-call | flops 2415919104 | bytes 10223616 | tf_op jit(solution)/shard_map/expand/pallas_call | solution.py:638
  145.9 4.9 %assemble.5 = bf16[16,2,96,768]{3,2,1,0:T(8,128)(2,1)} custom-call(s32[3,16]{1,0:T(4,128)} %get-tuple-element.292.idx_ref, bf16[8,96,768]{2,1,0:T(8,128)(2,1)} %copy-done.3, bf16[8,96,768]{2,1,0:T(8,128)(2,1)} %collective-permute-done.21.refs_1_, bf16[8,96,768]{2,1,0:T(8,128)(2,1)} %collective-permute-done.22.refs_2_, bf16[8,96,768]{2,1,0:T(8,128)(2,1)} %copy-done.11), custom_call_target="tpu_custom_call" | custom-call | bytes 9437184 | tf_op jit(solution)/shard_map/assemble/pallas_call | solution.py:118
  150.8 2.2 collective-permute-start.26
  153.1 11.6 %add_norm.3 = (f32[1024,768]{1,0:T(8,128)}, f32[1024,1]{1,0:T(8,128)}, bf16[1024,768]{1,0:T(8,128)(2,1)}) custom-call(bf16[1024,3072]{1,0:T(8,128)(2,1)} %get-tuple-element.373.left_ref, bf16[3072,768]{1,0:T(8,128)(2,1)} %bitcast.68, f32[1024,768]{1,0:T(8,128)} %get-tuple-element.381.base_ref, f32[1024,1]{1,0:T(8,128)} %convert_element_type.272.mask_ref, ...), custom_call_target="tpu_custom_call" | custom-call | flops 4831838208 | bytes 20447232 | tf_op jit(solution)/shard_map/add_norm/pallas_call | solution.py:762
  166.5 4.0 %collective-permute-done.27 = bf16[16,768]{1,0:T(8,128)(2,1)S(1)} collective-permute-done((bf16[16,768]{1,0:T(8,128)(2,1)S(1)}, bf16[16,768]{1,0:T(8,128)(2,1)S(1)}, u32[]{:S(2)}, u32[]{:S(2)}) %collective-permute-start.27) | collective-permute-done | bytes 24608 | tf_op jit(solution)/shard_map/ppermute | solution.py:72
  171.0 3.6 collective-permute-done.28
  177.6 2.7 join.1.cot_ref
  181.5 3.9 %collective-permute-done.30 = bf16[4,24,768]{2,1,0:T(8,128)(2,1)S(1)} collective-permute-done((bf16[4,24,768]{2,1,0:T(8,128)(2,1)S(1)}, bf16[4,24,768]{2,1,0:T(8,128)(2,1)S(1)}, u32[]{:S(2)}, u32[]{:S(2)}) %collective-permute-start.30) | collective-permute-done | bytes 147488 | tf_op jit(solution)/shard_map/ppermute | solution.py:1027
  190.0 6.5 %second_back.1 = (f32[1024,768]{1,0:T(8,128)}, bf16[1024,768]{1,0:T(8,128)(2,1)}, f32[8,768]{1,0:T(8,128)}) custom-call(bf16[1024,768]{1,0:T(8,128)(2,1)} %join.1.cot_ref, f32[4,4,768]{2,1,0:T(4,128)} %reshape.508.slot_ref, f32[1024,1]{1,0:T(8,128)} %convert_element_type.272.mask_ref, f32[1024,768]{1,0:T(8,128)} %get-tuple-element.395.norm_ref, ...), custom_call_target="tpu_custom_call" | custom-call | flops 15728640 | bytes 9437184 | tf_op jit(solution)/shard_map/second_back/pallas_call | solution.py:556
  197.2 10.1 %tall_grad.1 = (bf16[16,96,768]{2,1,0:T(8,128)(2,1)}, bf16[16,96,768]{2,1,0:T(8,128)(2,1)}) custom-call(s32[3,16]{1,0:T(4,128)} %get-tuple-element.291.table_ref, bf16[1024,3072]{1,0:T(8,128)(2,1)} %get-tuple-element.373.left_ref, bf16[1024,768]{1,0:T(8,128)(2,1)} %get-tuple-element.407.right_ref.grad_ref), custom_call_target="tpu_custom_call" | custom-call | flops 4831838208 | bytes 12582912 | tf_op jit(solution)/shard_map/tall_grad/pallas_call | solution.py:243
  209.8 11.7 %hidden_grad.1 = (bf16[1024,3072]{1,0:T(8,128)(2,1)}, f32[1,3072]{1,0:T(1,128)}) custom-call(bf16[1024,768]{1,0:T(8,128)(2,1)} %get-tuple-element.407.right_ref.grad_ref, bf16[3072,768]{1,0:T(8,128)(2,1)} %bitcast.69, bf16[1024,3072]{1,0:T(8,128)(2,1)} %get-tuple-element.408.slope_ref), custom_call_target="tpu_custom_call" | custom-call | flops 4831838208 | bytes 18874368 | tf_op jit(solution)/shard_map/hidden_grad/pallas_call | solution.py:289
  224.8 9.9 %weight_grad.3 = (bf16[16,24,3840]{2,1,0:T(8,128)(2,1)}, bf16[16,24,3840]{2,1,0:T(8,128)(2,1)}) custom-call(s32[3,16]{1,0:T(4,128)} %get-tuple-element.291.table_ref, bf16[1024,768]{1,0:T(8,128)(2,1)} %get-tuple-element.352.mid_ref.left_ref, bf16[1024,3072]{1,0:T(8,128)(2,1)} %get-tuple-element.425.right_ref.hidden_ref), custom_call_target="tpu_custom_call" | custom-call | flops 4831838208 | bytes 12582912 | tf_op jit(solution)/shard_map/weight_grad/pallas_call | solution.py:201
  236.4 12.4 %first_back.1 = (f32[1024,768]{1,0:T(8,128)}, bf16[1024,768]{1,0:T(8,128)(2,1)}, f32[8,768]{1,0:T(8,128)}) custom-call(bf16[1024,3072]{1,0:T(8,128)(2,1)} %get-tuple-element.425.right_ref.hidden_ref, bf16[768,3072]{1,0:T(8,128)(2,1)} %bitcast.64, f32[1024,768]{1,0:T(8,128)} %get-tuple-element.426.second_ref, f32[1024,768]{1,0:T(8,128)} %get-tuple-element.427.norm_ref, ...), custom_call_target="tpu_custom_call" | custom-call | flops 4831838208 | bytes 22020096 | tf_op jit(solution)/shard_map/first_back/pallas_call | solution.py:596
  248.8 5.1 %weight_grad.4 = (bf16[16,24,3840]{2,1,0:T(8,128)(2,1)}, bf16[16,24,3840]{2,1,0:T(8,128)(2,1)}) custom-call(s32[3,16]{1,0:T(4,128)} %get-tuple-element.291.table_ref, bf16[1024,768]{1,0:T(8,128)(2,1)} %get-tuple-element.333.left_ref, bf16[1024,768]{1,0:T(8,128)(2,1)} %get-tuple-element.445.right_ref, ...), custom_call_target="tpu_custom_call", output_to_operand_aliasing={{0}: (3, {}), {1}: (4, {})} | custom-call | flops 1207959552 | bytes 4325376 | tf_op jit(solution)/shard_map/weight_grad/pallas_call | solution.py:201
  254.0 2.2 add_convert_fusion.4
  257.0 3.8 convolution_convert_fusion.grad_ref
  260.9 11.9 %attention_back.2 = (bf16[1024,2304]{1,0:T(8,128)(2,1)}, f32[1,2304]{1,0:T(1,128)}) custom-call(bf16[1024,2304]{1,0:T(8,128)(2,1)} %get-tuple-element.320.qkv_ref, bf16[4,12,256,256]{3,2,1,0:T(8,128)(2,1)} %get-tuple-element.444.probs_ref, bf16[1024,768]{1,0:T(8,128)(2,1)} %convolution_convert_fusion.grad_ref), custom_call_target="tpu_custom_call" | custom-call | flops 1610612736 | bytes 8650752 | tf_op jit(solution)/shard_map/attention_back/pallas_call | solution.py:425
  278.5 6.2 %token_grad.2 = (bf16[160,768]{1,0:T(8,128)(2,1)}, bf16[96,768]{1,0:T(8,128)(2,1)}, bf16[96,768]{1,0:T(8,128)(2,1)}, bf16[160,768]{1,0:T(8,128)(2,1)}) custom-call(bf16[1024,2304]{1,0:T(8,128)(2,1)} %get-tuple-element.468.grad_ref._, bf16[768,2304]{1,0:T(8,128)(2,1)} %bitcast.66, f32[1024,768]{1,0:T(8,128)} %get-tuple-element.463.first_ref), custom_call_target="tpu_custom_call" | custom-call | flops 1811939328 | bytes 8257536 | tf_op jit(solution)/shard_map/token_grad/pallas_call | solution.py:682
  285.7 11.8 %attention_back.3 = (bf16[1024,2304]{1,0:T(8,128)(2,1)}, f32[1,2304]{1,0:T(1,128)}) custom-call(bf16[1024,2304]{1,0:T(8,128)(2,1)} %get-tuple-element.320.qkv_ref, bf16[4,12,256,256]{3,2,1,0:T(8,128)(2,1)} %get-tuple-element.444.probs_ref, bf16[1024,768]{1,0:T(8,128)(2,1)} %convolution_convert_fusion.grad_ref, ...), custom_call_target="tpu_custom_call", output_to_operand_aliasing={{0}: (3, {})} | custom-call | flops 1610612736 | bytes 8650752 | tf_op jit(solution)/shard_map/attention_back/pallas_call | solution.py:425
  305.2 2.1 collective-permute-start.45
  307.3 9.0 %weight_grad.5 = (bf16[16,24,2432]{2,1,0:T(8,128)(2,1)}, bf16[16,24,2432]{2,1,0:T(8,128)(2,1)}) custom-call(s32[3,16]{1,0:T(4,128)} %get-tuple-element.291.table_ref, bf16[1024,768]{1,0:T(8,128)(2,1)} %get-tuple-element.335.base_ref.left_ref, bf16[1024,2304]{1,0:T(8,128)(2,1)} %get-tuple-element.505.right_ref.grad_ref, ...), custom_call_target="tpu_custom_call" | custom-call | flops 3623878656 | bytes 9830400 | tf_op jit(solution)/shard_map/weight_grad/pallas_call | solution.py:201
  316.5 2.9 collective-permute-done.45.refs_1_
  319.4 2.7 deal.2
  322.1 6.6 %token_grad.3.own_ref = f32[512,768]{1,0:T(8,128)} custom-call(bf16[1024,2304]{1,0:T(8,128)(2,1)} %get-tuple-element.505.right_ref.grad_ref, bf16[768,2304]{1,0:T(8,128)(2,1)} %bitcast.67, f32[1024,768]{1,0:T(8,128)} %get-tuple-element.463.first_ref), custom_call_target="tpu_custom_call" | custom-call | flops 1811939328 | bytes 8257536 | tf_op jit(solution)/shard_map/token_grad/pallas_call | solution.py:682
  328.7 3.1 collective-permute-done.47.refs_2_
  336.1 2.5 collective-permute-start.50
  340.6 10.8 %collective-permute-done.49 = bf16[2,24,3840]{2,1,0:T(8,128)(2,1)S(1)} collective-permute-done((bf16[2,24,3840]{2,1,0:T(8,128)(2,1)S(1)}, bf16[2,24,3840]{2,1,0:T(8,128)(2,1)S(1)}, u32[]{:S(2)}, u32[]{:S(2)}) %collective-permute-start.49) | collective-permute-done | bytes 368672 | tf_op jit(solution)/shard_map/ppermute | solution.py:66
  357.1 3.6 deal.3
  360.7 5.3 %collective-permute-done.52 = bf16[1,24,3840]{2,1,0:T(8,128)(2,1)S(1)} collective-permute-done((bf16[1,24,3840]{2,1,0:T(8,128)(2,1)S(1)}, bf16[1,24,3840]{2,1,0:T(8,128)(2,1)S(1)}, u32[]{:S(2)}, u32[]{:S(2)}) %collective-permute-start.52) | collective-permute-done | bytes 184352 | tf_op jit(solution)/shard_map/ppermute | solution.py:66
  368.5 6.1 %collective-permute-done.53 = bf16[2,24,2432]{2,1,0:T(8,128)(2,1)S(1)} collective-permute-done((bf16[2,24,2432]{2,1,0:T(8,128)(2,1)S(1)}, bf16[2,24,2432]{2,1,0:T(8,128)(2,1)S(1)}, u32[]{:S(2)}, u32[]{:S(2)}) %collective-permute-start.53) | collective-permute-done | bytes 233504 | tf_op jit(solution)/shard_map/ppermute | solution.py:66
  378.4 4.8 %collective-permute-done.54 = bf16[1,24,2432]{2,1,0:T(8,128)(2,1)S(1)} collective-permute-done((bf16[1,24,2432]{2,1,0:T(8,128)(2,1)S(1)}, bf16[1,24,2432]{2,1,0:T(8,128)(2,1)S(1)}, u32[]{:S(2)}, u32[]{:S(2)}) %collective-permute-start.54) | collective-permute-done | bytes 116768 | tf_op jit(solution)/shard_map/ppermute | solution.py:66
  (334 shorter events, 98.5 us)
Async XLA Ops:
  3.5 11.4 %collective-permute-start = (bf16[1,24,3200]{2,1,0:T(8,128)(2,1)S(1)}, bf16[1,24,3200]{2,1,0:T(8,128)(2,1)S(1)}, u32[]{:S(2)}, u32[]{:S(2)}) collective-permute-start(bf16[1,24,3200]{2,1,0:T(8,128)(2,1)S(1)} %get-tuple-element.619), channel_id=1, source_target_pairs={{0,4},{1,5},{2,6},{3,7},{4,0},{5,1},{6,2},{7,3},{8,12},{9,13},{10,... | collective-permute-start | bytes 460808 | tf_op jit(solution)/shard_map/ppermute | solution.py:66
  15.0 13.8 %collective-permute-start.1 = (bf16[2,24,3200]{2,1,0:T(8,128)(2,1)S(1)}, bf16[2,24,3200]{2,1,0:T(8,128)(2,1)S(1)}, u32[]{:S(2)}, u32[]{:S(2)}) collective-permute-start(bf16[2,24,3200]{2,1,0:T(8,128)(2,1)S(1)} %pad_maximum_fusion.8), channel_id=1, source_target_pairs={{0,2},{1,3},{2,0},{3,1},{4,6},{5,7},{6,4},{7,5},{8,10},{9,11},{10,... | collective-permute-start | bytes 921608 | tf_op jit(solution)/shard_map/ppermute | solution.py:66
  15.8 13.1 %collective-permute-start.2 = (bf16[160,768]{1,0:T(8,128)(2,1)S(1)}, bf16[160,768]{1,0:T(8,128)(2,1)S(1)}, u32[]{:S(2)}, u32[]{:S(2)}) collective-permute-start(bf16[160,768]{1,0:T(8,128)(2,1)S(1)} %slice.382), channel_id=1, source_target_pairs={{0,4},{1,5},{2,6},{3,7},{4,0},{5,1},{6,2},{7,3},{8,12},{9,13},{10,... | collective-permute-start | bytes 737288 | tf_op jit(solution)/shard_map/ppermute | solution.py:72
  28.9 10.6 %collective-permute-start.3 = (bf16[4,24,3200]{2,1,0:T(8,128)(2,1)S(1)}, bf16[4,24,3200]{2,1,0:T(8,128)(2,1)S(1)}, u32[]{:S(2)}, u32[]{:S(2)}) collective-permute-start(bf16[4,24,3200]{2,1,0:T(8,128)(2,1)S(1)} %pad_maximum_fusion.4), channel_id=1, source_target_pairs={{0,8},{1,17},{2,10},{3,19},{4,12},{5,21},{6,14},{7,23},{8,0},{9,25... | collective-permute-start | bytes 1843208 | tf_op jit(solution)/shard_map/ppermute | solution.py:66
  30.2 9.2 %collective-permute-start.4 = (bf16[1,24,3072]{2,1,0:T(8,128)(2,1)S(1)}, bf16[1,24,3072]{2,1,0:T(8,128)(2,1)S(1)}, u32[]{:S(2)}, u32[]{:S(2)}) collective-permute-start(bf16[1,24,3072]{2,1,0:T(8,128)(2,1)S(1)} %get-tuple-element.294), channel_id=1, source_target_pairs={{0,4},{1,5},{2,6},{3,7},{4,0},{5,1},{6,2},{7,3},{8,12},{9,13},{10,... | collective-permute-start | bytes 442376 | tf_op jit(solution)/shard_map/ppermute | solution.py:66
  39.7 18.5 %collective-permute-start.5 = (bf16[8,24,3200]{2,1,0:T(8,128)(2,1)S(1)}, bf16[8,24,3200]{2,1,0:T(8,128)(2,1)}, u32[]{:S(2)}, u32[]{:S(2)}) collective-permute-start(bf16[8,24,3200]{2,1,0:T(8,128)(2,1)S(1)} %pad_maximum_fusion.refs_0_), channel_id=1, source_target_pairs={{0,16},{1,9},{2,18},{3,11},{4,20},{5,13},{6,22},{7,15},{8,24},{9,1... | collective-permute-start | bytes 3686408 | tf_op jit(solution)/shard_map/ppermute | solution.py:66
  41.0 8.2 %collective-permute-start.6 = (bf16[2,24,3072]{2,1,0:T(8,128)(2,1)S(1)}, bf16[2,24,3072]{2,1,0:T(8,128)(2,1)S(1)}, u32[]{:S(2)}, u32[]{:S(2)}) collective-permute-start(bf16[2,24,3072]{2,1,0:T(8,128)(2,1)S(1)} %pad_maximum_fusion.9), channel_id=1, source_target_pairs={{0,2},{1,3},{2,0},{3,1},{4,6},{5,7},{6,4},{7,5},{8,10},{9,11},{10,... | collective-permute-start | bytes 884744 | tf_op jit(solution)/shard_map/ppermute | solution.py:66
  46.0 24.1 %collective-permute-start.8 = (bf16[8,24,3200]{2,1,0:T(8,128)(2,1)S(1)}, bf16[8,24,3200]{2,1,0:T(8,128)(2,1)}, u32[]{:S(2)}, u32[]{:S(2)}) collective-permute-start(bf16[8,24,3200]{2,1,0:T(8,128)(2,1)S(1)} %pad_maximum_fusion.refs_0_), channel_id=1, source_target_pairs={{0,1},{1,0},{2,3},{3,2},{4,5},{5,4},{6,7},{7,6},{8,9},{9,8},{10,11... | collective-permute-start | bytes 3686408 | tf_op jit(solution)/shard_map/ppermute | solution.py:69
  46.0 12.1 %collective-permute-start.7 = (bf16[128,768]{1,0:T(8,128)(2,1)S(1)}, bf16[128,768]{1,0:T(8,128)(2,1)S(1)}, u32[]{:S(2)}, u32[]{:S(2)}) collective-permute-start(bf16[128,768]{1,0:T(8,128)(2,1)S(1)} %slice.383), channel_id=1, source_target_pairs={{0,4},{1,5},{2,6},{3,7},{4,0},{5,1},{6,2},{7,3},{8,12},{9,13},{10,... | collective-permute-start | bytes 589832 | tf_op jit(solution)/shard_map/ppermute | solution.py:72
  58.1 12.0 %collective-permute-start.9 = (bf16[8,24,3200]{2,1,0:T(8,128)(2,1)}, bf16[8,24,3200]{2,1,0:T(8,128)(2,1)}, u32[]{:S(2)}, u32[]{:S(2)}) collective-permute-start(bf16[8,24,3200]{2,1,0:T(8,128)(2,1)} %collective-permute-done.5.refs_1_), channel_id=1, source_target_pairs={{0,1},{1,0},{2,3},{3,2},{4,5},{5,4},{6,7},{7,6},{8,9},{9,8},{10,11... | collective-permute-start | bytes 3686408 | tf_op jit(solution)/shard_map/ppermute | solution.py:69
  58.9 10.0 %collective-permute-start.10 = (bf16[4,24,3072]{2,1,0:T(8,128)(2,1)S(1)}, bf16[4,24,3072]{2,1,0:T(8,128)(2,1)}, u32[]{:S(2)}, u32[]{:S(2)}) collective-permute-start(bf16[4,24,3072]{2,1,0:T(8,128)(2,1)S(1)} %pad_maximum_fusion.5), channel_id=1, source_target_pairs={{0,8},{1,17},{2,10},{3,19},{4,12},{5,21},{6,14},{7,23},{8,0},{9,25... | collective-permute-start | bytes 1769480 | tf_op jit(solution)/shard_map/ppermute | solution.py:66
  60.4 17.6 %collective-permute-start.11 = (bf16[224,768]{1,0:T(8,128)(2,1)S(1)}, bf16[224,768]{1,0:T(8,128)(2,1)}, u32[]{:S(2)}, u32[]{:S(2)}) collective-permute-start(bf16[224,768]{1,0:T(8,128)(2,1)S(1)} %slice.384), channel_id=1, source_target_pairs={{0,4},{1,5},{2,6},{3,7},{4,0},{5,1},{6,2},{7,3},{8,12},{9,13},{10,... | collective-permute-start | bytes 1032200 | tf_op jit(solution)/shard_map/ppermute | solution.py:72
  61.0 31.2 %collective-permute-start.13 = (s32[512]{0:T(512)S(1)}, s32[512]{0:T(512)S(1)}, u32[]{:S(2)}, u32[]{:S(2)}) collective-permute-start(s32[512]{0:T(512)S(1)} %get-tuple-element.633), channel_id=1, source_target_pairs={{0,4},{1,5},{2,6},{3,7},{4,0},{5,1},{6,2},{7,3},{8,12},{9,13},{10,... | collective-permute-start | bytes 6152 | tf_op jit(solution)/shard_map/ppermute | solution.py:72
  79.1 26.3 %collective-permute-start.14 = (bf16[8,24,3072]{2,1,0:T(8,128)(2,1)S(1)}, bf16[8,24,3072]{2,1,0:T(8,128)(2,1)}, u32[]{:S(2)}, u32[]{:S(2)}) collective-permute-start(bf16[8,24,3072]{2,1,0:T(8,128)(2,1)S(1)} %pad_maximum_fusion.1.refs_0_), channel_id=1, source_target_pairs={{0,16},{1,9},{2,18},{3,11},{4,20},{5,13},{6,22},{7,15},{8,24},{9,1... | collective-permute-start | bytes 3538952 | tf_op jit(solution)/shard_map/ppermute | solution.py:66
  81.9 8.8 %collective-permute-start.12 = (bf16[1,96,768]{2,1,0:T(8,128)(2,1)S(1)}, bf16[1,96,768]{2,1,0:T(8,128)(2,1)S(1)}, u32[]{:S(2)}, u32[]{:S(2)}) collective-permute-start(bf16[1,96,768]{2,1,0:T(8,128)(2,1)S(1)} %copy-done.42), channel_id=1, source_target_pairs={{0,4},{1,5},{2,6},{3,7},{4,0},{5,1},{6,2},{7,3},{8,12},{9,13},{10,... | collective-permute-start | bytes 442376 | tf_op jit(solution)/shard_map/ppermute | solution.py:66
  90.7 13.9 %collective-permute-start.15 = (bf16[2,96,768]{2,1,0:T(8,128)(2,1)S(1)}, bf16[2,96,768]{2,1,0:T(8,128)(2,1)S(1)}, u32[]{:S(2)}, u32[]{:S(2)}) collective-permute-start(bf16[2,96,768]{2,1,0:T(8,128)(2,1)S(1)} %pad_maximum_fusion.10), channel_id=1, source_target_pairs={{0,2},{1,3},{2,0},{3,1},{4,6},{5,7},{6,4},{7,5},{8,10},{9,11},{10,... | collective-permute-start | bytes 884744 | tf_op jit(solution)/shard_map/ppermute | solution.py:66
  92.8 25.1 %collective-permute-start.17 = (bf16[8,24,3072]{2,1,0:T(8,128)(2,1)S(1)}, bf16[8,24,3072]{2,1,0:T(8,128)(2,1)}, u32[]{:S(2)}, u32[]{:S(2)}) collective-permute-start(bf16[8,24,3072]{2,1,0:T(8,128)(2,1)S(1)} %pad_maximum_fusion.1.refs_0_), channel_id=1, source_target_pairs={{0,1},{1,0},{2,3},{3,2},{4,5},{5,4},{6,7},{7,6},{8,9},{9,8},{10,11... | collective-permute-start | bytes 3538952 | tf_op jit(solution)/shard_map/ppermute | solution.py:69
  92.9 12.5 %collective-permute-start.16 = (bf16[128,768]{1,0:T(8,128)(2,1)S(1)}, bf16[128,768]{1,0:T(8,128)(2,1)S(1)}, u32[]{:S(2)}, u32[]{:S(2)}) collective-permute-start(bf16[128,768]{1,0:T(8,128)(2,1)S(1)} %copy-done.35), channel_id=1, source_target_pairs={{0,4},{1,5},{2,6},{3,7},{4,0},{5,1},{6,2},{7,3},{8,12},{9,13},{10,... | collective-permute-start | bytes 589832 | tf_op jit(solution)/shard_map/ppermute | solution.py:72
  105.3 12.7 %collective-permute-start.18 = (bf16[8,24,3072]{2,1,0:T(8,128)(2,1)}, bf16[8,24,3072]{2,1,0:T(8,128)(2,1)}, u32[]{:S(2)}, u32[]{:S(2)}) collective-permute-start(bf16[8,24,3072]{2,1,0:T(8,128)(2,1)} %collective-permute-done.14.refs_1_), channel_id=1, source_target_pairs={{0,1},{1,0},{2,3},{3,2},{4,5},{5,4},{6,7},{7,6},{8,9},{9,8},{10,11... | collective-permute-start | bytes 3538952 | tf_op jit(solution)/shard_map/ppermute | solution.py:69
  105.3 11.4 %collective-permute-start.19 = (bf16[4,96,768]{2,1,0:T(8,128)(2,1)S(1)}, bf16[4,96,768]{2,1,0:T(8,128)(2,1)}, u32[]{:S(2)}, u32[]{:S(2)}) collective-permute-start(bf16[4,96,768]{2,1,0:T(8,128)(2,1)S(1)} %pad_maximum_fusion.6), channel_id=1, source_target_pairs={{0,8},{1,17},{2,10},{3,19},{4,12},{5,21},{6,14},{7,23},{8,0},{9,25... | collective-permute-start | bytes 1769480 | tf_op jit(solution)/shard_map/ppermute | solution.py:66
  107.6 10.4 %collective-permute-start.20 = (bf16[96,768]{1,0:T(8,128)(2,1)}, bf16[96,768]{1,0:T(8,128)(2,1)S(1)}, u32[]{:S(2)}, u32[]{:S(2)}) collective-permute-start(bf16[96,768]{1,0:T(8,128)(2,1)} %get-tuple-element.340), channel_id=1, source_target_pairs={{0,4},{1,5},{2,6},{3,7},{4,0},{5,1},{6,2},{7,3},{8,12},{9,13},{10,... | collective-permute-start | bytes 442376 | tf_op jit(solution)/shard_map/ppermute | solution.py:72
  118.0 17.6 %collective-permute-start.21 = (bf16[8,96,768]{2,1,0:T(8,128)(2,1)S(1)}, bf16[8,96,768]{2,1,0:T(8,128)(2,1)}, u32[]{:S(2)}, u32[]{:S(2)}) collective-permute-start(bf16[8,96,768]{2,1,0:T(8,128)(2,1)S(1)} %pad_maximum_fusion.2.refs_0_), channel_id=1, source_target_pairs={{0,16},{1,9},{2,18},{3,11},{4,20},{5,13},{6,22},{7,15},{8,24},{9,1... | collective-permute-start | bytes 3538952 | tf_op jit(solution)/shard_map/ppermute | solution.py:66
  119.3 16.3 %collective-permute-start.22 = (bf16[8,96,768]{2,1,0:T(8,128)(2,1)S(1)}, bf16[8,96,768]{2,1,0:T(8,128)(2,1)}, u32[]{:S(2)}, u32[]{:S(2)}) collective-permute-start(bf16[8,96,768]{2,1,0:T(8,128)(2,1)S(1)} %pad_maximum_fusion.2.refs_0_), channel_id=1, source_target_pairs={{0,1},{1,0},{2,3},{3,2},{4,5},{5,4},{6,7},{7,6},{8,9},{9,8},{10,11... | collective-permute-start | bytes 3538952 | tf_op jit(solution)/shard_map/ppermute | solution.py:69
  125.3 10.4 %collective-permute-start.23 = (bf16[96,768]{1,0:T(8,128)(2,1)S(1)}, bf16[96,768]{1,0:T(8,128)(2,1)S(1)}, u32[]{:S(2)}, u32[]{:S(2)}) collective-permute-start(bf16[96,768]{1,0:T(8,128)(2,1)S(1)} %copy-done.41), channel_id=1, source_target_pairs={{0,4},{1,5},{2,6},{3,7},{4,0},{5,1},{6,2},{7,3},{8,12},{9,13},{10,... | collective-permute-start | bytes 442376 | tf_op jit(solution)/shard_map/ppermute | solution.py:72
  135.7 9.2 %collective-permute-start.24 = (bf16[8,96,768]{2,1,0:T(8,128)(2,1)}, bf16[8,96,768]{2,1,0:T(8,128)(2,1)S(1)}, u32[]{:S(2)}, u32[]{:S(2)}) collective-permute-start(bf16[8,96,768]{2,1,0:T(8,128)(2,1)} %collective-permute-done.21.refs_1_), channel_id=1, source_target_pairs={{0,1},{1,0},{2,3},{3,2},{4,5},{5,4},{6,7},{7,6},{8,9},{9,8},{10,11... | collective-permute-start | bytes 3538952 | tf_op jit(solution)/shard_map/ppermute | solution.py:69
  136.2 8.7 %collective-permute-start.25 = (bf16[64,768]{1,0:T(8,128)(2,1)S(1)}, bf16[64,768]{1,0:T(8,128)(2,1)S(1)}, u32[]{:S(2)}, u32[]{:S(2)}) collective-permute-start(bf16[64,768]{1,0:T(8,128)(2,1)S(1)} %copy-done.46), channel_id=1, source_target_pairs={{0,4},{1,5},{2,6},{3,7},{4,0},{5,1},{6,2},{7,3},{8,12},{9,13},{10,... | collective-permute-start | bytes 294920 | tf_op jit(solution)/shard_map/ppermute | solution.py:72
  150.8 13.8 %collective-permute-start.26 = (bf16[128,768]{1,0:T(8,128)(2,1)S(1)}, bf16[128,768]{1,0:T(8,128)(2,1)S(1)}, u32[]{:S(2)}, u32[]{:S(2)}) collective-permute-start(bf16[128,768]{1,0:T(8,128)(2,1)S(1)} %copy-done.34), channel_id=1, source_target_pairs={{0,4},{1,5},{2,6},{3,7},{4,0},{5,1},{6,2},{7,3},{8,12},{9,13},{10,... | collective-permute-start | bytes 589832 | tf_op jit(solution)/shard_map/ppermute | solution.py:72
  196.6 11.9 %collective-permute-start.32 = (bf16[128,768]{1,0:T(8,128)(2,1)S(1)}, bf16[128,768]{1,0:T(8,128)(2,1)S(1)}, u32[]{:S(2)}, u32[]{:S(2)}) collective-permute-start(bf16[128,768]{1,0:T(8,128)(2,1)S(1)} %get-tuple-element.401), channel_id=1, source_target_pairs={{0,4},{1,5},{2,6},{3,7},{4,0},{5,1},{6,2},{7,3},{8,12},{9,13},{10,... | collective-permute-start | bytes 589832 | tf_op jit(solution)/shard_map/ppermute | solution.py:72
  208.4 13.2 %collective-permute-start.33 = (bf16[16,96,768]{2,1,0:T(8,128)(2,1)}, bf16[16,96,768]{2,1,0:T(8,128)(2,1)S(1)}, u32[]{:S(2)}, u32[]{:S(2)}) collective-permute-start(bf16[16,96,768]{2,1,0:T(8,128)(2,1)} %get-tuple-element.406), channel_id=1, source_target_pairs={{0,1},{1,0},{2,3},{3,2},{4,5},{5,4},{6,7},{7,6},{8,9},{9,8},{10,11... | collective-permute-start | bytes 7077896 | tf_op jit(solution)/shard_map/ppermute | solution.py:69
  208.4 13.1 %collective-permute-start.34 = (bf16[128,768]{1,0:T(8,128)(2,1)S(1)}, bf16[128,768]{1,0:T(8,128)(2,1)S(1)}, u32[]{:S(2)}, u32[]{:S(2)}) collective-permute-start(bf16[128,768]{1,0:T(8,128)(2,1)S(1)} %copy-done.32), channel_id=1, source_target_pairs={{0,4},{1,5},{2,6},{3,7},{4,0},{5,1},{6,2},{7,3},{8,12},{9,13},{10,... | collective-permute-start | bytes 589832 | tf_op jit(solution)/shard_map/ppermute | solution.py:72
  222.3 26.5 %collective-permute-start.35 = (bf16[8,96,768]{2,1,0:T(8,128)(2,1)S(1)}, bf16[8,96,768]{2,1,0:T(8,128)(2,1)S(1)}, u32[]{:S(2)}, u32[]{:S(2)}) collective-permute-start(bf16[8,96,768]{2,1,0:T(8,128)(2,1)S(1)} %add_convert_fusion.1), channel_id=1, source_target_pairs={{0,16},{1,9},{2,18},{3,11},{4,20},{5,13},{6,22},{7,15},{8,24},{9,1... | collective-permute-start | bytes 3538952 | tf_op jit(solution)/shard_map/ppermute | solution.py:66
  223.5 11.7 %collective-permute-start.36 = (bf16[128,768]{1,0:T(8,128)(2,1)S(1)}, bf16[128,768]{1,0:T(8,128)(2,1)S(1)}, u32[]{:S(2)}, u32[]{:S(2)}) collective-permute-start(bf16[128,768]{1,0:T(8,128)(2,1)S(1)} %get-tuple-element.421), channel_id=1, source_target_pairs={{0,4},{1,5},{2,6},{3,7},{4,0},{5,1},{6,2},{7,3},{8,12},{9,13},{10,... | collective-permute-start | bytes 589832 | tf_op jit(solution)/shard_map/ppermute | solution.py:72
  235.2 13.6 %collective-permute-start.37 = (bf16[128,768]{1,0:T(8,128)(2,1)S(1)}, bf16[128,768]{1,0:T(8,128)(2,1)S(1)}, u32[]{:S(2)}, u32[]{:S(2)}) collective-permute-start(bf16[128,768]{1,0:T(8,128)(2,1)S(1)} %copy-done.31), channel_id=1, source_target_pairs={{0,4},{1,5},{2,6},{3,7},{4,0},{5,1},{6,2},{7,3},{8,12},{9,13},{10,... | collective-permute-start | bytes 589832 | tf_op jit(solution)/shard_map/ppermute | solution.py:72
  253.9 18.9 %collective-permute-start.39 = (bf16[16,24,3840]{2,1,0:T(8,128)(2,1)}, bf16[16,24,3840]{2,1,0:T(8,128)(2,1)S(1)}, u32[]{:S(2)}, u32[]{:S(2)}) collective-permute-start(bf16[16,24,3840]{2,1,0:T(8,128)(2,1)} %get-tuple-element.443), channel_id=1, source_target_pairs={{0,1},{1,0},{2,3},{3,2},{4,5},{5,4},{6,7},{7,6},{8,9},{9,8},{10,11... | collective-permute-start | bytes 8847368 | tf_op jit(solution)/shard_map/ppermute | solution.py:69
  256.2 16.6 %collective-permute-start.38 = (bf16[4,96,768]{2,1,0:T(8,128)(2,1)}, bf16[4,96,768]{2,1,0:T(8,128)(2,1)S(1)}, u32[]{:S(2)}, u32[]{:S(2)}) collective-permute-start(bf16[4,96,768]{2,1,0:T(8,128)(2,1)} %add_convert_fusion.4), channel_id=1, source_target_pairs={{0,8},{1,17},{2,10},{3,19},{4,12},{5,21},{6,14},{7,23},{8,0},{9,25... | collective-permute-start | bytes 1769480 | tf_op jit(solution)/shard_map/ppermute | solution.py:66
  275.8 22.7 %collective-permute-start.41 = (bf16[8,24,3840]{2,1,0:T(8,128)(2,1)}, bf16[8,24,3840]{2,1,0:T(8,128)(2,1)S(1)}, u32[]{:S(2)}, u32[]{:S(2)}) collective-permute-start(bf16[8,24,3840]{2,1,0:T(8,128)(2,1)} %add_convert_fusion), channel_id=1, source_target_pairs={{0,16},{1,9},{2,18},{3,11},{4,20},{5,13},{6,22},{7,15},{8,24},{9,1... | collective-permute-start | bytes 4423688 | tf_op jit(solution)/shard_map/ppermute | solution.py:66
  277.1 21.5 %collective-permute-start.40 = (bf16[2,96,768]{2,1,0:T(8,128)(2,1)S(1)}, bf16[2,96,768]{2,1,0:T(8,128)(2,1)S(1)}, u32[]{:S(2)}, u32[]{:S(2)}) collective-permute-start(bf16[2,96,768]{2,1,0:T(8,128)(2,1)S(1)} %add_convert_fusion.7), channel_id=1, source_target_pairs={{0,2},{1,3},{2,0},{3,1},{4,6},{5,7},{6,4},{7,5},{8,10},{9,11},{10,... | collective-permute-start | bytes 884744 | tf_op jit(solution)/shard_map/ppermute | solution.py:66
  284.6 13.9 %collective-permute-start.42 = (bf16[160,768]{1,0:T(8,128)(2,1)}, bf16[160,768]{1,0:T(8,128)(2,1)}, u32[]{:S(2)}, u32[]{:S(2)}) collective-permute-start(bf16[160,768]{1,0:T(8,128)(2,1)} %get-tuple-element.471), channel_id=1, source_target_pairs={{0,4},{1,5},{2,6},{3,7},{4,0},{5,1},{6,2},{7,3},{8,12},{9,13},{10,... | collective-permute-start | bytes 737288 | tf_op jit(solution)/shard_map/ppermute | solution.py:72
  300.0 19.4 %collective-permute-start.43 = (bf16[4,24,3840]{2,1,0:T(8,128)(2,1)}, bf16[4,24,3840]{2,1,0:T(8,128)(2,1)}, u32[]{:S(2)}, u32[]{:S(2)}) collective-permute-start(bf16[4,24,3840]{2,1,0:T(8,128)(2,1)} %add_convert_fusion.3), channel_id=1, source_target_pairs={{0,8},{1,17},{2,10},{3,19},{4,12},{5,21},{6,14},{7,23},{8,0},{9,25... | collective-permute-start | bytes 2211848 | tf_op jit(solution)/shard_map/ppermute | solution.py:66
  304.3 12.2 %collective-permute-start.44 = (bf16[1,96,768]{2,1,0:T(8,128)(2,1)S(1)}, bf16[1,96,768]{2,1,0:T(8,128)(2,1)S(1)}, u32[]{:S(2)}, u32[]{:S(2)}) collective-permute-start(bf16[1,96,768]{2,1,0:T(8,128)(2,1)S(1)} %add_convert_fusion.10), channel_id=1, source_target_pairs={{0,4},{1,5},{2,6},{3,7},{4,0},{5,1},{6,2},{7,3},{8,12},{9,13},{10,... | collective-permute-start | bytes 442376 | tf_op jit(solution)/shard_map/ppermute | solution.py:66
  305.2 14.2 %collective-permute-start.45 = (bf16[96,768]{1,0:T(8,128)(2,1)}, bf16[96,768]{1,0:T(8,128)(2,1)S(1)}, u32[]{:S(2)}, u32[]{:S(2)}) collective-permute-start(bf16[96,768]{1,0:T(8,128)(2,1)} %get-tuple-element.500), channel_id=1, source_target_pairs={{0,4},{1,5},{2,6},{3,7},{4,0},{5,1},{6,2},{7,3},{8,12},{9,13},{10,... | collective-permute-start | bytes 442376 | tf_op jit(solution)/shard_map/ppermute | solution.py:72
  319.4 12.4 %collective-permute-start.46 = (bf16[16,24,2432]{2,1,0:T(8,128)(2,1)}, bf16[16,24,2432]{2,1,0:T(8,128)(2,1)}, u32[]{:S(2)}, u32[]{:S(2)}) collective-permute-start(bf16[16,24,2432]{2,1,0:T(8,128)(2,1)} %get-tuple-element.504), channel_id=1, source_target_pairs={{0,1},{1,0},{2,3},{3,2},{4,5},{5,4},{6,7},{7,6},{8,9},{9,8},{10,11... | collective-permute-start | bytes 5603336 | tf_op jit(solution)/shard_map/ppermute | solution.py:69
  322.1 9.7 %collective-permute-start.47 = (bf16[96,768]{1,0:T(8,128)(2,1)}, bf16[96,768]{1,0:T(8,128)(2,1)S(1)}, u32[]{:S(2)}, u32[]{:S(2)}) collective-permute-start(bf16[96,768]{1,0:T(8,128)(2,1)} %get-tuple-element.508), channel_id=1, source_target_pairs={{0,4},{1,5},{2,6},{3,7},{4,0},{5,1},{6,2},{7,3},{8,12},{9,13},{10,... | collective-permute-start | bytes 442376 | tf_op jit(solution)/shard_map/ppermute | solution.py:72
  333.3 18.1 %collective-permute-start.48 = (bf16[8,24,2432]{2,1,0:T(8,128)(2,1)S(1)}, bf16[8,24,2432]{2,1,0:T(8,128)(2,1)S(1)}, u32[]{:S(2)}, u32[]{:S(2)}) collective-permute-start(bf16[8,24,2432]{2,1,0:T(8,128)(2,1)S(1)} %add_convert_fusion.2), channel_id=1, source_target_pairs={{0,16},{1,9},{2,18},{3,11},{4,20},{5,13},{6,22},{7,15},{8,24},{9,1... | collective-permute-start | bytes 2801672 | tf_op jit(solution)/shard_map/ppermute | solution.py:66
  336.0 15.4 %collective-permute-start.49 = (bf16[2,24,3840]{2,1,0:T(8,128)(2,1)S(1)}, bf16[2,24,3840]{2,1,0:T(8,128)(2,1)S(1)}, u32[]{:S(2)}, u32[]{:S(2)}) collective-permute-start(bf16[2,24,3840]{2,1,0:T(8,128)(2,1)S(1)} %add_convert_fusion.6), channel_id=1, source_target_pairs={{0,2},{1,3},{2,0},{3,1},{4,6},{5,7},{6,4},{7,5},{8,10},{9,11},{10,... | collective-permute-start | bytes 1105928 | tf_op jit(solution)/shard_map/ppermute | solution.py:66
  336.1 15.4 %collective-permute-start.50 = (bf16[160,768]{1,0:T(8,128)(2,1)S(1)}, bf16[160,768]{1,0:T(8,128)(2,1)S(1)}, u32[]{:S(2)}, u32[]{:S(2)}) collective-permute-start(bf16[160,768]{1,0:T(8,128)(2,1)S(1)} %copy-done.62), channel_id=1, source_target_pairs={{0,4},{1,5},{2,6},{3,7},{4,0},{5,1},{6,2},{7,3},{8,12},{9,13},{10,... | collective-permute-start | bytes 737288 | tf_op jit(solution)/shard_map/ppermute | solution.py:72
  353.7 12.3 %collective-permute-start.51 = (bf16[4,24,2432]{2,1,0:T(8,128)(2,1)S(1)}, bf16[4,24,2432]{2,1,0:T(8,128)(2,1)S(1)}, u32[]{:S(2)}, u32[]{:S(2)}) collective-permute-start(bf16[4,24,2432]{2,1,0:T(8,128)(2,1)S(1)} %add_convert_fusion.5), channel_id=1, source_target_pairs={{0,8},{1,17},{2,10},{3,19},{4,12},{5,21},{6,14},{7,23},{8,0},{9,25... | collective-permute-start | bytes 1400840 | tf_op jit(solution)/shard_map/ppermute | solution.py:66
  355.8 10.2 %collective-permute-start.52 = (bf16[1,24,3840]{2,1,0:T(8,128)(2,1)S(1)}, bf16[1,24,3840]{2,1,0:T(8,128)(2,1)S(1)}, u32[]{:S(2)}, u32[]{:S(2)}) collective-permute-start(bf16[1,24,3840]{2,1,0:T(8,128)(2,1)S(1)} %add_convert_fusion.9), channel_id=1, source_target_pairs={{0,4},{1,5},{2,6},{3,7},{4,0},{5,1},{6,2},{7,3},{8,12},{9,13},{10,... | collective-permute-start | bytes 552968 | tf_op jit(solution)/shard_map/ppermute | solution.py:66
  (71 other events, 618.9 us)
